TPU v7x, 32 devices: a whole 2x2x4 slice. The times are simulated.
32 devices in a mesh: rep: 8 (over z, core), shard: 4 (over y, x).
Axes of the slice: x: 2, y: 2, z: 4, core: 2. Of those that a mesh axis runs over, the one named last changes fastest.
Arguments:
- block_input: bfloat16 [2, 8192, 960], P(None, ('rep', 'shard')), may hold values from -6 to 6
- parent_ids: int32 [2, 8, 8], P(None, 'rep'), may hold values from 0 to 6, as said below
- w_query: bfloat16 [960, 960], P('shard'), may hold values from -0.1875 to 0.1875
- key_weight: bfloat16 [960, 320], P('shard'), may hold values from -0.1875 to 0.1875
- value_weight: bfloat16 [960, 320], P('shard'), may hold values from -0.1875 to 0.1875
- w_output: bfloat16 [960, 960], P('shard'), may hold values from -3.5 to 3.5
- w_gate: bfloat16 [960, 2560], P('shard'), may hold values from -0.1875 to 0.1875
- w_up: bfloat16 [960, 2560], P('shard'), may hold values from -0.1875 to 0.1875
- w_down: bfloat16 [2560, 960], P('shard'), may hold values from -0.125 to 0.125
- norm_first: bfloat16 [960], P('shard'), may hold values from 0.25 to 1.75
- norm_second: bfloat16 [960], P('shard'), may hold values from 0.25 to 1.75
- out_cotangent: bfloat16 [2, 8192, 960], P(None, ('rep', 'shard')), may hold values from -6 to 6
Outputs:
- block_output: bfloat16 [2, 8192, 960], P(None, ('rep', 'shard'))
- input_grad: bfloat16 [2, 8192, 960], P(None, ('rep', 'shard'))
- grad_query: float32 [960, 960], P('shard')
- grad_key: float32 [960, 320], P('shard')
- grad_value: float32 [960, 320], P('shard')
- grad_output: float32 [960, 960], P('shard')
- grad_gate: float32 [960, 2560], P('shard')
- grad_upper: float32 [960, 2560], P('shard')
- grad_down: float32 [2560, 960], P('shard')
- grad_norm_first: float32 [960], P('shard')
- grad_norm_second: float32 [960], P('shard')
Inputs may be any that keep to these rules, and one draw needn't show every extreme that they name: `parent_ids`: segment 0 of every tree is its own parent; every odd segment's parent is the segment just before it; every even segment after 0 has as parent one of the two segments just before it.
All inputs are finite; a program needn't handle non-finite values.
Results may differ from a plain program's by a relative error of at most 0.022.
Values may be sent and summed in bfloat16 or wider, within the bound.
No kernel may reach another device: no remote copies, remote signals or barrier semaphores. Data moves between devices by JAX's collectives and lax.ppermute only.
A program may use at most 192 MiB of HBM per device.

v0:
```python
import math

import jax
import jax.numpy as jnp
from jax import lax
from jax.sharding import PartitionSpec as P

QUERY_HEADS = 15
KEY_VALUE_HEADS = 5
HEAD_SIZE = 64


EPS = 1e-05
HIGH = lax.Precision.HIGHEST


def shortened(shard):

    def short(part):
        return part.astype(jnp.bfloat16) if part.dtype == jnp.float32 else part

    return jax.tree.map(short, shard)


def ancestry(parents_row, seg_count):
    identity = jnp.eye(seg_count, dtype=jnp.float32)
    selector = (parents_row[:, None] == jnp.arange(seg_count, dtype=jnp.int32)[None, :]).astype(
        jnp.float32
    )

    def extend(counter, table):
        return jnp.maximum(identity, jnp.dot(selector, table, precision=HIGH))

    return lax.fori_loop(0, seg_count, extend, identity)


def rotation_tables(positions):
    freqs = jnp.exp(
        -math.log(10000.0) * jnp.arange(HEAD_SIZE // 2, dtype=jnp.float32) * (2.0 / HEAD_SIZE)
    )
    angles = positions[:, None] * freqs[None, :]
    return (jnp.cos(angles)[:, None, :], jnp.sin(angles)[:, None, :])


def apply_rotation(vectors, cosine_table, sine_table, heads, inverse):
    shaped = vectors.reshape(vectors.shape[0], heads, HEAD_SIZE)
    first_half = shaped[..., : HEAD_SIZE // 2]
    second_half = shaped[..., HEAD_SIZE // 2 :]
    if inverse:
        turned = jnp.concatenate(
            [
                first_half * cosine_table + second_half * sine_table,
                second_half * cosine_table - first_half * sine_table,
            ],
            axis=-1,
        )
    else:
        turned = jnp.concatenate(
            [
                first_half * cosine_table - second_half * sine_table,
                second_half * cosine_table + first_half * sine_table,
            ],
            axis=-1,
        )
    return turned.reshape(vectors.shape[0], heads * HEAD_SIZE)


def inverse_rms(value_matrix):
    return lax.rsqrt(jnp.mean(value_matrix * value_matrix, axis=-1, keepdims=True) + EPS)


def norm_backward(d_normed, normed, inverse_root, gain):
    d_scaled = d_normed * gain
    return inverse_root * (d_scaled - normed * jnp.mean(d_scaled * normed, axis=-1, keepdims=True))


def local(
    block_input,
    parent_ids,
    w_query,
    key_weight,
    value_weight,
    w_output,
    w_gate,
    w_up,
    w_down,
    norm_first,
    norm_second,
    out_cotangent,
):
    micro_count, token_rows, width = block_input.shape
    group_size = lax.axis_size("shard")
    tree_row_slice = token_rows * group_size
    seg_count = parent_ids.shape[2]
    seg_rows = tree_row_slice // seg_count
    heads_per_group = QUERY_HEADS // KEY_VALUE_HEADS
    scale = HEAD_SIZE ** (-0.5)
    first_row = lax.axis_index("shard") * token_rows
    full_sums = None
    outputs_list = []
    grads_list = []
    for micro_idx in range(micro_count):
        gathered = (
            lax.all_gather(w_query, "shard", axis=0, tiled=True),
            lax.all_gather(key_weight, "shard", axis=0, tiled=True),
            lax.all_gather(value_weight, "shard", axis=0, tiled=True),
            lax.all_gather(w_output, "shard", axis=0, tiled=True),
            lax.all_gather(w_gate, "shard", axis=0, tiled=True),
            lax.all_gather(w_up, "shard", axis=0, tiled=True),
            lax.all_gather(w_down, "shard", axis=0, tiled=True),
            lax.all_gather(norm_first, "shard", axis=0, tiled=True),
            lax.all_gather(norm_second, "shard", axis=0, tiled=True),
        )
        (
            full_query,
            full_key,
            full_value,
            full_output,
            full_gate,
            full_upper,
            full_down,
            gain_first,
            gain_second,
        ) = gathered
        gain_one = gain_first.astype(jnp.float32)
        gain_two = gain_second.astype(jnp.float32)
        table = ancestry(parent_ids[micro_idx, 0], seg_count)
        rows_all = jnp.arange(tree_row_slice, dtype=jnp.int32)
        segments = rows_all // seg_rows
        seg_onehot = (segments[:, None] == jnp.arange(seg_count, dtype=jnp.int32)[None, :]).astype(
            jnp.float32
        )
        depth = jnp.sum(table, axis=1) - 1.0
        positions_all = jnp.dot(seg_onehot, depth, precision=HIGH) * seg_rows + (
            rows_all % seg_rows
        ).astype(jnp.float32)
        my_rows = first_row + jnp.arange(token_rows, dtype=jnp.int32)
        my_onehot = lax.dynamic_slice_in_dim(seg_onehot, first_row, token_rows, 0)
        my_positions = lax.dynamic_slice_in_dim(positions_all, first_row, token_rows, 0)
        reach = jnp.dot(jnp.dot(my_onehot, table, precision=HIGH), seg_onehot.T, precision=HIGH)
        allowed = (reach > 0.5) & (rows_all[None, :] <= my_rows[:, None])
        cosine_table, sine_table = rotation_tables(my_positions)
        inputs = block_input[micro_idx].astype(jnp.float32)
        cotangent = out_cotangent[micro_idx]
        inv_first = inverse_rms(inputs)
        normed_first = inputs * inv_first
        act_first = (normed_first * gain_one).astype(jnp.bfloat16)
        query_lin = jnp.dot(act_first, full_query, preferred_element_type=jnp.float32)
        key_linear = jnp.dot(act_first, full_key, preferred_element_type=jnp.float32)
        value_linear = jnp.dot(act_first, full_value, preferred_element_type=jnp.float32)
        query_rotated = apply_rotation(
            query_lin, cosine_table, sine_table, QUERY_HEADS, False
        ).astype(jnp.bfloat16)
        key_rotated = apply_rotation(
            key_linear, cosine_table, sine_table, KEY_VALUE_HEADS, False
        ).astype(jnp.bfloat16)
        value_low = value_linear.astype(jnp.bfloat16)
        key_tree_rows, value_tree_rows = (
            lax.all_gather(key_rotated, "shard", axis=0, tiled=True),
            lax.all_gather(value_low, "shard", axis=0, tiled=True),
        )
        query_head_rows = query_rotated.reshape(
            token_rows, KEY_VALUE_HEADS, heads_per_group, HEAD_SIZE
        ).transpose(1, 2, 0, 3)
        key_head_rows = key_tree_rows.reshape(tree_row_slice, KEY_VALUE_HEADS, HEAD_SIZE).transpose(
            1, 0, 2
        )
        value_head_rows = value_tree_rows.reshape(
            tree_row_slice, KEY_VALUE_HEADS, HEAD_SIZE
        ).transpose(1, 0, 2)

        def head_forward(operands):
            query_part, key_part, value_part = operands
            raw = (
                jnp.einsum("gtd,nd->gtn", query_part, key_part, preferred_element_type=jnp.float32)
                * scale
            )
            masked = jnp.where(allowed[None], raw, -1e30)
            peak = jnp.max(masked, axis=-1, keepdims=True)
            expo = jnp.where(allowed[None], jnp.exp(masked - peak), 0.0)
            total = jnp.sum(expo, axis=-1, keepdims=True)
            probs = expo / total
            mixed = jnp.einsum(
                "gtn,nd->gtd",
                probs.astype(jnp.bfloat16),
                value_part,
                preferred_element_type=jnp.float32,
            )
            return (mixed, peak + jnp.log(total))

        head_out, log_totals = lax.map(
            head_forward, (query_head_rows, key_head_rows, value_head_rows)
        )
        attn_low = (
            head_out.transpose(2, 0, 1, 3)
            .reshape(token_rows, QUERY_HEADS * HEAD_SIZE)
            .astype(jnp.bfloat16)
        )
        resid = inputs + jnp.dot(attn_low, full_output, preferred_element_type=jnp.float32)
        inv_second = inverse_rms(resid)
        normed_second = resid * inv_second
        act_second = (normed_second * gain_two).astype(jnp.bfloat16)
        gate_lin = jnp.dot(act_second, full_gate, preferred_element_type=jnp.float32)
        upper_lin = jnp.dot(act_second, full_upper, preferred_element_type=jnp.float32)
        sigmoid_gate = jax.nn.sigmoid(gate_lin)
        silu_gate = gate_lin * sigmoid_gate
        inner = (silu_gate * upper_lin).astype(jnp.bfloat16)
        block_out = (resid + jnp.dot(inner, full_down, preferred_element_type=jnp.float32)).astype(
            jnp.bfloat16
        )
        cot_float = cotangent.astype(jnp.float32)
        grad_down_local = jnp.einsum(
            "tf,td->fd", inner, cotangent, preferred_element_type=jnp.float32
        )
        d_inner = jnp.einsum("td,fd->tf", cotangent, full_down, preferred_element_type=jnp.float32)
        d_gate = (
            d_inner * upper_lin * sigmoid_gate * (1.0 + gate_lin * (1.0 - sigmoid_gate))
        ).astype(jnp.bfloat16)
        d_upper = (d_inner * silu_gate).astype(jnp.bfloat16)
        grad_gate_local = jnp.einsum(
            "td,tf->df", act_second, d_gate, preferred_element_type=jnp.float32
        )
        grad_upper_local = jnp.einsum(
            "td,tf->df", act_second, d_upper, preferred_element_type=jnp.float32
        )
        d_act_second = jnp.einsum(
            "tf,df->td", d_gate, full_gate, preferred_element_type=jnp.float32
        ) + jnp.einsum("tf,df->td", d_upper, full_upper, preferred_element_type=jnp.float32)
        grad_gain_two = jnp.sum(d_act_second * normed_second, axis=0)
        d_resid = cot_float + norm_backward(d_act_second, normed_second, inv_second, gain_two)
        d_resid_low = d_resid.astype(jnp.bfloat16)
        grad_output_local = jnp.einsum(
            "tk,td->kd", attn_low, d_resid_low, preferred_element_type=jnp.float32
        )
        attention_grad = jnp.einsum(
            "td,kd->tk", d_resid_low, full_output, preferred_element_type=jnp.float32
        ).astype(jnp.bfloat16)
        attention_head_grad = attention_grad.reshape(
            token_rows, KEY_VALUE_HEADS, heads_per_group, HEAD_SIZE
        ).transpose(1, 2, 0, 3)

        def head_backward(operands):
            query_part, key_part, value_part, d_out_part, log_part = operands
            raw = (
                jnp.einsum("gtd,nd->gtn", query_part, key_part, preferred_element_type=jnp.float32)
                * scale
            )
            probs = jnp.where(
                allowed[None], jnp.exp(jnp.where(allowed[None], raw, -1e30) - log_part), 0.0
            )
            d_probs = jnp.einsum(
                "gtd,nd->gtn", d_out_part, value_part, preferred_element_type=jnp.float32
            )
            centre = jnp.sum(probs * d_probs, axis=-1, keepdims=True)
            d_scores = (probs * (d_probs - centre) * scale).astype(jnp.bfloat16)
            d_query_part = jnp.einsum(
                "gtn,nd->gtd", d_scores, key_part, preferred_element_type=jnp.float32
            )
            d_key_part = jnp.einsum(
                "gtn,gtd->nd", d_scores, query_part, preferred_element_type=jnp.float32
            )
            d_value_part = jnp.einsum(
                "gtn,gtd->nd",
                probs.astype(jnp.bfloat16),
                d_out_part,
                preferred_element_type=jnp.float32,
            )
            return (d_query_part, d_key_part, d_value_part)

        d_query_heads, key_head_grad, value_head_grad = lax.map(
            head_backward,
            (query_head_rows, key_head_rows, value_head_rows, attention_head_grad, log_totals),
        )
        key_tree_grad = key_head_grad.transpose(1, 0, 2).reshape(
            tree_row_slice, KEY_VALUE_HEADS * HEAD_SIZE
        )
        value_tree_grad = value_head_grad.transpose(1, 0, 2).reshape(
            tree_row_slice, KEY_VALUE_HEADS * HEAD_SIZE
        )
        key_grad_total, value_sum = (
            lax.psum_scatter(
                key_tree_grad.astype(jnp.bfloat16), "shard", scatter_dimension=0, tiled=True
            ).astype(jnp.float32),
            lax.psum_scatter(
                value_tree_grad.astype(jnp.bfloat16), "shard", scatter_dimension=0, tiled=True
            ).astype(jnp.float32),
        )
        d_query_rot = d_query_heads.transpose(2, 0, 1, 3).reshape(
            token_rows, QUERY_HEADS * HEAD_SIZE
        )
        d_query_low = apply_rotation(
            d_query_rot, cosine_table, sine_table, QUERY_HEADS, True
        ).astype(jnp.bfloat16)
        key_lower_grad = apply_rotation(
            key_grad_total, cosine_table, sine_table, KEY_VALUE_HEADS, True
        ).astype(jnp.bfloat16)
        d_value_low = value_sum.astype(jnp.bfloat16)
        grad_query_local = jnp.einsum(
            "td,tk->dk", act_first, d_query_low, preferred_element_type=jnp.float32
        )
        grad_key_local = jnp.einsum(
            "td,tk->dk", act_first, key_lower_grad, preferred_element_type=jnp.float32
        )
        grad_value_local = jnp.einsum(
            "td,tk->dk", act_first, d_value_low, preferred_element_type=jnp.float32
        )
        d_act_first = (
            jnp.einsum("tk,dk->td", d_query_low, full_query, preferred_element_type=jnp.float32)
            + jnp.einsum("tk,dk->td", key_lower_grad, full_key, preferred_element_type=jnp.float32)
            + jnp.einsum("tk,dk->td", d_value_low, full_value, preferred_element_type=jnp.float32)
        )
        grad_gain_one = jnp.sum(d_act_first * normed_first, axis=0)
        d_input = d_resid + norm_backward(d_act_first, normed_first, inv_first, gain_one)
        outputs_list.append(block_out)
        grads_list.append(d_input.astype(jnp.bfloat16))
        local_grads = (
            grad_query_local,
            grad_key_local,
            grad_value_local,
            grad_output_local,
            grad_gate_local,
            grad_upper_local,
            grad_down_local,
            grad_gain_one,
            grad_gain_two,
        )
        if full_sums is None:
            full_sums = local_grads
        else:
            full_sums = tuple((total + part for total, part in zip(full_sums, local_grads)))
    owned_final = jax.tree.map(
        lambda part: part.astype(jnp.float32),
        lax.psum_scatter(shortened(full_sums), "shard", scatter_dimension=0, tiled=True),
    )
    summed = jax.tree.map(
        lambda part: part.astype(jnp.float32), lax.psum(shortened(owned_final), "rep")
    )
    return (
        jnp.stack(outputs_list, axis=0),
        jnp.stack(grads_list, axis=0),
        summed[0],
        summed[1],
        summed[2],
        summed[3],
        summed[4],
        summed[5],
        summed[6],
        summed[7],
        summed[8],
    )


def solution(mesh):
    return jax.shard_map(
        local,
        mesh=mesh,
        in_specs=(
            P(None, ("rep", "shard"), None),
            P(None, "rep", None),
            P("shard", None),
            P("shard", None),
            P("shard", None),
            P("shard", None),
            P("shard", None),
            P("shard", None),
            P("shard", None),
            P("shard"),
            P("shard"),
            P(None, ("rep", "shard"), None),
        ),
        out_specs=(
            P(None, ("rep", "shard"), None),
            P(None, ("rep", "shard"), None),
            P("shard", None),
            P("shard", None),
            P("shard", None),
            P("shard", None),
            P("shard", None),
            P("shard", None),
            P("shard", None),
            P("shard"),
            P("shard"),
        ),
        check_vma=False,
    )
```

profile of v0, /device:TPU:0, one launch (start us, length us, event | category | flops | bytes accessed | tf_op | source)
XLA Modules:
  0.0 1025.1 jit_solution(1078447932777001471)
XLA Ops:
  12.7 11.4 %all-reduce.9 = (bf16[960]{0:T(1024)(128)(2,1)S(1)}, bf16[960]{0:T(1024)(128)(2,1)S(1)}) all-reduce(bf16[960]{0:T(1024)(128)(2,1)S(1)} %dynamic-update-slice, bf16[960]{0:T(1024)(128)(2,1)S(1)} %dynamic-update-slice.1), channel_id=1, replica_groups=mesh['rep'=8,'shard'=4] {'shard'}, use_global_device_ids=true, to_apply=%add | all-reduce | flops 1920 | bytes 7680
  24.4 10.5 %all-gather = bf16[4,240,320]{1,2,0:T(8,128)(2,1)S(1)} all-gather(bf16[1,240,320]{1,2,0:T(8,128)(2,1)S(1)} %bitcast.491), channel_id=1, replica_groups=mesh['rep'=8,'shard'=4] {'shard'}, dimensions={0}, use_global_device_ids=true | all-gather | bytes 768000 | tf_op jit(solution)/shard_map/all_gather | solution.py:105
  36.0 16.0 %all-gather.1 = bf16[4,240,320]{1,2,0:T(8,128)(2,1)S(1)} all-gather(bf16[1,240,320]{1,2,0:T(8,128)(2,1)S(1)} %bitcast.492), channel_id=1, replica_groups=mesh['rep'=8,'shard'=4] {'shard'}, dimensions={0}, use_global_device_ids=true | all-gather | bytes 768000 | tf_op jit(solution)/shard_map/all_gather | solution.py:106
  64.1 15.5 %all_gather.51 = bf16[1024,320]{0,1:T(8,128)(2,1)} all-gather(bf16[256,320]{0,1:T(8,128)(2,1)S(1)} %bitcast.487), channel_id=1, replica_groups=mesh['rep'=8,'shard'=4] {'shard'}, dimensions={0}, use_global_device_ids=true | all-gather | bytes 819200 | tf_op jit(solution)/shard_map/all_gather | solution.py:159
  79.6 18.2 %all_gather.53 = bf16[1024,320]{0,1:T(8,128)(2,1)S(1)} all-gather(bf16[256,320]{0,1:T(8,128)(2,1)S(1)} %convolution_convert_fusion.3), channel_id=1, replica_groups=mesh['rep'=8,'shard'=4] {'shard'}, dimensions={0}, use_global_device_ids=true | all-gather | bytes 819200 | tf_op jit(solution)/shard_map/all_gather | solution.py:160
  97.9 20.0 %all_gather.59 = bf16[1024,320]{0,1:T(8,128)(2,1)} all-gather(bf16[256,320]{0,1:T(8,128)(2,1)S(1)} %bitcast.488), channel_id=1, replica_groups=mesh['rep'=8,'shard'=4] {'shard'}, dimensions={0}, use_global_device_ids=true | all-gather | bytes 819200 | tf_op jit(solution)/shard_map/all_gather | solution.py:159
  119.9 13.1 %all_gather.60 = bf16[1024,320]{0,1:T(8,128)(2,1)S(1)} all-gather(bf16[256,320]{0,1:T(8,128)(2,1)S(1)} %copy-done.70), channel_id=1, replica_groups=mesh['rep'=8,'shard'=4] {'shard'}, dimensions={0}, use_global_device_ids=true | all-gather | bytes 819200 | tf_op jit(solution)/shard_map/all_gather | solution.py:160
  133.0 4.0 copy.27
  142.2 20.8 %while.74 = (s32[]{:T(128)}, bf16[5,3,256,64]{2,3,1,0:T(8,128)(2,1)S(1)}, f32[5,3,256,1]{2,1,3,0:T(4,128)S(1)}, pred[256,1024]{1,0:T(8,128)(4,1)S(1)}, bf16[5,3,...) while((s32[]{:T(128)}, ...), condition=%wide.region_7.8_spmd, body=%wide.region_4.7_spmd.sunk | while | flops 212335872 | bytes 10812505 | solution.py:191
  168.5 24.2 %while.75 = (s32[]{:T(128)}, bf16[5,3,256,64]{2,3,1,0:T(8,128)(2,1)S(1)}, f32[5,3,256,1]{2,1,3,0:T(4,128)}, pred[256,1024]{1,0:T(8,128)(4,1)S(1)}, bf16[5,3,256,...) while((s32[]{:T(128)}, ...), condition=%wide.region_16.17_spmd, body=%wide.region_13.16_spmd.sunk | while | flops 212335872 | bytes 10810965 | solution.py:191
  192.8 4.3 multiply_reduce_fusion.6
  197.3 5.6 fusion.278
  202.9 19.7 %all-gather.14.cloned.1.call-done = bf16[960,2560]{1,0:T(8,128)(2,1)} async-done(((bf16[240,2560]{1,0:T(8,128)(2,1)}), bf16[960,2560]{1,0:T(8,128)(2,1)}) %all-gather.14.cloned.1.call-update) | async-done | bytes 4915216 | tf_op jit(solution)/shard_map/all_gather | solution.py:109
  222.6 5.4 fusion.279
  228.0 55.0 %all-gather.16.cloned.1.call-done = bf16[2560,960]{0,1:T(8,128)(2,1)} async-done(((bf16[640,960]{0,1:T(8,128)(2,1)}), bf16[2560,960]{0,1:T(8,128)(2,1)}) %all-gather.16.cloned.1.call-update) | async-done | bytes 4915216 | tf_op jit(solution)/shard_map/all_gather | solution.py:110
  283.0 7.8 multiply_convert_fusion.4
  290.8 4.8 fusion.282
  300.7 3.8 multiply_convert_fusion.2
  315.2 79.8 %while.76 = (s32[]{:T(128)}, f32[5,3,256,64]{2,3,1,0:T(8,128)}, bf16[5,1024,64]{1,2,0:T(8,128)(2,1)}, bf16[5,1024,64]{1,2,0:T(8,128)(2,1)}, pred[256,1024]{1,0:T...) while((s32[]{:T(128)}, f32[5,3,256,64]{2,3,1,0:T(8,128)}, ...), condition=%wide.region_21.22_spmd, body=%wide.region_19.21_spmd.sunk | while | flops 515116544 | bytes 36386928 | solution.py:270
  320.5 4.4 fusion.417
  324.9 4.3 fusion.418
  336.4 4.4 fusion.417
  340.8 4.3 fusion.418
  352.4 4.4 fusion.417
  356.8 4.3 fusion.418
  368.4 4.4 fusion.417
  372.8 4.3 fusion.418
  384.4 4.4 fusion.417
  388.8 4.3 fusion.418
  395.1 3.3 convolution_convert_fusion
  401.2 82.7 %while.77 = (s32[]{:T(128)}, f32[5,3,256,64]{2,3,1,0:T(8,128)}, bf16[5,1024,64]{1,2,0:T(8,128)(2,1)}, bf16[5,1024,64]{1,2,0:T(8,128)(2,1)}, pred[256,1024]{1,0:T...) while((s32[]{:T(128)}, f32[5,3,256,64]{2,3,1,0:T(8,128)}, ...), condition=%wide.region_28.29_spmd, body=%wide.region_26.28_spmd.sunk | while | flops 515116544 | bytes 36386928 | solution.py:270
  403.9 3.2 fusion.430
  407.1 4.4 fusion.431
  411.5 4.3 fusion.432
  420.5 3.2 fusion.430
  423.7 4.4 fusion.431
  428.1 4.3 fusion.432
  437.0 3.2 fusion.430
  440.2 4.4 fusion.431
  444.6 4.3 fusion.432
  453.6 3.2 fusion.430
  456.7 4.4 fusion.431
  461.1 4.3 fusion.432
  470.1 3.2 fusion.430
  473.3 4.4 fusion.431
  477.7 4.3 fusion.432
  486.5 23.1 %reduce-scatter.18.cloned.1.call-done = bf16[256,320]{0,1:T(8,128)(2,1)} async-done(((bf16[1024,320]{0,1:T(8,128)(2,1)}), bf16[256,320]{0,1:T(8,128)(2,1)}) %reduce-scatter.18.cloned.1.call-update) | async-done | bytes 163856 | tf_op jit(solution)/shard_map/reduce_scatter | solution.py:281
  512.9 25.0 %reduce-scatter.16.cloned.1.call-done = bf16[256,320]{0,1:T(8,128)(2,1)} async-done(((bf16[1024,320]{0,1:T(8,128)(2,1)}), bf16[256,320]{0,1:T(8,128)(2,1)}) %reduce-scatter.16.cloned.1.call-update) | async-done | bytes 163856 | tf_op jit(solution)/shard_map/reduce_scatter | solution.py:284
  542.0 25.1 %reduce-scatter.20.cloned.1.call-done = bf16[256,320]{0,1:T(8,128)(2,1)} async-done(((bf16[1024,320]{0,1:T(8,128)(2,1)}), bf16[256,320]{0,1:T(8,128)(2,1)}) %reduce-scatter.20.cloned.1.call-update) | async-done | bytes 163856 | tf_op jit(solution)/shard_map/reduce_scatter | solution.py:284
  572.5 3.7 add_convert_fusion
  576.2 7.9 copy.34
  596.5 3.7 add_convert_fusion.1
  603.2 3.6 add_convert_fusion.2
  607.8 3.3 fusion.286
  614.0 4.1 fusion.177
  620.4 6.3 all-reduce.16.cloned.1.call-done
  630.1 61.0 %reduce-scatter.30.cloned.1.call-done = bf16[640,960]{1,0:T(8,128)(2,1)} async-done(((bf16[2560,960]{1,0:T(8,128)(2,1)}), bf16[640,960]{1,0:T(8,128)(2,1)}) %reduce-scatter.30.cloned.1.call-update) | async-done | bytes 1228816
  693.5 35.2 %reduce-scatter.24.cloned.1.call-done = bf16[240,960]{1,0:T(8,128)(2,1)} async-done(((bf16[960,960]{1,0:T(8,128)(2,1)}), bf16[240,960]{1,0:T(8,128)(2,1)}) %reduce-scatter.24.cloned.1.call-update) | async-done | bytes 460816 | tf_op jit(solution)/shard_map/reduce_scatter | solution.py:333
  728.7 37.8 %reduce-scatter.22.cloned.1.call-done = bf16[240,960]{1,0:T(8,128)(2,1)} async-done(((bf16[960,960]{1,0:T(8,128)(2,1)}), bf16[240,960]{1,0:T(8,128)(2,1)}) %reduce-scatter.22.cloned.1.call-update) | async-done | bytes 460816 | tf_op jit(solution)/shard_map/reduce_scatter | solution.py:333
  766.5 61.6 %reduce-scatter.28.cloned.1.call-done = bf16[240,2560]{1,0:T(8,128)(2,1)} async-done(((bf16[960,2560]{1,0:T(8,128)(2,1)}), bf16[240,2560]{1,0:T(8,128)(2,1)}) %reduce-scatter.28.cloned.1.call-update) | async-done | bytes 1228816 | tf_op jit(solution)/shard_map/reduce_scatter | solution.py:333
  828.1 61.6 %reduce-scatter.26.cloned.1.call-done = bf16[240,2560]{1,0:T(8,128)(2,1)} async-done(((bf16[960,2560]{1,0:T(8,128)(2,1)}), bf16[240,2560]{1,0:T(8,128)(2,1)}) %reduce-scatter.26.cloned.1.call-update) | async-done | bytes 1228816 | tf_op jit(solution)/shard_map/reduce_scatter | solution.py:333
  897.5 8.9 all-reduce.8
  906.6 15.6 %all-reduce.6 = (bf16[240]{0:T(256)(128)(2,1)S(1)}, bf16[240]{0:T(256)(128)(2,1)S(1)}) all-reduce(bf16[240]{0:T(256)(128)(2,1)S(1)} %dynamic-slice.7, bf16[240]{0:T(256)(128)(2,1)S(1)} %dynamic-slice.9), channel_id=1, replica_groups=mesh['rep'=8,'shard'=4] {'rep'}, use_global_device_ids=true, to_apply=%region_49.50 | all-reduce | flops 480 | bytes 1920 | tf_op jit(solution)/shard_map/psum | solution.py:336
  926.3 81.7 %all-reduce.14.cloned.1.call-done = (bf16[240,960]{1,0:T(8,128)(2,1)}, bf16[240,320]{0,1:T(8,128)(2,1)}, bf16[240,320]{0,1:T(8,128)(2,1)}, bf16[240,960]{1,0:T(8...) async-done(((bf16[240,960]{1,0:T(8,128)(2,1)}, bf16[240,320]{0,1:T(8,128)(2,1)}, bf16[240,320]{0,1:T(8,128)(2,1)}, ...) | async-done | bytes 4915216 | tf_op jit(solution)/shard_map/psum | solution.py:336
  (439 shorter events, 219.9 us)
Async XLA Ops:
  7.2 3.6 copy-start.78
  7.2 5.0 copy-start.80
  7.2 5.3 copy-start.81
  7.2 16.9 %copy-start.1 = (bf16[2,256,960]{1,2,0:T(8,128)(2,1)S(1)}, bf16[2,256,960]{1,2,0:T(8,128)(2,1)}, u32[]{:S(2)}) copy-start(bf16[2,256,960]{1,2,0:T(8,128)(2,1)} %param.24) | copy-start | bytes 2949124
  7.2 17.2 %copy-start.68 = (bf16[240,320]{0,1:T(8,128)(2,1)S(1)}, bf16[240,320]{0,1:T(8,128)(2,1)}, u32[]{:S(2)}) copy-start(bf16[240,320]{0,1:T(8,128)(2,1)} %param.27) | copy-start | bytes 460804
  7.2 125.7 %all-gather.8.cloned.1.call-start = ((), (), s32[]{:S(2)}) async-start(), calls=%async_computation.9 | async-start | bytes 2457600 | tf_op jit(solution)/shard_map/all_gather | solution.py:104
  8.0 155.1 %all-gather.10.cloned.1.call-start = ((), (), s32[]{:S(2)}) async-start(), calls=%async_computation.10 | async-start | bytes 2457600 | tf_op jit(solution)/shard_map/all_gather | solution.py:107
  8.7 188.6 %all-gather.12.cloned.1.call-start = ((), (), s32[]{:S(2)}) async-start(), calls=%async_computation.11 | async-start | bytes 6144000 | tf_op jit(solution)/shard_map/all_gather | solution.py:108
  9.5 213.1 %all-gather.14.cloned.1.call-start = ((), (), s32[]{:S(2)}) async-start(), calls=%async_computation.12 | async-start | bytes 6144000 | tf_op jit(solution)/shard_map/all_gather | solution.py:109
  10.0 25.9 %copy-start.69 = (bf16[240,320]{0,1:T(8,128)(2,1)S(1)}, bf16[240,320]{0,1:T(8,128)(2,1)}, u32[]{:S(2)}) copy-start(bf16[240,320]{0,1:T(8,128)(2,1)} %param.28) | copy-start | bytes 460804
  10.0 272.9 %all-gather.16.cloned.1.call-start = ((), (), s32[]{:S(2)}) async-start(), calls=%async_computation.13 | async-start | bytes 6144000 | tf_op jit(solution)/shard_map/all_gather | solution.py:110
  10.6 474.9 %reduce-scatter.14.cloned.1.call-start = ((), (), s32[]{:S(2)}) async-start(), calls=%async_computation.14 | async-start | bytes 819200 | tf_op jit(solution)/shard_map/reduce_scatter | solution.py:281
  10.7 41.8 %copy-start.61 = (f32[8,8]{1,0:T(8,128)}, f32[8,8]{1,0:T(8,128)S(1)}, u32[]{:S(2)}) copy-start(f32[8,8]{1,0:T(8,128)S(1)} %fusion.257) | copy-start | bytes 772
  10.8 53.3 %copy-start.18 = (bf16[5,3,256,64]{2,3,1,0:T(8,128)(2,1)}, bf16[5,3,256,64]{2,3,1,0:T(8,128)(2,1)S(1)}, u32[]{:S(2)}) copy-start(bf16[5,3,256,64]{2,3,1,0:T(8,128)(2,1)S(1)} %fusion.276) | copy-start | bytes 1474564
  24.1 115.3 %copy-start.65 = (f32[960]{0:T(1024)}, f32[960]{0:T(1024)S(1)}, u32[]{:S(2)}) copy-start(f32[960]{0:T(1024)S(1)} %convert_element_type.363) | copy-start | bytes 11524
  24.4 112.6 %copy-start.73 = (f32[256]{0:T(256)}, f32[256]{0:T(256)S(1)}, u32[]{:S(2)}) copy-start(f32[256]{0:T(256)S(1)} %add_rsqrt_fusion.3) | copy-start | bytes 3076
  35.9 20.7 %copy-start.15 = (bf16[960,320]{0,1:T(8,128)(2,1)}, bf16[960,320]{0,1:T(8,128)(2,1)S(1)}, u32[]{:S(2)}) copy-start(bf16[960,320]{0,1:T(8,128)(2,1)S(1)} %reshape.468) | copy-start | bytes 1843204
  56.6 4.1 copy-start.62
  56.7 82.8 %copy-start.75 = (f32[256]{0:T(256)}, f32[256]{0:T(256)S(1)}, u32[]{:S(2)}) copy-start(f32[256]{0:T(256)S(1)} %add_rsqrt_fusion.1) | copy-start | bytes 3076
  57.1 6.9 copy-start.64
  64.0 77.3 %copy-start.53 = (f32[256,32]{0,1:T(8,128)}, f32[256,32]{0,1:T(8,128)S(1)}, u32[]{:S(2)}) copy-start(f32[256,32]{0,1:T(8,128)S(1)} %get-tuple-element.411) | copy-start | bytes 98308
  64.0 77.2 %copy-start.55 = (f32[256,32]{0,1:T(8,128)}, f32[256,32]{0,1:T(8,128)S(1)}, u32[]{:S(2)}) copy-start(f32[256,32]{0,1:T(8,128)S(1)} %get-tuple-element.412) | copy-start | bytes 98308
  64.0 446.5 %copy-start.57 = (f32[256,32]{0,1:T(8,128)}, f32[256,32]{0,1:T(8,128)S(1)}, u32[]{:S(2)}) copy-start(f32[256,32]{0,1:T(8,128)S(1)} %get-tuple-element.420) | copy-start | bytes 98308
  97.9 22.0 %copy-start.70 = (bf16[256,320]{0,1:T(8,128)(2,1)S(1)}, bf16[256,320]{0,1:T(8,128)(2,1)}, u32[]{:S(2)}) copy-start(bf16[256,320]{0,1:T(8,128)(2,1)} %convolution_convert_fusion.2) | copy-start | bytes 491524
  163.1 3.7 copy-start.51
  164.1 4.4 copy-start.19
  166.8 141.6 %copy-start.11 = (f32[256,960]{0,1:T(8,128)}, f32[256,960]{0,1:T(8,128)S(1)}, u32[]{:S(2)}) copy-start(f32[256,960]{0,1:T(8,128)S(1)} %get-tuple-element.422) | copy-start | bytes 2949124
  192.8 10.1 copy-start.30
  192.8 35.2 %copy-start.20 = (bf16[5,3,256,64]{2,3,1,0:T(8,128)(2,1)}, bf16[5,3,256,64]{2,3,1,0:T(8,128)(2,1)S(1)}, u32[]{:S(2)}) copy-start(bf16[5,3,256,64]{2,3,1,0:T(8,128)(2,1)S(1)} %get-tuple-element.242) | copy-start | bytes 1474564
  197.2 25.3 %copy-start.3 = (bf16[256,960]{0,1:T(8,128)(2,1)}, bf16[256,960]{0,1:T(8,128)(2,1)S(1)}, u32[]{:S(2)}) copy-start(bf16[256,960]{0,1:T(8,128)(2,1)S(1)} %multiply_convert_fusion.9) | copy-start | bytes 1474564
  290.8 4.9 copy-start.48
  290.8 4.9 copy-start.17
  290.8 4.9 copy-start
  290.8 5.1 copy-start.28
  395.0 114.5 %reduce-scatter.18.cloned.1.call-start = ((), (), s32[]{:S(2)}) async-start(), calls=%async_computation.16 | async-start | bytes 819200 | tf_op jit(solution)/shard_map/reduce_scatter | solution.py:281
  401.2 109.3 %copy-start.54 = (f32[256,32]{0,1:T(8,128)S(1)}, f32[256,32]{0,1:T(8,128)}, u32[]{:S(2)}) copy-start(f32[256,32]{0,1:T(8,128)} %copy-done.53) | copy-start | bytes 98308
  401.2 109.3 %copy-start.56 = (f32[256,32]{0,1:T(8,128)S(1)}, f32[256,32]{0,1:T(8,128)}, u32[]{:S(2)}) copy-start(f32[256,32]{0,1:T(8,128)} %copy-done.55) | copy-start | bytes 98308
  483.9 27.4 %copy-start.2 = (bf16[2,256,960]{1,2,0:T(8,128)(2,1)S(1)}, bf16[2,256,960]{1,2,0:T(8,128)(2,1)}, u32[]{:S(2)}) copy-start(bf16[2,256,960]{1,2,0:T(8,128)(2,1)} %param.24) | copy-start | bytes 2949124
  483.9 27.4 %copy-start.66 = (f32[960]{0:T(1024)S(1)}, f32[960]{0:T(1024)}, u32[]{:S(2)}) copy-start(f32[960]{0:T(1024)} %copy-done.65) | copy-start | bytes 11524
  483.9 27.4 %copy-start.74 = (f32[256]{0:T(256)S(1)}, f32[256]{0:T(256)}, u32[]{:S(2)}) copy-start(f32[256]{0:T(256)} %copy-done.73) | copy-start | bytes 3076
  484.0 53.9 %reduce-scatter.16.cloned.1.call-start = ((), (), s32[]{:S(2)}) async-start(), calls=%async_computation.15 | async-start | bytes 819200 | tf_op jit(solution)/shard_map/reduce_scatter | solution.py:284
  484.7 82.3 %reduce-scatter.20.cloned.1.call-start = ((), (), s32[]{:S(2)}) async-start(), calls=%async_computation.17 | async-start | bytes 819200 | tf_op jit(solution)/shard_map/reduce_scatter | solution.py:284
  485.4 141.2 %all-reduce.16.cloned.1.call-start = ((), (), s32[]{:S(2)}) async-start(), calls=%async_computation.24 | async-start | bytes 2621440
  486.5 52.8 %copy-start.76 = (f32[256]{0:T(256)S(1)}, f32[256]{0:T(256)}, u32[]{:S(2)}) copy-start(f32[256]{0:T(256)} %copy-done.75) | copy-start | bytes 3076
  510.7 31.3 %copy-start.39 = (bf16[256,5,64]{0,2,1:T(8,128)(2,1)}, bf16[256,5,64]{0,2,1:T(8,128)(2,1)S(1)}, u32[]{:S(2)}) copy-start(bf16[256,5,64]{0,2,1:T(8,128)(2,1)S(1)} %maximum_convert_fusion.3) | copy-start | bytes 491524
  539.3 30.3 %copy-start.25 = (bf16[2,256,960]{1,2,0:T(8,128)(2,1)S(1)}, bf16[2,256,960]{1,2,0:T(8,128)(2,1)}, u32[]{:S(2)}) copy-start(bf16[2,256,960]{1,2,0:T(8,128)(2,1)} %param.35) | copy-start | bytes 2949124
  569.3 121.8 %reduce-scatter.30.cloned.1.call-start = ((), (), s32[]{:S(2)}) async-start(), calls=%async_computation.22 | async-start | bytes 6553600
  584.1 144.6 %reduce-scatter.24.cloned.1.call-start = ((), (), s32[]{:S(2)}) async-start(), calls=%async_computation.19 | async-start | bytes 2457600 | tf_op jit(solution)/shard_map/reduce_scatter | solution.py:333
  589.1 177.4 %reduce-scatter.22.cloned.1.call-start = ((), (), s32[]{:S(2)}) async-start(), calls=%async_computation.18 | async-start | bytes 2457600 | tf_op jit(solution)/shard_map/reduce_scatter | solution.py:333
  593.6 234.6 %reduce-scatter.28.cloned.1.call-start = ((), (), s32[]{:S(2)}) async-start(), calls=%async_computation.21 | async-start | bytes 6144000 | tf_op jit(solution)/shard_map/reduce_scatter | solution.py:333
  600.2 289.5 %reduce-scatter.26.cloned.1.call-start = ((), (), s32[]{:S(2)}) async-start(), calls=%async_computation.20 | async-start | bytes 6144000 | tf_op jit(solution)/shard_map/reduce_scatter | solution.py:333
  606.8 401.2 %all-reduce.14.cloned.1.call-start = ((), (), s32[]{:S(2)}) async-start(), calls=%async_computation.23 | async-start | bytes 9994240 | tf_op jit(solution)/shard_map/psum | solution.py:336
  607.8 3.4 copy-start.34
  607.8 10.3 %slice-start.4 = ((s8[4915200]{0:T(1024)(128)(4,1)}), s8[4194304]{0:T(1024)(128)(4,1)S(1)}, s32[]{:S(2)}) async-start(s8[4915200]{0:T(1024)(128)(4,1)} %bitcast.499), calls=%async_computation.29 | async-start | bytes 8388608
  611.1 6.9 slice-start.5
  614.0 4.1 copy-start.29
  614.0 4.2 copy-start.42
  889.8 4.0 copy-start.40
  889.8 4.0 copy-start.52
  894.3 28.9 %copy-start.10 = (f32[256,960]{0,1:T(8,128)S(1)}, f32[256,960]{0,1:T(8,128)}, u32[]{:S(2)}) copy-start(f32[256,960]{0,1:T(8,128)} %copy-done.8) | copy-start | bytes 2949124
  1008.0 4.9 copy-start.49
  1011.2 3.3 copy-start.60
  1012.9 3.7 copy-start.72
  1012.9 4.5 copy-start.71
  (40 other events, 87.7 us)
Sparse Core Ops, SparseCore 0:
  9.9 43.0 all-gather.7
  54.8 40.8 all-gather.9
  97.6 64.4 all-gather.11
  163.8 58.6 all-gather.13
  224.2 58.6 all-gather.15
  395.2 25.3 reduce-scatter.13
  484.1 25.4 reduce-scatter.17
  512.4 25.3 reduce-scatter.15
  541.6 25.4 reduce-scatter.19
  570.0 56.6 all-reduce.15
  629.7 61.4 reduce-scatter.29
  694.6 34.0 reduce-scatter.23
  732.4 34.0 reduce-scatter.21
  769.4 58.7 reduce-scatter.27
  831.0 58.7 reduce-scatter.25
  893.2 114.7 all-reduce.13
where the time goes:
time: 1030 us
  waiting for transfers between devices  498 us (48%)
  matrix products  302 us (29%)
  blocking collectives  129 us (13%)
  other arithmetic  39.7 us (4%)
  local copies, waits for them, and re-layouts  37.4 us (4%)
  between operations  17 us (2%)
    reduce_scatter x4, waiting for transfers between devices, local(): lax.psum_scatter(shortened(full_sums), 'shard', scatter_dimension=0, tile...  196 us
    psum x1, waiting for transfers between devices, local(): lax.psum(shortened(owned_final), 'rep')  81.7 us
    unnamed x18, waiting for transfers between devices  71.9 us
    all_gather x1, waiting for transfers between devices, local(): lax.all_gather(w_down, 'shard', axis=0, tiled=True)  55 us
    reduce_scatter x2, waiting for transfers between devices, local(): lax.psum_scatter(value_tree_grad.astype(jnp.bfloat16), 'shard', scatter_d...  50.1 us
    dot_general x10, matrix products, head_backward(): jnp.einsum('gtn,nd->gtd', d_scores, key_part, preferred_element_type=jnp....  44 us
    dot_general x10, matrix products, head_backward(): jnp.einsum('gtn,gtd->nd', d_scores, query_part, preferred_element_type=jn...  43.3 us
    all_gather x2, blocking collectives, local(): lax.all_gather(key_rotated, 'shard', axis=0, tiled=True)  35.5 us
  transfers between devices with their start and end apart: 16, of which 12 were waited for; matrix products, arithmetic and copies ran while one was open for 24% of the time, Pallas kernels for 0%

commit v1 on v0

v1 whole, which is shorter than its diff:
```python
import math

import jax
import jax.numpy as jnp
from jax import lax
from jax.sharding import PartitionSpec as P

QUERY_HEADS = 15
KEY_VALUE_HEADS = 5
HEAD_SIZE = 64
GROUP = QUERY_HEADS // KEY_VALUE_HEADS
EPS = 1e-05
AXES = ("rep", "shard")
BF = jnp.bfloat16
F32 = jnp.float32


def rms_inverse(x):
    return lax.rsqrt(jnp.mean(x * x, axis=-1, keepdims=True) + EPS)


def dot(a, b, dims):
    return lax.dot_general(a, b, (dims, ((), ())), preferred_element_type=F32)


def nn(a, b):
    return dot(a, b, ((1,), (0,)))


def nt(a, b):
    return dot(a, b, ((1,), (1,)))


def tn(a, b):
    return dot(a, b, ((0,), (0,)))


class Links:
    def __init__(self, reps, shards):
        self.reps, self.shards = reps, shards
        self.core = lax.axis_index("rep") % 2
        self.shard = lax.axis_index("shard")
        self.bits = shards.bit_length() - 1
        even = [1 << i for i in range(self.bits)]
        odd = even[:2][::-1] + even[2:]
        self.steps = list(zip(even, odd))
        self.hops = []
        for piece in range(shards):
            sums = [0, 0]
            for i, step in enumerate(self.steps):
                if piece >> i & 1:
                    sums = [sums[0] ^ step[0], sums[1] ^ step[1]]
            self.hops.append(jnp.where(self.core == 0, sums[0], sums[1]))

    def move(self, value, target):
        pairs = []
        for r in range(self.reps):
            for s in range(self.shards):
                goal = target(r, s)
                if goal is not None:
                    pairs.append((r * self.shards + s, goal[0] * self.shards + goal[1]))
        return lax.ppermute(value, AXES, pairs)

    def step(self, value, i):
        return self.move(value, lambda r, s: (r, s ^ self.steps[i][r % 2]))

    def swap(self, value):
        return self.move(value, lambda r, s: (r ^ 1, s))

    def chain(self, value):
        chips = self.reps // 2
        place = lax.axis_index("rep") // 2
        span = 1
        if chips % 4 == 0:
            inward, outward, middle = {0: 1, 3: 2}, {1: 0, 2: 3}, {1: 2, 2: 1}

            def along(value, table):
                def target(r, s):
                    chip = r // 2
                    if chip % 4 not in table:
                        return None
                    return ((chip - chip % 4 + table[chip % 4]) * 2 + r % 2, s)

                return self.move(value, target)

            value = add(value, along(value, inward))
            value = add(value, along(value, middle))
            back = along(value, outward)
            inner = (place % 4 == 1) | (place % 4 == 2)
            value = jnp.where(inner, value, back)
            span = 4
        while span < chips:
            value = add(value, self.move(value, lambda r, s: (r ^ (2 * span), s)))
            span *= 2
        return value

    def spread(self, value):
        pieces = [value]
        for i in range(self.bits):
            pieces = pieces + [self.step(piece, i) for piece in pieces]
        return pieces

    def collect(self, pieces):
        for i in reversed(range(self.bits)):
            keep = 1 << i
            pieces = [add(pieces[t], self.step(pieces[t + keep], i)) for t in range(keep)]
        return pieces[0]

    def half_rows(self, rows):
        return -(-rows // 16) * 8

    def gather(self, shard_value):
        rows, cols = shard_value.shape
        half = self.half_rows(rows)
        first = self.core * (rows - half)
        second = (1 - self.core) * (rows - half)
        mine = lax.dynamic_slice_in_dim(shard_value, first, half, 0)
        pieces = self.spread(mine)[1:]
        others = [self.swap(piece) for piece in pieces]
        whole = jnp.zeros((rows * self.shards, cols), shard_value.dtype)
        whole = lax.dynamic_update_slice(whole, shard_value, (self.shard * rows, 0))
        for piece, other, hop in zip(pieces, others, self.hops[1:]):
            whole = lax.dynamic_update_slice(whole, piece, ((self.shard ^ hop) * rows + first, 0))
        for t, other in enumerate(others, 1):
            hop = self.hops[self.twin(t)]
            whole = lax.dynamic_update_slice(whole, other, ((self.shard ^ hop) * rows + second, 0))
        return whole

    def twin(self, piece):
        return piece if self.bits < 2 else piece >> 2 << 2 | (piece & 1) << 1 | (piece >> 1 & 1)

    def gather_small(self, value):
        pieces = jnp.stack(
            [value if hop == 0 else self.move(value, lambda r, s, hop=hop: (r, s ^ hop))
                for hop in range(self.shards)
            ]
        )
        order = self.shard ^ jnp.arange(self.shards)
        hit = (order[:, None] == jnp.arange(self.shards)[None, :])[:, :, None, None]
        pieces = jnp.sum(jnp.where(hit, pieces[None], 0), axis=1, dtype=value.dtype)
        return jnp.concatenate([pieces[j] for j in range(self.shards)], axis=-1)

    def reduce_weight(self, grad):
        rows = grad.shape[0] // self.shards
        half = self.half_rows(rows)
        first = self.core * (rows - half)
        second = (1 - self.core) * (rows - half)
        parts = grad.astype(BF).reshape(self.shards, rows, grad.shape[1])
        kept = lax.dynamic_slice_in_dim(parts, first, half, 1)
        given = lax.dynamic_slice_in_dim(parts, second, half, 1)
        summed = add(kept, self.swap(given))
        owned = self.collect(
            [lax.dynamic_index_in_dim(summed, self.shard ^ hop, 0, keepdims=False) for hop in self.hops]
        )
        owned = self.chain(owned)
        other = self.swap(owned)
        low = jnp.where(self.core == 0, owned, other)
        high = jnp.where(self.core == 0, other, owned)
        return jnp.concatenate([low[: rows - half], high], axis=0).astype(F32)

    def reduce_small(self, value):
        summed = add(value, self.swap(value))
        for i in range(self.bits):
            summed = add(summed, self.step(summed, i))
        summed = self.chain(summed)
        width = value.shape[1] // self.shards
        return lax.dynamic_slice_in_dim(summed, self.shard * width, width, 1)


def add(left, right):
    return (left.astype(F32) + right.astype(F32)).astype(left.dtype)


def rotate(vectors, cosine, sine, heads, inverse):
    shaped = vectors.reshape(vectors.shape[0], heads, HEAD_SIZE)
    first = shaped[..., : HEAD_SIZE // 2]
    second = shaped[..., HEAD_SIZE // 2 :]
    cosine, sine = cosine[:, None, :], sine[:, None, :]
    if inverse:
        sine = -sine
    turned = jnp.concatenate(
        [first * cosine - second * sine, second * cosine + first * sine], axis=-1
    )
    return turned.reshape(vectors.shape[0], heads * HEAD_SIZE)


def local(
    block_input,
    parent_ids,
    w_query,
    key_weight,
    value_weight,
    w_output,
    w_gate,
    w_up,
    w_down,
    norm_first,
    norm_second,
    out_cotangent,
):
    micro, rows, width = block_input.shape
    shards = lax.axis_size("shard")
    links = Links(lax.axis_size("rep"), shards)
    tree = rows * shards
    segs = parent_ids.shape[2]
    seg_rows = tree // segs
    kv_width = KEY_VALUE_HEADS * HEAD_SIZE
    scale = HEAD_SIZE ** (-0.5)
    tokens = micro * rows

    gains = links.gather_small(jnp.stack([norm_first, norm_second])).astype(F32)
    gain_one, gain_two = gains[0:1], gains[1:2]
    full_qkv = links.gather(jnp.concatenate([w_query, key_weight, value_weight], axis=1))
    full_output = links.gather(w_output)
    full_gate = links.gather(w_gate)
    full_upper = links.gather(w_up)
    full_down = links.gather(w_down)

    parents = parent_ids[:, 0]
    seg = jnp.arange(segs)
    after = jnp.concatenate([parents[:, 1:], jnp.full((micro, 1), -1, parents.dtype)], axis=1)
    on_path = (seg % 2 == 0)[None] | (after == seg[None])
    depth = jnp.sum(jnp.where((seg[None, :] < seg[:, None])[None], on_path.astype(F32)[:, None, :], 0.0), axis=-1)

    def row_numbers(hop):
        return (links.shard ^ hop) * rows + jnp.arange(rows)

    def pick(table, numbers):
        hit = (numbers // seg_rows)[:, None] == seg[None]
        return jnp.sum(jnp.where(hit[None], table[:, None, :], 0), axis=-1)

    my_rows = row_numbers(0)
    positions = pick(depth, my_rows) * seg_rows + (my_rows % seg_rows).astype(F32)
    freqs = jnp.exp(-math.log(10000.0) * jnp.arange(HEAD_SIZE // 2, dtype=F32) * (2.0 / HEAD_SIZE))
    angles = positions.reshape(tokens)[:, None] * freqs[None, :]
    cosine, sine = jnp.cos(angles), jnp.sin(angles)
    key_rows = jnp.concatenate([row_numbers(hop) for hop in links.hops])
    key_on_path = pick(on_path.astype(F32), key_rows) > 0.5
    key_seg, my_seg = key_rows // seg_rows, my_rows // seg_rows
    allowed = ((key_seg[None, :] < my_seg[:, None])[None] & key_on_path[:, None, :]) | (
        (key_seg[None, :] == my_seg[:, None]) & (key_rows[None, :] <= my_rows[:, None])
    )[None]

    inputs = block_input.reshape(tokens, width).astype(F32)
    cotangent = out_cotangent.reshape(tokens, width)
    inv_first = rms_inverse(inputs)
    normed_first = inputs * inv_first
    act_first = (normed_first * gain_one).astype(BF)
    linear = nn(act_first, full_qkv)
    queries = rotate(linear[:, :width], cosine, sine, QUERY_HEADS, False).astype(BF)
    keys = rotate(linear[:, width : width + kv_width], cosine, sine, KEY_VALUE_HEADS, False)
    kv = jnp.concatenate([keys, linear[:, width + kv_width :]], axis=1).astype(BF)
    kv_all = jnp.concatenate(
        [piece.reshape(micro, rows, 2 * kv_width) for piece in links.spread(kv)], axis=1
    )

    def by_head(value, length):
        return value.reshape(micro, length, KEY_VALUE_HEADS, -1, HEAD_SIZE).transpose(0, 2, 3, 1, 4)

    query_heads = by_head(queries, rows)
    key_heads = by_head(kv_all[:, :, :kv_width], tree)[:, :, 0]
    value_heads = by_head(kv_all[:, :, kv_width:], tree)[:, :, 0]

    def forward(allowed, operands):
        query_part, key_part, value_part = operands
        raw = jnp.einsum("gtd,nd->gtn", query_part, key_part, preferred_element_type=F32) * scale
        masked = jnp.where(allowed[None], raw, -1e30)
        peak = jnp.max(masked, axis=-1, keepdims=True)
        expo = jnp.where(allowed[None], jnp.exp(masked - peak), 0.0)
        total = jnp.sum(expo, axis=-1, keepdims=True)
        mixed = jnp.einsum(
            "gtn,nd->gtd", (expo / total).astype(BF), value_part, preferred_element_type=F32
        )
        return mixed, peak + jnp.log(total)

    mixed, log_totals = [], []
    for m in range(micro):
        out, logs = lax.map(
            lambda ops, m=m: forward(allowed[m], ops), (query_heads[m], key_heads[m], value_heads[m])
        )
        mixed.append(out.transpose(2, 0, 1, 3).reshape(rows, width))
        log_totals.append(logs)
    attn = jnp.concatenate(mixed, axis=0).astype(BF)
    resid = inputs + nn(attn, full_output)
    inv_second = rms_inverse(resid)
    normed_second = resid * inv_second
    act_second = (normed_second * gain_two).astype(BF)
    gate = nn(act_second, full_gate)
    upper = nn(act_second, full_upper)
    sigmoid = jax.nn.sigmoid(gate)
    silu = gate * sigmoid
    inner = (silu * upper).astype(BF)
    block_out = (resid + nn(inner, full_down)).astype(BF)

    grad_down = links.reduce_weight(tn(inner, cotangent))
    d_inner = nt(cotangent, full_down)
    d_gate = (d_inner * upper * sigmoid * (1.0 + gate * (1.0 - sigmoid))).astype(BF)
    d_upper = (d_inner * silu).astype(BF)
    grad_gate = links.reduce_weight(tn(act_second, d_gate))
    grad_upper = links.reduce_weight(tn(act_second, d_upper))
    d_act_second = nt(d_gate, full_gate) + nt(d_upper, full_upper)
    gain_two_sum = jnp.sum(d_act_second * normed_second, axis=0)
    d_normed = d_act_second * gain_two
    d_resid = cotangent.astype(F32) + inv_second * (
        d_normed - normed_second * jnp.mean(d_normed * normed_second, axis=-1, keepdims=True)
    )
    d_resid_low = d_resid.astype(BF)
    grad_output = links.reduce_weight(tn(attn, d_resid_low))
    d_attn = nt(d_resid_low, full_output).astype(BF)
    d_attn_heads = by_head(d_attn, rows)

    def backward(allowed, operands):
        query_part, key_part, value_part, d_out, logs = operands
        raw = jnp.einsum("gtd,nd->gtn", query_part, key_part, preferred_element_type=F32) * scale
        probs = jnp.exp(jnp.where(allowed[None], raw, -1e30) - logs)
        d_probs = jnp.einsum("gtd,nd->gtn", d_out, value_part, preferred_element_type=F32)
        centre = jnp.sum(probs * d_probs, axis=-1, keepdims=True)
        d_scores = (probs * (d_probs - centre) * scale).astype(BF)
        d_query = jnp.einsum("gtn,nd->gtd", d_scores, key_part, preferred_element_type=F32)
        d_key = jnp.einsum("gtn,gtd->nd", d_scores, query_part, preferred_element_type=F32)
        d_value = jnp.einsum("gtn,gtd->nd", probs.astype(BF), d_out, preferred_element_type=F32)
        return d_query, d_key, d_value

    d_queries, d_kv = [], []
    for m in range(micro):
        d_query, d_key, d_value = lax.map(
            lambda ops, m=m: backward(allowed[m], ops),
            (query_heads[m], key_heads[m], value_heads[m], d_attn_heads[m], log_totals[m]),
        )
        d_queries.append(d_query.transpose(2, 0, 1, 3).reshape(rows, width))
        flat = [part.transpose(1, 0, 2).reshape(tree, kv_width) for part in (d_key, d_value)]
        d_kv.append(jnp.concatenate(flat, axis=1).astype(BF).reshape(shards, rows, 2 * kv_width))
    d_kv = jnp.stack(d_kv, axis=1).reshape(shards, tokens, 2 * kv_width)
    d_kv_sum = links.collect(list(d_kv)).astype(F32)
    d_query_low = rotate(jnp.concatenate(d_queries, axis=0), cosine, sine, QUERY_HEADS, True).astype(BF)
    d_key_low = rotate(d_kv_sum[:, :kv_width], cosine, sine, KEY_VALUE_HEADS, True).astype(BF)
    d_low = jnp.concatenate([d_query_low, d_key_low, d_kv_sum[:, kv_width:].astype(BF)], axis=1)
    grad_qkv = links.reduce_weight(tn(act_first, d_low))
    d_act_first = nt(d_low, full_qkv)
    gain_one_sum = jnp.sum(d_act_first * normed_first, axis=0)
    d_normed = d_act_first * gain_one
    d_input = d_resid + inv_first * (
        d_normed - normed_first * jnp.mean(d_normed * normed_first, axis=-1, keepdims=True)
    )
    gain_sums = links.reduce_small(jnp.stack([gain_one_sum, gain_two_sum]))
    return (
        block_out.reshape(micro, rows, width),
        d_input.astype(BF).reshape(micro, rows, width),
        grad_qkv[:, :width],
        grad_qkv[:, width : width + kv_width],
        grad_qkv[:, width + kv_width :],
        grad_output,
        grad_gate,
        grad_upper,
        grad_down,
        gain_sums[0],
        gain_sums[1],
    )


def solution(mesh):
    rows = P(None, AXES, None)
    weight, gain = P("shard", None), P("shard")
    return jax.shard_map(
        local,
        mesh=mesh,
        in_specs=(rows, P(None, "rep", None)) + (weight,) * 7 + (gain, gain, rows),
        out_specs=(rows, rows) + (weight,) * 7 + (gain, gain),
        check_vma=False,
    )
```

time: 1030 us -> 775 us (0.75)
  waiting for transfers between devices: 498 us -> 189 us
  local copies, waits for them, and re-layouts: 37.4 us -> 169 us
  blocking collectives: 129 us -> 0 us
  starting transfers between devices: 1.1 us -> 72.4 us
  matrix products: 302 us -> 266 us
  other arithmetic: 39.7 us -> 62.8 us
  between operations: 17 us -> 2.88 us
    reduce_scatter x8 -> x0, waiting for transfers between devices: 269 us -> none  [the longest x4 196 us: local(): lax.psum_scatter(shortened(full_sums), 'shard', scatter_dimension=0, tile...]
    ppermute x0 -> x85, waiting for transfers between devices: none -> 189 us  [move(): return lax.ppermute(value, AXES, pairs)]
    all_gather x6 -> x0, blocking collectives: 93.4 us -> none  [the longest x2 35.5 us: local(): lax.all_gather(key_rotated, 'shard', axis=0, tiled=True)]
    psum x1 -> x0, waiting for transfers between devices: 81.7 us -> none  [local(): lax.psum(shortened(owned_final), 'rep')]
    all_gather x5 -> x0, waiting for transfers between devices: 74.7 us -> none  [the longest x1 55 us: local(): lax.all_gather(w_down, 'shard', axis=0, tiled=True)]
    ppermute x0 -> x85, starting transfers between devices: none -> 72.4 us  [move(): return lax.ppermute(value, AXES, pairs)]
    unnamed x18 -> x0, waiting for transfers between devices: 71.9 us -> none
    dynamic_update_slice x0 -> x35, local copies, waits for them, and re-layouts: none -> 41.4 us  [the longest x15 20.3 us: gather(): lax.dynamic_update_slice(whole, piece, ((self.shard ^ hop) * rows + first...]
  transfers between devices with their start and end apart: 16 -> 85, of which waited for: 12 -> 25; matrix products, arithmetic and copies ran while one was open for 24% -> 22% of each run, Pallas kernels for 0% -> 0%
where the time goes in v1:
time: 775 us; the launch traced here: 763 us
  matrix products  266 us (34%)
  waiting for transfers between devices  189 us (24%)
  local copies, waits for them, and re-layouts  169 us (22%)
  starting transfers between devices  72.4 us (9%)
  other arithmetic  62.8 us (8%)
    ppermute x85, waiting for transfers between devices, move(): return lax.ppermute(value, AXES, pairs)  189 us
    ppermute x85, starting transfers between devices, move(): return lax.ppermute(value, AXES, pairs)  72.4 us
    dot_general x15, matrix products, dot(): return lax.dot_general(a, b, (dims, ((), ())), preferred_element_type=F32)  69.5 us
    dot_general x10, matrix products, backward(): jnp.einsum('gtn,nd->gtd', d_scores, key_part, preferred_element_type=F32)  43.9 us
    dot_general x10, matrix products, backward(): jnp.einsum('gtn,gtd->nd', d_scores, query_part, preferred_element_type=F32)  43.3 us
    dot_general x10, matrix products, backward(): jnp.einsum('gtd,nd->gtn', d_out, value_part, preferred_element_type=F32)  31.9 us
    dot_general x10, matrix products, forward(): jnp.einsum('gtn,nd->gtd', (expo / total).astype(BF), value_part, preferre...  21.4 us
    dynamic_update_slice x15, local copies, waits for them, and re-layouts, gather(): lax.dynamic_update_slice(whole, piece, ((self.shard ^ hop) * rows + first...  20.3 us
  transfers between devices with their start and end apart: 85, of which 25 were waited for; matrix products, arithmetic and copies ran while one was open for 22% of the time, Pallas kernels for 0%

profile of v1, /device:TPU:0, one launch (start us, length us, event | category | flops | bytes accessed | tf_op | source)
XLA Modules:
  0.0 762.7 jit_solution(6806867584313558885)
XLA Ops:
  46.4 3.7 collective-permute-done.12
  59.3 13.4 %collective-permute-done.14 = bf16[120,960]{1,0:T(8,128)(2,1)S(1)} collective-permute-done((bf16[120,960]{1,0:T(8,128)(2,1)S(1)}, bf16[120,960]{1,0:T(8,128)(2,1)S(1)}, u32[]{:S(2)}, u32[]{:S(2)}) %collective-permute-start.14) | collective-permute-done | bytes 230432 | tf_op jit(solution)/shard_map/ppermute | solution.py:62
  80.9 10.6 %collective-permute-done.24 = bf16[120,2560]{1,0:T(8,128)(2,1)S(1)} collective-permute-done((bf16[120,2560]{1,0:T(8,128)(2,1)S(1)}, bf16[120,2560]{1,0:T(8,128)(2,1)S(1)}, u32[]{:S(2)}, u32[]{:S(2)}) %collective-permute-start.24) | collective-permute-done | bytes 614432 | tf_op jit(solution)/shard_map/ppermute | solution.py:62
  92.4 4.8 collective-permute-done.25
  143.7 6.8 collective-permute-done.9
  164.1 7.2 fusion.187
  174.0 6.9 pad_maximum_fusion
  185.7 30.4 %while.52 = (s32[]{:T(128)}, bf16[5,3,256,64]{2,3,1,0:T(8,128)(2,1)S(1)}, f32[5,3,256,1]{2,1,3,0:T(4,128)S(1)}, pred[2,256,1024]{2,1,0:T(8,128)(4,1)}, bf16[5,3,...) while((s32[]{:T(128)}, ...), condition=%wide.region_8.9_spmd, body=%wide.region_5.8_spmd.sunk | while | flops 212335872 | bytes 11336793 | solution.py:278
  216.9 34.1 %while.53 = (s32[]{:T(128)}, bf16[5,3,256,64]{2,3,1,0:T(8,128)(2,1)}, f32[5,3,256,1]{2,1,3,0:T(4,128)S(1)}, pred[2,256,1024]{2,1,0:T(8,128)(4,1)}, bf16[5,3,256,...) while((s32[]{:T(128)}, ...), condition=%wide.region_12.13_spmd, body=%wide.region_9.12_spmd.sunk | while | flops 212335872 | bytes 15269009 | solution.py:278
  254.4 5.7 fusion.186
  260.2 8.7 %fusion.148 = (bf16[512,2560]{1,0:T(8,128)(2,1)S(1)}, bf16[512,2560]{1,0:T(8,128)(2,1)S(1)}, bf16[512,2560]{1,0:T(8,128)(2,1)}) fusion(f32[2560,512]{0,1:T(8,128)S(1)} %bitcast.492, f32[512,2560]{1,0:T(8,128)S(1)} %fusion.186, bf16[512,960]{0,1:T(8,128)(2,1)S(1)} %multiply_convert_fusion.3, bf16[960,2560]{1,0:T(8,128)(2,1)} %constant_dynamic-update-slice_fusion.7), kind=kOutput, calls=%fused_computation.137 | convolution fusion | flops 2536243200 | bytes 24248320 | tf_op jit(solution)/shard_map/dot_general | solution.py:23
  268.9 4.6 fusion.188
  273.5 4.9 convolution_convert_fusion.1
  278.4 4.4 convolution_convert_fusion.2
  282.8 5.4 multiply_reduce_fusion.2
  288.8 3.5 convolution_convert_fusion.5
  299.1 83.5 %while.54 = (s32[]{:T(128)}, f32[5,3,256,64]{2,3,1,0:T(8,128)}, bf16[5,1024,64]{1,2,0:T(8,128)(2,1)}, bf16[5,1024,64]{1,2,0:T(8,128)(2,1)}, pred[2,256,1024]{2,1...) while((s32[]{:T(128)}, f32[5,3,256,64]{2,3,1,0:T(8,128)}, ...), condition=%wide.region_17.18_spmd, body=%wide.region_15.17_spmd.sunk | while | flops 514330112 | bytes 36911216 | solution.py:326
  302.0 3.2 fusion.267
  305.2 4.4 fusion.268
  309.6 4.3 fusion.269
  321.9 4.4 fusion.268
  326.3 4.3 fusion.269
  338.6 4.4 fusion.268
  343.0 4.3 fusion.269
  355.3 4.4 fusion.268
  359.7 4.3 fusion.269
  372.0 4.4 fusion.268
  376.4 4.3 fusion.269
  385.6 83.8 %while.55 = (s32[]{:T(128)}, f32[5,3,256,64]{2,3,1,0:T(8,128)}, bf16[5,1024,64]{1,2,0:T(8,128)(2,1)}, bf16[5,1024,64]{1,2,0:T(8,128)(2,1)}, pred[2,256,1024]{2,1...) while((s32[]{:T(128)}, f32[5,3,256,64]{2,3,1,0:T(8,128)}, ...), condition=%wide.region_20.21_spmd, body=%wide.region_18.20_spmd.sunk | while | flops 514330112 | bytes 36911216 | solution.py:326
  388.6 3.2 fusion.281
  391.8 4.4 fusion.282
  396.2 4.3 fusion.283
  405.3 3.2 fusion.281
  408.5 4.4 fusion.282
  412.9 4.3 fusion.283
  422.0 3.2 fusion.281
  425.2 4.4 fusion.282
  429.6 4.3 fusion.283
  438.7 3.2 fusion.281
  441.9 4.4 fusion.282
  446.3 4.3 fusion.283
  458.6 4.4 fusion.282
  463.0 4.3 fusion.283
  490.5 7.0 convolution_convert_fusion
  497.5 8.1 %copy.181 = bf16[2560,960]{1,0:T(8,128)(2,1)} copy(bf16[2560,960]{0,1:T(8,128)(2,1)} %convolution_convert_fusion) | data formatting | bytes 9830400 | tf_op jit(solution)/shard_map/reshape | solution.py:148
  505.6 3.7 constant_dynamic-slice_fusion.2
  509.3 3.3 constant_dynamic-slice_fusion.3
  516.5 6.2 add_convert_fusion.6
  549.7 3.5 collective-permute-start.51
  553.5 3.4 collective-permute-done.81
  563.3 11.6 %collective-permute-done.53 = bf16[120,960]{1,0:T(8,128)(2,1)S(1)} collective-permute-done((bf16[120,960]{1,0:T(8,128)(2,1)S(1)}, bf16[120,960]{1,0:T(8,128)(2,1)S(1)}, u32[]{:S(2)}, u32[]{:S(2)}) %collective-permute-start.53) | collective-permute-done | bytes 230432 | tf_op jit(solution)/shard_map/ppermute | solution.py:62
  576.5 4.0 collective-permute-done.84
  594.8 15.8 %collective-permute-done.65 = bf16[120,2560]{1,0:T(8,128)(2,1)S(1)} collective-permute-done((bf16[120,2560]{1,0:T(8,128)(2,1)S(1)}, bf16[120,2560]{1,0:T(8,128)(2,1)S(1)}, u32[]{:S(2)}, u32[]{:S(2)}) %collective-permute-start.65) | collective-permute-done | bytes 614432 | tf_op jit(solution)/shard_map/ppermute | solution.py:62
  613.1 14.9 %collective-permute-done.41 = bf16[120,1600]{1,0:T(8,128)(2,1)S(1)} collective-permute-done((bf16[120,1600]{1,0:T(8,128)(2,1)S(1)}, bf16[120,1600]{1,0:T(8,128)(2,1)S(1)}, u32[]{:S(2)}, u32[]{:S(2)}) %collective-permute-start.41) | collective-permute-done | bytes 384032 | tf_op jit(solution)/shard_map/ppermute | solution.py:62
  630.4 4.3 collective-permute-done.40
  635.0 14.5 %collective-permute-done.42 = bf16[120,1600]{1,0:T(8,128)(2,1)S(1)} collective-permute-done((bf16[120,1600]{1,0:T(8,128)(2,1)S(1)}, bf16[120,1600]{1,0:T(8,128)(2,1)S(1)}, u32[]{:S(2)}, u32[]{:S(2)}) %collective-permute-start.42) | collective-permute-done | bytes 384032 | tf_op jit(solution)/shard_map/ppermute | solution.py:62
  655.1 4.5 collective-permute-done.66
  661.6 4.6 collective-permute-done.58
  669.0 8.2 %collective-permute-done.75 = bf16[320,960]{1,0:T(8,128)(2,1)S(1)} collective-permute-done((bf16[320,960]{1,0:T(8,128)(2,1)S(1)}, bf16[320,960]{1,0:T(8,128)(2,1)S(1)}, u32[]{:S(2)}, u32[]{:S(2)}) %collective-permute-start.75) | collective-permute-done | bytes 614432 | tf_op jit(solution)/shard_map/ppermute | solution.py:62
  678.1 12.2 %collective-permute-done.67 = bf16[120,2560]{1,0:T(8,128)(2,1)S(1)} collective-permute-done((bf16[120,2560]{1,0:T(8,128)(2,1)S(1)}, bf16[120,2560]{1,0:T(8,128)(2,1)S(1)}, u32[]{:S(2)}, u32[]{:S(2)}) %collective-permute-start.67) | collective-permute-done | bytes 614432 | tf_op jit(solution)/shard_map/ppermute | solution.py:62
  692.6 8.9 %collective-permute-done.59 = bf16[120,2560]{1,0:T(8,128)(2,1)S(1)} collective-permute-done((bf16[120,2560]{1,0:T(8,128)(2,1)S(1)}, bf16[120,2560]{1,0:T(8,128)(2,1)S(1)}, u32[]{:S(2)}, u32[]{:S(2)}) %collective-permute-start.59) | collective-permute-done | bytes 614432 | tf_op jit(solution)/shard_map/ppermute | solution.py:62
  711.4 13.5 %collective-permute-done.77 = bf16[320,960]{1,0:T(8,128)(2,1)} collective-permute-done((bf16[320,960]{1,0:T(8,128)(2,1)S(1)}, bf16[320,960]{1,0:T(8,128)(2,1)}, u32[]{:S(2)}, u32[]{:S(2)}) %collective-permute-start.77) | collective-permute-done | bytes 614432 | tf_op jit(solution)/shard_map/ppermute | solution.py:62
  726.2 11.9 %collective-permute-done.69 = bf16[120,2560]{1,0:T(8,128)(2,1)} collective-permute-done((bf16[120,2560]{1,0:T(8,128)(2,1)S(1)}, bf16[120,2560]{1,0:T(8,128)(2,1)}, u32[]{:S(2)}, u32[]{:S(2)}) %collective-permute-start.69) | collective-permute-done | bytes 614432 | tf_op jit(solution)/shard_map/ppermute | solution.py:62
  739.4 11.7 %collective-permute-done.61 = bf16[120,2560]{1,0:T(8,128)(2,1)} collective-permute-done((bf16[120,2560]{1,0:T(8,128)(2,1)S(1)}, bf16[120,2560]{1,0:T(8,128)(2,1)}, u32[]{:S(2)}, u32[]{:S(2)}) %collective-permute-start.61) | collective-permute-done | bytes 614432 | tf_op jit(solution)/shard_map/ppermute | solution.py:62
  (617 shorter events, 389.4 us)
Async XLA Ops:
  4.9 50.4 %collective-permute-start.3 = (bf16[120,1600]{1,0:T(8,128)(2,1)}, bf16[120,1600]{1,0:T(8,128)(2,1)}, u32[]{:S(2)}, u32[]{:S(2)}) collective-permute-start(bf16[120,1600]{1,0:T(8,128)(2,1)} %constant_dynamic-slice_fusion.11), channel_id=1, source_target_pairs={{0,1},{1,0},{2,3},{3,2},{4,6},{5,7},{6,4},{7,5},{8,9},{9,8},{10,11... | collective-permute-start | bytes 1152008 | tf_op jit(solution)/shard_map/ppermute | solution.py:62
  7.8 49.8 %collective-permute-start.4 = (bf16[120,1600]{1,0:T(8,128)(2,1)}, bf16[120,1600]{1,0:T(8,128)(2,1)}, u32[]{:S(2)}, u32[]{:S(2)}) collective-permute-start(bf16[120,1600]{1,0:T(8,128)(2,1)} %constant_dynamic-slice_fusion.11), channel_id=1, source_target_pairs={{0,2},{1,3},{2,0},{3,1},{4,5},{5,4},{6,7},{7,6},{8,10},{9,11},{10,... | collective-permute-start | bytes 1152008 | tf_op jit(solution)/shard_map/ppermute | solution.py:62
  9.4 34.3 %collective-permute-start = (bf16[2,240]{1,0:T(2,128)(2,1)S(1)}, bf16[2,240]{1,0:T(2,128)(2,1)S(1)}, u32[]{:S(2)}, u32[]{:S(2)}) collective-permute-start(bf16[2,240]{1,0:T(2,128)(2,1)S(1)} %pad_maximum_fusion.14), channel_id=1, source_target_pairs={{0,1},{1,0},{2,3},{3,2},{4,5},{5,4},{6,7},{7,6},{8,9},{9,8},{10,11... | collective-permute-start | bytes 2888 | tf_op jit(solution)/shard_map/ppermute | solution.py:62
  10.0 34.2 %collective-permute-start.1 = (bf16[2,240]{1,0:T(2,128)(2,1)S(1)}, bf16[2,240]{1,0:T(2,128)(2,1)S(1)}, u32[]{:S(2)}, u32[]{:S(2)}) collective-permute-start(bf16[2,240]{1,0:T(2,128)(2,1)S(1)} %pad_maximum_fusion.14), channel_id=1, source_target_pairs={{0,2},{1,3},{2,0},{3,1},{4,6},{5,7},{6,4},{7,5},{8,10},{9,11},{10,... | collective-permute-start | bytes 2888 | tf_op jit(solution)/shard_map/ppermute | solution.py:62
  10.0 34.2 %collective-permute-start.2 = (bf16[2,240]{1,0:T(2,128)(2,1)S(1)}, bf16[2,240]{1,0:T(2,128)(2,1)S(1)}, u32[]{:S(2)}, u32[]{:S(2)}) collective-permute-start(bf16[2,240]{1,0:T(2,128)(2,1)S(1)} %pad_maximum_fusion.14), channel_id=1, source_target_pairs={{0,3},{1,2},{2,1},{3,0},{4,7},{5,6},{6,5},{7,4},{8,11},{9,10},{10,... | collective-permute-start | bytes 2888 | tf_op jit(solution)/shard_map/ppermute | solution.py:62
  44.2 31.8 %collective-permute-start.18 = (bf16[120,2560]{1,0:T(8,128)(2,1)}, bf16[120,2560]{1,0:T(8,128)(2,1)}, u32[]{:S(2)}, u32[]{:S(2)}) collective-permute-start(bf16[120,2560]{1,0:T(8,128)(2,1)} %constant_dynamic-slice_fusion.9), channel_id=1, source_target_pairs={{0,1},{1,0},{2,3},{3,2},{4,6},{5,7},{6,4},{7,5},{8,9},{9,8},{10,11... | collective-permute-start | bytes 1843208 | tf_op jit(solution)/shard_map/ppermute | solution.py:62
  50.2 29.2 %collective-permute-start.19 = (bf16[120,2560]{1,0:T(8,128)(2,1)}, bf16[120,2560]{1,0:T(8,128)(2,1)S(1)}, u32[]{:S(2)}, u32[]{:S(2)}) collective-permute-start(bf16[120,2560]{1,0:T(8,128)(2,1)} %constant_dynamic-slice_fusion.9), channel_id=1, source_target_pairs={{0,2},{1,3},{2,0},{3,1},{4,5},{5,4},{6,7},{7,6},{8,10},{9,11},{10,... | collective-permute-start | bytes 1843208 | tf_op jit(solution)/shard_map/ppermute | solution.py:62
  53.3 44.8 %collective-permute-start.30 = (bf16[320,960]{1,0:T(8,128)(2,1)S(1)}, bf16[320,960]{1,0:T(8,128)(2,1)}, u32[]{:S(2)}, u32[]{:S(2)}) collective-permute-start(bf16[320,960]{1,0:T(8,128)(2,1)S(1)} %constant_dynamic-slice_fusion.7), channel_id=1, source_target_pairs={{0,1},{1,0},{2,3},{3,2},{4,6},{5,7},{6,4},{7,5},{8,9},{9,8},{10,11... | collective-permute-start | bytes 1843208 | tf_op jit(solution)/shard_map/ppermute | solution.py:62
  55.3 17.5 %collective-permute-start.14 = (bf16[120,960]{1,0:T(8,128)(2,1)S(1)}, bf16[120,960]{1,0:T(8,128)(2,1)S(1)}, u32[]{:S(2)}, u32[]{:S(2)}) collective-permute-start(bf16[120,960]{1,0:T(8,128)(2,1)S(1)} %collective-permute-done.12), channel_id=1, source_target_pairs={{0,2},{1,3},{2,0},{3,1},{4,5},{5,4},{6,7},{7,6},{8,10},{9,11},{10,... | collective-permute-start | bytes 691208 | tf_op jit(solution)/shard_map/ppermute | solution.py:62
  57.6 15.9 %collective-permute-start.15 = (bf16[120,960]{1,0:T(8,128)(2,1)S(1)}, bf16[120,960]{1,0:T(8,128)(2,1)S(1)}, u32[]{:S(2)}, u32[]{:S(2)}) collective-permute-start(bf16[120,960]{1,0:T(8,128)(2,1)S(1)} %collective-permute-done.12), channel_id=1, source_target_pairs={{0,4},{1,5},{2,6},{3,7},{4,0},{5,1},{6,2},{7,3},{8,12},{9,13},{10,... | collective-permute-start | bytes 691208 | tf_op jit(solution)/shard_map/ppermute | solution.py:62
  73.5 27.1 %collective-permute-start.31 = (bf16[320,960]{1,0:T(8,128)(2,1)S(1)}, bf16[320,960]{1,0:T(8,128)(2,1)}, u32[]{:S(2)}, u32[]{:S(2)}) collective-permute-start(bf16[320,960]{1,0:T(8,128)(2,1)S(1)} %constant_dynamic-slice_fusion.7), channel_id=1, source_target_pairs={{0,2},{1,3},{2,0},{3,1},{4,5},{5,4},{6,7},{7,6},{8,10},{9,11},{10,... | collective-permute-start | bytes 1843208 | tf_op jit(solution)/shard_map/ppermute | solution.py:62
  74.7 16.8 %collective-permute-start.24 = (bf16[120,2560]{1,0:T(8,128)(2,1)S(1)}, bf16[120,2560]{1,0:T(8,128)(2,1)S(1)}, u32[]{:S(2)}, u32[]{:S(2)}) collective-permute-start(bf16[120,2560]{1,0:T(8,128)(2,1)S(1)} %copy-done.41), channel_id=1, source_target_pairs={{0,1},{1,0},{2,3},{3,2},{4,6},{5,7},{6,4},{7,5},{8,9},{9,8},{10,11... | collective-permute-start | bytes 1843208 | tf_op jit(solution)/shard_map/ppermute | solution.py:62
  76.0 21.2 %collective-permute-start.25 = (bf16[120,2560]{1,0:T(8,128)(2,1)S(1)}, bf16[120,2560]{1,0:T(8,128)(2,1)S(1)}, u32[]{:S(2)}, u32[]{:S(2)}) collective-permute-start(bf16[120,2560]{1,0:T(8,128)(2,1)S(1)} %copy-done.41), channel_id=1, source_target_pairs={{0,2},{1,3},{2,0},{3,1},{4,5},{5,4},{6,7},{7,6},{8,10},{9,11},{10,... | collective-permute-start | bytes 1843208 | tf_op jit(solution)/shard_map/ppermute | solution.py:62
  79.4 24.6 %collective-permute-start.5 = (bf16[120,1600]{1,0:T(8,128)(2,1)}, bf16[120,1600]{1,0:T(8,128)(2,1)S(1)}, u32[]{:S(2)}, u32[]{:S(2)}) collective-permute-start(bf16[120,1600]{1,0:T(8,128)(2,1)} %collective-permute-done.3), channel_id=1, source_target_pairs={{0,2},{1,3},{2,0},{3,1},{4,5},{5,4},{6,7},{7,6},{8,10},{9,11},{10,... | collective-permute-start | bytes 1152008 | tf_op jit(solution)/shard_map/ppermute | solution.py:62
  91.5 13.9 %collective-permute-start.6 = (bf16[120,1600]{1,0:T(8,128)(2,1)}, bf16[120,1600]{1,0:T(8,128)(2,1)S(1)}, u32[]{:S(2)}, u32[]{:S(2)}) collective-permute-start(bf16[120,1600]{1,0:T(8,128)(2,1)} %collective-permute-done.3), channel_id=1, source_target_pairs={{0,4},{1,5},{2,6},{3,7},{4,0},{5,1},{6,2},{7,3},{8,12},{9,13},{10,... | collective-permute-start | bytes 1152008 | tf_op jit(solution)/shard_map/ppermute | solution.py:62
  100.6 31.7 %collective-permute-start.20 = (bf16[120,2560]{1,0:T(8,128)(2,1)}, bf16[120,2560]{1,0:T(8,128)(2,1)}, u32[]{:S(2)}, u32[]{:S(2)}) collective-permute-start(bf16[120,2560]{1,0:T(8,128)(2,1)} %collective-permute-done.18), channel_id=1, source_target_pairs={{0,2},{1,3},{2,0},{3,1},{4,5},{5,4},{6,7},{7,6},{8,10},{9,11},{10,... | collective-permute-start | bytes 1843208 | tf_op jit(solution)/shard_map/ppermute | solution.py:62
  103.2 31.6 %collective-permute-start.21 = (bf16[120,2560]{1,0:T(8,128)(2,1)}, bf16[120,2560]{1,0:T(8,128)(2,1)}, u32[]{:S(2)}, u32[]{:S(2)}) collective-permute-start(bf16[120,2560]{1,0:T(8,128)(2,1)} %collective-permute-done.18), channel_id=1, source_target_pairs={{0,4},{1,5},{2,6},{3,7},{4,0},{5,1},{6,2},{7,3},{8,12},{9,13},{10,... | collective-permute-start | bytes 1843208 | tf_op jit(solution)/shard_map/ppermute | solution.py:62
  103.9 21.4 %collective-permute-start.32 = (bf16[320,960]{1,0:T(8,128)(2,1)}, bf16[320,960]{1,0:T(8,128)(2,1)}, u32[]{:S(2)}, u32[]{:S(2)}) collective-permute-start(bf16[320,960]{1,0:T(8,128)(2,1)} %collective-permute-done.30), channel_id=1, source_target_pairs={{0,2},{1,3},{2,0},{3,1},{4,5},{5,4},{6,7},{7,6},{8,10},{9,11},{10,... | collective-permute-start | bytes 1843208 | tf_op jit(solution)/shard_map/ppermute | solution.py:62
  105.6 22.2 %collective-permute-start.33 = (bf16[320,960]{1,0:T(8,128)(2,1)}, bf16[320,960]{1,0:T(8,128)(2,1)}, u32[]{:S(2)}, u32[]{:S(2)}) collective-permute-start(bf16[320,960]{1,0:T(8,128)(2,1)} %collective-permute-done.30), channel_id=1, source_target_pairs={{0,4},{1,5},{2,6},{3,7},{4,0},{5,1},{6,2},{7,3},{8,12},{9,13},{10,... | collective-permute-start | bytes 1843208 | tf_op jit(solution)/shard_map/ppermute | solution.py:62
  107.2 23.1 %collective-permute-start.34 = (bf16[320,960]{1,0:T(8,128)(2,1)}, bf16[320,960]{1,0:T(8,128)(2,1)}, u32[]{:S(2)}, u32[]{:S(2)}) collective-permute-start(bf16[320,960]{1,0:T(8,128)(2,1)} %collective-permute-done.31), channel_id=1, source_target_pairs={{0,4},{1,5},{2,6},{3,7},{4,0},{5,1},{6,2},{7,3},{8,12},{9,13},{10,... | collective-permute-start | bytes 1843208 | tf_op jit(solution)/shard_map/ppermute | solution.py:62
  125.4 12.6 %collective-permute-start.22 = (bf16[120,2560]{1,0:T(8,128)(2,1)S(1)}, bf16[120,2560]{1,0:T(8,128)(2,1)S(1)}, u32[]{:S(2)}, u32[]{:S(2)}) collective-permute-start(bf16[120,2560]{1,0:T(8,128)(2,1)S(1)} %copy-done.40), channel_id=1, source_target_pairs={{0,4},{1,5},{2,6},{3,7},{4,0},{5,1},{6,2},{7,3},{8,12},{9,13},{10,... | collective-permute-start | bytes 1843208 | tf_op jit(solution)/shard_map/ppermute | solution.py:62
  127.7 11.7 %collective-permute-start.26 = (bf16[120,2560]{1,0:T(8,128)(2,1)S(1)}, bf16[120,2560]{1,0:T(8,128)(2,1)}, u32[]{:S(2)}, u32[]{:S(2)}) collective-permute-start(bf16[120,2560]{1,0:T(8,128)(2,1)S(1)} %copy-done.45), channel_id=1, source_target_pairs={{0,2},{1,3},{2,0},{3,1},{4,5},{5,4},{6,7},{7,6},{8,10},{9,11},{10,... | collective-permute-start | bytes 1843208 | tf_op jit(solution)/shard_map/ppermute | solution.py:62
  130.3 11.1 %collective-permute-start.27 = (bf16[120,2560]{1,0:T(8,128)(2,1)S(1)}, bf16[120,2560]{1,0:T(8,128)(2,1)S(1)}, u32[]{:S(2)}, u32[]{:S(2)}) collective-permute-start(bf16[120,2560]{1,0:T(8,128)(2,1)S(1)} %copy-done.45), channel_id=1, source_target_pairs={{0,4},{1,5},{2,6},{3,7},{4,0},{5,1},{6,2},{7,3},{8,12},{9,13},{10,... | collective-permute-start | bytes 1843208 | tf_op jit(solution)/shard_map/ppermute | solution.py:62
  132.3 10.5 %collective-permute-start.28 = (bf16[120,2560]{1,0:T(8,128)(2,1)S(1)}, bf16[120,2560]{1,0:T(8,128)(2,1)S(1)}, u32[]{:S(2)}, u32[]{:S(2)}) collective-permute-start(bf16[120,2560]{1,0:T(8,128)(2,1)S(1)} %copy-done.43), channel_id=1, source_target_pairs={{0,4},{1,5},{2,6},{3,7},{4,0},{5,1},{6,2},{7,3},{8,12},{9,13},{10,... | collective-permute-start | bytes 1843208 | tf_op jit(solution)/shard_map/ppermute | solution.py:62
  134.8 15.8 %collective-permute-start.9 = (bf16[512,640]{0,1:T(8,128)(2,1)}, bf16[512,640]{0,1:T(8,128)(2,1)}, u32[]{:S(2)}, u32[]{:S(2)}) collective-permute-start(bf16[512,640]{0,1:T(8,128)(2,1)} %pad_maximum_fusion.8), channel_id=1, source_target_pairs={{0,1},{1,0},{2,3},{3,2},{4,6},{5,7},{6,4},{7,5},{8,9},{9,8},{10,11... | collective-permute-start | bytes 1966088 | tf_op jit(solution)/shard_map/ppermute | solution.py:62
  138.0 17.4 %collective-permute-start.10 = (bf16[512,640]{0,1:T(8,128)(2,1)}, bf16[512,640]{0,1:T(8,128)(2,1)}, u32[]{:S(2)}, u32[]{:S(2)}) collective-permute-start(bf16[512,640]{0,1:T(8,128)(2,1)} %pad_maximum_fusion.8), channel_id=1, source_target_pairs={{0,2},{1,3},{2,0},{3,1},{4,5},{5,4},{6,7},{7,6},{8,10},{9,11},{10,... | collective-permute-start | bytes 1966088 | tf_op jit(solution)/shard_map/ppermute | solution.py:62
  139.5 18.7 %collective-permute-start.23 = (bf16[120,2560]{1,0:T(8,128)(2,1)}, bf16[120,2560]{1,0:T(8,128)(2,1)}, u32[]{:S(2)}, u32[]{:S(2)}) collective-permute-start(bf16[120,2560]{1,0:T(8,128)(2,1)} %collective-permute-done.20), channel_id=1, source_target_pairs={{0,4},{1,5},{2,6},{3,7},{4,0},{5,1},{6,2},{7,3},{8,12},{9,13},{10,... | collective-permute-start | bytes 1843208 | tf_op jit(solution)/shard_map/ppermute | solution.py:62
  141.4 20.7 %collective-permute-start.35 = (bf16[320,960]{1,0:T(8,128)(2,1)}, bf16[320,960]{1,0:T(8,128)(2,1)}, u32[]{:S(2)}, u32[]{:S(2)}) collective-permute-start(bf16[320,960]{1,0:T(8,128)(2,1)} %collective-permute-done.32), channel_id=1, source_target_pairs={{0,4},{1,5},{2,6},{3,7},{4,0},{5,1},{6,2},{7,3},{8,12},{9,13},{10,... | collective-permute-start | bytes 1843208 | tf_op jit(solution)/shard_map/ppermute | solution.py:62
  142.8 17.3 %collective-permute-start.29 = (bf16[120,2560]{1,0:T(8,128)(2,1)}, bf16[120,2560]{1,0:T(8,128)(2,1)}, u32[]{:S(2)}, u32[]{:S(2)}) collective-permute-start(bf16[120,2560]{1,0:T(8,128)(2,1)} %collective-permute-done.26), channel_id=1, source_target_pairs={{0,4},{1,5},{2,6},{3,7},{4,0},{5,1},{6,2},{7,3},{8,12},{9,13},{10,... | collective-permute-start | bytes 1843208 | tf_op jit(solution)/shard_map/ppermute | solution.py:62
  150.5 20.8 %collective-permute-start.11 = (bf16[512,640]{0,1:T(8,128)(2,1)}, bf16[512,640]{0,1:T(8,128)(2,1)}, u32[]{:S(2)}, u32[]{:S(2)}) collective-permute-start(bf16[512,640]{0,1:T(8,128)(2,1)} %collective-permute-done.9), channel_id=1, source_target_pairs={{0,2},{1,3},{2,0},{3,1},{4,5},{5,4},{6,7},{7,6},{8,10},{9,11},{10,... | collective-permute-start | bytes 1966088 | tf_op jit(solution)/shard_map/ppermute | solution.py:62
  486.2 36.5 %collective-permute-start.37 = (bf16[512,640]{0,1:T(8,128)(2,1)}, bf16[512,640]{0,1:T(8,128)(2,1)}, u32[]{:S(2)}, u32[]{:S(2)}) collective-permute-start(bf16[512,640]{0,1:T(8,128)(2,1)} %copy.171), channel_id=1, source_target_pairs={{0,2},{1,3},{2,0},{3,1},{4,5},{5,4},{6,7},{7,6},{8,10},{9,11},{10,... | collective-permute-start | bytes 1966088 | tf_op jit(solution)/shard_map/ppermute | solution.py:62
  488.5 50.6 %collective-permute-start.36 = (bf16[512,640]{0,1:T(8,128)(2,1)}, bf16[512,640]{0,1:T(8,128)(2,1)}, u32[]{:S(2)}, u32[]{:S(2)}) collective-permute-start(bf16[512,640]{0,1:T(8,128)(2,1)} %copy.169), channel_id=1, source_target_pairs={{0,2},{1,3},{2,0},{3,1},{4,5},{5,4},{6,7},{7,6},{8,10},{9,11},{10,... | collective-permute-start | bytes 1966088 | tf_op jit(solution)/shard_map/ppermute | solution.py:62
  509.3 73.8 %collective-permute-start.71 = (bf16[4,320,960]{2,1,0:T(8,128)(2,1)}, bf16[4,320,960]{2,1,0:T(8,128)(2,1)}, u32[]{:S(2)}, u32[]{:S(2)}) collective-permute-start(bf16[4,320,960]{2,1,0:T(8,128)(2,1)} %constant_dynamic-slice_fusion.2), channel_id=1, source_target_pairs={{0,4},{1,5},{2,6},{3,7},{4,0},{5,1},{6,2},{7,3},{8,12},{9,13},{10,... | collective-permute-start | bytes 7372808 | tf_op jit(solution)/shard_map/ppermute | solution.py:62
  512.5 75.9 %collective-permute-start.63 = (bf16[4,120,2560]{2,1,0:T(8,128)(2,1)}, bf16[4,120,2560]{2,1,0:T(8,128)(2,1)}, u32[]{:S(2)}, u32[]{:S(2)}) collective-permute-start(bf16[4,120,2560]{2,1,0:T(8,128)(2,1)} %constant_dynamic-slice_fusion.3), channel_id=1, source_target_pairs={{0,4},{1,5},{2,6},{3,7},{4,0},{5,1},{6,2},{7,3},{8,12},{9,13},{10,... | collective-permute-start | bytes 7372808 | tf_op jit(solution)/shard_map/ppermute | solution.py:62
  524.8 14.4 %collective-permute-start.38 = (bf16[512,640]{0,1:T(8,128)(2,1)}, bf16[512,640]{0,1:T(8,128)(2,1)}, u32[]{:S(2)}, u32[]{:S(2)}) collective-permute-start(bf16[512,640]{0,1:T(8,128)(2,1)} %add_convert_fusion.11), channel_id=1, source_target_pairs={{0,1},{1,0},{2,3},{3,2},{4,6},{5,7},{6,4},{7,5},{8,9},{9,8},{10,11... | collective-permute-start | bytes 1966088 | tf_op jit(solution)/shard_map/ppermute | solution.py:62
  536.2 11.4 %collective-permute-start.48 = (bf16[120,960]{1,0:T(8,128)(2,1)S(1)}, bf16[120,960]{1,0:T(8,128)(2,1)S(1)}, u32[]{:S(2)}, u32[]{:S(2)}) collective-permute-start(bf16[120,960]{1,0:T(8,128)(2,1)S(1)} %get-tuple-element.389), channel_id=1, source_target_pairs={{0,2},{1,3},{2,0},{3,1},{4,5},{5,4},{6,7},{7,6},{8,10},{9,11},{10,... | collective-permute-start | bytes 691208 | tf_op jit(solution)/shard_map/ppermute | solution.py:62
  539.1 10.5 %collective-permute-start.50 = (bf16[120,960]{1,0:T(8,128)(2,1)S(1)}, bf16[120,960]{1,0:T(8,128)(2,1)S(1)}, u32[]{:S(2)}, u32[]{:S(2)}) collective-permute-start(bf16[120,960]{1,0:T(8,128)(2,1)S(1)} %fusion.162), channel_id=1, source_target_pairs={{0,1},{1,0},{2,3},{3,2},{4,6},{5,7},{6,4},{7,5},{8,9},{9,8},{10,11... | collective-permute-start | bytes 691208 | tf_op jit(solution)/shard_map/ppermute | solution.py:62
  547.0 44.4 %collective-permute-start.55 = (bf16[4,120,2560]{2,1,0:T(8,128)(2,1)S(1)}, bf16[4,120,2560]{2,1,0:T(8,128)(2,1)S(1)}, u32[]{:S(2)}, u32[]{:S(2)}) collective-permute-start(bf16[4,120,2560]{2,1,0:T(8,128)(2,1)S(1)} %copy-done.24), channel_id=1, source_target_pairs={{0,4},{1,5},{2,6},{3,7},{4,0},{5,1},{6,2},{7,3},{8,12},{9,13},{10,... | collective-permute-start | bytes 7372808 | tf_op jit(solution)/shard_map/ppermute | solution.py:62
  560.8 14.1 %collective-permute-start.53 = (bf16[120,960]{1,0:T(8,128)(2,1)S(1)}, bf16[120,960]{1,0:T(8,128)(2,1)S(1)}, u32[]{:S(2)}, u32[]{:S(2)}) collective-permute-start(bf16[120,960]{1,0:T(8,128)(2,1)S(1)} %add_convert_fusion.24), channel_id=1, source_target_pairs={{8,0},{9,1},{10,2},{11,3},{12,4},{13,5},{14,6},{15,7},{16,24},{17,... | collective-permute-start | bytes 691208 | tf_op jit(solution)/shard_map/ppermute | solution.py:62
  563.3 30.5 %collective-permute-start.39 = (bf16[4,120,1600]{2,1,0:T(8,128)(2,1)S(1)}, bf16[4,120,1600]{2,1,0:T(8,128)(2,1)S(1)}, u32[]{:S(2)}, u32[]{:S(2)}) collective-permute-start(bf16[4,120,1600]{2,1,0:T(8,128)(2,1)S(1)} %constant_dynamic-slice_fusion.6), channel_id=1, source_target_pairs={{0,4},{1,5},{2,6},{3,7},{4,0},{5,1},{6,2},{7,3},{8,12},{9,13},{10,... | collective-permute-start | bytes 4608008 | tf_op jit(solution)/shard_map/ppermute | solution.py:62
  586.3 24.8 %collective-permute-start.73 = (bf16[320,960]{1,0:T(8,128)(2,1)S(1)}, bf16[320,960]{1,0:T(8,128)(2,1)S(1)}, u32[]{:S(2)}, u32[]{:S(2)}) collective-permute-start(bf16[320,960]{1,0:T(8,128)(2,1)S(1)} %get-tuple-element.362), channel_id=1, source_target_pairs={{0,2},{1,3},{2,0},{3,1},{4,5},{5,4},{6,7},{7,6},{8,10},{9,11},{10,... | collective-permute-start | bytes 1843208 | tf_op jit(solution)/shard_map/ppermute | solution.py:62
  586.8 63.4 %collective-permute-start.72 = (bf16[320,960]{1,0:T(8,128)(2,1)S(1)}, bf16[320,960]{1,0:T(8,128)(2,1)S(1)}, u32[]{:S(2)}, u32[]{:S(2)}) collective-permute-start(bf16[320,960]{1,0:T(8,128)(2,1)S(1)} %get-tuple-element.361), channel_id=1, source_target_pairs={{0,2},{1,3},{2,0},{3,1},{4,5},{5,4},{6,7},{7,6},{8,10},{9,11},{10,... | collective-permute-start | bytes 1843208 | tf_op jit(solution)/shard_map/ppermute | solution.py:62
  590.9 19.7 %collective-permute-start.65 = (bf16[120,2560]{1,0:T(8,128)(2,1)S(1)}, bf16[120,2560]{1,0:T(8,128)(2,1)S(1)}, u32[]{:S(2)}, u32[]{:S(2)}) collective-permute-start(bf16[120,2560]{1,0:T(8,128)(2,1)S(1)} %get-tuple-element.370), channel_id=1, source_target_pairs={{0,2},{1,3},{2,0},{3,1},{4,5},{5,4},{6,7},{7,6},{8,10},{9,11},{10,... | collective-permute-start | bytes 1843208 | tf_op jit(solution)/shard_map/ppermute | solution.py:62
  591.4 62.4 %collective-permute-start.64 = (bf16[120,2560]{1,0:T(8,128)(2,1)S(1)}, bf16[120,2560]{1,0:T(8,128)(2,1)S(1)}, u32[]{:S(2)}, u32[]{:S(2)}) collective-permute-start(bf16[120,2560]{1,0:T(8,128)(2,1)S(1)} %get-tuple-element.369), channel_id=1, source_target_pairs={{0,2},{1,3},{2,0},{3,1},{4,5},{5,4},{6,7},{7,6},{8,10},{9,11},{10,... | collective-permute-start | bytes 1843208 | tf_op jit(solution)/shard_map/ppermute | solution.py:62
  593.8 34.9 %collective-permute-start.57 = (bf16[120,2560]{1,0:T(8,128)(2,1)S(1)}, bf16[120,2560]{1,0:T(8,128)(2,1)S(1)}, u32[]{:S(2)}, u32[]{:S(2)}) collective-permute-start(bf16[120,2560]{1,0:T(8,128)(2,1)S(1)} %get-tuple-element.372), channel_id=1, source_target_pairs={{0,2},{1,3},{2,0},{3,1},{4,5},{5,4},{6,7},{7,6},{8,10},{9,11},{10,... | collective-permute-start | bytes 1843208 | tf_op jit(solution)/shard_map/ppermute | solution.py:62
  610.6 17.4 %collective-permute-start.41 = (bf16[120,1600]{1,0:T(8,128)(2,1)S(1)}, bf16[120,1600]{1,0:T(8,128)(2,1)S(1)}, u32[]{:S(2)}, u32[]{:S(2)}) collective-permute-start(bf16[120,1600]{1,0:T(8,128)(2,1)S(1)} %get-tuple-element.378), channel_id=1, source_target_pairs={{0,2},{1,3},{2,0},{3,1},{4,5},{5,4},{6,7},{7,6},{8,10},{9,11},{10,... | collective-permute-start | bytes 1152008 | tf_op jit(solution)/shard_map/ppermute | solution.py:62
  611.2 23.5 %collective-permute-start.40 = (bf16[120,1600]{1,0:T(8,128)(2,1)S(1)}, bf16[120,1600]{1,0:T(8,128)(2,1)S(1)}, u32[]{:S(2)}, u32[]{:S(2)}) collective-permute-start(bf16[120,1600]{1,0:T(8,128)(2,1)S(1)} %get-tuple-element.377), channel_id=1, source_target_pairs={{0,2},{1,3},{2,0},{3,1},{4,5},{5,4},{6,7},{7,6},{8,10},{9,11},{10,... | collective-permute-start | bytes 1152008 | tf_op jit(solution)/shard_map/ppermute | solution.py:62
  628.1 23.7 %collective-permute-start.74 = (bf16[320,960]{1,0:T(8,128)(2,1)S(1)}, bf16[320,960]{1,0:T(8,128)(2,1)S(1)}, u32[]{:S(2)}, u32[]{:S(2)}) collective-permute-start(bf16[320,960]{1,0:T(8,128)(2,1)S(1)} %fusion.152), channel_id=1, source_target_pairs={{0,1},{1,0},{2,3},{3,2},{4,6},{5,7},{6,4},{7,5},{8,9},{9,8},{10,11... | collective-permute-start | bytes 1843208 | tf_op jit(solution)/shard_map/ppermute | solution.py:62
  628.7 20.8 %collective-permute-start.42 = (bf16[120,1600]{1,0:T(8,128)(2,1)S(1)}, bf16[120,1600]{1,0:T(8,128)(2,1)S(1)}, u32[]{:S(2)}, u32[]{:S(2)}) collective-permute-start(bf16[120,1600]{1,0:T(8,128)(2,1)S(1)} %fusion.159), channel_id=1, source_target_pairs={{0,1},{1,0},{2,3},{3,2},{4,6},{5,7},{6,4},{7,5},{8,9},{9,8},{10,11... | collective-permute-start | bytes 1152008 | tf_op jit(solution)/shard_map/ppermute | solution.py:62
  634.7 26.9 %collective-permute-start.56 = (bf16[120,2560]{1,0:T(8,128)(2,1)S(1)}, bf16[120,2560]{1,0:T(8,128)(2,1)S(1)}, u32[]{:S(2)}, u32[]{:S(2)}) collective-permute-start(bf16[120,2560]{1,0:T(8,128)(2,1)S(1)} %get-tuple-element.371), channel_id=1, source_target_pairs={{0,2},{1,3},{2,0},{3,1},{4,5},{5,4},{6,7},{7,6},{8,10},{9,11},{10,... | collective-permute-start | bytes 1843208 | tf_op jit(solution)/shard_map/ppermute | solution.py:62
  650.2 16.0 %collective-permute-start.58 = (bf16[120,2560]{1,0:T(8,128)(2,1)S(1)}, bf16[120,2560]{1,0:T(8,128)(2,1)S(1)}, u32[]{:S(2)}, u32[]{:S(2)}) collective-permute-start(bf16[120,2560]{1,0:T(8,128)(2,1)S(1)} %fusion.156), channel_id=1, source_target_pairs={{0,1},{1,0},{2,3},{3,2},{4,6},{5,7},{6,4},{7,5},{8,9},{9,8},{10,11... | collective-permute-start | bytes 1843208 | tf_op jit(solution)/shard_map/ppermute | solution.py:62
  651.8 16.4 %collective-permute-start.43 = (bf16[120,1600]{1,0:T(8,128)(2,1)S(1)}, bf16[120,1600]{1,0:T(8,128)(2,1)S(1)}, u32[]{:S(2)}, u32[]{:S(2)}) collective-permute-start(bf16[120,1600]{1,0:T(8,128)(2,1)S(1)} %add_convert_fusion.23), channel_id=1, source_target_pairs={{0,8},{1,9},{2,10},{3,11},{4,12},{5,13},{6,14},{7,15},{24,16},{25,... | collective-permute-start | bytes 1152008 | tf_op jit(solution)/shard_map/ppermute | solution.py:62
  653.8 23.3 %collective-permute-start.75 = (bf16[320,960]{1,0:T(8,128)(2,1)S(1)}, bf16[320,960]{1,0:T(8,128)(2,1)S(1)}, u32[]{:S(2)}, u32[]{:S(2)}) collective-permute-start(bf16[320,960]{1,0:T(8,128)(2,1)S(1)} %add_convert_fusion.9), channel_id=1, source_target_pairs={{0,8},{1,9},{2,10},{3,11},{4,12},{5,13},{6,14},{7,15},{24,16},{25,... | collective-permute-start | bytes 1843208 | tf_op jit(solution)/shard_map/ppermute | solution.py:62
  659.9 30.4 %collective-permute-start.67 = (bf16[120,2560]{1,0:T(8,128)(2,1)S(1)}, bf16[120,2560]{1,0:T(8,128)(2,1)S(1)}, u32[]{:S(2)}, u32[]{:S(2)}) collective-permute-start(bf16[120,2560]{1,0:T(8,128)(2,1)S(1)} %add_convert_fusion.15), channel_id=1, source_target_pairs={{0,8},{1,9},{2,10},{3,11},{4,12},{5,13},{6,14},{7,15},{24,16},{25,... | collective-permute-start | bytes 1843208 | tf_op jit(solution)/shard_map/ppermute | solution.py:62
  666.5 35.0 %collective-permute-start.59 = (bf16[120,2560]{1,0:T(8,128)(2,1)S(1)}, bf16[120,2560]{1,0:T(8,128)(2,1)S(1)}, u32[]{:S(2)}, u32[]{:S(2)}) collective-permute-start(bf16[120,2560]{1,0:T(8,128)(2,1)S(1)} %add_convert_fusion.18), channel_id=1, source_target_pairs={{0,8},{1,9},{2,10},{3,11},{4,12},{5,13},{6,14},{7,15},{24,16},{25,... | collective-permute-start | bytes 1843208 | tf_op jit(solution)/shard_map/ppermute | solution.py:62
  668.3 22.9 %collective-permute-start.44 = (bf16[120,1600]{1,0:T(8,128)(2,1)S(1)}, bf16[120,1600]{1,0:T(8,128)(2,1)S(1)}, u32[]{:S(2)}, u32[]{:S(2)}) collective-permute-start(bf16[120,1600]{1,0:T(8,128)(2,1)S(1)} %add_convert_fusion.22), channel_id=1, source_target_pairs={{8,16},{9,17},{10,18},{11,19},{12,20},{13,21},{14,22},{15,23},{16,... | collective-permute-start | bytes 1152008 | tf_op jit(solution)/shard_map/ppermute | solution.py:62
  677.4 26.4 %collective-permute-start.76 = (bf16[320,960]{1,0:T(8,128)(2,1)S(1)}, bf16[320,960]{1,0:T(8,128)(2,1)S(1)}, u32[]{:S(2)}, u32[]{:S(2)}) collective-permute-start(bf16[320,960]{1,0:T(8,128)(2,1)S(1)} %add_convert_fusion.8), channel_id=1, source_target_pairs={{8,16},{9,17},{10,18},{11,19},{12,20},{13,21},{14,22},{15,23},{16,... | collective-permute-start | bytes 1843208 | tf_op jit(solution)/shard_map/ppermute | solution.py:62
  690.4 14.9 %collective-permute-start.68 = (bf16[120,2560]{1,0:T(8,128)(2,1)S(1)}, bf16[120,2560]{1,0:T(8,128)(2,1)S(1)}, u32[]{:S(2)}, u32[]{:S(2)}) collective-permute-start(bf16[120,2560]{1,0:T(8,128)(2,1)S(1)} %add_convert_fusion.14), channel_id=1, source_target_pairs={{8,16},{9,17},{10,18},{11,19},{12,20},{13,21},{14,22},{15,23},{16,... | collective-permute-start | bytes 1843208 | tf_op jit(solution)/shard_map/ppermute | solution.py:62
  691.3 12.4 %collective-permute-start.45 = (bf16[120,1600]{1,0:T(8,128)(2,1)S(1)}, bf16[120,1600]{1,0:T(8,128)(2,1)S(1)}, u32[]{:S(2)}, u32[]{:S(2)}) collective-permute-start(bf16[120,1600]{1,0:T(8,128)(2,1)S(1)} %add_convert_fusion.21), channel_id=1, source_target_pairs={{8,0},{9,1},{10,2},{11,3},{12,4},{13,5},{14,6},{15,7},{16,24},{17,... | collective-permute-start | bytes 1152008 | tf_op jit(solution)/shard_map/ppermute | solution.py:62
  704.0 20.9 %collective-permute-start.77 = (bf16[320,960]{1,0:T(8,128)(2,1)S(1)}, bf16[320,960]{1,0:T(8,128)(2,1)}, u32[]{:S(2)}, u32[]{:S(2)}) collective-permute-start(bf16[320,960]{1,0:T(8,128)(2,1)S(1)} %add_convert_fusion.7), channel_id=1, source_target_pairs={{8,0},{9,1},{10,2},{11,3},{12,4},{13,5},{14,6},{15,7},{16,24},{17,... | collective-permute-start | bytes 1843208 | tf_op jit(solution)/shard_map/ppermute | solution.py:62
  705.5 32.6 %collective-permute-start.69 = (bf16[120,2560]{1,0:T(8,128)(2,1)S(1)}, bf16[120,2560]{1,0:T(8,128)(2,1)}, u32[]{:S(2)}, u32[]{:S(2)}) collective-permute-start(bf16[120,2560]{1,0:T(8,128)(2,1)S(1)} %add_convert_fusion.13), channel_id=1, source_target_pairs={{8,0},{9,1},{10,2},{11,3},{12,4},{13,5},{14,6},{15,7},{16,24},{17,... | collective-permute-start | bytes 1843208 | tf_op jit(solution)/shard_map/ppermute | solution.py:62
  707.0 44.1 %collective-permute-start.61 = (bf16[120,2560]{1,0:T(8,128)(2,1)S(1)}, bf16[120,2560]{1,0:T(8,128)(2,1)}, u32[]{:S(2)}, u32[]{:S(2)}) collective-permute-start(bf16[120,2560]{1,0:T(8,128)(2,1)S(1)} %add_convert_fusion.16), channel_id=1, source_target_pairs={{8,0},{9,1},{10,2},{11,3},{12,4},{13,5},{14,6},{15,7},{16,24},{17,... | collective-permute-start | bytes 1843208 | tf_op jit(solution)/shard_map/ppermute | solution.py:62
  726.1 27.9 %collective-permute-start.78 = (bf16[320,960]{1,0:T(8,128)(2,1)S(1)}, bf16[320,960]{1,0:T(8,128)(2,1)S(1)}, u32[]{:S(2)}, u32[]{:S(2)}) collective-permute-start(bf16[320,960]{1,0:T(8,128)(2,1)S(1)} %broadcast_select_fusion), channel_id=1, source_target_pairs={{0,4},{1,5},{2,6},{3,7},{4,0},{5,1},{6,2},{7,3},{8,12},{9,13},{10,... | collective-permute-start | bytes 1843208 | tf_op jit(solution)/shard_map/ppermute | solution.py:62
  739.3 13.8 %collective-permute-start.70 = (bf16[120,2560]{1,0:T(8,128)(2,1)S(1)}, bf16[120,2560]{1,0:T(8,128)(2,1)S(1)}, u32[]{:S(2)}, u32[]{:S(2)}) collective-permute-start(bf16[120,2560]{1,0:T(8,128)(2,1)S(1)} %broadcast_select_fusion.3), channel_id=1, source_target_pairs={{0,4},{1,5},{2,6},{3,7},{4,0},{5,1},{6,2},{7,3},{8,12},{9,13},{10,... | collective-permute-start | bytes 1843208 | tf_op jit(solution)/shard_map/ppermute | solution.py:62
  (96 other events, 794.9 us)

commit v2 on v1

v2 whole, which is shorter than its diff:
```python
import functools
import math

import jax
import jax.numpy as jnp
from jax import lax
from jax.experimental import pallas as pl
from jax.experimental.pallas import tpu as pltpu
from jax.sharding import PartitionSpec as P

QUERY_HEADS = 15
KEY_VALUE_HEADS = 5
HEAD_SIZE = 64
HALF_HEAD = HEAD_SIZE // 2
GROUP = QUERY_HEADS // KEY_VALUE_HEADS
KV_WIDTH = KEY_VALUE_HEADS * HEAD_SIZE
SCALE = HEAD_SIZE ** (-0.5)
EPS = 1e-05
AXES = ("rep", "shard")
BF = jnp.bfloat16
F32 = jnp.float32
CLOSED = -1e30
VMEM_LIMIT = 48 << 20


def dot(a, b, dims):
    return lax.dot_general(a, b, (dims, ((), ())), preferred_element_type=F32)


def nn(a, b):
    return dot(a, b, ((1,), (0,)))


def nt(a, b):
    return dot(a, b, ((1,), (1,)))


def tn(a, b):
    return dot(a, b, ((0,), (0,)))


def add(left, right):
    return (left.astype(F32) + right.astype(F32)).astype(left.dtype)


def after(value, *earlier):
    return lax.optimization_barrier((value, earlier))[0]


def rms_inverse(x):
    return lax.rsqrt(jnp.mean(x * x, axis=-1, keepdims=True) + EPS)


def cost(flops, exps, *arrays):
    size = sum(a.size * a.dtype.itemsize for a in arrays)
    return pl.CostEstimate(flops=flops, transcendentals=exps, bytes_accessed=size)


class Links:
    def __init__(self, reps, shards):
        self.reps, self.shards = reps, shards
        self.core = lax.axis_index("rep") % 2
        self.shard = lax.axis_index("shard")
        self.bits = shards.bit_length() - 1
        even = [1 << i for i in range(self.bits)]
        odd = even[:2][::-1] + even[2:]
        self.steps = list(zip(even, odd))
        self.hops = []
        for piece in range(shards):
            sums = [0, 0]
            for i, step in enumerate(self.steps):
                if piece >> i & 1:
                    sums = [sums[0] ^ step[0], sums[1] ^ step[1]]
            self.hops.append(jnp.where(self.core == 0, sums[0], sums[1]))

    def move(self, value, target):
        pairs = []
        for r in range(self.reps):
            for s in range(self.shards):
                goal = target(r, s)
                if goal is not None:
                    pairs.append((r * self.shards + s, goal[0] * self.shards + goal[1]))
        return lax.ppermute(value, AXES, pairs)

    def step(self, value, i):
        return self.move(value, lambda r, s: (r, s ^ self.steps[i][r % 2]))

    def swap(self, value):
        return self.move(value, lambda r, s: (r ^ 1, s))

    def chain(self, value):
        chips = self.reps // 2
        place = lax.axis_index("rep") // 2
        span = 1
        if chips % 4 == 0:
            inward, outward, middle = {0: 1, 3: 2}, {1: 0, 2: 3}, {1: 2, 2: 1}

            def along(value, table):
                def target(r, s):
                    chip = r // 2
                    if chip % 4 not in table:
                        return None
                    return ((chip - chip % 4 + table[chip % 4]) * 2 + r % 2, s)

                return self.move(value, target)

            value = add(value, along(value, inward))
            value = add(value, along(value, middle))
            back = along(value, outward)
            inner = (place % 4 == 1) | (place % 4 == 2)
            value = jnp.where(inner, value, back)
            span = 4
        while span < chips:
            value = add(value, self.move(value, lambda r, s: (r ^ (2 * span), s)))
            span *= 2
        return value

    def spread(self, value):
        pieces = [value]
        for i in range(self.bits):
            pieces = pieces + [self.step(piece, i) for piece in pieces]
        return pieces

    def collect(self, pieces):
        for i in reversed(range(self.bits)):
            keep = 1 << i
            pieces = [add(pieces[t], self.step(pieces[t + keep], i)) for t in range(keep)]
        return pieces[0]

    def twin(self, piece):
        return piece if self.bits < 2 else piece >> 2 << 2 | (piece & 1) << 1 | (piece >> 1 & 1)

    def half_rows(self, rows):
        half = -(-rows // 32) * 16
        return half, self.core * (rows - half), (1 - self.core) * (rows - half)

    def gather_rows(self, shard_value):
        rows = shard_value.shape[0]
        half, first, second = self.half_rows(rows)
        mine = lax.dynamic_slice_in_dim(shard_value, first, half, 0)
        pieces = self.spread(mine)[1:]
        others = [self.swap(piece) for piece in pieces]
        starts = [self.shard * rows]
        starts += [(self.shard ^ hop) * rows + first for hop in self.hops[1:]]
        starts += [
            (self.shard ^ self.hops[self.twin(t)]) * rows + second for t in range(1, self.shards)
        ]
        return pieces, (shard_value, *pieces, *others), starts, rows * self.shards

    def gather_pair(self, left, right):
        rows = left.shape[0]
        mine = jnp.where(self.core == 0, left, right)
        pieces = self.spread(mine)[1:]
        others = [self.swap(piece) for piece in pieces]
        whole = rows * self.shards
        first, second = self.core * whole, (1 - self.core) * whole
        starts = [self.shard * rows, whole + self.shard * rows]
        starts += [(self.shard ^ hop) * rows + first for hop in self.hops[1:]]
        starts += [
            (self.shard ^ self.hops[self.twin(t)]) * rows + second for t in range(1, self.shards)
        ]
        return pieces, (left, right, *pieces, *others), starts, 2 * whole

    def gather_small(self, value):
        pieces = jnp.stack(
            [
                value if hop == 0 else self.move(value, lambda r, s, hop=hop: (r, s ^ hop))
                for hop in range(self.shards)
            ]
        )
        order = self.shard ^ jnp.arange(self.shards)
        hit = (order[:, None] == jnp.arange(self.shards)[None, :])[:, :, None, None]
        pieces = jnp.sum(jnp.where(hit, pieces[None], 0), axis=1, dtype=value.dtype)
        return jnp.concatenate([pieces[j] for j in range(self.shards)], axis=-1)

    def reduce_owned(self, kept, given):
        received = self.swap(given)
        pieces = []
        for hop in self.hops:
            mine, theirs = (
                lax.dynamic_index_in_dim(part, self.shard ^ hop, 0, keepdims=False)
                for part in (kept, received)
            )
            pieces.append(add(mine, theirs))
        return self.collect(pieces)

    def reduce_rows(self, grad):
        rows = grad.shape[0] // self.shards
        half, first, second = self.half_rows(rows)
        parts = grad.astype(BF).reshape(self.shards, rows, grad.shape[1])
        kept = lax.dynamic_slice_in_dim(parts, first, half, 1)
        given = lax.dynamic_slice_in_dim(parts, second, half, 1)
        return self.reduce_owned(kept, given), rows

    def finish_rows(self, owned, rows):
        owned = self.chain(owned)
        other = self.swap(owned)
        low = jnp.where(self.core == 0, owned, other)
        high = jnp.where(self.core == 0, other, owned)
        half = owned.shape[0]
        return jnp.concatenate([low[: rows - half], high], axis=0).astype(F32)

    def finish_pair(self, owned):
        owned = self.chain(owned)
        other = self.swap(owned)
        left = jnp.where(self.core == 0, owned, other)
        right = jnp.where(self.core == 0, other, owned)
        return left.astype(F32), right.astype(F32)

    def reduce_small(self, value):
        summed = add(value, self.swap(value))
        for i in range(self.bits):
            summed = add(summed, self.step(summed, i))
        summed = self.chain(summed)
        width = value.shape[1] // self.shards
        return lax.dynamic_slice_in_dim(summed, self.shard * width, width, 1)


def assemble_kernel(at_once, starts_ref, *refs):
    count = (len(refs) - 2)
    pieces, whole, sems = refs[:count], refs[count], refs[count + 1]
    copies = []
    for i, piece in enumerate(pieces):
        start = pl.multiple_of(starts_ref[i], 16)
        copies.append(
            pltpu.make_async_copy(piece, whole.at[pl.ds(start, piece.shape[0]), :], sems.at[i])
        )
    if at_once:
        for copy in copies:
            copy.start()
        for copy in copies:
            copy.wait()
    else:
        for copy in copies:
            copy.start()
            copy.wait()


def assemble(gathered):
    _, pieces, starts, rows = gathered
    columns = pieces[0].shape[1]
    if any(piece.shape[0] % 16 for piece in pieces):
        whole = jnp.zeros((rows, columns), pieces[0].dtype)
        for piece, start in zip(pieces, starts):
            whole = lax.dynamic_update_slice(whole, piece, (start, 0))
        return whole
    out = jax.ShapeDtypeStruct((rows, columns), pieces[0].dtype)
    return pl.pallas_call(
        functools.partial(assemble_kernel, sum(p.shape[0] for p in pieces) == rows),
        grid_spec=pltpu.PrefetchScalarGridSpec(
            num_scalar_prefetch=1,
            grid=(1,),
            in_specs=[pl.BlockSpec(memory_space=pl.ANY)] * len(pieces),
            out_specs=pl.BlockSpec(memory_space=pl.ANY),
            scratch_shapes=[pltpu.SemaphoreType.DMA((len(pieces),))],
        ),
        out_shape=out,
        name="assemble",
        cost_estimate=cost(0, 0, out, out),
    )(jnp.stack([jnp.int32(start) for start in starts]), *pieces)


def head(ref, h):
    return ref[:, h * HEAD_SIZE : (h + 1) * HEAD_SIZE]


def widen(value, columns):
    n = value.shape[0]
    lane = lax.broadcasted_iota(jnp.int32, (n, HEAD_SIZE), 1)
    tail = jnp.zeros((n, HEAD_SIZE), F32)
    for c, column in enumerate(columns):
        tail = jnp.where(lane == c, column, tail)
    return jnp.concatenate([value, tail.astype(BF)], axis=1)


def split(column):
    high = column.astype(BF).astype(F32)
    middle = (column - high).astype(BF).astype(F32)
    return [high, middle, column - high - middle]


def attend_kernel(shards, seg_rows, q_ref, *refs):
    kv = refs[:shards]
    bias_ref = refs[shards]
    o_ref, lse_ref = refs[-2:]
    rows = q_ref.shape[0]
    i = lax.broadcasted_iota(jnp.int32, (rows, rows), 0)
    j = lax.broadcasted_iota(jnp.int32, (rows, rows), 1)
    same = (i // seg_rows) == (j // seg_rows)
    own = jnp.where(j > i, CLOSED, jnp.where(same, 0.0, bias_ref[0:1, :]))
    one = jnp.ones((rows, 1), F32)
    bias_columns = jnp.transpose(bias_ref[...])
    lse = jnp.zeros((rows, 128), F32)
    lane = lax.broadcasted_iota(jnp.int32, (rows, 128), 1)
    for g in range(KEY_VALUE_HEADS):
        keys, values = [], []
        for t in range(shards):
            keys.append(widen(head(kv[t], g), [bias_columns[:, t : t + 1]] if t else []))
            values.append(widen(head(kv[t], KEY_VALUE_HEADS + g), [one]))
        for h in range(g * GROUP, g * GROUP + GROUP):
            q = widen(head(q_ref, h), [one])
            scores = [nt(q, k) for k in keys]
            scores[0] = scores[0] + own
            peak = functools.reduce(jnp.maximum, scores)
            peak = jnp.max(peak, axis=1, keepdims=True)
            terms = [nn(jnp.exp(s - peak).astype(BF), v) for s, v in zip(scores, values)]
            mixed = sum(terms[1:], terms[0])
            total = mixed[:, HEAD_SIZE : HEAD_SIZE + 1]
            o_ref[:, h * HEAD_SIZE : (h + 1) * HEAD_SIZE] = (mixed[:, :HEAD_SIZE] / total).astype(BF)
            lse = jnp.where(lane == h, peak + jnp.log(total), lse)
    lse_ref[...] = lse


def attend_back_kernel(shards, seg_rows, q_ref, *refs):
    kv = refs[:shards]
    bias_ref, o_ref, do_ref, lse_ref, cos_ref, sin_ref = refs[shards : shards + 6]
    dq_ref = refs[-1 - shards]
    dkv = refs[-shards:]
    rows = q_ref.shape[0]
    i = lax.broadcasted_iota(jnp.int32, (rows, rows), 1)
    j = lax.broadcasted_iota(jnp.int32, (rows, rows), 0)
    bias_columns = jnp.transpose(bias_ref[...])
    same = (i // seg_rows) == (j // seg_rows)
    own_column = jnp.broadcast_to(bias_columns[:, 0:1], (rows, rows))
    own = jnp.where(j > i, CLOSED, jnp.where(same, 0.0, own_column))
    one, zero = jnp.ones((rows, 1), F32), jnp.zeros((rows, 1), F32)
    cosine, sine = cos_ref[...], sin_ref[...]
    for g in range(KEY_VALUE_HEADS):
        keys, values, turned = [], [], []
        for t in range(shards):
            k = head(kv[t], g)
            turned.append(jnp.transpose(k))
            keys.append(widen(k, [bias_columns[:, t : t + 1] if t else zero, one, one, one]))
            values.append(widen(head(kv[t], KEY_VALUE_HEADS + g), [one, one, one]))
        dk, dv = [None] * shards, [None] * shards
        for h in range(g * GROUP, g * GROUP + GROUP):
            q, do = head(q_ref, h), head(do_ref, h)
            centre = jnp.sum(head(o_ref, h).astype(F32) * do.astype(F32), axis=1, keepdims=True)
            q_wide = widen(q, [one] + split(-lse_ref[:, h : h + 1]))
            do_wide = widen(do, split(-centre))
            dq = None
            for t in range(shards):
                scores = nt(keys[t], q_wide)
                if t == 0:
                    scores = scores + own
                probs = jnp.exp(scores)
                ds = (probs * nt(values[t], do_wide)).astype(BF)
                v_term = nn(probs.astype(BF), do)
                k_term = nn(ds, q)
                q_term = nn(turned[t], ds)
                dv[t] = v_term if dv[t] is None else dv[t] + v_term
                dk[t] = k_term if dk[t] is None else dk[t] + k_term
                dq = q_term if dq is None else dq + q_term
            dq = dq * SCALE
            first, second = dq[:HALF_HEAD], dq[HALF_HEAD:]
            back = jnp.concatenate(
                [first * cosine + second * sine, second * cosine - first * sine], axis=0
            )
            dq_ref[:, h * HEAD_SIZE : (h + 1) * HEAD_SIZE] = jnp.transpose(back).astype(BF)
        for t in range(shards):
            dkv[t][:, g * HEAD_SIZE : (g + 1) * HEAD_SIZE] = dk[t].astype(BF)
            g_value = KEY_VALUE_HEADS + g
            dkv[t][:, g_value * HEAD_SIZE : (g_value + 1) * HEAD_SIZE] = dv[t].astype(BF)


def attend(m, rows, seg_rows, q, kv, bias, earlier):
    shards, tokens, width = len(kv), q.shape[0], q.shape[1]
    here = lambda w: pl.BlockSpec((rows, w), lambda i: (m, 0))
    whole = pl.BlockSpec((rows, 2 * KV_WIDTH), lambda i: (0, 0))
    outs = (jax.ShapeDtypeStruct((tokens, width), BF), jax.ShapeDtypeStruct((tokens, 128), F32))
    pairs = rows * rows * shards * QUERY_HEADS
    args = (q, *kv, bias, *earlier)
    return pl.pallas_call(
        functools.partial(attend_kernel, shards, seg_rows),
        grid=(1,),
        name="attend",
        in_specs=[here(width)]
        + [whole] * shards
        + [pl.BlockSpec((None,) + bias.shape[1:], lambda i: (m, 0, 0))]
        + [pl.BlockSpec(memory_space=pl.ANY)] * len(earlier),
        out_specs=(here(width), here(128)),
        out_shape=outs,
        input_output_aliases={shards + 2 + i: i for i in range(len(earlier))},
        cost_estimate=cost(16 * HEAD_SIZE * pairs, pairs, q),
        compiler_params=pltpu.CompilerParams(vmem_limit_bytes=VMEM_LIMIT),
    )(*args)


def attend_back(m, rows, seg_rows, q, kv, bias, o, do, lse, cosine, sine, earlier):
    shards, tokens, width = len(kv), q.shape[0], q.shape[1]
    here = lambda w: pl.BlockSpec((rows, w), lambda i: (m, 0))
    turned = pl.BlockSpec((HALF_HEAD, rows), lambda i: (0, m))
    whole = pl.BlockSpec((rows, 2 * KV_WIDTH), lambda i: (0, 0))
    outs = (jax.ShapeDtypeStruct((tokens, width), BF),)
    outs += (jax.ShapeDtypeStruct((rows, 2 * KV_WIDTH), BF),) * shards
    pairs = rows * rows * shards * QUERY_HEADS
    args = (q, *kv, bias, o, do, lse, cosine, sine, *earlier)
    return pl.pallas_call(
        functools.partial(attend_back_kernel, shards, seg_rows),
        grid=(1,),
        name="attend_back",
        in_specs=[here(width)]
        + [whole] * shards
        + [pl.BlockSpec((None,) + bias.shape[1:], lambda i: (m, 0, 0))]
        + [here(width), here(width), here(128), turned, turned]
        + [pl.BlockSpec(memory_space=pl.ANY)] * len(earlier),
        out_specs=(here(width),) + (whole,) * shards,
        out_shape=outs,
        input_output_aliases={shards + 7 + i: i for i in range(len(earlier))},
        cost_estimate=cost(40 * HEAD_SIZE * pairs, pairs, q),
        compiler_params=pltpu.CompilerParams(vmem_limit_bytes=VMEM_LIMIT),
    )(*args)


def rotate(vectors, cosine, sine, heads, inverse):
    shaped = vectors.reshape(vectors.shape[0], heads, HEAD_SIZE)
    first = shaped[..., :HALF_HEAD]
    second = shaped[..., HALF_HEAD:]
    cosine, sine = cosine[:, None, :], sine[:, None, :]
    if inverse:
        sine = -sine
    turned = jnp.concatenate(
        [first * cosine - second * sine, second * cosine + first * sine], axis=-1
    )
    return turned.reshape(vectors.shape[0], heads * HEAD_SIZE)


def local(
    block_input,
    parent_ids,
    w_query,
    key_weight,
    value_weight,
    w_output,
    w_gate,
    w_up,
    w_down,
    norm_first,
    norm_second,
    out_cotangent,
):
    micro, rows, width = block_input.shape
    shards = lax.axis_size("shard")
    links = Links(lax.axis_size("rep"), shards)
    tree = rows * shards
    segs = parent_ids.shape[2]
    seg_rows = tree // segs
    tokens = micro * rows
    hidden = w_gate.shape[1]

    gains = links.gather_small(jnp.stack([norm_first, norm_second])).astype(F32)
    gain_one, gain_two = gains[0:1], gains[1:2]
    attention_got = links.gather_pair(
        jnp.concatenate([w_query, key_weight], axis=1),
        jnp.concatenate([w_output, value_weight], axis=1),
    )
    attention_whole = assemble(attention_got)
    full_qk, full_output, full_value = (
        attention_whole[:width],
        attention_whole[width:, :width],
        attention_whole[width:, width:],
    )
    pair_got = links.gather_pair(*after((w_gate, w_up), attention_got[0]))
    down_got = links.gather_rows(after(w_down, pair_got[0]))

    parents = parent_ids[:, 0]
    seg = jnp.arange(segs)
    after_parent = jnp.concatenate([parents[:, 1:], jnp.full((micro, 1), -1, parents.dtype)], axis=1)
    on_path = (seg % 2 == 0)[None] | (after_parent == seg[None])
    below = (seg[None, :] < seg[:, None])[None]
    depth = jnp.sum(jnp.where(below, on_path.astype(F32)[:, None, :], 0.0), axis=-1)

    def row_numbers(hop):
        return (links.shard ^ hop) * rows + jnp.arange(rows)

    def pick(table, numbers):
        hit = (numbers // seg_rows)[..., None] == seg
        return jnp.sum(jnp.where(hit[None], table.reshape(micro, *(1,) * numbers.ndim, segs), 0), axis=-1)

    my_rows = row_numbers(0)
    positions = pick(depth, my_rows) * seg_rows + (my_rows % seg_rows).astype(F32)
    freqs = jnp.exp(-math.log(10000.0) * jnp.arange(HALF_HEAD, dtype=F32) * (2.0 / HEAD_SIZE))
    angles = freqs[:, None] * positions.reshape(tokens)[None, :]
    cosine_t, sine_t = jnp.cos(angles), jnp.sin(angles)
    cosine, sine = cosine_t.T, sine_t.T
    key_rows = jnp.stack([row_numbers(hop) for hop in links.hops])
    open_key = (pick(on_path.astype(F32), key_rows) > 0.5) & (
        (key_rows < links.shard * rows) | (jnp.arange(shards) == 0)[:, None]
    )
    bias = jnp.where(open_key, 0.0, CLOSED)
    bias = jnp.pad(bias, ((0, 0), (0, 8 - shards), (0, 0)))

    inputs = block_input.reshape(tokens, width).astype(F32)
    cotangent = out_cotangent.reshape(tokens, width)
    inv_first = rms_inverse(inputs)
    normed_first = inputs * inv_first
    act_first = (normed_first * gain_one).astype(BF)
    linear = nn(act_first, full_qk)
    keys = rotate(linear[:, width:], cosine, sine, KEY_VALUE_HEADS, False)
    kv = jnp.concatenate([keys, nn(act_first, full_value)], axis=1).astype(BF)
    kv_all = [links.spread(kv[m * rows : (m + 1) * rows]) for m in range(micro)]
    queries = (rotate(linear[:, :width], cosine, sine, QUERY_HEADS, False) * SCALE).astype(BF)
    attended = ()
    for m in range(micro):
        attended = attend(m, rows, seg_rows, queries, kv_all[m], bias, attended)
    attn, lse = attended

    resid = inputs + nn(attn, full_output)
    inv_second = rms_inverse(resid)
    normed_second = resid * inv_second
    act_second = (normed_second * gain_two).astype(BF)
    pair_whole = assemble(pair_got)
    full_gate, full_upper = pair_whole[:width], pair_whole[width:]
    full_down = assemble(down_got)
    gate = nn(act_second, full_gate)
    upper = nn(act_second, full_upper)
    sigmoid = jax.nn.sigmoid(gate)
    silu = gate * sigmoid
    inner = (silu * upper).astype(BF)
    block_out = (resid + nn(inner, full_down)).astype(BF)

    down_owned, down_rows = links.reduce_rows(tn(inner, cotangent))
    d_inner = nt(cotangent, full_down)
    d_gate = (d_inner * upper * sigmoid * (1.0 + gate * (1.0 - sigmoid))).astype(BF)
    d_upper = (d_inner * silu).astype(BF)
    even = links.core == 0
    kept, given = (
        tn(act_second, part).astype(BF).reshape(shards, width // shards, hidden)
        for part in (jnp.where(even, d_gate, d_upper), jnp.where(even, d_upper, d_gate))
    )
    pair_owned = links.reduce_owned(kept, given)
    d_act_second = nt(d_gate, full_gate) + nt(d_upper, full_upper)
    gain_two_sum = jnp.sum(d_act_second * normed_second, axis=0)
    d_normed = d_act_second * gain_two
    d_resid = cotangent.astype(F32) + inv_second * (
        d_normed - normed_second * jnp.mean(d_normed * normed_second, axis=-1, keepdims=True)
    )
    d_resid_low = d_resid.astype(BF)
    output_owned, output_rows = links.reduce_rows(tn(attn, d_resid_low))
    d_attn = nt(d_resid_low, full_output).astype(BF)

    d_queries, d_kv = (), []
    for m in range(micro):
        d_queries, *pieces = attend_back(
            m, rows, seg_rows, queries, kv_all[m], bias, attn, d_attn, lse, cosine_t, sine_t, d_queries
        )
        d_queries = (d_queries,)
        d_kv.append(links.collect(pieces))
    d_kv = jnp.concatenate(d_kv, axis=0).astype(F32)
    d_key_low = rotate(d_kv[:, :KV_WIDTH], cosine, sine, KEY_VALUE_HEADS, True).astype(BF)
    d_qk_low = jnp.concatenate([d_queries[0], d_key_low], axis=1)
    d_value_low = d_kv[:, KV_WIDTH:].astype(BF)
    qkv_owned, qkv_rows = links.reduce_rows(
        tn(act_first, jnp.concatenate([d_qk_low, d_value_low], axis=1))
    )
    d_act_first = nt(d_qk_low, full_qk) + nt(d_value_low, full_value)
    gain_one_sum = jnp.sum(d_act_first * normed_first, axis=0)
    d_normed = d_act_first * gain_one
    d_input = d_resid + inv_first * (
        d_normed - normed_first * jnp.mean(d_normed * normed_first, axis=-1, keepdims=True)
    )
    gain_sums = links.reduce_small(jnp.stack([gain_one_sum, gain_two_sum]))
    grad_down = links.finish_rows(down_owned, down_rows)
    grad_gate, grad_upper = links.finish_pair(pair_owned)
    grad_output = links.finish_rows(output_owned, output_rows)
    grad_qkv = links.finish_rows(qkv_owned, qkv_rows)
    return (
        block_out.reshape(micro, rows, width),
        d_input.astype(BF).reshape(micro, rows, width),
        grad_qkv[:, :width],
        grad_qkv[:, width : width + KV_WIDTH],
        grad_qkv[:, width + KV_WIDTH :],
        grad_output,
        grad_gate,
        grad_upper,
        grad_down,
        gain_sums[0],
        gain_sums[1],
    )


def solution(mesh):
    rows = P(None, AXES, None)
    weight, gain = P("shard", None), P("shard")
    return jax.shard_map(
        local,
        mesh=mesh,
        in_specs=(rows, P(None, "rep", None)) + (weight,) * 7 + (gain, gain, rows),
        out_specs=(rows, rows) + (weight,) * 7 + (gain, gain),
        check_vma=False,
    )
```

time: 775 us -> 1080 us (1.39)
  Pallas kernels: 0 us -> 662 us
  matrix products: 266 us -> 76.7 us
  local copies, waits for them, and re-layouts: 169 us -> 54.5 us
  waiting for transfers between devices: 189 us -> 133 us
  starting transfers between devices: 72.4 us -> 87.9 us
    pallas_call x0 -> x7, Pallas kernels: none -> 662 us  [the longest x3 611 us: assemble(): pl.pallas_call(functools.partial(assemble_kernel, sum((p.shape[0] for p i...]
    dot_general x70 -> x0, matrix products: 196 us -> none  [the longest x10 43.9 us: backward(): jnp.einsum('gtn,nd->gtd', d_scores, key_part, preferred_element_type=F32)]
    ppermute x85 -> x71, waiting for transfers between devices: 189 us -> 133 us  [move(): return lax.ppermute(value, AXES, pairs)]
    dynamic_update_slice x35 -> x0, local copies, waits for them, and re-layouts: 41.4 us -> none  [the longest x15 20.3 us: gather(): lax.dynamic_update_slice(whole, piece, ((self.shard ^ hop) * rows + first...]
    broadcast_in_dim x23 -> x0, local copies, waits for them, and re-layouts: 24.1 us -> none  [the longest x10 9.68 us: forward(): expo = jnp.where(allowed[None], jnp.exp(masked - peak), 0.0)]
    ppermute x85 -> x71, starting transfers between devices: 72.4 us -> 87.9 us  [move(): return lax.ppermute(value, AXES, pairs)]
    another operation x13 -> x3, local copies, waits for them, and re-layouts: 15.4 us -> 1.54 us  [the longest x2 1.33 us: assemble(): jnp.stack([jnp.int32(start) for start in starts])]
    concatenate x11 -> x1, local copies, waits for them, and re-layouts: 14.9 us -> 2.06 us  [local(): jnp.concatenate([d_qk_low, d_value_low], axis=1)]
  transfers between devices with their start and end apart: 85 -> 71, of which waited for: 25 -> 17; matrix products, arithmetic and copies ran while one was open for 22% -> 12% of each run, Pallas kernels for 0% -> 44%
where the time goes in v2:
time: 1080 us; the launch traced here: 1070 us
  Pallas kernels  662 us (61%)
  waiting for transfers between devices  133 us (12%)
  starting transfers between devices  87.9 us (8%)
  matrix products  76.7 us (7%)
  local copies, waits for them, and re-layouts  54.5 us (5%)
  other arithmetic  53.1 us (5%)
    pallas_call x3, Pallas kernels, assemble(): pl.pallas_call(functools.partial(assemble_kernel, sum((p.shape[0] for p i...  611 us
    ppermute x71, waiting for transfers between devices, move(): return lax.ppermute(value, AXES, pairs)  133 us
    ppermute x71, starting transfers between devices, move(): return lax.ppermute(value, AXES, pairs)  87.9 us
    dot_general x17, matrix products, dot(): return lax.dot_general(a, b, (dims, ((), ())), preferred_element_type=F32)  76.7 us
    pallas_call x2, Pallas kernels, attend_back(): pl.pallas_call(functools.partial(attend_back_kernel, shards, seg_rows), g...  33.1 us
    convert_element_type x24, other arithmetic, add(): return (left.astype(F32) + right.astype(F32)).astype(left.dtype)  27.2 us
  transfers between devices with their start and end apart: 71, of which 17 were waited for; matrix products, arithmetic and copies ran while one was open for 12% of the time, Pallas kernels for 44%

profile of v2, /device:TPU:0, one launch (start us, length us, event | category | flops | bytes accessed | tf_op | source)
XLA Modules:
  0.0 1069.0 jit_solution(17104377491742246785)
XLA Ops:
  2.9 2.7 broadcast_select_fusion.5
  5.6 2.9 collective-permute-start.3
  10.8 2.9 collective-permute-start.2
  17.0 6.0 collective-permute-done.3.refs_2_
  24.6 1.9 copy.256
  28.0 5.4 collective-permute-done.5.refs_4_
  34.7 2.5 collective-permute-start.15
  38.8 150.7 %assemble.3 = bf16[1920,1280]{1,0:T(8,128)(2,1)} custom-call(s32[8]{0:T(128)} %stack.116.starts_ref, bf16[240,1280]{1,0:T(8,128)(2,1)} %get-tuple-element.117.refs_0_, bf16[240,1280]{1,0:T(8,128)(2,1)} %get-tuple-element.116.refs_1_, bf16[240,1280]{1,0:T(8,128)(2,1)} %collective-permute-done.3.refs_2_, bf16[240,1280]{1,0:T(8,128)(2,1)} %collective-permute-done.4.refs_3_, ...), custom_call_target="tpu_custom_call" | custom-call | bytes 9830400 | tf_op jit(solution)/shard_map/assemble/pallas_call | solution.py:248
  189.6 3.3 fusion.21
  196.6 2.1 convolution_convert_fusion.5
  199.4 2.2 copy.257
  203.5 3.2 slice.132
  206.7 2.8 copy.205
  217.0 3.2 collective-permute-done.9.refs_1_
  222.2 2.9 copy.212.refs_0_
  228.5 8.0 attend.2
  237.2 9.3 attend.3
  248.6 2.8 multiply_reduce_fusion.4
  253.1 4.2 collective-permute-done.22.refs_2_
  257.3 7.0 collective-permute-done.23.refs_3_
  264.3 299.6 %assemble.4 = bf16[1920,2560]{1,0:T(8,128)(2,1)} custom-call(s32[8]{0:T(128)} %stack.116.starts_ref, bf16[240,2560]{1,0:T(8,128)(2,1)} %refs_0_, bf16[240,2560]{1,0:T(8,128)(2,1)} %refs_1_, bf16[240,2560]{1,0:T(8,128)(2,1)} %collective-permute-done.15.refs_2_, bf16[240,2560]{1,0:T(8,128)(2,1)} %collective-permute-done.16.refs_3_, ...), custom_call_target="tpu_custom_call" | custom-call | bytes 19660800 | tf_op jit(solution)/shard_map/assemble/pallas_call | solution.py:248
  564.0 7.1 fusion.11
  571.0 160.8 %assemble.5 = bf16[2560,960]{1,0:T(8,128)(2,1)} custom-call(s32[7]{0:T(128)} %stack.125.starts_ref, bf16[640,960]{1,0:T(8,128)(2,1)} %copy.212.refs_0_, bf16[320,960]{1,0:T(8,128)(2,1)} %collective-permute-done.21.refs_1_, bf16[320,960]{1,0:T(8,128)(2,1)} %collective-permute-done.22.refs_2_, bf16[320,960]{1,0:T(8,128)(2,1)} %collective-permute-done.23.refs_3_, ...), custom_call_target="tpu_custom_call" | custom-call | bytes 9830400 | tf_op jit(solution)/shard_map/assemble/pallas_call | solution.py:248
  731.9 7.4 fusion.85
  739.3 9.7 fusion.2
  749.0 4.0 fusion.5
  753.0 4.4 convolution_convert_fusion.2
  757.4 4.5 convolution_convert_fusion.1
  761.9 4.8 convolution_convert_fusion
  766.7 3.7 add_convert_fusion.8
  770.4 5.2 multiply_reduce_fusion
  776.2 4.6 fusion.29.refs_6_
  780.8 16.5 %attend_back.2 = (bf16[512,960]{1,0:T(8,128)(2,1)S(1)}, bf16[256,640]{1,0:T(8,128)(2,1)S(1)}, bf16[256,640]{1,0:T(8,128)(2,1)S(1)}, bf16[256,640]{1,0:T(8,128)(2,1)}, bf16[256,640]{1,0:T(8,128)(2,1)}) custom-call(bf16[512,960]{1,0:T(8,128)(2,1)S(1)} %copy.210.q_ref, bf16[256,640]{1,0:T(8,128)(2,1)S(1)} %get-tuple-element.147.refs_0_, ...), custom_call_target="tpu_custom_call" | custom-call | flops 10066329600 | bytes 983040 | tf_op jit(solution)/shard_map/attend_back/pallas_call | solution.py:398
  797.3 16.6 %attend_back.3 = (bf16[512,960]{1,0:T(8,128)(2,1)S(1)}, bf16[256,640]{1,0:T(8,128)(2,1)S(1)}, bf16[256,640]{1,0:T(8,128)(2,1)S(1)}, bf16[256,640]{1,0:T(8,128)(2,1)}, bf16[256,640]{1,0:T(8,128)(2,1)}) custom-call(bf16[512,960]{1,0:T(8,128)(2,1)S(1)} %copy.210.q_ref, ...), custom_call_target="tpu_custom_call", output_to_operand_aliasing={{0}: (11, {})} | custom-call | flops 10066329600 | bytes 983040 | tf_op jit(solution)/shard_map/attend_back/pallas_call | solution.py:398
  815.4 2.7 convolution_convert_fusion.4
  820.6 7.8 copy.243
  828.5 3.6 constant_dynamic-slice_fusion.1
  837.5 2.8 collective-permute-done.32
  841.5 2.2 collective-permute-done.29
  845.0 1.8 fusion.56
  846.9 5.4 multiply_reduce_fusion.1
  854.8 2.2 copy.263
  857.0 2.1 concatenate.73
  861.9 3.4 convolution_convert_fusion.3
  868.5 2.1 collective-permute-start.44
  870.7 3.2 collective-permute-start.68
  874.0 2.3 copy.245
  878.0 6.1 collective-permute-start.45
  884.2 4.6 fusion.47
  900.2 5.7 collective-permute-done.51
  905.9 2.5 fusion.17
  912.9 1.9 fusion.53
  914.8 21.7 %collective-permute-done.35 = bf16[128,1600]{0,1:T(8,128)(2,1)S(1)} collective-permute-done((bf16[128,1600]{0,1:T(8,128)(2,1)S(1)}, bf16[128,1600]{0,1:T(8,128)(2,1)S(1)}, u32[]{:S(2)}, u32[]{:S(2)}) %collective-permute-start.35) | collective-permute-done | bytes 409632 | tf_op jit(solution)/shard_map/ppermute | solution.py:83
  940.1 2.3 add_convert_fusion.2
  942.5 6.7 collective-permute-start.53
  949.2 3.0 collective-permute-done.36
  953.4 5.4 collective-permute-start.37
  962.1 17.4 %collective-permute-done.37 = bf16[128,1600]{0,1:T(8,128)(2,1)S(1)} collective-permute-done((bf16[128,1600]{0,1:T(8,128)(2,1)S(1)}, bf16[128,1600]{0,1:T(8,128)(2,1)S(1)}, u32[]{:S(2)}, u32[]{:S(2)}) %collective-permute-start.37) | collective-permute-done | bytes 409632 | tf_op jit(solution)/shard_map/ppermute | solution.py:83
  983.0 8.8 collective-permute-start.61
  993.3 6.6 collective-permute-done.61
  1007.9 45.2 %collective-permute-done.63 = bf16[320,960]{1,0:T(8,128)(2,1)} collective-permute-done((bf16[320,960]{1,0:T(8,128)(2,1)S(1)}, bf16[320,960]{1,0:T(8,128)(2,1)}, u32[]{:S(2)}, u32[]{:S(2)}) %collective-permute-start.63) | collective-permute-done | bytes 614432 | tf_op jit(solution)/shard_map/ppermute | solution.py:83
  1054.4 2.5 broadcast_select_fusion
  1062.5 2.0 copy.240
  1064.6 4.2 select_convert_fusion
  (370 shorter events, 103.7 us)
Async XLA Ops:
  5.6 17.4 %collective-permute-start.3 = (bf16[240,1280]{1,0:T(8,128)(2,1)}, bf16[240,1280]{1,0:T(8,128)(2,1)}, u32[]{:S(2)}, u32[]{:S(2)}) collective-permute-start(bf16[240,1280]{1,0:T(8,128)(2,1)} %get-tuple-element.115), channel_id=1, source_target_pairs={{0,1},{1,0},{2,3},{3,2},{4,6},{5,7},{6,4},{7,5},{8,9},{9,8},{10,11... | collective-permute-start | bytes 1843208 | tf_op jit(solution)/shard_map/ppermute | solution.py:83
  8.5 19.0 %collective-permute-start.4 = (bf16[240,1280]{1,0:T(8,128)(2,1)}, bf16[240,1280]{1,0:T(8,128)(2,1)}, u32[]{:S(2)}, u32[]{:S(2)}) collective-permute-start(bf16[240,1280]{1,0:T(8,128)(2,1)} %get-tuple-element.115), channel_id=1, source_target_pairs={{0,2},{1,3},{2,0},{3,1},{4,5},{5,4},{6,7},{7,6},{8,10},{9,11},{10,... | collective-permute-start | bytes 1843208 | tf_op jit(solution)/shard_map/ppermute | solution.py:83
  10.1 17.2 %collective-permute-start = (bf16[2,240]{1,0:T(2,128)(2,1)S(1)}, bf16[2,240]{1,0:T(2,128)(2,1)S(1)}, u32[]{:S(2)}, u32[]{:S(2)}) collective-permute-start(bf16[2,240]{1,0:T(2,128)(2,1)S(1)} %pad_maximum_fusion.8), channel_id=1, source_target_pairs={{0,1},{1,0},{2,3},{3,2},{4,5},{5,4},{6,7},{7,6},{8,9},{9,8},{10,11... | collective-permute-start | bytes 2888 | tf_op jit(solution)/shard_map/ppermute | solution.py:83
  10.7 16.6 %collective-permute-start.1 = (bf16[2,240]{1,0:T(2,128)(2,1)S(1)}, bf16[2,240]{1,0:T(2,128)(2,1)S(1)}, u32[]{:S(2)}, u32[]{:S(2)}) collective-permute-start(bf16[2,240]{1,0:T(2,128)(2,1)S(1)} %pad_maximum_fusion.8), channel_id=1, source_target_pairs={{0,2},{1,3},{2,0},{3,1},{4,6},{5,7},{6,4},{7,5},{8,10},{9,11},{10,... | collective-permute-start | bytes 2888 | tf_op jit(solution)/shard_map/ppermute | solution.py:83
  10.8 16.5 %collective-permute-start.2 = (bf16[2,240]{1,0:T(2,128)(2,1)S(1)}, bf16[2,240]{1,0:T(2,128)(2,1)S(1)}, u32[]{:S(2)}, u32[]{:S(2)}) collective-permute-start(bf16[2,240]{1,0:T(2,128)(2,1)S(1)} %pad_maximum_fusion.8), channel_id=1, source_target_pairs={{0,3},{1,2},{2,1},{3,0},{4,7},{5,6},{6,5},{7,4},{8,11},{9,10},{10,... | collective-permute-start | bytes 2888 | tf_op jit(solution)/shard_map/ppermute | solution.py:83
  23.0 10.5 collective-permute-start.5
  27.5 11.3 %collective-permute-start.6 = (bf16[240,1280]{1,0:T(8,128)(2,1)}, bf16[240,1280]{1,0:T(8,128)(2,1)}, u32[]{:S(2)}, u32[]{:S(2)}) collective-permute-start(bf16[240,1280]{1,0:T(8,128)(2,1)} %collective-permute-done.3.refs_2_), channel_id=1, source_target_pairs={{0,4},{1,5},{2,6},{3,7},{4,0},{5,1},{6,2},{7,3},{8,12},{9,13},{10,... | collective-permute-start | bytes 1843208 | tf_op jit(solution)/shard_map/ppermute | solution.py:83
  27.5 11.3 %collective-permute-start.7 = (bf16[240,1280]{1,0:T(8,128)(2,1)}, bf16[240,1280]{1,0:T(8,128)(2,1)}, u32[]{:S(2)}, u32[]{:S(2)}) collective-permute-start(bf16[240,1280]{1,0:T(8,128)(2,1)} %collective-permute-done.4.refs_3_), channel_id=1, source_target_pairs={{0,4},{1,5},{2,6},{3,7},{4,0},{5,1},{6,2},{7,3},{8,12},{9,13},{10,... | collective-permute-start | bytes 1843208 | tf_op jit(solution)/shard_map/ppermute | solution.py:83
  34.7 160.6 %collective-permute-start.15 = (bf16[240,2560]{1,0:T(8,128)(2,1)}, bf16[240,2560]{1,0:T(8,128)(2,1)}, u32[]{:S(2)}, u32[]{:S(2)}) collective-permute-start(bf16[240,2560]{1,0:T(8,128)(2,1)} %broadcast_select_fusion.1), channel_id=1, source_target_pairs={{0,1},{1,0},{2,3},{3,2},{4,6},{5,7},{6,4},{7,5},{8,9},{9,8},{10,11... | collective-permute-start | bytes 3686408 | tf_op jit(solution)/shard_map/ppermute | solution.py:83
  38.0 183.2 %collective-permute-start.16 = (bf16[240,2560]{1,0:T(8,128)(2,1)}, bf16[240,2560]{1,0:T(8,128)(2,1)}, u32[]{:S(2)}, u32[]{:S(2)}) collective-permute-start(bf16[240,2560]{1,0:T(8,128)(2,1)} %broadcast_select_fusion.1), channel_id=1, source_target_pairs={{0,2},{1,3},{2,0},{3,1},{4,5},{5,4},{6,7},{7,6},{8,10},{9,11},{10,... | collective-permute-start | bytes 3686408 | tf_op jit(solution)/shard_map/ppermute | solution.py:83
  195.2 26.9 %collective-permute-start.17 = (bf16[240,2560]{1,0:T(8,128)(2,1)}, bf16[240,2560]{1,0:T(8,128)(2,1)}, u32[]{:S(2)}, u32[]{:S(2)}) collective-permute-start(bf16[240,2560]{1,0:T(8,128)(2,1)} %collective-permute-done.15.refs_2_), channel_id=1, source_target_pairs={{0,2},{1,3},{2,0},{3,1},{4,5},{5,4},{6,7},{7,6},{8,10},{9,11},{10,... | collective-permute-start | bytes 3686408 | tf_op jit(solution)/shard_map/ppermute | solution.py:83
  199.2 12.0 %collective-permute-start.12 = (bf16[256,640]{1,0:T(8,128)(2,1)S(1)}, bf16[256,640]{1,0:T(8,128)(2,1)S(1)}, u32[]{:S(2)}, u32[]{:S(2)}) collective-permute-start(bf16[256,640]{1,0:T(8,128)(2,1)S(1)} %get-tuple-element.147.refs_0_), channel_id=1, source_target_pairs={{0,1},{1,0},{2,3},{3,2},{4,6},{5,7},{6,4},{7,5},{8,9},{9,8},{10,11... | collective-permute-start | bytes 983048 | tf_op jit(solution)/shard_map/ppermute | solution.py:83
  202.5 23.7 %collective-permute-start.13 = (bf16[256,640]{1,0:T(8,128)(2,1)S(1)}, bf16[256,640]{1,0:T(8,128)(2,1)S(1)}, u32[]{:S(2)}, u32[]{:S(2)}) collective-permute-start(bf16[256,640]{1,0:T(8,128)(2,1)S(1)} %get-tuple-element.147.refs_0_), channel_id=1, source_target_pairs={{0,2},{1,3},{2,0},{3,1},{4,5},{5,4},{6,7},{7,6},{8,10},{9,11},{10,... | collective-permute-start | bytes 983048 | tf_op jit(solution)/shard_map/ppermute | solution.py:83
  209.5 10.7 collective-permute-start.9
  211.2 15.6 %collective-permute-start.14 = (bf16[256,640]{1,0:T(8,128)(2,1)S(1)}, bf16[256,640]{1,0:T(8,128)(2,1)S(1)}, u32[]{:S(2)}, u32[]{:S(2)}) collective-permute-start(bf16[256,640]{1,0:T(8,128)(2,1)S(1)} %collective-permute-done.12.refs_1_), channel_id=1, source_target_pairs={{0,2},{1,3},{2,0},{3,1},{4,5},{5,4},{6,7},{7,6},{8,10},{9,11},{10,... | collective-permute-start | bytes 983048 | tf_op jit(solution)/shard_map/ppermute | solution.py:83
  220.1 16.4 %collective-permute-start.10 = (bf16[256,640]{1,0:T(8,128)(2,1)S(1)}, bf16[256,640]{1,0:T(8,128)(2,1)S(1)}, u32[]{:S(2)}, u32[]{:S(2)}) collective-permute-start(bf16[256,640]{1,0:T(8,128)(2,1)S(1)} %get-tuple-element.148.refs_0_), channel_id=1, source_target_pairs={{0,2},{1,3},{2,0},{3,1},{4,5},{5,4},{6,7},{7,6},{8,10},{9,11},{10,... | collective-permute-start | bytes 983048 | tf_op jit(solution)/shard_map/ppermute | solution.py:83
  221.2 15.9 %collective-permute-start.11 = (bf16[256,640]{1,0:T(8,128)(2,1)S(1)}, bf16[256,640]{1,0:T(8,128)(2,1)}, u32[]{:S(2)}, u32[]{:S(2)}) collective-permute-start(bf16[256,640]{1,0:T(8,128)(2,1)S(1)} %collective-permute-done.9.refs_1_), channel_id=1, source_target_pairs={{0,2},{1,3},{2,0},{3,1},{4,5},{5,4},{6,7},{7,6},{8,10},{9,11},{10,... | collective-permute-start | bytes 983048 | tf_op jit(solution)/shard_map/ppermute | solution.py:83
  222.2 30.8 %collective-permute-start.18 = (bf16[240,2560]{1,0:T(8,128)(2,1)}, bf16[240,2560]{1,0:T(8,128)(2,1)}, u32[]{:S(2)}, u32[]{:S(2)}) collective-permute-start(bf16[240,2560]{1,0:T(8,128)(2,1)} %collective-permute-done.15.refs_2_), channel_id=1, source_target_pairs={{0,4},{1,5},{2,6},{3,7},{4,0},{5,1},{6,2},{7,3},{8,12},{9,13},{10,... | collective-permute-start | bytes 3686408 | tf_op jit(solution)/shard_map/ppermute | solution.py:83
  226.2 38.1 %collective-permute-start.19 = (bf16[240,2560]{1,0:T(8,128)(2,1)}, bf16[240,2560]{1,0:T(8,128)(2,1)}, u32[]{:S(2)}, u32[]{:S(2)}) collective-permute-start(bf16[240,2560]{1,0:T(8,128)(2,1)} %collective-permute-done.16.refs_3_), channel_id=1, source_target_pairs={{0,4},{1,5},{2,6},{3,7},{4,0},{5,1},{6,2},{7,3},{8,12},{9,13},{10,... | collective-permute-start | bytes 3686408 | tf_op jit(solution)/shard_map/ppermute | solution.py:83
  226.8 21.3 %collective-permute-start.21 = (bf16[320,960]{1,0:T(8,128)(2,1)S(1)}, bf16[320,960]{1,0:T(8,128)(2,1)}, u32[]{:S(2)}, u32[]{:S(2)}) collective-permute-start(bf16[320,960]{1,0:T(8,128)(2,1)S(1)} %constant_dynamic-slice_fusion.13), channel_id=1, source_target_pairs={{0,1},{1,0},{2,3},{3,2},{4,6},{5,7},{6,4},{7,5},{8,9},{9,8},{10,11... | collective-permute-start | bytes 1843208 | tf_op jit(solution)/shard_map/ppermute | solution.py:83
  236.6 27.7 %collective-permute-start.20 = (bf16[240,2560]{1,0:T(8,128)(2,1)}, bf16[240,2560]{1,0:T(8,128)(2,1)}, u32[]{:S(2)}, u32[]{:S(2)}) collective-permute-start(bf16[240,2560]{1,0:T(8,128)(2,1)} %collective-permute-done.17.refs_4_), channel_id=1, source_target_pairs={{0,4},{1,5},{2,6},{3,7},{4,0},{5,1},{6,2},{7,3},{8,12},{9,13},{10,... | collective-permute-start | bytes 3686408 | tf_op jit(solution)/shard_map/ppermute | solution.py:83
  246.5 10.8 %collective-permute-start.22 = (bf16[320,960]{1,0:T(8,128)(2,1)S(1)}, bf16[320,960]{1,0:T(8,128)(2,1)}, u32[]{:S(2)}, u32[]{:S(2)}) collective-permute-start(bf16[320,960]{1,0:T(8,128)(2,1)S(1)} %constant_dynamic-slice_fusion.13), channel_id=1, source_target_pairs={{0,2},{1,3},{2,0},{3,1},{4,5},{5,4},{6,7},{7,6},{8,10},{9,11},{10,... | collective-permute-start | bytes 1843208 | tf_op jit(solution)/shard_map/ppermute | solution.py:83
  248.1 16.2 %collective-permute-start.23 = (bf16[320,960]{1,0:T(8,128)(2,1)}, bf16[320,960]{1,0:T(8,128)(2,1)}, u32[]{:S(2)}, u32[]{:S(2)}) collective-permute-start(bf16[320,960]{1,0:T(8,128)(2,1)} %collective-permute-done.21.refs_1_), channel_id=1, source_target_pairs={{0,2},{1,3},{2,0},{3,1},{4,5},{5,4},{6,7},{7,6},{8,10},{9,11},{10,... | collective-permute-start | bytes 1843208 | tf_op jit(solution)/shard_map/ppermute | solution.py:83
  253.0 318.1 %collective-permute-start.24 = (bf16[320,960]{1,0:T(8,128)(2,1)}, bf16[320,960]{1,0:T(8,128)(2,1)}, u32[]{:S(2)}, u32[]{:S(2)}) collective-permute-start(bf16[320,960]{1,0:T(8,128)(2,1)} %collective-permute-done.21.refs_1_), channel_id=1, source_target_pairs={{0,4},{1,5},{2,6},{3,7},{4,0},{5,1},{6,2},{7,3},{8,12},{9,13},{10,... | collective-permute-start | bytes 1843208 | tf_op jit(solution)/shard_map/ppermute | solution.py:83
  257.3 313.8 %collective-permute-start.25 = (bf16[320,960]{1,0:T(8,128)(2,1)}, bf16[320,960]{1,0:T(8,128)(2,1)}, u32[]{:S(2)}, u32[]{:S(2)}) collective-permute-start(bf16[320,960]{1,0:T(8,128)(2,1)} %collective-permute-done.22.refs_2_), channel_id=1, source_target_pairs={{0,4},{1,5},{2,6},{3,7},{4,0},{5,1},{6,2},{7,3},{8,12},{9,13},{10,... | collective-permute-start | bytes 1843208 | tf_op jit(solution)/shard_map/ppermute | solution.py:83
  264.3 306.7 %collective-permute-start.26 = (bf16[320,960]{1,0:T(8,128)(2,1)}, bf16[320,960]{1,0:T(8,128)(2,1)}, u32[]{:S(2)}, u32[]{:S(2)}) collective-permute-start(bf16[320,960]{1,0:T(8,128)(2,1)} %collective-permute-done.23.refs_3_), channel_id=1, source_target_pairs={{0,4},{1,5},{2,6},{3,7},{4,0},{5,1},{6,2},{7,3},{8,12},{9,13},{10,... | collective-permute-start | bytes 1843208 | tf_op jit(solution)/shard_map/ppermute | solution.py:83
  813.9 18.2 %collective-permute-start.31 = (bf16[256,640]{1,0:T(8,128)(2,1)}, bf16[256,640]{1,0:T(8,128)(2,1)S(1)}, u32[]{:S(2)}, u32[]{:S(2)}) collective-permute-start(bf16[256,640]{1,0:T(8,128)(2,1)} %get-tuple-element.44), channel_id=1, source_target_pairs={{0,2},{1,3},{2,0},{3,1},{4,5},{5,4},{6,7},{7,6},{8,10},{9,11},{10,... | collective-permute-start | bytes 983048 | tf_op jit(solution)/shard_map/ppermute | solution.py:83
  818.1 19.4 %collective-permute-start.30 = (bf16[256,640]{1,0:T(8,128)(2,1)}, bf16[256,640]{1,0:T(8,128)(2,1)}, u32[]{:S(2)}, u32[]{:S(2)}) collective-permute-start(bf16[256,640]{1,0:T(8,128)(2,1)} %get-tuple-element.42), channel_id=1, source_target_pairs={{0,2},{1,3},{2,0},{3,1},{4,5},{5,4},{6,7},{7,6},{8,10},{9,11},{10,... | collective-permute-start | bytes 983048 | tf_op jit(solution)/shard_map/ppermute | solution.py:83
  818.6 14.8 %collective-permute-start.28 = (bf16[256,640]{1,0:T(8,128)(2,1)}, bf16[256,640]{1,0:T(8,128)(2,1)S(1)}, u32[]{:S(2)}, u32[]{:S(2)}) collective-permute-start(bf16[256,640]{1,0:T(8,128)(2,1)} %get-tuple-element.40), channel_id=1, source_target_pairs={{0,2},{1,3},{2,0},{3,1},{4,5},{5,4},{6,7},{7,6},{8,10},{9,11},{10,... | collective-permute-start | bytes 983048 | tf_op jit(solution)/shard_map/ppermute | solution.py:83
  820.1 21.4 %collective-permute-start.27 = (bf16[256,640]{1,0:T(8,128)(2,1)}, bf16[256,640]{1,0:T(8,128)(2,1)S(1)}, u32[]{:S(2)}, u32[]{:S(2)}) collective-permute-start(bf16[256,640]{1,0:T(8,128)(2,1)} %get-tuple-element.38), channel_id=1, source_target_pairs={{0,2},{1,3},{2,0},{3,1},{4,5},{5,4},{6,7},{7,6},{8,10},{9,11},{10,... | collective-permute-start | bytes 983048 | tf_op jit(solution)/shard_map/ppermute | solution.py:83
  828.5 55.7 %collective-permute-start.49 = (bf16[4,240,2560]{2,1,0:T(8,128)(2,1)}, bf16[4,240,2560]{2,1,0:T(8,128)(2,1)}, u32[]{:S(2)}, u32[]{:S(2)}) collective-permute-start(bf16[4,240,2560]{2,1,0:T(8,128)(2,1)} %bitcast.217), channel_id=1, source_target_pairs={{0,4},{1,5},{2,6},{3,7},{4,0},{5,1},{6,2},{7,3},{8,12},{9,13},{10,... | collective-permute-start | bytes 14745608 | tf_op jit(solution)/shard_map/ppermute | solution.py:83
  832.9 7.4 collective-permute-start.32
  834.3 9.4 collective-permute-start.29
  837.5 74.6 %collective-permute-start.57 = (bf16[4,320,960]{2,1,0:T(8,128)(2,1)}, bf16[4,320,960]{2,1,0:T(8,128)(2,1)}, u32[]{:S(2)}, u32[]{:S(2)}) collective-permute-start(bf16[4,320,960]{2,1,0:T(8,128)(2,1)} %constant_dynamic-slice_fusion.1), channel_id=1, source_target_pairs={{0,4},{1,5},{2,6},{3,7},{4,0},{5,1},{6,2},{7,3},{8,12},{9,13},{10,... | collective-permute-start | bytes 7372808 | tf_op jit(solution)/shard_map/ppermute | solution.py:83
  840.2 19.5 %collective-permute-start.41 = (bf16[4,128,960]{1,2,0:T(8,128)(2,1)}, bf16[4,128,960]{1,2,0:T(8,128)(2,1)}, u32[]{:S(2)}, u32[]{:S(2)}) collective-permute-start(bf16[4,128,960]{1,2,0:T(8,128)(2,1)} %copy.250), channel_id=1, source_target_pairs={{0,4},{1,5},{2,6},{3,7},{4,0},{5,1},{6,2},{7,3},{8,12},{9,13},{10,... | collective-permute-start | bytes 2949128 | tf_op jit(solution)/shard_map/ppermute | solution.py:83
  852.3 6.7 collective-permute-start.65
  859.1 6.3 collective-permute-start.66
  860.9 6.5 collective-permute-start.43
  866.5 9.7 collective-permute-start.42
  868.5 8.4 collective-permute-start.44
  876.2 32.5 %collective-permute-start.33 = (bf16[4,128,1600]{1,2,0:T(8,128)(2,1)}, bf16[4,128,1600]{1,2,0:T(8,128)(2,1)}, u32[]{:S(2)}, u32[]{:S(2)}) collective-permute-start(bf16[4,128,1600]{1,2,0:T(8,128)(2,1)} %copy.245), channel_id=1, source_target_pairs={{0,4},{1,5},{2,6},{3,7},{4,0},{5,1},{6,2},{7,3},{8,12},{9,13},{10,... | collective-permute-start | bytes 4915208 | tf_op jit(solution)/shard_map/ppermute | solution.py:83
  876.3 13.8 %collective-permute-start.69 = (f32[2,960]{1,0:T(2,128)S(1)}, f32[2,960]{1,0:T(2,128)S(1)}, u32[]{:S(2)}, u32[]{:S(2)}) collective-permute-start(f32[2,960]{1,0:T(2,128)S(1)} %add.604), channel_id=1, source_target_pairs={{8,16},{9,17},{10,18},{11,19},{12,20},{13,21},{14,22},{15,23},{16,... | collective-permute-start | bytes 23048 | tf_op jit(solution)/shard_map/ppermute | solution.py:83
  878.0 13.5 %collective-permute-start.45 = (bf16[128,960]{0,1:T(8,128)(2,1)S(1)}, bf16[128,960]{0,1:T(8,128)(2,1)S(1)}, u32[]{:S(2)}, u32[]{:S(2)}) collective-permute-start(bf16[128,960]{0,1:T(8,128)(2,1)S(1)} %add_convert_fusion.31), channel_id=1, source_target_pairs={{0,8},{1,9},{2,10},{3,11},{4,12},{5,13},{6,14},{7,15},{24,16},{25,... | collective-permute-start | bytes 737288 | tf_op jit(solution)/shard_map/ppermute | solution.py:83
  888.8 17.0 %collective-permute-start.51 = (bf16[240,2560]{1,0:T(8,128)(2,1)}, bf16[240,2560]{1,0:T(8,128)(2,1)}, u32[]{:S(2)}, u32[]{:S(2)}) collective-permute-start(bf16[240,2560]{1,0:T(8,128)(2,1)} %get-tuple-element.122), channel_id=1, source_target_pairs={{0,2},{1,3},{2,0},{3,1},{4,5},{5,4},{6,7},{7,6},{8,10},{9,11},{10,... | collective-permute-start | bytes 3686408 | tf_op jit(solution)/shard_map/ppermute | solution.py:83
  897.3 14.6 %collective-permute-start.47 = (bf16[128,960]{0,1:T(8,128)(2,1)S(1)}, bf16[128,960]{0,1:T(8,128)(2,1)S(1)}, u32[]{:S(2)}, u32[]{:S(2)}) collective-permute-start(bf16[128,960]{0,1:T(8,128)(2,1)S(1)} %add_convert_fusion.29), channel_id=1, source_target_pairs={{8,0},{9,1},{10,2},{11,3},{12,4},{13,5},{14,6},{15,7},{16,24},{17,... | collective-permute-start | bytes 737288 | tf_op jit(solution)/shard_map/ppermute | solution.py:83
  898.8 39.6 %collective-permute-start.50 = (bf16[240,2560]{1,0:T(8,128)(2,1)S(1)}, bf16[240,2560]{1,0:T(8,128)(2,1)S(1)}, u32[]{:S(2)}, u32[]{:S(2)}) collective-permute-start(bf16[240,2560]{1,0:T(8,128)(2,1)S(1)} %copy-done.35), channel_id=1, source_target_pairs={{0,2},{1,3},{2,0},{3,1},{4,5},{5,4},{6,7},{7,6},{8,10},{9,11},{10,... | collective-permute-start | bytes 3686408 | tf_op jit(solution)/shard_map/ppermute | solution.py:83
  908.3 31.4 %collective-permute-start.52 = (bf16[240,2560]{1,0:T(8,128)(2,1)S(1)}, bf16[240,2560]{1,0:T(8,128)(2,1)S(1)}, u32[]{:S(2)}, u32[]{:S(2)}) collective-permute-start(bf16[240,2560]{1,0:T(8,128)(2,1)S(1)} %fusion.17), channel_id=1, source_target_pairs={{0,1},{1,0},{2,3},{3,2},{4,6},{5,7},{6,4},{7,5},{8,9},{9,8},{10,11... | collective-permute-start | bytes 3686408 | tf_op jit(solution)/shard_map/ppermute | solution.py:83
  910.1 26.4 %collective-permute-start.35 = (bf16[128,1600]{0,1:T(8,128)(2,1)S(1)}, bf16[128,1600]{0,1:T(8,128)(2,1)S(1)}, u32[]{:S(2)}, u32[]{:S(2)}) collective-permute-start(bf16[128,1600]{0,1:T(8,128)(2,1)S(1)} %get-tuple-element.138), channel_id=1, source_target_pairs={{0,2},{1,3},{2,0},{3,1},{4,5},{5,4},{6,7},{7,6},{8,10},{9,11},{10,... | collective-permute-start | bytes 1228808 | tf_op jit(solution)/shard_map/ppermute | solution.py:83
  912.0 46.8 %collective-permute-start.48 = (bf16[128,960]{0,1:T(8,128)(2,1)S(1)}, bf16[128,960]{0,1:T(8,128)(2,1)S(1)}, u32[]{:S(2)}, u32[]{:S(2)}) collective-permute-start(bf16[128,960]{0,1:T(8,128)(2,1)S(1)} %broadcast_select_fusion.8), channel_id=1, source_target_pairs={{0,4},{1,5},{2,6},{3,7},{4,0},{5,1},{6,2},{7,3},{8,12},{9,13},{10,... | collective-permute-start | bytes 737288 | tf_op jit(solution)/shard_map/ppermute | solution.py:83
  912.1 30.4 %collective-permute-start.34 = (bf16[128,1600]{0,1:T(8,128)(2,1)S(1)}, bf16[128,1600]{0,1:T(8,128)(2,1)S(1)}, u32[]{:S(2)}, u32[]{:S(2)}) collective-permute-start(bf16[128,1600]{0,1:T(8,128)(2,1)S(1)} %get-tuple-element.137), channel_id=1, source_target_pairs={{0,2},{1,3},{2,0},{3,1},{4,5},{5,4},{6,7},{7,6},{8,10},{9,11},{10,... | collective-permute-start | bytes 1228808 | tf_op jit(solution)/shard_map/ppermute | solution.py:83
  936.5 22.4 %collective-permute-start.59 = (bf16[320,960]{1,0:T(8,128)(2,1)S(1)}, bf16[320,960]{1,0:T(8,128)(2,1)S(1)}, u32[]{:S(2)}, u32[]{:S(2)}) collective-permute-start(bf16[320,960]{1,0:T(8,128)(2,1)S(1)} %get-tuple-element.124), channel_id=1, source_target_pairs={{0,2},{1,3},{2,0},{3,1},{4,5},{5,4},{6,7},{7,6},{8,10},{9,11},{10,... | collective-permute-start | bytes 1843208 | tf_op jit(solution)/shard_map/ppermute | solution.py:83
  938.4 42.9 %collective-permute-start.58 = (bf16[320,960]{1,0:T(8,128)(2,1)S(1)}, bf16[320,960]{1,0:T(8,128)(2,1)S(1)}, u32[]{:S(2)}, u32[]{:S(2)}) collective-permute-start(bf16[320,960]{1,0:T(8,128)(2,1)S(1)} %get-tuple-element.123), channel_id=1, source_target_pairs={{0,2},{1,3},{2,0},{3,1},{4,5},{5,4},{6,7},{7,6},{8,10},{9,11},{10,... | collective-permute-start | bytes 1843208 | tf_op jit(solution)/shard_map/ppermute | solution.py:83
  939.8 12.4 %collective-permute-start.36 = (bf16[128,1600]{0,1:T(8,128)(2,1)S(1)}, bf16[128,1600]{0,1:T(8,128)(2,1)S(1)}, u32[]{:S(2)}, u32[]{:S(2)}) collective-permute-start(bf16[128,1600]{0,1:T(8,128)(2,1)S(1)} %fusion.50), channel_id=1, source_target_pairs={{0,1},{1,0},{2,3},{3,2},{4,6},{5,7},{6,4},{7,5},{8,9},{9,8},{10,11... | collective-permute-start | bytes 1228808 | tf_op jit(solution)/shard_map/ppermute | solution.py:83
  942.5 37.8 %collective-permute-start.53 = (bf16[240,2560]{1,0:T(8,128)(2,1)S(1)}, bf16[240,2560]{1,0:T(8,128)(2,1)S(1)}, u32[]{:S(2)}, u32[]{:S(2)}) collective-permute-start(bf16[240,2560]{1,0:T(8,128)(2,1)S(1)} %add_convert_fusion.2), channel_id=1, source_target_pairs={{0,8},{1,9},{2,10},{3,11},{4,12},{5,13},{6,14},{7,15},{24,16},{25,... | collective-permute-start | bytes 3686408 | tf_op jit(solution)/shard_map/ppermute | solution.py:83
  953.4 26.1 %collective-permute-start.37 = (bf16[128,1600]{0,1:T(8,128)(2,1)S(1)}, bf16[128,1600]{0,1:T(8,128)(2,1)S(1)}, u32[]{:S(2)}, u32[]{:S(2)}) collective-permute-start(bf16[128,1600]{0,1:T(8,128)(2,1)S(1)} %add_convert_fusion.18), channel_id=1, source_target_pairs={{0,8},{1,9},{2,10},{3,11},{4,12},{5,13},{6,14},{7,15},{24,16},{25,... | collective-permute-start | bytes 1228808 | tf_op jit(solution)/shard_map/ppermute | solution.py:83
  960.3 21.0 %collective-permute-start.60 = (bf16[320,960]{1,0:T(8,128)(2,1)S(1)}, bf16[320,960]{1,0:T(8,128)(2,1)S(1)}, u32[]{:S(2)}, u32[]{:S(2)}) collective-permute-start(bf16[320,960]{1,0:T(8,128)(2,1)S(1)} %fusion.44), channel_id=1, source_target_pairs={{0,1},{1,0},{2,3},{3,2},{4,6},{5,7},{6,4},{7,5},{8,9},{9,8},{10,11... | collective-permute-start | bytes 1843208 | tf_op jit(solution)/shard_map/ppermute | solution.py:83
  979.6 12.3 %collective-permute-start.38 = (bf16[128,1600]{0,1:T(8,128)(2,1)S(1)}, bf16[128,1600]{0,1:T(8,128)(2,1)S(1)}, u32[]{:S(2)}, u32[]{:S(2)}) collective-permute-start(bf16[128,1600]{0,1:T(8,128)(2,1)S(1)} %add_convert_fusion.17), channel_id=1, source_target_pairs={{8,16},{9,17},{10,18},{11,19},{12,20},{13,21},{14,22},{15,23},{16,... | collective-permute-start | bytes 1228808 | tf_op jit(solution)/shard_map/ppermute | solution.py:83
  980.6 20.3 %collective-permute-start.54 = (bf16[240,2560]{1,0:T(8,128)(2,1)S(1)}, bf16[240,2560]{1,0:T(8,128)(2,1)S(1)}, u32[]{:S(2)}, u32[]{:S(2)}) collective-permute-start(bf16[240,2560]{1,0:T(8,128)(2,1)S(1)} %add_convert_fusion.1), channel_id=1, source_target_pairs={{8,16},{9,17},{10,18},{11,19},{12,20},{13,21},{14,22},{15,23},{16,... | collective-permute-start | bytes 3686408 | tf_op jit(solution)/shard_map/ppermute | solution.py:83
  983.0 16.9 %collective-permute-start.61 = (bf16[320,960]{1,0:T(8,128)(2,1)S(1)}, bf16[320,960]{1,0:T(8,128)(2,1)S(1)}, u32[]{:S(2)}, u32[]{:S(2)}) collective-permute-start(bf16[320,960]{1,0:T(8,128)(2,1)S(1)} %add_convert_fusion.11), channel_id=1, source_target_pairs={{0,8},{1,9},{2,10},{3,11},{4,12},{5,13},{6,14},{7,15},{24,16},{25,... | collective-permute-start | bytes 1843208 | tf_op jit(solution)/shard_map/ppermute | solution.py:83
  992.0 11.7 %collective-permute-start.39 = (bf16[128,1600]{0,1:T(8,128)(2,1)S(1)}, bf16[128,1600]{0,1:T(8,128)(2,1)S(1)}, u32[]{:S(2)}, u32[]{:S(2)}) collective-permute-start(bf16[128,1600]{0,1:T(8,128)(2,1)S(1)} %add_convert_fusion.16), channel_id=1, source_target_pairs={{8,0},{9,1},{10,2},{11,3},{12,4},{13,5},{14,6},{15,7},{16,24},{17,... | collective-permute-start | bytes 1228808 | tf_op jit(solution)/shard_map/ppermute | solution.py:83
  1001.1 53.2 %collective-permute-start.55 = (bf16[240,2560]{1,0:T(8,128)(2,1)S(1)}, bf16[240,2560]{1,0:T(8,128)(2,1)}, u32[]{:S(2)}, u32[]{:S(2)}) collective-permute-start(bf16[240,2560]{1,0:T(8,128)(2,1)S(1)} %add_convert_fusion), channel_id=1, source_target_pairs={{8,0},{9,1},{10,2},{11,3},{12,4},{13,5},{14,6},{15,7},{16,24},{17,... | collective-permute-start | bytes 3686408 | tf_op jit(solution)/shard_map/ppermute | solution.py:83
  1004.1 49.0 %collective-permute-start.63 = (bf16[320,960]{1,0:T(8,128)(2,1)S(1)}, bf16[320,960]{1,0:T(8,128)(2,1)}, u32[]{:S(2)}, u32[]{:S(2)}) collective-permute-start(bf16[320,960]{1,0:T(8,128)(2,1)S(1)} %add_convert_fusion.9), channel_id=1, source_target_pairs={{8,0},{9,1},{10,2},{11,3},{12,4},{13,5},{14,6},{15,7},{16,24},{17,... | collective-permute-start | bytes 1843208 | tf_op jit(solution)/shard_map/ppermute | solution.py:83
  1054.3 6.8 collective-permute-start.64
  1056.8 7.7 collective-permute-start.56
  (69 other events, 1475.1 us)

commit v3 on v2

--- a/solution.py
+++ b/solution.py
@@ -21,6 +21,7 @@
 F32 = jnp.float32
 CLOSED = -1e30
 VMEM_LIMIT = 48 << 20
+VMEM_MOST = 60 << 20
 
 
 def dot(a, b, dims):
@@ -130,28 +131,23 @@
     def twin(self, piece):
         return piece if self.bits < 2 else piece >> 2 << 2 | (piece & 1) << 1 | (piece >> 1 & 1)
 
-    def half_rows(self, rows):
-        half = -(-rows // 32) * 16
-        return half, self.core * (rows - half), (1 - self.core) * (rows - half)
-
     def gather_rows(self, shard_value):
         rows = shard_value.shape[0]
-        half, first, second = self.half_rows(rows)
-        mine = lax.dynamic_slice_in_dim(shard_value, first, half, 0)
-        pieces = self.spread(mine)[1:]
-        others = [self.swap(piece) for piece in pieces]
+        half = rows // 2
+        mine = lax.dynamic_slice_in_dim(shard_value, self.core * half, half, 0)
+        direct = self.spread(mine)[1:]
         starts = [self.shard * rows]
-        starts += [(self.shard ^ hop) * rows + first for hop in self.hops[1:]]
+        starts += [(self.shard ^ hop) * rows + self.core * half for hop in self.hops[1:]]
         starts += [
-            (self.shard ^ self.hops[self.twin(t)]) * rows + second for t in range(1, self.shards)
+            (self.shard ^ self.hops[self.twin(t)]) * rows + (1 - self.core) * half
+            for t in range(1, self.shards)
         ]
-        return pieces, (shard_value, *pieces, *others), starts, rows * self.shards
+        return direct, *joined((shard_value, *direct, *map(self.swap, direct)), starts)
 
     def gather_pair(self, left, right):
         rows = left.shape[0]
         mine = jnp.where(self.core == 0, left, right)
-        pieces = self.spread(mine)[1:]
-        others = [self.swap(piece) for piece in pieces]
+        direct = self.spread(mine)[1:]
         whole = rows * self.shards
         first, second = self.core * whole, (1 - self.core) * whole
         starts = [self.shard * rows, whole + self.shard * rows]
@@ -159,7 +155,7 @@
         starts += [
             (self.shard ^ self.hops[self.twin(t)]) * rows + second for t in range(1, self.shards)
         ]
-        return pieces, (left, right, *pieces, *others), starts, 2 * whole
+        return direct, *joined((left, right, *direct, *map(self.swap, direct)), starts)
 
     def gather_small(self, value):
         pieces = jnp.stack(
@@ -173,36 +169,26 @@
         pieces = jnp.sum(jnp.where(hit, pieces[None], 0), axis=1, dtype=value.dtype)
         return jnp.concatenate([pieces[j] for j in range(self.shards)], axis=-1)
 
-    def reduce_owned(self, kept, given):
-        received = self.swap(given)
-        pieces = []
-        for hop in self.hops:
-            mine, theirs = (
-                lax.dynamic_index_in_dim(part, self.shard ^ hop, 0, keepdims=False)
-                for part in (kept, received)
-            )
-            pieces.append(add(mine, theirs))
-        return self.collect(pieces)
-
-    def reduce_rows(self, grad):
-        rows = grad.shape[0] // self.shards
-        half, first, second = self.half_rows(rows)
-        parts = grad.astype(BF).reshape(self.shards, rows, grad.shape[1])
-        kept = lax.dynamic_slice_in_dim(parts, first, half, 1)
-        given = lax.dynamic_slice_in_dim(parts, second, half, 1)
-        return self.reduce_owned(kept, given), rows
-
-    def finish_rows(self, owned, rows):
-        owned = self.chain(owned)
-        other = self.swap(owned)
+    def half_rows(self, rows):
+        half = -(-rows // 32) * 16
+        return half, self.core * (rows - half), (1 - self.core) * (rows - half)
+
+    def order(self, scale, mine, theirs):
+        kept = [(self.shard ^ hop) * scale + mine for hop in self.hops]
+        given = [(self.shard ^ self.hops[self.twin(t)]) * scale + theirs for t in range(self.shards)]
+        return kept, given
+
+    def reduce_owned(self, kept, received):
+        block = kept.shape[0] // self.shards
+        cut = lambda value, t: value[t * block : (t + 1) * block]
+        return self.collect([add(cut(kept, t), cut(received, t)) for t in range(self.shards)])
+
+    def finish_rows(self, owned, other, rows):
         low = jnp.where(self.core == 0, owned, other)
         high = jnp.where(self.core == 0, other, owned)
-        half = owned.shape[0]
-        return jnp.concatenate([low[: rows - half], high], axis=0).astype(F32)
-
-    def finish_pair(self, owned):
-        owned = self.chain(owned)
-        other = self.swap(owned)
+        return jnp.concatenate([low[: rows - owned.shape[0]], high], axis=0).astype(F32)
+
+    def finish_pair(self, owned, other):
         left = jnp.where(self.core == 0, owned, other)
         right = jnp.where(self.core == 0, other, owned)
         return left.astype(F32), right.astype(F32)
@@ -216,48 +202,315 @@
         return lax.dynamic_slice_in_dim(summed, self.shard * width, width, 1)
 
 
-def assemble_kernel(at_once, starts_ref, *refs):
-    count = (len(refs) - 2)
-    pieces, whole, sems = refs[:count], refs[count], refs[count + 1]
+def joined(pieces, starts):
+    if any(piece.shape[0] % 16 for piece in pieces):
+        rows = sum(piece.shape[0] for piece in pieces)
+        whole = jnp.zeros((rows, pieces[0].shape[1]), pieces[0].dtype)
+        for piece, start in zip(pieces, starts):
+            whole = lax.dynamic_update_slice(whole, piece, (start, 0))
+        pieces, starts = (whole,), [0]
+    return pieces, numbers(starts)
+
+
+def numbers(values):
+    return jnp.stack([jnp.asarray(value, jnp.int32) for value in values])
+
+
+def joined_shape(pieces):
+    return sum(piece.shape[0] for piece in pieces), pieces[0].shape[1]
+
+
+def load(pieces, starts_ref, whole, sems):
     copies = []
     for i, piece in enumerate(pieces):
         start = pl.multiple_of(starts_ref[i], 16)
         copies.append(
             pltpu.make_async_copy(piece, whole.at[pl.ds(start, piece.shape[0]), :], sems.at[i])
         )
-    if at_once:
-        for copy in copies:
-            copy.start()
-        for copy in copies:
-            copy.wait()
-    else:
-        for copy in copies:
-            copy.start()
-            copy.wait()
-
-
-def assemble(gathered):
-    _, pieces, starts, rows = gathered
-    columns = pieces[0].shape[1]
-    if any(piece.shape[0] % 16 for piece in pieces):
-        whole = jnp.zeros((rows, columns), pieces[0].dtype)
-        for piece, start in zip(pieces, starts):
-            whole = lax.dynamic_update_slice(whole, piece, (start, 0))
-        return whole
-    out = jax.ShapeDtypeStruct((rows, columns), pieces[0].dtype)
+        copies[-1].start()
+    return copies
+
+
+def wait(copies):
+    for copy in copies:
+        copy.wait()
+
+
+IN_VMEM = pl.BlockSpec(memory_space=pltpu.VMEM)
+IN_SMEM = pl.BlockSpec(memory_space=pltpu.SMEM)
+ANYWHERE = pl.BlockSpec(memory_space=pl.ANY)
+
+
+def turn(chunk, cosine, sine):
+    lane = lax.broadcasted_iota(jnp.int32, chunk.shape, 1)
+    partner = jnp.where(
+        lane % HEAD_SIZE < HALF_HEAD,
+        pltpu.roll(chunk, 128 - HALF_HEAD, 1),
+        pltpu.roll(chunk, HALF_HEAD, 1),
+    )
+    return chunk * cosine + partner * sine
+
+
+def project_kernel(count, starts_ref, x_ref, gains_ref, cos_ref, sin_ref, *refs):
+    pieces = refs[:count]
+    q_ref, kv_ref, act_ref, whole, sems = refs[count:]
+    copies = load(pieces, starts_ref, whole, sems)
+    x = x_ref[...].astype(F32)
+    width = x.shape[1]
+    act_ref[...] = (x * rms_inverse(x) * gains_ref[0:1, :]).astype(BF)
+    wait(copies)
+    act = act_ref[...]
+    cosine, sine = cos_ref[...], sin_ref[...]
+    for first in range(0, width + KV_WIDTH, 256):
+        linear = nn(act, whole[:width, first : first + 256])
+        for at in range(first, first + 256, 128):
+            chunk = turn(linear[:, at - first : at - first + 128], cosine, sine)
+            if at + 128 <= width:
+                q_ref[:, at : at + 128] = (chunk * SCALE).astype(BF)
+            elif at < width:
+                q_ref[:, at:width] = (chunk[:, : width - at] * SCALE).astype(BF)
+                kv_ref[:, : at + 128 - width] = chunk[:, width - at :].astype(BF)
+            else:
+                kv_ref[:, at - width : at - width + 128] = chunk.astype(BF)
+    kv_ref[:, KV_WIDTH:] = nn(act, whole[width:, width:]).astype(BF)
+
+
+def project(x, gains, cosine, sine, pieces, starts):
+    tokens, width = x.shape
+    outs = (
+        jax.ShapeDtypeStruct((tokens, width), BF),
+        jax.ShapeDtypeStruct((tokens, 2 * KV_WIDTH), BF),
+        jax.ShapeDtypeStruct((tokens, width), BF),
+    )
     return pl.pallas_call(
-        functools.partial(assemble_kernel, sum(p.shape[0] for p in pieces) == rows),
+        functools.partial(project_kernel, len(pieces)),
+        name="project",
+        in_specs=[IN_SMEM] + [IN_VMEM] * 4 + [ANYWHERE] * len(pieces),
+        out_specs=(IN_VMEM,) * 3,
+        out_shape=outs,
+        scratch_shapes=[
+            pltpu.VMEM(joined_shape(pieces), BF),
+            pltpu.SemaphoreType.DMA((len(pieces),)),
+        ],
+        cost_estimate=cost(2 * tokens * width * (width + 2 * KV_WIDTH), 0, x, *outs, *pieces),
+        compiler_params=pltpu.CompilerParams(vmem_limit_bytes=VMEM_LIMIT),
+    )(starts, x, gains, cosine, sine, *pieces)
+
+
+def feed_kernel(counts, s0_ref, s1_ref, s2_ref, x_ref, attn_ref, dy_ref, gains_ref, *refs):
+    total = sum(counts)
+    attention_pieces = refs[: counts[0]]
+    pair_pieces = refs[counts[0] : counts[0] + counts[1]]
+    down_pieces = refs[counts[0] + counts[1] : total]
+    out_ref, inner_ref, slopes_ref, act_ref, dres_ref, low_ref, dattn_ref, gain_ref = refs[total : total + 8]
+    w_attn, w_pair, w_down, resid_ref, dact_ref, sems0, sems1, sems2 = refs[total + 8 :]
+    attention_copies = load(attention_pieces, s0_ref, w_attn, sems0)
+    pair_copies = load(pair_pieces, s1_ref, w_pair, sems1)
+    down_copies = load(down_pieces, s2_ref, w_down, sems2)
+    tokens, width = x_ref.shape
+    hidden = w_pair.shape[1]
+    tile = hidden // 5
+    gain = gains_ref[1:2, :]
+    wait(attention_copies)
+    w_output = w_attn[width:, :width]
+    resid = x_ref[...].astype(F32) + nn(attn_ref[...], w_output)
+    resid_ref[...] = resid
+    dres_ref[...] = resid
+    root = rms_inverse(resid)
+    act_ref[...] = (resid * root * gain).astype(BF)
+    wait(pair_copies)
+    wait(down_copies)
+    act, dy = act_ref[...], dy_ref[...]
+    for first in range(0, hidden, tile):
+        here = slice(first, first + tile)
+        gate = nn(act, w_pair[:width, here])
+        upper = nn(act, w_pair[width:, here])
+        d_inner = nt(dy, w_down[here, :])
+        sigmoid = 1.0 / (1.0 + jnp.exp(-gate))
+        silu = gate * sigmoid
+        inner = (silu * upper).astype(BF)
+        inner_ref[:, here] = inner
+        d_gate = (d_inner * upper * sigmoid * (1.0 + gate * (1.0 - sigmoid))).astype(BF)
+        d_upper = (d_inner * silu).astype(BF)
+        slopes_ref[0, :, here] = d_gate
+        slopes_ref[1, :, here] = d_upper
+        out = nn(inner, w_down[here, :])
+        d_act = nt(d_gate, w_pair[:width, here]) + nt(d_upper, w_pair[width:, here])
+        resid_ref[...] += out
+        if first == 0:
+            dact_ref[...] = d_act
+        else:
+            dact_ref[...] += d_act
+    out_ref[...] = resid_ref[...].astype(BF)
+    normed = dres_ref[...] * root
+    d_act = dact_ref[...]
+    gain_ref[...] = jnp.broadcast_to(jnp.sum(d_act * normed, axis=0, keepdims=True), gain_ref.shape)
+    d_normed = d_act * gain
+    d_resid = dy.astype(F32) + root * (
+        d_normed - normed * jnp.mean(d_normed * normed, axis=-1, keepdims=True)
+    )
+    dres_ref[...] = d_resid
+    low = d_resid.astype(BF)
+    low_ref[...] = low
+    dattn_ref[...] = nt(low, w_output).astype(BF)
+
+
+def feed(x, attn, dy, gains, attention_got, pair_got, down_got):
+    tokens, width = x.shape
+    groups = [attention_got, pair_got, down_got]
+    counts = [len(pieces) for pieces, _ in groups]
+    shapes = [joined_shape(pieces) for pieces, _ in groups]
+    hidden = shapes[1][1]
+    outs = (
+        jax.ShapeDtypeStruct((tokens, width), BF),
+        jax.ShapeDtypeStruct((tokens, hidden), BF),
+        jax.ShapeDtypeStruct((2, tokens, hidden), BF),
+        jax.ShapeDtypeStruct((tokens, width), BF),
+        jax.ShapeDtypeStruct((tokens, width), F32),
+        jax.ShapeDtypeStruct((tokens, width), BF),
+        jax.ShapeDtypeStruct((tokens, width), BF),
+        jax.ShapeDtypeStruct((8, width), F32),
+    )
+    every = [piece for pieces, _ in groups for piece in pieces]
+    return pl.pallas_call(
+        functools.partial(feed_kernel, counts),
+        name="feed",
+        in_specs=[IN_SMEM] * 3 + [IN_VMEM] * 4 + [ANYWHERE] * len(every),
+        out_specs=(IN_VMEM,) * 8,
+        out_shape=outs,
+        scratch_shapes=[pltpu.VMEM(shape, BF) for shape in shapes]
+        + [pltpu.VMEM((tokens, width), F32)] * 2
+        + [pltpu.SemaphoreType.DMA((count,)) for count in counts],
+        cost_estimate=cost(
+            2 * tokens * width * (6 * hidden + 3 * width), tokens * hidden, x, x, x, *outs, *every
+        ),
+        compiler_params=pltpu.CompilerParams(vmem_limit_bytes=VMEM_MOST),
+    )(*(starts for _, starts in groups), x, attn, dy, gains, *every)
+
+
+def weight_grad_kernel(parts, block, starts_ref, *refs):
+    operands = refs[: 2 * len(parts)]
+    out_ref = refs[2 * len(parts)]
+    turned = refs[2 * len(parts) + 1 :]
+    step = pl.program_id(0)
+
+    @pl.when(step == 0)
+    def _():
+        for i in range(len(parts)):
+            turned[i][...] = jnp.transpose(operands[2 * i][...])
+
+    at = 0
+    for i, rows in enumerate(parts):
+        start = pl.multiple_of(starts_ref[1 + i * pl.num_programs(0) + step], 16)
+        left = turned[i][pl.ds(start, rows), :]
+        out_ref[at : at + rows, :] = nn(left, operands[2 * i + 1][...]).astype(BF)
+        at += rows
+
+
+def weight_grad(terms, column=0, columns=None, choice=0):
+    count = len(terms[0][3])
+    parts = [term[2] for term in terms]
+    block = sum(parts)
+    tokens = terms[0][0].shape[0]
+    columns = columns or terms[0][1].shape[-1]
+    if any(rows % 16 for rows in parts) or any(term[0].shape[1] // count % 16 for term in terms):
+        made = []
+        for left, right, rows, starts in terms:
+            right = right if right.ndim == 2 else lax.dynamic_index_in_dim(right, choice, 0, keepdims=False)
+            grad = tn(left, right[:, column * columns : (column + 1) * columns]).astype(BF)
+            made.append([lax.dynamic_slice_in_dim(grad, start, rows, 0) for start in starts])
+        return jnp.concatenate([part for group in zip(*made) for part in group], axis=0)
+    in_specs, args, flops = [], [], 0
+    for left, right, rows, starts in terms:
+        in_specs.append(pl.BlockSpec(left.shape, lambda t, info: (0, 0)))
+        if right.ndim == 2:
+            in_specs.append(pl.BlockSpec((tokens, columns), lambda t, info: (0, column)))
+        else:
+            in_specs.append(pl.BlockSpec((None, tokens, columns), lambda t, info: (info[0], 0, column)))
+        args += [left, right]
+        flops += 2 * tokens * rows * count * columns
+    out = jax.ShapeDtypeStruct((count * block, columns), BF)
+    info = numbers([choice] + [start for term in terms for start in term[3]])
+    return pl.pallas_call(
+        functools.partial(weight_grad_kernel, parts, block),
         grid_spec=pltpu.PrefetchScalarGridSpec(
             num_scalar_prefetch=1,
-            grid=(1,),
-            in_specs=[pl.BlockSpec(memory_space=pl.ANY)] * len(pieces),
-            out_specs=pl.BlockSpec(memory_space=pl.ANY),
-            scratch_shapes=[pltpu.SemaphoreType.DMA((len(pieces),))],
+            grid=(count,),
+            in_specs=in_specs,
+            out_specs=pl.BlockSpec((block, columns), lambda t, info: (t, 0)),
+            scratch_shapes=[pltpu.VMEM((term[0].shape[1], tokens), BF) for term in terms],
         ),
         out_shape=out,
-        name="assemble",
+        name="weight_grad",
+        cost_estimate=cost(flops, 0, out, *args),
+        compiler_params=pltpu.CompilerParams(vmem_limit_bytes=VMEM_LIMIT),
+    )(info, *args)
+
+
+def finish_kernel(count, starts_ref, x_ref, low_ref, kv_ref, dres_ref, gains_ref, *refs):
+    pieces = refs[:count]
+    dx_ref, gain_ref, whole, sems = refs[count:]
+    copies = load(pieces, starts_ref, whole, sems)
+    x = x_ref[...].astype(F32)
+    width = x.shape[1]
+    root = rms_inverse(x)
+    normed = x * root
+    wait(copies)
+    d_act = nt(low_ref[...], whole[:width, :width])
+    d_act += nt(kv_ref[:, :KV_WIDTH], whole[:width, width:])
+    d_act += nt(kv_ref[:, KV_WIDTH:], whole[width:, width:])
+    gain_ref[...] = jnp.broadcast_to(jnp.sum(d_act * normed, axis=0, keepdims=True), gain_ref.shape)
+    d_normed = d_act * gains_ref[0:1, :]
+    dx_ref[...] = (
+        dres_ref[...]
+        + root * (d_normed - normed * jnp.mean(d_normed * normed, axis=-1, keepdims=True))
+    ).astype(BF)
+
+
+def finish(x, low, kv, dres, gains, pieces, starts):
+    tokens, width = x.shape
+    outs = (jax.ShapeDtypeStruct((tokens, width), BF), jax.ShapeDtypeStruct((8, width), F32))
+    return pl.pallas_call(
+        functools.partial(finish_kernel, len(pieces)),
+        name="finish",
+        in_specs=[IN_SMEM] + [IN_VMEM] * 5 + [ANYWHERE] * len(pieces),
+        out_specs=(IN_VMEM,) * 2,
+        out_shape=outs,
+        scratch_shapes=[
+            pltpu.VMEM(joined_shape(pieces), BF),
+            pltpu.SemaphoreType.DMA((len(pieces),)),
+        ],
+        cost_estimate=cost(2 * tokens * width * (width + 2 * KV_WIDTH), 0, x, low, dres, *pieces),
+        compiler_params=pltpu.CompilerParams(vmem_limit_bytes=VMEM_LIMIT),
+    )(starts, x, low, kv, dres, gains, *pieces)
+
+
+def turn_back_kernel(*refs):
+    parts = refs[:-3]
+    cos_ref, sin_ref, out_ref = refs[-3:]
+    at = 0
+    for part in parts:
+        here = slice(at, at + part.shape[0])
+        for first in range(0, KV_WIDTH, 128):
+            chunk = part[:, first : first + 128].astype(F32)
+            chunk = turn(chunk, cos_ref[here, :], -sin_ref[here, :]).astype(BF)
+            last = min(first + 128, KV_WIDTH)
+            out_ref[here, first:last] = chunk[:, : last - first]
+        out_ref[here, KV_WIDTH:] = part[:, KV_WIDTH:]
+        at += part.shape[0]
+
+
+def turn_back(parts, cosine, sine):
+    out = jax.ShapeDtypeStruct((sum(part.shape[0] for part in parts), 2 * KV_WIDTH), BF)
+    return pl.pallas_call(
+        turn_back_kernel,
+        name="turn_back",
+        in_specs=[IN_VMEM] * (len(parts) + 2),
+        out_specs=IN_VMEM,
+        out_shape=out,
         cost_estimate=cost(0, 0, out, out),
-    )(jnp.stack([jnp.int32(start) for start in starts]), *pieces)
+        compiler_params=pltpu.CompilerParams(vmem_limit_bytes=VMEM_LIMIT),
+    )(*parts, cosine, sine)
 
 
 def head(ref, h):
@@ -412,19 +665,6 @@
     )(*args)
 
 
-def rotate(vectors, cosine, sine, heads, inverse):
-    shaped = vectors.reshape(vectors.shape[0], heads, HEAD_SIZE)
-    first = shaped[..., :HALF_HEAD]
-    second = shaped[..., HALF_HEAD:]
-    cosine, sine = cosine[:, None, :], sine[:, None, :]
-    if inverse:
-        sine = -sine
-    turned = jnp.concatenate(
-        [first * cosine - second * sine, second * cosine + first * sine], axis=-1
-    )
-    return turned.reshape(vectors.shape[0], heads * HEAD_SIZE)
-
-
 def local(
     block_input,
     parent_ids,
@@ -449,19 +689,12 @@
     hidden = w_gate.shape[1]
 
     gains = links.gather_small(jnp.stack([norm_first, norm_second])).astype(F32)
-    gain_one, gain_two = gains[0:1], gains[1:2]
-    attention_got = links.gather_pair(
+    direct, *attention_got = links.gather_pair(
         jnp.concatenate([w_query, key_weight], axis=1),
         jnp.concatenate([w_output, value_weight], axis=1),
     )
-    attention_whole = assemble(attention_got)
-    full_qk, full_output, full_value = (
-        attention_whole[:width],
-        attention_whole[width:, :width],
-        attention_whole[width:, width:],
-    )
-    pair_got = links.gather_pair(*after((w_gate, w_up), attention_got[0]))
-    down_got = links.gather_rows(after(w_down, pair_got[0]))
+    direct, *pair_got = links.gather_pair(*after((w_gate, w_up), direct))
+    direct, *down_got = links.gather_rows(after(w_down, direct))
 
     parents = parent_ids[:, 0]
     seg = jnp.arange(segs)
@@ -482,7 +715,8 @@
     freqs = jnp.exp(-math.log(10000.0) * jnp.arange(HALF_HEAD, dtype=F32) * (2.0 / HEAD_SIZE))
     angles = freqs[:, None] * positions.reshape(tokens)[None, :]
     cosine_t, sine_t = jnp.cos(angles), jnp.sin(angles)
-    cosine, sine = cosine_t.T, sine_t.T
+    cosine = jnp.tile(cosine_t.T, (1, 4))
+    sine = jnp.tile(jnp.concatenate([-sine_t.T, sine_t.T], axis=1), (1, 2))
     key_rows = jnp.stack([row_numbers(hop) for hop in links.hops])
     open_key = (pick(on_path.astype(F32), key_rows) > 0.5) & (
         (key_rows < links.shard * rows) | (jnp.arange(shards) == 0)[:, None]
@@ -490,86 +724,81 @@
     bias = jnp.where(open_key, 0.0, CLOSED)
     bias = jnp.pad(bias, ((0, 0), (0, 8 - shards), (0, 0)))
 
-    inputs = block_input.reshape(tokens, width).astype(F32)
+    inputs = block_input.reshape(tokens, width)
     cotangent = out_cotangent.reshape(tokens, width)
-    inv_first = rms_inverse(inputs)
-    normed_first = inputs * inv_first
-    act_first = (normed_first * gain_one).astype(BF)
-    linear = nn(act_first, full_qk)
-    keys = rotate(linear[:, width:], cosine, sine, KEY_VALUE_HEADS, False)
-    kv = jnp.concatenate([keys, nn(act_first, full_value)], axis=1).astype(BF)
+    queries, kv, act_first = project(inputs, gains, cosine, sine, *attention_got)
     kv_all = [links.spread(kv[m * rows : (m + 1) * rows]) for m in range(micro)]
-    queries = (rotate(linear[:, :width], cosine, sine, QUERY_HEADS, False) * SCALE).astype(BF)
     attended = ()
     for m in range(micro):
         attended = attend(m, rows, seg_rows, queries, kv_all[m], bias, attended)
     attn, lse = attended
 
-    resid = inputs + nn(attn, full_output)
-    inv_second = rms_inverse(resid)
-    normed_second = resid * inv_second
-    act_second = (normed_second * gain_two).astype(BF)
-    pair_whole = assemble(pair_got)
-    full_gate, full_upper = pair_whole[:width], pair_whole[width:]
-    full_down = assemble(down_got)
-    gate = nn(act_second, full_gate)
-    upper = nn(act_second, full_upper)
-    sigmoid = jax.nn.sigmoid(gate)
-    silu = gate * sigmoid
-    inner = (silu * upper).astype(BF)
-    block_out = (resid + nn(inner, full_down)).astype(BF)
-
-    down_owned, down_rows = links.reduce_rows(tn(inner, cotangent))
-    d_inner = nt(cotangent, full_down)
-    d_gate = (d_inner * upper * sigmoid * (1.0 + gate * (1.0 - sigmoid))).astype(BF)
-    d_upper = (d_inner * silu).astype(BF)
-    even = links.core == 0
-    kept, given = (
-        tn(act_second, part).astype(BF).reshape(shards, width // shards, hidden)
-        for part in (jnp.where(even, d_gate, d_upper), jnp.where(even, d_upper, d_gate))
-    )
-    pair_owned = links.reduce_owned(kept, given)
-    d_act_second = nt(d_gate, full_gate) + nt(d_upper, full_upper)
-    gain_two_sum = jnp.sum(d_act_second * normed_second, axis=0)
-    d_normed = d_act_second * gain_two
-    d_resid = cotangent.astype(F32) + inv_second * (
-        d_normed - normed_second * jnp.mean(d_normed * normed_second, axis=-1, keepdims=True)
-    )
-    d_resid_low = d_resid.astype(BF)
-    output_owned, output_rows = links.reduce_rows(tn(attn, d_resid_low))
-    d_attn = nt(d_resid_low, full_output).astype(BF)
+    block_out, inner, slopes, act_second, d_resid, d_resid_low, d_attn, gain_two_sum = feed(
+        inputs, attn, cotangent, gains, attention_got, pair_got, down_got
+    )
+    down_rows, output_rows, wide_rows = hidden // shards, width // shards, width // shards
+    down_half, output_half = down_rows // 2, links.half_rows(output_rows)
+    down_kept, down_given = links.order(
+        down_rows, links.core * down_half, (1 - links.core) * down_half
+    )
+    output_kept, output_given = links.order(output_rows, *output_half[1:])
+    rows_grads = lambda down, output: weight_grad(
+        (
+            (inner, cotangent, down_half, down),
+            (attn, d_resid_low, output_half[0], output),
+        )
+    )
+    rows_received = links.swap(rows_grads(down_given, output_given))
+    rows_kept = rows_grads(down_kept, output_kept)
+    rows_owned = links.reduce_owned(rows_kept, rows_received)
+    wide_kept, wide_given = links.order(wide_rows, 0, 0)
+    chunks = 2
+    wide_owned = []
+    wide_received = []
+    for c in range(chunks):
+        given, kept = (
+            weight_grad(((act_second, slopes, wide_rows, starts),), c, hidden // chunks, choice)
+            for starts, choice in ((wide_given, 1 - links.core), (wide_kept, links.core))
+        )
+        wide_received.append(links.swap(given))
+        wide_owned.append(links.reduce_owned(kept, wide_received[c]))
 
     d_queries, d_kv = (), []
+    d_attn = after(d_attn, rows_received, *wide_received)
     for m in range(micro):
         d_queries, *pieces = attend_back(
             m, rows, seg_rows, queries, kv_all[m], bias, attn, d_attn, lse, cosine_t, sine_t, d_queries
         )
         d_queries = (d_queries,)
         d_kv.append(links.collect(pieces))
-    d_kv = jnp.concatenate(d_kv, axis=0).astype(F32)
-    d_key_low = rotate(d_kv[:, :KV_WIDTH], cosine, sine, KEY_VALUE_HEADS, True).astype(BF)
-    d_qk_low = jnp.concatenate([d_queries[0], d_key_low], axis=1)
-    d_value_low = d_kv[:, KV_WIDTH:].astype(BF)
-    qkv_owned, qkv_rows = links.reduce_rows(
-        tn(act_first, jnp.concatenate([d_qk_low, d_value_low], axis=1))
-    )
-    d_act_first = nt(d_qk_low, full_qk) + nt(d_value_low, full_value)
-    gain_one_sum = jnp.sum(d_act_first * normed_first, axis=0)
-    d_normed = d_act_first * gain_one
-    d_input = d_resid + inv_first * (
-        d_normed - normed_first * jnp.mean(d_normed * normed_first, axis=-1, keepdims=True)
-    )
-    gain_sums = links.reduce_small(jnp.stack([gain_one_sum, gain_two_sum]))
-    grad_down = links.finish_rows(down_owned, down_rows)
-    grad_gate, grad_upper = links.finish_pair(pair_owned)
-    grad_output = links.finish_rows(output_owned, output_rows)
-    grad_qkv = links.finish_rows(qkv_owned, qkv_rows)
+    d_queries = d_queries[0]
+    d_kv = turn_back(d_kv, cosine, sine)
+    half, mine, theirs = links.half_rows(width // shards)
+    qkv_kept, qkv_given = links.order(width // shards, mine, theirs)
+    q_received = links.swap(weight_grad(((act_first, d_queries, half, qkv_given),)))
+    q_owned = links.reduce_owned(weight_grad(((act_first, d_queries, half, qkv_kept),)), q_received)
+    kv_received = links.swap(weight_grad(((act_first, d_kv, half, qkv_given),)))
+    kv_owned = links.reduce_owned(weight_grad(((act_first, d_kv, half, qkv_kept),)), kv_received)
+    d_input, gain_one_sum = finish(inputs, d_queries, d_kv, d_resid, gains, *attention_got)
+    gain_sums = links.reduce_small(jnp.concatenate([gain_one_sum[:1], gain_two_sum[:1]]))
+
+    def whole_sum(owned):
+        owned = links.chain(owned)
+        return owned, links.swap(owned)
+
+    rows_owned, rows_other = whole_sum(rows_owned)
+    grad_down = links.finish_rows(rows_owned[:down_half], rows_other[:down_half], down_rows)
+    grad_output = links.finish_rows(rows_owned[down_half:], rows_other[down_half:], output_rows)
+    wide = [links.finish_pair(*whole_sum(owned)) for owned in wide_owned]
+    grad_gate, grad_upper = (jnp.concatenate(parts, axis=1) for parts in zip(*wide))
+    grad_query = links.finish_rows(*whole_sum(q_owned), width // shards)
+    grad_kv = links.finish_rows(*whole_sum(kv_owned), width // shards)
     return (
         block_out.reshape(micro, rows, width),
-        d_input.astype(BF).reshape(micro, rows, width),
-        grad_qkv[:, :width],
-        grad_qkv[:, width : width + KV_WIDTH],
-        grad_qkv[:, width + KV_WIDTH :],
+        d_input.reshape(micro, rows, width),
+        grad_query,
+        grad_kv[:, :KV_WIDTH],
+        grad_kv[:, KV_WIDTH:],
         grad_output,
         grad_gate,
         grad_upper,

time: 1080 us -> 541 us (0.50)
  Pallas kernels: 662 us -> 135 us
  matrix products: 76.7 us -> 0 us
  waiting for transfers between devices: 133 us -> 166 us
  local copies, waits for them, and re-layouts: 54.5 us -> 68 us
  starting transfers between devices: 87.9 us -> 101 us
    pallas_call x3 -> x14, Pallas kernels: 611 us -> 85.9 us  [the longest x10 38.8 us: weight_grad(): pl.pallas_call(functools.partial(weight_grad_kernel, parts, block), grid_...]
    dot_general x17 -> x0, matrix products: 76.7 us -> none  [dot(): return lax.dot_general(a, b, (dims, ((), ())), preferred_element_type=F32)]
    ppermute x71 -> x79, waiting for transfers between devices: 133 us -> 166 us  [move(): return lax.ppermute(value, AXES, pairs)]
    unnamed x141 -> x162, local copies, waits for them, and re-layouts: 17.2 us -> 42.9 us
    convert_element_type x24 -> x29, other arithmetic: 27.2 us -> 44.1 us  [add(): return (left.astype(F32) + right.astype(F32)).astype(left.dtype)]
    reshape x6 -> x0, local copies, waits for them, and re-layouts: 13.7 us -> none  [the longest x1 7.84 us: reduce_rows(): parts = grad.astype(BF).reshape(self.shards, rows, grad.shape[1])]
    ppermute x71 -> x79, starting transfers between devices: 87.9 us -> 101 us  [move(): return lax.ppermute(value, AXES, pairs)]
  transfers between devices with their start and end apart: 71 -> 79, of which waited for: 17 -> 21; matrix products, arithmetic and copies ran while one was open for 12% -> 20% of each run, Pallas kernels for 44% -> 19%
where the time goes in v3:
time: 541 us; the launch traced here: 533 us
  waiting for transfers between devices  166 us (31%)
  Pallas kernels  135 us (25%)
  starting transfers between devices  101 us (19%)
  local copies, waits for them, and re-layouts  68 us (13%)
  other arithmetic  61 us (11%)
    ppermute x79, waiting for transfers between devices, move(): return lax.ppermute(value, AXES, pairs)  166 us
    ppermute x79, starting transfers between devices, move(): return lax.ppermute(value, AXES, pairs)  101 us
    convert_element_type x29, other arithmetic, add(): return (left.astype(F32) + right.astype(F32)).astype(left.dtype)  44.1 us
    unnamed x162, local copies, waits for them, and re-layouts  42.9 us
    pallas_call x10, Pallas kernels, weight_grad(): pl.pallas_call(functools.partial(weight_grad_kernel, parts, block), grid_...  38.8 us
    pallas_call x2, Pallas kernels, attend_back(): pl.pallas_call(functools.partial(attend_back_kernel, shards, seg_rows), g...  32.7 us
    pallas_call x1, Pallas kernels, feed(): pl.pallas_call(functools.partial(feed_kernel, counts), name='feed', in_sp...  30.8 us
    pallas_call x2, Pallas kernels, attend(): pl.pallas_call(functools.partial(attend_kernel, shards, seg_rows), grid=(...  16.3 us
  transfers between devices with their start and end apart: 79, of which 21 were waited for; matrix products, arithmetic and copies ran while one was open for 20% of the time, Pallas kernels for 19%

profile of v3, /device:TPU:0, one launch (start us, length us, event | category | flops | bytes accessed | tf_op | source)
XLA Modules:
  0.0 533.0 jit_solution(7712766233644164428)
XLA Ops:
  2.8 2.4 broadcast_select_fusion.10
  5.2 2.9 collective-permute-start.3
  9.7 12.9 %collective-permute-done.3.refs_2_ = bf16[240,1280]{1,0:T(8,128)(2,1)S(1)} collective-permute-done((bf16[240,1280]{1,0:T(8,128)(2,1)}, bf16[240,1280]{1,0:T(8,128)(2,1)S(1)}, u32[]{:S(2)}, u32[]{:S(2)}) %collective-permute-start.3) | collective-permute-done | bytes 614432 | tf_op jit(solution)/shard_map/ppermute | solution.py:84
  27.8 5.0 collective-permute-done.5.refs_4_
  32.8 2.7 broadcast_select_fusion
  35.5 2.4 collective-permute-start.15
  39.2 26.9 %collective-permute-done.15.refs_10_ = bf16[240,2560]{1,0:T(8,128)(2,1)} collective-permute-done((bf16[240,2560]{1,0:T(8,128)(2,1)}, bf16[240,2560]{1,0:T(8,128)(2,1)}, u32[]{:S(2)}, u32[]{:S(2)}) %collective-permute-start.15) | collective-permute-done | bytes 1228832 | tf_op jit(solution)/shard_map/ppermute | solution.py:84
  72.4 2.3 copy.105
  76.0 7.3 %project.1 = (bf16[512,960]{1,0:T(8,128)(2,1)}, bf16[512,640]{1,0:T(8,128)(2,1)S(1)}, bf16[512,960]{1,0:T(8,128)(2,1)}) custom-call(s32[8]{0:T(128)S(1)} %stack.203.starts_ref.s0_ref.s1_ref, bf16[512,960]{1,0:T(8,128)(2,1)} %bitcast.58, f32[2,960]{1,0:T(2,128)S(1)} %maximum_convert_fusion.6.gains_ref, f32[512,128]{1,0:T(8,128)S(1)} %copy-done.29, ...), custom_call_target="tpu_custom_call" | custom-call | flops 1572864000 | bytes 8519680 | tf_op jit(solution)/shard_map/project/pallas_call | solution.py:285
  92.9 6.9 %collective-permute-done.13.refs_2_ = bf16[256,640]{1,0:T(8,128)(2,1)S(1)} collective-permute-done((bf16[256,640]{1,0:T(8,128)(2,1)S(1)}, bf16[256,640]{1,0:T(8,128)(2,1)S(1)}, u32[]{:S(2)}, u32[]{:S(2)}) %collective-permute-start.13) | collective-permute-done | bytes 327712 | tf_op jit(solution)/shard_map/ppermute | solution.py:84
  100.9 11.8 %collective-permute-done.9.refs_1_ = bf16[256,640]{1,0:T(8,128)(2,1)S(1)} collective-permute-done((bf16[256,640]{1,0:T(8,128)(2,1)S(1)}, bf16[256,640]{1,0:T(8,128)(2,1)S(1)}, u32[]{:S(2)}, u32[]{:S(2)}) %collective-permute-start.9) | collective-permute-done | bytes 327712 | tf_op jit(solution)/shard_map/ppermute | solution.py:84
  116.8 2.9 collective-permute-done.11.refs_3_
  120.5 2.7 copy.111
  124.5 2.4 collective-permute-done.22.refs_18_
  126.9 7.0 %collective-permute-done.23.refs_19_ = bf16[320,960]{1,0:T(8,128)(2,1)} collective-permute-done((bf16[320,960]{1,0:T(8,128)(2,1)}, bf16[320,960]{1,0:T(8,128)(2,1)}, u32[]{:S(2)}, u32[]{:S(2)}) %collective-permute-start.23) | collective-permute-done | bytes 614432 | tf_op jit(solution)/shard_map/ppermute | solution.py:84
  134.9 8.0 %attend.2 = (bf16[512,960]{1,0:T(8,128)(2,1)S(1)}, f32[512,128]{1,0:T(8,128)S(1)}) custom-call(bf16[512,960]{1,0:T(8,128)(2,1)S(1)} %copy-done.43, bf16[256,640]{1,0:T(8,128)(2,1)S(1)} %get-tuple-element.158.refs_0_, bf16[256,640]{1,0:T(8,128)(2,1)S(1)} %collective-permute-done.12.refs_1_, bf16[256,640]{1,0:T(8,128)(2,1)S(1)} %collective-permute-done.13.refs_2_, ...), custom_call_target="tpu_custom_call" | custom-call | flops 4026531840 | bytes 983040 | tf_op jit(solution)/shard_map/attend/pallas_call | solution.py:626
  143.0 8.2 %attend.3 = (bf16[512,960]{1,0:T(8,128)(2,1)S(1)}, f32[512,128]{1,0:T(8,128)S(1)}) custom-call(bf16[512,960]{1,0:T(8,128)(2,1)S(1)} %copy-done.43, bf16[256,640]{1,0:T(8,128)(2,1)S(1)} %get-tuple-element.159.refs_0_, bf16[256,640]{1,0:T(8,128)(2,1)S(1)} %collective-permute-done.9.refs_1_, ...), custom_call_target="tpu_custom_call", output_to_operand_aliasing={{0}: (6, {}), {1}: (7, {})} | custom-call | flops 4026531840 | bytes 983040 | tf_op jit(solution)/shard_map/attend/pallas_call | solution.py:626
  152.3 30.8 %feed.1 = (bf16[512,960]{1,0:T(8,128)(2,1)}, bf16[512,2560]{1,0:T(8,128)(2,1)}, bf16[2,512,2560]{2,1,0:T(8,128)(2,1)}, bf16[512,960]{1,0:T(8,128)(2,1)}, f32[512...) custom-call(s32[8]{0:T(128)} %copy-done.41, s32[8]{0:T(128)} %copy-done.41, ...), custom_call_target="tpu_custom_call" | custom-call | flops 17930649600 | bytes 36403200 | tf_op jit(solution)/shard_map/feed/pallas_call | solution.py:375
  184.4 5.3 %weight_grad.11 = bf16[960,1280]{1,0:T(8,128)(2,1)} custom-call(s32[5]{0:T(128)S(1)} %stack.231.starts_ref, bf16[512,960]{1,0:T(8,128)(2,1)S(1)} %copy-done, bf16[2,512,2560]{2,1,0:T(8,128)(2,1)} %get-tuple-element.55.refs_1_), custom_call_target="tpu_custom_call" | custom-call | flops 1258291200 | bytes 8683520 | tf_op jit(solution)/shard_map/weight_grad/pallas_call | solution.py:434
  190.2 5.6 %weight_grad.12 = bf16[960,1280]{1,0:T(8,128)(2,1)} custom-call(s32[5]{0:T(128)S(1)} %stack.231.starts_ref, bf16[512,960]{1,0:T(8,128)(2,1)S(1)} %copy-done, bf16[2,512,2560]{2,1,0:T(8,128)(2,1)} %get-tuple-element.55.refs_1_), custom_call_target="tpu_custom_call" | custom-call | flops 1258291200 | bytes 8683520 | tf_op jit(solution)/shard_map/weight_grad/pallas_call | solution.py:434
  199.5 5.5 %weight_grad.10 = bf16[1792,960]{1,0:T(8,128)(2,1)} custom-call(s32[9]{0:T(128)S(1)} %stack.226.starts_ref, bf16[512,2560]{1,0:T(8,128)(2,1)S(1)} %copy-done.3, bf16[512,960]{1,0:T(8,128)(2,1)S(1)} %bitcast.56, bf16[512,960]{1,0:T(8,128)(2,1)S(1)} %copy-done.18, bf16[512,960]{1,0:T(8,128)(2,1)S(1)} %copy-done.15), custom_call_target="tpu_custom_call" | custom-call | flops 1761607680 | bytes 9011200 | tf_op jit(solution)/shard_map/weight_grad/pallas_call | solution.py:434
  205.0 6.0 %copy.114 = bf16[1792,960]{0,1:T(8,128)(2,1)} copy(bf16[1792,960]{1,0:T(8,128)(2,1)} %weight_grad.10) | data formatting | bytes 6881280 | tf_op jit(solution)/shard_map/weight_grad/pallas_call | solution.py:434
  212.8 4.2 weight_grad.18
  217.0 4.5 weight_grad.19
  221.6 3.5 add_convert_fusion.25
  226.3 2.6 add_convert_fusion.16
  230.0 5.4 %weight_grad.17 = bf16[1792,960]{1,0:T(8,128)(2,1)} custom-call(s32[9]{0:T(128)S(1)} %stack.239.starts_ref, bf16[512,2560]{1,0:T(8,128)(2,1)S(1)} %copy-done.4, bf16[512,960]{1,0:T(8,128)(2,1)S(1)} %bitcast.57, bf16[512,960]{1,0:T(8,128)(2,1)S(1)} %copy-done.19, bf16[512,960]{1,0:T(8,128)(2,1)S(1)} %copy-done.16), custom_call_target="tpu_custom_call" | custom-call | flops 1761607680 | bytes 9011200 | tf_op jit(solution)/shard_map/weight_grad/pallas_call | solution.py:434
  236.1 2.4 copy.126
  239.5 2.5 add_convert_fusion.21
  242.1 2.5 add_convert_fusion.12
  244.7 16.0 %attend_back.2 = (bf16[512,960]{1,0:T(8,128)(2,1)S(1)}, bf16[256,640]{1,0:T(8,128)(2,1)S(1)}, bf16[256,640]{1,0:T(8,128)(2,1)S(1)}, bf16[256,640]{1,0:T(8,128)(2,1)S(1)}, bf16[256,640]{1,0:T(8,128)(2,1)S(1)}) custom-call(bf16[512,960]{1,0:T(8,128)(2,1)S(1)} %copy-done.44, bf16[256,640]{1,0:T(8,128)(2,1)S(1)} %copy-done.36, bf16[256,640]{1,0:T(8,128)(2,1)S(1)} %copy-done.46, ...), custom_call_target="tpu_custom_call" | custom-call | flops 10066329600 | bytes 983040 | tf_op jit(solution)/shard_map/attend_back/pallas_call | solution.py:651
  260.7 16.7 %attend_back.3 = (bf16[512,960]{1,0:T(8,128)(2,1)S(1)}, bf16[256,640]{1,0:T(8,128)(2,1)S(1)}, bf16[256,640]{1,0:T(8,128)(2,1)S(1)}, bf16[256,640]{1,0:T(8,128)(2,1)S(1)}, bf16[256,640]{1,0:T(8,128)(2,1)}) custom-call(bf16[512,960]{1,0:T(8,128)(2,1)S(1)} %copy-done.44, bf16[256,640]{1,0:T(8,128)(2,1)S(1)} %copy-done.34, ...), custom_call_target="tpu_custom_call", output_to_operand_aliasing={{0}: (11, {})} | custom-call | flops 10066329600 | bytes 983040 | tf_op jit(solution)/shard_map/attend_back/pallas_call | solution.py:651
  281.5 4.9 fusion.7
  286.4 2.2 copy.136
  294.4 3.6 add_convert_fusion.7
  302.4 2.5 collective-permute-done.32
  307.5 8.5 %finish.1 = (bf16[512,960]{1,0:T(8,128)(2,1)}, f32[8,960]{1,0:T(8,128)S(1)}) custom-call(s32[8]{0:T(128)S(1)} %copy-done.42, bf16[512,960]{1,0:T(8,128)(2,1)} %bitcast.60, bf16[512,960]{1,0:T(8,128)(2,1)} %copy-done.9, bf16[512,640]{1,0:T(8,128)(2,1)S(1)} %turn_back.1.kv_ref.refs_1_, f32[512,960]{1,0:T(8,128)} %get-tuple-element.68.dres_ref, ...), custom_call_target="tpu_custom_call" | custom-call | flops 1572864000 | bytes 8847360 | tf_op jit(solution)/shard_map/finish/pallas_call | solution.py:473
  316.2 2.2 weight_grad.13
  319.6 2.2 weight_grad.14
  322.7 2.4 copy.137
  325.1 2.2 copy.135
  327.3 2.2 copy.117
  332.4 2.8 add_convert_fusion.20
  335.2 18.0 %collective-permute-done.75 = f32[2,960]{1,0:T(2,128)S(1)} collective-permute-done((f32[2,960]{1,0:T(2,128)S(1)}, f32[2,960]{1,0:T(2,128)S(1)}, u32[]{:S(2)}, u32[]{:S(2)}) %collective-permute-start.75) | collective-permute-done | bytes 7712 | tf_op jit(solution)/shard_map/ppermute | solution.py:84
  353.2 4.5 collective-permute-start.62
  359.0 2.6 add_convert_fusion.11
  361.6 9.5 %collective-permute-done.76 = f32[2,960]{1,0:T(2,128)S(1)} collective-permute-done((f32[2,960]{1,0:T(2,128)S(1)}, f32[2,960]{1,0:T(2,128)S(1)}, u32[]{:S(2)}, u32[]{:S(2)}) %collective-permute-start.76) | collective-permute-done | bytes 7712 | tf_op jit(solution)/shard_map/ppermute | solution.py:84
  377.1 2.3 copy.127
  379.4 2.6 collective-permute-done.78
  382.0 4.7 collective-permute-start.69
  387.4 2.2 add_convert_fusion.19
  389.6 9.9 %collective-permute-done.69 = bf16[240,1280]{1,0:T(8,128)(2,1)S(1)} collective-permute-done((bf16[240,1280]{1,0:T(8,128)(2,1)S(1)}, bf16[240,1280]{1,0:T(8,128)(2,1)S(1)}, u32[]{:S(2)}, u32[]{:S(2)}) %collective-permute-start.69) | collective-permute-done | bytes 614432 | tf_op jit(solution)/shard_map/ppermute | solution.py:84
  403.5 2.3 fusion.8
  412.9 2.9 add_convert_fusion.3
  424.6 4.1 collective-permute-done.46
  433.9 6.7 %collective-permute-start.40 = (bf16[128,960]{1,0:T(8,128)(2,1)S(1)}, bf16[128,960]{1,0:T(8,128)(2,1)S(1)}, u32[]{:S(2)}, u32[]{:S(2)}) collective-permute-start(bf16[128,960]{1,0:T(8,128)(2,1)S(1)} %add_convert_fusion.35), channel_id=1, source_target_pairs={{0,8},{1,9},{2,10},{3,11},{4,12},{5,13},{6,14},{7,15},{24,16},{25,... | collective-permute-start | bytes 737288 | tf_op jit(solution)/shard_map/ppermute | solution.py:84
  446.1 7.9 %collective-permute-start.48 = (bf16[128,640]{1,0:T(8,128)(2,1)S(1)}, bf16[128,640]{1,0:T(8,128)(2,1)S(1)}, u32[]{:S(2)}, u32[]{:S(2)}) collective-permute-start(bf16[128,640]{1,0:T(8,128)(2,1)S(1)} %add_convert_fusion.44), channel_id=1, source_target_pairs={{0,8},{1,9},{2,10},{3,11},{4,12},{5,13},{6,14},{7,15},{24,16},{25,... | collective-permute-start | bytes 491528 | tf_op jit(solution)/shard_map/ppermute | solution.py:84
  454.1 2.7 collective-permute-done.48
  458.3 2.2 add_convert_fusion.2
  460.5 8.9 %collective-permute-start.55 = (bf16[448,960]{1,0:T(8,128)(2,1)S(1)}, bf16[448,960]{1,0:T(8,128)(2,1)S(1)}, u32[]{:S(2)}, u32[]{:S(2)}) collective-permute-start(bf16[448,960]{1,0:T(8,128)(2,1)S(1)} %add_convert_fusion.2), channel_id=1, source_target_pairs={{0,8},{1,9},{2,10},{3,11},{4,12},{5,13},{6,14},{7,15},{24,16},{25,... | collective-permute-start | bytes 2580488 | tf_op jit(solution)/shard_map/ppermute | solution.py:84
  473.0 3.7 collective-permute-done.50
  476.9 2.7 collective-permute-done.42
  479.7 4.8 collective-permute-done.55
  493.6 29.1 %collective-permute-done.57 = bf16[448,960]{1,0:T(8,128)(2,1)S(1)} collective-permute-done((bf16[448,960]{1,0:T(8,128)(2,1)S(1)}, bf16[448,960]{1,0:T(8,128)(2,1)S(1)}, u32[]{:S(2)}, u32[]{:S(2)}) %collective-permute-start.57) | collective-permute-done | bytes 860192 | tf_op jit(solution)/shard_map/ppermute | solution.py:84
  (388 shorter events, 132.3 us)
Async XLA Ops:
  5.2 17.4 %collective-permute-start.3 = (bf16[240,1280]{1,0:T(8,128)(2,1)}, bf16[240,1280]{1,0:T(8,128)(2,1)S(1)}, u32[]{:S(2)}, u32[]{:S(2)}) collective-permute-start(bf16[240,1280]{1,0:T(8,128)(2,1)} %get-tuple-element.128), channel_id=1, source_target_pairs={{0,1},{1,0},{2,3},{3,2},{4,6},{5,7},{6,4},{7,5},{8,9},{9,8},{10,11... | collective-permute-start | bytes 1843208 | tf_op jit(solution)/shard_map/ppermute | solution.py:84
  8.2 19.6 %collective-permute-start.4 = (bf16[240,1280]{1,0:T(8,128)(2,1)}, bf16[240,1280]{1,0:T(8,128)(2,1)S(1)}, u32[]{:S(2)}, u32[]{:S(2)}) collective-permute-start(bf16[240,1280]{1,0:T(8,128)(2,1)} %get-tuple-element.128), channel_id=1, source_target_pairs={{0,2},{1,3},{2,0},{3,1},{4,5},{5,4},{6,7},{7,6},{8,10},{9,11},{10,... | collective-permute-start | bytes 1843208 | tf_op jit(solution)/shard_map/ppermute | solution.py:84
  22.6 10.2 %collective-permute-start.5 = (bf16[240,1280]{1,0:T(8,128)(2,1)S(1)}, bf16[240,1280]{1,0:T(8,128)(2,1)S(1)}, u32[]{:S(2)}, u32[]{:S(2)}) collective-permute-start(bf16[240,1280]{1,0:T(8,128)(2,1)S(1)} %collective-permute-done.3.refs_2_), channel_id=1, source_target_pairs={{0,2},{1,3},{2,0},{3,1},{4,5},{5,4},{6,7},{7,6},{8,10},{9,11},{10,... | collective-permute-start | bytes 1843208 | tf_op jit(solution)/shard_map/ppermute | solution.py:84
  24.1 43.2 %collective-permute-start = (bf16[2,240]{1,0:T(2,128)(2,1)S(1)}, bf16[2,240]{1,0:T(2,128)(2,1)S(1)}, u32[]{:S(2)}, u32[]{:S(2)}) collective-permute-start(bf16[2,240]{1,0:T(2,128)(2,1)S(1)} %pad_maximum_fusion.5), channel_id=1, source_target_pairs={{0,1},{1,0},{2,3},{3,2},{4,5},{5,4},{6,7},{7,6},{8,9},{9,8},{10,11... | collective-permute-start | bytes 2888 | tf_op jit(solution)/shard_map/ppermute | solution.py:84
  25.8 41.5 %collective-permute-start.1 = (bf16[2,240]{1,0:T(2,128)(2,1)S(1)}, bf16[2,240]{1,0:T(2,128)(2,1)S(1)}, u32[]{:S(2)}, u32[]{:S(2)}) collective-permute-start(bf16[2,240]{1,0:T(2,128)(2,1)S(1)} %pad_maximum_fusion.5), channel_id=1, source_target_pairs={{0,2},{1,3},{2,0},{3,1},{4,6},{5,7},{6,4},{7,5},{8,10},{9,11},{10,... | collective-permute-start | bytes 2888 | tf_op jit(solution)/shard_map/ppermute | solution.py:84
  27.1 40.7 %collective-permute-start.2 = (bf16[2,240]{1,0:T(2,128)(2,1)S(1)}, bf16[2,240]{1,0:T(2,128)(2,1)S(1)}, u32[]{:S(2)}, u32[]{:S(2)}) collective-permute-start(bf16[2,240]{1,0:T(2,128)(2,1)S(1)} %pad_maximum_fusion.5), channel_id=1, source_target_pairs={{0,3},{1,2},{2,1},{3,0},{4,7},{5,6},{6,5},{7,4},{8,11},{9,10},{10,... | collective-permute-start | bytes 2888 | tf_op jit(solution)/shard_map/ppermute | solution.py:84
  35.5 30.6 %collective-permute-start.15 = (bf16[240,2560]{1,0:T(8,128)(2,1)}, bf16[240,2560]{1,0:T(8,128)(2,1)}, u32[]{:S(2)}, u32[]{:S(2)}) collective-permute-start(bf16[240,2560]{1,0:T(8,128)(2,1)} %broadcast_select_fusion), channel_id=1, source_target_pairs={{0,1},{1,0},{2,3},{3,2},{4,6},{5,7},{6,4},{7,5},{8,9},{9,8},{10,11... | collective-permute-start | bytes 3686408 | tf_op jit(solution)/shard_map/ppermute | solution.py:84
  38.4 46.8 %collective-permute-start.16 = (bf16[240,2560]{1,0:T(8,128)(2,1)}, bf16[240,2560]{1,0:T(8,128)(2,1)}, u32[]{:S(2)}, u32[]{:S(2)}) collective-permute-start(bf16[240,2560]{1,0:T(8,128)(2,1)} %broadcast_select_fusion), channel_id=1, source_target_pairs={{0,2},{1,3},{2,0},{3,1},{4,5},{5,4},{6,7},{7,6},{8,10},{9,11},{10,... | collective-permute-start | bytes 3686408 | tf_op jit(solution)/shard_map/ppermute | solution.py:84
  66.1 19.1 %collective-permute-start.17 = (bf16[240,2560]{1,0:T(8,128)(2,1)}, bf16[240,2560]{1,0:T(8,128)(2,1)}, u32[]{:S(2)}, u32[]{:S(2)}) collective-permute-start(bf16[240,2560]{1,0:T(8,128)(2,1)} %collective-permute-done.15.refs_10_), channel_id=1, source_target_pairs={{0,2},{1,3},{2,0},{3,1},{4,5},{5,4},{6,7},{7,6},{8,10},{9,11},{10,... | collective-permute-start | bytes 3686408 | tf_op jit(solution)/shard_map/ppermute | solution.py:84
  88.8 26.0 %collective-permute-start.21 = (bf16[320,960]{1,0:T(8,128)(2,1)}, bf16[320,960]{1,0:T(8,128)(2,1)}, u32[]{:S(2)}, u32[]{:S(2)}) collective-permute-start(bf16[320,960]{1,0:T(8,128)(2,1)} %constant_dynamic-slice_fusion), channel_id=1, source_target_pairs={{0,1},{1,0},{2,3},{3,2},{4,6},{5,7},{6,4},{7,5},{8,9},{9,8},{10,11... | collective-permute-start | bytes 1843208 | tf_op jit(solution)/shard_map/ppermute | solution.py:84
  89.1 10.7 %collective-permute-start.13 = (bf16[256,640]{1,0:T(8,128)(2,1)S(1)}, bf16[256,640]{1,0:T(8,128)(2,1)S(1)}, u32[]{:S(2)}, u32[]{:S(2)}) collective-permute-start(bf16[256,640]{1,0:T(8,128)(2,1)S(1)} %get-tuple-element.158.refs_0_), channel_id=1, source_target_pairs={{0,2},{1,3},{2,0},{3,1},{4,5},{5,4},{6,7},{7,6},{8,10},{9,11},{10,... | collective-permute-start | bytes 983048 | tf_op jit(solution)/shard_map/ppermute | solution.py:84
  90.2 22.5 %collective-permute-start.9 = (bf16[256,640]{1,0:T(8,128)(2,1)S(1)}, bf16[256,640]{1,0:T(8,128)(2,1)S(1)}, u32[]{:S(2)}, u32[]{:S(2)}) collective-permute-start(bf16[256,640]{1,0:T(8,128)(2,1)S(1)} %get-tuple-element.159.refs_0_), channel_id=1, source_target_pairs={{0,1},{1,0},{2,3},{3,2},{4,6},{5,7},{6,4},{7,5},{8,9},{9,8},{10,11... | collective-permute-start | bytes 983048 | tf_op jit(solution)/shard_map/ppermute | solution.py:84
  92.1 31.9 %collective-permute-start.18 = (bf16[240,2560]{1,0:T(8,128)(2,1)}, bf16[240,2560]{1,0:T(8,128)(2,1)}, u32[]{:S(2)}, u32[]{:S(2)}) collective-permute-start(bf16[240,2560]{1,0:T(8,128)(2,1)} %collective-permute-done.15.refs_10_), channel_id=1, source_target_pairs={{0,4},{1,5},{2,6},{3,7},{4,0},{5,1},{6,2},{7,3},{8,12},{9,13},{10,... | collective-permute-start | bytes 3686408 | tf_op jit(solution)/shard_map/ppermute | solution.py:84
  92.1 21.8 %collective-permute-start.10 = (bf16[256,640]{1,0:T(8,128)(2,1)S(1)}, bf16[256,640]{1,0:T(8,128)(2,1)S(1)}, u32[]{:S(2)}, u32[]{:S(2)}) collective-permute-start(bf16[256,640]{1,0:T(8,128)(2,1)S(1)} %get-tuple-element.159.refs_0_), channel_id=1, source_target_pairs={{0,2},{1,3},{2,0},{3,1},{4,5},{5,4},{6,7},{7,6},{8,10},{9,11},{10,... | collective-permute-start | bytes 983048 | tf_op jit(solution)/shard_map/ppermute | solution.py:84
  99.8 16.3 %collective-permute-start.14 = (bf16[256,640]{1,0:T(8,128)(2,1)S(1)}, bf16[256,640]{1,0:T(8,128)(2,1)S(1)}, u32[]{:S(2)}, u32[]{:S(2)}) collective-permute-start(bf16[256,640]{1,0:T(8,128)(2,1)S(1)} %collective-permute-done.12.refs_1_), channel_id=1, source_target_pairs={{0,2},{1,3},{2,0},{3,1},{4,5},{5,4},{6,7},{7,6},{8,10},{9,11},{10,... | collective-permute-start | bytes 983048 | tf_op jit(solution)/shard_map/ppermute | solution.py:84
  113.9 13.0 %collective-permute-start.22 = (bf16[320,960]{1,0:T(8,128)(2,1)}, bf16[320,960]{1,0:T(8,128)(2,1)}, u32[]{:S(2)}, u32[]{:S(2)}) collective-permute-start(bf16[320,960]{1,0:T(8,128)(2,1)} %constant_dynamic-slice_fusion), channel_id=1, source_target_pairs={{0,2},{1,3},{2,0},{3,1},{4,5},{5,4},{6,7},{7,6},{8,10},{9,11},{10,... | collective-permute-start | bytes 1843208 | tf_op jit(solution)/shard_map/ppermute | solution.py:84
  114.8 19.1 %collective-permute-start.23 = (bf16[320,960]{1,0:T(8,128)(2,1)}, bf16[320,960]{1,0:T(8,128)(2,1)}, u32[]{:S(2)}, u32[]{:S(2)}) collective-permute-start(bf16[320,960]{1,0:T(8,128)(2,1)} %collective-permute-done.21.refs_17_), channel_id=1, source_target_pairs={{0,2},{1,3},{2,0},{3,1},{4,5},{5,4},{6,7},{7,6},{8,10},{9,11},{10,... | collective-permute-start | bytes 1843208 | tf_op jit(solution)/shard_map/ppermute | solution.py:84
  116.8 35.4 %collective-permute-start.19 = (bf16[240,2560]{1,0:T(8,128)(2,1)}, bf16[240,2560]{1,0:T(8,128)(2,1)}, u32[]{:S(2)}, u32[]{:S(2)}) collective-permute-start(bf16[240,2560]{1,0:T(8,128)(2,1)} %collective-permute-done.16.refs_11_), channel_id=1, source_target_pairs={{0,4},{1,5},{2,6},{3,7},{4,0},{5,1},{6,2},{7,3},{8,12},{9,13},{10,... | collective-permute-start | bytes 3686408 | tf_op jit(solution)/shard_map/ppermute | solution.py:84
  120.5 31.8 %collective-permute-start.20 = (bf16[240,2560]{1,0:T(8,128)(2,1)}, bf16[240,2560]{1,0:T(8,128)(2,1)}, u32[]{:S(2)}, u32[]{:S(2)}) collective-permute-start(bf16[240,2560]{1,0:T(8,128)(2,1)} %collective-permute-done.17.refs_12_), channel_id=1, source_target_pairs={{0,4},{1,5},{2,6},{3,7},{4,0},{5,1},{6,2},{7,3},{8,12},{9,13},{10,... | collective-permute-start | bytes 3686408 | tf_op jit(solution)/shard_map/ppermute | solution.py:84
  124.0 28.3 %collective-permute-start.24 = (bf16[320,960]{1,0:T(8,128)(2,1)}, bf16[320,960]{1,0:T(8,128)(2,1)}, u32[]{:S(2)}, u32[]{:S(2)}) collective-permute-start(bf16[320,960]{1,0:T(8,128)(2,1)} %collective-permute-done.21.refs_17_), channel_id=1, source_target_pairs={{0,4},{1,5},{2,6},{3,7},{4,0},{5,1},{6,2},{7,3},{8,12},{9,13},{10,... | collective-permute-start | bytes 1843208 | tf_op jit(solution)/shard_map/ppermute | solution.py:84
  126.9 25.4 %collective-permute-start.25 = (bf16[320,960]{1,0:T(8,128)(2,1)}, bf16[320,960]{1,0:T(8,128)(2,1)}, u32[]{:S(2)}, u32[]{:S(2)}) collective-permute-start(bf16[320,960]{1,0:T(8,128)(2,1)} %collective-permute-done.22.refs_18_), channel_id=1, source_target_pairs={{0,4},{1,5},{2,6},{3,7},{4,0},{5,1},{6,2},{7,3},{8,12},{9,13},{10,... | collective-permute-start | bytes 1843208 | tf_op jit(solution)/shard_map/ppermute | solution.py:84
  133.9 18.4 %collective-permute-start.26 = (bf16[320,960]{1,0:T(8,128)(2,1)}, bf16[320,960]{1,0:T(8,128)(2,1)}, u32[]{:S(2)}, u32[]{:S(2)}) collective-permute-start(bf16[320,960]{1,0:T(8,128)(2,1)} %collective-permute-done.23.refs_19_), channel_id=1, source_target_pairs={{0,4},{1,5},{2,6},{3,7},{4,0},{5,1},{6,2},{7,3},{8,12},{9,13},{10,... | collective-permute-start | bytes 1843208 | tf_op jit(solution)/shard_map/ppermute | solution.py:84
  189.7 31.9 %collective-permute-start.28 = (bf16[960,1280]{1,0:T(8,128)(2,1)}, bf16[960,1280]{1,0:T(8,128)(2,1)}, u32[]{:S(2)}, u32[]{:S(2)}) collective-permute-start(bf16[960,1280]{1,0:T(8,128)(2,1)} %weight_grad.11), channel_id=1, source_target_pairs={{0,4},{1,5},{2,6},{3,7},{4,0},{5,1},{6,2},{7,3},{8,12},{9,13},{10,... | collective-permute-start | bytes 7372808 | tf_op jit(solution)/shard_map/ppermute | solution.py:84
  195.8 30.5 %collective-permute-start.29 = (bf16[960,1280]{1,0:T(8,128)(2,1)}, bf16[960,1280]{1,0:T(8,128)(2,1)}, u32[]{:S(2)}, u32[]{:S(2)}) collective-permute-start(bf16[960,1280]{1,0:T(8,128)(2,1)} %weight_grad.12), channel_id=1, source_target_pairs={{0,4},{1,5},{2,6},{3,7},{4,0},{5,1},{6,2},{7,3},{8,12},{9,13},{10,... | collective-permute-start | bytes 7372808 | tf_op jit(solution)/shard_map/ppermute | solution.py:84
  211.0 33.6 %collective-permute-start.27 = (bf16[1792,960]{0,1:T(8,128)(2,1)}, bf16[1792,960]{0,1:T(8,128)(2,1)}, u32[]{:S(2)}, u32[]{:S(2)}) collective-permute-start(bf16[1792,960]{0,1:T(8,128)(2,1)} %copy.114), channel_id=1, source_target_pairs={{0,4},{1,5},{2,6},{3,7},{4,0},{5,1},{6,2},{7,3},{8,12},{9,13},{10,... | collective-permute-start | bytes 10321928 | tf_op jit(solution)/shard_map/ppermute | solution.py:84
  225.1 14.5 %collective-permute-start.60 = (bf16[240,1280]{1,0:T(8,128)(2,1)}, bf16[240,1280]{1,0:T(8,128)(2,1)}, u32[]{:S(2)}, u32[]{:S(2)}) collective-permute-start(bf16[240,1280]{1,0:T(8,128)(2,1)} %get-tuple-element.132), channel_id=1, source_target_pairs={{0,2},{1,3},{2,0},{3,1},{4,5},{5,4},{6,7},{7,6},{8,10},{9,11},{10,... | collective-permute-start | bytes 1843208 | tf_op jit(solution)/shard_map/ppermute | solution.py:84
  228.9 13.3 %collective-permute-start.67 = (bf16[240,1280]{1,0:T(8,128)(2,1)}, bf16[240,1280]{1,0:T(8,128)(2,1)}, u32[]{:S(2)}, u32[]{:S(2)}) collective-permute-start(bf16[240,1280]{1,0:T(8,128)(2,1)} %get-tuple-element.134), channel_id=1, source_target_pairs={{0,2},{1,3},{2,0},{3,1},{4,5},{5,4},{6,7},{7,6},{8,10},{9,11},{10,... | collective-permute-start | bytes 1843208 | tf_op jit(solution)/shard_map/ppermute | solution.py:84
  238.5 91.8 %collective-permute-start.59 = (bf16[240,1280]{1,0:T(8,128)(2,1)}, bf16[240,1280]{1,0:T(8,128)(2,1)}, u32[]{:S(2)}, u32[]{:S(2)}) collective-permute-start(bf16[240,1280]{1,0:T(8,128)(2,1)} %get-tuple-element.131), channel_id=1, source_target_pairs={{0,2},{1,3},{2,0},{3,1},{4,5},{5,4},{6,7},{7,6},{8,10},{9,11},{10,... | collective-permute-start | bytes 1843208 | tf_op jit(solution)/shard_map/ppermute | solution.py:84
  277.4 12.5 %collective-permute-start.34 = (bf16[256,640]{1,0:T(8,128)(2,1)}, bf16[256,640]{1,0:T(8,128)(2,1)}, u32[]{:S(2)}, u32[]{:S(2)}) collective-permute-start(bf16[256,640]{1,0:T(8,128)(2,1)} %get-tuple-element.67), channel_id=1, source_target_pairs={{0,2},{1,3},{2,0},{3,1},{4,5},{5,4},{6,7},{7,6},{8,10},{9,11},{10,... | collective-permute-start | bytes 983048 | tf_op jit(solution)/shard_map/ppermute | solution.py:84
  278.6 19.3 %collective-permute-start.33 = (bf16[256,640]{1,0:T(8,128)(2,1)S(1)}, bf16[256,640]{1,0:T(8,128)(2,1)}, u32[]{:S(2)}, u32[]{:S(2)}) collective-permute-start(bf16[256,640]{1,0:T(8,128)(2,1)S(1)} %get-tuple-element.65), channel_id=1, source_target_pairs={{0,2},{1,3},{2,0},{3,1},{4,5},{5,4},{6,7},{7,6},{8,10},{9,11},{10,... | collective-permute-start | bytes 983048 | tf_op jit(solution)/shard_map/ppermute | solution.py:84
  279.5 12.7 %collective-permute-start.31 = (bf16[256,640]{1,0:T(8,128)(2,1)S(1)}, bf16[256,640]{1,0:T(8,128)(2,1)}, u32[]{:S(2)}, u32[]{:S(2)}) collective-permute-start(bf16[256,640]{1,0:T(8,128)(2,1)S(1)} %get-tuple-element.63), channel_id=1, source_target_pairs={{0,2},{1,3},{2,0},{3,1},{4,5},{5,4},{6,7},{7,6},{8,10},{9,11},{10,... | collective-permute-start | bytes 983048 | tf_op jit(solution)/shard_map/ppermute | solution.py:84
  280.6 20.4 %collective-permute-start.30 = (bf16[256,640]{1,0:T(8,128)(2,1)S(1)}, bf16[256,640]{1,0:T(8,128)(2,1)}, u32[]{:S(2)}, u32[]{:S(2)}) collective-permute-start(bf16[256,640]{1,0:T(8,128)(2,1)S(1)} %get-tuple-element.61), channel_id=1, source_target_pairs={{0,2},{1,3},{2,0},{3,1},{4,5},{5,4},{6,7},{7,6},{8,10},{9,11},{10,... | collective-permute-start | bytes 983048 | tf_op jit(solution)/shard_map/ppermute | solution.py:84
  293.2 11.7 %collective-permute-start.32 = (bf16[256,640]{1,0:T(8,128)(2,1)S(1)}, bf16[256,640]{1,0:T(8,128)(2,1)S(1)}, u32[]{:S(2)}, u32[]{:S(2)}) collective-permute-start(bf16[256,640]{1,0:T(8,128)(2,1)S(1)} %add_convert_fusion.31), channel_id=1, source_target_pairs={{0,1},{1,0},{2,3},{3,2},{4,6},{5,7},{6,4},{7,5},{8,9},{9,8},{10,11... | collective-permute-start | bytes 983048 | tf_op jit(solution)/shard_map/ppermute | solution.py:84
  298.0 55.2 %collective-permute-start.66 = (bf16[240,1280]{1,0:T(8,128)(2,1)}, bf16[240,1280]{1,0:T(8,128)(2,1)S(1)}, u32[]{:S(2)}, u32[]{:S(2)}) collective-permute-start(bf16[240,1280]{1,0:T(8,128)(2,1)} %get-tuple-element.133), channel_id=1, source_target_pairs={{0,2},{1,3},{2,0},{3,1},{4,5},{5,4},{6,7},{7,6},{8,10},{9,11},{10,... | collective-permute-start | bytes 1843208 | tf_op jit(solution)/shard_map/ppermute | solution.py:84
  299.1 32.6 %collective-permute-start.61 = (bf16[240,1280]{1,0:T(8,128)(2,1)}, bf16[240,1280]{1,0:T(8,128)(2,1)}, u32[]{:S(2)}, u32[]{:S(2)}) collective-permute-start(bf16[240,1280]{1,0:T(8,128)(2,1)} %add_convert_fusion.21), channel_id=1, source_target_pairs={{0,1},{1,0},{2,3},{3,2},{4,6},{5,7},{6,4},{7,5},{8,9},{9,8},{10,11... | collective-permute-start | bytes 1843208 | tf_op jit(solution)/shard_map/ppermute | solution.py:84
  301.0 56.7 %collective-permute-start.68 = (bf16[240,1280]{1,0:T(8,128)(2,1)}, bf16[240,1280]{1,0:T(8,128)(2,1)}, u32[]{:S(2)}, u32[]{:S(2)}) collective-permute-start(bf16[240,1280]{1,0:T(8,128)(2,1)} %add_convert_fusion.12), channel_id=1, source_target_pairs={{0,1},{1,0},{2,3},{3,2},{4,6},{5,7},{6,4},{7,5},{8,9},{9,8},{10,11... | collective-permute-start | bytes 1843208 | tf_op jit(solution)/shard_map/ppermute | solution.py:84
  318.4 11.2 %collective-permute-start.74 = (f32[2,960]{1,0:T(2,128)S(1)}, f32[2,960]{1,0:T(2,128)S(1)}, u32[]{:S(2)}, u32[]{:S(2)}) collective-permute-start(f32[2,960]{1,0:T(2,128)S(1)} %fusion.6), channel_id=1, source_target_pairs={{0,1},{1,0},{2,3},{3,2},{4,6},{5,7},{6,4},{7,5},{8,9},{9,8},{10,11... | collective-permute-start | bytes 23048 | tf_op jit(solution)/shard_map/ppermute | solution.py:84
  329.6 81.9 %collective-permute-start.53 = (bf16[448,960]{1,0:T(8,128)(2,1)}, bf16[448,960]{1,0:T(8,128)(2,1)}, u32[]{:S(2)}, u32[]{:S(2)}) collective-permute-start(bf16[448,960]{1,0:T(8,128)(2,1)} %get-tuple-element.136), channel_id=1, source_target_pairs={{0,2},{1,3},{2,0},{3,1},{4,5},{5,4},{6,7},{7,6},{8,10},{9,11},{10,... | collective-permute-start | bytes 2580488 | tf_op jit(solution)/shard_map/ppermute | solution.py:84
  330.3 127.3 %collective-permute-start.52 = (bf16[448,960]{1,0:T(8,128)(2,1)}, bf16[448,960]{1,0:T(8,128)(2,1)}, u32[]{:S(2)}, u32[]{:S(2)}) collective-permute-start(bf16[448,960]{1,0:T(8,128)(2,1)} %get-tuple-element.135), channel_id=1, source_target_pairs={{0,2},{1,3},{2,0},{3,1},{4,5},{5,4},{6,7},{7,6},{8,10},{9,11},{10,... | collective-permute-start | bytes 2580488 | tf_op jit(solution)/shard_map/ppermute | solution.py:84
  331.7 21.4 %collective-permute-start.75 = (f32[2,960]{1,0:T(2,128)S(1)}, f32[2,960]{1,0:T(2,128)S(1)}, u32[]{:S(2)}, u32[]{:S(2)}) collective-permute-start(f32[2,960]{1,0:T(2,128)S(1)} %fusion.13), channel_id=1, source_target_pairs={{0,2},{1,3},{2,0},{3,1},{4,5},{5,4},{6,7},{7,6},{8,10},{9,11},{10,... | collective-permute-start | bytes 23048 | tf_op jit(solution)/shard_map/ppermute | solution.py:84
  353.1 48.8 %collective-permute-start.36 = (bf16[512,960]{0,1:T(8,128)(2,1)}, bf16[512,960]{0,1:T(8,128)(2,1)}, u32[]{:S(2)}, u32[]{:S(2)}) collective-permute-start(bf16[512,960]{0,1:T(8,128)(2,1)} %copy.117), channel_id=1, source_target_pairs={{0,4},{1,5},{2,6},{3,7},{4,0},{5,1},{6,2},{7,3},{8,12},{9,13},{10,... | collective-permute-start | bytes 2949128 | tf_op jit(solution)/shard_map/ppermute | solution.py:84
  353.2 34.3 %collective-permute-start.62 = (bf16[240,1280]{1,0:T(8,128)(2,1)}, bf16[240,1280]{1,0:T(8,128)(2,1)}, u32[]{:S(2)}, u32[]{:S(2)}) collective-permute-start(bf16[240,1280]{1,0:T(8,128)(2,1)} %add_convert_fusion.20), channel_id=1, source_target_pairs={{0,8},{1,9},{2,10},{3,11},{4,12},{5,13},{6,14},{7,15},{24,16},{25,... | collective-permute-start | bytes 1843208 | tf_op jit(solution)/shard_map/ppermute | solution.py:84
  357.7 13.3 %collective-permute-start.76 = (f32[2,960]{1,0:T(2,128)S(1)}, f32[2,960]{1,0:T(2,128)S(1)}, u32[]{:S(2)}, u32[]{:S(2)}) collective-permute-start(f32[2,960]{1,0:T(2,128)S(1)} %add.517), channel_id=1, source_target_pairs={{0,8},{1,9},{2,10},{3,11},{4,12},{5,13},{6,14},{7,15},{24,16},{25,... | collective-permute-start | bytes 23048 | tf_op jit(solution)/shard_map/ppermute | solution.py:84
  382.0 17.5 %collective-permute-start.69 = (bf16[240,1280]{1,0:T(8,128)(2,1)S(1)}, bf16[240,1280]{1,0:T(8,128)(2,1)S(1)}, u32[]{:S(2)}, u32[]{:S(2)}) collective-permute-start(bf16[240,1280]{1,0:T(8,128)(2,1)S(1)} %copy-done.66), channel_id=1, source_target_pairs={{0,8},{1,9},{2,10},{3,11},{4,12},{5,13},{6,14},{7,15},{24,16},{25,... | collective-permute-start | bytes 1843208 | tf_op jit(solution)/shard_map/ppermute | solution.py:84
  387.4 33.3 %collective-permute-start.44 = (bf16[512,640]{1,0:T(8,128)(2,1)S(1)}, bf16[512,640]{1,0:T(8,128)(2,1)}, u32[]{:S(2)}, u32[]{:S(2)}) collective-permute-start(bf16[512,640]{1,0:T(8,128)(2,1)S(1)} %copy-done.32), channel_id=1, source_target_pairs={{0,4},{1,5},{2,6},{3,7},{4,0},{5,1},{6,2},{7,3},{8,12},{9,13},{10,... | collective-permute-start | bytes 1966088 | tf_op jit(solution)/shard_map/ppermute | solution.py:84
  399.5 23.2 %collective-permute-start.63 = (bf16[240,1280]{1,0:T(8,128)(2,1)}, bf16[240,1280]{1,0:T(8,128)(2,1)}, u32[]{:S(2)}, u32[]{:S(2)}) collective-permute-start(bf16[240,1280]{1,0:T(8,128)(2,1)} %add_convert_fusion.19), channel_id=1, source_target_pairs={{8,16},{9,17},{10,18},{11,19},{12,20},{13,21},{14,22},{15,23},{16,... | collective-permute-start | bytes 1843208 | tf_op jit(solution)/shard_map/ppermute | solution.py:84
  402.0 31.9 %collective-permute-start.70 = (bf16[240,1280]{1,0:T(8,128)(2,1)}, bf16[240,1280]{1,0:T(8,128)(2,1)}, u32[]{:S(2)}, u32[]{:S(2)}) collective-permute-start(bf16[240,1280]{1,0:T(8,128)(2,1)} %add_convert_fusion.10), channel_id=1, source_target_pairs={{8,16},{9,17},{10,18},{11,19},{12,20},{13,21},{14,22},{15,23},{16,... | collective-permute-start | bytes 1843208 | tf_op jit(solution)/shard_map/ppermute | solution.py:84
  418.1 12.9 %collective-permute-start.37 = (bf16[128,960]{1,0:T(8,128)(2,1)}, bf16[128,960]{1,0:T(8,128)(2,1)S(1)}, u32[]{:S(2)}, u32[]{:S(2)}) collective-permute-start(bf16[128,960]{1,0:T(8,128)(2,1)} %get-tuple-element.149), channel_id=1, source_target_pairs={{0,2},{1,3},{2,0},{3,1},{4,5},{5,4},{6,7},{7,6},{8,10},{9,11},{10,... | collective-permute-start | bytes 737288 | tf_op jit(solution)/shard_map/ppermute | solution.py:84
  420.7 11.6 %collective-permute-start.39 = (bf16[128,960]{1,0:T(8,128)(2,1)S(1)}, bf16[128,960]{1,0:T(8,128)(2,1)S(1)}, u32[]{:S(2)}, u32[]{:S(2)}) collective-permute-start(bf16[128,960]{1,0:T(8,128)(2,1)S(1)} %add_convert_fusion.36), channel_id=1, source_target_pairs={{0,1},{1,0},{2,3},{3,2},{4,6},{5,7},{6,4},{7,5},{8,9},{9,8},{10,11... | collective-permute-start | bytes 737288 | tf_op jit(solution)/shard_map/ppermute | solution.py:84
  428.7 29.6 %collective-permute-start.54 = (bf16[448,960]{1,0:T(8,128)(2,1)S(1)}, bf16[448,960]{1,0:T(8,128)(2,1)S(1)}, u32[]{:S(2)}, u32[]{:S(2)}) collective-permute-start(bf16[448,960]{1,0:T(8,128)(2,1)S(1)} %copy-done.67), channel_id=1, source_target_pairs={{0,1},{1,0},{2,3},{3,2},{4,6},{5,7},{6,4},{7,5},{8,9},{9,8},{10,11... | collective-permute-start | bytes 2580488 | tf_op jit(solution)/shard_map/ppermute | solution.py:84
  431.0 11.0 %collective-permute-start.45 = (bf16[128,640]{1,0:T(8,128)(2,1)S(1)}, bf16[128,640]{1,0:T(8,128)(2,1)S(1)}, u32[]{:S(2)}, u32[]{:S(2)}) collective-permute-start(bf16[128,640]{1,0:T(8,128)(2,1)S(1)} %get-tuple-element.143), channel_id=1, source_target_pairs={{0,2},{1,3},{2,0},{3,1},{4,5},{5,4},{6,7},{7,6},{8,10},{9,11},{10,... | collective-permute-start | bytes 491528 | tf_op jit(solution)/shard_map/ppermute | solution.py:84
  432.4 11.5 %collective-permute-start.47 = (bf16[128,640]{1,0:T(8,128)(2,1)S(1)}, bf16[128,640]{1,0:T(8,128)(2,1)S(1)}, u32[]{:S(2)}, u32[]{:S(2)}) collective-permute-start(bf16[128,640]{1,0:T(8,128)(2,1)S(1)} %add_convert_fusion.45), channel_id=1, source_target_pairs={{0,1},{1,0},{2,3},{3,2},{4,6},{5,7},{6,4},{7,5},{8,9},{9,8},{10,11... | collective-permute-start | bytes 491528 | tf_op jit(solution)/shard_map/ppermute | solution.py:84
  433.9 12.3 %collective-permute-start.40 = (bf16[128,960]{1,0:T(8,128)(2,1)S(1)}, bf16[128,960]{1,0:T(8,128)(2,1)S(1)}, u32[]{:S(2)}, u32[]{:S(2)}) collective-permute-start(bf16[128,960]{1,0:T(8,128)(2,1)S(1)} %add_convert_fusion.35), channel_id=1, source_target_pairs={{0,8},{1,9},{2,10},{3,11},{4,12},{5,13},{6,14},{7,15},{24,16},{25,... | collective-permute-start | bytes 737288 | tf_op jit(solution)/shard_map/ppermute | solution.py:84
  442.0 30.2 %collective-permute-start.64 = (bf16[240,1280]{1,0:T(8,128)(2,1)S(1)}, bf16[240,1280]{1,0:T(8,128)(2,1)S(1)}, u32[]{:S(2)}, u32[]{:S(2)}) collective-permute-start(bf16[240,1280]{1,0:T(8,128)(2,1)S(1)} %add_convert_fusion.18), channel_id=1, source_target_pairs={{8,0},{9,1},{10,2},{11,3},{12,4},{13,5},{14,6},{15,7},{16,24},{17,... | collective-permute-start | bytes 1843208 | tf_op jit(solution)/shard_map/ppermute | solution.py:84
  443.8 28.6 %collective-permute-start.71 = (bf16[240,1280]{1,0:T(8,128)(2,1)S(1)}, bf16[240,1280]{1,0:T(8,128)(2,1)S(1)}, u32[]{:S(2)}, u32[]{:S(2)}) collective-permute-start(bf16[240,1280]{1,0:T(8,128)(2,1)S(1)} %add_convert_fusion.9), channel_id=1, source_target_pairs={{8,0},{9,1},{10,2},{11,3},{12,4},{13,5},{14,6},{15,7},{16,24},{17,... | collective-permute-start | bytes 1843208 | tf_op jit(solution)/shard_map/ppermute | solution.py:84
  446.1 10.7 %collective-permute-start.48 = (bf16[128,640]{1,0:T(8,128)(2,1)S(1)}, bf16[128,640]{1,0:T(8,128)(2,1)S(1)}, u32[]{:S(2)}, u32[]{:S(2)}) collective-permute-start(bf16[128,640]{1,0:T(8,128)(2,1)S(1)} %add_convert_fusion.44), channel_id=1, source_target_pairs={{0,8},{1,9},{2,10},{3,11},{4,12},{5,13},{6,14},{7,15},{24,16},{25,... | collective-permute-start | bytes 491528 | tf_op jit(solution)/shard_map/ppermute | solution.py:84
  456.9 14.0 %collective-permute-start.41 = (bf16[128,960]{1,0:T(8,128)(2,1)S(1)}, bf16[128,960]{1,0:T(8,128)(2,1)S(1)}, u32[]{:S(2)}, u32[]{:S(2)}) collective-permute-start(bf16[128,960]{1,0:T(8,128)(2,1)S(1)} %add_convert_fusion.34), channel_id=1, source_target_pairs={{8,16},{9,17},{10,18},{11,19},{12,20},{13,21},{14,22},{15,23},{16,... | collective-permute-start | bytes 737288 | tf_op jit(solution)/shard_map/ppermute | solution.py:84
  457.6 11.9 %collective-permute-start.49 = (bf16[128,640]{1,0:T(8,128)(2,1)S(1)}, bf16[128,640]{1,0:T(8,128)(2,1)S(1)}, u32[]{:S(2)}, u32[]{:S(2)}) collective-permute-start(bf16[128,640]{1,0:T(8,128)(2,1)S(1)} %add_convert_fusion.43), channel_id=1, source_target_pairs={{8,16},{9,17},{10,18},{11,19},{12,20},{13,21},{14,22},{15,23},{16,... | collective-permute-start | bytes 491528 | tf_op jit(solution)/shard_map/ppermute | solution.py:84
  460.5 23.9 %collective-permute-start.55 = (bf16[448,960]{1,0:T(8,128)(2,1)S(1)}, bf16[448,960]{1,0:T(8,128)(2,1)S(1)}, u32[]{:S(2)}, u32[]{:S(2)}) collective-permute-start(bf16[448,960]{1,0:T(8,128)(2,1)S(1)} %add_convert_fusion.2), channel_id=1, source_target_pairs={{0,8},{1,9},{2,10},{3,11},{4,12},{5,13},{6,14},{7,15},{24,16},{25,... | collective-permute-start | bytes 2580488 | tf_op jit(solution)/shard_map/ppermute | solution.py:84
  470.9 8.6 %collective-permute-start.42 = (bf16[128,960]{1,0:T(8,128)(2,1)S(1)}, bf16[128,960]{1,0:T(8,128)(2,1)S(1)}, u32[]{:S(2)}, u32[]{:S(2)}) collective-permute-start(bf16[128,960]{1,0:T(8,128)(2,1)S(1)} %add_convert_fusion.33), channel_id=1, source_target_pairs={{8,0},{9,1},{10,2},{11,3},{12,4},{13,5},{14,6},{15,7},{16,24},{17,... | collective-permute-start | bytes 737288 | tf_op jit(solution)/shard_map/ppermute | solution.py:84
  472.3 20.1 %collective-permute-start.65 = (bf16[240,1280]{1,0:T(8,128)(2,1)S(1)}, bf16[240,1280]{1,0:T(8,128)(2,1)}, u32[]{:S(2)}, u32[]{:S(2)}) collective-permute-start(bf16[240,1280]{1,0:T(8,128)(2,1)S(1)} %broadcast_select_fusion.5), channel_id=1, source_target_pairs={{0,4},{1,5},{2,6},{3,7},{4,0},{5,1},{6,2},{7,3},{8,12},{9,13},{10,... | collective-permute-start | bytes 1843208 | tf_op jit(solution)/shard_map/ppermute | solution.py:84
  472.5 50.4 %collective-permute-start.72 = (bf16[240,1280]{1,0:T(8,128)(2,1)S(1)}, bf16[240,1280]{1,0:T(8,128)(2,1)}, u32[]{:S(2)}, u32[]{:S(2)}) collective-permute-start(bf16[240,1280]{1,0:T(8,128)(2,1)S(1)} %broadcast_select_fusion.4), channel_id=1, source_target_pairs={{0,4},{1,5},{2,6},{3,7},{4,0},{5,1},{6,2},{7,3},{8,12},{9,13},{10,... | collective-permute-start | bytes 1843208 | tf_op jit(solution)/shard_map/ppermute | solution.py:84
  479.6 8.8 %collective-permute-start.43 = (bf16[128,960]{1,0:T(8,128)(2,1)S(1)}, bf16[128,960]{1,0:T(8,128)(2,1)S(1)}, u32[]{:S(2)}, u32[]{:S(2)}) collective-permute-start(bf16[128,960]{1,0:T(8,128)(2,1)S(1)} %broadcast_select_fusion.11), channel_id=1, source_target_pairs={{0,4},{1,5},{2,6},{3,7},{4,0},{5,1},{6,2},{7,3},{8,12},{9,13},{10,... | collective-permute-start | bytes 737288 | tf_op jit(solution)/shard_map/ppermute | solution.py:84
  490.0 32.7 %collective-permute-start.57 = (bf16[448,960]{1,0:T(8,128)(2,1)S(1)}, bf16[448,960]{1,0:T(8,128)(2,1)S(1)}, u32[]{:S(2)}, u32[]{:S(2)}) collective-permute-start(bf16[448,960]{1,0:T(8,128)(2,1)S(1)} %add_convert_fusion), channel_id=1, source_target_pairs={{8,0},{9,1},{10,2},{11,3},{12,4},{13,5},{14,6},{15,7},{16,24},{17,... | collective-permute-start | bytes 2580488 | tf_op jit(solution)/shard_map/ppermute | solution.py:84
  (87 other events, 1081.7 us)

commit v4 on v3

--- a/solution.py
+++ b/solution.py
@@ -89,25 +89,25 @@
     def swap(self, value):
         return self.move(value, lambda r, s: (r ^ 1, s))
 
-    def chain(self, value):
+    def chain(self, value, streams):
         chips = self.reps // 2
         place = lax.axis_index("rep") // 2
         span = 1
         if chips % 4 == 0:
             inward, outward, middle = {0: 1, 3: 2}, {1: 0, 2: 3}, {1: 2, 2: 1}
 
-            def along(value, table):
+            def along(value, table, stream):
                 def target(r, s):
                     chip = r // 2
                     if chip % 4 not in table:
                         return None
                     return ((chip - chip % 4 + table[chip % 4]) * 2 + r % 2, s)
 
-                return self.move(value, target)
-
-            value = add(value, along(value, inward))
-            value = add(value, along(value, middle))
-            back = along(value, outward)
+                return stream(value, lambda v: self.move(v, target))
+
+            value = add(value, along(value, inward, streams[0]))
+            value = add(value, along(value, middle, streams[1]))
+            back = along(value, outward, streams[2])
             inner = (place % 4 == 1) | (place % 4 == 2)
             value = jnp.where(inner, value, back)
             span = 4
@@ -116,54 +116,38 @@
             span *= 2
         return value
 
-    def spread(self, value):
+    def beside(self, value):
+        return self.move(value, lambda r, s: (r ^ 2, s))
+
+    def near(self, value):
+        return {1 << i: self.step(value, i) for i in range(self.bits)}
+
+    def far(self, value, near):
         pieces = [value]
-        for i in range(self.bits):
-            pieces = pieces + [self.step(piece, i) for piece in pieces]
+        for t in range(1, self.shards):
+            top = t.bit_length() - 1
+            pieces.append(near[t] if t in near else self.step(pieces[t - (1 << top)], top))
         return pieces
 
-    def collect(self, pieces):
+    def collect(self, pieces, stream):
         for i in reversed(range(self.bits)):
             keep = 1 << i
-            pieces = [add(pieces[t], self.step(pieces[t + keep], i)) for t in range(keep)]
+            got = [stream(pieces[t + keep], lambda v: self.step(v, i)) for t in range(keep)]
+            pieces = [add(pieces[t], got[t]) for t in range(keep)]
         return pieces[0]
 
     def twin(self, piece):
         return piece if self.bits < 2 else piece >> 2 << 2 | (piece & 1) << 1 | (piece >> 1 & 1)
 
-    def gather_rows(self, shard_value):
-        rows = shard_value.shape[0]
-        half = rows // 2
-        mine = lax.dynamic_slice_in_dim(shard_value, self.core * half, half, 0)
-        direct = self.spread(mine)[1:]
-        starts = [self.shard * rows]
-        starts += [(self.shard ^ hop) * rows + self.core * half for hop in self.hops[1:]]
-        starts += [
-            (self.shard ^ self.hops[self.twin(t)]) * rows + (1 - self.core) * half
-            for t in range(1, self.shards)
+    def small_pieces(self, value):
+        return [
+            value if hop == 0 else self.move(value, lambda r, s, hop=hop: (r, s ^ hop))
+            for hop in range(self.shards)
         ]
-        return direct, *joined((shard_value, *direct, *map(self.swap, direct)), starts)
-
-    def gather_pair(self, left, right):
-        rows = left.shape[0]
-        mine = jnp.where(self.core == 0, left, right)
-        direct = self.spread(mine)[1:]
-        whole = rows * self.shards
-        first, second = self.core * whole, (1 - self.core) * whole
-        starts = [self.shard * rows, whole + self.shard * rows]
-        starts += [(self.shard ^ hop) * rows + first for hop in self.hops[1:]]
-        starts += [
-            (self.shard ^ self.hops[self.twin(t)]) * rows + second for t in range(1, self.shards)
-        ]
-        return direct, *joined((left, right, *direct, *map(self.swap, direct)), starts)
-
-    def gather_small(self, value):
-        pieces = jnp.stack(
-            [
-                value if hop == 0 else self.move(value, lambda r, s, hop=hop: (r, s ^ hop))
-                for hop in range(self.shards)
-            ]
-        )
+
+    def in_order(self, pieces):
+        pieces = jnp.stack(pieces)
+        value = pieces
         order = self.shard ^ jnp.arange(self.shards)
         hit = (order[:, None] == jnp.arange(self.shards)[None, :])[:, :, None, None]
         pieces = jnp.sum(jnp.where(hit, pieces[None], 0), axis=1, dtype=value.dtype)
@@ -178,10 +162,11 @@
         given = [(self.shard ^ self.hops[self.twin(t)]) * scale + theirs for t in range(self.shards)]
         return kept, given
 
-    def reduce_owned(self, kept, received):
+    def reduce_owned(self, kept, received, stream):
         block = kept.shape[0] // self.shards
         cut = lambda value, t: value[t * block : (t + 1) * block]
-        return self.collect([add(cut(kept, t), cut(received, t)) for t in range(self.shards)])
+        pieces = [add(cut(kept, t), cut(received, t)) for t in range(self.shards)]
+        return self.collect(pieces, stream)
 
     def finish_rows(self, owned, other, rows):
         low = jnp.where(self.core == 0, owned, other)
@@ -197,36 +182,54 @@
         summed = add(value, self.swap(value))
         for i in range(self.bits):
             summed = add(summed, self.step(summed, i))
-        summed = self.chain(summed)
+        summed = self.chain(summed, [direct] * 3)
         width = value.shape[1] // self.shards
         return lax.dynamic_slice_in_dim(summed, self.shard * width, width, 1)
 
 
-def joined(pieces, starts):
-    if any(piece.shape[0] % 16 for piece in pieces):
-        rows = sum(piece.shape[0] for piece in pieces)
-        whole = jnp.zeros((rows, pieces[0].shape[1]), pieces[0].dtype)
+def direct(value, move):
+    return move(value)
+
+
+def in_turn(depth):
+    done = []
+
+    def stream(value, move):
+        if len(done) >= depth:
+            value = after(value, done[-depth])
+        done.append(move(value))
+        return done[-1]
+
+    return stream
+
+
+def meet(*values):
+    return lax.optimization_barrier(values)
+
+
+def joined(pieces, starts, shape):
+    if any(piece.shape[0] % 16 or piece.shape[1] % 128 and piece.shape[1] < shape[1] for piece in pieces):
+        whole = jnp.zeros(shape, pieces[0].dtype)
         for piece, start in zip(pieces, starts):
-            whole = lax.dynamic_update_slice(whole, piece, (start, 0))
-        pieces, starts = (whole,), [0]
-    return pieces, numbers(starts)
+            whole = lax.dynamic_update_slice(whole, piece, start)
+        pieces, starts = (whole,), [(0, 0)]
+    return tuple(pieces), numbers([at for start in starts for at in start]), shape
 
 
 def numbers(values):
     return jnp.stack([jnp.asarray(value, jnp.int32) for value in values])
-
-
-def joined_shape(pieces):
-    return sum(piece.shape[0] for piece in pieces), pieces[0].shape[1]
 
 
 def load(pieces, starts_ref, whole, sems):
     copies = []
     for i, piece in enumerate(pieces):
-        start = pl.multiple_of(starts_ref[i], 16)
-        copies.append(
-            pltpu.make_async_copy(piece, whole.at[pl.ds(start, piece.shape[0]), :], sems.at[i])
-        )
+        rows = pl.ds(pl.multiple_of(starts_ref[2 * i], 16), piece.shape[0])
+        if piece.shape[1] == whole.shape[1]:
+            place = whole.at[rows, :]
+        else:
+            columns = pl.ds(pl.multiple_of(starts_ref[2 * i + 1], 128), piece.shape[1])
+            place = whole.at[rows, columns]
+        copies.append(pltpu.make_async_copy(piece, place, sems.at[i]))
         copies[-1].start()
     return copies
 
@@ -275,7 +278,7 @@
     kv_ref[:, KV_WIDTH:] = nn(act, whole[width:, width:]).astype(BF)
 
 
-def project(x, gains, cosine, sine, pieces, starts):
+def project(x, gains, cosine, sine, pieces, starts, shape):
     tokens, width = x.shape
     outs = (
         jax.ShapeDtypeStruct((tokens, width), BF),
@@ -289,7 +292,7 @@
         out_specs=(IN_VMEM,) * 3,
         out_shape=outs,
         scratch_shapes=[
-            pltpu.VMEM(joined_shape(pieces), BF),
+            pltpu.VMEM(shape, BF),
             pltpu.SemaphoreType.DMA((len(pieces),)),
         ],
         cost_estimate=cost(2 * tokens * width * (width + 2 * KV_WIDTH), 0, x, *outs, *pieces),
@@ -358,8 +361,8 @@
 def feed(x, attn, dy, gains, attention_got, pair_got, down_got):
     tokens, width = x.shape
     groups = [attention_got, pair_got, down_got]
-    counts = [len(pieces) for pieces, _ in groups]
-    shapes = [joined_shape(pieces) for pieces, _ in groups]
+    counts = [len(pieces) for pieces, _, _ in groups]
+    shapes = [shape for _, _, shape in groups]
     hidden = shapes[1][1]
     outs = (
         jax.ShapeDtypeStruct((tokens, width), BF),
@@ -371,7 +374,7 @@
         jax.ShapeDtypeStruct((tokens, width), BF),
         jax.ShapeDtypeStruct((8, width), F32),
     )
-    every = [piece for pieces, _ in groups for piece in pieces]
+    every = [piece for pieces, _, _ in groups for piece in pieces]
     return pl.pallas_call(
         functools.partial(feed_kernel, counts),
         name="feed",
@@ -385,25 +388,29 @@
             2 * tokens * width * (6 * hidden + 3 * width), tokens * hidden, x, x, x, *outs, *every
         ),
         compiler_params=pltpu.CompilerParams(vmem_limit_bytes=VMEM_MOST),
-    )(*(starts for _, starts in groups), x, attn, dy, gains, *every)
-
-
-def weight_grad_kernel(parts, block, starts_ref, *refs):
+    )(*(starts for _, starts, _ in groups), x, attn, dy, gains, *every)
+
+
+def weight_grad_kernel(parts, count, starts_ref, *refs):
     operands = refs[: 2 * len(parts)]
     out_ref = refs[2 * len(parts)]
-    turned = refs[2 * len(parts) + 1 :]
-    step = pl.program_id(0)
-
-    @pl.when(step == 0)
+    turned = refs[2 * len(parts) + 1 : 3 * len(parts) + 1]
+    ordered = refs[3 * len(parts) + 1 :]
+    block = sum(parts)
+
+    @pl.when(pl.program_id(0) == 0)
     def _():
-        for i in range(len(parts)):
+        for i, rows in enumerate(parts):
             turned[i][...] = jnp.transpose(operands[2 * i][...])
+            for t in range(count):
+                start = pl.multiple_of(starts_ref[1 + i * count + t], 16)
+                ordered[i][t * rows : (t + 1) * rows, :] = turned[i][pl.ds(start, rows), :]
 
     at = 0
     for i, rows in enumerate(parts):
-        start = pl.multiple_of(starts_ref[1 + i * pl.num_programs(0) + step], 16)
-        left = turned[i][pl.ds(start, rows), :]
-        out_ref[at : at + rows, :] = nn(left, operands[2 * i + 1][...]).astype(BF)
+        made = nn(ordered[i][...], operands[2 * i + 1][...]).astype(BF)
+        for t in range(count):
+            out_ref[t * block + at : t * block + at + rows, :] = made[t * rows : (t + 1) * rows]
         at += rows
 
 
@@ -421,24 +428,27 @@
             made.append([lax.dynamic_slice_in_dim(grad, start, rows, 0) for start in starts])
         return jnp.concatenate([part for group in zip(*made) for part in group], axis=0)
     in_specs, args, flops = [], [], 0
+    tile = next((size for size in (256, 320) if columns % size == 0 and size % 128 == 0), columns)
+    skip = column * (columns // tile)
     for left, right, rows, starts in terms:
-        in_specs.append(pl.BlockSpec(left.shape, lambda t, info: (0, 0)))
+        in_specs.append(pl.BlockSpec(left.shape, lambda n, info: (0, 0)))
         if right.ndim == 2:
-            in_specs.append(pl.BlockSpec((tokens, columns), lambda t, info: (0, column)))
+            in_specs.append(pl.BlockSpec((tokens, tile), lambda n, info: (0, skip + n)))
         else:
-            in_specs.append(pl.BlockSpec((None, tokens, columns), lambda t, info: (info[0], 0, column)))
+            in_specs.append(pl.BlockSpec((None, tokens, tile), lambda n, info: (info[0], 0, skip + n)))
         args += [left, right]
         flops += 2 * tokens * rows * count * columns
     out = jax.ShapeDtypeStruct((count * block, columns), BF)
     info = numbers([choice] + [start for term in terms for start in term[3]])
     return pl.pallas_call(
-        functools.partial(weight_grad_kernel, parts, block),
+        functools.partial(weight_grad_kernel, parts, count),
         grid_spec=pltpu.PrefetchScalarGridSpec(
             num_scalar_prefetch=1,
-            grid=(count,),
+            grid=(columns // tile,),
             in_specs=in_specs,
-            out_specs=pl.BlockSpec((block, columns), lambda t, info: (t, 0)),
-            scratch_shapes=[pltpu.VMEM((term[0].shape[1], tokens), BF) for term in terms],
+            out_specs=pl.BlockSpec((count * block, tile), lambda n, info: (0, n)),
+            scratch_shapes=[pltpu.VMEM((term[0].shape[1], tokens), BF) for term in terms]
+            + [pltpu.VMEM((count * rows, tokens), BF) for rows in parts],
         ),
         out_shape=out,
         name="weight_grad",
@@ -467,7 +477,7 @@
     ).astype(BF)
 
 
-def finish(x, low, kv, dres, gains, pieces, starts):
+def finish(x, low, kv, dres, gains, pieces, starts, shape):
     tokens, width = x.shape
     outs = (jax.ShapeDtypeStruct((tokens, width), BF), jax.ShapeDtypeStruct((8, width), F32))
     return pl.pallas_call(
@@ -477,7 +487,7 @@
         out_specs=(IN_VMEM,) * 2,
         out_shape=outs,
         scratch_shapes=[
-            pltpu.VMEM(joined_shape(pieces), BF),
+            pltpu.VMEM(shape, BF),
             pltpu.SemaphoreType.DMA((len(pieces),)),
         ],
         cost_estimate=cost(2 * tokens * width * (width + 2 * KV_WIDTH), 0, x, low, dres, *pieces),
@@ -688,13 +698,43 @@
     tokens = micro * rows
     hidden = w_gate.shape[1]
 
-    gains = links.gather_small(jnp.stack([norm_first, norm_second])).astype(F32)
-    direct, *attention_got = links.gather_pair(
-        jnp.concatenate([w_query, key_weight], axis=1),
-        jnp.concatenate([w_output, value_weight], axis=1),
-    )
-    direct, *pair_got = links.gather_pair(*after((w_gate, w_up), direct))
-    direct, *down_got = links.gather_rows(after(w_down, direct))
+    even = links.core == 0
+    side = lax.axis_index("rep") // 2 % 2
+    left = jnp.concatenate([w_query, key_weight], axis=1)
+    right = jnp.concatenate([w_output, value_weight], axis=1)
+    attn_mine = jnp.where(even, left, right)
+    pair_cut = hidden // 2
+    pair_mine = lax.dynamic_slice_in_dim(jnp.where(even, w_gate, w_up), side * pair_cut, pair_cut, 1)
+    down_cut = w_down.shape[0] // 4
+    down_mine = lax.dynamic_slice_in_dim(w_down, (links.core * 2 + side) * down_cut, down_cut, 0)
+    attn_near = links.near(attn_mine)
+    gain_pieces = links.small_pieces(jnp.stack([norm_first, norm_second]))
+    attn_mine, attn_near, gain_pieces, pair_mine, down_mine = meet(
+        attn_mine, attn_near, gain_pieces, pair_mine, down_mine
+    )
+    gains = links.in_order(gain_pieces).astype(F32)
+    attn_all = links.far(attn_mine, attn_near)
+    attn_swapped = {t: links.swap(attn_near[t]) for t in attn_near}
+    pair_near = {1: links.step(pair_mine, 0)}
+    attn_all, attn_swapped, pair_mine, pair_near, gains = meet(
+        attn_all, attn_swapped, pair_mine, pair_near, gains
+    )
+    attn_swapped = [attn_swapped.get(t, None) for t in range(shards)]
+    attn_swapped = [links.swap(attn_all[t]) if t and v is None else v for t, v in enumerate(attn_swapped)]
+    deep, shard_rows = width, width // shards
+
+    def attention_weights():
+        pieces, starts = [left, right], [(links.shard * shard_rows, 0), (deep + links.shard * shard_rows, 0)]
+        for t in range(1, shards):
+            twin = links.hops[links.twin(t)]
+            pieces += [attn_all[t], attn_swapped[t]]
+            starts += [
+                (links.core * deep + (links.shard ^ links.hops[t]) * shard_rows, 0),
+                ((1 - links.core) * deep + (links.shard ^ twin) * shard_rows, 0),
+            ]
+        return joined(pieces, starts, (2 * deep, left.shape[1]))
+
+    attention_got = attention_weights()
 
     parents = parent_ids[:, 0]
     seg = jnp.arange(segs)
@@ -726,15 +766,74 @@
 
     inputs = block_input.reshape(tokens, width)
     cotangent = out_cotangent.reshape(tokens, width)
+    pair_near |= {1 << i: links.step(pair_mine, i) for i in range(1, links.bits)}
+    pair_beside = {1: links.beside(pair_near[1])}
     queries, kv, act_first = project(inputs, gains, cosine, sine, *attention_got)
-    kv_all = [links.spread(kv[m * rows : (m + 1) * rows]) for m in range(micro)]
-    attended = ()
-    for m in range(micro):
+    kv_own = [kv[m * rows : (m + 1) * rows] for m in range(micro)]
+    queries, act_first, kv_own, pair_mine, pair_near, pair_beside = meet(
+        queries, act_first, kv_own, pair_mine, pair_near, pair_beside
+    )
+
+    kv_near = [None] * micro
+    kv_all = [None] * micro
+    kv_near[0] = links.near(kv_own[0])
+    pair_all = links.far(pair_mine, pair_near)
+    pair_beside[2] = links.beside(pair_near[2])
+    kv_near, pair_all, pair_beside, down_mine = meet(kv_near, pair_all, pair_beside, down_mine)
+
+    kv_all[0] = links.far(kv_own[0], kv_near[0])
+    for m in range(1, micro):
+        kv_near[m] = links.near(kv_own[m])
+    pair_beside |= {t: links.beside(pair_all[t]) for t in range(3, shards)}
+    pair_swapped = [None] + [links.swap(pair_all[t]) for t in range(1, shards)]
+    pair_beside_swapped = [None] + [links.swap(pair_beside[t]) for t in range(1, 3)]
+    kv_all, kv_near, kv_own, pair_beside, queries, down_mine, pair_swapped, pair_beside_swapped = meet(
+        kv_all, kv_near, kv_own, pair_beside, queries, down_mine, pair_swapped, pair_beside_swapped
+    )
+
+    for m in range(1, micro):
+        kv_all[m] = links.far(kv_own[m], kv_near[m])
+    down_near = links.near(down_mine)
+    pair_beside_swapped += [links.swap(pair_beside[t]) for t in range(3, shards)]
+    attended = attend(0, rows, seg_rows, queries, kv_all[0], bias, ())
+    kv_all, down_mine, down_near, attended, queries, pair_beside_swapped = meet(
+        kv_all, down_mine, down_near, attended, queries, pair_beside_swapped
+    )
+
+    down_all = links.far(down_mine, down_near)
+    down_beside = {t: links.beside(down_near[t]) for t in down_near}
+    down_swapped = {t: links.swap(down_near[t]) for t in down_near}
+    for m in range(1, micro):
         attended = attend(m, rows, seg_rows, queries, kv_all[m], bias, attended)
+    attended, down_all, down_beside, down_swapped = meet(attended, down_all, down_beside, down_swapped)
     attn, lse = attended
+    down_beside = [down_beside[t] if t in down_beside else links.beside(down_all[t]) for t in range(1, shards)]
+    down_swapped = [down_swapped[t] if t in down_swapped else links.swap(down_all[t]) for t in range(1, shards)]
+    down_beside_swapped = [links.swap(piece) for piece in down_beside]
+
+    def pair_weights():
+        pieces, starts = [w_gate, w_up], [(links.shard * shard_rows, 0), (deep + links.shard * shard_rows, 0)]
+        for t in range(1, shards):
+            twin = links.hops[links.twin(t)]
+            row = links.core * deep + (links.shard ^ links.hops[t]) * shard_rows
+            far_row = (1 - links.core) * deep + (links.shard ^ twin) * shard_rows
+            pieces += [pair_all[t], pair_beside[t], pair_swapped[t], pair_beside_swapped[t]]
+            starts += [(at, turn * pair_cut) for at in (row, far_row) for turn in (side, 1 - side)]
+        return joined(pieces, starts, (2 * deep, hidden))
+
+    def down_weights():
+        own = w_down.shape[0]
+        pieces, starts = [w_down], [(links.shard * own, 0)]
+        for t in range(1, shards):
+            twin = links.hops[links.twin(t)]
+            row = (links.shard ^ links.hops[t]) * own + links.core * 2 * down_cut
+            far_row = (links.shard ^ twin) * own + (1 - links.core) * 2 * down_cut
+            pieces += [down_all[t], down_beside[t - 1], down_swapped[t - 1], down_beside_swapped[t - 1]]
+            starts += [(at + turn * down_cut, 0) for at in (row, far_row) for turn in (side, 1 - side)]
+        return joined(pieces, starts, (own * shards, width))
 
     block_out, inner, slopes, act_second, d_resid, d_resid_low, d_attn, gain_two_sum = feed(
-        inputs, attn, cotangent, gains, attention_got, pair_got, down_got
+        inputs, attn, cotangent, gains, attention_got, pair_weights(), down_weights()
     )
     down_rows, output_rows, wide_rows = hidden // shards, width // shards, width // shards
     down_half, output_half = down_rows // 2, links.half_rows(output_rows)
@@ -748,51 +847,58 @@
             (attn, d_resid_low, output_half[0], output),
         )
     )
+    around = in_turn(2)
+    along = [in_turn(1) for _ in range(3)]
+    wide_kept, wide_given = links.order(wide_rows, 0, 0)
+    chunks = 2
+    wide_grads = lambda c, starts, choice: weight_grad(
+        ((act_second, slopes, wide_rows, starts),), c, hidden // chunks, choice
+    )
+
+    def whole_sum(kept, received):
+        owned = links.chain(links.reduce_owned(kept, received, around), along)
+        return owned, links.swap(owned)
+
     rows_received = links.swap(rows_grads(down_given, output_given))
     rows_kept = rows_grads(down_kept, output_kept)
-    rows_owned = links.reduce_owned(rows_kept, rows_received)
-    wide_kept, wide_given = links.order(wide_rows, 0, 0)
-    chunks = 2
-    wide_owned = []
-    wide_received = []
-    for c in range(chunks):
-        given, kept = (
-            weight_grad(((act_second, slopes, wide_rows, starts),), c, hidden // chunks, choice)
-            for starts, choice in ((wide_given, 1 - links.core), (wide_kept, links.core))
-        )
-        wide_received.append(links.swap(given))
-        wide_owned.append(links.reduce_owned(kept, wide_received[c]))
+    wide_received = [links.swap(wide_grads(c, wide_given, 1 - links.core)) for c in range(chunks)]
+    wide_parts = [wide_grads(c, wide_kept, links.core) for c in range(chunks)]
+    d_attn, rows_received, rows_kept, wide_received, wide_parts = meet(
+        d_attn, rows_received, rows_kept, wide_received, wide_parts
+    )
 
     d_queries, d_kv = (), []
-    d_attn = after(d_attn, rows_received, *wide_received)
+    rows_sum = whole_sum(rows_kept, rows_received)
+    wide_sums = []
     for m in range(micro):
         d_queries, *pieces = attend_back(
             m, rows, seg_rows, queries, kv_all[m], bias, attn, d_attn, lse, cosine_t, sine_t, d_queries
         )
         d_queries = (d_queries,)
-        d_kv.append(links.collect(pieces))
+        d_kv.append(links.collect(pieces, around))
+        if m < chunks:
+            wide_sums.append(whole_sum(wide_parts[m], wide_received[m]))
+    for m in range(micro, chunks):
+        wide_sums.append(whole_sum(wide_parts[m], wide_received[m]))
     d_queries = d_queries[0]
     d_kv = turn_back(d_kv, cosine, sine)
     half, mine, theirs = links.half_rows(width // shards)
     qkv_kept, qkv_given = links.order(width // shards, mine, theirs)
     q_received = links.swap(weight_grad(((act_first, d_queries, half, qkv_given),)))
-    q_owned = links.reduce_owned(weight_grad(((act_first, d_queries, half, qkv_kept),)), q_received)
+    q_sum = whole_sum(weight_grad(((act_first, d_queries, half, qkv_kept),)), q_received)
     kv_received = links.swap(weight_grad(((act_first, d_kv, half, qkv_given),)))
-    kv_owned = links.reduce_owned(weight_grad(((act_first, d_kv, half, qkv_kept),)), kv_received)
+    kv_sum = whole_sum(weight_grad(((act_first, d_kv, half, qkv_kept),)), kv_received)
     d_input, gain_one_sum = finish(inputs, d_queries, d_kv, d_resid, gains, *attention_got)
     gain_sums = links.reduce_small(jnp.concatenate([gain_one_sum[:1], gain_two_sum[:1]]))
 
-    def whole_sum(owned):
-        owned = links.chain(owned)
-        return owned, links.swap(owned)
-
-    rows_owned, rows_other = whole_sum(rows_owned)
+    rows_owned, rows_other = rows_sum
     grad_down = links.finish_rows(rows_owned[:down_half], rows_other[:down_half], down_rows)
     grad_output = links.finish_rows(rows_owned[down_half:], rows_other[down_half:], output_rows)
-    wide = [links.finish_pair(*whole_sum(owned)) for owned in wide_owned]
-    grad_gate, grad_upper = (jnp.concatenate(parts, axis=1) for parts in zip(*wide))
-    grad_query = links.finish_rows(*whole_sum(q_owned), width // shards)
-    grad_kv = links.finish_rows(*whole_sum(kv_owned), width // shards)
+    grad_gate, grad_upper = (
+        jnp.concatenate(parts, axis=1) for parts in zip(*(links.finish_pair(*pair) for pair in wide_sums))
+    )
+    grad_query = links.finish_rows(*q_sum, width // shards)
+    grad_kv = links.finish_rows(*kv_sum, width // shards)
     return (
         block_out.reshape(micro, rows, width),
         d_input.reshape(micro, rows, width),

time: 541 us -> 531 us (0.982)
  waiting for transfers between devices: 166 us -> 144 us
  starting transfers between devices: 101 us -> 110 us
    ppermute x79 -> x91, waiting for transfers between devices: 166 us -> 144 us  [move(): return lax.ppermute(value, AXES, pairs)]
    ppermute x79 -> x91, starting transfers between devices: 101 us -> 110 us  [move(): return lax.ppermute(value, AXES, pairs)]
    convert_element_type x29, other arithmetic: 44.1 us -> 37.6 us  [add(): return (left.astype(F32) + right.astype(F32)).astype(left.dtype)]
    unnamed x162 -> x233, local copies, waits for them, and re-layouts: 42.9 us -> 48.5 us
  transfers between devices with their start and end apart: 79 -> 91, of which waited for: 21 -> 33; matrix products, arithmetic and copies ran while one was open for 20% -> 16% of each run, Pallas kernels for 19% -> 19%
where the time goes in v4:
time: 531 us; the launch traced here: 525 us
  waiting for transfers between devices  144 us (27%)
  Pallas kernels  137 us (26%)
  starting transfers between devices  110 us (21%)
  local copies, waits for them, and re-layouts  72.9 us (14%)
  other arithmetic  58.1 us (11%)
    ppermute x91, waiting for transfers between devices, move(): return lax.ppermute(value, AXES, pairs)  144 us
    ppermute x91, starting transfers between devices, move(): return lax.ppermute(value, AXES, pairs)  110 us
    unnamed x233, local copies, waits for them, and re-layouts  48.5 us
    pallas_call x10, Pallas kernels, weight_grad(): pl.pallas_call(functools.partial(weight_grad_kernel, parts, count), grid_...  40 us
    convert_element_type x29, other arithmetic, add(): return (left.astype(F32) + right.astype(F32)).astype(left.dtype)  37.6 us
    pallas_call x2, Pallas kernels, attend_back(): pl.pallas_call(functools.partial(attend_back_kernel, shards, seg_rows), g...  32.6 us
    pallas_call x1, Pallas kernels, feed(): pl.pallas_call(functools.partial(feed_kernel, counts), name='feed', in_sp...  31.4 us
    pallas_call x2, Pallas kernels, attend(): pl.pallas_call(functools.partial(attend_kernel, shards, seg_rows), grid=(...  16.1 us
  transfers between devices with their start and end apart: 91, of which 33 were waited for; matrix products, arithmetic and copies ran while one was open for 16% of the time, Pallas kernels for 19%

profile of v4, /device:TPU:0, one launch (start us, length us, event | category | flops | bytes accessed | tf_op | source)
XLA Modules:
  0.0 524.9 jit_solution(16058489650745548189)
XLA Ops:
  4.4 3.0 collective-permute-start
  9.6 2.9 collective-permute-start.4
  12.5 2.4 copy.108.refs_22_
  16.9 2.2 dynamic-slice_select_fusion
  19.2 2.4 collective-permute-done.2
  26.5 11.7 %collective-permute-done.5.refs_6_ = bf16[240,1280]{1,0:T(8,128)(2,1)S(1)} collective-permute-done((bf16[240,1280]{1,0:T(8,128)(2,1)S(1)}, bf16[240,1280]{1,0:T(8,128)(2,1)S(1)}, u32[]{:S(2)}, u32[]{:S(2)}) %collective-permute-start.5) | collective-permute-done | bytes 614432 | tf_op jit(solution)/shard_map/ppermute | solution.py:84
  40.1 3.1 collective-permute-start.11
  46.7 2.3 copy.105
  53.3 7.7 %project.1 = (bf16[512,960]{1,0:T(8,128)(2,1)}, bf16[512,640]{1,0:T(8,128)(2,1)S(1)}, bf16[512,960]{1,0:T(8,128)(2,1)}) custom-call(s32[16]{0:T(128)S(1)} %stack.257.starts_ref.s0_ref, bf16[512,960]{1,0:T(8,128)(2,1)} %bitcast.71, f32[2,960]{1,0:T(2,128)S(1)} %maximum_convert_fusion.6.gains_ref, f32[512,128]{1,0:T(8,128)S(1)} %copy-done.42, ...), custom_call_target="tpu_custom_call" | custom-call | flops 1572864000 | bytes 8519680 | tf_op jit(solution)/shard_map/project/pallas_call | solution.py:288
  66.4 6.9 %collective-permute-done.12.refs_1_ = bf16[256,640]{1,0:T(8,128)(2,1)S(1)} collective-permute-done((bf16[256,640]{1,0:T(8,128)(2,1)S(1)}, bf16[256,640]{1,0:T(8,128)(2,1)S(1)}, u32[]{:S(2)}, u32[]{:S(2)}) %collective-permute-start.12) | collective-permute-done | bytes 327712 | tf_op jit(solution)/shard_map/ppermute | solution.py:84
  73.3 5.3 %collective-permute-done.13.refs_2_ = bf16[256,640]{1,0:T(8,128)(2,1)S(1)} collective-permute-done((bf16[256,640]{1,0:T(8,128)(2,1)S(1)}, bf16[256,640]{1,0:T(8,128)(2,1)S(1)}, u32[]{:S(2)}, u32[]{:S(2)}) %collective-permute-start.13) | collective-permute-done | bytes 327712 | tf_op jit(solution)/shard_map/ppermute | solution.py:84
  80.3 2.6 collective-permute-start.17
  85.0 6.4 %collective-permute-done.17.refs_1_ = bf16[256,640]{1,0:T(8,128)(2,1)S(1)} collective-permute-done((bf16[256,640]{1,0:T(8,128)(2,1)S(1)}, bf16[256,640]{1,0:T(8,128)(2,1)S(1)}, u32[]{:S(2)}, u32[]{:S(2)}) %collective-permute-start.17) | collective-permute-done | bytes 327712 | tf_op jit(solution)/shard_map/ppermute | solution.py:84
  102.1 8.0 %attend.2 = (bf16[512,960]{1,0:T(8,128)(2,1)S(1)}, f32[512,128]{1,0:T(8,128)S(1)}) custom-call(bf16[512,960]{1,0:T(8,128)(2,1)S(1)} %copy-done.60, bf16[256,640]{1,0:T(8,128)(2,1)S(1)} %get-tuple-element.231.refs_0_, bf16[256,640]{1,0:T(8,128)(2,1)S(1)} %collective-permute-done.12.refs_1_, bf16[256,640]{1,0:T(8,128)(2,1)S(1)} %collective-permute-done.13.refs_2_, ...), custom_call_target="tpu_custom_call" | custom-call | flops 4026531840 | bytes 983040 | tf_op jit(solution)/shard_map/attend/pallas_call | solution.py:636
  115.9 8.0 %attend.3 = (bf16[512,960]{1,0:T(8,128)(2,1)S(1)}, f32[512,128]{1,0:T(8,128)S(1)}) custom-call(bf16[512,960]{1,0:T(8,128)(2,1)S(1)} %copy-done.60, bf16[256,640]{1,0:T(8,128)(2,1)S(1)} %get-tuple-element.197.refs_0_, bf16[256,640]{1,0:T(8,128)(2,1)S(1)} %collective-permute-done.17.refs_1_, ...), custom_call_target="tpu_custom_call", output_to_operand_aliasing={{0}: (6, {}), {1}: (7, {})} | custom-call | flops 4026531840 | bytes 983040 | tf_op jit(solution)/shard_map/attend/pallas_call | solution.py:636
  124.7 4.9 collective-permute-done.31.refs_28_
  131.1 6.5 %collective-permute-done.36.refs_32_ = bf16[160,960]{1,0:T(8,128)(2,1)S(1)} collective-permute-done((bf16[160,960]{1,0:T(8,128)(2,1)S(1)}, bf16[160,960]{1,0:T(8,128)(2,1)S(1)}, u32[]{:S(2)}, u32[]{:S(2)}) %collective-permute-start.36) | collective-permute-done | bytes 307232 | tf_op jit(solution)/shard_map/ppermute | solution.py:84
  141.5 31.4 %feed.1 = (bf16[512,960]{1,0:T(8,128)(2,1)}, bf16[512,2560]{1,0:T(8,128)(2,1)}, bf16[2,512,2560]{2,1,0:T(8,128)(2,1)}, bf16[512,960]{1,0:T(8,128)(2,1)}, f32[512...) custom-call(s32[16]{0:T(128)} %copy-done.58, s32[28]{0:T(128)} %stack.260.s1_ref, ...), custom_call_target="tpu_custom_call" | custom-call | flops 17930649600 | bytes 36403200 | tf_op jit(solution)/shard_map/feed/pallas_call | solution.py:378
  177.0 5.1 weight_grad.10
  182.1 6.0 %copy.114 = bf16[1792,960]{0,1:T(8,128)(2,1)} copy(bf16[1792,960]{1,0:T(8,128)(2,1)} %weight_grad.10) | data formatting | bytes 6881280 | tf_op jit(solution)/shard_map/weight_grad/pallas_call | solution.py:443
  188.6 6.2 %weight_grad.13 = bf16[960,1280]{1,0:T(8,128)(2,1)} custom-call(s32[5]{0:T(128)S(1)} %stack.306.starts_ref, bf16[512,960]{1,0:T(8,128)(2,1)S(1)} %copy-done, bf16[2,512,2560]{2,1,0:T(8,128)(2,1)} %get-tuple-element.228.refs_1_), custom_call_target="tpu_custom_call" | custom-call | flops 1258291200 | bytes 8683520 | tf_op jit(solution)/shard_map/weight_grad/pallas_call | solution.py:443
  194.8 6.2 %weight_grad.12 = bf16[960,1280]{1,0:T(8,128)(2,1)} custom-call(s32[5]{0:T(128)S(1)} %stack.306.starts_ref, bf16[512,960]{1,0:T(8,128)(2,1)S(1)} %copy-done, bf16[2,512,2560]{2,1,0:T(8,128)(2,1)} %get-tuple-element.228.refs_1_), custom_call_target="tpu_custom_call" | custom-call | flops 1258291200 | bytes 8683520 | tf_op jit(solution)/shard_map/weight_grad/pallas_call | solution.py:443
  201.8 5.1 weight_grad.15
  206.9 5.4 %weight_grad.14 = bf16[960,1280]{1,0:T(8,128)(2,1)S(1)} custom-call(s32[5]{0:T(128)S(1)} %stack.308.starts_ref, bf16[512,960]{1,0:T(8,128)(2,1)S(1)} %copy-done, bf16[2,512,2560]{2,1,0:T(8,128)(2,1)} %get-tuple-element.228.refs_1_), custom_call_target="tpu_custom_call" | custom-call | flops 1258291200 | bytes 8683520 | tf_op jit(solution)/shard_map/weight_grad/pallas_call | solution.py:443
  213.8 5.2 weight_grad.11
  219.1 6.0 %copy.115 = bf16[1792,960]{1,0:T(8,128)(2,1)} copy(bf16[1792,960]{0,1:T(8,128)(2,1)} %collective-permute-done.39) | data formatting | bytes 6881280 | tf_op jit(solution)/shard_map/optimization_barrier | solution.py:207
  227.0 2.3 collective-permute-start.42
  229.3 11.4 %collective-permute-done.42 = bf16[448,960]{1,0:T(8,128)(2,1)S(1)} collective-permute-done((bf16[448,960]{1,0:T(8,128)(2,1)S(1)}, bf16[448,960]{1,0:T(8,128)(2,1)S(1)}, u32[]{:S(2)}, u32[]{:S(2)}) %collective-permute-start.42) | collective-permute-done | bytes 860192 | tf_op jit(solution)/shard_map/ppermute | solution.py:84
  240.7 3.0 add_convert_fusion.5
  246.2 11.0 %collective-permute-done.44 = bf16[448,960]{1,0:T(8,128)(2,1)S(1)} collective-permute-done((bf16[448,960]{1,0:T(8,128)(2,1)S(1)}, bf16[448,960]{1,0:T(8,128)(2,1)S(1)}, u32[]{:S(2)}, u32[]{:S(2)}) %collective-permute-start.44) | collective-permute-done | bytes 860192 | tf_op jit(solution)/shard_map/ppermute | solution.py:84
  259.3 16.1 %attend_back.2 = (bf16[512,960]{1,0:T(8,128)(2,1)S(1)}, bf16[256,640]{1,0:T(8,128)(2,1)S(1)}, bf16[256,640]{1,0:T(8,128)(2,1)S(1)}, bf16[256,640]{1,0:T(8,128)(2,1)S(1)}, bf16[256,640]{1,0:T(8,128)(2,1)S(1)}) custom-call(bf16[512,960]{1,0:T(8,128)(2,1)S(1)} %copy-done.61, bf16[256,640]{1,0:T(8,128)(2,1)S(1)} %copy-done.47, bf16[256,640]{1,0:T(8,128)(2,1)S(1)} %copy-done.68, ...), custom_call_target="tpu_custom_call" | custom-call | flops 10066329600 | bytes 983040 | tf_op jit(solution)/shard_map/attend_back/pallas_call | solution.py:661
  279.2 5.0 collective-permute-done.46
  284.3 3.5 collective-permute-done.43
  288.6 2.2 add_convert_fusion.26
  290.8 4.0 collective-permute-done.47
  295.6 3.2 collective-permute-start.48
  299.0 3.6 add_convert_fusion.2
  302.6 3.9 collective-permute-start.61
  307.3 2.9 add_convert_fusion.23
  312.3 16.5 %attend_back.3 = (bf16[512,960]{1,0:T(8,128)(2,1)S(1)}, bf16[256,640]{1,0:T(8,128)(2,1)S(1)}, bf16[256,640]{1,0:T(8,128)(2,1)S(1)}, bf16[256,640]{1,0:T(8,128)(2,1)S(1)}, bf16[256,640]{1,0:T(8,128)(2,1)}) custom-call(bf16[512,960]{1,0:T(8,128)(2,1)S(1)} %copy-done.62, bf16[256,640]{1,0:T(8,128)(2,1)S(1)} %copy-done.45, ...), custom_call_target="tpu_custom_call", output_to_operand_aliasing={{0}: (11, {})} | custom-call | flops 10066329600 | bytes 983040 | tf_op jit(solution)/shard_map/attend_back/pallas_call | solution.py:661
  334.5 2.2 copy.120
  337.6 2.2 copy.126
  342.7 2.3 add_convert_fusion.22
  345.1 2.7 add_convert_fusion.1
  349.4 3.6 collective-permute-done.51
  353.0 2.3 fusion.7
  360.9 2.2 add_convert_fusion.40
  376.6 8.4 %finish.1 = (bf16[512,960]{1,0:T(8,128)(2,1)}, f32[8,960]{1,0:T(8,128)S(1)}) custom-call(s32[16]{0:T(128)S(1)} %copy-done.59, bf16[512,960]{1,0:T(8,128)(2,1)} %bitcast.73, bf16[512,960]{1,0:T(8,128)(2,1)} %copy-done.10, bf16[512,640]{1,0:T(8,128)(2,1)S(1)} %turn_back.1.kv_ref.refs_1_, f32[512,960]{1,0:T(8,128)} %get-tuple-element.259.dres_ref, ...), custom_call_target="tpu_custom_call" | custom-call | flops 1572864000 | bytes 8847360 | tf_op jit(solution)/shard_map/finish/pallas_call | solution.py:483
  387.0 4.8 collective-permute-start.62
  391.9 6.2 %collective-permute-done.69 = bf16[448,960]{1,0:T(8,128)(2,1)S(1)} collective-permute-done((bf16[448,960]{1,0:T(8,128)(2,1)S(1)}, bf16[448,960]{1,0:T(8,128)(2,1)S(1)}, u32[]{:S(2)}, u32[]{:S(2)}) %collective-permute-start.69) | collective-permute-done | bytes 860192 | tf_op jit(solution)/shard_map/ppermute | solution.py:84
  401.3 4.2 collective-permute-done.62
  409.7 5.1 collective-permute-start.88
  414.7 2.2 weight_grad.19
  419.9 2.2 copy.127
  425.4 4.4 collective-permute-done.90
  431.8 3.7 collective-permute-done.57
  439.6 8.8 %collective-permute-done.58 = bf16[240,1280]{1,0:T(8,128)(2,1)S(1)} collective-permute-done((bf16[240,1280]{1,0:T(8,128)(2,1)S(1)}, bf16[240,1280]{1,0:T(8,128)(2,1)S(1)}, u32[]{:S(2)}, u32[]{:S(2)}) %collective-permute-start.58) | collective-permute-done | bytes 614432 | tf_op jit(solution)/shard_map/ppermute | solution.py:84
  449.9 8.9 %collective-permute-start.63 = (bf16[240,1280]{1,0:T(8,128)(2,1)S(1)}, bf16[240,1280]{1,0:T(8,128)(2,1)S(1)}, u32[]{:S(2)}, u32[]{:S(2)}) collective-permute-start(bf16[240,1280]{1,0:T(8,128)(2,1)S(1)} %add_convert_fusion.16), channel_id=1, source_target_pairs={{0,8},{1,9},{2,10},{3,11},{4,12},{5,13},{6,14},{7,15},{24,16},{25,... | collective-permute-start | bytes 1843208 | tf_op jit(solution)/shard_map/ppermute | solution.py:84
  468.5 9.1 %collective-permute-start.64 = (bf16[128,960]{1,0:T(8,128)(2,1)S(1)}, bf16[128,960]{1,0:T(8,128)(2,1)S(1)}, u32[]{:S(2)}, u32[]{:S(2)}) collective-permute-start(bf16[128,960]{1,0:T(8,128)(2,1)S(1)} %add_convert_fusion.35), channel_id=1, source_target_pairs={{0,8},{1,9},{2,10},{3,11},{4,12},{5,13},{6,14},{7,15},{24,16},{25,... | collective-permute-start | bytes 737288 | tf_op jit(solution)/shard_map/ppermute | solution.py:84
  479.0 4.1 collective-permute-done.77
  483.9 2.6 collective-permute-start.78
  495.4 5.5 %collective-permute-done.71 = bf16[240,1280]{1,0:T(8,128)(2,1)} collective-permute-done((bf16[240,1280]{1,0:T(8,128)(2,1)S(1)}, bf16[240,1280]{1,0:T(8,128)(2,1)}, u32[]{:S(2)}, u32[]{:S(2)}) %collective-permute-start.71) | collective-permute-done | bytes 614432 | tf_op jit(solution)/shard_map/ppermute | solution.py:84
  503.7 6.8 %collective-permute-done.72 = bf16[128,960]{1,0:T(8,128)(2,1)S(1)} collective-permute-done((bf16[128,960]{1,0:T(8,128)(2,1)S(1)}, bf16[128,960]{1,0:T(8,128)(2,1)S(1)}, u32[]{:S(2)}, u32[]{:S(2)}) %collective-permute-start.72) | collective-permute-done | bytes 245792 | tf_op jit(solution)/shard_map/ppermute | solution.py:84
  513.5 4.1 collective-permute-done.80
  (482 shorter events, 161.1 us)
Async XLA Ops:
  4.4 18.2 %collective-permute-start = (bf16[240,1280]{1,0:T(8,128)(2,1)S(1)}, bf16[240,1280]{1,0:T(8,128)(2,1)S(1)}, u32[]{:S(2)}, u32[]{:S(2)}) collective-permute-start(bf16[240,1280]{1,0:T(8,128)(2,1)S(1)} %get-tuple-element.342), channel_id=1, source_target_pairs={{0,1},{1,0},{2,3},{3,2},{4,6},{5,7},{6,4},{7,5},{8,9},{9,8},{10,11... | collective-permute-start | bytes 1843208 | tf_op jit(solution)/shard_map/ppermute | solution.py:84
  7.4 15.2 %collective-permute-start.1 = (bf16[240,1280]{1,0:T(8,128)(2,1)S(1)}, bf16[240,1280]{1,0:T(8,128)(2,1)S(1)}, u32[]{:S(2)}, u32[]{:S(2)}) collective-permute-start(bf16[240,1280]{1,0:T(8,128)(2,1)S(1)} %get-tuple-element.342), channel_id=1, source_target_pairs={{0,2},{1,3},{2,0},{3,1},{4,5},{5,4},{6,7},{7,6},{8,10},{9,11},{10,... | collective-permute-start | bytes 1843208 | tf_op jit(solution)/shard_map/ppermute | solution.py:84
  9.0 12.6 %collective-permute-start.2 = (bf16[2,240]{1,0:T(2,128)(2,1)S(1)}, bf16[2,240]{1,0:T(2,128)(2,1)S(1)}, u32[]{:S(2)}, u32[]{:S(2)}) collective-permute-start(bf16[2,240]{1,0:T(2,128)(2,1)S(1)} %pad_maximum_fusion.5), channel_id=1, source_target_pairs={{0,1},{1,0},{2,3},{3,2},{4,5},{5,4},{6,7},{7,6},{8,9},{9,8},{10,11... | collective-permute-start | bytes 2888 | tf_op jit(solution)/shard_map/ppermute | solution.py:84
  9.6 12.0 %collective-permute-start.3 = (bf16[2,240]{1,0:T(2,128)(2,1)S(1)}, bf16[2,240]{1,0:T(2,128)(2,1)S(1)}, u32[]{:S(2)}, u32[]{:S(2)}) collective-permute-start(bf16[2,240]{1,0:T(2,128)(2,1)S(1)} %pad_maximum_fusion.5), channel_id=1, source_target_pairs={{0,2},{1,3},{2,0},{3,1},{4,6},{5,7},{6,4},{7,5},{8,10},{9,11},{10,... | collective-permute-start | bytes 2888 | tf_op jit(solution)/shard_map/ppermute | solution.py:84
  9.6 13.0 %collective-permute-start.4 = (bf16[2,240]{1,0:T(2,128)(2,1)S(1)}, bf16[2,240]{1,0:T(2,128)(2,1)S(1)}, u32[]{:S(2)}, u32[]{:S(2)}) collective-permute-start(bf16[2,240]{1,0:T(2,128)(2,1)S(1)} %pad_maximum_fusion.5), channel_id=1, source_target_pairs={{0,3},{1,2},{2,1},{3,0},{4,7},{5,6},{6,5},{7,4},{8,11},{9,10},{10,... | collective-permute-start | bytes 2888 | tf_op jit(solution)/shard_map/ppermute | solution.py:84
  22.6 15.6 %collective-permute-start.5 = (bf16[240,1280]{1,0:T(8,128)(2,1)S(1)}, bf16[240,1280]{1,0:T(8,128)(2,1)S(1)}, u32[]{:S(2)}, u32[]{:S(2)}) collective-permute-start(bf16[240,1280]{1,0:T(8,128)(2,1)S(1)} %collective-permute-done.refs_2_), channel_id=1, source_target_pairs={{0,2},{1,3},{2,0},{3,1},{4,5},{5,4},{6,7},{7,6},{8,10},{9,11},{10,... | collective-permute-start | bytes 1843208 | tf_op jit(solution)/shard_map/ppermute | solution.py:84
  23.3 14.9 %collective-permute-start.6 = (bf16[240,1280]{1,0:T(8,128)(2,1)S(1)}, bf16[240,1280]{1,0:T(8,128)(2,1)S(1)}, u32[]{:S(2)}, u32[]{:S(2)}) collective-permute-start(bf16[240,1280]{1,0:T(8,128)(2,1)S(1)} %collective-permute-done.refs_2_), channel_id=1, source_target_pairs={{0,4},{1,5},{2,6},{3,7},{4,0},{5,1},{6,2},{7,3},{8,12},{9,13},{10,... | collective-permute-start | bytes 1843208 | tf_op jit(solution)/shard_map/ppermute | solution.py:84
  24.1 15.0 %collective-permute-start.7 = (bf16[240,1280]{1,0:T(8,128)(2,1)S(1)}, bf16[240,1280]{1,0:T(8,128)(2,1)S(1)}, u32[]{:S(2)}, u32[]{:S(2)}) collective-permute-start(bf16[240,1280]{1,0:T(8,128)(2,1)S(1)} %collective-permute-done.1.refs_4_), channel_id=1, source_target_pairs={{0,4},{1,5},{2,6},{3,7},{4,0},{5,1},{6,2},{7,3},{8,12},{9,13},{10,... | collective-permute-start | bytes 1843208 | tf_op jit(solution)/shard_map/ppermute | solution.py:84
  24.1 15.8 %collective-permute-start.8 = (bf16[240,1280]{1,0:T(8,128)(2,1)}, bf16[240,1280]{1,0:T(8,128)(2,1)}, u32[]{:S(2)}, u32[]{:S(2)}) collective-permute-start(bf16[240,1280]{1,0:T(8,128)(2,1)} %dynamic-slice_select_fusion), channel_id=1, source_target_pairs={{0,1},{1,0},{2,3},{3,2},{4,6},{5,7},{6,4},{7,5},{8,9},{9,8},{10,11... | collective-permute-start | bytes 1843208 | tf_op jit(solution)/shard_map/ppermute | solution.py:84
  40.0 21.7 %collective-permute-start.10 = (bf16[240,1280]{1,0:T(8,128)(2,1)}, bf16[240,1280]{1,0:T(8,128)(2,1)}, u32[]{:S(2)}, u32[]{:S(2)}) collective-permute-start(bf16[240,1280]{1,0:T(8,128)(2,1)} %dynamic-slice_select_fusion), channel_id=1, source_target_pairs={{0,2},{1,3},{2,0},{3,1},{4,5},{5,4},{6,7},{7,6},{8,10},{9,11},{10,... | collective-permute-start | bytes 1843208 | tf_op jit(solution)/shard_map/ppermute | solution.py:84
  40.1 21.6 %collective-permute-start.11 = (bf16[240,1280]{1,0:T(8,128)(2,1)}, bf16[240,1280]{1,0:T(8,128)(2,1)}, u32[]{:S(2)}, u32[]{:S(2)}) collective-permute-start(bf16[240,1280]{1,0:T(8,128)(2,1)} %collective-permute-done.8.refs_10_), channel_id=1, source_target_pairs={{0,8},{1,9},{2,10},{3,11},{4,12},{5,13},{6,14},{7,15},{8,0},{9,1},... | collective-permute-start | bytes 1843208 | tf_op jit(solution)/shard_map/ppermute | solution.py:84
  61.7 16.9 %collective-permute-start.14 = (bf16[240,1280]{1,0:T(8,128)(2,1)}, bf16[240,1280]{1,0:T(8,128)(2,1)S(1)}, u32[]{:S(2)}, u32[]{:S(2)}) collective-permute-start(bf16[240,1280]{1,0:T(8,128)(2,1)} %collective-permute-done.8.refs_10_), channel_id=1, source_target_pairs={{0,2},{1,3},{2,0},{3,1},{4,5},{5,4},{6,7},{7,6},{8,10},{9,11},{10,... | collective-permute-start | bytes 1843208 | tf_op jit(solution)/shard_map/ppermute | solution.py:84
  62.5 16.1 %collective-permute-start.15 = (bf16[240,1280]{1,0:T(8,128)(2,1)}, bf16[240,1280]{1,0:T(8,128)(2,1)S(1)}, u32[]{:S(2)}, u32[]{:S(2)}) collective-permute-start(bf16[240,1280]{1,0:T(8,128)(2,1)} %collective-permute-done.10.refs_14_), channel_id=1, source_target_pairs={{0,8},{1,9},{2,10},{3,11},{4,12},{5,13},{6,14},{7,15},{8,0},{9,1},... | collective-permute-start | bytes 1843208 | tf_op jit(solution)/shard_map/ppermute | solution.py:84
  62.7 10.6 %collective-permute-start.12 = (bf16[256,640]{1,0:T(8,128)(2,1)S(1)}, bf16[256,640]{1,0:T(8,128)(2,1)S(1)}, u32[]{:S(2)}, u32[]{:S(2)}) collective-permute-start(bf16[256,640]{1,0:T(8,128)(2,1)S(1)} %get-tuple-element.231.refs_0_), channel_id=1, source_target_pairs={{0,1},{1,0},{2,3},{3,2},{4,6},{5,7},{6,4},{7,5},{8,9},{9,8},{10,11... | collective-permute-start | bytes 983048 | tf_op jit(solution)/shard_map/ppermute | solution.py:84
  64.5 14.1 %collective-permute-start.13 = (bf16[256,640]{1,0:T(8,128)(2,1)S(1)}, bf16[256,640]{1,0:T(8,128)(2,1)S(1)}, u32[]{:S(2)}, u32[]{:S(2)}) collective-permute-start(bf16[256,640]{1,0:T(8,128)(2,1)S(1)} %get-tuple-element.231.refs_0_), channel_id=1, source_target_pairs={{0,2},{1,3},{2,0},{3,1},{4,5},{5,4},{6,7},{7,6},{8,10},{9,11},{10,... | collective-permute-start | bytes 983048 | tf_op jit(solution)/shard_map/ppermute | solution.py:84
  79.7 15.7 %collective-permute-start.19 = (bf16[240,1280]{1,0:T(8,128)(2,1)S(1)}, bf16[240,1280]{1,0:T(8,128)(2,1)}, u32[]{:S(2)}, u32[]{:S(2)}) collective-permute-start(bf16[240,1280]{1,0:T(8,128)(2,1)S(1)} %collective-permute-done.14.refs_18_), channel_id=1, source_target_pairs={{0,8},{1,9},{2,10},{3,11},{4,12},{5,13},{6,14},{7,15},{8,0},{9,1},... | collective-permute-start | bytes 1843208 | tf_op jit(solution)/shard_map/ppermute | solution.py:84
  80.3 11.1 %collective-permute-start.17 = (bf16[256,640]{1,0:T(8,128)(2,1)S(1)}, bf16[256,640]{1,0:T(8,128)(2,1)S(1)}, u32[]{:S(2)}, u32[]{:S(2)}) collective-permute-start(bf16[256,640]{1,0:T(8,128)(2,1)S(1)} %get-tuple-element.197.refs_0_), channel_id=1, source_target_pairs={{0,1},{1,0},{2,3},{3,2},{4,6},{5,7},{6,4},{7,5},{8,9},{9,8},{10,11... | collective-permute-start | bytes 983048 | tf_op jit(solution)/shard_map/ppermute | solution.py:84
  83.0 10.5 %collective-permute-start.16 = (bf16[256,640]{1,0:T(8,128)(2,1)S(1)}, bf16[256,640]{1,0:T(8,128)(2,1)S(1)}, u32[]{:S(2)}, u32[]{:S(2)}) collective-permute-start(bf16[256,640]{1,0:T(8,128)(2,1)S(1)} %collective-permute-done.12.refs_1_), channel_id=1, source_target_pairs={{0,2},{1,3},{2,0},{3,1},{4,5},{5,4},{6,7},{7,6},{8,10},{9,11},{10,... | collective-permute-start | bytes 983048 | tf_op jit(solution)/shard_map/ppermute | solution.py:84
  84.9 10.7 %collective-permute-start.22 = (bf16[240,1280]{1,0:T(8,128)(2,1)S(1)}, bf16[240,1280]{1,0:T(8,128)(2,1)S(1)}, u32[]{:S(2)}, u32[]{:S(2)}) collective-permute-start(bf16[240,1280]{1,0:T(8,128)(2,1)S(1)} %collective-permute-done.14.refs_18_), channel_id=1, source_target_pairs={{0,4},{1,5},{2,6},{3,7},{4,0},{5,1},{6,2},{7,3},{8,12},{9,13},{10,... | collective-permute-start | bytes 1843208 | tf_op jit(solution)/shard_map/ppermute | solution.py:84
  97.7 14.0 %collective-permute-start.28 = (bf16[240,1280]{1,0:T(8,128)(2,1)}, bf16[240,1280]{1,0:T(8,128)(2,1)S(1)}, u32[]{:S(2)}, u32[]{:S(2)}) collective-permute-start(bf16[240,1280]{1,0:T(8,128)(2,1)} %collective-permute-done.19.refs_19_), channel_id=1, source_target_pairs={{0,4},{1,5},{2,6},{3,7},{4,0},{5,1},{6,2},{7,3},{8,12},{9,13},{10,... | collective-permute-start | bytes 1843208 | tf_op jit(solution)/shard_map/ppermute | solution.py:84
  97.9 12.2 %collective-permute-start.26 = (bf16[160,960]{1,0:T(8,128)(2,1)}, bf16[160,960]{1,0:T(8,128)(2,1)S(1)}, u32[]{:S(2)}, u32[]{:S(2)}) collective-permute-start(bf16[160,960]{1,0:T(8,128)(2,1)} %constant_dynamic-slice_fusion), channel_id=1, source_target_pairs={{0,1},{1,0},{2,3},{3,2},{4,6},{5,7},{6,4},{7,5},{8,9},{9,8},{10,11... | collective-permute-start | bytes 921608 | tf_op jit(solution)/shard_map/ppermute | solution.py:84
  98.7 11.4 %collective-permute-start.27 = (bf16[160,960]{1,0:T(8,128)(2,1)}, bf16[160,960]{1,0:T(8,128)(2,1)S(1)}, u32[]{:S(2)}, u32[]{:S(2)}) collective-permute-start(bf16[160,960]{1,0:T(8,128)(2,1)} %constant_dynamic-slice_fusion), channel_id=1, source_target_pairs={{0,2},{1,3},{2,0},{3,1},{4,5},{5,4},{6,7},{7,6},{8,10},{9,11},{10,... | collective-permute-start | bytes 921608 | tf_op jit(solution)/shard_map/ppermute | solution.py:84
  100.3 11.4 %collective-permute-start.25 = (bf16[256,640]{1,0:T(8,128)(2,1)S(1)}, bf16[256,640]{1,0:T(8,128)(2,1)S(1)}, u32[]{:S(2)}, u32[]{:S(2)}) collective-permute-start(bf16[256,640]{1,0:T(8,128)(2,1)S(1)} %collective-permute-done.17.refs_1_), channel_id=1, source_target_pairs={{0,2},{1,3},{2,0},{3,1},{4,5},{5,4},{6,7},{7,6},{8,10},{9,11},{10,... | collective-permute-start | bytes 983048 | tf_op jit(solution)/shard_map/ppermute | solution.py:84
  111.7 13.0 %collective-permute-start.29 = (bf16[160,960]{1,0:T(8,128)(2,1)S(1)}, bf16[160,960]{1,0:T(8,128)(2,1)S(1)}, u32[]{:S(2)}, u32[]{:S(2)}) collective-permute-start(bf16[160,960]{1,0:T(8,128)(2,1)S(1)} %collective-permute-done.26.refs_23_), channel_id=1, source_target_pairs={{0,2},{1,3},{2,0},{3,1},{4,5},{5,4},{6,7},{7,6},{8,10},{9,11},{10,... | collective-permute-start | bytes 921608 | tf_op jit(solution)/shard_map/ppermute | solution.py:84
  113.6 11.1 %collective-permute-start.30 = (bf16[160,960]{1,0:T(8,128)(2,1)S(1)}, bf16[160,960]{1,0:T(8,128)(2,1)}, u32[]{:S(2)}, u32[]{:S(2)}) collective-permute-start(bf16[160,960]{1,0:T(8,128)(2,1)S(1)} %collective-permute-done.26.refs_23_), channel_id=1, source_target_pairs={{0,8},{1,9},{2,10},{3,11},{4,12},{5,13},{6,14},{7,15},{8,0},{9,1},... | collective-permute-start | bytes 921608 | tf_op jit(solution)/shard_map/ppermute | solution.py:84
  114.1 15.5 %collective-permute-start.32 = (bf16[160,960]{1,0:T(8,128)(2,1)S(1)}, bf16[160,960]{1,0:T(8,128)(2,1)S(1)}, u32[]{:S(2)}, u32[]{:S(2)}) collective-permute-start(bf16[160,960]{1,0:T(8,128)(2,1)S(1)} %collective-permute-done.26.refs_23_), channel_id=1, source_target_pairs={{0,4},{1,5},{2,6},{3,7},{4,0},{5,1},{6,2},{7,3},{8,12},{9,13},{10,... | collective-permute-start | bytes 921608 | tf_op jit(solution)/shard_map/ppermute | solution.py:84
  114.1 15.5 %collective-permute-start.31 = (bf16[160,960]{1,0:T(8,128)(2,1)S(1)}, bf16[160,960]{1,0:T(8,128)(2,1)}, u32[]{:S(2)}, u32[]{:S(2)}) collective-permute-start(bf16[160,960]{1,0:T(8,128)(2,1)S(1)} %collective-permute-done.27.refs_27_), channel_id=1, source_target_pairs={{0,8},{1,9},{2,10},{3,11},{4,12},{5,13},{6,14},{7,15},{8,0},{9,1},... | collective-permute-start | bytes 921608 | tf_op jit(solution)/shard_map/ppermute | solution.py:84
  115.7 13.9 %collective-permute-start.33 = (bf16[160,960]{1,0:T(8,128)(2,1)S(1)}, bf16[160,960]{1,0:T(8,128)(2,1)S(1)}, u32[]{:S(2)}, u32[]{:S(2)}) collective-permute-start(bf16[160,960]{1,0:T(8,128)(2,1)S(1)} %collective-permute-done.27.refs_27_), channel_id=1, source_target_pairs={{0,4},{1,5},{2,6},{3,7},{4,0},{5,1},{6,2},{7,3},{8,12},{9,13},{10,... | collective-permute-start | bytes 921608 | tf_op jit(solution)/shard_map/ppermute | solution.py:84
  130.6 10.1 %collective-permute-start.37 = (bf16[160,960]{1,0:T(8,128)(2,1)S(1)}, bf16[160,960]{1,0:T(8,128)(2,1)S(1)}, u32[]{:S(2)}, u32[]{:S(2)}) collective-permute-start(bf16[160,960]{1,0:T(8,128)(2,1)S(1)} %collective-permute-done.29.refs_31_), channel_id=1, source_target_pairs={{0,4},{1,5},{2,6},{3,7},{4,0},{5,1},{6,2},{7,3},{8,12},{9,13},{10,... | collective-permute-start | bytes 921608 | tf_op jit(solution)/shard_map/ppermute | solution.py:84
  130.6 10.1 %collective-permute-start.34 = (bf16[160,960]{1,0:T(8,128)(2,1)}, bf16[160,960]{1,0:T(8,128)(2,1)}, u32[]{:S(2)}, u32[]{:S(2)}) collective-permute-start(bf16[160,960]{1,0:T(8,128)(2,1)} %collective-permute-done.30.refs_24_), channel_id=1, source_target_pairs={{0,4},{1,5},{2,6},{3,7},{4,0},{5,1},{6,2},{7,3},{8,12},{9,13},{10,... | collective-permute-start | bytes 921608 | tf_op jit(solution)/shard_map/ppermute | solution.py:84
  131.1 9.6 %collective-permute-start.35 = (bf16[160,960]{1,0:T(8,128)(2,1)}, bf16[160,960]{1,0:T(8,128)(2,1)}, u32[]{:S(2)}, u32[]{:S(2)}) collective-permute-start(bf16[160,960]{1,0:T(8,128)(2,1)} %collective-permute-done.31.refs_28_), channel_id=1, source_target_pairs={{0,4},{1,5},{2,6},{3,7},{4,0},{5,1},{6,2},{7,3},{8,12},{9,13},{10,... | collective-permute-start | bytes 921608 | tf_op jit(solution)/shard_map/ppermute | solution.py:84
  188.1 31.0 %collective-permute-start.39 = (bf16[1792,960]{0,1:T(8,128)(2,1)}, bf16[1792,960]{0,1:T(8,128)(2,1)}, u32[]{:S(2)}, u32[]{:S(2)}) collective-permute-start(bf16[1792,960]{0,1:T(8,128)(2,1)} %copy.114), channel_id=1, source_target_pairs={{0,4},{1,5},{2,6},{3,7},{4,0},{5,1},{6,2},{7,3},{8,12},{9,13},{10,... | collective-permute-start | bytes 10321928 | tf_op jit(solution)/shard_map/ppermute | solution.py:84
  201.1 18.0 %collective-permute-start.41 = (bf16[960,1280]{1,0:T(8,128)(2,1)}, bf16[960,1280]{1,0:T(8,128)(2,1)}, u32[]{:S(2)}, u32[]{:S(2)}) collective-permute-start(bf16[960,1280]{1,0:T(8,128)(2,1)} %weight_grad.13), channel_id=1, source_target_pairs={{0,4},{1,5},{2,6},{3,7},{4,0},{5,1},{6,2},{7,3},{8,12},{9,13},{10,... | collective-permute-start | bytes 7372808 | tf_op jit(solution)/shard_map/ppermute | solution.py:84
  201.2 17.9 %collective-permute-start.40 = (bf16[960,1280]{1,0:T(8,128)(2,1)}, bf16[960,1280]{1,0:T(8,128)(2,1)}, u32[]{:S(2)}, u32[]{:S(2)}) collective-permute-start(bf16[960,1280]{1,0:T(8,128)(2,1)} %weight_grad.12), channel_id=1, source_target_pairs={{0,4},{1,5},{2,6},{3,7},{4,0},{5,1},{6,2},{7,3},{8,12},{9,13},{10,... | collective-permute-start | bytes 7372808 | tf_op jit(solution)/shard_map/ppermute | solution.py:84
  227.0 13.7 %collective-permute-start.42 = (bf16[448,960]{1,0:T(8,128)(2,1)S(1)}, bf16[448,960]{1,0:T(8,128)(2,1)S(1)}, u32[]{:S(2)}, u32[]{:S(2)}) collective-permute-start(bf16[448,960]{1,0:T(8,128)(2,1)S(1)} %add_convert_fusion.8), channel_id=1, source_target_pairs={{0,2},{1,3},{2,0},{3,1},{4,5},{5,4},{6,7},{7,6},{8,10},{9,11},{10,... | collective-permute-start | bytes 2580488 | tf_op jit(solution)/shard_map/ppermute | solution.py:84
  243.8 13.5 %collective-permute-start.44 = (bf16[448,960]{1,0:T(8,128)(2,1)S(1)}, bf16[448,960]{1,0:T(8,128)(2,1)S(1)}, u32[]{:S(2)}, u32[]{:S(2)}) collective-permute-start(bf16[448,960]{1,0:T(8,128)(2,1)S(1)} %get-tuple-element.345), channel_id=1, source_target_pairs={{0,2},{1,3},{2,0},{3,1},{4,5},{5,4},{6,7},{7,6},{8,10},{9,11},{10,... | collective-permute-start | bytes 2580488 | tf_op jit(solution)/shard_map/ppermute | solution.py:84
  257.2 19.9 %collective-permute-start.45 = (bf16[448,960]{1,0:T(8,128)(2,1)S(1)}, bf16[448,960]{1,0:T(8,128)(2,1)S(1)}, u32[]{:S(2)}, u32[]{:S(2)}) collective-permute-start(bf16[448,960]{1,0:T(8,128)(2,1)S(1)} %get-tuple-element.244), channel_id=1, source_target_pairs={{0,1},{1,0},{2,3},{3,2},{4,6},{5,7},{6,4},{7,5},{8,9},{9,8},{10,11... | collective-permute-start | bytes 2580488 | tf_op jit(solution)/shard_map/ppermute | solution.py:84
  295.6 11.7 %collective-permute-start.48 = (bf16[240,1280]{1,0:T(8,128)(2,1)}, bf16[240,1280]{1,0:T(8,128)(2,1)}, u32[]{:S(2)}, u32[]{:S(2)}) collective-permute-start(bf16[240,1280]{1,0:T(8,128)(2,1)} %add_convert_fusion.26), channel_id=1, source_target_pairs={{0,2},{1,3},{2,0},{3,1},{4,5},{5,4},{6,7},{7,6},{8,10},{9,11},{10,... | collective-permute-start | bytes 1843208 | tf_op jit(solution)/shard_map/ppermute | solution.py:84
  302.6 42.5 %collective-permute-start.61 = (bf16[448,960]{1,0:T(8,128)(2,1)}, bf16[448,960]{1,0:T(8,128)(2,1)}, u32[]{:S(2)}, u32[]{:S(2)}) collective-permute-start(bf16[448,960]{1,0:T(8,128)(2,1)} %add_convert_fusion.2), channel_id=1, source_target_pairs={{0,8},{1,9},{2,10},{3,11},{4,12},{5,13},{6,14},{7,15},{24,16},{25,... | collective-permute-start | bytes 2580488 | tf_op jit(solution)/shard_map/ppermute | solution.py:84
  310.2 32.4 %collective-permute-start.50 = (bf16[240,1280]{1,0:T(8,128)(2,1)}, bf16[240,1280]{1,0:T(8,128)(2,1)}, u32[]{:S(2)}, u32[]{:S(2)}) collective-permute-start(bf16[240,1280]{1,0:T(8,128)(2,1)} %get-tuple-element.255), channel_id=1, source_target_pairs={{0,2},{1,3},{2,0},{3,1},{4,5},{5,4},{6,7},{7,6},{8,10},{9,11},{10,... | collective-permute-start | bytes 1843208 | tf_op jit(solution)/shard_map/ppermute | solution.py:84
  336.8 16.2 %collective-permute-start.54 = (bf16[512,960]{0,1:T(8,128)(2,1)}, bf16[512,960]{0,1:T(8,128)(2,1)}, u32[]{:S(2)}, u32[]{:S(2)}) collective-permute-start(bf16[512,960]{0,1:T(8,128)(2,1)} %copy.120), channel_id=1, source_target_pairs={{0,4},{1,5},{2,6},{3,7},{4,0},{5,1},{6,2},{7,3},{8,12},{9,13},{10,... | collective-permute-start | bytes 2949128 | tf_op jit(solution)/shard_map/ppermute | solution.py:84
  342.7 10.3 %collective-permute-start.51 = (bf16[240,1280]{1,0:T(8,128)(2,1)S(1)}, bf16[240,1280]{1,0:T(8,128)(2,1)}, u32[]{:S(2)}, u32[]{:S(2)}) collective-permute-start(bf16[240,1280]{1,0:T(8,128)(2,1)S(1)} %copy-done.86), channel_id=1, source_target_pairs={{0,1},{1,0},{2,3},{3,2},{4,6},{5,7},{6,4},{7,5},{8,9},{9,8},{10,11... | collective-permute-start | bytes 1843208 | tf_op jit(solution)/shard_map/ppermute | solution.py:84
  347.8 21.4 %collective-permute-start.65 = (bf16[448,960]{1,0:T(8,128)(2,1)}, bf16[448,960]{1,0:T(8,128)(2,1)}, u32[]{:S(2)}, u32[]{:S(2)}) collective-permute-start(bf16[448,960]{1,0:T(8,128)(2,1)} %add_convert_fusion.1), channel_id=1, source_target_pairs={{8,16},{9,17},{10,18},{11,19},{12,20},{13,21},{14,22},{15,23},{16,... | collective-permute-start | bytes 2580488 | tf_op jit(solution)/shard_map/ppermute | solution.py:84
  353.0 13.6 %collective-permute-start.52 = (bf16[256,640]{1,0:T(8,128)(2,1)}, bf16[256,640]{1,0:T(8,128)(2,1)}, u32[]{:S(2)}, u32[]{:S(2)}) collective-permute-start(bf16[256,640]{1,0:T(8,128)(2,1)} %get-tuple-element.257), channel_id=1, source_target_pairs={{0,2},{1,3},{2,0},{3,1},{4,5},{5,4},{6,7},{7,6},{8,10},{9,11},{10,... | collective-permute-start | bytes 983048 | tf_op jit(solution)/shard_map/ppermute | solution.py:84
  371.3 26.9 %collective-permute-start.69 = (bf16[448,960]{1,0:T(8,128)(2,1)S(1)}, bf16[448,960]{1,0:T(8,128)(2,1)S(1)}, u32[]{:S(2)}, u32[]{:S(2)}) collective-permute-start(bf16[448,960]{1,0:T(8,128)(2,1)S(1)} %add_convert_fusion), channel_id=1, source_target_pairs={{8,0},{9,1},{10,2},{11,3},{12,4},{13,5},{14,6},{15,7},{16,24},{17,... | collective-permute-start | bytes 2580488 | tf_op jit(solution)/shard_map/ppermute | solution.py:84
  387.0 18.5 %collective-permute-start.62 = (bf16[240,1280]{1,0:T(8,128)(2,1)S(1)}, bf16[240,1280]{1,0:T(8,128)(2,1)S(1)}, u32[]{:S(2)}, u32[]{:S(2)}) collective-permute-start(bf16[240,1280]{1,0:T(8,128)(2,1)S(1)} %add_convert_fusion.13), channel_id=1, source_target_pairs={{0,8},{1,9},{2,10},{3,11},{4,12},{5,13},{6,14},{7,15},{24,16},{25,... | collective-permute-start | bytes 1843208 | tf_op jit(solution)/shard_map/ppermute | solution.py:84
  399.2 31.2 %collective-permute-start.82 = (bf16[448,960]{1,0:T(8,128)(2,1)}, bf16[448,960]{1,0:T(8,128)(2,1)}, u32[]{:S(2)}, u32[]{:S(2)}) collective-permute-start(bf16[448,960]{1,0:T(8,128)(2,1)} %broadcast_select_fusion), channel_id=1, source_target_pairs={{0,4},{1,5},{2,6},{3,7},{4,0},{5,1},{6,2},{7,3},{8,12},{9,13},{10,... | collective-permute-start | bytes 2580488 | tf_op jit(solution)/shard_map/ppermute | solution.py:84
  399.2 24.3 %collective-permute-start.55 = (bf16[240,1280]{1,0:T(8,128)(2,1)}, bf16[240,1280]{1,0:T(8,128)(2,1)}, u32[]{:S(2)}, u32[]{:S(2)}) collective-permute-start(bf16[240,1280]{1,0:T(8,128)(2,1)} %add_convert_fusion.22), channel_id=1, source_target_pairs={{0,2},{1,3},{2,0},{3,1},{4,5},{5,4},{6,7},{7,6},{8,10},{9,11},{10,... | collective-permute-start | bytes 1843208 | tf_op jit(solution)/shard_map/ppermute | solution.py:84
  400.1 9.5 %collective-permute-start.87 = (f32[2,960]{1,0:T(2,128)S(1)}, f32[2,960]{1,0:T(2,128)S(1)}, u32[]{:S(2)}, u32[]{:S(2)}) collective-permute-start(f32[2,960]{1,0:T(2,128)S(1)} %fusion.12), channel_id=1, source_target_pairs={{0,2},{1,3},{2,0},{3,1},{4,5},{5,4},{6,7},{7,6},{8,10},{9,11},{10,... | collective-permute-start | bytes 23048 | tf_op jit(solution)/shard_map/ppermute | solution.py:84
  406.5 53.9 %collective-permute-start.66 = (bf16[240,1280]{1,0:T(8,128)(2,1)}, bf16[240,1280]{1,0:T(8,128)(2,1)}, u32[]{:S(2)}, u32[]{:S(2)}) collective-permute-start(bf16[240,1280]{1,0:T(8,128)(2,1)} %add_convert_fusion.11), channel_id=1, source_target_pairs={{8,16},{9,17},{10,18},{11,19},{12,20},{13,21},{14,22},{15,23},{16,... | collective-permute-start | bytes 1843208 | tf_op jit(solution)/shard_map/ppermute | solution.py:84
  419.9 43.2 %collective-permute-start.74 = (bf16[512,640]{1,0:T(8,128)(2,1)}, bf16[512,640]{1,0:T(8,128)(2,1)S(1)}, u32[]{:S(2)}, u32[]{:S(2)}) collective-permute-start(bf16[512,640]{1,0:T(8,128)(2,1)} %weight_grad.19), channel_id=1, source_target_pairs={{0,4},{1,5},{2,6},{3,7},{4,0},{5,1},{6,2},{7,3},{8,12},{9,13},{10,... | collective-permute-start | bytes 1966088 | tf_op jit(solution)/shard_map/ppermute | solution.py:84
  425.3 10.2 %collective-permute-start.57 = (bf16[240,1280]{1,0:T(8,128)(2,1)S(1)}, bf16[240,1280]{1,0:T(8,128)(2,1)S(1)}, u32[]{:S(2)}, u32[]{:S(2)}) collective-permute-start(bf16[240,1280]{1,0:T(8,128)(2,1)S(1)} %get-tuple-element.266), channel_id=1, source_target_pairs={{0,2},{1,3},{2,0},{3,1},{4,5},{5,4},{6,7},{7,6},{8,10},{9,11},{10,... | collective-permute-start | bytes 1843208 | tf_op jit(solution)/shard_map/ppermute | solution.py:84
  435.5 13.0 %collective-permute-start.58 = (bf16[240,1280]{1,0:T(8,128)(2,1)S(1)}, bf16[240,1280]{1,0:T(8,128)(2,1)S(1)}, u32[]{:S(2)}, u32[]{:S(2)}) collective-permute-start(bf16[240,1280]{1,0:T(8,128)(2,1)S(1)} %get-tuple-element.267), channel_id=1, source_target_pairs={{0,1},{1,0},{2,3},{3,2},{4,6},{5,7},{6,4},{7,5},{8,9},{9,8},{10,11... | collective-permute-start | bytes 1843208 | tf_op jit(solution)/shard_map/ppermute | solution.py:84
  438.5 20.5 %collective-permute-start.56 = (bf16[128,960]{1,0:T(8,128)(2,1)S(1)}, bf16[128,960]{1,0:T(8,128)(2,1)S(1)}, u32[]{:S(2)}, u32[]{:S(2)}) collective-permute-start(bf16[128,960]{1,0:T(8,128)(2,1)S(1)} %copy-done.89), channel_id=1, source_target_pairs={{0,2},{1,3},{2,0},{3,1},{4,5},{5,4},{6,7},{7,6},{8,10},{9,11},{10,... | collective-permute-start | bytes 737288 | tf_op jit(solution)/shard_map/ppermute | solution.py:84
  448.5 10.3 %collective-permute-start.59 = (bf16[128,960]{1,0:T(8,128)(2,1)S(1)}, bf16[128,960]{1,0:T(8,128)(2,1)S(1)}, u32[]{:S(2)}, u32[]{:S(2)}) collective-permute-start(bf16[128,960]{1,0:T(8,128)(2,1)S(1)} %copy-done.90), channel_id=1, source_target_pairs={{0,2},{1,3},{2,0},{3,1},{4,5},{5,4},{6,7},{7,6},{8,10},{9,11},{10,... | collective-permute-start | bytes 737288 | tf_op jit(solution)/shard_map/ppermute | solution.py:84
  449.9 17.7 %collective-permute-start.63 = (bf16[240,1280]{1,0:T(8,128)(2,1)S(1)}, bf16[240,1280]{1,0:T(8,128)(2,1)S(1)}, u32[]{:S(2)}, u32[]{:S(2)}) collective-permute-start(bf16[240,1280]{1,0:T(8,128)(2,1)S(1)} %add_convert_fusion.16), channel_id=1, source_target_pairs={{0,8},{1,9},{2,10},{3,11},{4,12},{5,13},{6,14},{7,15},{24,16},{25,... | collective-permute-start | bytes 1843208 | tf_op jit(solution)/shard_map/ppermute | solution.py:84
  461.8 16.3 %collective-permute-start.70 = (bf16[240,1280]{1,0:T(8,128)(2,1)S(1)}, bf16[240,1280]{1,0:T(8,128)(2,1)S(1)}, u32[]{:S(2)}, u32[]{:S(2)}) collective-permute-start(bf16[240,1280]{1,0:T(8,128)(2,1)S(1)} %add_convert_fusion.9), channel_id=1, source_target_pairs={{8,0},{9,1},{10,2},{11,3},{12,4},{13,5},{14,6},{15,7},{16,24},{17,... | collective-permute-start | bytes 1843208 | tf_op jit(solution)/shard_map/ppermute | solution.py:84
  463.2 14.5 %collective-permute-start.75 = (bf16[128,640]{1,0:T(8,128)(2,1)S(1)}, bf16[128,640]{1,0:T(8,128)(2,1)S(1)}, u32[]{:S(2)}, u32[]{:S(2)}) collective-permute-start(bf16[128,640]{1,0:T(8,128)(2,1)S(1)} %get-tuple-element.279), channel_id=1, source_target_pairs={{0,2},{1,3},{2,0},{3,1},{4,5},{5,4},{6,7},{7,6},{8,10},{9,11},{10,... | collective-permute-start | bytes 491528 | tf_op jit(solution)/shard_map/ppermute | solution.py:84
  465.4 12.2 %collective-permute-start.76 = (bf16[128,640]{1,0:T(8,128)(2,1)S(1)}, bf16[128,640]{1,0:T(8,128)(2,1)S(1)}, u32[]{:S(2)}, u32[]{:S(2)}) collective-permute-start(bf16[128,640]{1,0:T(8,128)(2,1)S(1)} %get-tuple-element.280), channel_id=1, source_target_pairs={{0,2},{1,3},{2,0},{3,1},{4,5},{5,4},{6,7},{7,6},{8,10},{9,11},{10,... | collective-permute-start | bytes 491528 | tf_op jit(solution)/shard_map/ppermute | solution.py:84
  467.8 18.8 %collective-permute-start.67 = (bf16[240,1280]{1,0:T(8,128)(2,1)S(1)}, bf16[240,1280]{1,0:T(8,128)(2,1)S(1)}, u32[]{:S(2)}, u32[]{:S(2)}) collective-permute-start(bf16[240,1280]{1,0:T(8,128)(2,1)S(1)} %add_convert_fusion.12), channel_id=1, source_target_pairs={{8,16},{9,17},{10,18},{11,19},{12,20},{13,21},{14,22},{15,23},{16,... | collective-permute-start | bytes 1843208 | tf_op jit(solution)/shard_map/ppermute | solution.py:84
  468.5 15.4 %collective-permute-start.64 = (bf16[128,960]{1,0:T(8,128)(2,1)S(1)}, bf16[128,960]{1,0:T(8,128)(2,1)S(1)}, u32[]{:S(2)}, u32[]{:S(2)}) collective-permute-start(bf16[128,960]{1,0:T(8,128)(2,1)S(1)} %add_convert_fusion.35), channel_id=1, source_target_pairs={{0,8},{1,9},{2,10},{3,11},{4,12},{5,13},{6,14},{7,15},{24,16},{25,... | collective-permute-start | bytes 737288 | tf_op jit(solution)/shard_map/ppermute | solution.py:84
  479.0 23.3 %collective-permute-start.83 = (bf16[240,1280]{1,0:T(8,128)(2,1)}, bf16[240,1280]{1,0:T(8,128)(2,1)}, u32[]{:S(2)}, u32[]{:S(2)}) collective-permute-start(bf16[240,1280]{1,0:T(8,128)(2,1)} %broadcast_select_fusion.4), channel_id=1, source_target_pairs={{0,4},{1,5},{2,6},{3,7},{4,0},{5,1},{6,2},{7,3},{8,12},{9,13},{10,... | collective-permute-start | bytes 1843208 | tf_op jit(solution)/shard_map/ppermute | solution.py:84
  486.8 14.2 %collective-permute-start.71 = (bf16[240,1280]{1,0:T(8,128)(2,1)S(1)}, bf16[240,1280]{1,0:T(8,128)(2,1)}, u32[]{:S(2)}, u32[]{:S(2)}) collective-permute-start(bf16[240,1280]{1,0:T(8,128)(2,1)S(1)} %add_convert_fusion.10), channel_id=1, source_target_pairs={{8,0},{9,1},{10,2},{11,3},{12,4},{13,5},{14,6},{15,7},{16,24},{17,... | collective-permute-start | bytes 1843208 | tf_op jit(solution)/shard_map/ppermute | solution.py:84
  493.7 9.9 %collective-permute-start.79 = (bf16[128,640]{1,0:T(8,128)(2,1)S(1)}, bf16[128,640]{1,0:T(8,128)(2,1)S(1)}, u32[]{:S(2)}, u32[]{:S(2)}) collective-permute-start(bf16[128,640]{1,0:T(8,128)(2,1)S(1)} %add_convert_fusion.43), channel_id=1, source_target_pairs={{8,16},{9,17},{10,18},{11,19},{12,20},{13,21},{14,22},{15,23},{16,... | collective-permute-start | bytes 491528 | tf_op jit(solution)/shard_map/ppermute | solution.py:84
  (136 other events, 1493.9 us)

commit v5 on v4

v5 whole, which is shorter than its diff:
```python
import functools
import math

import jax
import jax.numpy as jnp
from jax import lax
from jax.experimental import pallas as pl
from jax.experimental.pallas import tpu as pltpu
from jax.sharding import PartitionSpec as P

QUERY_HEADS = 15
KEY_VALUE_HEADS = 5
HEAD_SIZE = 64
HALF_HEAD = HEAD_SIZE // 2
GROUP = QUERY_HEADS // KEY_VALUE_HEADS
KV_WIDTH = KEY_VALUE_HEADS * HEAD_SIZE
SCALE = HEAD_SIZE ** (-0.5)
EPS = 1e-05
AXES = ("rep", "shard")
BF = jnp.bfloat16
F32 = jnp.float32
CLOSED = -1e30
VMEM_LIMIT = 48 << 20
VMEM_MOST = 60 << 20


def dot(a, b, dims):
    return lax.dot_general(a, b, (dims, ((), ())), preferred_element_type=F32)


def nn(a, b):
    return dot(a, b, ((1,), (0,)))


def nt(a, b):
    return dot(a, b, ((1,), (1,)))


def tn(a, b):
    return dot(a, b, ((0,), (0,)))


def total(parts):
    return sum(part.astype(F32) for part in parts).astype(parts[0].dtype)


def meet(*values):
    return lax.optimization_barrier(values)


def rounded_up(columns):
    return -(-columns // 128) * 128


def rms_inverse(x):
    return lax.rsqrt(jnp.mean(x * x, axis=-1, keepdims=True) + EPS)


def cost(flops, exps, *arrays):
    size = sum(a.size * a.dtype.itemsize for a in arrays)
    return pl.CostEstimate(flops=flops, transcendentals=exps, bytes_accessed=size)


class Links:
    def __init__(self, reps, shards):
        self.reps, self.shards = reps, shards
        self.core = lax.axis_index("rep") % 2
        self.shard = lax.axis_index("shard")
        self.bits = shards.bit_length() - 1
        even = [1 << i for i in range(self.bits)]
        odd = even[:2][::-1] + even[2:]
        self.steps = list(zip(even, odd))
        self.hops = []
        for piece in range(shards):
            sums = [0, 0]
            for i, step in enumerate(self.steps):
                if piece >> i & 1:
                    sums = [sums[0] ^ step[0], sums[1] ^ step[1]]
            self.hops.append(jnp.where(self.core == 0, sums[0], sums[1]))

    def move(self, value, target):
        pairs = []
        for r in range(self.reps):
            for s in range(self.shards):
                goal = target(r, s)
                if goal is not None:
                    pairs.append((r * self.shards + s, goal[0] * self.shards + goal[1]))
        return lax.ppermute(value, AXES, pairs)

    def step(self, value, i):
        return self.move(value, lambda r, s: (r, s ^ self.steps[i][r % 2]))

    def swap(self, value):
        return self.move(value, lambda r, s: (r ^ 1, s))

    def reduce(self, plan, name):
        got = yield self.swap(plan.have[name + ".given"])
        sums = [plan.have.pop(name + ".kept"), got]
        del plan.have[name + ".given"]
        for i in reversed(range(self.bits)):
            block = sums[0].shape[0] // 2
            got = yield self.step(total([part[block:] for part in sums]), i)
            sums = [part[:block] for part in sums] + [got]
        value = total(sums)
        chips = self.reps // 2
        place = lax.axis_index("rep") // 2
        span = 1
        if chips % 4 == 0:
            inward, outward, middle = {0: 1, 3: 2}, {1: 0, 2: 3}, {1: 2, 2: 1}

            def along(value, table):
                def target(r, s):
                    chip = r // 2
                    if chip % 4 not in table:
                        return None
                    return ((chip - chip % 4 + table[chip % 4]) * 2 + r % 2, s)

                return self.move(value, target)

            value = total([value, (yield along(value, inward))])
            value = total([value, (yield along(value, middle))])
            back = yield along(value, outward)
            inner = (place % 4 == 1) | (place % 4 == 2)
            value = jnp.where(inner, value, back)
            span = 4
        while span < chips:
            value = total([value, self.move(value, lambda r, s: (r ^ (2 * span), s))])
            span *= 2
        other = yield self.swap(value)
        plan.have[name] = (value, other)

    def collect(self, plan, name):
        pieces = plan.have[name + ".pieces"]
        for i in reversed(range(self.bits)):
            keep = 1 << i
            got = yield [self.step(pieces[t + keep], i) for t in range(keep)]
            pieces = [total([pieces[t], got[t]]) for t in range(keep)]
        plan.have[name] = pieces[0]

    def beside(self, value):
        return self.move(value, lambda r, s: (r ^ 2, s))

    def near(self, value):
        return {1 << i: self.step(value, i) for i in range(self.bits)}

    def far(self, value, near):
        pieces = [value]
        for t in range(1, self.shards):
            top = t.bit_length() - 1
            pieces.append(near[t] if t in near else self.step(pieces[t - (1 << top)], top))
        return pieces

    def twin(self, piece):
        return piece if self.bits < 2 else piece >> 2 << 2 | (piece & 1) << 1 | (piece >> 1 & 1)

    def small_pieces(self, value):
        return [
            value if hop == 0 else self.move(value, lambda r, s, hop=hop: (r, s ^ hop))
            for hop in range(self.shards)
        ]

    def in_order(self, pieces):
        pieces = jnp.stack(pieces)
        value = pieces
        order = self.shard ^ jnp.arange(self.shards)
        hit = (order[:, None] == jnp.arange(self.shards)[None, :])[:, :, None, None]
        pieces = jnp.sum(jnp.where(hit, pieces[None], 0), axis=1, dtype=value.dtype)
        return jnp.concatenate([pieces[j] for j in range(self.shards)], axis=-1)

    def half_rows(self, rows):
        half = -(-rows // 32) * 16
        return half, self.core * (rows - half), (1 - self.core) * (rows - half)

    def order(self, scale, mine, theirs):
        kept = [(self.shard ^ hop) * scale + mine for hop in self.hops]
        given = [(self.shard ^ self.hops[self.twin(t)]) * scale + theirs for t in range(self.shards)]
        return kept, given

    def finish_rows(self, owned, other, rows):
        low = jnp.where(self.core == 0, owned, other)
        high = jnp.where(self.core == 0, other, owned)
        return jnp.concatenate([low[: rows - owned.shape[0]], high], axis=0).astype(F32)

    def finish_pair(self, owned, other):
        left = jnp.where(self.core == 0, owned, other)
        right = jnp.where(self.core == 0, other, owned)
        return left.astype(F32), right.astype(F32)


class Plan:
    def __init__(self):
        self.have, self.tasks, self.made = {}, {}, {}

    def start(self, name, task):
        self.tasks[name] = task
        self.made[name] = None

    def advance(self, *names):
        for name in names:
            if name in self.tasks:
                try:
                    self.made[name] = self.tasks[name].send(self.made[name])
                except StopIteration:
                    del self.tasks[name], self.made[name]

    def close(self):
        self.have, self.made = lax.optimization_barrier((self.have, self.made))


def joined(pieces, starts, shape):
    if any(piece.shape[0] % 16 or piece.shape[1] % 128 and piece.shape[1] < shape[1] for piece in pieces):
        whole = jnp.zeros(shape, pieces[0].dtype)
        for piece, start in zip(pieces, starts):
            whole = lax.dynamic_update_slice(whole, piece, start)
        pieces, starts = (whole,), [(0, 0)]
    return tuple(pieces), numbers([at for start in starts for at in start]), shape


def numbers(values):
    return jnp.stack([jnp.asarray(value, jnp.int32) for value in values])


def load(pieces, starts_ref, whole, sems):
    copies = []
    for i, piece in enumerate(pieces):
        rows = pl.ds(pl.multiple_of(starts_ref[2 * i], 16), piece.shape[0])
        if piece.shape[1] == whole.shape[1]:
            place = whole.at[rows, :]
        else:
            columns = pl.ds(pl.multiple_of(starts_ref[2 * i + 1], 128), piece.shape[1])
            place = whole.at[rows, columns]
        copies.append(pltpu.make_async_copy(piece, place, sems.at[i]))
        copies[-1].start()
    return copies


def wait(copies):
    for copy in copies:
        copy.wait()


IN_VMEM = pl.BlockSpec(memory_space=pltpu.VMEM)
IN_SMEM = pl.BlockSpec(memory_space=pltpu.SMEM)
ANYWHERE = pl.BlockSpec(memory_space=pl.ANY)


def upright(ref):
    return jnp.concatenate([jnp.transpose(ref[m]) for m in range(ref.shape[0])], axis=0)


def lay_down(value, ref):
    rows = ref.shape[2]
    for m in range(ref.shape[0]):
        ref[m] = jnp.transpose(value[m * rows : (m + 1) * rows])


def turn(chunk, cosine, sine):
    lane = lax.broadcasted_iota(jnp.int32, chunk.shape, 1)
    partner = jnp.where(
        lane % HEAD_SIZE < HALF_HEAD,
        pltpu.roll(chunk, 128 - HALF_HEAD, 1),
        pltpu.roll(chunk, HALF_HEAD, 1),
    )
    return chunk * cosine + partner * sine


def project_kernel(count, starts_ref, x_ref, gains_ref, cos_ref, sin_ref, *refs):
    pieces = refs[:count]
    q_ref, kv_ref, whole, sems = refs[count:]
    copies = load(pieces, starts_ref, whole, sems)
    x = upright(x_ref).astype(F32)
    width = x.shape[1]
    act = (x * rms_inverse(x) * gains_ref[0:1, :]).astype(BF)
    wait(copies)
    cosine, sine = cos_ref[...], sin_ref[...]
    for first in range(0, width + KV_WIDTH, 256):
        linear = nn(act, whole[:width, first : first + 256])
        for at in range(first, first + 256, 128):
            chunk = turn(linear[:, at - first : at - first + 128], cosine, sine)
            if at + 128 <= width:
                q_ref[:, at : at + 128] = (chunk * SCALE).astype(BF)
            elif at < width:
                q_ref[:, at:width] = (chunk[:, : width - at] * SCALE).astype(BF)
                kv_ref[:, : at + 128 - width] = chunk[:, width - at :].astype(BF)
            else:
                kv_ref[:, at - width : at - width + 128] = chunk.astype(BF)
    kv_ref[:, KV_WIDTH:] = nn(act, whole[width:, width:]).astype(BF)


def project(x, gains, cosine, sine, pieces, starts, shape):
    micro, width, rows = x.shape
    tokens = micro * rows
    outs = (
        jax.ShapeDtypeStruct((tokens, width), BF),
        jax.ShapeDtypeStruct((tokens, 2 * KV_WIDTH), BF),
    )
    table = pl.BlockSpec((tokens, 128), lambda i: (0, 0))
    return pl.pallas_call(
        functools.partial(project_kernel, len(pieces)),
        grid=(1,),
        name="project",
        in_specs=[IN_SMEM] + [IN_VMEM] * 2 + [table] * 2 + [ANYWHERE] * len(pieces),
        out_specs=(IN_VMEM,) * 2,
        out_shape=outs,
        scratch_shapes=[pltpu.VMEM(shape, BF), pltpu.SemaphoreType.DMA((len(pieces),))],
        cost_estimate=cost(2 * tokens * width * (width + 2 * KV_WIDTH), 0, x, *outs, *pieces),
        compiler_params=pltpu.CompilerParams(vmem_limit_bytes=VMEM_LIMIT),
    )(starts, x, gains, cosine, sine, *pieces)


def feed_kernel(counts, s0_ref, s1_ref, s2_ref, x_ref, attn_ref, cot_ref, gains_ref, *refs):
    total = sum(counts)
    attention_pieces = refs[: counts[0]]
    pair_pieces = refs[counts[0] : counts[0] + counts[1]]
    down_pieces = refs[counts[0] + counts[1] : total]
    out_ref, inner_ref, slopes_ref, act_t_ref, attn_t_ref, dy_ref, dres_ref, low_ref, dattn_ref = refs[
        total : total + 9
    ]
    w_attn, w_pair, w_down, resid_ref, dact_ref, sems0, sems1, sems2 = refs[total + 9 :]
    attention_copies = load(attention_pieces, s0_ref, w_attn, sems0)
    pair_copies = load(pair_pieces, s1_ref, w_pair, sems1)
    down_copies = load(down_pieces, s2_ref, w_down, sems2)
    width = x_ref.shape[1]
    hidden = w_pair.shape[1]
    tile = hidden // 5
    gain = gains_ref[1:2, :]
    x = upright(x_ref).astype(F32)
    dy_ref[...] = upright(cot_ref)
    attn_t_ref[...] = jnp.transpose(attn_ref[...])
    wait(attention_copies)
    w_output = w_attn[width:, :width]
    resid = x + nn(attn_ref[...], w_output)
    resid_ref[...] = resid
    dres_ref[...] = resid
    root = rms_inverse(resid)
    act = (resid * root * gain).astype(BF)
    act_t_ref[...] = jnp.transpose(act)
    wait(pair_copies)
    wait(down_copies)
    dy = dy_ref[...]
    for first in range(0, hidden, tile):
        here = slice(first, first + tile)
        gate = nn(act, w_pair[:width, here])
        upper = nn(act, w_pair[width:, here])
        d_inner = nt(dy, w_down[here, :])
        sigmoid = 1.0 / (1.0 + jnp.exp(-gate))
        silu = gate * sigmoid
        inner = (silu * upper).astype(BF)
        inner_ref[here, :] = jnp.transpose(inner)
        d_gate = (d_inner * upper * sigmoid * (1.0 + gate * (1.0 - sigmoid))).astype(BF)
        d_upper = (d_inner * silu).astype(BF)
        slopes_ref[0, :, here] = d_gate
        slopes_ref[1, :, here] = d_upper
        out = nn(inner, w_down[here, :])
        d_act = nt(d_gate, w_pair[:width, here]) + nt(d_upper, w_pair[width:, here])
        resid_ref[...] += out
        if first == 0:
            dact_ref[...] = d_act
        else:
            dact_ref[...] += d_act
    lay_down(resid_ref[...].astype(BF), out_ref)
    normed = dres_ref[...] * root
    d_act = dact_ref[...]
    d_normed = d_act * gain
    d_resid = dy.astype(F32) + root * (
        d_normed - normed * jnp.mean(d_normed * normed, axis=-1, keepdims=True)
    )
    dres_ref[...] = d_resid
    low = d_resid.astype(BF)
    low_ref[...] = low
    dattn_ref[...] = nt(low, w_output).astype(BF)


def feed(x, attn, dy, gains, attention_got, pair_got, down_got):
    micro, width, rows = x.shape
    tokens = micro * rows
    groups = [attention_got, pair_got, down_got]
    counts = [len(pieces) for pieces, _, _ in groups]
    shapes = [shape for _, _, shape in groups]
    hidden = shapes[1][1]
    outs = (
        jax.ShapeDtypeStruct(x.shape, BF),
        jax.ShapeDtypeStruct((hidden, tokens), BF),
        jax.ShapeDtypeStruct((2, tokens, hidden), BF),
        jax.ShapeDtypeStruct((width, tokens), BF),
        jax.ShapeDtypeStruct((width, tokens), BF),
        jax.ShapeDtypeStruct((tokens, width), BF),
        jax.ShapeDtypeStruct((tokens, width), F32),
        jax.ShapeDtypeStruct((tokens, width), BF),
        jax.ShapeDtypeStruct((tokens, width), BF),
    )
    every = [piece for pieces, _, _ in groups for piece in pieces]
    return pl.pallas_call(
        functools.partial(feed_kernel, counts),
        name="feed",
        in_specs=[IN_SMEM] * 3 + [IN_VMEM] * 4 + [ANYWHERE] * len(every),
        out_specs=(IN_VMEM,) * 9,
        out_shape=outs,
        scratch_shapes=[pltpu.VMEM(shape, BF) for shape in shapes]
        + [pltpu.VMEM((tokens, width), F32)] * 2
        + [pltpu.SemaphoreType.DMA((count,)) for count in counts],
        cost_estimate=cost(
            2 * tokens * width * (6 * hidden + 3 * width), tokens * hidden, x, x, x, *outs, *every
        ),
        compiler_params=pltpu.CompilerParams(vmem_limit_bytes=VMEM_MOST),
    )(*(starts for _, starts, _ in groups), x, attn, dy, gains, *every)


def pick_rows(source, starts_ref, base, rows, count, target):
    for t in range(count):
        start = pl.multiple_of(starts_ref[base + t], 16)
        target[t * rows : (t + 1) * rows, :] = source[pl.ds(start, rows), :]


def weight_grad_kernel(parts, count, starts_ref, *refs):
    operands = refs[: 2 * len(parts)]
    out_ref = refs[2 * len(parts)]
    ordered = refs[2 * len(parts) + 1 :]
    block = sum(parts)

    @pl.when(pl.program_id(0) == 0)
    def _():
        for i, rows in enumerate(parts):
            pick_rows(operands[2 * i], starts_ref, 1 + i * count, rows, count, ordered[i])

    at = 0
    for i, rows in enumerate(parts):
        made = nn(ordered[i][...], operands[2 * i + 1][...]).astype(BF)
        columns = made.shape[1]
        for t in range(count):
            place = slice(t * block + at, t * block + at + rows)
            out_ref[place, :columns] = made[t * rows : (t + 1) * rows]
            if columns < out_ref.shape[1]:
                out_ref[place, columns:] = jnp.zeros((rows, out_ref.shape[1] - columns), BF)
        at += rows


def weight_grad(terms, column=0, columns=None, choice=0):
    count = len(terms[0][3])
    parts = [term[2] for term in terms]
    block = sum(parts)
    tokens = terms[0][0].shape[1]
    columns = columns or terms[0][1].shape[-1]
    wide = rounded_up(columns)
    if any(rows % 16 for rows in parts) or any(term[0].shape[0] // count % 16 for term in terms):
        made = []
        for left, right, rows, starts in terms:
            right = right if right.ndim == 2 else lax.dynamic_index_in_dim(right, choice, 0, keepdims=False)
            grad = nn(left, right[:, column * columns : (column + 1) * columns]).astype(BF)
            grad = jnp.pad(grad, ((0, 0), (0, wide - columns)))
            made.append([lax.dynamic_slice_in_dim(grad, start, rows, 0) for start in starts])
        return jnp.concatenate([part for group in zip(*made) for part in group], axis=0)
    in_specs, args, flops = [], [], 0
    tile = 256 if columns % 256 == 0 else columns
    skip = column * (columns // tile)
    for left, right, rows, starts in terms:
        in_specs.append(pl.BlockSpec(left.shape, lambda n, info: (0, 0)))
        if right.ndim == 2:
            in_specs.append(pl.BlockSpec((tokens, tile), lambda n, info: (0, skip + n)))
        else:
            in_specs.append(pl.BlockSpec((None, tokens, tile), lambda n, info: (info[0], 0, skip + n)))
        args += [left, right]
        flops += 2 * tokens * rows * count * columns
    out = jax.ShapeDtypeStruct((count * block, wide), BF)
    info = numbers([choice] + [start for term in terms for start in term[3]])
    return pl.pallas_call(
        functools.partial(weight_grad_kernel, parts, count),
        grid_spec=pltpu.PrefetchScalarGridSpec(
            num_scalar_prefetch=1,
            grid=(columns // tile,),
            in_specs=in_specs,
            out_specs=pl.BlockSpec((count * block, rounded_up(tile)), lambda n, info: (0, n)),
            scratch_shapes=[pltpu.VMEM((count * rows, tokens), BF) for rows in parts],
        ),
        out_shape=out,
        name="weight_grad",
        cost_estimate=cost(flops, 0, out, *args),
        compiler_params=pltpu.CompilerParams(vmem_limit_bytes=VMEM_LIMIT),
    )(info, *args)


def turn_keys(source, target, at, cosine, sine):
    rows = source.shape[0]
    for first in range(0, KV_WIDTH, 128):
        chunk = turn(source[:, first : first + 128].astype(F32), cosine, -sine).astype(BF)
        last = min(first + 128, KV_WIDTH)
        target[at : at + rows, first:last] = chunk[:, : last - first]
    target[at : at + rows, KV_WIDTH:] = source[:, KV_WIDTH:]


def attention_grad_kernel(shards, half, starts_ref, gain_ref, cos_ref, sin_ref, dq_ref, *refs):
    xs, dkvs = refs[:shards], refs[shards : 2 * shards]
    outs, (act, dkv, ordered) = refs[2 * shards : 2 * shards + 2], refs[2 * shards + 2 :]
    micro, width, rows = xs[0].shape
    tokens = micro * rows
    for t in range(shards):
        here = slice(t * tokens, (t + 1) * tokens)
        turn_keys(dkvs[t], dkv, t * tokens, cos_ref[here, :], sin_ref[here, :])
        for m in range(micro):
            x = xs[t][m].astype(F32)
            root = lax.rsqrt(jnp.mean(x * x, axis=0, keepdims=True) + EPS)
            first = t * tokens + m * rows
            act[:, first : first + rows] = (x * root * gain_ref[...]).astype(BF)
    for i, out_ref in enumerate(outs):
        pick_rows(act, starts_ref, i * shards, half, shards, ordered)
        out_ref[:, :width] = nn(ordered[:, :tokens], dq_ref[...]).astype(BF)
        start = rounded_up(width)
        if start > width:
            out_ref[:, width:start] = jnp.zeros((out_ref.shape[0], start - width), BF)
        out_ref[:, start:] = nn(ordered[...], dkv[...]).astype(BF)


def attention_grad(x_all, gain, cosine, sine, dq, dkv_all, half, given, kept):
    shards = len(x_all)
    micro, width, rows = x_all[0].shape
    every = shards * micro * rows
    columns = rounded_up(width) + 2 * KV_WIDTH
    out = jax.ShapeDtypeStruct((shards * half, columns), BF)
    if half % 16 or width // shards % 16:
        xs = jnp.concatenate([x[m] for x in x_all for m in range(micro)], axis=1).astype(F32)
        act = xs * lax.rsqrt(jnp.mean(xs * xs, axis=0, keepdims=True) + EPS) * gain
        act = act.astype(BF)
        dkv = jnp.concatenate(dkv_all, axis=0)
        keys = dkv[:, :KV_WIDTH].astype(F32).reshape(every, -1, 2, HALF_HEAD)
        c, s = cosine[:, None, :HALF_HEAD], sine[:, None, HALF_HEAD:HEAD_SIZE]
        first, second = keys[:, :, 0], keys[:, :, 1]
        keys = jnp.stack([first * c + second * s, second * c - first * s], axis=2)
        dkv = jnp.concatenate([keys.reshape(every, KV_WIDTH).astype(BF), dkv[:, KV_WIDTH:]], axis=1)
        q = jnp.pad(nn(act[:, : micro * rows], dq), ((0, 0), (0, rounded_up(width) - width)))
        grad = jnp.concatenate([q, nn(act, dkv)], axis=1).astype(BF)
        return [
            jnp.concatenate([lax.dynamic_slice_in_dim(grad, start, half, 0) for start in starts])
            for starts in (given, kept)
        ]
    return pl.pallas_call(
        functools.partial(attention_grad_kernel, shards, half),
        name="attention_grad",
        in_specs=[IN_SMEM] + [IN_VMEM] * (4 + 2 * shards),
        out_specs=(IN_VMEM,) * 2,
        out_shape=(out, out),
        scratch_shapes=[
            pltpu.VMEM((width, every), BF),
            pltpu.VMEM((every, 2 * KV_WIDTH), BF),
            pltpu.VMEM((shards * half, every), BF),
        ],
        cost_estimate=cost(
            4 * shards * half * (every * 2 * KV_WIDTH + micro * rows * width), 0, *x_all, *dkv_all, out, out
        ),
        compiler_params=pltpu.CompilerParams(vmem_limit_bytes=VMEM_MOST),
    )(numbers(given + kept), gain, cosine, sine, dq, *x_all, *dkv_all)


def finish_kernel(count, starts_ref, x_ref, low_ref, kv_ref, dres_ref, gains_ref, cos_ref, sin_ref, *refs):
    pieces = refs[:count]
    dx_ref, whole, kv_turned, sems = refs[count:]
    copies = load(pieces, starts_ref, whole, sems)
    turn_keys(kv_ref, kv_turned, 0, cos_ref[...], sin_ref[...])
    x = upright(x_ref).astype(F32)
    width = x.shape[1]
    root = rms_inverse(x)
    normed = x * root
    wait(copies)
    d_act = nt(low_ref[...], whole[:width, :width])
    d_act += nt(kv_turned[:, :KV_WIDTH], whole[:width, width:])
    d_act += nt(kv_turned[:, KV_WIDTH:], whole[width:, width:])
    d_normed = d_act * gains_ref[0:1, :]
    d_x = dres_ref[...] + root * (d_normed - normed * jnp.mean(d_normed * normed, axis=-1, keepdims=True))
    lay_down(d_x.astype(BF), dx_ref)


def finish(x, low, kv, dres, gains, cosine, sine, pieces, starts, shape):
    micro, width, rows = x.shape
    tokens = micro * rows
    table = pl.BlockSpec((tokens, 128), lambda i: (0, 0))
    return pl.pallas_call(
        functools.partial(finish_kernel, len(pieces)),
        grid=(1,),
        name="finish",
        in_specs=[IN_SMEM] + [IN_VMEM] * 5 + [table] * 2 + [ANYWHERE] * len(pieces),
        out_specs=IN_VMEM,
        out_shape=jax.ShapeDtypeStruct(x.shape, BF),
        scratch_shapes=[
            pltpu.VMEM(shape, BF),
            pltpu.VMEM((tokens, 2 * KV_WIDTH), BF),
            pltpu.SemaphoreType.DMA((len(pieces),)),
        ],
        cost_estimate=cost(2 * tokens * width * (width + 2 * KV_WIDTH), 0, x, low, dres, *pieces),
        compiler_params=pltpu.CompilerParams(vmem_limit_bytes=VMEM_LIMIT),
    )(starts, x, low, kv, dres, gains, cosine, sine, *pieces)


def head(ref, h):
    return ref[:, h * HEAD_SIZE : (h + 1) * HEAD_SIZE]


def widen(value, columns):
    n = value.shape[0]
    lane = lax.broadcasted_iota(jnp.int32, (n, HEAD_SIZE), 1)
    tail = jnp.zeros((n, HEAD_SIZE), F32)
    for c, column in enumerate(columns):
        tail = jnp.where(lane == c, column, tail)
    return jnp.concatenate([value, tail.astype(BF)], axis=1)


def split(column):
    high = column.astype(BF).astype(F32)
    middle = (column - high).astype(BF).astype(F32)
    return [high, middle, column - high - middle]


def attend_kernel(shards, seg_rows, q_ref, *refs):
    kv = refs[:shards]
    bias_ref = refs[shards]
    o_ref, lse_ref = refs[-2:]
    rows = q_ref.shape[0]
    i = lax.broadcasted_iota(jnp.int32, (rows, rows), 0)
    j = lax.broadcasted_iota(jnp.int32, (rows, rows), 1)
    same = (i // seg_rows) == (j // seg_rows)
    own = jnp.where(j > i, CLOSED, jnp.where(same, 0.0, bias_ref[0:1, :]))
    one = jnp.ones((rows, 1), F32)
    bias_columns = jnp.transpose(bias_ref[...])
    lse = jnp.zeros((rows, 128), F32)
    lane = lax.broadcasted_iota(jnp.int32, (rows, 128), 1)
    for g in range(KEY_VALUE_HEADS):
        keys, values = [], []
        for t in range(shards):
            keys.append(widen(head(kv[t], g), [bias_columns[:, t : t + 1]] if t else []))
            values.append(widen(head(kv[t], KEY_VALUE_HEADS + g), [one]))
        for h in range(g * GROUP, g * GROUP + GROUP):
            q = widen(head(q_ref, h), [one])
            scores = [nt(q, k) for k in keys]
            scores[0] = scores[0] + own
            peak = functools.reduce(jnp.maximum, scores)
            peak = jnp.max(peak, axis=1, keepdims=True)
            terms = [nn(jnp.exp(s - peak).astype(BF), v) for s, v in zip(scores, values)]
            mixed = sum(terms[1:], terms[0])
            total = mixed[:, HEAD_SIZE : HEAD_SIZE + 1]
            o_ref[:, h * HEAD_SIZE : (h + 1) * HEAD_SIZE] = (mixed[:, :HEAD_SIZE] / total).astype(BF)
            lse = jnp.where(lane == h, peak + jnp.log(total), lse)
    lse_ref[...] = lse


def attend_back_kernel(shards, seg_rows, q_ref, *refs):
    kv = refs[:shards]
    bias_ref, o_ref, do_ref, lse_ref, cos_ref, sin_ref = refs[shards : shards + 6]
    dq_ref = refs[-1 - shards]
    dkv = refs[-shards:]
    rows = q_ref.shape[0]
    i = lax.broadcasted_iota(jnp.int32, (rows, rows), 1)
    j = lax.broadcasted_iota(jnp.int32, (rows, rows), 0)
    bias_columns = jnp.transpose(bias_ref[...])
    same = (i // seg_rows) == (j // seg_rows)
    own_column = jnp.broadcast_to(bias_columns[:, 0:1], (rows, rows))
    own = jnp.where(j > i, CLOSED, jnp.where(same, 0.0, own_column))
    one, zero = jnp.ones((rows, 1), F32), jnp.zeros((rows, 1), F32)
    cosine, sine = cos_ref[...], sin_ref[...]
    for g in range(KEY_VALUE_HEADS):
        keys, values, turned = [], [], []
        for t in range(shards):
            k = head(kv[t], g)
            turned.append(jnp.transpose(k))
            keys.append(widen(k, [bias_columns[:, t : t + 1] if t else zero, one, one, one]))
            values.append(widen(head(kv[t], KEY_VALUE_HEADS + g), [one, one, one]))
        dk, dv = [None] * shards, [None] * shards
        for h in range(g * GROUP, g * GROUP + GROUP):
            q, do = head(q_ref, h), head(do_ref, h)
            centre = jnp.sum(head(o_ref, h).astype(F32) * do.astype(F32), axis=1, keepdims=True)
            q_wide = widen(q, [one] + split(-lse_ref[:, h : h + 1]))
            do_wide = widen(do, split(-centre))
            dq = None
            for t in range(shards):
                scores = nt(keys[t], q_wide)
                if t == 0:
                    scores = scores + own
                probs = jnp.exp(scores)
                ds = (probs * nt(values[t], do_wide)).astype(BF)
                v_term = nn(probs.astype(BF), do)
                k_term = nn(ds, q)
                q_term = nn(turned[t], ds)
                dv[t] = v_term if dv[t] is None else dv[t] + v_term
                dk[t] = k_term if dk[t] is None else dk[t] + k_term
                dq = q_term if dq is None else dq + q_term
            dq = dq * SCALE
            first, second = dq[:HALF_HEAD], dq[HALF_HEAD:]
            back = jnp.concatenate(
                [first * cosine + second * sine, second * cosine - first * sine], axis=0
            )
            dq_ref[:, h * HEAD_SIZE : (h + 1) * HEAD_SIZE] = jnp.transpose(back).astype(BF)
        for t in range(shards):
            dkv[t][:, g * HEAD_SIZE : (g + 1) * HEAD_SIZE] = dk[t].astype(BF)
            g_value = KEY_VALUE_HEADS + g
            dkv[t][:, g_value * HEAD_SIZE : (g_value + 1) * HEAD_SIZE] = dv[t].astype(BF)


def attend(micro, seg_rows, q, kv, bias):
    shards, tokens, width = len(kv), q.shape[0], q.shape[1]
    rows = tokens // micro
    here = lambda w: pl.BlockSpec((rows, w), lambda m: (m, 0))
    outs = (jax.ShapeDtypeStruct((tokens, width), BF), jax.ShapeDtypeStruct((tokens, 128), F32))
    pairs = tokens * rows * shards * QUERY_HEADS
    return pl.pallas_call(
        functools.partial(attend_kernel, shards, seg_rows),
        grid=(micro,),
        name="attend",
        in_specs=[here(width)]
        + [here(2 * KV_WIDTH)] * shards
        + [pl.BlockSpec((None,) + bias.shape[1:], lambda m: (m, 0, 0))],
        out_specs=(here(width), here(128)),
        out_shape=outs,
        cost_estimate=cost(16 * HEAD_SIZE * pairs, pairs, q),
        compiler_params=pltpu.CompilerParams(vmem_limit_bytes=VMEM_LIMIT),
    )(q, *kv, bias)


def attend_back(m, rows, seg_rows, q, kv, bias, o, do, lse, cosine, sine, earlier):
    shards, tokens, width = len(kv), q.shape[0], q.shape[1]
    here = lambda w: pl.BlockSpec((rows, w), lambda i: (m, 0))
    turned = pl.BlockSpec((HALF_HEAD, rows), lambda i: (0, m))
    outs = (jax.ShapeDtypeStruct((tokens, width), BF),)
    outs += (jax.ShapeDtypeStruct((tokens, 2 * KV_WIDTH), BF),) * shards
    pairs = rows * rows * shards * QUERY_HEADS
    return pl.pallas_call(
        functools.partial(attend_back_kernel, shards, seg_rows),
        grid=(1,),
        name="attend_back",
        in_specs=[here(width)]
        + [here(2 * KV_WIDTH)] * shards
        + [pl.BlockSpec((None,) + bias.shape[1:], lambda i: (m, 0, 0))]
        + [here(width), here(width), here(128), turned, turned]
        + [pl.BlockSpec(memory_space=pl.ANY)] * len(earlier),
        out_specs=(here(width),) + (here(2 * KV_WIDTH),) * shards,
        out_shape=outs,
        input_output_aliases={shards + 7 + i: i for i in range(len(earlier))},
        cost_estimate=cost(40 * HEAD_SIZE * pairs, pairs, q),
        compiler_params=pltpu.CompilerParams(vmem_limit_bytes=VMEM_LIMIT),
    )(q, *kv, bias, o, do, lse, cosine, sine, *earlier)


def local(
    block_input,
    parent_ids,
    w_query,
    key_weight,
    value_weight,
    w_output,
    w_gate,
    w_up,
    w_down,
    norm_first,
    norm_second,
    out_cotangent,
):
    micro, rows, width = block_input.shape
    shards = lax.axis_size("shard")
    links = Links(lax.axis_size("rep"), shards)
    tree = rows * shards
    segs = parent_ids.shape[2]
    seg_rows = tree // segs
    tokens = micro * rows
    hidden = w_gate.shape[1]

    inputs = block_input.swapaxes(1, 2)
    cotangent = out_cotangent.swapaxes(1, 2)

    even = links.core == 0
    side = lax.axis_index("rep") // 2 % 2
    left = jnp.concatenate([w_query, key_weight], axis=1)
    right = jnp.concatenate([w_output, value_weight], axis=1)
    attn_mine = jnp.where(even, left, right)
    pair_cut = hidden // 2
    pair_mine = lax.dynamic_slice_in_dim(jnp.where(even, w_gate, w_up), side * pair_cut, pair_cut, 1)
    down_cut = w_down.shape[0] // 2
    down_mine = lax.dynamic_slice_in_dim(w_down, links.core * down_cut, down_cut, 0)

    attn_near = links.near(attn_mine)
    gain_pieces = links.small_pieces(jnp.stack([norm_first, norm_second]))
    attn_mine, attn_near, gain_pieces, pair_mine, down_mine = meet(
        attn_mine, attn_near, gain_pieces, pair_mine, down_mine
    )

    gains = links.in_order(gain_pieces).astype(F32)
    attn_all = links.far(attn_mine, attn_near)
    attn_swapped = {t: links.swap(attn_near[t]) for t in attn_near}
    pair_near = {1: links.step(pair_mine, 0)}
    parents = parent_ids[:, 0]
    seg = jnp.arange(segs)
    after_parent = jnp.concatenate([parents[:, 1:], jnp.full((micro, 1), -1, parents.dtype)], axis=1)
    on_path = (seg % 2 == 0)[None] | (after_parent == seg[None])
    below = (seg[None, :] < seg[:, None])[None]
    depth = jnp.sum(jnp.where(below, on_path.astype(F32)[:, None, :], 0.0), axis=-1)

    def row_numbers(hop):
        return (links.shard ^ hop) * rows + jnp.arange(rows)

    def pick(table, numbers):
        hit = (numbers // seg_rows)[..., None] == seg
        return jnp.sum(jnp.where(hit[None], table.reshape(micro, *(1,) * numbers.ndim, segs), 0), axis=-1)

    key_rows = jnp.stack([row_numbers(hop) for hop in links.hops])
    positions = pick(depth, key_rows) * seg_rows + (key_rows % seg_rows).astype(F32)
    freqs = jnp.exp(-math.log(10000.0) * jnp.arange(HALF_HEAD, dtype=F32) * (2.0 / HEAD_SIZE))
    angles = freqs[:, None] * positions.swapaxes(0, 1).reshape(1, shards * tokens)
    cosine_t, sine_t = jnp.cos(angles), jnp.sin(angles)
    cosine = jnp.tile(cosine_t.T, (1, 4))
    sine = jnp.tile(jnp.concatenate([-sine_t.T, sine_t.T], axis=1), (1, 2))
    open_key = (pick(on_path.astype(F32), key_rows) > 0.5) & (
        (key_rows < links.shard * rows) | (jnp.arange(shards) == 0)[:, None]
    )
    bias = jnp.where(open_key, 0.0, CLOSED)
    bias = jnp.pad(bias, ((0, 0), (0, 8 - shards), (0, 0)))

    attn_all, attn_swapped, pair_mine, pair_near, gains, cosine, sine, bias, down_mine = meet(
        attn_all, attn_swapped, pair_mine, pair_near, gains, cosine, sine, bias, down_mine
    )

    for t in range(1, shards):
        if t not in attn_swapped:
            attn_swapped[t] = links.swap(attn_all[t])
    shard_rows = width // shards

    def pair_place(weight, hop):
        return weight * width + (links.shard ^ hop) * shard_rows

    pieces, starts = [left, right], [(pair_place(0, 0), 0), (pair_place(1, 0), 0)]
    for t in range(1, shards):
        pieces += [attn_all[t], attn_swapped[t]]
        starts += [
            (pair_place(links.core, links.hops[t]), 0),
            (pair_place(1 - links.core, links.hops[links.twin(t)]), 0),
        ]
    attention_got = joined(pieces, starts, (2 * width, left.shape[1]))
    pair_near |= {1 << i: links.step(pair_mine, i) for i in range(1, links.bits)}
    pair_beside = {1: links.beside(pair_near[1])}
    down_near = {1: links.step(down_mine, 0)}
    queries, kv = project(inputs, gains, cosine, sine, *attention_got)
    queries, kv, pair_mine, pair_near, pair_beside, down_mine, down_near = meet(
        queries, kv, pair_mine, pair_near, pair_beside, down_mine, down_near
    )

    kv_near = links.near(kv)
    pair_beside |= {t: links.beside(pair_near[t]) for t in pair_near if t > 1}
    kv_near, kv, pair_beside, pair_near, pair_mine = meet(kv_near, kv, pair_beside, pair_near, pair_mine)

    kv_all = links.far(kv, kv_near)
    pair_all = links.far(pair_mine, pair_near)
    pair_swapped = {t: links.swap(pair_near[t]) for t in pair_near}
    pair_crossed = {t: links.swap(pair_beside[t]) for t in pair_beside}
    kv_all, pair_all, pair_swapped, pair_crossed, pair_beside, down_mine, down_near = meet(
        kv_all, pair_all, pair_swapped, pair_crossed, pair_beside, down_mine, down_near
    )

    down_near |= {1 << i: links.step(down_mine, i) for i in range(1, links.bits)}
    down_all = links.far(down_mine, down_near)
    pair_beside |= {t: links.beside(pair_all[t]) for t in range(1, shards) if t not in pair_beside}
    attn, lse = attend(micro, seg_rows, queries, kv_all, bias)
    pair_swapped |= {t: links.swap(pair_all[t]) for t in range(1, shards) if t not in pair_swapped}
    attn, lse, down_all, pair_beside, pair_all, pair_swapped = meet(
        attn, lse, down_all, pair_beside, pair_all, pair_swapped
    )

    pair_crossed |= {t: links.swap(pair_beside[t]) for t in range(1, shards) if t not in pair_crossed}
    down_swapped = [None] + [links.swap(down_all[t]) for t in range(1, shards)]
    pieces, starts = [w_gate, w_up], [(pair_place(0, 0), 0), (pair_place(1, 0), 0)]
    for t in range(1, shards):
        pieces += [pair_all[t], pair_beside[t], pair_swapped[t], pair_crossed[t]]
        for row in (
            pair_place(links.core, links.hops[t]),
            pair_place(1 - links.core, links.hops[links.twin(t)]),
        ):
            starts += [(row, side * pair_cut), (row, (1 - side) * pair_cut)]
    pair_got = joined(pieces, starts, (2 * width, hidden))
    own = w_down.shape[0]
    pieces, starts = [w_down], [(links.shard * own, 0)]
    for t in range(1, shards):
        pieces += [down_all[t], down_swapped[t]]
        starts += [
            ((links.shard ^ links.hops[t]) * own + links.core * down_cut, 0),
            ((links.shard ^ links.hops[links.twin(t)]) * own + (1 - links.core) * down_cut, 0),
        ]
    down_got = joined(pieces, starts, (own * shards, width))
    attn, pair_pieces, down_pieces = meet(attn, pair_got[0], down_got[0])
    pair_got, down_got = (pair_pieces, *pair_got[1:]), (down_pieces, *down_got[1:])

    plan = Plan()
    have = lambda *names: [plan.have[name] for name in names]
    x_near = links.near(inputs)
    made = feed(inputs, attn, cotangent, gains, attention_got, pair_got, down_got)
    names = ("out", "inner", "slopes", "act", "attn_t", "dy", "d_resid", "d_resid_low", "d_attn")
    plan.have = dict(zip(names, made)) | {"x_near": x_near, "queries": queries, "kv": kv_all, "lse": lse, "attn": attn}
    plan.close()

    down_half = own // 2
    output_half, output_mine, output_theirs = links.half_rows(shard_rows)
    down_kept, down_given = links.order(own, links.core * down_half, (1 - links.core) * down_half)
    wide_kept, wide_given = links.order(shard_rows, 0, 0)
    some_kept, some_given = links.order(shard_rows, output_mine, output_theirs)

    def rows_grads(down, output):
        inner, dy, attn_t, low = have("inner", "dy", "attn_t", "d_resid_low")
        return weight_grad(((inner, dy, down_half, down), (attn_t, low, output_half, output)))

    def wide_grads(chunk, starts, choice):
        act, slopes = have("act", "slopes")
        return weight_grad(((act, slopes, shard_rows, starts),), chunk, hidden // 2, choice)

    plan.have["x_all"] = links.far(inputs, plan.have.pop("x_near"))
    plan.have["rows.given"] = rows_grads(down_given, some_given)
    plan.have["rows.kept"] = rows_grads(down_kept, some_kept)
    plan.close()

    for name in ("rows", "wide0", "wide1", "some"):
        plan.start(name, links.reduce(plan, name))
    plan.advance("rows")
    for chunk, name in enumerate(("wide0", "wide1")):
        plan.have[name + ".given"] = wide_grads(chunk, wide_given, 1 - links.core)
        plan.have[name + ".kept"] = wide_grads(chunk, wide_kept, links.core)
    plan.close()

    made = ()
    hops = [("rows", "wide0", "wide1"), ("rows", "wide0")]
    for m in range(micro):
        plan.advance(*hops[min(m, 1)])
        q, kv_now, o, do, lse_now = have("queries", "kv", "attn", "d_attn", "lse")
        made = attend_back(m, rows, seg_rows, q, kv_now, bias, o, do, lse_now, cosine_t, sine_t, made)
        plan.have["attn_grads"] = made = tuple(made)
        plan.close()
        made = plan.have["attn_grads"]

    d_queries, *d_kv = plan.have.pop("attn_grads")
    plan.have["dkv.pieces"] = d_kv
    plan.have["d_queries"] = d_queries
    plan.start("dkv", links.collect(plan, "dkv"))
    plan.advance("rows", "wide0", "wide1")
    given, kept = attention_grad(
        plan.have["x_all"], gains[0][:, None], cosine, sine, d_queries, d_kv, output_half, some_given, some_kept
    )
    plan.have["some.given"], plan.have["some.kept"] = given, kept
    plan.close()

    order = [("rows", "wide0", "wide1", "some", "dkv")] * 5 + [("wide1", "some")]
    while plan.tasks:
        plan.advance(*(order.pop(0) if order else tuple(plan.tasks)))
        if "dkv" in plan.have and "d_input" not in plan.have:
            plan.have["d_input"] = finish(
                inputs, *have("d_queries", "dkv", "d_resid"), gains, cosine, sine, *attention_got
            )
        plan.close()

    def owned(name, rows_of):
        value, other = plan.have[name]
        return links.finish_rows(value, other, rows_of)

    rows_own, rows_other = plan.have["rows"]
    grad_down = links.finish_rows(rows_own[:down_half, :width], rows_other[:down_half, :width], own)
    grad_output = links.finish_rows(rows_own[down_half:, :width], rows_other[down_half:, :width], shard_rows)
    grad_gate, grad_upper = (
        jnp.concatenate(parts, axis=1)
        for parts in zip(*(links.finish_pair(*plan.have[name]) for name in ("wide0", "wide1")))
    )
    some = owned("some", shard_rows)
    first = rounded_up(width)
    grad_query, grad_key, grad_value = (
        some[:, :width],
        some[:, first : first + KV_WIDTH],
        some[:, first + KV_WIDTH :],
    )

    def gain_grad(gain, *pairs):
        sums = sum(jnp.sum(weight.astype(F32) * grad, axis=1) for weight, grad in pairs)
        return sums / gain.astype(F32)

    return (
        plan.have["out"].swapaxes(1, 2),
        plan.have["d_input"].swapaxes(1, 2),
        grad_query,
        grad_key,
        grad_value,
        grad_output,
        grad_gate,
        grad_upper,
        grad_down,
        gain_grad(norm_first, (w_query, grad_query), (key_weight, grad_key), (value_weight, grad_value)),
        gain_grad(norm_second, (w_gate, grad_gate), (w_up, grad_upper)),
    )


def solution(mesh):
    rows = P(None, AXES, None)
    weight, gain = P("shard", None), P("shard")
    return jax.shard_map(
        local,
        mesh=mesh,
        in_specs=(rows, P(None, "rep", None)) + (weight,) * 7 + (gain, gain, rows),
        out_specs=(rows, rows) + (weight,) * 7 + (gain, gain),
        check_vma=False,
    )
```

time: 531 us -> 445 us (0.84)
  starting transfers between devices: 110 us -> 74.1 us
  local copies, waits for them, and re-layouts: 72.9 us -> 39.6 us
  waiting for transfers between devices: 144 us -> 121 us
    ppermute x91 -> x64, starting transfers between devices: 110 us -> 74.1 us  [move(): return lax.ppermute(value, AXES, pairs)]
    unnamed x233 -> x178, local copies, waits for them, and re-layouts: 48.5 us -> 23.6 us
    ppermute x91 -> x64, waiting for transfers between devices: 144 us -> 121 us  [move(): return lax.ppermute(value, AXES, pairs)]
    pallas_call x3, Pallas kernels: 16.5 us -> 27 us  [the longest x1 11.2 us: attention_grad(): pl.pallas_call(functools.partial(attention_grad_kernel, shards, half), na...]
    pallas_call x10 -> x6, Pallas kernels: 40 us -> 29.9 us  [weight_grad(): pl.pallas_call(functools.partial(weight_grad_kernel, parts, count), grid_...]
    pallas_call x2 -> x0, local copies, waits for them, and re-layouts: 8.26 us -> none  [weight_grad(): pl.pallas_call(functools.partial(weight_grad_kernel, parts, count), grid_...]
    convert_element_type x29 -> x23, other arithmetic: 37.6 us -> 35.4 us  [the longest x22 35.4 us: total(): return sum((part.astype(F32) for part in parts)).astype(parts[0].dtype)]
    pallas_call x2 -> x1, Pallas kernels: 16.1 us -> 16.6 us  [attend(): pl.pallas_call(functools.partial(attend_kernel, shards, seg_rows), grid=(...]
  transfers between devices with their start and end apart: 91 -> 64, of which waited for: 33 -> 22; matrix products, arithmetic and copies ran while one was open for 16% -> 11% of each run, Pallas kernels for 19% -> 32%
where the time goes in v5:
time: 445 us; the launch traced here: 437 us
  Pallas kernels  141 us (32%)
  waiting for transfers between devices  121 us (27%)
  starting transfers between devices  74.1 us (17%)
  other arithmetic  58.8 us (13%)
  local copies, waits for them, and re-layouts  39.6 us (9%)
    ppermute x64, waiting for transfers between devices, move(): return lax.ppermute(value, AXES, pairs)  121 us
    ppermute x64, starting transfers between devices, move(): return lax.ppermute(value, AXES, pairs)  74.1 us
    convert_element_type x22, other arithmetic, total(): return sum((part.astype(F32) for part in parts)).astype(parts[0].dtype)  35.4 us
    pallas_call x2, Pallas kernels, attend_back(): pl.pallas_call(functools.partial(attend_back_kernel, shards, seg_rows), g...  34 us
    pallas_call x1, Pallas kernels, feed(): pl.pallas_call(functools.partial(feed_kernel, counts), name='feed', in_sp...  33.8 us
    pallas_call x6, Pallas kernels, weight_grad(): pl.pallas_call(functools.partial(weight_grad_kernel, parts, count), grid_...  29.9 us
    unnamed x178, local copies, waits for them, and re-layouts  23.6 us
    pallas_call x1, Pallas kernels, attend(): pl.pallas_call(functools.partial(attend_kernel, shards, seg_rows), grid=(...  16.6 us
  transfers between devices with their start and end apart: 64, of which 22 were waited for; matrix products, arithmetic and copies ran while one was open for 11% of the time, Pallas kernels for 32%

profile of v5, /device:TPU:0, one launch (start us, length us, event | category | flops | bytes accessed | tf_op | source)
XLA Modules:
  0.0 437.1 jit_solution(17419833786699325863)
XLA Ops:
  2.9 2.4 broadcast_select_fusion.9
  5.4 3.0 collective-permute-start
  8.4 1.5 collective-permute-start.1
  10.6 2.9 collective-permute-start.4
  14.1 1.8 fusion
  15.9 1.5 constant_dynamic-slice_fusion
  17.5 1.9 pad_maximum_fusion.2
  19.3 2.2 dynamic-slice_select_fusion
  25.3 2.0 collective-permute-start.8
  27.6 11.8 %collective-permute-done.5.refs_6_ = bf16[240,1280]{1,0:T(8,128)(2,1)S(1)} collective-permute-done((bf16[240,1280]{1,0:T(8,128)(2,1)S(1)}, bf16[240,1280]{1,0:T(8,128)(2,1)S(1)}, u32[]{:S(2)}, u32[]{:S(2)}) %collective-permute-start.5) | collective-permute-done | bytes 614432 | tf_op jit(solution)/shard_map/ppermute | solution.py:88
  43.3 3.1 collective-permute-start.11
  46.4 2.2 collective-permute-start.12
  48.7 2.6 copy.78.cos_ref
  51.3 2.6 copy.79.sin_ref
  56.1 6.6 %project.1 = (bf16[512,960]{1,0:T(8,128)(2,1)}, bf16[512,640]{1,0:T(8,128)(2,1)S(1)}) custom-call(s32[16]{0:T(128)S(1)} %stack.106.starts_ref.s0_ref, bf16[2,960,256]{2,1,0:T(8,128)(2,1)} %bitcast.8.x_ref.refs_0_, f32[2,960]{1,0:T(2,128)S(1)} %maximum_convert_fusion.7.gains_ref, f32[2048,128]{1,0:T(8,128)} %copy.78.cos_ref, f32[2048,128]{1,0:T(8,128)} %copy.79.sin_ref, ...), custom_call_target="tpu_custom_call" | custom-call | flops 1572864000 | bytes 7536640 | tf_op jit(solution)/shard_map/project/pallas_call | solution.py:298
  64.0 1.6 collective-permute-start.15
  65.7 14.1 %collective-permute-done.15.refs_15_ = bf16[240,1280]{1,0:T(8,128)(2,1)S(1)} collective-permute-done((bf16[240,1280]{1,0:T(8,128)(2,1)}, bf16[240,1280]{1,0:T(8,128)(2,1)S(1)}, u32[]{:S(2)}, u32[]{:S(2)}) %collective-permute-start.15) | collective-permute-done | bytes 614432 | tf_op jit(solution)/shard_map/ppermute | solution.py:88
  82.5 7.8 %collective-permute-done.17.refs_18_ = bf16[240,1280]{1,0:T(8,128)(2,1)S(1)} collective-permute-done((bf16[240,1280]{1,0:T(8,128)(2,1)}, bf16[240,1280]{1,0:T(8,128)(2,1)S(1)}, u32[]{:S(2)}, u32[]{:S(2)}) %collective-permute-start.17) | collective-permute-done | bytes 614432 | tf_op jit(solution)/shard_map/ppermute | solution.py:88
  90.3 2.0 collective-permute-done.21.refs_17_
  92.3 5.0 %collective-permute-done.16.refs_3_ = bf16[512,640]{1,0:T(8,128)(2,1)S(1)} collective-permute-done((bf16[512,640]{1,0:T(8,128)(2,1)S(1)}, bf16[512,640]{1,0:T(8,128)(2,1)S(1)}, u32[]{:S(2)}, u32[]{:S(2)}) %collective-permute-start.16) | collective-permute-done | bytes 655392 | tf_op jit(solution)/shard_map/ppermute | solution.py:88
  99.0 1.7 collective-permute-start.23
  102.0 16.6 %attend.1 = (bf16[512,960]{1,0:T(8,128)(2,1)S(1)}, f32[512,128]{1,0:T(8,128)S(1)}) custom-call(bf16[512,960]{1,0:T(8,128)(2,1)S(1)} %copy-done.30, bf16[512,640]{1,0:T(8,128)(2,1)S(1)} %get-tuple-element.456.refs_0_, bf16[512,640]{1,0:T(8,128)(2,1)S(1)} %collective-permute-done.13.refs_1_, bf16[512,640]{1,0:T(8,128)(2,1)S(1)} %collective-permute-done.14.refs_2_, ...), custom_call_target="tpu_custom_call" | custom-call | flops 8053063680 | bytes 983040 | tf_op jit(solution)/shard_map/attend/pallas_call | solution.py:701
  123.3 1.6 collective-permute-start.31
  125.5 2.6 copy.80.refs_22_
  128.1 33.8 %feed.1 = (bf16[2,960,256]{2,1,0:T(8,128)(2,1)}, bf16[2560,512]{1,0:T(8,128)(2,1)}, bf16[2,512,2560]{2,1,0:T(8,128)(2,1)}, bf16[960,512]{1,0:T(8,128)(2,1)}, bf1...) custom-call(s32[16]{0:T(128)} %copy-done.28, ...), custom_call_target="tpu_custom_call" | custom-call | flops 17930649600 | bytes 38338560 | tf_op jit(solution)/shard_map/feed/pallas_call | solution.py:393
  163.0 1.7 copy-done.1
  168.4 4.4 %weight_grad.6 = bf16[1792,1024]{1,0:T(8,128)(2,1)} custom-call(s32[9]{0:T(128)S(1)} %stack.240.starts_ref, bf16[2560,512]{1,0:T(8,128)(2,1)S(1)} %copy-done.1, bf16[512,960]{1,0:T(8,128)(2,1)S(1)} %copy-done.7, bf16[960,512]{1,0:T(8,128)(2,1)S(1)} %copy-done.9, bf16[512,960]{1,0:T(8,128)(2,1)S(1)} %copy-done.8), custom_call_target="tpu_custom_call" | custom-call | flops 1761607680 | bytes 9240576 | tf_op jit(solution)/shard_map/weight_grad/pallas_call | solution.py:466
  172.8 4.5 %weight_grad.7 = bf16[1792,1024]{1,0:T(8,128)(2,1)} custom-call(s32[9]{0:T(128)S(1)} %stack.246.starts_ref, bf16[2560,512]{1,0:T(8,128)(2,1)S(1)} %copy-done.1, bf16[512,960]{1,0:T(8,128)(2,1)S(1)} %copy-done.7, bf16[960,512]{1,0:T(8,128)(2,1)S(1)} %copy-done.9, bf16[512,960]{1,0:T(8,128)(2,1)S(1)} %copy-done.8), custom_call_target="tpu_custom_call" | custom-call | flops 1761607680 | bytes 9240576 | tf_op jit(solution)/shard_map/weight_grad/pallas_call | solution.py:466
  177.6 5.9 %weight_grad.8 = bf16[960,1280]{1,0:T(8,128)(2,1)} custom-call(s32[5]{0:T(128)S(1)} %stack.251.starts_ref, bf16[960,512]{1,0:T(8,128)(2,1)S(1)} %copy-done, bf16[2,512,2560]{2,1,0:T(8,128)(2,1)} %get-tuple-element.424.refs_1_), custom_call_target="tpu_custom_call" | custom-call | flops 1258291200 | bytes 8683520 | tf_op jit(solution)/shard_map/weight_grad/pallas_call | solution.py:466
  183.5 4.8 %weight_grad.10 = bf16[960,1280]{1,0:T(8,128)(2,1)S(1)} custom-call(s32[5]{0:T(128)S(1)} %stack.251.starts_ref, bf16[960,512]{1,0:T(8,128)(2,1)S(1)} %copy-done, bf16[2,512,2560]{2,1,0:T(8,128)(2,1)} %get-tuple-element.424.refs_1_), custom_call_target="tpu_custom_call" | custom-call | flops 1258291200 | bytes 8683520 | tf_op jit(solution)/shard_map/weight_grad/pallas_call | solution.py:466
  188.3 4.8 %weight_grad.9 = bf16[960,1280]{1,0:T(8,128)(2,1)S(1)} custom-call(s32[5]{0:T(128)S(1)} %stack.253.starts_ref, bf16[960,512]{1,0:T(8,128)(2,1)S(1)} %copy-done, bf16[2,512,2560]{2,1,0:T(8,128)(2,1)} %get-tuple-element.424.refs_1_), custom_call_target="tpu_custom_call" | custom-call | flops 1258291200 | bytes 8683520 | tf_op jit(solution)/shard_map/weight_grad/pallas_call | solution.py:466
  193.2 5.4 %weight_grad.11 = bf16[960,1280]{1,0:T(8,128)(2,1)S(1)} custom-call(s32[5]{0:T(128)S(1)} %stack.253.starts_ref, bf16[960,512]{1,0:T(8,128)(2,1)S(1)} %copy-done, bf16[2,512,2560]{2,1,0:T(8,128)(2,1)} %get-tuple-element.424.refs_1_), custom_call_target="tpu_custom_call" | custom-call | flops 1258291200 | bytes 8683520 | tf_op jit(solution)/shard_map/weight_grad/pallas_call | solution.py:466
  199.2 4.4 add_convert_fusion
  205.7 17.0 %attend_back.2 = (bf16[512,960]{1,0:T(8,128)(2,1)}, bf16[512,640]{1,0:T(8,128)(2,1)S(1)}, bf16[512,640]{1,0:T(8,128)(2,1)S(1)}, bf16[512,640]{1,0:T(8,128)(2,1)S(1)}, bf16[512,640]{1,0:T(8,128)(2,1)S(1)}) custom-call(bf16[512,960]{1,0:T(8,128)(2,1)} %get-tuple-element.455.q_ref, bf16[512,640]{1,0:T(8,128)(2,1)S(1)} %copy-done.32, ...), custom_call_target="tpu_custom_call" | custom-call | flops 10066329600 | bytes 983040 | tf_op jit(solution)/shard_map/attend_back/pallas_call | solution.py:722
  222.7 4.4 collective-permute-done.34
  228.3 2.7 add_convert_fusion.2
  232.1 2.0 add_convert_fusion.6
  235.0 17.0 %attend_back.3 = (bf16[512,960]{1,0:T(8,128)(2,1)}, bf16[512,640]{1,0:T(8,128)(2,1)S(1)}, bf16[512,640]{1,0:T(8,128)(2,1)S(1)}, bf16[512,640]{1,0:T(8,128)(2,1)S(1)}, bf16[512,640]{1,0:T(8,128)(2,1)S(1)}) custom-call(bf16[512,960]{1,0:T(8,128)(2,1)} %get-tuple-element.455.q_ref, ...), custom_call_target="tpu_custom_call", output_to_operand_aliasing={{0}: (11, {}), {1}: (12, {}), {2}: (13, {}), {3}: (14, {}),... | custom-call | flops 10066329600 | bytes 983040 | tf_op jit(solution)/shard_map/attend_back/pallas_call | solution.py:722
  252.0 4.4 %collective-permute-done.37 = bf16[448,1024]{1,0:T(8,128)(2,1)S(1)} collective-permute-done((bf16[448,1024]{1,0:T(8,128)(2,1)S(1)}, bf16[448,1024]{1,0:T(8,128)(2,1)S(1)}, u32[]{:S(2)}, u32[]{:S(2)}) %collective-permute-start.37) | collective-permute-done | bytes 917536 | tf_op jit(solution)/shard_map/ppermute | solution.py:88
  256.4 1.5 collective-permute-done.38
  257.9 2.8 add_convert_fusion.1
  261.9 2.9 add_convert_fusion.5
  264.7 4.6 %collective-permute-start.39 = (bf16[448,1024]{1,0:T(8,128)(2,1)}, bf16[448,1024]{1,0:T(8,128)(2,1)}, u32[]{:S(2)}, u32[]{:S(2)}) collective-permute-start(bf16[448,1024]{1,0:T(8,128)(2,1)} %add_convert_fusion.5), channel_id=1, source_target_pairs={{0,8},{1,9},{2,10},{3,11},{4,12},{5,13},{6,14},{7,15},{24,16},{25,... | collective-permute-start | bytes 2752520 | tf_op jit(solution)/shard_map/ppermute | solution.py:88
  269.4 2.3 add_convert_fusion.18
  274.5 11.2 %attention_grad.1 = (bf16[512,1664]{1,0:T(8,128)(2,1)}, bf16[512,1664]{1,0:T(8,128)(2,1)}) custom-call(s32[8]{0:T(128)} %stack.254.starts_ref, f32[960,1]{1,0:T(8,128)} %copy.81.gain_ref, f32[2048,128]{1,0:T(8,128)} %copy.78.cos_ref, f32[2048,128]{1,0:T(8,128)} %copy.79.sin_ref, bf16[512,960]{1,0:T(8,128)(2,1)} %get-tuple-element.521.dq_ref.low_ref, ...), custom_call_target="tpu_custom_call" | custom-call | flops 3690987520 | bytes 9961472 | tf_op jit(solution)/shard_map/attention_grad/pallas_call | solution.py:535
  287.9 1.9 add_convert_fusion.17
  289.9 4.4 %collective-permute-start.46 = (bf16[240,1280]{1,0:T(8,128)(2,1)S(1)}, bf16[240,1280]{1,0:T(8,128)(2,1)S(1)}, u32[]{:S(2)}, u32[]{:S(2)}) collective-permute-start(bf16[240,1280]{1,0:T(8,128)(2,1)S(1)} %add_convert_fusion.17), channel_id=1, source_target_pairs={{0,8},{1,9},{2,10},{3,11},{4,12},{5,13},{6,14},{7,15},{24,16},{25,... | collective-permute-start | bytes 1843208 | tf_op jit(solution)/shard_map/ppermute | solution.py:88
  294.3 1.8 add_convert_fusion.4
  297.0 1.5 add_convert_fusion.16
  298.4 9.6 %collective-permute-done.46 = bf16[240,1280]{1,0:T(8,128)(2,1)S(1)} collective-permute-done((bf16[240,1280]{1,0:T(8,128)(2,1)S(1)}, bf16[240,1280]{1,0:T(8,128)(2,1)S(1)}, u32[]{:S(2)}, u32[]{:S(2)}) %collective-permute-start.46) | collective-permute-done | bytes 614432 | tf_op jit(solution)/shard_map/ppermute | solution.py:88
  309.2 8.9 %collective-permute-done.47 = bf16[240,1280]{1,0:T(8,128)(2,1)S(1)} collective-permute-done((bf16[240,1280]{1,0:T(8,128)(2,1)S(1)}, bf16[240,1280]{1,0:T(8,128)(2,1)S(1)}, u32[]{:S(2)}, u32[]{:S(2)}) %collective-permute-start.47) | collective-permute-done | bytes 614432 | tf_op jit(solution)/shard_map/ppermute | solution.py:88
  327.5 2.4 add_convert_fusion.14
  329.9 7.7 %collective-permute-start.52 = (bf16[240,1280]{1,0:T(8,128)(2,1)}, bf16[240,1280]{1,0:T(8,128)(2,1)S(1)}, u32[]{:S(2)}, u32[]{:S(2)}) collective-permute-start(bf16[240,1280]{1,0:T(8,128)(2,1)} %add_convert_fusion.14), channel_id=1, source_target_pairs={{0,8},{1,9},{2,10},{3,11},{4,12},{5,13},{6,14},{7,15},{24,16},{25,... | collective-permute-start | bytes 1843208 | tf_op jit(solution)/shard_map/ppermute | solution.py:88
  337.6 11.4 %collective-permute-done.52 = bf16[240,1280]{1,0:T(8,128)(2,1)S(1)} collective-permute-done((bf16[240,1280]{1,0:T(8,128)(2,1)}, bf16[240,1280]{1,0:T(8,128)(2,1)S(1)}, u32[]{:S(2)}, u32[]{:S(2)}) %collective-permute-start.52) | collective-permute-done | bytes 614432 | tf_op jit(solution)/shard_map/ppermute | solution.py:88
  350.5 1.5 add_convert_fusion.13
  359.7 9.1 %finish.1 = bf16[2,960,256]{2,1,0:T(8,128)(2,1)} custom-call(s32[16]{0:T(128)S(1)} %copy-done.29, bf16[2,960,256]{2,1,0:T(8,128)(2,1)} %bitcast.8.x_ref.refs_0_, bf16[512,960]{1,0:T(8,128)(2,1)} %get-tuple-element.521.dq_ref.low_ref, bf16[512,640]{1,0:T(8,128)(2,1)S(1)} %add_convert_fusion.8.kv_ref, f32[512,960]{1,0:T(8,128)} %get-tuple-element.524.dres_ref, ...), custom_call_target="tpu_custom_call" | custom-call | flops 1572864000 | bytes 8847360 | tf_op jit(solution)/shard_map/finish/pallas_call | solution.py:575
  373.1 6.9 %collective-permute-start.57 = (bf16[128,1664]{1,0:T(8,128)(2,1)S(1)}, bf16[128,1664]{1,0:T(8,128)(2,1)S(1)}, u32[]{:S(2)}, u32[]{:S(2)}) collective-permute-start(bf16[128,1664]{1,0:T(8,128)(2,1)S(1)} %add_convert_fusion.21), channel_id=1, source_target_pairs={{0,8},{1,9},{2,10},{3,11},{4,12},{5,13},{6,14},{7,15},{24,16},{25,... | collective-permute-start | bytes 1277960 | tf_op jit(solution)/shard_map/ppermute | solution.py:88
  380.0 9.7 %collective-permute-done.57 = bf16[128,1664]{1,0:T(8,128)(2,1)S(1)} collective-permute-done((bf16[128,1664]{1,0:T(8,128)(2,1)S(1)}, bf16[128,1664]{1,0:T(8,128)(2,1)S(1)}, u32[]{:S(2)}, u32[]{:S(2)}) %collective-permute-start.57) | collective-permute-done | bytes 426016 | tf_op jit(solution)/shard_map/ppermute | solution.py:88
  389.7 1.5 collective-permute-done.59
  394.8 22.8 %collective-permute-done.62 = bf16[128,1664]{1,0:T(8,128)(2,1)S(1)} collective-permute-done((bf16[128,1664]{1,0:T(8,128)(2,1)S(1)}, bf16[128,1664]{1,0:T(8,128)(2,1)S(1)}, u32[]{:S(2)}, u32[]{:S(2)}) %collective-permute-start.62) | collective-permute-done | bytes 426016 | tf_op jit(solution)/shard_map/ppermute | solution.py:88
  417.8 1.8 collective-permute-done.63
  427.0 2.0 copy.90
  432.3 1.8 multiply_reduce_fusion.1
  434.0 1.8 multiply_reduce_fusion
  (347 shorter events, 82.6 us)
Async XLA Ops:
  5.4 18.4 %collective-permute-start = (bf16[240,1280]{1,0:T(8,128)(2,1)}, bf16[240,1280]{1,0:T(8,128)(2,1)S(1)}, u32[]{:S(2)}, u32[]{:S(2)}) collective-permute-start(bf16[240,1280]{1,0:T(8,128)(2,1)} %get-tuple-element.635), channel_id=1, source_target_pairs={{0,1},{1,0},{2,3},{3,2},{4,6},{5,7},{6,4},{7,5},{8,9},{9,8},{10,11... | collective-permute-start | bytes 1843208 | tf_op jit(solution)/shard_map/ppermute | solution.py:88
  8.4 15.4 %collective-permute-start.1 = (bf16[240,1280]{1,0:T(8,128)(2,1)}, bf16[240,1280]{1,0:T(8,128)(2,1)S(1)}, u32[]{:S(2)}, u32[]{:S(2)}) collective-permute-start(bf16[240,1280]{1,0:T(8,128)(2,1)} %get-tuple-element.635), channel_id=1, source_target_pairs={{0,2},{1,3},{2,0},{3,1},{4,5},{5,4},{6,7},{7,6},{8,10},{9,11},{10,... | collective-permute-start | bytes 1843208 | tf_op jit(solution)/shard_map/ppermute | solution.py:88
  10.0 12.9 %collective-permute-start.2 = (bf16[2,240]{1,0:T(2,128)(2,1)S(1)}, bf16[2,240]{1,0:T(2,128)(2,1)S(1)}, u32[]{:S(2)}, u32[]{:S(2)}) collective-permute-start(bf16[2,240]{1,0:T(2,128)(2,1)S(1)} %pad_maximum_fusion.4), channel_id=1, source_target_pairs={{0,1},{1,0},{2,3},{3,2},{4,5},{5,4},{6,7},{7,6},{8,9},{9,8},{10,11... | collective-permute-start | bytes 2888 | tf_op jit(solution)/shard_map/ppermute | solution.py:88
  10.6 12.3 %collective-permute-start.3 = (bf16[2,240]{1,0:T(2,128)(2,1)S(1)}, bf16[2,240]{1,0:T(2,128)(2,1)S(1)}, u32[]{:S(2)}, u32[]{:S(2)}) collective-permute-start(bf16[2,240]{1,0:T(2,128)(2,1)S(1)} %pad_maximum_fusion.4), channel_id=1, source_target_pairs={{0,2},{1,3},{2,0},{3,1},{4,6},{5,7},{6,4},{7,5},{8,10},{9,11},{10,... | collective-permute-start | bytes 2888 | tf_op jit(solution)/shard_map/ppermute | solution.py:88
  10.6 13.2 %collective-permute-start.4 = (bf16[2,240]{1,0:T(2,128)(2,1)S(1)}, bf16[2,240]{1,0:T(2,128)(2,1)S(1)}, u32[]{:S(2)}, u32[]{:S(2)}) collective-permute-start(bf16[2,240]{1,0:T(2,128)(2,1)S(1)} %pad_maximum_fusion.4), channel_id=1, source_target_pairs={{0,3},{1,2},{2,1},{3,0},{4,7},{5,6},{6,5},{7,4},{8,11},{9,10},{10,... | collective-permute-start | bytes 2888 | tf_op jit(solution)/shard_map/ppermute | solution.py:88
  23.8 15.6 %collective-permute-start.5 = (bf16[240,1280]{1,0:T(8,128)(2,1)S(1)}, bf16[240,1280]{1,0:T(8,128)(2,1)S(1)}, u32[]{:S(2)}, u32[]{:S(2)}) collective-permute-start(bf16[240,1280]{1,0:T(8,128)(2,1)S(1)} %collective-permute-done.refs_2_), channel_id=1, source_target_pairs={{0,2},{1,3},{2,0},{3,1},{4,5},{5,4},{6,7},{7,6},{8,10},{9,11},{10,... | collective-permute-start | bytes 1843208 | tf_op jit(solution)/shard_map/ppermute | solution.py:88
  24.5 14.9 %collective-permute-start.6 = (bf16[240,1280]{1,0:T(8,128)(2,1)S(1)}, bf16[240,1280]{1,0:T(8,128)(2,1)S(1)}, u32[]{:S(2)}, u32[]{:S(2)}) collective-permute-start(bf16[240,1280]{1,0:T(8,128)(2,1)S(1)} %collective-permute-done.refs_2_), channel_id=1, source_target_pairs={{0,4},{1,5},{2,6},{3,7},{4,0},{5,1},{6,2},{7,3},{8,12},{9,13},{10,... | collective-permute-start | bytes 1843208 | tf_op jit(solution)/shard_map/ppermute | solution.py:88
  25.3 14.9 %collective-permute-start.7 = (bf16[240,1280]{1,0:T(8,128)(2,1)S(1)}, bf16[240,1280]{1,0:T(8,128)(2,1)S(1)}, u32[]{:S(2)}, u32[]{:S(2)}) collective-permute-start(bf16[240,1280]{1,0:T(8,128)(2,1)S(1)} %collective-permute-done.1.refs_4_), channel_id=1, source_target_pairs={{0,4},{1,5},{2,6},{3,7},{4,0},{5,1},{6,2},{7,3},{8,12},{9,13},{10,... | collective-permute-start | bytes 1843208 | tf_op jit(solution)/shard_map/ppermute | solution.py:88
  25.3 15.8 %collective-permute-start.8 = (bf16[240,1280]{1,0:T(8,128)(2,1)}, bf16[240,1280]{1,0:T(8,128)(2,1)}, u32[]{:S(2)}, u32[]{:S(2)}) collective-permute-start(bf16[240,1280]{1,0:T(8,128)(2,1)} %dynamic-slice_select_fusion), channel_id=1, source_target_pairs={{0,1},{1,0},{2,3},{3,2},{4,6},{5,7},{6,4},{7,5},{8,9},{9,8},{10,11... | collective-permute-start | bytes 1843208 | tf_op jit(solution)/shard_map/ppermute | solution.py:88
  43.3 10.7 %collective-permute-start.9 = (bf16[240,1280]{1,0:T(8,128)(2,1)S(1)}, bf16[240,1280]{1,0:T(8,128)(2,1)}, u32[]{:S(2)}, u32[]{:S(2)}) collective-permute-start(bf16[240,1280]{1,0:T(8,128)(2,1)S(1)} %collective-permute-done.5.refs_6_), channel_id=1, source_target_pairs={{0,4},{1,5},{2,6},{3,7},{4,0},{5,1},{6,2},{7,3},{8,12},{9,13},{10,... | collective-permute-start | bytes 1843208 | tf_op jit(solution)/shard_map/ppermute | solution.py:88
  43.3 20.1 %collective-permute-start.10 = (bf16[240,1280]{1,0:T(8,128)(2,1)}, bf16[240,1280]{1,0:T(8,128)(2,1)}, u32[]{:S(2)}, u32[]{:S(2)}) collective-permute-start(bf16[240,1280]{1,0:T(8,128)(2,1)} %dynamic-slice_select_fusion), channel_id=1, source_target_pairs={{0,2},{1,3},{2,0},{3,1},{4,5},{5,4},{6,7},{7,6},{8,10},{9,11},{10,... | collective-permute-start | bytes 1843208 | tf_op jit(solution)/shard_map/ppermute | solution.py:88
  43.3 20.0 %collective-permute-start.11 = (bf16[240,1280]{1,0:T(8,128)(2,1)}, bf16[240,1280]{1,0:T(8,128)(2,1)}, u32[]{:S(2)}, u32[]{:S(2)}) collective-permute-start(bf16[240,1280]{1,0:T(8,128)(2,1)} %collective-permute-done.8.refs_10_), channel_id=1, source_target_pairs={{0,8},{1,9},{2,10},{3,11},{4,12},{5,13},{6,14},{7,15},{8,0},{9,1},... | collective-permute-start | bytes 1843208 | tf_op jit(solution)/shard_map/ppermute | solution.py:88
  46.4 17.0 %collective-permute-start.12 = (bf16[320,960]{1,0:T(8,128)(2,1)}, bf16[320,960]{1,0:T(8,128)(2,1)}, u32[]{:S(2)}, u32[]{:S(2)}) collective-permute-start(bf16[320,960]{1,0:T(8,128)(2,1)} %copy.91), channel_id=1, source_target_pairs={{0,1},{1,0},{2,3},{3,2},{4,6},{5,7},{6,4},{7,5},{8,9},{9,8},{10,11... | collective-permute-start | bytes 1843208 | tf_op jit(solution)/shard_map/ppermute | solution.py:88
  63.4 16.4 %collective-permute-start.13 = (bf16[512,640]{1,0:T(8,128)(2,1)S(1)}, bf16[512,640]{1,0:T(8,128)(2,1)S(1)}, u32[]{:S(2)}, u32[]{:S(2)}) collective-permute-start(bf16[512,640]{1,0:T(8,128)(2,1)S(1)} %get-tuple-element.456.refs_0_), channel_id=1, source_target_pairs={{0,1},{1,0},{2,3},{3,2},{4,6},{5,7},{6,4},{7,5},{8,9},{9,8},{10,11... | collective-permute-start | bytes 1966088 | tf_op jit(solution)/shard_map/ppermute | solution.py:88
  63.5 16.4 %collective-permute-start.14 = (bf16[512,640]{1,0:T(8,128)(2,1)S(1)}, bf16[512,640]{1,0:T(8,128)(2,1)S(1)}, u32[]{:S(2)}, u32[]{:S(2)}) collective-permute-start(bf16[512,640]{1,0:T(8,128)(2,1)S(1)} %get-tuple-element.456.refs_0_), channel_id=1, source_target_pairs={{0,2},{1,3},{2,0},{3,1},{4,5},{5,4},{6,7},{7,6},{8,10},{9,11},{10,... | collective-permute-start | bytes 1966088 | tf_op jit(solution)/shard_map/ppermute | solution.py:88
  64.0 15.7 %collective-permute-start.15 = (bf16[240,1280]{1,0:T(8,128)(2,1)}, bf16[240,1280]{1,0:T(8,128)(2,1)S(1)}, u32[]{:S(2)}, u32[]{:S(2)}) collective-permute-start(bf16[240,1280]{1,0:T(8,128)(2,1)} %collective-permute-done.10.refs_14_), channel_id=1, source_target_pairs={{0,8},{1,9},{2,10},{3,11},{4,12},{5,13},{6,14},{7,15},{8,0},{9,1},... | collective-permute-start | bytes 1843208 | tf_op jit(solution)/shard_map/ppermute | solution.py:88
  79.9 10.4 %collective-permute-start.17 = (bf16[240,1280]{1,0:T(8,128)(2,1)}, bf16[240,1280]{1,0:T(8,128)(2,1)S(1)}, u32[]{:S(2)}, u32[]{:S(2)}) collective-permute-start(bf16[240,1280]{1,0:T(8,128)(2,1)} %collective-permute-done.8.refs_10_), channel_id=1, source_target_pairs={{0,2},{1,3},{2,0},{3,1},{4,5},{5,4},{6,7},{7,6},{8,10},{9,11},{10,... | collective-permute-start | bytes 1843208 | tf_op jit(solution)/shard_map/ppermute | solution.py:88
  80.9 16.4 %collective-permute-start.16 = (bf16[512,640]{1,0:T(8,128)(2,1)S(1)}, bf16[512,640]{1,0:T(8,128)(2,1)S(1)}, u32[]{:S(2)}, u32[]{:S(2)}) collective-permute-start(bf16[512,640]{1,0:T(8,128)(2,1)S(1)} %collective-permute-done.13.refs_1_), channel_id=1, source_target_pairs={{0,2},{1,3},{2,0},{3,1},{4,5},{5,4},{6,7},{7,6},{8,10},{9,11},{10,... | collective-permute-start | bytes 1966088 | tf_op jit(solution)/shard_map/ppermute | solution.py:88
  81.9 8.3 %collective-permute-start.18 = (bf16[240,1280]{1,0:T(8,128)(2,1)}, bf16[240,1280]{1,0:T(8,128)(2,1)S(1)}, u32[]{:S(2)}, u32[]{:S(2)}) collective-permute-start(bf16[240,1280]{1,0:T(8,128)(2,1)} %collective-permute-done.8.refs_10_), channel_id=1, source_target_pairs={{0,4},{1,5},{2,6},{3,7},{4,0},{5,1},{6,2},{7,3},{8,12},{9,13},{10,... | collective-permute-start | bytes 1843208 | tf_op jit(solution)/shard_map/ppermute | solution.py:88
  81.9 8.4 %collective-permute-start.19 = (bf16[240,1280]{1,0:T(8,128)(2,1)}, bf16[240,1280]{1,0:T(8,128)(2,1)S(1)}, u32[]{:S(2)}, u32[]{:S(2)}) collective-permute-start(bf16[240,1280]{1,0:T(8,128)(2,1)} %collective-permute-done.10.refs_14_), channel_id=1, source_target_pairs={{0,4},{1,5},{2,6},{3,7},{4,0},{5,1},{6,2},{7,3},{8,12},{9,13},{10,... | collective-permute-start | bytes 1843208 | tf_op jit(solution)/shard_map/ppermute | solution.py:88
  82.4 7.9 %collective-permute-start.20 = (bf16[240,1280]{1,0:T(8,128)(2,1)}, bf16[240,1280]{1,0:T(8,128)(2,1)S(1)}, u32[]{:S(2)}, u32[]{:S(2)}) collective-permute-start(bf16[240,1280]{1,0:T(8,128)(2,1)} %collective-permute-done.11.refs_11_), channel_id=1, source_target_pairs={{0,4},{1,5},{2,6},{3,7},{4,0},{5,1},{6,2},{7,3},{8,12},{9,13},{10,... | collective-permute-start | bytes 1843208 | tf_op jit(solution)/shard_map/ppermute | solution.py:88
  90.3 2.0 collective-permute-start.21
  97.3 23.1 %collective-permute-start.24 = (bf16[240,1280]{1,0:T(8,128)(2,1)S(1)}, bf16[240,1280]{1,0:T(8,128)(2,1)}, u32[]{:S(2)}, u32[]{:S(2)}) collective-permute-start(bf16[240,1280]{1,0:T(8,128)(2,1)S(1)} %collective-permute-done.17.refs_18_), channel_id=1, source_target_pairs={{0,8},{1,9},{2,10},{3,11},{4,12},{5,13},{6,14},{7,15},{8,0},{9,1},... | collective-permute-start | bytes 1843208 | tf_op jit(solution)/shard_map/ppermute | solution.py:88
  98.6 21.7 %collective-permute-start.25 = (bf16[240,1280]{1,0:T(8,128)(2,1)S(1)}, bf16[240,1280]{1,0:T(8,128)(2,1)S(1)}, u32[]{:S(2)}, u32[]{:S(2)}) collective-permute-start(bf16[240,1280]{1,0:T(8,128)(2,1)S(1)} %collective-permute-done.17.refs_18_), channel_id=1, source_target_pairs={{0,4},{1,5},{2,6},{3,7},{4,0},{5,1},{6,2},{7,3},{8,12},{9,13},{10,... | collective-permute-start | bytes 1843208 | tf_op jit(solution)/shard_map/ppermute | solution.py:88
  98.7 21.7 %collective-permute-start.22 = (bf16[320,960]{1,0:T(8,128)(2,1)}, bf16[320,960]{1,0:T(8,128)(2,1)S(1)}, u32[]{:S(2)}, u32[]{:S(2)}) collective-permute-start(bf16[320,960]{1,0:T(8,128)(2,1)} %copy.91), channel_id=1, source_target_pairs={{0,2},{1,3},{2,0},{3,1},{4,5},{5,4},{6,7},{7,6},{8,10},{9,11},{10,... | collective-permute-start | bytes 1843208 | tf_op jit(solution)/shard_map/ppermute | solution.py:88
  99.0 21.3 %collective-permute-start.23 = (bf16[320,960]{1,0:T(8,128)(2,1)}, bf16[320,960]{1,0:T(8,128)(2,1)S(1)}, u32[]{:S(2)}, u32[]{:S(2)}) collective-permute-start(bf16[320,960]{1,0:T(8,128)(2,1)} %collective-permute-done.12.refs_23_), channel_id=1, source_target_pairs={{0,2},{1,3},{2,0},{3,1},{4,5},{5,4},{6,7},{7,6},{8,10},{9,11},{10,... | collective-permute-start | bytes 1843208 | tf_op jit(solution)/shard_map/ppermute | solution.py:88
  120.4 2.9 collective-permute-start.26
  120.5 4.4 %collective-permute-start.27 = (bf16[320,960]{1,0:T(8,128)(2,1)}, bf16[320,960]{1,0:T(8,128)(2,1)S(1)}, u32[]{:S(2)}, u32[]{:S(2)}) collective-permute-start(bf16[320,960]{1,0:T(8,128)(2,1)} %collective-permute-done.12.refs_23_), channel_id=1, source_target_pairs={{0,4},{1,5},{2,6},{3,7},{4,0},{5,1},{6,2},{7,3},{8,12},{9,13},{10,... | collective-permute-start | bytes 1843208 | tf_op jit(solution)/shard_map/ppermute | solution.py:88
  121.3 3.6 collective-permute-start.28
  121.3 4.2 collective-permute-start.29
  121.8 40.0 %collective-permute-start.30 = (bf16[2,960,256]{2,1,0:T(8,128)(2,1)}, bf16[2,960,256]{2,1,0:T(8,128)(2,1)}, u32[]{:S(2)}, u32[]{:S(2)}) collective-permute-start(bf16[2,960,256]{2,1,0:T(8,128)(2,1)} %bitcast.8.x_ref.refs_0_), channel_id=1, source_target_pairs={{0,1},{1,0},{2,3},{3,2},{4,6},{5,7},{6,4},{7,5},{8,9},{9,8},{10,11... | collective-permute-start | bytes 2949128 | tf_op jit(solution)/shard_map/ppermute | solution.py:88
  123.3 38.6 %collective-permute-start.31 = (bf16[2,960,256]{2,1,0:T(8,128)(2,1)}, bf16[2,960,256]{2,1,0:T(8,128)(2,1)S(1)}, u32[]{:S(2)}, u32[]{:S(2)}) collective-permute-start(bf16[2,960,256]{2,1,0:T(8,128)(2,1)} %bitcast.8.x_ref.refs_0_), channel_id=1, source_target_pairs={{0,2},{1,3},{2,0},{3,1},{4,5},{5,4},{6,7},{7,6},{8,10},{9,11},{10,... | collective-permute-start | bytes 2949128 | tf_op jit(solution)/shard_map/ppermute | solution.py:88
  161.9 15.5 %collective-permute-start.32 = (bf16[2,960,256]{2,1,0:T(8,128)(2,1)}, bf16[2,960,256]{2,1,0:T(8,128)(2,1)}, u32[]{:S(2)}, u32[]{:S(2)}) collective-permute-start(bf16[2,960,256]{2,1,0:T(8,128)(2,1)} %collective-permute-done.30.refs_1_), channel_id=1, source_target_pairs={{0,2},{1,3},{2,0},{3,1},{4,5},{5,4},{6,7},{7,6},{8,10},{9,11},{10,... | collective-permute-start | bytes 2949128 | tf_op jit(solution)/shard_map/ppermute | solution.py:88
  177.3 21.3 %collective-permute-start.33 = (bf16[1792,1024]{1,0:T(8,128)(2,1)}, bf16[1792,1024]{1,0:T(8,128)(2,1)}, u32[]{:S(2)}, u32[]{:S(2)}) collective-permute-start(bf16[1792,1024]{1,0:T(8,128)(2,1)} %weight_grad.6), channel_id=1, source_target_pairs={{0,4},{1,5},{2,6},{3,7},{4,0},{5,1},{6,2},{7,3},{8,12},{9,13},{10,... | collective-permute-start | bytes 11010056 | tf_op jit(solution)/shard_map/ppermute | solution.py:88
  198.7 28.4 %collective-permute-start.35 = (bf16[960,1280]{1,0:T(8,128)(2,1)}, bf16[960,1280]{1,0:T(8,128)(2,1)}, u32[]{:S(2)}, u32[]{:S(2)}) collective-permute-start(bf16[960,1280]{1,0:T(8,128)(2,1)} %weight_grad.8), channel_id=1, source_target_pairs={{0,4},{1,5},{2,6},{3,7},{4,0},{5,1},{6,2},{7,3},{8,12},{9,13},{10,... | collective-permute-start | bytes 7372808 | tf_op jit(solution)/shard_map/ppermute | solution.py:88
  199.1 27.9 %collective-permute-start.36 = (bf16[960,1280]{1,0:T(8,128)(2,1)S(1)}, bf16[960,1280]{1,0:T(8,128)(2,1)}, u32[]{:S(2)}, u32[]{:S(2)}) collective-permute-start(bf16[960,1280]{1,0:T(8,128)(2,1)S(1)} %weight_grad.10), channel_id=1, source_target_pairs={{0,4},{1,5},{2,6},{3,7},{4,0},{5,1},{6,2},{7,3},{8,12},{9,13},{10,... | collective-permute-start | bytes 7372808 | tf_op jit(solution)/shard_map/ppermute | solution.py:88
  203.6 23.4 %collective-permute-start.34 = (bf16[896,1024]{1,0:T(8,128)(2,1)}, bf16[896,1024]{1,0:T(8,128)(2,1)S(1)}, u32[]{:S(2)}, u32[]{:S(2)}) collective-permute-start(bf16[896,1024]{1,0:T(8,128)(2,1)} %add_convert_fusion), channel_id=1, source_target_pairs={{0,2},{1,3},{2,0},{3,1},{4,5},{5,4},{6,7},{7,6},{8,10},{9,11},{10,... | collective-permute-start | bytes 5505032 | tf_op jit(solution)/shard_map/ppermute | solution.py:88
  231.1 26.9 %collective-permute-start.38 = (bf16[480,1280]{1,0:T(8,128)(2,1)}, bf16[480,1280]{1,0:T(8,128)(2,1)}, u32[]{:S(2)}, u32[]{:S(2)}) collective-permute-start(bf16[480,1280]{1,0:T(8,128)(2,1)} %add_convert_fusion.2), channel_id=1, source_target_pairs={{0,2},{1,3},{2,0},{3,1},{4,5},{5,4},{6,7},{7,6},{8,10},{9,11},{10,... | collective-permute-start | bytes 3686408 | tf_op jit(solution)/shard_map/ppermute | solution.py:88
  234.1 22.3 %collective-permute-start.37 = (bf16[448,1024]{1,0:T(8,128)(2,1)S(1)}, bf16[448,1024]{1,0:T(8,128)(2,1)S(1)}, u32[]{:S(2)}, u32[]{:S(2)}) collective-permute-start(bf16[448,1024]{1,0:T(8,128)(2,1)S(1)} %add_convert_fusion.6), channel_id=1, source_target_pairs={{0,1},{1,0},{2,3},{3,2},{4,6},{5,7},{6,4},{7,5},{8,9},{9,8},{10,11... | collective-permute-start | bytes 2752520 | tf_op jit(solution)/shard_map/ppermute | solution.py:88
  260.8 25.1 %collective-permute-start.41 = (bf16[480,1280]{1,0:T(8,128)(2,1)}, bf16[480,1280]{1,0:T(8,128)(2,1)}, u32[]{:S(2)}, u32[]{:S(2)}) collective-permute-start(bf16[480,1280]{1,0:T(8,128)(2,1)} %add_convert_fusion.1), channel_id=1, source_target_pairs={{0,2},{1,3},{2,0},{3,1},{4,5},{5,4},{6,7},{7,6},{8,10},{9,11},{10,... | collective-permute-start | bytes 3686408 | tf_op jit(solution)/shard_map/ppermute | solution.py:88
  264.7 21.2 %collective-permute-start.39 = (bf16[448,1024]{1,0:T(8,128)(2,1)}, bf16[448,1024]{1,0:T(8,128)(2,1)}, u32[]{:S(2)}, u32[]{:S(2)}) collective-permute-start(bf16[448,1024]{1,0:T(8,128)(2,1)} %add_convert_fusion.5), channel_id=1, source_target_pairs={{0,8},{1,9},{2,10},{3,11},{4,12},{5,13},{6,14},{7,15},{24,16},{25,... | collective-permute-start | bytes 2752520 | tf_op jit(solution)/shard_map/ppermute | solution.py:88
  271.7 14.0 %collective-permute-start.40 = (bf16[240,1280]{1,0:T(8,128)(2,1)}, bf16[240,1280]{1,0:T(8,128)(2,1)}, u32[]{:S(2)}, u32[]{:S(2)}) collective-permute-start(bf16[240,1280]{1,0:T(8,128)(2,1)} %add_convert_fusion.18), channel_id=1, source_target_pairs={{0,1},{1,0},{2,3},{3,2},{4,6},{5,7},{6,4},{7,5},{8,9},{9,8},{10,11... | collective-permute-start | bytes 1843208 | tf_op jit(solution)/shard_map/ppermute | solution.py:88
  285.9 32.3 %collective-permute-start.42 = (bf16[512,640]{1,0:T(8,128)(2,1)S(1)}, bf16[512,640]{1,0:T(8,128)(2,1)S(1)}, u32[]{:S(2)}, u32[]{:S(2)}) collective-permute-start(bf16[512,640]{1,0:T(8,128)(2,1)S(1)} %copy-done.40), channel_id=1, source_target_pairs={{0,2},{1,3},{2,0},{3,1},{4,5},{5,4},{6,7},{7,6},{8,10},{9,11},{10,... | collective-permute-start | bytes 1966088 | tf_op jit(solution)/shard_map/ppermute | solution.py:88
  286.9 31.3 %collective-permute-start.43 = (bf16[512,640]{1,0:T(8,128)(2,1)}, bf16[512,640]{1,0:T(8,128)(2,1)S(1)}, u32[]{:S(2)}, u32[]{:S(2)}) collective-permute-start(bf16[512,640]{1,0:T(8,128)(2,1)} %copy-done.41), channel_id=1, source_target_pairs={{0,2},{1,3},{2,0},{3,1},{4,5},{5,4},{6,7},{7,6},{8,10},{9,11},{10,... | collective-permute-start | bytes 1966088 | tf_op jit(solution)/shard_map/ppermute | solution.py:88
  287.9 30.3 %collective-permute-start.45 = (bf16[512,1664]{1,0:T(8,128)(2,1)}, bf16[512,1664]{1,0:T(8,128)(2,1)S(1)}, u32[]{:S(2)}, u32[]{:S(2)}) collective-permute-start(bf16[512,1664]{1,0:T(8,128)(2,1)} %get-tuple-element.507), channel_id=1, source_target_pairs={{0,4},{1,5},{2,6},{3,7},{4,0},{5,1},{6,2},{7,3},{8,12},{9,13},{10,... | collective-permute-start | bytes 5111816 | tf_op jit(solution)/shard_map/ppermute | solution.py:88
  289.9 18.2 %collective-permute-start.46 = (bf16[240,1280]{1,0:T(8,128)(2,1)S(1)}, bf16[240,1280]{1,0:T(8,128)(2,1)S(1)}, u32[]{:S(2)}, u32[]{:S(2)}) collective-permute-start(bf16[240,1280]{1,0:T(8,128)(2,1)S(1)} %add_convert_fusion.17), channel_id=1, source_target_pairs={{0,8},{1,9},{2,10},{3,11},{4,12},{5,13},{6,14},{7,15},{24,16},{25,... | collective-permute-start | bytes 1843208 | tf_op jit(solution)/shard_map/ppermute | solution.py:88
  296.1 22.1 %collective-permute-start.44 = (bf16[448,1024]{1,0:T(8,128)(2,1)S(1)}, bf16[448,1024]{1,0:T(8,128)(2,1)S(1)}, u32[]{:S(2)}, u32[]{:S(2)}) collective-permute-start(bf16[448,1024]{1,0:T(8,128)(2,1)S(1)} %add_convert_fusion.4), channel_id=1, source_target_pairs={{8,16},{9,17},{10,18},{11,19},{12,20},{13,21},{14,22},{15,23},{16,... | collective-permute-start | bytes 2752520 | tf_op jit(solution)/shard_map/ppermute | solution.py:88
  308.0 10.1 %collective-permute-start.47 = (bf16[240,1280]{1,0:T(8,128)(2,1)S(1)}, bf16[240,1280]{1,0:T(8,128)(2,1)S(1)}, u32[]{:S(2)}, u32[]{:S(2)}) collective-permute-start(bf16[240,1280]{1,0:T(8,128)(2,1)S(1)} %add_convert_fusion.16), channel_id=1, source_target_pairs={{0,1},{1,0},{2,3},{3,2},{4,6},{5,7},{6,4},{7,5},{8,9},{9,8},{10,11... | collective-permute-start | bytes 1843208 | tf_op jit(solution)/shard_map/ppermute | solution.py:88
  320.2 28.8 %collective-permute-start.48 = (bf16[512,640]{1,0:T(8,128)(2,1)}, bf16[512,640]{1,0:T(8,128)(2,1)}, u32[]{:S(2)}, u32[]{:S(2)}) collective-permute-start(bf16[512,640]{1,0:T(8,128)(2,1)} %add_convert_fusion.10), channel_id=1, source_target_pairs={{0,1},{1,0},{2,3},{3,2},{4,6},{5,7},{6,4},{7,5},{8,9},{9,8},{10,11... | collective-permute-start | bytes 1966088 | tf_op jit(solution)/shard_map/ppermute | solution.py:88
  321.7 27.2 %collective-permute-start.49 = (bf16[448,1024]{1,0:T(8,128)(2,1)S(1)}, bf16[448,1024]{1,0:T(8,128)(2,1)}, u32[]{:S(2)}, u32[]{:S(2)}) collective-permute-start(bf16[448,1024]{1,0:T(8,128)(2,1)S(1)} %add_convert_fusion.3), channel_id=1, source_target_pairs={{8,0},{9,1},{10,2},{11,3},{12,4},{13,5},{14,6},{15,7},{16,24},{17,... | collective-permute-start | bytes 2752520 | tf_op jit(solution)/shard_map/ppermute | solution.py:88
  324.2 24.8 %collective-permute-start.50 = (bf16[256,1664]{1,0:T(8,128)(2,1)}, bf16[256,1664]{1,0:T(8,128)(2,1)}, u32[]{:S(2)}, u32[]{:S(2)}) collective-permute-start(bf16[256,1664]{1,0:T(8,128)(2,1)} %add_convert_fusion.7), channel_id=1, source_target_pairs={{0,2},{1,3},{2,0},{3,1},{4,5},{5,4},{6,7},{7,6},{8,10},{9,11},{10,... | collective-permute-start | bytes 2555912 | tf_op jit(solution)/shard_map/ppermute | solution.py:88
  326.0 11.6 %collective-permute-start.51 = (bf16[240,1280]{1,0:T(8,128)(2,1)}, bf16[240,1280]{1,0:T(8,128)(2,1)}, u32[]{:S(2)}, u32[]{:S(2)}) collective-permute-start(bf16[240,1280]{1,0:T(8,128)(2,1)} %add_convert_fusion.15), channel_id=1, source_target_pairs={{8,16},{9,17},{10,18},{11,19},{12,20},{13,21},{14,22},{15,23},{16,... | collective-permute-start | bytes 1843208 | tf_op jit(solution)/shard_map/ppermute | solution.py:88
  329.9 19.1 %collective-permute-start.52 = (bf16[240,1280]{1,0:T(8,128)(2,1)}, bf16[240,1280]{1,0:T(8,128)(2,1)S(1)}, u32[]{:S(2)}, u32[]{:S(2)}) collective-permute-start(bf16[240,1280]{1,0:T(8,128)(2,1)} %add_convert_fusion.14), channel_id=1, source_target_pairs={{0,8},{1,9},{2,10},{3,11},{4,12},{5,13},{6,14},{7,15},{24,16},{25,... | collective-permute-start | bytes 1843208 | tf_op jit(solution)/shard_map/ppermute | solution.py:88
  350.4 19.8 %collective-permute-start.53 = (bf16[448,1024]{1,0:T(8,128)(2,1)S(1)}, bf16[448,1024]{1,0:T(8,128)(2,1)S(1)}, u32[]{:S(2)}, u32[]{:S(2)}) collective-permute-start(bf16[448,1024]{1,0:T(8,128)(2,1)S(1)} %broadcast_select_fusion), channel_id=1, source_target_pairs={{0,4},{1,5},{2,6},{3,7},{4,0},{5,1},{6,2},{7,3},{8,12},{9,13},{10,... | collective-permute-start | bytes 2752520 | tf_op jit(solution)/shard_map/ppermute | solution.py:88
  352.0 18.2 %collective-permute-start.55 = (bf16[240,1280]{1,0:T(8,128)(2,1)S(1)}, bf16[240,1280]{1,0:T(8,128)(2,1)S(1)}, u32[]{:S(2)}, u32[]{:S(2)}) collective-permute-start(bf16[240,1280]{1,0:T(8,128)(2,1)S(1)} %add_convert_fusion.13), channel_id=1, source_target_pairs={{8,0},{9,1},{10,2},{11,3},{12,4},{13,5},{14,6},{15,7},{16,24},{17,... | collective-permute-start | bytes 1843208 | tf_op jit(solution)/shard_map/ppermute | solution.py:88
  354.7 15.5 %collective-permute-start.56 = (bf16[240,1280]{1,0:T(8,128)(2,1)S(1)}, bf16[240,1280]{1,0:T(8,128)(2,1)S(1)}, u32[]{:S(2)}, u32[]{:S(2)}) collective-permute-start(bf16[240,1280]{1,0:T(8,128)(2,1)S(1)} %add_convert_fusion.12), channel_id=1, source_target_pairs={{8,16},{9,17},{10,18},{11,19},{12,20},{13,21},{14,22},{15,23},{16,... | collective-permute-start | bytes 1843208 | tf_op jit(solution)/shard_map/ppermute | solution.py:88
  357.0 11.8 %collective-permute-start.54 = (bf16[128,1664]{1,0:T(8,128)(2,1)S(1)}, bf16[128,1664]{1,0:T(8,128)(2,1)S(1)}, u32[]{:S(2)}, u32[]{:S(2)}) collective-permute-start(bf16[128,1664]{1,0:T(8,128)(2,1)S(1)} %add_convert_fusion.22), channel_id=1, source_target_pairs={{0,1},{1,0},{2,3},{3,2},{4,6},{5,7},{6,4},{7,5},{8,9},{9,8},{10,11... | collective-permute-start | bytes 1277960 | tf_op jit(solution)/shard_map/ppermute | solution.py:88
  370.3 19.4 %collective-permute-start.58 = (bf16[240,1280]{1,0:T(8,128)(2,1)S(1)}, bf16[240,1280]{1,0:T(8,128)(2,1)S(1)}, u32[]{:S(2)}, u32[]{:S(2)}) collective-permute-start(bf16[240,1280]{1,0:T(8,128)(2,1)S(1)} %broadcast_select_fusion.4), channel_id=1, source_target_pairs={{0,4},{1,5},{2,6},{3,7},{4,0},{5,1},{6,2},{7,3},{8,12},{9,13},{10,... | collective-permute-start | bytes 1843208 | tf_op jit(solution)/shard_map/ppermute | solution.py:88
  370.5 20.7 %collective-permute-start.59 = (bf16[240,1280]{1,0:T(8,128)(2,1)S(1)}, bf16[240,1280]{1,0:T(8,128)(2,1)S(1)}, u32[]{:S(2)}, u32[]{:S(2)}) collective-permute-start(bf16[240,1280]{1,0:T(8,128)(2,1)S(1)} %add_convert_fusion.11), channel_id=1, source_target_pairs={{8,0},{9,1},{10,2},{11,3},{12,4},{13,5},{14,6},{15,7},{16,24},{17,... | collective-permute-start | bytes 1843208 | tf_op jit(solution)/shard_map/ppermute | solution.py:88
  373.1 16.6 %collective-permute-start.57 = (bf16[128,1664]{1,0:T(8,128)(2,1)S(1)}, bf16[128,1664]{1,0:T(8,128)(2,1)S(1)}, u32[]{:S(2)}, u32[]{:S(2)}) collective-permute-start(bf16[128,1664]{1,0:T(8,128)(2,1)S(1)} %add_convert_fusion.21), channel_id=1, source_target_pairs={{0,8},{1,9},{2,10},{3,11},{4,12},{5,13},{6,14},{7,15},{24,16},{25,... | collective-permute-start | bytes 1277960 | tf_op jit(solution)/shard_map/ppermute | solution.py:88
  391.3 2.1 collective-permute-start.61
  391.5 0.7 collective-permute-start.60
  393.5 24.1 %collective-permute-start.62 = (bf16[128,1664]{1,0:T(8,128)(2,1)S(1)}, bf16[128,1664]{1,0:T(8,128)(2,1)S(1)}, u32[]{:S(2)}, u32[]{:S(2)}) collective-permute-start(bf16[128,1664]{1,0:T(8,128)(2,1)S(1)} %add_convert_fusion.19), channel_id=1, source_target_pairs={{8,0},{9,1},{10,2},{11,3},{12,4},{13,5},{14,6},{15,7},{16,24},{17,... | collective-permute-start | bytes 1277960 | tf_op jit(solution)/shard_map/ppermute | solution.py:88
  417.7 1.8 collective-permute-start.63
  (86 other events, 856.0 us)

commit v6 on v5

--- a/solution.py
+++ b/solution.py
@@ -5,6 +5,7 @@
 import jax.numpy as jnp
 from jax import lax
 from jax.experimental import pallas as pl
+from jax.experimental.layout import Layout, with_layout_constraint
 from jax.experimental.pallas import tpu as pltpu
 from jax.sharding import PartitionSpec as P
 
@@ -130,12 +131,14 @@
         plan.have[name] = (value, other)
 
     def collect(self, plan, name):
-        pieces = plan.have[name + ".pieces"]
-        for i in reversed(range(self.bits)):
-            keep = 1 << i
-            got = yield [self.step(pieces[t + keep], i) for t in range(keep)]
-            pieces = [total([pieces[t], got[t]]) for t in range(keep)]
-        plan.have[name] = pieces[0]
+        low, high = plan.have[name + ".pieces"]
+        got = yield self.step(high, self.bits - 1)
+        sums = [low, got]
+        for i in reversed(range(self.bits - 1)):
+            block = sums[0].shape[0] // 2
+            got = yield self.step(total([part[block:] for part in sums]), i)
+            sums = [part[:block] for part in sums] + [got]
+        plan.have[name] = total(sums)[0]
 
     def beside(self, value):
         return self.move(value, lambda r, s: (r ^ 2, s))
@@ -412,71 +415,110 @@
         target[t * rows : (t + 1) * rows, :] = source[pl.ds(start, rows), :]
 
 
-def weight_grad_kernel(parts, count, starts_ref, *refs):
+def rows_grad_kernel(parts, count, starts_ref, *refs):
     operands = refs[: 2 * len(parts)]
-    out_ref = refs[2 * len(parts)]
-    ordered = refs[2 * len(parts) + 1 :]
+    outs = refs[2 * len(parts) : 2 * len(parts) + 2]
+    ordered = refs[2 * len(parts) + 2 :]
     block = sum(parts)
+    for o, out_ref in enumerate(outs):
+        at = 0
+        for i, rows in enumerate(parts):
+            pick_rows(operands[2 * i], starts_ref, (o * len(parts) + i) * count, rows, count, ordered[i])
+            made = nn(ordered[i][...], operands[2 * i + 1][...]).astype(BF)
+            columns = made.shape[1]
+            for t in range(count):
+                place = slice(t * block + at, t * block + at + rows)
+                out_ref[place, :columns] = made[t * rows : (t + 1) * rows]
+                if columns < out_ref.shape[1]:
+                    out_ref[place, columns:] = jnp.zeros((rows, out_ref.shape[1] - columns), BF)
+            at += rows
+
+
+def rows_grad(terms):
+    count = len(terms[0][3])
+    parts = [term[2] for term in terms]
+    block, columns = sum(parts), terms[0][1].shape[1]
+    wide = rounded_up(columns)
+    if any(rows % 16 for rows in parts) or any(term[0].shape[0] // count % 16 for term in terms):
+        outs = []
+        for o in (3, 4):
+            made = []
+            for term in terms:
+                grad = jnp.pad(nn(term[0], term[1]).astype(BF), ((0, 0), (0, wide - columns)))
+                made.append([lax.dynamic_slice_in_dim(grad, start, term[2], 0) for start in term[o]])
+            outs.append(jnp.concatenate([part for group in zip(*made) for part in group], axis=0))
+        return outs
+    args = [operand for term in terms for operand in term[:2]]
+    out = jax.ShapeDtypeStruct((count * block, wide), BF)
+    flops = sum(4 * left.shape[1] * rows * count * columns for left, _, rows, _, _ in terms)
+    return pl.pallas_call(
+        functools.partial(rows_grad_kernel, parts, count),
+        name="rows_grad",
+        in_specs=[IN_SMEM] + [IN_VMEM] * len(args),
+        out_specs=(IN_VMEM,) * 2,
+        out_shape=(out, out),
+        scratch_shapes=[pltpu.VMEM((count * rows, terms[0][0].shape[1]), BF) for rows in parts],
+        cost_estimate=cost(flops, 0, out, out, *args),
+        compiler_params=pltpu.CompilerParams(vmem_limit_bytes=VMEM_LIMIT),
+    )(numbers([start for o in (3, 4) for term in terms for start in term[o]]), *args)
+
+
+def wide_grad_kernel(cuts, count, rows, info_ref, left_ref, given_ref, kept_ref, *refs):
+    outs, ordered = refs[: 2 * len(cuts)], refs[2 * len(cuts)]
 
     @pl.when(pl.program_id(0) == 0)
     def _():
-        for i, rows in enumerate(parts):
-            pick_rows(operands[2 * i], starts_ref, 1 + i * count, rows, count, ordered[i])
-
-    at = 0
-    for i, rows in enumerate(parts):
-        made = nn(ordered[i][...], operands[2 * i + 1][...]).astype(BF)
-        columns = made.shape[1]
-        for t in range(count):
-            place = slice(t * block + at, t * block + at + rows)
-            out_ref[place, :columns] = made[t * rows : (t + 1) * rows]
-            if columns < out_ref.shape[1]:
-                out_ref[place, columns:] = jnp.zeros((rows, out_ref.shape[1] - columns), BF)
-        at += rows
-
-
-def weight_grad(terms, column=0, columns=None, choice=0):
-    count = len(terms[0][3])
-    parts = [term[2] for term in terms]
-    block = sum(parts)
-    tokens = terms[0][0].shape[1]
-    columns = columns or terms[0][1].shape[-1]
-    wide = rounded_up(columns)
-    if any(rows % 16 for rows in parts) or any(term[0].shape[0] // count % 16 for term in terms):
+        at = 0
+        for o in range(2):
+            first = 0
+            for cut in cuts:
+                for t in range(count):
+                    start = pl.multiple_of(info_ref[2 + o * count + t] + first, 16)
+                    ordered[at : at + cut, :] = left_ref[pl.ds(start, cut), :]
+                    at += cut
+                first += cut
+
+    for o, right_ref in enumerate((given_ref, kept_ref)):
+        made = nn(ordered[o * count * rows : (o + 1) * count * rows, :], right_ref[...]).astype(BF)
+        at = 0
+        for c, cut in enumerate(cuts):
+            outs[o * len(cuts) + c][...] = made[at : at + count * cut]
+            at += count * cut
+
+
+def wide_grad(left, rights, rows, cuts, given, kept, core):
+    count, (_, tokens, columns) = len(given), rights.shape
+    outs = tuple(jax.ShapeDtypeStruct((count * cut, columns), BF) for cut in cuts) * 2
+    if rows % 16 or any(cut % 16 for cut in cuts):
         made = []
-        for left, right, rows, starts in terms:
-            right = right if right.ndim == 2 else lax.dynamic_index_in_dim(right, choice, 0, keepdims=False)
-            grad = nn(left, right[:, column * columns : (column + 1) * columns]).astype(BF)
-            grad = jnp.pad(grad, ((0, 0), (0, wide - columns)))
-            made.append([lax.dynamic_slice_in_dim(grad, start, rows, 0) for start in starts])
-        return jnp.concatenate([part for group in zip(*made) for part in group], axis=0)
-    in_specs, args, flops = [], [], 0
-    tile = 256 if columns % 256 == 0 else columns
-    skip = column * (columns // tile)
-    for left, right, rows, starts in terms:
-        in_specs.append(pl.BlockSpec(left.shape, lambda n, info: (0, 0)))
-        if right.ndim == 2:
-            in_specs.append(pl.BlockSpec((tokens, tile), lambda n, info: (0, skip + n)))
-        else:
-            in_specs.append(pl.BlockSpec((None, tokens, tile), lambda n, info: (info[0], 0, skip + n)))
-        args += [left, right]
-        flops += 2 * tokens * rows * count * columns
-    out = jax.ShapeDtypeStruct((count * block, wide), BF)
-    info = numbers([choice] + [start for term in terms for start in term[3]])
+        for starts, choice in ((given, 1 - core), (kept, core)):
+            grad = nn(left, lax.dynamic_index_in_dim(rights, choice, 0, keepdims=False)).astype(BF)
+            first = 0
+            for cut in cuts:
+                made.append(
+                    jnp.concatenate([lax.dynamic_slice_in_dim(grad, start + first, cut, 0) for start in starts])
+                )
+                first += cut
+        return made
+    tile = 512 if columns % 512 == 0 else columns
     return pl.pallas_call(
-        functools.partial(weight_grad_kernel, parts, count),
+        functools.partial(wide_grad_kernel, cuts, count, rows),
         grid_spec=pltpu.PrefetchScalarGridSpec(
             num_scalar_prefetch=1,
             grid=(columns // tile,),
-            in_specs=in_specs,
-            out_specs=pl.BlockSpec((count * block, rounded_up(tile)), lambda n, info: (0, n)),
-            scratch_shapes=[pltpu.VMEM((count * rows, tokens), BF) for rows in parts],
+            in_specs=[
+                pl.BlockSpec(left.shape, lambda n, info: (0, 0)),
+                pl.BlockSpec((None, tokens, tile), lambda n, info: (info[0], 0, n)),
+                pl.BlockSpec((None, tokens, tile), lambda n, info: (info[1], 0, n)),
+            ],
+            out_specs=tuple(pl.BlockSpec((out.shape[0], tile), lambda n, info: (0, n)) for out in outs),
+            scratch_shapes=[pltpu.VMEM((2 * count * rows, tokens), BF)],
         ),
-        out_shape=out,
-        name="weight_grad",
-        cost_estimate=cost(flops, 0, out, *args),
+        out_shape=outs,
+        name="wide_grad",
+        cost_estimate=cost(4 * tokens * rows * count * columns, 0, left, rights, *outs),
         compiler_params=pltpu.CompilerParams(vmem_limit_bytes=VMEM_LIMIT),
-    )(info, *args)
+    )(numbers([1 - core, core] + given + kept), left, rights, rights)
 
 
 def turn_keys(source, target, at, cosine, sine):
@@ -489,8 +531,9 @@
 
 
 def attention_grad_kernel(shards, half, starts_ref, gain_ref, cos_ref, sin_ref, dq_ref, *refs):
-    xs, dkvs = refs[:shards], refs[shards : 2 * shards]
-    outs, (act, dkv, ordered) = refs[2 * shards : 2 * shards + 2], refs[2 * shards + 2 :]
+    xs, halves = refs[:shards], refs[shards : shards + 2]
+    dkvs = [ref.at[t] for ref in halves for t in range(shards // 2)]
+    outs, (act, dkv, ordered) = refs[shards + 2 : shards + 4], refs[shards + 4 :]
     micro, width, rows = xs[0].shape
     tokens = micro * rows
     for t in range(shards):
@@ -520,7 +563,7 @@
         xs = jnp.concatenate([x[m] for x in x_all for m in range(micro)], axis=1).astype(F32)
         act = xs * lax.rsqrt(jnp.mean(xs * xs, axis=0, keepdims=True) + EPS) * gain
         act = act.astype(BF)
-        dkv = jnp.concatenate(dkv_all, axis=0)
+        dkv = jnp.concatenate(dkv_all, axis=0).reshape(every, 2 * KV_WIDTH)
         keys = dkv[:, :KV_WIDTH].astype(F32).reshape(every, -1, 2, HALF_HEAD)
         c, s = cosine[:, None, :HALF_HEAD], sine[:, None, HALF_HEAD:HEAD_SIZE]
         first, second = keys[:, :, 0], keys[:, :, 1]
@@ -535,7 +578,7 @@
     return pl.pallas_call(
         functools.partial(attention_grad_kernel, shards, half),
         name="attention_grad",
-        in_specs=[IN_SMEM] + [IN_VMEM] * (4 + 2 * shards),
+        in_specs=[IN_SMEM] + [IN_VMEM] * (6 + shards),
         out_specs=(IN_VMEM,) * 2,
         out_shape=(out, out),
         scratch_shapes=[
@@ -643,8 +686,8 @@
 def attend_back_kernel(shards, seg_rows, q_ref, *refs):
     kv = refs[:shards]
     bias_ref, o_ref, do_ref, lse_ref, cos_ref, sin_ref = refs[shards : shards + 6]
-    dq_ref = refs[-1 - shards]
-    dkv = refs[-shards:]
+    dq_ref, low_ref, high_ref = refs[-3:]
+    dkv = [ref.at[t] for ref in (low_ref, high_ref) for t in range(shards // 2)]
     rows = q_ref.shape[0]
     i = lax.broadcasted_iota(jnp.int32, (rows, rows), 1)
     j = lax.broadcasted_iota(jnp.int32, (rows, rows), 0)
@@ -717,7 +760,8 @@
     here = lambda w: pl.BlockSpec((rows, w), lambda i: (m, 0))
     turned = pl.BlockSpec((HALF_HEAD, rows), lambda i: (0, m))
     outs = (jax.ShapeDtypeStruct((tokens, width), BF),)
-    outs += (jax.ShapeDtypeStruct((tokens, 2 * KV_WIDTH), BF),) * shards
+    outs += (jax.ShapeDtypeStruct((shards // 2, tokens, 2 * KV_WIDTH), BF),) * 2
+    pieces = pl.BlockSpec((shards // 2, rows, 2 * KV_WIDTH), lambda i: (0, m, 0))
     pairs = rows * rows * shards * QUERY_HEADS
     return pl.pallas_call(
         functools.partial(attend_back_kernel, shards, seg_rows),
@@ -728,7 +772,7 @@
         + [pl.BlockSpec((None,) + bias.shape[1:], lambda i: (m, 0, 0))]
         + [here(width), here(width), here(128), turned, turned]
         + [pl.BlockSpec(memory_space=pl.ANY)] * len(earlier),
-        out_specs=(here(width),) + (here(2 * KV_WIDTH),) * shards,
+        out_specs=(here(width), pieces, pieces),
         out_shape=outs,
         input_output_aliases={shards + 7 + i: i for i in range(len(earlier))},
         cost_estimate=cost(40 * HEAD_SIZE * pairs, pairs, q),
@@ -773,6 +817,7 @@
     down_mine = lax.dynamic_slice_in_dim(w_down, links.core * down_cut, down_cut, 0)
 
     attn_near = links.near(attn_mine)
+    pair_near = {1: links.step(pair_mine, 0)}
     gain_pieces = links.small_pieces(jnp.stack([norm_first, norm_second]))
     attn_mine, attn_near, gain_pieces, pair_mine, down_mine = meet(
         attn_mine, attn_near, gain_pieces, pair_mine, down_mine
@@ -781,7 +826,8 @@
     gains = links.in_order(gain_pieces).astype(F32)
     attn_all = links.far(attn_mine, attn_near)
     attn_swapped = {t: links.swap(attn_near[t]) for t in attn_near}
-    pair_near = {1: links.step(pair_mine, 0)}
+    pair_later = {1 << i: links.step(pair_mine, i) for i in range(1, links.bits)}
+    own_down = with_layout_constraint(w_down, Layout(major_to_minor=(0, 1)))
     parents = parent_ids[:, 0]
     seg = jnp.arange(segs)
     after_parent = jnp.concatenate([parents[:, 1:], jnp.full((micro, 1), -1, parents.dtype)], axis=1)
@@ -809,8 +855,8 @@
     bias = jnp.where(open_key, 0.0, CLOSED)
     bias = jnp.pad(bias, ((0, 0), (0, 8 - shards), (0, 0)))
 
-    attn_all, attn_swapped, pair_mine, pair_near, gains, cosine, sine, bias, down_mine = meet(
-        attn_all, attn_swapped, pair_mine, pair_near, gains, cosine, sine, bias, down_mine
+    attn_all, attn_swapped, pair_mine, pair_near, gains, cosine, sine, bias, down_mine, own_down = meet(
+        attn_all, attn_swapped, pair_mine, pair_near, gains, cosine, sine, bias, down_mine, own_down
     )
 
     for t in range(1, shards):
@@ -829,27 +875,28 @@
             (pair_place(1 - links.core, links.hops[links.twin(t)]), 0),
         ]
     attention_got = joined(pieces, starts, (2 * width, left.shape[1]))
-    pair_near |= {1 << i: links.step(pair_mine, i) for i in range(1, links.bits)}
+    pair_near |= pair_later
     pair_beside = {1: links.beside(pair_near[1])}
     down_near = {1: links.step(down_mine, 0)}
     queries, kv = project(inputs, gains, cosine, sine, *attention_got)
-    queries, kv, pair_mine, pair_near, pair_beside, down_mine, down_near = meet(
-        queries, kv, pair_mine, pair_near, pair_beside, down_mine, down_near
-    )
+    queries, kv, pair_mine, pair_near = meet(queries, kv, pair_mine, pair_near)
 
     kv_near = links.near(kv)
-    pair_beside |= {t: links.beside(pair_near[t]) for t in pair_near if t > 1}
-    kv_near, kv, pair_beside, pair_near, pair_mine = meet(kv_near, kv, pair_beside, pair_near, pair_mine)
+    pair_all = links.far(pair_mine, pair_near)
+    pair_further = {t: links.beside(pair_near[t]) for t in pair_near if t > 1}
+    kv_near, kv, pair_beside, pair_near, down_near, down_mine = meet(
+        kv_near, kv, pair_beside, pair_near, down_near, down_mine
+    )
 
     kv_all = links.far(kv, kv_near)
-    pair_all = links.far(pair_mine, pair_near)
+    down_near |= {1 << i: links.step(down_mine, i) for i in range(1, links.bits)}
     pair_swapped = {t: links.swap(pair_near[t]) for t in pair_near}
     pair_crossed = {t: links.swap(pair_beside[t]) for t in pair_beside}
-    kv_all, pair_all, pair_swapped, pair_crossed, pair_beside, down_mine, down_near = meet(
-        kv_all, pair_all, pair_swapped, pair_crossed, pair_beside, down_mine, down_near
-    )
-
-    down_near |= {1 << i: links.step(down_mine, i) for i in range(1, links.bits)}
+    pair_beside |= pair_further
+    kv_all, pair_all, pair_swapped, pair_crossed, pair_beside = meet(
+        kv_all, pair_all, pair_swapped, pair_crossed, pair_beside
+    )
+
     down_all = links.far(down_mine, down_near)
     pair_beside |= {t: links.beside(pair_all[t]) for t in range(1, shards) if t not in pair_beside}
     attn, lse = attend(micro, seg_rows, queries, kv_all, bias)
@@ -870,7 +917,7 @@
             starts += [(row, side * pair_cut), (row, (1 - side) * pair_cut)]
     pair_got = joined(pieces, starts, (2 * width, hidden))
     own = w_down.shape[0]
-    pieces, starts = [w_down], [(links.shard * own, 0)]
+    pieces, starts = [own_down], [(links.shard * own, 0)]
     for t in range(1, shards):
         pieces += [down_all[t], down_swapped[t]]
         starts += [
@@ -895,25 +942,24 @@
     wide_kept, wide_given = links.order(shard_rows, 0, 0)
     some_kept, some_given = links.order(shard_rows, output_mine, output_theirs)
 
-    def rows_grads(down, output):
-        inner, dy, attn_t, low = have("inner", "dy", "attn_t", "d_resid_low")
-        return weight_grad(((inner, dy, down_half, down), (attn_t, low, output_half, output)))
-
-    def wide_grads(chunk, starts, choice):
-        act, slopes = have("act", "slopes")
-        return weight_grad(((act, slopes, shard_rows, starts),), chunk, hidden // 2, choice)
-
+    inner, dy, attn_t, low = have("inner", "dy", "attn_t", "d_resid_low")
     plan.have["x_all"] = links.far(inputs, plan.have.pop("x_near"))
-    plan.have["rows.given"] = rows_grads(down_given, some_given)
-    plan.have["rows.kept"] = rows_grads(down_kept, some_kept)
+    plan.have["rows.given"], plan.have["rows.kept"] = rows_grad(
+        (
+            (inner, dy, down_half, down_given, down_kept),
+            (attn_t, low, output_half, some_given, some_kept),
+        )
+    )
     plan.close()
 
     for name in ("rows", "wide0", "wide1", "some"):
         plan.start(name, links.reduce(plan, name))
     plan.advance("rows")
-    for chunk, name in enumerate(("wide0", "wide1")):
-        plan.have[name + ".given"] = wide_grads(chunk, wide_given, 1 - links.core)
-        plan.have[name + ".kept"] = wide_grads(chunk, wide_kept, links.core)
+    cuts = (-(-shard_rows // 32) * 16, shard_rows - -(-shard_rows // 32) * 16)
+    act, slopes = have("act", "slopes")
+    made = wide_grad(act, slopes, shard_rows, cuts, wide_given, wide_kept, links.core)
+    names = [name + part for part in (".given", ".kept") for name in ("wide0", "wide1")]
+    plan.have |= dict(zip(names, made))
     plan.close()
 
     made = ()
@@ -937,50 +983,50 @@
     plan.have["some.given"], plan.have["some.kept"] = given, kept
     plan.close()
 
+    def gain_grad(gain, *pairs):
+        sums = sum(jnp.sum(weight.astype(F32) * grad, axis=1) for weight, grad in pairs)
+        return sums / gain.astype(F32)
+
+    def settle():
+        have, done = plan.have, plan.have.setdefault("done", {})
+        if "dkv" in have and "d_input" not in done:
+            done["d_input"] = finish(
+                inputs, have["d_queries"], have["dkv"], have["d_resid"], gains, cosine, sine, *attention_got
+            )
+        if "rows" in have and "down" not in done:
+            value, other = have["rows"]
+            done["down"] = links.finish_rows(value[:down_half, :width], other[:down_half, :width], own)
+            done["output"] = links.finish_rows(value[down_half:, :width], other[down_half:, :width], shard_rows)
+        if "wide0" in have and "wide1" in have and "gate" not in done:
+            halves = [links.finish_pair(*have[name]) for name in ("wide0", "wide1")]
+            done["gate"], done["upper"] = (jnp.concatenate(parts, axis=0) for parts in zip(*halves))
+            done["gain_two"] = gain_grad(norm_second, (w_gate, done["gate"]), (w_up, done["upper"]))
+        if "some" in have and "query" not in done:
+            grad = links.finish_rows(*have["some"], shard_rows)
+            first = rounded_up(width)
+            done["query"], done["key"] = grad[:, :width], grad[:, first : first + KV_WIDTH]
+            done["value"] = grad[:, first + KV_WIDTH :]
+            done["gain_one"] = gain_grad(
+                norm_first,
+                (w_query, done["query"]),
+                (key_weight, done["key"]),
+                (value_weight, done["value"]),
+            )
+
     order = [("rows", "wide0", "wide1", "some", "dkv")] * 5 + [("wide1", "some")]
     while plan.tasks:
         plan.advance(*(order.pop(0) if order else tuple(plan.tasks)))
-        if "dkv" in plan.have and "d_input" not in plan.have:
-            plan.have["d_input"] = finish(
-                inputs, *have("d_queries", "dkv", "d_resid"), gains, cosine, sine, *attention_got
-            )
-        plan.close()
-
-    def owned(name, rows_of):
-        value, other = plan.have[name]
-        return links.finish_rows(value, other, rows_of)
-
-    rows_own, rows_other = plan.have["rows"]
-    grad_down = links.finish_rows(rows_own[:down_half, :width], rows_other[:down_half, :width], own)
-    grad_output = links.finish_rows(rows_own[down_half:, :width], rows_other[down_half:, :width], shard_rows)
-    grad_gate, grad_upper = (
-        jnp.concatenate(parts, axis=1)
-        for parts in zip(*(links.finish_pair(*plan.have[name]) for name in ("wide0", "wide1")))
-    )
-    some = owned("some", shard_rows)
-    first = rounded_up(width)
-    grad_query, grad_key, grad_value = (
-        some[:, :width],
-        some[:, first : first + KV_WIDTH],
-        some[:, first + KV_WIDTH :],
-    )
-
-    def gain_grad(gain, *pairs):
-        sums = sum(jnp.sum(weight.astype(F32) * grad, axis=1) for weight, grad in pairs)
-        return sums / gain.astype(F32)
-
+        settle()
+        if plan.tasks:
+            plan.close()
+
+    done = plan.have["done"]
     return (
         plan.have["out"].swapaxes(1, 2),
-        plan.have["d_input"].swapaxes(1, 2),
-        grad_query,
-        grad_key,
-        grad_value,
-        grad_output,
-        grad_gate,
-        grad_upper,
-        grad_down,
-        gain_grad(norm_first, (w_query, grad_query), (key_weight, grad_key), (value_weight, grad_value)),
-        gain_grad(norm_second, (w_gate, grad_gate), (w_up, grad_upper)),
+        done["d_input"].swapaxes(1, 2),
+        *(done[name] for name in ("query", "key", "value", "output", "gate", "upper", "down")),
+        done["gain_one"],
+        done["gain_two"],
     )
 
 

time: 445 us -> 434 us (0.975)
  Pallas kernels: 141 us -> 129 us
  other arithmetic: 58.8 us -> 53.5 us
    pallas_call x6 -> x2, Pallas kernels: 29.9 us -> 17.2 us  [the longest x1 9.81 us: wide_grad(): pl.pallas_call(functools.partial(wide_grad_kernel, cuts, count, rows), gr...]
    ppermute x64 -> x63, starting transfers between devices: 74.1 us -> 78.5 us  [move(): return lax.ppermute(value, AXES, pairs)]
    optimization_barrier x4 -> x2, local copies, waits for them, and re-layouts: 8.92 us -> 5.12 us  [meet(): return lax.optimization_barrier(values)]
    unnamed x178 -> x159, local copies, waits for them, and re-layouts: 23.6 us -> 26.2 us
    convert_element_type x22 -> x21, other arithmetic: 35.4 us -> 33.1 us  [total(): return sum((part.astype(F32) for part in parts)).astype(parts[0].dtype)]
    ppermute x64 -> x63, waiting for transfers between devices: 121 us -> 123 us  [move(): return lax.ppermute(value, AXES, pairs)]
  transfers between devices with their start and end apart: 64 -> 63, of which waited for: 22 -> 19; matrix products, arithmetic and copies ran while one was open for 11% -> 12% of each run, Pallas kernels for 32% -> 30%
where the time goes in v6:
time: 434 us; the launch traced here: 426 us
  Pallas kernels  129 us (30%)
  waiting for transfers between devices  123 us (28%)
  starting transfers between devices  78.5 us (18%)
  other arithmetic  53.5 us (12%)
  local copies, waits for them, and re-layouts  39.7 us (9%)
    ppermute x63, waiting for transfers between devices, move(): return lax.ppermute(value, AXES, pairs)  123 us
    ppermute x63, starting transfers between devices, move(): return lax.ppermute(value, AXES, pairs)  78.5 us
    pallas_call x2, Pallas kernels, attend_back(): pl.pallas_call(functools.partial(attend_back_kernel, shards, seg_rows), g...  34.2 us
    pallas_call x1, Pallas kernels, feed(): pl.pallas_call(functools.partial(feed_kernel, counts), name='feed', in_sp...  33.7 us
    convert_element_type x21, other arithmetic, total(): return sum((part.astype(F32) for part in parts)).astype(parts[0].dtype)  33.1 us
    unnamed x159, local copies, waits for them, and re-layouts  26.2 us
    pallas_call x1, Pallas kernels, attend(): pl.pallas_call(functools.partial(attend_kernel, shards, seg_rows), grid=(...  16.8 us
    pallas_call x1, Pallas kernels, attention_grad(): pl.pallas_call(functools.partial(attention_grad_kernel, shards, half), na...  11.2 us
  transfers between devices with their start and end apart: 63, of which 19 were waited for; matrix products, arithmetic and copies ran while one was open for 12% of the time, Pallas kernels for 30%

profile of v6, /device:TPU:0, one launch (start us, length us, event | category | flops | bytes accessed | tf_op | source)
XLA Modules:
  0.0 426.2 jit_solution(1442081118036526489)
XLA Ops:
  2.9 2.4 broadcast_select_fusion.6
  5.3 3.0 collective-permute-start
  10.5 2.9 collective-permute-start.4
  13.5 2.4 copy.73.refs_22_
  16.4 1.7 fusion.1
  18.2 2.0 constant_dynamic-slice_fusion
  20.2 2.2 dynamic-slice_select_fusion
  22.8 2.4 collective-permute-start.8
  26.8 12.7 %collective-permute-done.8.refs_10_ = bf16[240,1280]{1,0:T(8,128)(2,1)S(1)} collective-permute-done((bf16[240,1280]{1,0:T(8,128)(2,1)}, bf16[240,1280]{1,0:T(8,128)(2,1)S(1)}, u32[]{:S(2)}, u32[]{:S(2)}) %collective-permute-start.8) | collective-permute-done | bytes 614432 | tf_op jit(solution)/shard_map/ppermute | solution.py:89
  41.4 2.0 tile.8
  44.5 1.7 collective-permute-start.10
  46.3 2.6 copy.77.cos_ref
  48.9 2.5 copy.78.sin_ref
  53.6 6.7 %project.1 = (bf16[512,960]{1,0:T(8,128)(2,1)}, bf16[512,640]{1,0:T(8,128)(2,1)S(1)}) custom-call(s32[16]{0:T(128)S(1)} %stack.196.starts_ref.s0_ref, bf16[2,960,256]{2,1,0:T(8,128)(2,1)} %bitcast.63, f32[2,960]{1,0:T(2,128)S(1)} %maximum_convert_fusion.7.gains_ref, f32[2048,128]{1,0:T(8,128)} %copy.77.cos_ref, f32[2048,128]{1,0:T(8,128)} %copy.78.sin_ref, ...), custom_call_target="tpu_custom_call" | custom-call | flops 1572864000 | bytes 7536640 | tf_op jit(solution)/shard_map/project/pallas_call | solution.py:301
  60.9 1.5 collective-permute-start.11
  63.0 1.6 collective-permute-start.13
  66.6 11.8 %collective-permute-done.13.refs_11_ = bf16[240,1280]{1,0:T(8,128)(2,1)S(1)} collective-permute-done((bf16[240,1280]{1,0:T(8,128)(2,1)S(1)}, bf16[240,1280]{1,0:T(8,128)(2,1)S(1)}, u32[]{:S(2)}, u32[]{:S(2)}) %collective-permute-start.13) | collective-permute-done | bytes 614432 | tf_op jit(solution)/shard_map/ppermute | solution.py:89
  78.4 13.7 %collective-permute-done.14.refs_23_ = bf16[320,960]{1,0:T(8,128)(2,1)S(1)} collective-permute-done((bf16[320,960]{1,0:T(8,128)(2,1)S(1)}, bf16[320,960]{1,0:T(8,128)(2,1)S(1)}, u32[]{:S(2)}, u32[]{:S(2)}) %collective-permute-start.14) | collective-permute-done | bytes 614432 | tf_op jit(solution)/shard_map/ppermute | solution.py:89
  92.4 2.1 collective-permute-start.20
  95.0 11.3 %collective-permute-done.20.refs_15_ = bf16[240,1280]{1,0:T(8,128)(2,1)} collective-permute-done((bf16[240,1280]{1,0:T(8,128)(2,1)}, bf16[240,1280]{1,0:T(8,128)(2,1)}, u32[]{:S(2)}, u32[]{:S(2)}) %collective-permute-start.20) | collective-permute-done | bytes 614432 | tf_op jit(solution)/shard_map/ppermute | solution.py:89
  106.3 2.5 collective-permute-start.21
  111.5 16.8 %attend.1 = (bf16[512,960]{1,0:T(8,128)(2,1)S(1)}, f32[512,128]{1,0:T(8,128)S(1)}) custom-call(bf16[512,960]{1,0:T(8,128)(2,1)S(1)} %copy-done.21, bf16[512,640]{1,0:T(8,128)(2,1)S(1)} %get-tuple-element.433.refs_0_, bf16[512,640]{1,0:T(8,128)(2,1)S(1)} %collective-permute-done.11.refs_1_, bf16[512,640]{1,0:T(8,128)(2,1)S(1)} %collective-permute-done.12.refs_2_, ...), custom_call_target="tpu_custom_call" | custom-call | flops 8053063680 | bytes 983040 | tf_op jit(solution)/shard_map/attend/pallas_call | solution.py:744
  134.5 2.0 collective-permute-start.31
  136.5 33.7 %feed.1 = (bf16[2,960,256]{2,1,0:T(8,128)(2,1)}, bf16[2560,512]{1,0:T(8,128)(2,1)}, bf16[2,512,2560]{2,1,0:T(8,128)(2,1)}, bf16[960,512]{1,0:T(8,128)(2,1)}, bf1...) custom-call(s32[16]{0:T(128)} %copy-done.19, ...), custom_call_target="tpu_custom_call" | custom-call | flops 17930649600 | bytes 38338560 | tf_op jit(solution)/shard_map/feed/pallas_call | solution.py:396
  170.3 1.6 collective-permute-start.32
  172.0 1.7 copy-done.31
  177.4 7.4 %rows_grad.1 = (bf16[1792,1024]{1,0:T(8,128)(2,1)}, bf16[1792,1024]{1,0:T(8,128)(2,1)}) custom-call(s32[16]{0:T(128)S(1)} %stack.227.starts_ref, bf16[2560,512]{1,0:T(8,128)(2,1)S(1)} %copy-done.31, bf16[512,960]{1,0:T(8,128)(2,1)S(1)} %copy-done.32, bf16[960,512]{1,0:T(8,128)(2,1)S(1)} %copy-done.35, bf16[512,960]{1,0:T(8,128)(2,1)S(1)} %copy-done.33), custom_call_target="tpu_custom_call" | custom-call | flops 3523215360 | bytes 12910592 | tf_op jit(solution)/shard_map/rows_grad/pallas_call | solution.py:454
  184.9 9.8 %wide_grad.1 = (bf16[512,2560]{1,0:T(8,128)(2,1)}, bf16[448,2560]{1,0:T(8,128)(2,1)S(1)}, bf16[512,2560]{1,0:T(8,128)(2,1)}, bf16[448,2560]{1,0:T(8,128)(2,1)S(1)}) custom-call(s32[10]{0:T(128)S(1)} %stack.233.info_ref, bf16[960,512]{1,0:T(8,128)(2,1)S(1)} %copy-done.34, bf16[2,512,2560]{2,1,0:T(8,128)(2,1)} %get-tuple-element.399.given_ref.kept_ref, ...), custom_call_target="tpu_custom_call" | custom-call | flops 5033164800 | bytes 16056320 | tf_op jit(solution)/shard_map/wide_grad/pallas_call | solution.py:504
  195.4 3.9 add_convert_fusion
  201.9 17.1 %attend_back.2 = (bf16[512,960]{1,0:T(8,128)(2,1)S(1)}, bf16[2,512,640]{2,1,0:T(8,128)(2,1)}, bf16[2,512,640]{2,1,0:T(8,128)(2,1)}) custom-call(bf16[512,960]{1,0:T(8,128)(2,1)S(1)} %copy-done.22, bf16[512,640]{1,0:T(8,128)(2,1)S(1)} %copy-done.24, bf16[512,640]{1,0:T(8,128)(2,1)S(1)} %copy-done.26, bf16[512,640]{1,0:T(8,128)(2,1)S(1)} %copy-done.28, ...), custom_call_target="tpu_custom_call" | custom-call | flops 10066329600 | bytes 983040 | tf_op jit(solution)/shard_map/attend_back/pallas_call | solution.py:766
  219.0 3.9 collective-permute-done.34
  222.9 2.0 add_convert_fusion.1
  224.9 1.6 collective-permute-start.38
  226.5 2.0 add_convert_fusion.6
  228.5 1.6 collective-permute-start.37
  230.1 17.1 %attend_back.3 = (bf16[512,960]{1,0:T(8,128)(2,1)S(1)}, bf16[2,512,640]{2,1,0:T(8,128)(2,1)}, bf16[2,512,640]{2,1,0:T(8,128)(2,1)}) custom-call(bf16[512,960]{1,0:T(8,128)(2,1)S(1)} %copy-done.22, bf16[512,640]{1,0:T(8,128)(2,1)S(1)} %copy-done.24, bf16[512,640]{1,0:T(8,128)(2,1)S(1)} %copy-done.26, ...), custom_call_target="tpu_custom_call", output_to_operand_aliasing={{0}: (11, {}), {1}: (12, {}), {2}: (13, {})} | custom-call | flops 10066329600 | bytes 983040 | tf_op jit(solution)/shard_map/attend_back/pallas_call | solution.py:766
  247.2 3.8 collective-permute-done.37
  252.4 3.0 add_convert_fusion.5
  255.4 4.1 collective-permute-start.39
  259.5 2.6 add_convert_fusion.2
  263.7 2.4 add_convert_fusion.13
  269.1 11.2 %attention_grad.1 = (bf16[512,1664]{1,0:T(8,128)(2,1)}, bf16[512,1664]{1,0:T(8,128)(2,1)}) custom-call(s32[8]{0:T(128)} %stack.234.starts_ref, f32[960,1]{1,0:T(8,128)} %copy.79.gain_ref, f32[2048,128]{1,0:T(8,128)} %copy.77.cos_ref, f32[2048,128]{1,0:T(8,128)} %copy.78.sin_ref, bf16[512,960]{1,0:T(8,128)(2,1)} %copy-done.16, bf16[2,960,256]{2,1,0:T(8,128)(2,1)} %bitcast.67, ...), custom_call_target="tpu_custom_call" | custom-call | flops 3690987520 | bytes 9961472 | tf_op jit(solution)/shard_map/attention_grad/pallas_call | solution.py:578
  280.3 2.0 collective-permute-done.40
  282.3 3.0 collective-permute-done.41
  289.2 1.8 add_convert_fusion.12
  291.0 4.0 collective-permute-start.45
  296.4 1.5 collective-permute-start.46
  298.0 8.2 %collective-permute-done.46 = bf16[112,2560]{1,0:T(8,128)(2,1)S(1)} collective-permute-done((bf16[112,2560]{1,0:T(8,128)(2,1)S(1)}, bf16[112,2560]{1,0:T(8,128)(2,1)S(1)}, u32[]{:S(2)}, u32[]{:S(2)}) %collective-permute-start.46) | collective-permute-done | bytes 573472 | tf_op jit(solution)/shard_map/ppermute | solution.py:89
  306.2 3.4 collective-permute-done.45
  319.0 2.3 add_convert_fusion.16
  321.4 8.9 %collective-permute-start.51 = (bf16[112,2560]{1,0:T(8,128)(2,1)}, bf16[112,2560]{1,0:T(8,128)(2,1)S(1)}, u32[]{:S(2)}, u32[]{:S(2)}) collective-permute-start(bf16[112,2560]{1,0:T(8,128)(2,1)} %add_convert_fusion.16), channel_id=1, source_target_pairs={{0,8},{1,9},{2,10},{3,11},{4,12},{5,13},{6,14},{7,15},{24,16},{25,... | collective-permute-start | bytes 1720328 | tf_op jit(solution)/shard_map/ppermute | solution.py:89
  330.3 10.7 %collective-permute-done.51 = bf16[112,2560]{1,0:T(8,128)(2,1)S(1)} collective-permute-done((bf16[112,2560]{1,0:T(8,128)(2,1)}, bf16[112,2560]{1,0:T(8,128)(2,1)S(1)}, u32[]{:S(2)}, u32[]{:S(2)}) %collective-permute-start.51) | collective-permute-done | bytes 573472 | tf_op jit(solution)/shard_map/ppermute | solution.py:89
  343.4 1.6 add_convert_fusion.8
  348.6 2.1 add_convert_fusion.21
  352.9 9.1 %finish.1 = bf16[2,960,256]{2,1,0:T(8,128)(2,1)} custom-call(s32[16]{0:T(128)S(1)} %copy-done.20, bf16[2,960,256]{2,1,0:T(8,128)(2,1)} %bitcast.68, bf16[512,960]{1,0:T(8,128)(2,1)} %copy-done.16, bf16[512,640]{1,0:T(8,128)(2,1)S(1)} %fusion.kv_ref, f32[512,960]{1,0:T(8,128)} %get-tuple-element.491.dres_ref, f32[2,960]{1,0:T(2,128)S(1)} %copy-done.18, ...), custom_call_target="tpu_custom_call" | custom-call | flops 1572864000 | bytes 8847360 | tf_op jit(solution)/shard_map/finish/pallas_call | solution.py:618
  362.0 1.9 collective-permute-done.54
  365.2 5.4 %collective-permute-start.56 = (bf16[128,1664]{1,0:T(8,128)(2,1)S(1)}, bf16[128,1664]{1,0:T(8,128)(2,1)S(1)}, u32[]{:S(2)}, u32[]{:S(2)}) collective-permute-start(bf16[128,1664]{1,0:T(8,128)(2,1)S(1)} %add_convert_fusion.20), channel_id=1, source_target_pairs={{0,8},{1,9},{2,10},{3,11},{4,12},{5,13},{6,14},{7,15},{24,16},{25,... | collective-permute-start | bytes 1277960 | tf_op jit(solution)/shard_map/ppermute | solution.py:89
  374.7 4.4 %collective-permute-done.56 = bf16[128,1664]{1,0:T(8,128)(2,1)S(1)} collective-permute-done((bf16[128,1664]{1,0:T(8,128)(2,1)S(1)}, bf16[128,1664]{1,0:T(8,128)(2,1)S(1)}, u32[]{:S(2)}, u32[]{:S(2)}) %collective-permute-start.56) | collective-permute-done | bytes 426016 | tf_op jit(solution)/shard_map/ppermute | solution.py:89
  379.1 9.2 %collective-permute-done.58 = bf16[112,2560]{1,0:T(8,128)(2,1)S(1)} collective-permute-done((bf16[112,2560]{1,0:T(8,128)(2,1)S(1)}, bf16[112,2560]{1,0:T(8,128)(2,1)S(1)}, u32[]{:S(2)}, u32[]{:S(2)}) %collective-permute-start.58) | collective-permute-done | bytes 573472 | tf_op jit(solution)/shard_map/ppermute | solution.py:89
  392.1 1.7 maximum_convert_fusion.1
  396.3 1.7 maximum_convert_fusion.2
  398.0 18.8 %collective-permute-done.61 = bf16[128,1664]{1,0:T(8,128)(2,1)S(1)} collective-permute-done((bf16[128,1664]{1,0:T(8,128)(2,1)S(1)}, bf16[128,1664]{1,0:T(8,128)(2,1)S(1)}, u32[]{:S(2)}, u32[]{:S(2)}) %collective-permute-start.61) | collective-permute-done | bytes 426016 | tf_op jit(solution)/shard_map/ppermute | solution.py:89
  416.9 1.8 collective-permute-done.62
  423.4 2.0 copy.88
  (319 shorter events, 77.5 us)
Async XLA Ops:
  5.3 19.9 %collective-permute-start = (bf16[240,1280]{1,0:T(8,128)(2,1)}, bf16[240,1280]{1,0:T(8,128)(2,1)S(1)}, u32[]{:S(2)}, u32[]{:S(2)}) collective-permute-start(bf16[240,1280]{1,0:T(8,128)(2,1)} %get-tuple-element.587), channel_id=1, source_target_pairs={{0,1},{1,0},{2,3},{3,2},{4,6},{5,7},{6,4},{7,5},{8,9},{9,8},{10,11... | collective-permute-start | bytes 1843208 | tf_op jit(solution)/shard_map/ppermute | solution.py:89
  8.3 16.9 %collective-permute-start.1 = (bf16[240,1280]{1,0:T(8,128)(2,1)}, bf16[240,1280]{1,0:T(8,128)(2,1)S(1)}, u32[]{:S(2)}, u32[]{:S(2)}) collective-permute-start(bf16[240,1280]{1,0:T(8,128)(2,1)} %get-tuple-element.587), channel_id=1, source_target_pairs={{0,2},{1,3},{2,0},{3,1},{4,5},{5,4},{6,7},{7,6},{8,10},{9,11},{10,... | collective-permute-start | bytes 1843208 | tf_op jit(solution)/shard_map/ppermute | solution.py:89
  9.9 12.9 %collective-permute-start.2 = (bf16[2,240]{1,0:T(2,128)(2,1)S(1)}, bf16[2,240]{1,0:T(2,128)(2,1)S(1)}, u32[]{:S(2)}, u32[]{:S(2)}) collective-permute-start(bf16[2,240]{1,0:T(2,128)(2,1)S(1)} %pad_maximum_fusion.4), channel_id=1, source_target_pairs={{0,1},{1,0},{2,3},{3,2},{4,5},{5,4},{6,7},{7,6},{8,9},{9,8},{10,11... | collective-permute-start | bytes 2888 | tf_op jit(solution)/shard_map/ppermute | solution.py:89
  10.5 14.7 %collective-permute-start.3 = (bf16[2,240]{1,0:T(2,128)(2,1)S(1)}, bf16[2,240]{1,0:T(2,128)(2,1)S(1)}, u32[]{:S(2)}, u32[]{:S(2)}) collective-permute-start(bf16[2,240]{1,0:T(2,128)(2,1)S(1)} %pad_maximum_fusion.4), channel_id=1, source_target_pairs={{0,2},{1,3},{2,0},{3,1},{4,6},{5,7},{6,4},{7,5},{8,10},{9,11},{10,... | collective-permute-start | bytes 2888 | tf_op jit(solution)/shard_map/ppermute | solution.py:89
  10.5 14.7 %collective-permute-start.4 = (bf16[2,240]{1,0:T(2,128)(2,1)S(1)}, bf16[2,240]{1,0:T(2,128)(2,1)S(1)}, u32[]{:S(2)}, u32[]{:S(2)}) collective-permute-start(bf16[2,240]{1,0:T(2,128)(2,1)S(1)} %pad_maximum_fusion.4), channel_id=1, source_target_pairs={{0,3},{1,2},{2,1},{3,0},{4,7},{5,6},{6,5},{7,4},{8,11},{9,10},{10,... | collective-permute-start | bytes 2888 | tf_op jit(solution)/shard_map/ppermute | solution.py:89
  22.8 16.8 %collective-permute-start.8 = (bf16[240,1280]{1,0:T(8,128)(2,1)}, bf16[240,1280]{1,0:T(8,128)(2,1)S(1)}, u32[]{:S(2)}, u32[]{:S(2)}) collective-permute-start(bf16[240,1280]{1,0:T(8,128)(2,1)} %dynamic-slice_select_fusion), channel_id=1, source_target_pairs={{0,1},{1,0},{2,3},{3,2},{4,6},{5,7},{6,4},{7,5},{8,9},{9,8},{10,11... | collective-permute-start | bytes 1843208 | tf_op jit(solution)/shard_map/ppermute | solution.py:89
  25.2 14.3 %collective-permute-start.5 = (bf16[240,1280]{1,0:T(8,128)(2,1)S(1)}, bf16[240,1280]{1,0:T(8,128)(2,1)S(1)}, u32[]{:S(2)}, u32[]{:S(2)}) collective-permute-start(bf16[240,1280]{1,0:T(8,128)(2,1)S(1)} %collective-permute-done.refs_2_), channel_id=1, source_target_pairs={{0,2},{1,3},{2,0},{3,1},{4,5},{5,4},{6,7},{7,6},{8,10},{9,11},{10,... | collective-permute-start | bytes 1843208 | tf_op jit(solution)/shard_map/ppermute | solution.py:89
  26.0 13.5 %collective-permute-start.6 = (bf16[240,1280]{1,0:T(8,128)(2,1)S(1)}, bf16[240,1280]{1,0:T(8,128)(2,1)S(1)}, u32[]{:S(2)}, u32[]{:S(2)}) collective-permute-start(bf16[240,1280]{1,0:T(8,128)(2,1)S(1)} %collective-permute-done.refs_2_), channel_id=1, source_target_pairs={{0,4},{1,5},{2,6},{3,7},{4,0},{5,1},{6,2},{7,3},{8,12},{9,13},{10,... | collective-permute-start | bytes 1843208 | tf_op jit(solution)/shard_map/ppermute | solution.py:89
  26.0 14.4 %collective-permute-start.7 = (bf16[240,1280]{1,0:T(8,128)(2,1)S(1)}, bf16[240,1280]{1,0:T(8,128)(2,1)S(1)}, u32[]{:S(2)}, u32[]{:S(2)}) collective-permute-start(bf16[240,1280]{1,0:T(8,128)(2,1)S(1)} %collective-permute-done.1.refs_4_), channel_id=1, source_target_pairs={{0,4},{1,5},{2,6},{3,7},{4,0},{5,1},{6,2},{7,3},{8,12},{9,13},{10,... | collective-permute-start | bytes 1843208 | tf_op jit(solution)/shard_map/ppermute | solution.py:89
  44.5 6.9 %collective-permute-start.9 = (bf16[240,1280]{1,0:T(8,128)(2,1)S(1)}, bf16[240,1280]{1,0:T(8,128)(2,1)}, u32[]{:S(2)}, u32[]{:S(2)}) collective-permute-start(bf16[240,1280]{1,0:T(8,128)(2,1)S(1)} %collective-permute-done.5.refs_6_), channel_id=1, source_target_pairs={{0,4},{1,5},{2,6},{3,7},{4,0},{5,1},{6,2},{7,3},{8,12},{9,13},{10,... | collective-permute-start | bytes 1843208 | tf_op jit(solution)/shard_map/ppermute | solution.py:89
  44.5 16.4 %collective-permute-start.10 = (bf16[240,1280]{1,0:T(8,128)(2,1)}, bf16[240,1280]{1,0:T(8,128)(2,1)}, u32[]{:S(2)}, u32[]{:S(2)}) collective-permute-start(bf16[240,1280]{1,0:T(8,128)(2,1)} %dynamic-slice_select_fusion), channel_id=1, source_target_pairs={{0,2},{1,3},{2,0},{3,1},{4,5},{5,4},{6,7},{7,6},{8,10},{9,11},{10,... | collective-permute-start | bytes 1843208 | tf_op jit(solution)/shard_map/ppermute | solution.py:89
  60.9 67.4 %copy-start.23 = (bf16[512,640]{1,0:T(8,128)(2,1)}, bf16[512,640]{1,0:T(8,128)(2,1)S(1)}, u32[]{:S(2)}) copy-start(bf16[512,640]{1,0:T(8,128)(2,1)S(1)} %get-tuple-element.433.refs_0_) | copy-start | bytes 1966084
  60.9 31.2 %collective-permute-start.11 = (bf16[512,640]{1,0:T(8,128)(2,1)S(1)}, bf16[512,640]{1,0:T(8,128)(2,1)S(1)}, u32[]{:S(2)}, u32[]{:S(2)}) collective-permute-start(bf16[512,640]{1,0:T(8,128)(2,1)S(1)} %get-tuple-element.433.refs_0_), channel_id=1, source_target_pairs={{0,1},{1,0},{2,3},{3,2},{4,6},{5,7},{6,4},{7,5},{8,9},{9,8},{10,11... | collective-permute-start | bytes 1966088 | tf_op jit(solution)/shard_map/ppermute | solution.py:89
  62.5 29.7 %collective-permute-start.12 = (bf16[512,640]{1,0:T(8,128)(2,1)S(1)}, bf16[512,640]{1,0:T(8,128)(2,1)S(1)}, u32[]{:S(2)}, u32[]{:S(2)}) collective-permute-start(bf16[512,640]{1,0:T(8,128)(2,1)S(1)} %get-tuple-element.433.refs_0_), channel_id=1, source_target_pairs={{0,2},{1,3},{2,0},{3,1},{4,5},{5,4},{6,7},{7,6},{8,10},{9,11},{10,... | collective-permute-start | bytes 1966088 | tf_op jit(solution)/shard_map/ppermute | solution.py:89
  63.0 15.4 %collective-permute-start.13 = (bf16[240,1280]{1,0:T(8,128)(2,1)S(1)}, bf16[240,1280]{1,0:T(8,128)(2,1)S(1)}, u32[]{:S(2)}, u32[]{:S(2)}) collective-permute-start(bf16[240,1280]{1,0:T(8,128)(2,1)S(1)} %copy-done.69), channel_id=1, source_target_pairs={{0,8},{1,9},{2,10},{3,11},{4,12},{5,13},{6,14},{7,15},{8,0},{9,1},... | collective-permute-start | bytes 1843208 | tf_op jit(solution)/shard_map/ppermute | solution.py:89
  64.6 27.5 %collective-permute-start.14 = (bf16[320,960]{1,0:T(8,128)(2,1)S(1)}, bf16[320,960]{1,0:T(8,128)(2,1)S(1)}, u32[]{:S(2)}, u32[]{:S(2)}) collective-permute-start(bf16[320,960]{1,0:T(8,128)(2,1)S(1)} %copy-done.57), channel_id=1, source_target_pairs={{0,1},{1,0},{2,3},{3,2},{4,6},{5,7},{6,4},{7,5},{8,9},{9,8},{10,11... | collective-permute-start | bytes 1843208 | tf_op jit(solution)/shard_map/ppermute | solution.py:89
  65.2 29.8 %collective-permute-start.16 = (bf16[240,1280]{1,0:T(8,128)(2,1)S(1)}, bf16[240,1280]{1,0:T(8,128)(2,1)S(1)}, u32[]{:S(2)}, u32[]{:S(2)}) collective-permute-start(bf16[240,1280]{1,0:T(8,128)(2,1)S(1)} %copy-done.69), channel_id=1, source_target_pairs={{0,2},{1,3},{2,0},{3,1},{4,5},{5,4},{6,7},{7,6},{8,10},{9,11},{10,... | collective-permute-start | bytes 1843208 | tf_op jit(solution)/shard_map/ppermute | solution.py:89
  92.1 16.7 %collective-permute-start.15 = (bf16[512,640]{1,0:T(8,128)(2,1)S(1)}, bf16[512,640]{1,0:T(8,128)(2,1)S(1)}, u32[]{:S(2)}, u32[]{:S(2)}) collective-permute-start(bf16[512,640]{1,0:T(8,128)(2,1)S(1)} %collective-permute-done.11.refs_1_), channel_id=1, source_target_pairs={{0,2},{1,3},{2,0},{3,1},{4,5},{5,4},{6,7},{7,6},{8,10},{9,11},{10,... | collective-permute-start | bytes 1966088 | tf_op jit(solution)/shard_map/ppermute | solution.py:89
  92.4 13.9 %collective-permute-start.20 = (bf16[240,1280]{1,0:T(8,128)(2,1)}, bf16[240,1280]{1,0:T(8,128)(2,1)}, u32[]{:S(2)}, u32[]{:S(2)}) collective-permute-start(bf16[240,1280]{1,0:T(8,128)(2,1)} %collective-permute-done.10.refs_14_), channel_id=1, source_target_pairs={{0,8},{1,9},{2,10},{3,11},{4,12},{5,13},{6,14},{7,15},{8,0},{9,1},... | collective-permute-start | bytes 1843208 | tf_op jit(solution)/shard_map/ppermute | solution.py:89
  94.4 14.3 %collective-permute-start.17 = (bf16[240,1280]{1,0:T(8,128)(2,1)S(1)}, bf16[240,1280]{1,0:T(8,128)(2,1)}, u32[]{:S(2)}, u32[]{:S(2)}) collective-permute-start(bf16[240,1280]{1,0:T(8,128)(2,1)S(1)} %copy-done.69), channel_id=1, source_target_pairs={{0,4},{1,5},{2,6},{3,7},{4,0},{5,1},{6,2},{7,3},{8,12},{9,13},{10,... | collective-permute-start | bytes 1843208 | tf_op jit(solution)/shard_map/ppermute | solution.py:89
  94.4 14.4 %collective-permute-start.18 = (bf16[240,1280]{1,0:T(8,128)(2,1)}, bf16[240,1280]{1,0:T(8,128)(2,1)S(1)}, u32[]{:S(2)}, u32[]{:S(2)}) collective-permute-start(bf16[240,1280]{1,0:T(8,128)(2,1)} %collective-permute-done.10.refs_14_), channel_id=1, source_target_pairs={{0,4},{1,5},{2,6},{3,7},{4,0},{5,1},{6,2},{7,3},{8,12},{9,13},{10,... | collective-permute-start | bytes 1843208 | tf_op jit(solution)/shard_map/ppermute | solution.py:89
  94.9 13.8 %collective-permute-start.19 = (bf16[240,1280]{1,0:T(8,128)(2,1)S(1)}, bf16[240,1280]{1,0:T(8,128)(2,1)S(1)}, u32[]{:S(2)}, u32[]{:S(2)}) collective-permute-start(bf16[240,1280]{1,0:T(8,128)(2,1)S(1)} %collective-permute-done.13.refs_11_), channel_id=1, source_target_pairs={{0,4},{1,5},{2,6},{3,7},{4,0},{5,1},{6,2},{7,3},{8,12},{9,13},{10,... | collective-permute-start | bytes 1843208 | tf_op jit(solution)/shard_map/ppermute | solution.py:89
  106.3 23.8 %collective-permute-start.21 = (bf16[320,960]{1,0:T(8,128)(2,1)S(1)}, bf16[320,960]{1,0:T(8,128)(2,1)S(1)}, u32[]{:S(2)}, u32[]{:S(2)}) collective-permute-start(bf16[320,960]{1,0:T(8,128)(2,1)S(1)} %copy-done.57), channel_id=1, source_target_pairs={{0,2},{1,3},{2,0},{3,1},{4,5},{5,4},{6,7},{7,6},{8,10},{9,11},{10,... | collective-permute-start | bytes 1843208 | tf_op jit(solution)/shard_map/ppermute | solution.py:89
  108.7 21.3 %collective-permute-start.22 = (bf16[320,960]{1,0:T(8,128)(2,1)S(1)}, bf16[320,960]{1,0:T(8,128)(2,1)S(1)}, u32[]{:S(2)}, u32[]{:S(2)}) collective-permute-start(bf16[320,960]{1,0:T(8,128)(2,1)S(1)} %collective-permute-done.14.refs_23_), channel_id=1, source_target_pairs={{0,2},{1,3},{2,0},{3,1},{4,5},{5,4},{6,7},{7,6},{8,10},{9,11},{10,... | collective-permute-start | bytes 1843208 | tf_op jit(solution)/shard_map/ppermute | solution.py:89
  108.8 21.3 %collective-permute-start.23 = (bf16[240,1280]{1,0:T(8,128)(2,1)S(1)}, bf16[240,1280]{1,0:T(8,128)(2,1)}, u32[]{:S(2)}, u32[]{:S(2)}) collective-permute-start(bf16[240,1280]{1,0:T(8,128)(2,1)S(1)} %collective-permute-done.16.refs_18_), channel_id=1, source_target_pairs={{0,8},{1,9},{2,10},{3,11},{4,12},{5,13},{6,14},{7,15},{8,0},{9,1},... | collective-permute-start | bytes 1843208 | tf_op jit(solution)/shard_map/ppermute | solution.py:89
  110.3 19.8 %collective-permute-start.24 = (bf16[240,1280]{1,0:T(8,128)(2,1)S(1)}, bf16[240,1280]{1,0:T(8,128)(2,1)S(1)}, u32[]{:S(2)}, u32[]{:S(2)}) collective-permute-start(bf16[240,1280]{1,0:T(8,128)(2,1)S(1)} %collective-permute-done.16.refs_18_), channel_id=1, source_target_pairs={{0,4},{1,5},{2,6},{3,7},{4,0},{5,1},{6,2},{7,3},{8,12},{9,13},{10,... | collective-permute-start | bytes 1843208 | tf_op jit(solution)/shard_map/ppermute | solution.py:89
  130.1 2.9 collective-permute-start.25
  130.7 3.8 collective-permute-start.26
  130.7 5.7 %collective-permute-start.27 = (bf16[320,960]{1,0:T(8,128)(2,1)S(1)}, bf16[320,960]{1,0:T(8,128)(2,1)}, u32[]{:S(2)}, u32[]{:S(2)}) collective-permute-start(bf16[320,960]{1,0:T(8,128)(2,1)S(1)} %collective-permute-done.14.refs_23_), channel_id=1, source_target_pairs={{0,4},{1,5},{2,6},{3,7},{4,0},{5,1},{6,2},{7,3},{8,12},{9,13},{10,... | collective-permute-start | bytes 1843208 | tf_op jit(solution)/shard_map/ppermute | solution.py:89
  131.2 5.3 %collective-permute-start.28 = (bf16[320,960]{1,0:T(8,128)(2,1)S(1)}, bf16[320,960]{1,0:T(8,128)(2,1)}, u32[]{:S(2)}, u32[]{:S(2)}) collective-permute-start(bf16[320,960]{1,0:T(8,128)(2,1)S(1)} %collective-permute-done.21.refs_25_), channel_id=1, source_target_pairs={{0,4},{1,5},{2,6},{3,7},{4,0},{5,1},{6,2},{7,3},{8,12},{9,13},{10,... | collective-permute-start | bytes 1843208 | tf_op jit(solution)/shard_map/ppermute | solution.py:89
  131.5 5.0 %collective-permute-start.29 = (bf16[320,960]{1,0:T(8,128)(2,1)S(1)}, bf16[320,960]{1,0:T(8,128)(2,1)}, u32[]{:S(2)}, u32[]{:S(2)}) collective-permute-start(bf16[320,960]{1,0:T(8,128)(2,1)S(1)} %collective-permute-done.22.refs_27_), channel_id=1, source_target_pairs={{0,4},{1,5},{2,6},{3,7},{4,0},{5,1},{6,2},{7,3},{8,12},{9,13},{10,... | collective-permute-start | bytes 1843208 | tf_op jit(solution)/shard_map/ppermute | solution.py:89
  133.0 37.3 %collective-permute-start.30 = (bf16[2,960,256]{2,1,0:T(8,128)(2,1)}, bf16[2,960,256]{2,1,0:T(8,128)(2,1)}, u32[]{:S(2)}, u32[]{:S(2)}) collective-permute-start(bf16[2,960,256]{2,1,0:T(8,128)(2,1)} %bitcast.64), channel_id=1, source_target_pairs={{0,1},{1,0},{2,3},{3,2},{4,6},{5,7},{6,4},{7,5},{8,9},{9,8},{10,11... | collective-permute-start | bytes 2949128 | tf_op jit(solution)/shard_map/ppermute | solution.py:89
  134.5 35.8 %collective-permute-start.31 = (bf16[2,960,256]{2,1,0:T(8,128)(2,1)}, bf16[2,960,256]{2,1,0:T(8,128)(2,1)S(1)}, u32[]{:S(2)}, u32[]{:S(2)}) collective-permute-start(bf16[2,960,256]{2,1,0:T(8,128)(2,1)} %bitcast.65), channel_id=1, source_target_pairs={{0,2},{1,3},{2,0},{3,1},{4,5},{5,4},{6,7},{7,6},{8,10},{9,11},{10,... | collective-permute-start | bytes 2949128 | tf_op jit(solution)/shard_map/ppermute | solution.py:89
  170.3 14.5 %collective-permute-start.32 = (bf16[2,960,256]{2,1,0:T(8,128)(2,1)}, bf16[2,960,256]{2,1,0:T(8,128)(2,1)}, u32[]{:S(2)}, u32[]{:S(2)}) collective-permute-start(bf16[2,960,256]{2,1,0:T(8,128)(2,1)} %collective-permute-done.30.refs_1_), channel_id=1, source_target_pairs={{0,2},{1,3},{2,0},{3,1},{4,5},{5,4},{6,7},{7,6},{8,10},{9,11},{10,... | collective-permute-start | bytes 2949128 | tf_op jit(solution)/shard_map/ppermute | solution.py:89
  184.8 9.9 %collective-permute-start.33 = (bf16[1792,1024]{1,0:T(8,128)(2,1)}, bf16[1792,1024]{1,0:T(8,128)(2,1)}, u32[]{:S(2)}, u32[]{:S(2)}) collective-permute-start(bf16[1792,1024]{1,0:T(8,128)(2,1)} %get-tuple-element.397), channel_id=1, source_target_pairs={{0,4},{1,5},{2,6},{3,7},{4,0},{5,1},{6,2},{7,3},{8,12},{9,13},{10,... | collective-permute-start | bytes 11010056 | tf_op jit(solution)/shard_map/ppermute | solution.py:89
  194.8 28.1 %collective-permute-start.35 = (bf16[512,2560]{1,0:T(8,128)(2,1)}, bf16[512,2560]{1,0:T(8,128)(2,1)}, u32[]{:S(2)}, u32[]{:S(2)}) collective-permute-start(bf16[512,2560]{1,0:T(8,128)(2,1)} %get-tuple-element.421), channel_id=1, source_target_pairs={{0,4},{1,5},{2,6},{3,7},{4,0},{5,1},{6,2},{7,3},{8,12},{9,13},{10,... | collective-permute-start | bytes 7864328 | tf_op jit(solution)/shard_map/ppermute | solution.py:89
  195.4 27.5 %collective-permute-start.36 = (bf16[448,2560]{1,0:T(8,128)(2,1)S(1)}, bf16[448,2560]{1,0:T(8,128)(2,1)}, u32[]{:S(2)}, u32[]{:S(2)}) collective-permute-start(bf16[448,2560]{1,0:T(8,128)(2,1)S(1)} %get-tuple-element.423), channel_id=1, source_target_pairs={{0,4},{1,5},{2,6},{3,7},{4,0},{5,1},{6,2},{7,3},{8,12},{9,13},{10,... | collective-permute-start | bytes 6881288 | tf_op jit(solution)/shard_map/ppermute | solution.py:89
  199.3 23.5 %collective-permute-start.34 = (bf16[896,1024]{1,0:T(8,128)(2,1)}, bf16[896,1024]{1,0:T(8,128)(2,1)}, u32[]{:S(2)}, u32[]{:S(2)}) collective-permute-start(bf16[896,1024]{1,0:T(8,128)(2,1)} %add_convert_fusion), channel_id=1, source_target_pairs={{0,2},{1,3},{2,0},{3,1},{4,5},{5,4},{6,7},{7,6},{8,10},{9,11},{10,... | collective-permute-start | bytes 5505032 | tf_op jit(solution)/shard_map/ppermute | solution.py:89
  224.9 27.5 %collective-permute-start.38 = (bf16[256,2560]{1,0:T(8,128)(2,1)S(1)}, bf16[256,2560]{1,0:T(8,128)(2,1)S(1)}, u32[]{:S(2)}, u32[]{:S(2)}) collective-permute-start(bf16[256,2560]{1,0:T(8,128)(2,1)S(1)} %add_convert_fusion.1), channel_id=1, source_target_pairs={{0,2},{1,3},{2,0},{3,1},{4,5},{5,4},{6,7},{7,6},{8,10},{9,11},{10,... | collective-permute-start | bytes 3932168 | tf_op jit(solution)/shard_map/ppermute | solution.py:89
  228.5 22.5 %collective-permute-start.37 = (bf16[448,1024]{1,0:T(8,128)(2,1)S(1)}, bf16[448,1024]{1,0:T(8,128)(2,1)S(1)}, u32[]{:S(2)}, u32[]{:S(2)}) collective-permute-start(bf16[448,1024]{1,0:T(8,128)(2,1)S(1)} %add_convert_fusion.6), channel_id=1, source_target_pairs={{0,1},{1,0},{2,3},{3,2},{4,6},{5,7},{6,4},{7,5},{8,9},{9,8},{10,11... | collective-permute-start | bytes 2752520 | tf_op jit(solution)/shard_map/ppermute | solution.py:89
  255.4 26.9 %collective-permute-start.39 = (bf16[448,1024]{1,0:T(8,128)(2,1)S(1)}, bf16[448,1024]{1,0:T(8,128)(2,1)}, u32[]{:S(2)}, u32[]{:S(2)}) collective-permute-start(bf16[448,1024]{1,0:T(8,128)(2,1)S(1)} %add_convert_fusion.5), channel_id=1, source_target_pairs={{0,8},{1,9},{2,10},{3,11},{4,12},{5,13},{6,14},{7,15},{24,16},{25,... | collective-permute-start | bytes 2752520 | tf_op jit(solution)/shard_map/ppermute | solution.py:89
  262.1 23.2 %collective-permute-start.41 = (bf16[224,2560]{1,0:T(8,128)(2,1)}, bf16[224,2560]{1,0:T(8,128)(2,1)}, u32[]{:S(2)}, u32[]{:S(2)}) collective-permute-start(bf16[224,2560]{1,0:T(8,128)(2,1)} %add_convert_fusion.2), channel_id=1, source_target_pairs={{0,2},{1,3},{2,0},{3,1},{4,5},{5,4},{6,7},{7,6},{8,10},{9,11},{10,... | collective-permute-start | bytes 3440648 | tf_op jit(solution)/shard_map/ppermute | solution.py:89
  266.0 16.3 %collective-permute-start.40 = (bf16[128,2560]{1,0:T(8,128)(2,1)}, bf16[128,2560]{1,0:T(8,128)(2,1)}, u32[]{:S(2)}, u32[]{:S(2)}) collective-permute-start(bf16[128,2560]{1,0:T(8,128)(2,1)} %add_convert_fusion.13), channel_id=1, source_target_pairs={{0,1},{1,0},{2,3},{3,2},{4,6},{5,7},{6,4},{7,5},{8,9},{9,8},{10,11... | collective-permute-start | bytes 1966088 | tf_op jit(solution)/shard_map/ppermute | solution.py:89
  285.3 24.3 %collective-permute-start.42 = (bf16[2,512,640]{2,1,0:T(8,128)(2,1)}, bf16[2,512,640]{2,1,0:T(8,128)(2,1)S(1)}, u32[]{:S(2)}, u32[]{:S(2)}) collective-permute-start(bf16[2,512,640]{2,1,0:T(8,128)(2,1)} %get-tuple-element.474.refs_5_), channel_id=1, source_target_pairs={{0,2},{1,3},{2,0},{3,1},{4,5},{5,4},{6,7},{7,6},{8,10},{9,11},{10,... | collective-permute-start | bytes 3932168 | tf_op jit(solution)/shard_map/ppermute | solution.py:89
  288.4 21.2 %collective-permute-start.43 = (bf16[448,1024]{1,0:T(8,128)(2,1)S(1)}, bf16[448,1024]{1,0:T(8,128)(2,1)S(1)}, u32[]{:S(2)}, u32[]{:S(2)}) collective-permute-start(bf16[448,1024]{1,0:T(8,128)(2,1)S(1)} %add_convert_fusion.4), channel_id=1, source_target_pairs={{8,16},{9,17},{10,18},{11,19},{12,20},{13,21},{14,22},{15,23},{16,... | collective-permute-start | bytes 2752520 | tf_op jit(solution)/shard_map/ppermute | solution.py:89
  289.1 20.5 %collective-permute-start.44 = (bf16[512,1664]{1,0:T(8,128)(2,1)}, bf16[512,1664]{1,0:T(8,128)(2,1)S(1)}, u32[]{:S(2)}, u32[]{:S(2)}) collective-permute-start(bf16[512,1664]{1,0:T(8,128)(2,1)} %get-tuple-element.476), channel_id=1, source_target_pairs={{0,4},{1,5},{2,6},{3,7},{4,0},{5,1},{6,2},{7,3},{8,12},{9,13},{10,... | collective-permute-start | bytes 5111816 | tf_op jit(solution)/shard_map/ppermute | solution.py:89
  291.0 18.6 %collective-permute-start.45 = (bf16[128,2560]{1,0:T(8,128)(2,1)S(1)}, bf16[128,2560]{1,0:T(8,128)(2,1)S(1)}, u32[]{:S(2)}, u32[]{:S(2)}) collective-permute-start(bf16[128,2560]{1,0:T(8,128)(2,1)S(1)} %add_convert_fusion.12), channel_id=1, source_target_pairs={{0,8},{1,9},{2,10},{3,11},{4,12},{5,13},{6,14},{7,15},{24,16},{25,... | collective-permute-start | bytes 1966088 | tf_op jit(solution)/shard_map/ppermute | solution.py:89
  296.4 9.8 %collective-permute-start.46 = (bf16[112,2560]{1,0:T(8,128)(2,1)S(1)}, bf16[112,2560]{1,0:T(8,128)(2,1)S(1)}, u32[]{:S(2)}, u32[]{:S(2)}) collective-permute-start(bf16[112,2560]{1,0:T(8,128)(2,1)S(1)} %add_convert_fusion.17), channel_id=1, source_target_pairs={{0,1},{1,0},{2,3},{3,2},{4,6},{5,7},{6,4},{7,5},{8,9},{9,8},{10,11... | collective-permute-start | bytes 1720328 | tf_op jit(solution)/shard_map/ppermute | solution.py:89
  311.8 29.3 %collective-permute-start.47 = (bf16[1,512,640]{2,1,0:T(8,128)(2,1)}, bf16[1,512,640]{2,1,0:T(8,128)(2,1)}, u32[]{:S(2)}, u32[]{:S(2)}) collective-permute-start(bf16[1,512,640]{2,1,0:T(8,128)(2,1)} %add_convert_fusion.11), channel_id=1, source_target_pairs={{0,1},{1,0},{2,3},{3,2},{4,6},{5,7},{6,4},{7,5},{8,9},{9,8},{10,11... | collective-permute-start | bytes 1966088 | tf_op jit(solution)/shard_map/ppermute | solution.py:89
  313.7 28.3 %collective-permute-start.48 = (bf16[448,1024]{1,0:T(8,128)(2,1)S(1)}, bf16[448,1024]{1,0:T(8,128)(2,1)}, u32[]{:S(2)}, u32[]{:S(2)}) collective-permute-start(bf16[448,1024]{1,0:T(8,128)(2,1)S(1)} %add_convert_fusion.3), channel_id=1, source_target_pairs={{8,0},{9,1},{10,2},{11,3},{12,4},{13,5},{14,6},{15,7},{16,24},{17,... | collective-permute-start | bytes 2752520 | tf_op jit(solution)/shard_map/ppermute | solution.py:89
  316.1 25.0 %collective-permute-start.49 = (bf16[256,1664]{1,0:T(8,128)(2,1)}, bf16[256,1664]{1,0:T(8,128)(2,1)}, u32[]{:S(2)}, u32[]{:S(2)}) collective-permute-start(bf16[256,1664]{1,0:T(8,128)(2,1)} %add_convert_fusion.7), channel_id=1, source_target_pairs={{0,2},{1,3},{2,0},{3,1},{4,5},{5,4},{6,7},{7,6},{8,10},{9,11},{10,... | collective-permute-start | bytes 2555912 | tf_op jit(solution)/shard_map/ppermute | solution.py:89
  317.6 23.5 %collective-permute-start.50 = (bf16[128,2560]{1,0:T(8,128)(2,1)}, bf16[128,2560]{1,0:T(8,128)(2,1)}, u32[]{:S(2)}, u32[]{:S(2)}) collective-permute-start(bf16[128,2560]{1,0:T(8,128)(2,1)} %add_convert_fusion.10), channel_id=1, source_target_pairs={{8,16},{9,17},{10,18},{11,19},{12,20},{13,21},{14,22},{15,23},{16,... | collective-permute-start | bytes 1966088 | tf_op jit(solution)/shard_map/ppermute | solution.py:89
  321.4 19.7 %collective-permute-start.51 = (bf16[112,2560]{1,0:T(8,128)(2,1)}, bf16[112,2560]{1,0:T(8,128)(2,1)S(1)}, u32[]{:S(2)}, u32[]{:S(2)}) collective-permute-start(bf16[112,2560]{1,0:T(8,128)(2,1)} %add_convert_fusion.16), channel_id=1, source_target_pairs={{0,8},{1,9},{2,10},{3,11},{4,12},{5,13},{6,14},{7,15},{24,16},{25,... | collective-permute-start | bytes 1720328 | tf_op jit(solution)/shard_map/ppermute | solution.py:89
  343.4 20.5 %collective-permute-start.52 = (bf16[448,1024]{1,0:T(8,128)(2,1)S(1)}, bf16[448,1024]{1,0:T(8,128)(2,1)S(1)}, u32[]{:S(2)}, u32[]{:S(2)}) collective-permute-start(bf16[448,1024]{1,0:T(8,128)(2,1)S(1)} %broadcast_select_fusion), channel_id=1, source_target_pairs={{0,4},{1,5},{2,6},{3,7},{4,0},{5,1},{6,2},{7,3},{8,12},{9,13},{10,... | collective-permute-start | bytes 2752520 | tf_op jit(solution)/shard_map/ppermute | solution.py:89
  345.0 18.9 %collective-permute-start.54 = (bf16[128,2560]{1,0:T(8,128)(2,1)S(1)}, bf16[128,2560]{1,0:T(8,128)(2,1)S(1)}, u32[]{:S(2)}, u32[]{:S(2)}) collective-permute-start(bf16[128,2560]{1,0:T(8,128)(2,1)S(1)} %add_convert_fusion.8), channel_id=1, source_target_pairs={{8,0},{9,1},{10,2},{11,3},{12,4},{13,5},{14,6},{15,7},{16,24},{17,... | collective-permute-start | bytes 1966088 | tf_op jit(solution)/shard_map/ppermute | solution.py:89
  347.7 14.3 %collective-permute-start.55 = (bf16[112,2560]{1,0:T(8,128)(2,1)S(1)}, bf16[112,2560]{1,0:T(8,128)(2,1)S(1)}, u32[]{:S(2)}, u32[]{:S(2)}) collective-permute-start(bf16[112,2560]{1,0:T(8,128)(2,1)S(1)} %add_convert_fusion.15), channel_id=1, source_target_pairs={{8,16},{9,17},{10,18},{11,19},{12,20},{13,21},{14,22},{15,23},{16,... | collective-permute-start | bytes 1720328 | tf_op jit(solution)/shard_map/ppermute | solution.py:89
  350.7 11.3 %collective-permute-start.53 = (bf16[128,1664]{1,0:T(8,128)(2,1)}, bf16[128,1664]{1,0:T(8,128)(2,1)S(1)}, u32[]{:S(2)}, u32[]{:S(2)}) collective-permute-start(bf16[128,1664]{1,0:T(8,128)(2,1)} %add_convert_fusion.21), channel_id=1, source_target_pairs={{0,1},{1,0},{2,3},{3,2},{4,6},{5,7},{6,4},{7,5},{8,9},{9,8},{10,11... | collective-permute-start | bytes 1277960 | tf_op jit(solution)/shard_map/ppermute | solution.py:89
  365.2 13.8 %collective-permute-start.56 = (bf16[128,1664]{1,0:T(8,128)(2,1)S(1)}, bf16[128,1664]{1,0:T(8,128)(2,1)S(1)}, u32[]{:S(2)}, u32[]{:S(2)}) collective-permute-start(bf16[128,1664]{1,0:T(8,128)(2,1)S(1)} %add_convert_fusion.20), channel_id=1, source_target_pairs={{0,8},{1,9},{2,10},{3,11},{4,12},{5,13},{6,14},{7,15},{24,16},{25,... | collective-permute-start | bytes 1277960 | tf_op jit(solution)/shard_map/ppermute | solution.py:89
  370.7 17.5 %collective-permute-start.57 = (bf16[128,2560]{1,0:T(8,128)(2,1)S(1)}, bf16[128,2560]{1,0:T(8,128)(2,1)S(1)}, u32[]{:S(2)}, u32[]{:S(2)}) collective-permute-start(bf16[128,2560]{1,0:T(8,128)(2,1)S(1)} %broadcast_select_fusion.3), channel_id=1, source_target_pairs={{0,4},{1,5},{2,6},{3,7},{4,0},{5,1},{6,2},{7,3},{8,12},{9,13},{10,... | collective-permute-start | bytes 1966088 | tf_op jit(solution)/shard_map/ppermute | solution.py:89
  371.9 16.4 %collective-permute-start.58 = (bf16[112,2560]{1,0:T(8,128)(2,1)S(1)}, bf16[112,2560]{1,0:T(8,128)(2,1)S(1)}, u32[]{:S(2)}, u32[]{:S(2)}) collective-permute-start(bf16[112,2560]{1,0:T(8,128)(2,1)S(1)} %add_convert_fusion.14), channel_id=1, source_target_pairs={{8,0},{9,1},{10,2},{11,3},{12,4},{13,5},{14,6},{15,7},{16,24},{17,... | collective-permute-start | bytes 1720328 | tf_op jit(solution)/shard_map/ppermute | solution.py:89
  388.3 2.0 collective-permute-start.60
  388.5 0.7 collective-permute-start.59
  394.0 22.8 %collective-permute-start.61 = (bf16[128,1664]{1,0:T(8,128)(2,1)S(1)}, bf16[128,1664]{1,0:T(8,128)(2,1)S(1)}, u32[]{:S(2)}, u32[]{:S(2)}) collective-permute-start(bf16[128,1664]{1,0:T(8,128)(2,1)S(1)} %add_convert_fusion.18), channel_id=1, source_target_pairs={{8,0},{9,1},{10,2},{11,3},{12,4},{13,5},{14,6},{15,7},{16,24},{17,... | collective-permute-start | bytes 1277960 | tf_op jit(solution)/shard_map/ppermute | solution.py:89
  416.8 1.8 collective-permute-start.62
  (75 other events, 650.1 us)

commit v7 on v6

--- a/solution.py
+++ b/solution.py
@@ -94,7 +94,7 @@
     def swap(self, value):
         return self.move(value, lambda r, s: (r ^ 1, s))
 
-    def reduce(self, plan, name):
+    def reduce(self, plan, name, quick=False):
         got = yield self.swap(plan.have[name + ".given"])
         sums = [plan.have.pop(name + ".kept"), got]
         del plan.have[name + ".given"]
@@ -106,7 +106,19 @@
         chips = self.reps // 2
         place = lax.axis_index("rep") // 2
         span = 1
-        if chips % 4 == 0:
+        if chips % 4 == 0 and quick and value.shape[0] % 4 == 0:
+            quarter = value.shape[0] // 4
+            across = lambda value, j: self.move(value, lambda r, s: (r ^ (2 * j), s))
+            cut = lambda j: lax.dynamic_slice_in_dim(value, (place % 4 ^ j) * quarter, quarter, 0)
+            got = yield [across(cut(j), j) for j in range(1, 4)]
+            mine = total([cut(0)] + got)
+            got = yield [across(mine, j) for j in range(1, 4)]
+            parts = jnp.stack([mine] + got).reshape(2, 2, quarter, -1)
+            parts = jnp.where(place % 4 >= 2, parts[::-1], parts)
+            parts = jnp.where(place % 2 == 1, parts[:, ::-1], parts)
+            value = parts.reshape(4 * quarter, -1)
+            span = 4
+        elif chips % 4 == 0:
             inward, outward, middle = {0: 1, 3: 2}, {1: 0, 2: 3}, {1: 2, 2: 1}
 
             def along(value, table):
@@ -312,31 +324,26 @@
 
 
 def feed_kernel(counts, s0_ref, s1_ref, s2_ref, x_ref, attn_ref, cot_ref, gains_ref, *refs):
-    total = sum(counts)
+    total_count = sum(counts)
     attention_pieces = refs[: counts[0]]
     pair_pieces = refs[counts[0] : counts[0] + counts[1]]
-    down_pieces = refs[counts[0] + counts[1] : total]
-    out_ref, inner_ref, slopes_ref, act_t_ref, attn_t_ref, dy_ref, dres_ref, low_ref, dattn_ref = refs[
-        total : total + 9
-    ]
-    w_attn, w_pair, w_down, resid_ref, dact_ref, sems0, sems1, sems2 = refs[total + 9 :]
+    down_pieces = refs[counts[0] + counts[1] : total_count]
+    out_ref, inner_ref, slopes_ref, act_t_ref, attn_t_ref, dy_ref, resid_ref = refs[total_count : total_count + 7]
+    w_attn, w_pair, w_down, sum_ref, sems0, sems1, sems2 = refs[total_count + 7 :]
     attention_copies = load(attention_pieces, s0_ref, w_attn, sems0)
     pair_copies = load(pair_pieces, s1_ref, w_pair, sems1)
     down_copies = load(down_pieces, s2_ref, w_down, sems2)
     width = x_ref.shape[1]
     hidden = w_pair.shape[1]
     tile = hidden // 5
-    gain = gains_ref[1:2, :]
     x = upright(x_ref).astype(F32)
     dy_ref[...] = upright(cot_ref)
     attn_t_ref[...] = jnp.transpose(attn_ref[...])
     wait(attention_copies)
-    w_output = w_attn[width:, :width]
-    resid = x + nn(attn_ref[...], w_output)
+    resid = x + nn(attn_ref[...], w_attn[width:, :width])
     resid_ref[...] = resid
-    dres_ref[...] = resid
-    root = rms_inverse(resid)
-    act = (resid * root * gain).astype(BF)
+    sum_ref[...] = resid
+    act = (resid * rms_inverse(resid) * gains_ref[1:2, :]).astype(BF)
     act_t_ref[...] = jnp.transpose(act)
     wait(pair_copies)
     wait(down_copies)
@@ -350,28 +357,10 @@
         silu = gate * sigmoid
         inner = (silu * upper).astype(BF)
         inner_ref[here, :] = jnp.transpose(inner)
-        d_gate = (d_inner * upper * sigmoid * (1.0 + gate * (1.0 - sigmoid))).astype(BF)
-        d_upper = (d_inner * silu).astype(BF)
-        slopes_ref[0, :, here] = d_gate
-        slopes_ref[1, :, here] = d_upper
-        out = nn(inner, w_down[here, :])
-        d_act = nt(d_gate, w_pair[:width, here]) + nt(d_upper, w_pair[width:, here])
-        resid_ref[...] += out
-        if first == 0:
-            dact_ref[...] = d_act
-        else:
-            dact_ref[...] += d_act
-    lay_down(resid_ref[...].astype(BF), out_ref)
-    normed = dres_ref[...] * root
-    d_act = dact_ref[...]
-    d_normed = d_act * gain
-    d_resid = dy.astype(F32) + root * (
-        d_normed - normed * jnp.mean(d_normed * normed, axis=-1, keepdims=True)
-    )
-    dres_ref[...] = d_resid
-    low = d_resid.astype(BF)
-    low_ref[...] = low
-    dattn_ref[...] = nt(low, w_output).astype(BF)
+        slopes_ref[0, :, here] = (d_inner * upper * sigmoid * (1.0 + gate * (1.0 - sigmoid))).astype(BF)
+        slopes_ref[1, :, here] = (d_inner * silu).astype(BF)
+        sum_ref[...] += nn(inner, w_down[here, :])
+    lay_down(sum_ref[...].astype(BF), out_ref)
 
 
 def feed(x, attn, dy, gains, attention_got, pair_got, down_got):
@@ -389,24 +378,70 @@
         jax.ShapeDtypeStruct((width, tokens), BF),
         jax.ShapeDtypeStruct((tokens, width), BF),
         jax.ShapeDtypeStruct((tokens, width), F32),
-        jax.ShapeDtypeStruct((tokens, width), BF),
-        jax.ShapeDtypeStruct((tokens, width), BF),
     )
     every = [piece for pieces, _, _ in groups for piece in pieces]
     return pl.pallas_call(
         functools.partial(feed_kernel, counts),
         name="feed",
         in_specs=[IN_SMEM] * 3 + [IN_VMEM] * 4 + [ANYWHERE] * len(every),
-        out_specs=(IN_VMEM,) * 9,
+        out_specs=(IN_VMEM,) * 7,
         out_shape=outs,
         scratch_shapes=[pltpu.VMEM(shape, BF) for shape in shapes]
-        + [pltpu.VMEM((tokens, width), F32)] * 2
+        + [pltpu.VMEM((tokens, width), F32)]
         + [pltpu.SemaphoreType.DMA((count,)) for count in counts],
         cost_estimate=cost(
-            2 * tokens * width * (6 * hidden + 3 * width), tokens * hidden, x, x, x, *outs, *every
+            2 * tokens * width * (4 * hidden + width), tokens * hidden, x, x, x, *outs, *every
         ),
         compiler_params=pltpu.CompilerParams(vmem_limit_bytes=VMEM_MOST),
     )(*(starts for _, starts, _ in groups), x, attn, dy, gains, *every)
+
+
+def feed_back_kernel(counts, s0_ref, s1_ref, resid_ref, dy_ref, slopes_ref, gains_ref, *refs):
+    total_count = sum(counts)
+    dres_ref, low_ref, dattn_ref, w_attn, w_pair, sems0, sems1 = refs[total_count:]
+    pair_copies = load(refs[counts[0] : total_count], s1_ref, w_pair, sems1)
+    attention_copies = load(refs[: counts[0]], s0_ref, w_attn, sems0)
+    width = resid_ref.shape[1]
+    resid = resid_ref[...]
+    root = rms_inverse(resid)
+    normed = resid * root
+    wait(pair_copies)
+    d_act = nt(slopes_ref[0], w_pair[:width, :]) + nt(slopes_ref[1], w_pair[width:, :])
+    d_normed = d_act * gains_ref[1:2, :]
+    d_resid = dy_ref[...].astype(F32) + root * (
+        d_normed - normed * jnp.mean(d_normed * normed, axis=-1, keepdims=True)
+    )
+    dres_ref[...] = d_resid
+    low = d_resid.astype(BF)
+    low_ref[...] = low
+    wait(attention_copies)
+    dattn_ref[...] = nt(low, w_attn[width:, :width]).astype(BF)
+
+
+def feed_back(resid, dy, slopes, gains, attention_got, pair_got):
+    tokens, width = resid.shape
+    groups = [attention_got, pair_got]
+    counts = [len(pieces) for pieces, _, _ in groups]
+    shapes = [shape for _, _, shape in groups]
+    outs = (
+        jax.ShapeDtypeStruct((tokens, width), F32),
+        jax.ShapeDtypeStruct((tokens, width), BF),
+        jax.ShapeDtypeStruct((tokens, width), BF),
+    )
+    every = [piece for pieces, _, _ in groups for piece in pieces]
+    return pl.pallas_call(
+        functools.partial(feed_back_kernel, counts),
+        name="feed_back",
+        in_specs=[IN_SMEM] * 2 + [IN_VMEM] * 4 + [ANYWHERE] * len(every),
+        out_specs=(IN_VMEM,) * 3,
+        out_shape=outs,
+        scratch_shapes=[pltpu.VMEM(shape, BF) for shape in shapes]
+        + [pltpu.SemaphoreType.DMA((count,)) for count in counts],
+        cost_estimate=cost(
+            2 * tokens * width * (2 * shapes[1][1] + width), 0, resid, dy, slopes, *outs, *every
+        ),
+        compiler_params=pltpu.CompilerParams(vmem_limit_bytes=VMEM_MOST),
+    )(*(starts for _, starts, _ in groups), resid, dy, slopes, gains, *every)
 
 
 def pick_rows(source, starts_ref, base, rows, count, target):
@@ -530,12 +565,13 @@
     target[at : at + rows, KV_WIDTH:] = source[:, KV_WIDTH:]
 
 
-def attention_grad_kernel(shards, half, starts_ref, gain_ref, cos_ref, sin_ref, dq_ref, *refs):
+def attention_grad_kernel(shards, half, starts_ref, gain_ref, cos_ref, sin_ref, dq_ref, attn_ref, low_ref, *refs):
     xs, halves = refs[:shards], refs[shards : shards + 2]
     dkvs = [ref.at[t] for ref in halves for t in range(shards // 2)]
-    outs, (act, dkv, ordered) = refs[shards + 2 : shards + 4], refs[shards + 4 :]
+    outs, (act, dkv, ordered, attn_ordered) = refs[shards + 2 : shards + 4], refs[shards + 4 :]
     micro, width, rows = xs[0].shape
     tokens = micro * rows
+    wide = rounded_up(width)
     for t in range(shards):
         here = slice(t * tokens, (t + 1) * tokens)
         turn_keys(dkvs[t], dkv, t * tokens, cos_ref[here, :], sin_ref[here, :])
@@ -546,19 +582,23 @@
             act[:, first : first + rows] = (x * root * gain_ref[...]).astype(BF)
     for i, out_ref in enumerate(outs):
         pick_rows(act, starts_ref, i * shards, half, shards, ordered)
-        out_ref[:, :width] = nn(ordered[:, :tokens], dq_ref[...]).astype(BF)
-        start = rounded_up(width)
-        if start > width:
-            out_ref[:, width:start] = jnp.zeros((out_ref.shape[0], start - width), BF)
-        out_ref[:, start:] = nn(ordered[...], dkv[...]).astype(BF)
-
-
-def attention_grad(x_all, gain, cosine, sine, dq, dkv_all, half, given, kept):
+        pick_rows(attn_ref, starts_ref, i * shards, half, shards, attn_ordered)
+        for first, made in (
+            (0, nn(ordered[:, :tokens], dq_ref[...])),
+            (wide, nn(attn_ordered[...], low_ref[...])),
+        ):
+            out_ref[:, first : first + width] = made.astype(BF)
+            if wide > width:
+                out_ref[:, first + width : first + wide] = jnp.zeros((made.shape[0], wide - width), BF)
+        out_ref[:, 2 * wide :] = nn(ordered[...], dkv[...]).astype(BF)
+
+
+def attention_grad(x_all, gain, cosine, sine, dq, attn_t, low, dkv_all, half, given, kept):
     shards = len(x_all)
     micro, width, rows = x_all[0].shape
     every = shards * micro * rows
-    columns = rounded_up(width) + 2 * KV_WIDTH
-    out = jax.ShapeDtypeStruct((shards * half, columns), BF)
+    wide = rounded_up(width)
+    out = jax.ShapeDtypeStruct((shards * half, 2 * wide + 2 * KV_WIDTH), BF)
     if half % 16 or width // shards % 16:
         xs = jnp.concatenate([x[m] for x in x_all for m in range(micro)], axis=1).astype(F32)
         act = xs * lax.rsqrt(jnp.mean(xs * xs, axis=0, keepdims=True) + EPS) * gain
@@ -569,8 +609,9 @@
         first, second = keys[:, :, 0], keys[:, :, 1]
         keys = jnp.stack([first * c + second * s, second * c - first * s], axis=2)
         dkv = jnp.concatenate([keys.reshape(every, KV_WIDTH).astype(BF), dkv[:, KV_WIDTH:]], axis=1)
-        q = jnp.pad(nn(act[:, : micro * rows], dq), ((0, 0), (0, rounded_up(width) - width)))
-        grad = jnp.concatenate([q, nn(act, dkv)], axis=1).astype(BF)
+        space = ((0, 0), (0, wide - width))
+        parts = [jnp.pad(nn(act[:, : micro * rows], dq), space), jnp.pad(nn(attn_t, low), space), nn(act, dkv)]
+        grad = jnp.concatenate(parts, axis=1).astype(BF)
         return [
             jnp.concatenate([lax.dynamic_slice_in_dim(grad, start, half, 0) for start in starts])
             for starts in (given, kept)
@@ -578,19 +619,25 @@
     return pl.pallas_call(
         functools.partial(attention_grad_kernel, shards, half),
         name="attention_grad",
-        in_specs=[IN_SMEM] + [IN_VMEM] * (6 + shards),
+        in_specs=[IN_SMEM] + [IN_VMEM] * (8 + shards),
         out_specs=(IN_VMEM,) * 2,
         out_shape=(out, out),
         scratch_shapes=[
             pltpu.VMEM((width, every), BF),
             pltpu.VMEM((every, 2 * KV_WIDTH), BF),
             pltpu.VMEM((shards * half, every), BF),
+            pltpu.VMEM((shards * half, micro * rows), BF),
         ],
         cost_estimate=cost(
-            4 * shards * half * (every * 2 * KV_WIDTH + micro * rows * width), 0, *x_all, *dkv_all, out, out
+            4 * shards * half * (every * 2 * KV_WIDTH + 2 * micro * rows * width),
+            0,
+            *x_all,
+            *dkv_all,
+            out,
+            out,
         ),
         compiler_params=pltpu.CompilerParams(vmem_limit_bytes=VMEM_MOST),
-    )(numbers(given + kept), gain, cosine, sine, dq, *x_all, *dkv_all)
+    )(numbers(given + kept), gain, cosine, sine, dq, attn_t, low, *x_all, *dkv_all)
 
 
 def finish_kernel(count, starts_ref, x_ref, low_ref, kv_ref, dres_ref, gains_ref, cos_ref, sin_ref, *refs):
@@ -817,7 +864,6 @@
     down_mine = lax.dynamic_slice_in_dim(w_down, links.core * down_cut, down_cut, 0)
 
     attn_near = links.near(attn_mine)
-    pair_near = {1: links.step(pair_mine, 0)}
     gain_pieces = links.small_pieces(jnp.stack([norm_first, norm_second]))
     attn_mine, attn_near, gain_pieces, pair_mine, down_mine = meet(
         attn_mine, attn_near, gain_pieces, pair_mine, down_mine
@@ -826,7 +872,7 @@
     gains = links.in_order(gain_pieces).astype(F32)
     attn_all = links.far(attn_mine, attn_near)
     attn_swapped = {t: links.swap(attn_near[t]) for t in attn_near}
-    pair_later = {1 << i: links.step(pair_mine, i) for i in range(1, links.bits)}
+    pair_near = {1: links.step(pair_mine, 0)}
     own_down = with_layout_constraint(w_down, Layout(major_to_minor=(0, 1)))
     parents = parent_ids[:, 0]
     seg = jnp.arange(segs)
@@ -875,28 +921,27 @@
             (pair_place(1 - links.core, links.hops[links.twin(t)]), 0),
         ]
     attention_got = joined(pieces, starts, (2 * width, left.shape[1]))
-    pair_near |= pair_later
+    pair_near |= {1 << i: links.step(pair_mine, i) for i in range(1, links.bits)}
     pair_beside = {1: links.beside(pair_near[1])}
     down_near = {1: links.step(down_mine, 0)}
     queries, kv = project(inputs, gains, cosine, sine, *attention_got)
-    queries, kv, pair_mine, pair_near = meet(queries, kv, pair_mine, pair_near)
+    queries, kv, pair_mine, pair_near, pair_beside, down_mine, down_near = meet(
+        queries, kv, pair_mine, pair_near, pair_beside, down_mine, down_near
+    )
 
     kv_near = links.near(kv)
+    pair_beside |= {t: links.beside(pair_near[t]) for t in pair_near if t > 1}
+    kv_near, kv, pair_beside, pair_near, pair_mine = meet(kv_near, kv, pair_beside, pair_near, pair_mine)
+
+    kv_all = links.far(kv, kv_near)
     pair_all = links.far(pair_mine, pair_near)
-    pair_further = {t: links.beside(pair_near[t]) for t in pair_near if t > 1}
-    kv_near, kv, pair_beside, pair_near, down_near, down_mine = meet(
-        kv_near, kv, pair_beside, pair_near, down_near, down_mine
-    )
-
-    kv_all = links.far(kv, kv_near)
-    down_near |= {1 << i: links.step(down_mine, i) for i in range(1, links.bits)}
     pair_swapped = {t: links.swap(pair_near[t]) for t in pair_near}
     pair_crossed = {t: links.swap(pair_beside[t]) for t in pair_beside}
-    pair_beside |= pair_further
-    kv_all, pair_all, pair_swapped, pair_crossed, pair_beside = meet(
-        kv_all, pair_all, pair_swapped, pair_crossed, pair_beside
-    )
-
+    kv_all, pair_all, pair_swapped, pair_crossed, pair_beside, down_mine, down_near = meet(
+        kv_all, pair_all, pair_swapped, pair_crossed, pair_beside, down_mine, down_near
+    )
+
+    down_near |= {1 << i: links.step(down_mine, i) for i in range(1, links.bits)}
     down_all = links.far(down_mine, down_near)
     pair_beside |= {t: links.beside(pair_all[t]) for t in range(1, shards) if t not in pair_beside}
     attn, lse = attend(micro, seg_rows, queries, kv_all, bias)
@@ -932,7 +977,7 @@
     have = lambda *names: [plan.have[name] for name in names]
     x_near = links.near(inputs)
     made = feed(inputs, attn, cotangent, gains, attention_got, pair_got, down_got)
-    names = ("out", "inner", "slopes", "act", "attn_t", "dy", "d_resid", "d_resid_low", "d_attn")
+    names = ("out", "inner", "slopes", "act", "attn_t", "dy", "resid")
     plan.have = dict(zip(names, made)) | {"x_near": x_near, "queries": queries, "kv": kv_all, "lse": lse, "attn": attn}
     plan.close()
 
@@ -942,18 +987,14 @@
     wide_kept, wide_given = links.order(shard_rows, 0, 0)
     some_kept, some_given = links.order(shard_rows, output_mine, output_theirs)
 
-    inner, dy, attn_t, low = have("inner", "dy", "attn_t", "d_resid_low")
     plan.have["x_all"] = links.far(inputs, plan.have.pop("x_near"))
     plan.have["rows.given"], plan.have["rows.kept"] = rows_grad(
-        (
-            (inner, dy, down_half, down_given, down_kept),
-            (attn_t, low, output_half, some_given, some_kept),
-        )
+        ((*have("inner", "dy"), down_half, down_given, down_kept),)
     )
     plan.close()
 
     for name in ("rows", "wide0", "wide1", "some"):
-        plan.start(name, links.reduce(plan, name))
+        plan.start(name, links.reduce(plan, name, name == "some"))
     plan.advance("rows")
     cuts = (-(-shard_rows // 32) * 16, shard_rows - -(-shard_rows // 32) * 16)
     act, slopes = have("act", "slopes")
@@ -962,8 +1003,14 @@
     plan.have |= dict(zip(names, made))
     plan.close()
 
+    plan.advance("rows", "wide0", "wide1")
+    names = ("d_resid", "d_resid_low", "d_attn")
+    made = feed_back(*have("resid", "dy", "slopes"), gains, attention_got, pair_got)
+    plan.have |= dict(zip(names, made))
+    plan.close()
+
     made = ()
-    hops = [("rows", "wide0", "wide1"), ("rows", "wide0")]
+    hops = [("rows", "wide0"), ("rows", "wide0", "wide1")]
     for m in range(micro):
         plan.advance(*hops[min(m, 1)])
         q, kv_now, o, do, lse_now = have("queries", "kv", "attn", "d_attn", "lse")
@@ -976,9 +1023,18 @@
     plan.have["dkv.pieces"] = d_kv
     plan.have["d_queries"] = d_queries
     plan.start("dkv", links.collect(plan, "dkv"))
-    plan.advance("rows", "wide0", "wide1")
+    plan.advance("dkv", "wide0", "wide1", "rows")
     given, kept = attention_grad(
-        plan.have["x_all"], gains[0][:, None], cosine, sine, d_queries, d_kv, output_half, some_given, some_kept
+        plan.have["x_all"],
+        gains[0][:, None],
+        cosine,
+        sine,
+        d_queries,
+        *have("attn_t", "d_resid_low"),
+        d_kv,
+        output_half,
+        some_given,
+        some_kept,
     )
     plan.have["some.given"], plan.have["some.kept"] = given, kept
     plan.close()
@@ -995,8 +1051,7 @@
             )
         if "rows" in have and "down" not in done:
             value, other = have["rows"]
-            done["down"] = links.finish_rows(value[:down_half, :width], other[:down_half, :width], own)
-            done["output"] = links.finish_rows(value[down_half:, :width], other[down_half:, :width], shard_rows)
+            done["down"] = links.finish_rows(value[:, :width], other[:, :width], own)
         if "wide0" in have and "wide1" in have and "gate" not in done:
             halves = [links.finish_pair(*have[name]) for name in ("wide0", "wide1")]
             done["gate"], done["upper"] = (jnp.concatenate(parts, axis=0) for parts in zip(*halves))
@@ -1004,8 +1059,8 @@
         if "some" in have and "query" not in done:
             grad = links.finish_rows(*have["some"], shard_rows)
             first = rounded_up(width)
-            done["query"], done["key"] = grad[:, :width], grad[:, first : first + KV_WIDTH]
-            done["value"] = grad[:, first + KV_WIDTH :]
+            done["query"], done["output"] = grad[:, :width], grad[:, first : first + width]
+            done["key"], done["value"] = jnp.split(grad[:, 2 * first :], 2, axis=1)
             done["gain_one"] = gain_grad(
                 norm_first,
                 (w_query, done["query"]),
@@ -1013,7 +1068,7 @@
                 (value_weight, done["value"]),
             )
 
-    order = [("rows", "wide0", "wide1", "some", "dkv")] * 5 + [("wide1", "some")]
+    order = [("rows", "wide0", "wide1", "dkv", "some")]
     while plan.tasks:
         plan.advance(*(order.pop(0) if order else tuple(plan.tasks)))
         settle()

time: 434 us -> 430 us (level)
  Pallas kernels: 129 us -> 139 us
  waiting for transfers between devices: 123 us -> 113 us
  starting transfers between devices: 78.5 us -> 70.9 us
  other arithmetic: 53.5 us -> 60 us
    pallas_call x0 -> x1, Pallas kernels: none -> 17 us  [feed_back(): pl.pallas_call(functools.partial(feed_back_kernel, counts), name='feed_ba...]
    ppermute x63 -> x66, waiting for transfers between devices: 123 us -> 113 us  [move(): return lax.ppermute(value, AXES, pairs)]
    ppermute x63 -> x66, starting transfers between devices: 78.5 us -> 70.9 us  [move(): return lax.ppermute(value, AXES, pairs)]
    pallas_call x1, Pallas kernels: 33.7 us -> 26.4 us  [feed(): pl.pallas_call(functools.partial(feed_kernel, counts), name='feed', in_sp...]
    unnamed x159 -> x153, local copies, waits for them, and re-layouts: 26.2 us -> 23.8 us
    convert_element_type x21 -> x20, other arithmetic: 33.1 us -> 35 us  [total(): return sum((part.astype(F32) for part in parts)).astype(parts[0].dtype)]
  transfers between devices with their start and end apart: 63 -> 66, of which waited for: 19 -> 22; matrix products, arithmetic and copies ran while one was open for 12% -> 12% of each run, Pallas kernels for 30% -> 33%
where the time goes in v7:
time: 430 us; the launch traced here: 422 us
  Pallas kernels  139 us (32%)
  waiting for transfers between devices  113 us (26%)
  starting transfers between devices  70.9 us (16%)
  other arithmetic  60 us (14%)
  local copies, waits for them, and re-layouts  37.2 us (9%)
    ppermute x66, waiting for transfers between devices, move(): return lax.ppermute(value, AXES, pairs)  113 us
    ppermute x66, starting transfers between devices, move(): return lax.ppermute(value, AXES, pairs)  70.9 us
    convert_element_type x20, other arithmetic, total(): return sum((part.astype(F32) for part in parts)).astype(parts[0].dtype)  35 us
    pallas_call x2, Pallas kernels, attend_back(): pl.pallas_call(functools.partial(attend_back_kernel, shards, seg_rows), g...  34.3 us
    pallas_call x1, Pallas kernels, feed(): pl.pallas_call(functools.partial(feed_kernel, counts), name='feed', in_sp...  26.4 us
    unnamed x153, local copies, waits for them, and re-layouts  23.8 us
    pallas_call x1, Pallas kernels, feed_back(): pl.pallas_call(functools.partial(feed_back_kernel, counts), name='feed_ba...  17 us
    pallas_call x1, Pallas kernels, attend(): pl.pallas_call(functools.partial(attend_kernel, shards, seg_rows), grid=(...  16.7 us
  transfers between devices with their start and end apart: 66, of which 22 were waited for; matrix products, arithmetic and copies ran while one was open for 12% of the time, Pallas kernels for 33%

profile of v7, /device:TPU:0, one launch (start us, length us, event | category | flops | bytes accessed | tf_op | source)
XLA Modules:
  0.0 422.0 jit_solution(13157799363845340131)
XLA Ops:
  2.9 2.4 broadcast_select_fusion.7
  5.4 3.0 collective-permute-start
  8.4 1.5 collective-permute-start.1
  10.6 2.9 collective-permute-start.4
  13.6 2.4 copy.73.refs_22_
  17.5 2.0 constant_dynamic-slice_fusion.3
  19.5 2.2 dynamic-slice_select_fusion
  25.3 2.0 collective-permute-start.8
  27.6 11.8 %collective-permute-done.5.refs_6_ = bf16[240,1280]{1,0:T(8,128)(2,1)S(1)} collective-permute-done((bf16[240,1280]{1,0:T(8,128)(2,1)S(1)}, bf16[240,1280]{1,0:T(8,128)(2,1)S(1)}, u32[]{:S(2)}, u32[]{:S(2)}) %collective-permute-start.5) | collective-permute-done | bytes 614432 | tf_op jit(solution)/shard_map/ppermute | solution.py:89
  43.3 3.1 collective-permute-start.11
  46.4 2.2 collective-permute-start.12
  48.7 2.6 copy.77.cos_ref
  51.3 2.5 copy.78.sin_ref
  56.0 6.6 %project.1 = (bf16[512,960]{1,0:T(8,128)(2,1)}, bf16[512,640]{1,0:T(8,128)(2,1)S(1)}) custom-call(s32[16]{0:T(128)S(1)} %stack.203.starts_ref.s0_ref, bf16[2,960,256]{2,1,0:T(8,128)(2,1)} %bitcast.17.x_ref.refs_0_, f32[2,960]{1,0:T(2,128)S(1)} %maximum_convert_fusion.7.gains_ref, f32[2048,128]{1,0:T(8,128)} %copy.77.cos_ref, f32[2048,128]{1,0:T(8,128)} %copy.78.sin_ref, ...), custom_call_target="tpu_custom_call" | custom-call | flops 1572864000 | bytes 7536640 | tf_op jit(solution)/shard_map/project/pallas_call | solution.py:313
  64.0 1.6 collective-permute-start.15
  65.6 14.1 %collective-permute-done.15.refs_15_ = bf16[240,1280]{1,0:T(8,128)(2,1)S(1)} collective-permute-done((bf16[240,1280]{1,0:T(8,128)(2,1)}, bf16[240,1280]{1,0:T(8,128)(2,1)S(1)}, u32[]{:S(2)}, u32[]{:S(2)}) %collective-permute-start.15) | collective-permute-done | bytes 614432 | tf_op jit(solution)/shard_map/ppermute | solution.py:89
  82.3 7.8 %collective-permute-done.17.refs_18_ = bf16[240,1280]{1,0:T(8,128)(2,1)S(1)} collective-permute-done((bf16[240,1280]{1,0:T(8,128)(2,1)}, bf16[240,1280]{1,0:T(8,128)(2,1)S(1)}, u32[]{:S(2)}, u32[]{:S(2)}) %collective-permute-start.17) | collective-permute-done | bytes 614432 | tf_op jit(solution)/shard_map/ppermute | solution.py:89
  90.2 2.0 collective-permute-done.21.refs_17_
  92.2 5.0 %collective-permute-done.16.refs_3_ = bf16[512,640]{1,0:T(8,128)(2,1)S(1)} collective-permute-done((bf16[512,640]{1,0:T(8,128)(2,1)S(1)}, bf16[512,640]{1,0:T(8,128)(2,1)S(1)}, u32[]{:S(2)}, u32[]{:S(2)}) %collective-permute-start.16) | collective-permute-done | bytes 655392 | tf_op jit(solution)/shard_map/ppermute | solution.py:89
  98.9 1.7 collective-permute-start.23
  101.9 16.7 %attend.1 = (bf16[512,960]{1,0:T(8,128)(2,1)S(1)}, f32[512,128]{1,0:T(8,128)S(1)}) custom-call(bf16[512,960]{1,0:T(8,128)(2,1)S(1)} %copy-done.24, bf16[512,640]{1,0:T(8,128)(2,1)S(1)} %get-tuple-element.484.refs_0_, bf16[512,640]{1,0:T(8,128)(2,1)S(1)} %collective-permute-done.13.refs_1_, bf16[512,640]{1,0:T(8,128)(2,1)S(1)} %collective-permute-done.14.refs_2_, ...), custom_call_target="tpu_custom_call" | custom-call | flops 8053063680 | bytes 983040 | tf_op jit(solution)/shard_map/attend/pallas_call | solution.py:791
  126.5 26.4 %feed.1 = (bf16[2,960,256]{2,1,0:T(8,128)(2,1)}, bf16[2560,512]{1,0:T(8,128)(2,1)}, bf16[2,512,2560]{2,1,0:T(8,128)(2,1)}, bf16[960,512]{1,0:T(8,128)(2,1)}, bf1...) custom-call(s32[16]{0:T(128)} %copy-done.22, s32[28]{0:T(128)} %stack.206.s1_ref, ...), custom_call_target="tpu_custom_call" | custom-call | flops 11010048000 | bytes 36372480 | tf_op jit(solution)/shard_map/feed/pallas_call | solution.py:383
  155.2 6.8 %rows_grad.1 = (bf16[1280,1024]{1,0:T(8,128)(2,1)}, bf16[1280,1024]{1,0:T(8,128)(2,1)}) custom-call(s32[8]{0:T(128)S(1)} %stack.226.starts_ref, bf16[2560,512]{1,0:T(8,128)(2,1)} %get-tuple-element.396.refs_0_, bf16[512,960]{1,0:T(8,128)(2,1)S(1)} %copy-done.17), custom_call_target="tpu_custom_call" | custom-call | flops 2516582400 | bytes 8847360 | tf_op jit(solution)/shard_map/rows_grad/pallas_call | solution.py:489
  162.1 5.1 %collective-permute-done.32.refs_3_ = bf16[2,960,256]{2,1,0:T(8,128)(2,1)} collective-permute-done((bf16[2,960,256]{2,1,0:T(8,128)(2,1)S(1)}, bf16[2,960,256]{2,1,0:T(8,128)(2,1)}, u32[]{:S(2)}, u32[]{:S(2)}) %collective-permute-start.32) | collective-permute-done | bytes 983072 | tf_op jit(solution)/shard_map/ppermute | solution.py:89
  167.3 9.0 %wide_grad.1 = (bf16[512,2560]{1,0:T(8,128)(2,1)}, bf16[448,2560]{1,0:T(8,128)(2,1)}, bf16[512,2560]{1,0:T(8,128)(2,1)}, bf16[448,2560]{1,0:T(8,128)(2,1)S(1)}) custom-call(s32[10]{0:T(128)S(1)} %stack.232.info_ref, bf16[960,512]{1,0:T(8,128)(2,1)S(1)} %copy-done.34, bf16[2,512,2560]{2,1,0:T(8,128)(2,1)} %get-tuple-element.437.given_ref.kept_ref.slopes_ref, ...), custom_call_target="tpu_custom_call" | custom-call | flops 5033164800 | bytes 16056320 | tf_op jit(solution)/shard_map/wide_grad/pallas_call | solution.py:539
  176.9 3.0 add_convert_fusion.2
  180.2 17.0 %feed_back.1 = (f32[512,960]{1,0:T(8,128)}, bf16[512,960]{1,0:T(8,128)(2,1)}, bf16[512,960]{1,0:T(8,128)(2,1)}) custom-call(s32[16]{0:T(128)} %copy-done.22, s32[28]{0:T(128)} %stack.206.s1_ref, f32[512,960]{1,0:T(8,128)} %get-tuple-element.435.resid_ref, bf16[512,960]{1,0:T(8,128)(2,1)} %get-tuple-element.436.refs_1_.dy_ref, ...), custom_call_target="tpu_custom_call" | custom-call | flops 5976883200 | bytes 26869760 | tf_op jit(solution)/shard_map/feed_back/pallas_call | solution.py:432
  197.8 3.1 add_convert_fusion.1
  202.0 2.2 multiply_sine_fusion
  204.9 2.0 add_convert_fusion.15
  210.9 17.0 %attend_back.2 = (bf16[512,960]{1,0:T(8,128)(2,1)S(1)}, bf16[2,512,640]{2,1,0:T(8,128)(2,1)}, bf16[2,512,640]{2,1,0:T(8,128)(2,1)}) custom-call(bf16[512,960]{1,0:T(8,128)(2,1)S(1)} %copy-done.25, bf16[512,640]{1,0:T(8,128)(2,1)S(1)} %copy-done.27, bf16[512,640]{1,0:T(8,128)(2,1)S(1)} %copy-done.29, bf16[512,640]{1,0:T(8,128)(2,1)S(1)} %copy-done.31, ...), custom_call_target="tpu_custom_call" | custom-call | flops 10066329600 | bytes 983040 | tf_op jit(solution)/shard_map/attend_back/pallas_call | solution.py:813
  228.0 2.0 add_convert_fusion.14
  230.0 3.8 collective-permute-start.39
  233.7 1.5 add_convert_fusion.3
  236.5 1.5 add_convert_fusion.13
  238.3 17.3 %attend_back.3 = (bf16[512,960]{1,0:T(8,128)(2,1)S(1)}, bf16[2,512,640]{2,1,0:T(8,128)(2,1)}, bf16[2,512,640]{2,1,0:T(8,128)(2,1)}) custom-call(bf16[512,960]{1,0:T(8,128)(2,1)S(1)} %copy-done.25, bf16[512,640]{1,0:T(8,128)(2,1)S(1)} %copy-done.27, bf16[512,640]{1,0:T(8,128)(2,1)S(1)} %copy-done.29, ...), custom_call_target="tpu_custom_call", output_to_operand_aliasing={{0}: (11, {}), {1}: (12, {}), {2}: (13, {})} | custom-call | flops 10066329600 | bytes 983040 | tf_op jit(solution)/shard_map/attend_back/pallas_call | solution.py:813
  255.7 2.5 collective-permute-done.41
  259.6 1.5 collective-permute-start.43
  261.1 2.5 add_convert_fusion.11
  263.6 4.1 collective-permute-start.44
  271.1 13.2 %attention_grad.1 = (bf16[512,2688]{1,0:T(8,128)(2,1)}, bf16[512,2688]{1,0:T(8,128)(2,1)}) custom-call(s32[8]{0:T(128)} %stack.241.starts_ref, f32[960,1]{1,0:T(8,128)} %copy.79.gain_ref, f32[2048,128]{1,0:T(8,128)} %copy.77.cos_ref, f32[2048,128]{1,0:T(8,128)} %copy.78.sin_ref, bf16[512,960]{1,0:T(8,128)(2,1)} %copy-done.16, ...), custom_call_target="tpu_custom_call" | custom-call | flops 4697620480 | bytes 12058624 | tf_op jit(solution)/shard_map/attention_grad/pallas_call | solution.py:619
  284.5 2.3 add_convert_fusion.10
  290.5 2.3 add_convert_fusion.8
  295.8 6.3 %collective-permute-start.50 = (bf16[112,2560]{1,0:T(8,128)(2,1)S(1)}, bf16[112,2560]{1,0:T(8,128)(2,1)S(1)}, u32[]{:S(2)}, u32[]{:S(2)}) collective-permute-start(bf16[112,2560]{1,0:T(8,128)(2,1)S(1)} %add_convert_fusion.18), channel_id=1, source_target_pairs={{0,8},{1,9},{2,10},{3,11},{4,12},{5,13},{6,14},{7,15},{24,16},{25,... | collective-permute-start | bytes 1720328 | tf_op jit(solution)/shard_map/ppermute | solution.py:89
  302.1 12.0 %collective-permute-done.50 = bf16[112,2560]{1,0:T(8,128)(2,1)S(1)} collective-permute-done((bf16[112,2560]{1,0:T(8,128)(2,1)S(1)}, bf16[112,2560]{1,0:T(8,128)(2,1)S(1)}, u32[]{:S(2)}, u32[]{:S(2)}) %collective-permute-start.50) | collective-permute-done | bytes 573472 | tf_op jit(solution)/shard_map/ppermute | solution.py:89
  316.2 2.1 add_convert_fusion
  319.2 1.5 add_convert_fusion.6
  323.3 1.8 fusion.kv_ref
  325.2 9.1 %finish.1 = bf16[2,960,256]{2,1,0:T(8,128)(2,1)} custom-call(s32[16]{0:T(128)S(1)} %copy-done.23, bf16[2,960,256]{2,1,0:T(8,128)(2,1)} %bitcast.17.x_ref.refs_0_, bf16[512,960]{1,0:T(8,128)(2,1)} %copy-done.16, bf16[512,640]{1,0:T(8,128)(2,1)S(1)} %fusion.kv_ref, f32[512,960]{1,0:T(8,128)} %get-tuple-element.534.dres_ref, f32[2,960]{1,0:T(2,128)S(1)} %copy-done.21, ...), custom_call_target="tpu_custom_call" | custom-call | flops 1572864000 | bytes 8847360 | tf_op jit(solution)/shard_map/finish/pallas_call | solution.py:665
  334.3 5.1 %collective-permute-done.53 = bf16[128,2560]{1,0:T(8,128)(2,1)S(1)} collective-permute-done((bf16[128,2560]{1,0:T(8,128)(2,1)S(1)}, bf16[128,2560]{1,0:T(8,128)(2,1)S(1)}, u32[]{:S(2)}, u32[]{:S(2)}) %collective-permute-start.53) | collective-permute-done | bytes 655392 | tf_op jit(solution)/shard_map/ppermute | solution.py:89
  339.5 2.9 add_convert_fusion.5
  346.5 16.3 %collective-permute-done.57 = bf16[112,2560]{1,0:T(8,128)(2,1)} collective-permute-done((bf16[112,2560]{1,0:T(8,128)(2,1)}, bf16[112,2560]{1,0:T(8,128)(2,1)}, u32[]{:S(2)}, u32[]{:S(2)}) %collective-permute-start.57) | collective-permute-done | bytes 573472 | tf_op jit(solution)/shard_map/ppermute | solution.py:89
  362.8 1.9 broadcast_select_fusion.10
  364.8 1.9 add_convert_fusion.4
  367.5 3.2 collective-permute-start.59
  371.9 6.0 %collective-permute-done.58 = bf16[32,2688]{1,0:T(8,128)(2,1)S(1)} collective-permute-done((bf16[32,2688]{1,0:T(8,128)(2,1)}, bf16[32,2688]{1,0:T(8,128)(2,1)S(1)}, u32[]{:S(2)}, u32[]{:S(2)}) %collective-permute-start.58) | collective-permute-done | bytes 172064 | tf_op jit(solution)/shard_map/ppermute | solution.py:89
  377.8 5.7 %collective-permute-done.59 = bf16[32,2688]{1,0:T(8,128)(2,1)} collective-permute-done((bf16[32,2688]{1,0:T(8,128)(2,1)}, bf16[32,2688]{1,0:T(8,128)(2,1)}, u32[]{:S(2)}, u32[]{:S(2)}) %collective-permute-start.59) | collective-permute-done | bytes 172064 | tf_op jit(solution)/shard_map/ppermute | solution.py:89
  386.8 1.7 maximum_convert_fusion.2
  388.9 1.7 maximum_convert_fusion.3
  391.7 3.9 collective-permute-start.62
  398.7 3.8 collective-permute-done.62
  402.5 8.8 %collective-permute-done.63 = bf16[32,2688]{1,0:T(8,128)(2,1)S(1)} collective-permute-done((bf16[32,2688]{1,0:T(8,128)(2,1)S(1)}, bf16[32,2688]{1,0:T(8,128)(2,1)S(1)}, u32[]{:S(2)}, u32[]{:S(2)}) %collective-permute-start.63) | collective-permute-done | bytes 172064 | tf_op jit(solution)/shard_map/ppermute | solution.py:89
  411.7 2.1 collective-permute-done.65
  419.2 2.0 copy.88
  (320 shorter events, 77.5 us)
Async XLA Ops:
  5.4 18.4 %collective-permute-start = (bf16[240,1280]{1,0:T(8,128)(2,1)}, bf16[240,1280]{1,0:T(8,128)(2,1)S(1)}, u32[]{:S(2)}, u32[]{:S(2)}) collective-permute-start(bf16[240,1280]{1,0:T(8,128)(2,1)} %get-tuple-element.631), channel_id=1, source_target_pairs={{0,1},{1,0},{2,3},{3,2},{4,6},{5,7},{6,4},{7,5},{8,9},{9,8},{10,11... | collective-permute-start | bytes 1843208 | tf_op jit(solution)/shard_map/ppermute | solution.py:89
  8.4 15.4 %collective-permute-start.1 = (bf16[240,1280]{1,0:T(8,128)(2,1)}, bf16[240,1280]{1,0:T(8,128)(2,1)S(1)}, u32[]{:S(2)}, u32[]{:S(2)}) collective-permute-start(bf16[240,1280]{1,0:T(8,128)(2,1)} %get-tuple-element.631), channel_id=1, source_target_pairs={{0,2},{1,3},{2,0},{3,1},{4,5},{5,4},{6,7},{7,6},{8,10},{9,11},{10,... | collective-permute-start | bytes 1843208 | tf_op jit(solution)/shard_map/ppermute | solution.py:89
  10.0 12.9 %collective-permute-start.2 = (bf16[2,240]{1,0:T(2,128)(2,1)S(1)}, bf16[2,240]{1,0:T(2,128)(2,1)S(1)}, u32[]{:S(2)}, u32[]{:S(2)}) collective-permute-start(bf16[2,240]{1,0:T(2,128)(2,1)S(1)} %pad_maximum_fusion.5), channel_id=1, source_target_pairs={{0,1},{1,0},{2,3},{3,2},{4,5},{5,4},{6,7},{7,6},{8,9},{9,8},{10,11... | collective-permute-start | bytes 2888 | tf_op jit(solution)/shard_map/ppermute | solution.py:89
  10.6 12.3 %collective-permute-start.3 = (bf16[2,240]{1,0:T(2,128)(2,1)S(1)}, bf16[2,240]{1,0:T(2,128)(2,1)S(1)}, u32[]{:S(2)}, u32[]{:S(2)}) collective-permute-start(bf16[2,240]{1,0:T(2,128)(2,1)S(1)} %pad_maximum_fusion.5), channel_id=1, source_target_pairs={{0,2},{1,3},{2,0},{3,1},{4,6},{5,7},{6,4},{7,5},{8,10},{9,11},{10,... | collective-permute-start | bytes 2888 | tf_op jit(solution)/shard_map/ppermute | solution.py:89
  10.6 13.2 %collective-permute-start.4 = (bf16[2,240]{1,0:T(2,128)(2,1)S(1)}, bf16[2,240]{1,0:T(2,128)(2,1)S(1)}, u32[]{:S(2)}, u32[]{:S(2)}) collective-permute-start(bf16[2,240]{1,0:T(2,128)(2,1)S(1)} %pad_maximum_fusion.5), channel_id=1, source_target_pairs={{0,3},{1,2},{2,1},{3,0},{4,7},{5,6},{6,5},{7,4},{8,11},{9,10},{10,... | collective-permute-start | bytes 2888 | tf_op jit(solution)/shard_map/ppermute | solution.py:89
  23.8 15.6 %collective-permute-start.5 = (bf16[240,1280]{1,0:T(8,128)(2,1)S(1)}, bf16[240,1280]{1,0:T(8,128)(2,1)S(1)}, u32[]{:S(2)}, u32[]{:S(2)}) collective-permute-start(bf16[240,1280]{1,0:T(8,128)(2,1)S(1)} %collective-permute-done.refs_2_), channel_id=1, source_target_pairs={{0,2},{1,3},{2,0},{3,1},{4,5},{5,4},{6,7},{7,6},{8,10},{9,11},{10,... | collective-permute-start | bytes 1843208 | tf_op jit(solution)/shard_map/ppermute | solution.py:89
  24.5 14.9 %collective-permute-start.6 = (bf16[240,1280]{1,0:T(8,128)(2,1)S(1)}, bf16[240,1280]{1,0:T(8,128)(2,1)S(1)}, u32[]{:S(2)}, u32[]{:S(2)}) collective-permute-start(bf16[240,1280]{1,0:T(8,128)(2,1)S(1)} %collective-permute-done.refs_2_), channel_id=1, source_target_pairs={{0,4},{1,5},{2,6},{3,7},{4,0},{5,1},{6,2},{7,3},{8,12},{9,13},{10,... | collective-permute-start | bytes 1843208 | tf_op jit(solution)/shard_map/ppermute | solution.py:89
  25.3 14.9 %collective-permute-start.7 = (bf16[240,1280]{1,0:T(8,128)(2,1)S(1)}, bf16[240,1280]{1,0:T(8,128)(2,1)S(1)}, u32[]{:S(2)}, u32[]{:S(2)}) collective-permute-start(bf16[240,1280]{1,0:T(8,128)(2,1)S(1)} %collective-permute-done.1.refs_4_), channel_id=1, source_target_pairs={{0,4},{1,5},{2,6},{3,7},{4,0},{5,1},{6,2},{7,3},{8,12},{9,13},{10,... | collective-permute-start | bytes 1843208 | tf_op jit(solution)/shard_map/ppermute | solution.py:89
  25.3 15.8 %collective-permute-start.8 = (bf16[240,1280]{1,0:T(8,128)(2,1)}, bf16[240,1280]{1,0:T(8,128)(2,1)}, u32[]{:S(2)}, u32[]{:S(2)}) collective-permute-start(bf16[240,1280]{1,0:T(8,128)(2,1)} %dynamic-slice_select_fusion), channel_id=1, source_target_pairs={{0,1},{1,0},{2,3},{3,2},{4,6},{5,7},{6,4},{7,5},{8,9},{9,8},{10,11... | collective-permute-start | bytes 1843208 | tf_op jit(solution)/shard_map/ppermute | solution.py:89
  43.2 10.6 %collective-permute-start.9 = (bf16[240,1280]{1,0:T(8,128)(2,1)S(1)}, bf16[240,1280]{1,0:T(8,128)(2,1)}, u32[]{:S(2)}, u32[]{:S(2)}) collective-permute-start(bf16[240,1280]{1,0:T(8,128)(2,1)S(1)} %collective-permute-done.5.refs_6_), channel_id=1, source_target_pairs={{0,4},{1,5},{2,6},{3,7},{4,0},{5,1},{6,2},{7,3},{8,12},{9,13},{10,... | collective-permute-start | bytes 1843208 | tf_op jit(solution)/shard_map/ppermute | solution.py:89
  43.2 20.0 %collective-permute-start.10 = (bf16[240,1280]{1,0:T(8,128)(2,1)}, bf16[240,1280]{1,0:T(8,128)(2,1)}, u32[]{:S(2)}, u32[]{:S(2)}) collective-permute-start(bf16[240,1280]{1,0:T(8,128)(2,1)} %dynamic-slice_select_fusion), channel_id=1, source_target_pairs={{0,2},{1,3},{2,0},{3,1},{4,5},{5,4},{6,7},{7,6},{8,10},{9,11},{10,... | collective-permute-start | bytes 1843208 | tf_op jit(solution)/shard_map/ppermute | solution.py:89
  43.3 19.9 %collective-permute-start.11 = (bf16[240,1280]{1,0:T(8,128)(2,1)}, bf16[240,1280]{1,0:T(8,128)(2,1)}, u32[]{:S(2)}, u32[]{:S(2)}) collective-permute-start(bf16[240,1280]{1,0:T(8,128)(2,1)} %collective-permute-done.8.refs_10_), channel_id=1, source_target_pairs={{0,8},{1,9},{2,10},{3,11},{4,12},{5,13},{6,14},{7,15},{8,0},{9,1},... | collective-permute-start | bytes 1843208 | tf_op jit(solution)/shard_map/ppermute | solution.py:89
  46.4 16.9 %collective-permute-start.12 = (bf16[320,960]{1,0:T(8,128)(2,1)}, bf16[320,960]{1,0:T(8,128)(2,1)}, u32[]{:S(2)}, u32[]{:S(2)}) collective-permute-start(bf16[320,960]{1,0:T(8,128)(2,1)} %constant_dynamic-slice_fusion.3), channel_id=1, source_target_pairs={{0,1},{1,0},{2,3},{3,2},{4,6},{5,7},{6,4},{7,5},{8,9},{9,8},{10,11... | collective-permute-start | bytes 1843208 | tf_op jit(solution)/shard_map/ppermute | solution.py:89
  63.3 16.5 %collective-permute-start.13 = (bf16[512,640]{1,0:T(8,128)(2,1)S(1)}, bf16[512,640]{1,0:T(8,128)(2,1)S(1)}, u32[]{:S(2)}, u32[]{:S(2)}) collective-permute-start(bf16[512,640]{1,0:T(8,128)(2,1)S(1)} %get-tuple-element.484.refs_0_), channel_id=1, source_target_pairs={{0,1},{1,0},{2,3},{3,2},{4,6},{5,7},{6,4},{7,5},{8,9},{9,8},{10,11... | collective-permute-start | bytes 1966088 | tf_op jit(solution)/shard_map/ppermute | solution.py:89
  63.4 16.4 %collective-permute-start.14 = (bf16[512,640]{1,0:T(8,128)(2,1)S(1)}, bf16[512,640]{1,0:T(8,128)(2,1)S(1)}, u32[]{:S(2)}, u32[]{:S(2)}) collective-permute-start(bf16[512,640]{1,0:T(8,128)(2,1)S(1)} %get-tuple-element.484.refs_0_), channel_id=1, source_target_pairs={{0,2},{1,3},{2,0},{3,1},{4,5},{5,4},{6,7},{7,6},{8,10},{9,11},{10,... | collective-permute-start | bytes 1966088 | tf_op jit(solution)/shard_map/ppermute | solution.py:89
  64.0 15.7 %collective-permute-start.15 = (bf16[240,1280]{1,0:T(8,128)(2,1)}, bf16[240,1280]{1,0:T(8,128)(2,1)S(1)}, u32[]{:S(2)}, u32[]{:S(2)}) collective-permute-start(bf16[240,1280]{1,0:T(8,128)(2,1)} %collective-permute-done.10.refs_14_), channel_id=1, source_target_pairs={{0,8},{1,9},{2,10},{3,11},{4,12},{5,13},{6,14},{7,15},{8,0},{9,1},... | collective-permute-start | bytes 1843208 | tf_op jit(solution)/shard_map/ppermute | solution.py:89
  79.7 10.4 %collective-permute-start.17 = (bf16[240,1280]{1,0:T(8,128)(2,1)}, bf16[240,1280]{1,0:T(8,128)(2,1)S(1)}, u32[]{:S(2)}, u32[]{:S(2)}) collective-permute-start(bf16[240,1280]{1,0:T(8,128)(2,1)} %collective-permute-done.8.refs_10_), channel_id=1, source_target_pairs={{0,2},{1,3},{2,0},{3,1},{4,5},{5,4},{6,7},{7,6},{8,10},{9,11},{10,... | collective-permute-start | bytes 1843208 | tf_op jit(solution)/shard_map/ppermute | solution.py:89
  80.8 16.4 %collective-permute-start.16 = (bf16[512,640]{1,0:T(8,128)(2,1)S(1)}, bf16[512,640]{1,0:T(8,128)(2,1)S(1)}, u32[]{:S(2)}, u32[]{:S(2)}) collective-permute-start(bf16[512,640]{1,0:T(8,128)(2,1)S(1)} %collective-permute-done.13.refs_1_), channel_id=1, source_target_pairs={{0,2},{1,3},{2,0},{3,1},{4,5},{5,4},{6,7},{7,6},{8,10},{9,11},{10,... | collective-permute-start | bytes 1966088 | tf_op jit(solution)/shard_map/ppermute | solution.py:89
  81.8 8.3 %collective-permute-start.18 = (bf16[240,1280]{1,0:T(8,128)(2,1)}, bf16[240,1280]{1,0:T(8,128)(2,1)S(1)}, u32[]{:S(2)}, u32[]{:S(2)}) collective-permute-start(bf16[240,1280]{1,0:T(8,128)(2,1)} %collective-permute-done.8.refs_10_), channel_id=1, source_target_pairs={{0,4},{1,5},{2,6},{3,7},{4,0},{5,1},{6,2},{7,3},{8,12},{9,13},{10,... | collective-permute-start | bytes 1843208 | tf_op jit(solution)/shard_map/ppermute | solution.py:89
  81.8 8.4 %collective-permute-start.19 = (bf16[240,1280]{1,0:T(8,128)(2,1)}, bf16[240,1280]{1,0:T(8,128)(2,1)S(1)}, u32[]{:S(2)}, u32[]{:S(2)}) collective-permute-start(bf16[240,1280]{1,0:T(8,128)(2,1)} %collective-permute-done.10.refs_14_), channel_id=1, source_target_pairs={{0,4},{1,5},{2,6},{3,7},{4,0},{5,1},{6,2},{7,3},{8,12},{9,13},{10,... | collective-permute-start | bytes 1843208 | tf_op jit(solution)/shard_map/ppermute | solution.py:89
  82.3 7.9 %collective-permute-start.20 = (bf16[240,1280]{1,0:T(8,128)(2,1)}, bf16[240,1280]{1,0:T(8,128)(2,1)S(1)}, u32[]{:S(2)}, u32[]{:S(2)}) collective-permute-start(bf16[240,1280]{1,0:T(8,128)(2,1)} %collective-permute-done.11.refs_11_), channel_id=1, source_target_pairs={{0,4},{1,5},{2,6},{3,7},{4,0},{5,1},{6,2},{7,3},{8,12},{9,13},{10,... | collective-permute-start | bytes 1843208 | tf_op jit(solution)/shard_map/ppermute | solution.py:89
  97.2 23.2 %collective-permute-start.24 = (bf16[240,1280]{1,0:T(8,128)(2,1)S(1)}, bf16[240,1280]{1,0:T(8,128)(2,1)}, u32[]{:S(2)}, u32[]{:S(2)}) collective-permute-start(bf16[240,1280]{1,0:T(8,128)(2,1)S(1)} %collective-permute-done.17.refs_18_), channel_id=1, source_target_pairs={{0,8},{1,9},{2,10},{3,11},{4,12},{5,13},{6,14},{7,15},{8,0},{9,1},... | collective-permute-start | bytes 1843208 | tf_op jit(solution)/shard_map/ppermute | solution.py:89
  98.6 21.8 %collective-permute-start.25 = (bf16[240,1280]{1,0:T(8,128)(2,1)S(1)}, bf16[240,1280]{1,0:T(8,128)(2,1)S(1)}, u32[]{:S(2)}, u32[]{:S(2)}) collective-permute-start(bf16[240,1280]{1,0:T(8,128)(2,1)S(1)} %collective-permute-done.17.refs_18_), channel_id=1, source_target_pairs={{0,4},{1,5},{2,6},{3,7},{4,0},{5,1},{6,2},{7,3},{8,12},{9,13},{10,... | collective-permute-start | bytes 1843208 | tf_op jit(solution)/shard_map/ppermute | solution.py:89
  98.6 21.8 %collective-permute-start.22 = (bf16[320,960]{1,0:T(8,128)(2,1)}, bf16[320,960]{1,0:T(8,128)(2,1)}, u32[]{:S(2)}, u32[]{:S(2)}) collective-permute-start(bf16[320,960]{1,0:T(8,128)(2,1)} %constant_dynamic-slice_fusion.3), channel_id=1, source_target_pairs={{0,2},{1,3},{2,0},{3,1},{4,5},{5,4},{6,7},{7,6},{8,10},{9,11},{10,... | collective-permute-start | bytes 1843208 | tf_op jit(solution)/shard_map/ppermute | solution.py:89
  98.9 21.5 %collective-permute-start.23 = (bf16[320,960]{1,0:T(8,128)(2,1)}, bf16[320,960]{1,0:T(8,128)(2,1)}, u32[]{:S(2)}, u32[]{:S(2)}) collective-permute-start(bf16[320,960]{1,0:T(8,128)(2,1)} %collective-permute-done.12.refs_23_), channel_id=1, source_target_pairs={{0,2},{1,3},{2,0},{3,1},{4,5},{5,4},{6,7},{7,6},{8,10},{9,11},{10,... | collective-permute-start | bytes 1843208 | tf_op jit(solution)/shard_map/ppermute | solution.py:89
  121.3 3.1 collective-permute-start.26
  121.3 4.1 collective-permute-start.27
  121.8 3.7 collective-permute-start.28
  121.8 4.7 %collective-permute-start.29 = (bf16[320,960]{1,0:T(8,128)(2,1)}, bf16[320,960]{1,0:T(8,128)(2,1)}, u32[]{:S(2)}, u32[]{:S(2)}) collective-permute-start(bf16[320,960]{1,0:T(8,128)(2,1)} %collective-permute-done.23.refs_27_), channel_id=1, source_target_pairs={{0,4},{1,5},{2,6},{3,7},{4,0},{5,1},{6,2},{7,3},{8,12},{9,13},{10,... | collective-permute-start | bytes 1843208 | tf_op jit(solution)/shard_map/ppermute | solution.py:89
  122.3 30.6 %collective-permute-start.30 = (bf16[2,960,256]{2,1,0:T(8,128)(2,1)}, bf16[2,960,256]{2,1,0:T(8,128)(2,1)S(1)}, u32[]{:S(2)}, u32[]{:S(2)}) collective-permute-start(bf16[2,960,256]{2,1,0:T(8,128)(2,1)} %bitcast.17.x_ref.refs_0_), channel_id=1, source_target_pairs={{0,1},{1,0},{2,3},{3,2},{4,6},{5,7},{6,4},{7,5},{8,9},{9,8},{10,11... | collective-permute-start | bytes 2949128 | tf_op jit(solution)/shard_map/ppermute | solution.py:89
  124.4 28.5 %collective-permute-start.31 = (bf16[2,960,256]{2,1,0:T(8,128)(2,1)}, bf16[2,960,256]{2,1,0:T(8,128)(2,1)S(1)}, u32[]{:S(2)}, u32[]{:S(2)}) collective-permute-start(bf16[2,960,256]{2,1,0:T(8,128)(2,1)} %bitcast.17.x_ref.refs_0_), channel_id=1, source_target_pairs={{0,2},{1,3},{2,0},{3,1},{4,5},{5,4},{6,7},{7,6},{8,10},{9,11},{10,... | collective-permute-start | bytes 2949128 | tf_op jit(solution)/shard_map/ppermute | solution.py:89
  152.9 14.3 %collective-permute-start.32 = (bf16[2,960,256]{2,1,0:T(8,128)(2,1)S(1)}, bf16[2,960,256]{2,1,0:T(8,128)(2,1)}, u32[]{:S(2)}, u32[]{:S(2)}) collective-permute-start(bf16[2,960,256]{2,1,0:T(8,128)(2,1)S(1)} %collective-permute-done.30.refs_1_), channel_id=1, source_target_pairs={{0,2},{1,3},{2,0},{3,1},{4,5},{5,4},{6,7},{7,6},{8,10},{9,11},{10,... | collective-permute-start | bytes 2949128 | tf_op jit(solution)/shard_map/ppermute | solution.py:89
  167.2 9.1 %collective-permute-start.33 = (bf16[1280,1024]{1,0:T(8,128)(2,1)}, bf16[1280,1024]{1,0:T(8,128)(2,1)}, u32[]{:S(2)}, u32[]{:S(2)}) collective-permute-start(bf16[1280,1024]{1,0:T(8,128)(2,1)} %get-tuple-element.422), channel_id=1, source_target_pairs={{0,4},{1,5},{2,6},{3,7},{4,0},{5,1},{6,2},{7,3},{8,12},{9,13},{10,... | collective-permute-start | bytes 7864328 | tf_op jit(solution)/shard_map/ppermute | solution.py:89
  176.3 21.5 %collective-permute-start.35 = (bf16[512,2560]{1,0:T(8,128)(2,1)}, bf16[512,2560]{1,0:T(8,128)(2,1)}, u32[]{:S(2)}, u32[]{:S(2)}) collective-permute-start(bf16[512,2560]{1,0:T(8,128)(2,1)} %get-tuple-element.448), channel_id=1, source_target_pairs={{0,4},{1,5},{2,6},{3,7},{4,0},{5,1},{6,2},{7,3},{8,12},{9,13},{10,... | collective-permute-start | bytes 7864328 | tf_op jit(solution)/shard_map/ppermute | solution.py:89
  176.8 21.0 %collective-permute-start.36 = (bf16[448,2560]{1,0:T(8,128)(2,1)}, bf16[448,2560]{1,0:T(8,128)(2,1)}, u32[]{:S(2)}, u32[]{:S(2)}) collective-permute-start(bf16[448,2560]{1,0:T(8,128)(2,1)} %get-tuple-element.450), channel_id=1, source_target_pairs={{0,4},{1,5},{2,6},{3,7},{4,0},{5,1},{6,2},{7,3},{8,12},{9,13},{10,... | collective-permute-start | bytes 6881288 | tf_op jit(solution)/shard_map/ppermute | solution.py:89
  179.9 17.9 %collective-permute-start.34 = (bf16[640,1024]{1,0:T(8,128)(2,1)}, bf16[640,1024]{1,0:T(8,128)(2,1)}, u32[]{:S(2)}, u32[]{:S(2)}) collective-permute-start(bf16[640,1024]{1,0:T(8,128)(2,1)} %add_convert_fusion.2), channel_id=1, source_target_pairs={{0,2},{1,3},{2,0},{3,1},{4,5},{5,4},{6,7},{7,6},{8,10},{9,11},{10,... | collective-permute-start | bytes 3932168 | tf_op jit(solution)/shard_map/ppermute | solution.py:89
  200.9 27.1 %collective-permute-start.38 = (bf16[256,2560]{1,0:T(8,128)(2,1)}, bf16[256,2560]{1,0:T(8,128)(2,1)}, u32[]{:S(2)}, u32[]{:S(2)}) collective-permute-start(bf16[256,2560]{1,0:T(8,128)(2,1)} %add_convert_fusion.1), channel_id=1, source_target_pairs={{0,2},{1,3},{2,0},{3,1},{4,5},{5,4},{6,7},{7,6},{8,10},{9,11},{10,... | collective-permute-start | bytes 3932168 | tf_op jit(solution)/shard_map/ppermute | solution.py:89
  206.9 21.1 %collective-permute-start.37 = (bf16[320,1024]{1,0:T(8,128)(2,1)S(1)}, bf16[320,1024]{1,0:T(8,128)(2,1)S(1)}, u32[]{:S(2)}, u32[]{:S(2)}) collective-permute-start(bf16[320,1024]{1,0:T(8,128)(2,1)S(1)} %add_convert_fusion.15), channel_id=1, source_target_pairs={{0,1},{1,0},{2,3},{3,2},{4,6},{5,7},{6,4},{7,5},{8,9},{9,8},{10,11... | collective-permute-start | bytes 1966088 | tf_op jit(solution)/shard_map/ppermute | solution.py:89
  230.0 25.6 %collective-permute-start.39 = (bf16[320,1024]{1,0:T(8,128)(2,1)S(1)}, bf16[320,1024]{1,0:T(8,128)(2,1)S(1)}, u32[]{:S(2)}, u32[]{:S(2)}) collective-permute-start(bf16[320,1024]{1,0:T(8,128)(2,1)S(1)} %add_convert_fusion.14), channel_id=1, source_target_pairs={{0,8},{1,9},{2,10},{3,11},{4,12},{5,13},{6,14},{7,15},{24,16},{25,... | collective-permute-start | bytes 1966088 | tf_op jit(solution)/shard_map/ppermute | solution.py:89
  235.3 22.9 %collective-permute-start.41 = (bf16[224,2560]{1,0:T(8,128)(2,1)S(1)}, bf16[224,2560]{1,0:T(8,128)(2,1)S(1)}, u32[]{:S(2)}, u32[]{:S(2)}) collective-permute-start(bf16[224,2560]{1,0:T(8,128)(2,1)S(1)} %add_convert_fusion.3), channel_id=1, source_target_pairs={{0,2},{1,3},{2,0},{3,1},{4,5},{5,4},{6,7},{7,6},{8,10},{9,11},{10,... | collective-permute-start | bytes 3440648 | tf_op jit(solution)/shard_map/ppermute | solution.py:89
  238.0 17.7 %collective-permute-start.40 = (bf16[128,2560]{1,0:T(8,128)(2,1)S(1)}, bf16[128,2560]{1,0:T(8,128)(2,1)S(1)}, u32[]{:S(2)}, u32[]{:S(2)}) collective-permute-start(bf16[128,2560]{1,0:T(8,128)(2,1)S(1)} %add_convert_fusion.13), channel_id=1, source_target_pairs={{0,1},{1,0},{2,3},{3,2},{4,6},{5,7},{6,4},{7,5},{8,9},{9,8},{10,11... | collective-permute-start | bytes 1966088 | tf_op jit(solution)/shard_map/ppermute | solution.py:89
  258.2 26.2 %collective-permute-start.42 = (bf16[2,512,640]{2,1,0:T(8,128)(2,1)}, bf16[2,512,640]{2,1,0:T(8,128)(2,1)}, u32[]{:S(2)}, u32[]{:S(2)}) collective-permute-start(bf16[2,512,640]{2,1,0:T(8,128)(2,1)} %get-tuple-element.513.refs_5_), channel_id=1, source_target_pairs={{0,2},{1,3},{2,0},{3,1},{4,5},{5,4},{6,7},{7,6},{8,10},{9,11},{10,... | collective-permute-start | bytes 3932168 | tf_op jit(solution)/shard_map/ppermute | solution.py:89
  259.6 24.8 %collective-permute-start.43 = (bf16[320,1024]{1,0:T(8,128)(2,1)S(1)}, bf16[320,1024]{1,0:T(8,128)(2,1)}, u32[]{:S(2)}, u32[]{:S(2)}) collective-permute-start(bf16[320,1024]{1,0:T(8,128)(2,1)S(1)} %add_convert_fusion.12), channel_id=1, source_target_pairs={{8,16},{9,17},{10,18},{11,19},{12,20},{13,21},{14,22},{15,23},{16,... | collective-permute-start | bytes 1966088 | tf_op jit(solution)/shard_map/ppermute | solution.py:89
  263.6 20.8 %collective-permute-start.44 = (bf16[128,2560]{1,0:T(8,128)(2,1)}, bf16[128,2560]{1,0:T(8,128)(2,1)}, u32[]{:S(2)}, u32[]{:S(2)}) collective-permute-start(bf16[128,2560]{1,0:T(8,128)(2,1)} %add_convert_fusion.11), channel_id=1, source_target_pairs={{0,8},{1,9},{2,10},{3,11},{4,12},{5,13},{6,14},{7,15},{24,16},{25,... | collective-permute-start | bytes 1966088 | tf_op jit(solution)/shard_map/ppermute | solution.py:89
  268.9 15.5 %collective-permute-start.45 = (bf16[112,2560]{1,0:T(8,128)(2,1)S(1)}, bf16[112,2560]{1,0:T(8,128)(2,1)}, u32[]{:S(2)}, u32[]{:S(2)}) collective-permute-start(bf16[112,2560]{1,0:T(8,128)(2,1)S(1)} %add_convert_fusion.19), channel_id=1, source_target_pairs={{0,1},{1,0},{2,3},{3,2},{4,6},{5,7},{6,4},{7,5},{8,9},{9,8},{10,11... | collective-permute-start | bytes 1720328 | tf_op jit(solution)/shard_map/ppermute | solution.py:89
  284.4 30.6 %collective-permute-start.48 = (bf16[512,2688]{1,0:T(8,128)(2,1)}, bf16[512,2688]{1,0:T(8,128)(2,1)}, u32[]{:S(2)}, u32[]{:S(2)}) collective-permute-start(bf16[512,2688]{1,0:T(8,128)(2,1)} %get-tuple-element.527), channel_id=1, source_target_pairs={{0,4},{1,5},{2,6},{3,7},{4,0},{5,1},{6,2},{7,3},{8,12},{9,13},{10,... | collective-permute-start | bytes 8257544 | tf_op jit(solution)/shard_map/ppermute | solution.py:89
  286.8 27.3 %collective-permute-start.46 = (bf16[1,512,640]{2,1,0:T(8,128)(2,1)}, bf16[1,512,640]{2,1,0:T(8,128)(2,1)}, u32[]{:S(2)}, u32[]{:S(2)}) collective-permute-start(bf16[1,512,640]{2,1,0:T(8,128)(2,1)} %add_convert_fusion.10), channel_id=1, source_target_pairs={{0,1},{1,0},{2,3},{3,2},{4,6},{5,7},{6,4},{7,5},{8,9},{9,8},{10,11... | collective-permute-start | bytes 1966088 | tf_op jit(solution)/shard_map/ppermute | solution.py:89
  289.1 25.1 %collective-permute-start.47 = (bf16[320,1024]{1,0:T(8,128)(2,1)S(1)}, bf16[320,1024]{1,0:T(8,128)(2,1)}, u32[]{:S(2)}, u32[]{:S(2)}) collective-permute-start(bf16[320,1024]{1,0:T(8,128)(2,1)S(1)} %add_convert_fusion.9), channel_id=1, source_target_pairs={{8,0},{9,1},{10,2},{11,3},{12,4},{13,5},{14,6},{15,7},{16,24},{17,... | collective-permute-start | bytes 1966088 | tf_op jit(solution)/shard_map/ppermute | solution.py:89
  292.8 21.4 %collective-permute-start.49 = (bf16[128,2560]{1,0:T(8,128)(2,1)}, bf16[128,2560]{1,0:T(8,128)(2,1)}, u32[]{:S(2)}, u32[]{:S(2)}) collective-permute-start(bf16[128,2560]{1,0:T(8,128)(2,1)} %add_convert_fusion.8), channel_id=1, source_target_pairs={{8,16},{9,17},{10,18},{11,19},{12,20},{13,21},{14,22},{15,23},{16,... | collective-permute-start | bytes 1966088 | tf_op jit(solution)/shard_map/ppermute | solution.py:89
  295.8 18.4 %collective-permute-start.50 = (bf16[112,2560]{1,0:T(8,128)(2,1)S(1)}, bf16[112,2560]{1,0:T(8,128)(2,1)S(1)}, u32[]{:S(2)}, u32[]{:S(2)}) collective-permute-start(bf16[112,2560]{1,0:T(8,128)(2,1)S(1)} %add_convert_fusion.18), channel_id=1, source_target_pairs={{0,8},{1,9},{2,10},{3,11},{4,12},{5,13},{6,14},{7,15},{24,16},{25,... | collective-permute-start | bytes 1720328 | tf_op jit(solution)/shard_map/ppermute | solution.py:89
  316.1 18.2 %collective-permute-start.51 = (bf16[320,1024]{1,0:T(8,128)(2,1)S(1)}, bf16[320,1024]{1,0:T(8,128)(2,1)S(1)}, u32[]{:S(2)}, u32[]{:S(2)}) collective-permute-start(bf16[320,1024]{1,0:T(8,128)(2,1)S(1)} %broadcast_select_fusion.6), channel_id=1, source_target_pairs={{0,4},{1,5},{2,6},{3,7},{4,0},{5,1},{6,2},{7,3},{8,12},{9,13},{10,... | collective-permute-start | bytes 1966088 | tf_op jit(solution)/shard_map/ppermute | solution.py:89
  318.3 21.1 %collective-permute-start.52 = (bf16[256,2688]{1,0:T(8,128)(2,1)S(1)}, bf16[256,2688]{1,0:T(8,128)(2,1)S(1)}, u32[]{:S(2)}, u32[]{:S(2)}) collective-permute-start(bf16[256,2688]{1,0:T(8,128)(2,1)S(1)} %add_convert_fusion), channel_id=1, source_target_pairs={{0,2},{1,3},{2,0},{3,1},{4,5},{5,4},{6,7},{7,6},{8,10},{9,11},{10,... | collective-permute-start | bytes 4128776 | tf_op jit(solution)/shard_map/ppermute | solution.py:89
  320.8 18.7 %collective-permute-start.53 = (bf16[128,2560]{1,0:T(8,128)(2,1)S(1)}, bf16[128,2560]{1,0:T(8,128)(2,1)S(1)}, u32[]{:S(2)}, u32[]{:S(2)}) collective-permute-start(bf16[128,2560]{1,0:T(8,128)(2,1)S(1)} %add_convert_fusion.6), channel_id=1, source_target_pairs={{8,0},{9,1},{10,2},{11,3},{12,4},{13,5},{14,6},{15,7},{16,24},{17,... | collective-permute-start | bytes 1966088 | tf_op jit(solution)/shard_map/ppermute | solution.py:89
  322.5 11.8 %collective-permute-start.54 = (bf16[112,2560]{1,0:T(8,128)(2,1)S(1)}, bf16[112,2560]{1,0:T(8,128)(2,1)S(1)}, u32[]{:S(2)}, u32[]{:S(2)}) collective-permute-start(bf16[112,2560]{1,0:T(8,128)(2,1)S(1)} %add_convert_fusion.17), channel_id=1, source_target_pairs={{8,16},{9,17},{10,18},{11,19},{12,20},{13,21},{14,22},{15,23},{16,... | collective-permute-start | bytes 1720328 | tf_op jit(solution)/shard_map/ppermute | solution.py:89
  342.4 20.4 %collective-permute-start.55 = (bf16[128,2688]{1,0:T(8,128)(2,1)}, bf16[128,2688]{1,0:T(8,128)(2,1)}, u32[]{:S(2)}, u32[]{:S(2)}) collective-permute-start(bf16[128,2688]{1,0:T(8,128)(2,1)} %add_convert_fusion.5), channel_id=1, source_target_pairs={{0,1},{1,0},{2,3},{3,2},{4,6},{5,7},{6,4},{7,5},{8,9},{9,8},{10,11... | collective-permute-start | bytes 2064392 | tf_op jit(solution)/shard_map/ppermute | solution.py:89
  343.7 19.1 %collective-permute-start.56 = (bf16[128,2560]{1,0:T(8,128)(2,1)S(1)}, bf16[128,2560]{1,0:T(8,128)(2,1)}, u32[]{:S(2)}, u32[]{:S(2)}) collective-permute-start(bf16[128,2560]{1,0:T(8,128)(2,1)S(1)} %broadcast_select_fusion.3), channel_id=1, source_target_pairs={{0,4},{1,5},{2,6},{3,7},{4,0},{5,1},{6,2},{7,3},{8,12},{9,13},{10,... | collective-permute-start | bytes 1966088 | tf_op jit(solution)/shard_map/ppermute | solution.py:89
  344.7 18.1 %collective-permute-start.57 = (bf16[112,2560]{1,0:T(8,128)(2,1)}, bf16[112,2560]{1,0:T(8,128)(2,1)}, u32[]{:S(2)}, u32[]{:S(2)}) collective-permute-start(bf16[112,2560]{1,0:T(8,128)(2,1)} %add_convert_fusion.16), channel_id=1, source_target_pairs={{8,0},{9,1},{10,2},{11,3},{12,4},{13,5},{14,6},{15,7},{16,24},{17,... | collective-permute-start | bytes 1720328 | tf_op jit(solution)/shard_map/ppermute | solution.py:89
  364.8 18.8 %collective-permute-start.61 = (bf16[112,2560]{1,0:T(8,128)(2,1)}, bf16[112,2560]{1,0:T(8,128)(2,1)}, u32[]{:S(2)}, u32[]{:S(2)}) collective-permute-start(bf16[112,2560]{1,0:T(8,128)(2,1)} %broadcast_select_fusion.10), channel_id=1, source_target_pairs={{0,4},{1,5},{2,6},{3,7},{4,0},{5,1},{6,2},{7,3},{8,12},{9,13},{10,... | collective-permute-start | bytes 1720328 | tf_op jit(solution)/shard_map/ppermute | solution.py:89
  367.5 10.4 %collective-permute-start.58 = (bf16[32,2688]{1,0:T(8,128)(2,1)}, bf16[32,2688]{1,0:T(8,128)(2,1)S(1)}, u32[]{:S(2)}, u32[]{:S(2)}) collective-permute-start(bf16[32,2688]{1,0:T(8,128)(2,1)} %get-tuple-element.644), channel_id=1, source_target_pairs={{0,8},{1,9},{2,10},{3,11},{4,12},{5,13},{6,14},{7,15},{8,0},{9,1},... | collective-permute-start | bytes 516104 | tf_op jit(solution)/shard_map/ppermute | solution.py:89
  367.5 16.1 %collective-permute-start.59 = (bf16[32,2688]{1,0:T(8,128)(2,1)}, bf16[32,2688]{1,0:T(8,128)(2,1)}, u32[]{:S(2)}, u32[]{:S(2)}) collective-permute-start(bf16[32,2688]{1,0:T(8,128)(2,1)} %get-tuple-element.643), channel_id=1, source_target_pairs={{0,16},{1,17},{2,18},{3,19},{4,20},{5,21},{6,22},{7,23},{8,24},{9,... | collective-permute-start | bytes 516104 | tf_op jit(solution)/shard_map/ppermute | solution.py:89
  370.7 12.9 %collective-permute-start.60 = (bf16[32,2688]{1,0:T(8,128)(2,1)}, bf16[32,2688]{1,0:T(8,128)(2,1)}, u32[]{:S(2)}, u32[]{:S(2)}) collective-permute-start(bf16[32,2688]{1,0:T(8,128)(2,1)} %get-tuple-element.642), channel_id=1, source_target_pairs={{0,24},{1,25},{2,26},{3,27},{4,28},{5,29},{6,30},{7,31},{8,16},{9,... | collective-permute-start | bytes 516104 | tf_op jit(solution)/shard_map/ppermute | solution.py:89
  391.7 10.8 %collective-permute-start.62 = (bf16[32,2688]{1,0:T(8,128)(2,1)S(1)}, bf16[32,2688]{1,0:T(8,128)(2,1)S(1)}, u32[]{:S(2)}, u32[]{:S(2)}) collective-permute-start(bf16[32,2688]{1,0:T(8,128)(2,1)S(1)} %add_convert_fusion.20), channel_id=1, source_target_pairs={{0,8},{1,9},{2,10},{3,11},{4,12},{5,13},{6,14},{7,15},{8,0},{9,1},... | collective-permute-start | bytes 516104 | tf_op jit(solution)/shard_map/ppermute | solution.py:89
  395.7 15.6 %collective-permute-start.63 = (bf16[32,2688]{1,0:T(8,128)(2,1)S(1)}, bf16[32,2688]{1,0:T(8,128)(2,1)S(1)}, u32[]{:S(2)}, u32[]{:S(2)}) collective-permute-start(bf16[32,2688]{1,0:T(8,128)(2,1)S(1)} %add_convert_fusion.20), channel_id=1, source_target_pairs={{0,16},{1,17},{2,18},{3,19},{4,20},{5,21},{6,22},{7,23},{8,24},{9,... | collective-permute-start | bytes 516104 | tf_op jit(solution)/shard_map/ppermute | solution.py:89
  396.6 14.6 %collective-permute-start.64 = (bf16[32,2688]{1,0:T(8,128)(2,1)S(1)}, bf16[32,2688]{1,0:T(8,128)(2,1)S(1)}, u32[]{:S(2)}, u32[]{:S(2)}) collective-permute-start(bf16[32,2688]{1,0:T(8,128)(2,1)S(1)} %add_convert_fusion.20), channel_id=1, source_target_pairs={{0,24},{1,25},{2,26},{3,27},{4,28},{5,29},{6,30},{7,31},{8,16},{9,... | collective-permute-start | bytes 516104 | tf_op jit(solution)/shard_map/ppermute | solution.py:89
  (75 other events, 713.4 us)

commit v8 on v7

--- a/solution.py
+++ b/solution.py
@@ -5,7 +5,6 @@
 import jax.numpy as jnp
 from jax import lax
 from jax.experimental import pallas as pl
-from jax.experimental.layout import Layout, with_layout_constraint
 from jax.experimental.pallas import tpu as pltpu
 from jax.sharding import PartitionSpec as P
 
@@ -95,10 +94,15 @@
         return self.move(value, lambda r, s: (r ^ 1, s))
 
     def reduce(self, plan, name, quick=False):
-        got = yield self.swap(plan.have[name + ".given"])
-        sums = [plan.have.pop(name + ".kept"), got]
-        del plan.have[name + ".given"]
-        for i in reversed(range(self.bits)):
+        top = self.bits
+        if name + ".given" in plan.have:
+            got = yield self.swap(plan.have.pop(name + ".given"))
+            sums = [plan.have.pop(name + ".kept"), got]
+        else:
+            got = yield self.step(plan.have.pop(name + ".high"), top - 1)
+            sums = [plan.have.pop(name + ".low"), got]
+            top -= 1
+        for i in reversed(range(top)):
             block = sums[0].shape[0] // 2
             got = yield self.step(total([part[block:] for part in sums]), i)
             sums = [part[:block] for part in sums] + [got]
@@ -196,11 +200,6 @@
         high = jnp.where(self.core == 0, other, owned)
         return jnp.concatenate([low[: rows - owned.shape[0]], high], axis=0).astype(F32)
 
-    def finish_pair(self, owned, other):
-        left = jnp.where(self.core == 0, owned, other)
-        right = jnp.where(self.core == 0, other, owned)
-        return left.astype(F32), right.astype(F32)
-
 
 class Plan:
     def __init__(self):
@@ -261,12 +260,6 @@
 
 def upright(ref):
     return jnp.concatenate([jnp.transpose(ref[m]) for m in range(ref.shape[0])], axis=0)
-
-
-def lay_down(value, ref):
-    rows = ref.shape[2]
-    for m in range(ref.shape[0]):
-        ref[m] = jnp.transpose(value[m * rows : (m + 1) * rows])
 
 
 def turn(chunk, cosine, sine):
@@ -299,7 +292,8 @@
                 kv_ref[:, : at + 128 - width] = chunk[:, width - at :].astype(BF)
             else:
                 kv_ref[:, at - width : at - width + 128] = chunk.astype(BF)
-    kv_ref[:, KV_WIDTH:] = nn(act, whole[width:, width:]).astype(BF)
+    start = width // 128 * 128
+    kv_ref[:, KV_WIDTH:] = nn(act, whole[width:, start:])[:, width - start :].astype(BF)
 
 
 def project(x, gains, cosine, sine, pieces, starts, shape):
@@ -323,12 +317,22 @@
     )(starts, x, gains, cosine, sine, *pieces)
 
 
-def feed_kernel(counts, s0_ref, s1_ref, s2_ref, x_ref, attn_ref, cot_ref, gains_ref, *refs):
+def across(ref):
+    return jnp.concatenate([ref[m] for m in range(ref.shape[0])], axis=1)
+
+
+def spread_out(value, ref):
+    rows = ref.shape[2]
+    for m in range(ref.shape[0]):
+        ref[m] = value[:, m * rows : (m + 1) * rows]
+
+
+def feed_kernel(counts, core_ref, s0_ref, s1_ref, s2_ref, x_ref, attn_ref, cot_ref, gains_ref, *refs):
     total_count = sum(counts)
     attention_pieces = refs[: counts[0]]
     pair_pieces = refs[counts[0] : counts[0] + counts[1]]
     down_pieces = refs[counts[0] + counts[1] : total_count]
-    out_ref, inner_ref, slopes_ref, act_t_ref, attn_t_ref, dy_ref, resid_ref = refs[total_count : total_count + 7]
+    out_ref, inner_ref, kept_ref, given_ref, act_t_ref, attn_t_ref, resid_ref = refs[total_count : total_count + 7]
     w_attn, w_pair, w_down, sum_ref, sems0, sems1, sems2 = refs[total_count + 7 :]
     attention_copies = load(attention_pieces, s0_ref, w_attn, sems0)
     pair_copies = load(pair_pieces, s1_ref, w_pair, sems1)
@@ -336,112 +340,113 @@
     width = x_ref.shape[1]
     hidden = w_pair.shape[1]
     tile = hidden // 5
+    even = core_ref[0] == 0
     x = upright(x_ref).astype(F32)
-    dy_ref[...] = upright(cot_ref)
+    dy = upright(cot_ref)
     attn_t_ref[...] = jnp.transpose(attn_ref[...])
     wait(attention_copies)
-    resid = x + nn(attn_ref[...], w_attn[width:, :width])
-    resid_ref[...] = resid
-    sum_ref[...] = resid
+    resid = x + nn(attn_ref[...], w_attn[width:, : rounded_up(width)])[:, :width]
+    resid_t = jnp.transpose(resid)
+    resid_ref[...] = resid_t
+    sum_ref[...] = resid_t
     act = (resid * rms_inverse(resid) * gains_ref[1:2, :]).astype(BF)
     act_t_ref[...] = jnp.transpose(act)
     wait(pair_copies)
     wait(down_copies)
-    dy = dy_ref[...]
     for first in range(0, hidden, tile):
         here = slice(first, first + tile)
         gate = nn(act, w_pair[:width, here])
         upper = nn(act, w_pair[width:, here])
-        d_inner = nt(dy, w_down[here, :])
+        d_inner = nn(dy, w_down[:, here])
         sigmoid = 1.0 / (1.0 + jnp.exp(-gate))
         silu = gate * sigmoid
         inner = (silu * upper).astype(BF)
-        inner_ref[here, :] = jnp.transpose(inner)
-        slopes_ref[0, :, here] = (d_inner * upper * sigmoid * (1.0 + gate * (1.0 - sigmoid))).astype(BF)
-        slopes_ref[1, :, here] = (d_inner * silu).astype(BF)
-        sum_ref[...] += nn(inner, w_down[here, :])
-    lay_down(sum_ref[...].astype(BF), out_ref)
-
-
-def feed(x, attn, dy, gains, attention_got, pair_got, down_got):
+        inner_ref[:, here] = inner
+        d_gate = d_inner * upper * sigmoid * (1.0 + gate * (1.0 - sigmoid))
+        d_upper = d_inner * silu
+        kept_ref[:, here] = jnp.where(even, d_gate, d_upper).astype(BF)
+        given_ref[:, here] = jnp.where(even, d_upper, d_gate).astype(BF)
+        sum_ref[...] += nn(w_down[:, here], jnp.transpose(inner))
+    spread_out(sum_ref[...].astype(BF), out_ref)
+
+
+def feed(core, x, attn, dy, gains, attention_got, pair_got, down_got):
     micro, width, rows = x.shape
     tokens = micro * rows
     groups = [attention_got, pair_got, down_got]
     counts = [len(pieces) for pieces, _, _ in groups]
     shapes = [shape for _, _, shape in groups]
     hidden = shapes[1][1]
-    outs = (
-        jax.ShapeDtypeStruct(x.shape, BF),
-        jax.ShapeDtypeStruct((hidden, tokens), BF),
-        jax.ShapeDtypeStruct((2, tokens, hidden), BF),
-        jax.ShapeDtypeStruct((width, tokens), BF),
-        jax.ShapeDtypeStruct((width, tokens), BF),
-        jax.ShapeDtypeStruct((tokens, width), BF),
-        jax.ShapeDtypeStruct((tokens, width), F32),
-    )
+    outs = (jax.ShapeDtypeStruct(x.shape, BF),)
+    outs += (jax.ShapeDtypeStruct((tokens, hidden), BF),) * 3
+    outs += (jax.ShapeDtypeStruct((width, tokens), BF),) * 2
+    outs += (jax.ShapeDtypeStruct((width, tokens), F32),)
     every = [piece for pieces, _, _ in groups for piece in pieces]
     return pl.pallas_call(
         functools.partial(feed_kernel, counts),
         name="feed",
-        in_specs=[IN_SMEM] * 3 + [IN_VMEM] * 4 + [ANYWHERE] * len(every),
+        in_specs=[IN_SMEM] * 4 + [IN_VMEM] * 4 + [ANYWHERE] * len(every),
         out_specs=(IN_VMEM,) * 7,
         out_shape=outs,
         scratch_shapes=[pltpu.VMEM(shape, BF) for shape in shapes]
-        + [pltpu.VMEM((tokens, width), F32)]
+        + [pltpu.VMEM((width, tokens), F32)]
         + [pltpu.SemaphoreType.DMA((count,)) for count in counts],
         cost_estimate=cost(
             2 * tokens * width * (4 * hidden + width), tokens * hidden, x, x, x, *outs, *every
         ),
         compiler_params=pltpu.CompilerParams(vmem_limit_bytes=VMEM_MOST),
-    )(*(starts for _, starts, _ in groups), x, attn, dy, gains, *every)
-
-
-def feed_back_kernel(counts, s0_ref, s1_ref, resid_ref, dy_ref, slopes_ref, gains_ref, *refs):
+    )(core, *(starts for _, starts, _ in groups), x, attn, dy, gains, *every)
+
+
+def feed_back_kernel(counts, core_ref, s0_ref, s1_ref, resid_ref, cot_ref, kept_ref, given_ref, gain_ref, *refs):
     total_count = sum(counts)
     dres_ref, low_ref, dattn_ref, w_attn, w_pair, sems0, sems1 = refs[total_count:]
     pair_copies = load(refs[counts[0] : total_count], s1_ref, w_pair, sems1)
     attention_copies = load(refs[: counts[0]], s0_ref, w_attn, sems0)
-    width = resid_ref.shape[1]
+    width = resid_ref.shape[0]
     resid = resid_ref[...]
-    root = rms_inverse(resid)
+    root = lax.rsqrt(jnp.mean(resid * resid, axis=0, keepdims=True) + EPS)
     normed = resid * root
     wait(pair_copies)
-    d_act = nt(slopes_ref[0], w_pair[:width, :]) + nt(slopes_ref[1], w_pair[width:, :])
-    d_normed = d_act * gains_ref[1:2, :]
-    d_resid = dy_ref[...].astype(F32) + root * (
-        d_normed - normed * jnp.mean(d_normed * normed, axis=-1, keepdims=True)
+    weight = lambda i: w_pair[pl.ds(pl.multiple_of(i * width, 16), width), :]
+    d_act = nt(weight(core_ref[0]), kept_ref[...]) + nt(weight(1 - core_ref[0]), given_ref[...])
+    d_normed = d_act * gain_ref[...]
+    d_resid = across(cot_ref).astype(F32) + root * (
+        d_normed - normed * jnp.mean(d_normed * normed, axis=0, keepdims=True)
     )
     dres_ref[...] = d_resid
     low = d_resid.astype(BF)
-    low_ref[...] = low
+    low_ref[:, :width] = jnp.transpose(low)
+    if low_ref.shape[1] > width:
+        low_ref[:, width:] = jnp.zeros((low_ref.shape[0], low_ref.shape[1] - width), BF)
     wait(attention_copies)
-    dattn_ref[...] = nt(low, w_attn[width:, :width]).astype(BF)
-
-
-def feed_back(resid, dy, slopes, gains, attention_got, pair_got):
-    tokens, width = resid.shape
+    dattn_ref[...] = jnp.transpose(nn(w_attn[width:, :width], low).astype(BF))
+
+
+def feed_back(core, resid, dy, kept, given, gain, attention_got, pair_got):
+    width, tokens = resid.shape
     groups = [attention_got, pair_got]
     counts = [len(pieces) for pieces, _, _ in groups]
     shapes = [shape for _, _, shape in groups]
     outs = (
-        jax.ShapeDtypeStruct((tokens, width), F32),
-        jax.ShapeDtypeStruct((tokens, width), BF),
+        jax.ShapeDtypeStruct((width, tokens), F32),
+        jax.ShapeDtypeStruct((tokens, rounded_up(width)), BF),
         jax.ShapeDtypeStruct((tokens, width), BF),
     )
     every = [piece for pieces, _, _ in groups for piece in pieces]
     return pl.pallas_call(
         functools.partial(feed_back_kernel, counts),
         name="feed_back",
-        in_specs=[IN_SMEM] * 2 + [IN_VMEM] * 4 + [ANYWHERE] * len(every),
+        in_specs=[IN_SMEM] * 3 + [IN_VMEM] * 5 + [ANYWHERE] * len(every),
         out_specs=(IN_VMEM,) * 3,
         out_shape=outs,
         scratch_shapes=[pltpu.VMEM(shape, BF) for shape in shapes]
         + [pltpu.SemaphoreType.DMA((count,)) for count in counts],
         cost_estimate=cost(
-            2 * tokens * width * (2 * shapes[1][1] + width), 0, resid, dy, slopes, *outs, *every
+            2 * tokens * width * (2 * shapes[1][1] + width), 0, resid, dy, kept, given, *outs, *every
         ),
         compiler_params=pltpu.CompilerParams(vmem_limit_bytes=VMEM_MOST),
-    )(*(starts for _, starts, _ in groups), resid, dy, slopes, gains, *every)
+    )(core, *(starts for _, starts, _ in groups), resid, dy, kept, given, gain, *every)
 
 
 def pick_rows(source, starts_ref, base, rows, count, target):
@@ -450,110 +455,129 @@
         target[t * rows : (t + 1) * rows, :] = source[pl.ds(start, rows), :]
 
 
-def rows_grad_kernel(parts, count, starts_ref, *refs):
-    operands = refs[: 2 * len(parts)]
-    outs = refs[2 * len(parts) : 2 * len(parts) + 2]
-    ordered = refs[2 * len(parts) + 2 :]
-    block = sum(parts)
-    for o, out_ref in enumerate(outs):
-        at = 0
-        for i, rows in enumerate(parts):
-            pick_rows(operands[2 * i], starts_ref, (o * len(parts) + i) * count, rows, count, ordered[i])
-            made = nn(ordered[i][...], operands[2 * i + 1][...]).astype(BF)
-            columns = made.shape[1]
-            for t in range(count):
-                place = slice(t * block + at, t * block + at + rows)
-                out_ref[place, :columns] = made[t * rows : (t + 1) * rows]
-                if columns < out_ref.shape[1]:
-                    out_ref[place, columns:] = jnp.zeros((rows, out_ref.shape[1] - columns), BF)
-            at += rows
-
-
-def rows_grad(terms):
-    count = len(terms[0][3])
-    parts = [term[2] for term in terms]
-    block, columns = sum(parts), terms[0][1].shape[1]
-    wide = rounded_up(columns)
-    if any(rows % 16 for rows in parts) or any(term[0].shape[0] // count % 16 for term in terms):
-        outs = []
-        for o in (3, 4):
-            made = []
-            for term in terms:
-                grad = jnp.pad(nn(term[0], term[1]).astype(BF), ((0, 0), (0, wide - columns)))
-                made.append([lax.dynamic_slice_in_dim(grad, start, term[2], 0) for start in term[o]])
-            outs.append(jnp.concatenate([part for group in zip(*made) for part in group], axis=0))
-        return outs
-    args = [operand for term in terms for operand in term[:2]]
-    out = jax.ShapeDtypeStruct((count * block, wide), BF)
-    flops = sum(4 * left.shape[1] * rows * count * columns for left, _, rows, _, _ in terms)
+def down_grad_kernel(shards, cut, info_ref, cot_ref, far_cot_ref, inner_ref, far_inner_ref, low_ref, high_ref, dy):
+    micro, width, rows = cot_ref.shape
+    tokens, part = micro * rows, low_ref.shape[0] // (shards // 2)
+    first = pl.multiple_of(info_ref[0], 16)
+    for i, ref in enumerate((cot_ref, far_cot_ref)):
+        for m in range(micro):
+            at = i * tokens + m * rows
+            dy[:, at : at + rows] = ref[m, pl.ds(first, part), :]
+    for t in range(shards):
+        columns = pl.ds(pl.multiple_of(info_ref[1 + t], 128), cut)
+        made = nn(dy[:, :tokens], inner_ref[:, columns]) + nn(dy[:, tokens:], far_inner_ref[:, columns])
+        out_ref, at = (low_ref, t) if t < shards // 2 else (high_ref, t - shards // 2)
+        out_ref[at * part : (at + 1) * part, :] = made.astype(BF)
+
+
+def down_grad(cot, far_cot, inner, far_inner, first, starts):
+    shards, (micro, width, rows), (tokens, hidden) = len(starts), cot.shape, inner.shape
+    part, cut = width // 2, hidden // shards
+    outs = (jax.ShapeDtypeStruct((shards // 2 * part, cut), BF),) * 2
+    if part % 16 or cut % 128:
+        grad = nn(jnp.concatenate(list(cot), axis=1), inner) + nn(jnp.concatenate(list(far_cot), axis=1), far_inner)
+        grad = lax.dynamic_slice_in_dim(grad.astype(BF), first, part, 0)
+        blocks = [lax.dynamic_slice_in_dim(grad, start, cut, 1) for start in starts]
+        return [jnp.concatenate(blocks[: shards // 2]), jnp.concatenate(blocks[shards // 2 :])]
     return pl.pallas_call(
-        functools.partial(rows_grad_kernel, parts, count),
-        name="rows_grad",
-        in_specs=[IN_SMEM] + [IN_VMEM] * len(args),
+        functools.partial(down_grad_kernel, shards, cut),
+        name="down_grad",
+        in_specs=[IN_SMEM] + [IN_VMEM] * 4,
         out_specs=(IN_VMEM,) * 2,
-        out_shape=(out, out),
-        scratch_shapes=[pltpu.VMEM((count * rows, terms[0][0].shape[1]), BF) for rows in parts],
-        cost_estimate=cost(flops, 0, out, out, *args),
+        out_shape=outs,
+        scratch_shapes=[pltpu.VMEM((part, 2 * tokens), BF)],
+        cost_estimate=cost(4 * part * tokens * hidden, 0, cot, cot, inner, inner, *outs),
         compiler_params=pltpu.CompilerParams(vmem_limit_bytes=VMEM_LIMIT),
-    )(numbers([start for o in (3, 4) for term in terms for start in term[o]]), *args)
-
-
-def wide_grad_kernel(cuts, count, rows, info_ref, left_ref, given_ref, kept_ref, *refs):
+    )(numbers([first] + starts), cot, far_cot, inner, far_inner)
+
+
+def wide_grad_kernel(cuts, count, starts_ref, left_ref, far_left_ref, right_ref, far_right_ref, *refs):
     outs, ordered = refs[: 2 * len(cuts)], refs[2 * len(cuts)]
+    tokens = left_ref.shape[1]
 
     @pl.when(pl.program_id(0) == 0)
     def _():
-        at = 0
-        for o in range(2):
-            first = 0
-            for cut in cuts:
-                for t in range(count):
-                    start = pl.multiple_of(info_ref[2 + o * count + t] + first, 16)
-                    ordered[at : at + cut, :] = left_ref[pl.ds(start, cut), :]
-                    at += cut
-                first += cut
-
-    for o, right_ref in enumerate((given_ref, kept_ref)):
-        made = nn(ordered[o * count * rows : (o + 1) * count * rows, :], right_ref[...]).astype(BF)
-        at = 0
-        for c, cut in enumerate(cuts):
-            outs[o * len(cuts) + c][...] = made[at : at + count * cut]
-            at += count * cut
-
-
-def wide_grad(left, rights, rows, cuts, given, kept, core):
-    count, (_, tokens, columns) = len(given), rights.shape
-    outs = tuple(jax.ShapeDtypeStruct((count * cut, columns), BF) for cut in cuts) * 2
+        at = first = 0
+        for cut in cuts:
+            for t in range(count):
+                start = pl.multiple_of(starts_ref[t] + first, 16)
+                ordered[at : at + cut, :tokens] = left_ref[pl.ds(start, cut), :]
+                ordered[at : at + cut, tokens:] = far_left_ref[pl.ds(start, cut), :]
+                at += cut
+            first += cut
+
+    made = nn(ordered[:, :tokens], right_ref[...]) + nn(ordered[:, tokens:], far_right_ref[...])
+    at = 0
+    for i, out_ref in enumerate(outs):
+        size = out_ref.shape[0]
+        out_ref[...] = made[at : at + size].astype(BF)
+        at += size
+
+
+def wide_grad(left, far_left, right, far_right, rows, cuts, starts):
+    count, (tokens, columns) = len(starts), right.shape
+    outs = tuple(jax.ShapeDtypeStruct((count // 2 * cut, columns), BF) for cut in cuts for _ in range(2))
     if rows % 16 or any(cut % 16 for cut in cuts):
-        made = []
-        for starts, choice in ((given, 1 - core), (kept, core)):
-            grad = nn(left, lax.dynamic_index_in_dim(rights, choice, 0, keepdims=False)).astype(BF)
-            first = 0
-            for cut in cuts:
-                made.append(
-                    jnp.concatenate([lax.dynamic_slice_in_dim(grad, start + first, cut, 0) for start in starts])
-                )
-                first += cut
+        grad = (nn(left, right) + nn(far_left, far_right)).astype(BF)
+        made, first = [], 0
+        for cut in cuts:
+            blocks = [lax.dynamic_slice_in_dim(grad, start + first, cut, 0) for start in starts]
+            made += [jnp.concatenate(blocks[: count // 2]), jnp.concatenate(blocks[count // 2 :])]
+            first += cut
         return made
     tile = 512 if columns % 512 == 0 else columns
+    part = pl.BlockSpec((tokens, tile), lambda n, starts: (0, n))
+    whole = pl.BlockSpec(left.shape, lambda n, starts: (0, 0))
     return pl.pallas_call(
-        functools.partial(wide_grad_kernel, cuts, count, rows),
+        functools.partial(wide_grad_kernel, cuts, count),
         grid_spec=pltpu.PrefetchScalarGridSpec(
             num_scalar_prefetch=1,
             grid=(columns // tile,),
-            in_specs=[
-                pl.BlockSpec(left.shape, lambda n, info: (0, 0)),
-                pl.BlockSpec((None, tokens, tile), lambda n, info: (info[0], 0, n)),
-                pl.BlockSpec((None, tokens, tile), lambda n, info: (info[1], 0, n)),
-            ],
-            out_specs=tuple(pl.BlockSpec((out.shape[0], tile), lambda n, info: (0, n)) for out in outs),
-            scratch_shapes=[pltpu.VMEM((2 * count * rows, tokens), BF)],
+            in_specs=[whole, whole, part, part],
+            out_specs=tuple(pl.BlockSpec((out.shape[0], tile), lambda n, starts: (0, n)) for out in outs),
+            scratch_shapes=[pltpu.VMEM((count * rows, 2 * tokens), BF)],
         ),
         out_shape=outs,
         name="wide_grad",
-        cost_estimate=cost(4 * tokens * rows * count * columns, 0, left, rights, *outs),
+        cost_estimate=cost(4 * tokens * rows * count * columns, 0, left, left, right, right, *outs),
         compiler_params=pltpu.CompilerParams(vmem_limit_bytes=VMEM_LIMIT),
-    )(numbers([1 - core, core] + given + kept), left, rights, rights)
+    )(numbers(starts), left, far_left, right, far_right)
+
+
+def settle_wide_kernel(cuts, core_ref, gain_ref, *refs):
+    sums = refs[: 2 * len(cuts)]
+    w_left, w_right, left_ref, right_ref, sum_ref = refs[2 * len(cuts) :]
+    even = core_ref[0] == 0
+    at = 0
+    for c, cut in enumerate(cuts):
+        here = slice(at, at + cut)
+        mine, theirs = sums[2 * c][...].astype(F32), sums[2 * c + 1][...].astype(F32)
+        left, right = jnp.where(even, mine, theirs), jnp.where(even, theirs, mine)
+        left_ref[here, :], right_ref[here, :] = left, right
+        both = w_left[here, :].astype(F32) * left + w_right[here, :].astype(F32) * right
+        sum_ref[here, :] = jnp.sum(both, axis=1, keepdims=True) / gain_ref[here, :]
+        at += cut
+
+
+def settle_wide(core, gain, sums, cuts, w_left, w_right):
+    out = jax.ShapeDtypeStruct(w_left.shape, F32)
+    column = jax.ShapeDtypeStruct((w_left.shape[0], 1), F32)
+    if any(cut % 16 for cut in cuts):
+        pairs = [(mine.astype(F32), theirs.astype(F32)) for mine, theirs in sums]
+        left = jnp.concatenate([jnp.where(core[0] == 0, a, b) for a, b in pairs])
+        right = jnp.concatenate([jnp.where(core[0] == 0, b, a) for a, b in pairs])
+        both = w_left.astype(F32) * left + w_right.astype(F32) * right
+        return left, right, jnp.sum(both, axis=1, keepdims=True) / gain
+    args = [value for pair in sums for value in pair]
+    return pl.pallas_call(
+        functools.partial(settle_wide_kernel, cuts),
+        name="settle",
+        in_specs=[IN_SMEM] + [IN_VMEM] * (3 + len(args)),
+        out_specs=(IN_VMEM,) * 3,
+        out_shape=(out, out, column),
+        cost_estimate=cost(4 * w_left.size, 0, out, out, *args),
+        compiler_params=pltpu.CompilerParams(vmem_limit_bytes=VMEM_LIMIT),
+    )(core, gain, *args, w_left, w_right)
 
 
 def turn_keys(source, target, at, cosine, sine):
@@ -583,13 +607,8 @@
     for i, out_ref in enumerate(outs):
         pick_rows(act, starts_ref, i * shards, half, shards, ordered)
         pick_rows(attn_ref, starts_ref, i * shards, half, shards, attn_ordered)
-        for first, made in (
-            (0, nn(ordered[:, :tokens], dq_ref[...])),
-            (wide, nn(attn_ordered[...], low_ref[...])),
-        ):
-            out_ref[:, first : first + width] = made.astype(BF)
-            if wide > width:
-                out_ref[:, first + width : first + wide] = jnp.zeros((made.shape[0], wide - width), BF)
+        out_ref[:, :wide] = nn(ordered[:, :tokens], dq_ref[...]).astype(BF)
+        out_ref[:, wide : 2 * wide] = nn(attn_ordered[...], low_ref[...]).astype(BF)
         out_ref[:, 2 * wide :] = nn(ordered[...], dkv[...]).astype(BF)
 
 
@@ -609,8 +628,7 @@
         first, second = keys[:, :, 0], keys[:, :, 1]
         keys = jnp.stack([first * c + second * s, second * c - first * s], axis=2)
         dkv = jnp.concatenate([keys.reshape(every, KV_WIDTH).astype(BF), dkv[:, KV_WIDTH:]], axis=1)
-        space = ((0, 0), (0, wide - width))
-        parts = [jnp.pad(nn(act[:, : micro * rows], dq), space), jnp.pad(nn(attn_t, low), space), nn(act, dkv)]
+        parts = [nn(act[:, : micro * rows], dq), nn(attn_t, low), nn(act, dkv)]
         grad = jnp.concatenate(parts, axis=1).astype(BF)
         return [
             jnp.concatenate([lax.dynamic_slice_in_dim(grad, start, half, 0) for start in starts])
@@ -640,25 +658,25 @@
     )(numbers(given + kept), gain, cosine, sine, dq, attn_t, low, *x_all, *dkv_all)
 
 
-def finish_kernel(count, starts_ref, x_ref, low_ref, kv_ref, dres_ref, gains_ref, cos_ref, sin_ref, *refs):
+def finish_kernel(count, starts_ref, x_ref, low_ref, kv_ref, dres_ref, gain_ref, cos_ref, sin_ref, *refs):
     pieces = refs[:count]
     dx_ref, whole, kv_turned, sems = refs[count:]
     copies = load(pieces, starts_ref, whole, sems)
     turn_keys(kv_ref, kv_turned, 0, cos_ref[...], sin_ref[...])
-    x = upright(x_ref).astype(F32)
-    width = x.shape[1]
-    root = rms_inverse(x)
+    x = across(x_ref).astype(F32)
+    width = x.shape[0]
+    root = lax.rsqrt(jnp.mean(x * x, axis=0, keepdims=True) + EPS)
     normed = x * root
     wait(copies)
-    d_act = nt(low_ref[...], whole[:width, :width])
-    d_act += nt(kv_turned[:, :KV_WIDTH], whole[:width, width:])
-    d_act += nt(kv_turned[:, KV_WIDTH:], whole[width:, width:])
-    d_normed = d_act * gains_ref[0:1, :]
-    d_x = dres_ref[...] + root * (d_normed - normed * jnp.mean(d_normed * normed, axis=-1, keepdims=True))
-    lay_down(d_x.astype(BF), dx_ref)
-
-
-def finish(x, low, kv, dres, gains, cosine, sine, pieces, starts, shape):
+    d_act = nt(whole[:width, :width], low_ref[:, :width])
+    d_act += nt(whole[:width, width:], kv_turned[:, :KV_WIDTH])
+    d_act += nt(whole[width:, width:], kv_turned[:, KV_WIDTH:])
+    d_normed = d_act * gain_ref[...]
+    d_x = dres_ref[...] + root * (d_normed - normed * jnp.mean(d_normed * normed, axis=0, keepdims=True))
+    spread_out(d_x.astype(BF), dx_ref)
+
+
+def finish(x, low, kv, dres, gain, cosine, sine, pieces, starts, shape):
     micro, width, rows = x.shape
     tokens = micro * rows
     table = pl.BlockSpec((tokens, 128), lambda i: (0, 0))
@@ -676,7 +694,7 @@
         ],
         cost_estimate=cost(2 * tokens * width * (width + 2 * KV_WIDTH), 0, x, low, dres, *pieces),
         compiler_params=pltpu.CompilerParams(vmem_limit_bytes=VMEM_LIMIT),
-    )(starts, x, low, kv, dres, gains, cosine, sine, *pieces)
+    )(starts, x, low, kv, dres, gain, cosine, sine, *pieces)
 
 
 def head(ref, h):
@@ -744,6 +762,8 @@
     own = jnp.where(j > i, CLOSED, jnp.where(same, 0.0, own_column))
     one, zero = jnp.ones((rows, 1), F32), jnp.zeros((rows, 1), F32)
     cosine, sine = cos_ref[...], sin_ref[...]
+    if dq_ref.shape[1] > QUERY_HEADS * HEAD_SIZE:
+        dq_ref[:, QUERY_HEADS * HEAD_SIZE :] = jnp.zeros((rows, dq_ref.shape[1] - QUERY_HEADS * HEAD_SIZE), BF)
     for g in range(KEY_VALUE_HEADS):
         keys, values, turned = [], [], []
         for t in range(shards):
@@ -775,7 +795,7 @@
             back = jnp.concatenate(
                 [first * cosine + second * sine, second * cosine - first * sine], axis=0
             )
-            dq_ref[:, h * HEAD_SIZE : (h + 1) * HEAD_SIZE] = jnp.transpose(back).astype(BF)
+            dq_ref[:, h * HEAD_SIZE : (h + 1) * HEAD_SIZE] = jnp.transpose(back.astype(BF))
         for t in range(shards):
             dkv[t][:, g * HEAD_SIZE : (g + 1) * HEAD_SIZE] = dk[t].astype(BF)
             g_value = KEY_VALUE_HEADS + g
@@ -806,7 +826,7 @@
     shards, tokens, width = len(kv), q.shape[0], q.shape[1]
     here = lambda w: pl.BlockSpec((rows, w), lambda i: (m, 0))
     turned = pl.BlockSpec((HALF_HEAD, rows), lambda i: (0, m))
-    outs = (jax.ShapeDtypeStruct((tokens, width), BF),)
+    outs = (jax.ShapeDtypeStruct((tokens, rounded_up(width)), BF),)
     outs += (jax.ShapeDtypeStruct((shards // 2, tokens, 2 * KV_WIDTH), BF),) * 2
     pieces = pl.BlockSpec((shards // 2, rows, 2 * KV_WIDTH), lambda i: (0, m, 0))
     pairs = rows * rows * shards * QUERY_HEADS
@@ -819,7 +839,7 @@
         + [pl.BlockSpec((None,) + bias.shape[1:], lambda i: (m, 0, 0))]
         + [here(width), here(width), here(128), turned, turned]
         + [pl.BlockSpec(memory_space=pl.ANY)] * len(earlier),
-        out_specs=(here(width), pieces, pieces),
+        out_specs=(here(rounded_up(width)), pieces, pieces),
         out_shape=outs,
         input_output_aliases={shards + 7 + i: i for i in range(len(earlier))},
         cost_estimate=cost(40 * HEAD_SIZE * pairs, pairs, q),
@@ -860,8 +880,10 @@
     attn_mine = jnp.where(even, left, right)
     pair_cut = hidden // 2
     pair_mine = lax.dynamic_slice_in_dim(jnp.where(even, w_gate, w_up), side * pair_cut, pair_cut, 1)
-    down_cut = w_down.shape[0] // 2
-    down_mine = lax.dynamic_slice_in_dim(w_down, links.core * down_cut, down_cut, 0)
+    down_own = w_down.T
+    down_cut = width // 2
+    down_mine = lax.dynamic_slice_in_dim(down_own, links.core * down_cut, down_cut, 0)
+    core = numbers([links.core])
 
     attn_near = links.near(attn_mine)
     gain_pieces = links.small_pieces(jnp.stack([norm_first, norm_second]))
@@ -873,7 +895,6 @@
     attn_all = links.far(attn_mine, attn_near)
     attn_swapped = {t: links.swap(attn_near[t]) for t in attn_near}
     pair_near = {1: links.step(pair_mine, 0)}
-    own_down = with_layout_constraint(w_down, Layout(major_to_minor=(0, 1)))
     parents = parent_ids[:, 0]
     seg = jnp.arange(segs)
     after_parent = jnp.concatenate([parents[:, 1:], jnp.full((micro, 1), -1, parents.dtype)], axis=1)
@@ -901,9 +922,12 @@
     bias = jnp.where(open_key, 0.0, CLOSED)
     bias = jnp.pad(bias, ((0, 0), (0, 8 - shards), (0, 0)))
 
-    attn_all, attn_swapped, pair_mine, pair_near, gains, cosine, sine, bias, down_mine, own_down = meet(
-        attn_all, attn_swapped, pair_mine, pair_near, gains, cosine, sine, bias, down_mine, own_down
-    )
+    gain_one, gain_two = gains[0][:, None], gains[1][:, None]
+    tables = (cosine, sine, cosine_t, sine_t, bias, gains, gain_one, gain_two)
+    attn_all, attn_swapped, pair_mine, pair_near, down_mine, tables = meet(
+        attn_all, attn_swapped, pair_mine, pair_near, down_mine, tables
+    )
+    cosine, sine, cosine_t, sine_t, bias, gains, gain_one, gain_two = tables
 
     for t in range(1, shards):
         if t not in attn_swapped:
@@ -962,55 +986,55 @@
             starts += [(row, side * pair_cut), (row, (1 - side) * pair_cut)]
     pair_got = joined(pieces, starts, (2 * width, hidden))
     own = w_down.shape[0]
-    pieces, starts = [own_down], [(links.shard * own, 0)]
+    pieces, starts = [down_own], [(0, links.shard * own)]
     for t in range(1, shards):
         pieces += [down_all[t], down_swapped[t]]
         starts += [
-            ((links.shard ^ links.hops[t]) * own + links.core * down_cut, 0),
-            ((links.shard ^ links.hops[links.twin(t)]) * own + (1 - links.core) * down_cut, 0),
+            (links.core * down_cut, (links.shard ^ links.hops[t]) * own),
+            ((1 - links.core) * down_cut, (links.shard ^ links.hops[links.twin(t)]) * own),
         ]
-    down_got = joined(pieces, starts, (own * shards, width))
+    down_got = joined(pieces, starts, (width, own * shards))
     attn, pair_pieces, down_pieces = meet(attn, pair_got[0], down_got[0])
     pair_got, down_got = (pair_pieces, *pair_got[1:]), (down_pieces, *down_got[1:])
 
     plan = Plan()
     have = lambda *names: [plan.have[name] for name in names]
     x_near = links.near(inputs)
-    made = feed(inputs, attn, cotangent, gains, attention_got, pair_got, down_got)
-    names = ("out", "inner", "slopes", "act", "attn_t", "dy", "resid")
-    plan.have = dict(zip(names, made)) | {"x_near": x_near, "queries": queries, "kv": kv_all, "lse": lse, "attn": attn}
+    far_cotangent = links.swap(cotangent)
+    made = feed(core, inputs, attn, cotangent, gains, attention_got, pair_got, down_got)
+    names = ("out", "inner", "kept", "given", "act", "attn_t", "resid")
+    plan.have = dict(zip(names, made)) | {"x_near": x_near, "far_dy": far_cotangent, "queries": queries, "kv": kv_all, "lse": lse, "attn": attn}
     plan.close()
 
-    down_half = own // 2
-    output_half, output_mine, output_theirs = links.half_rows(shard_rows)
-    down_kept, down_given = links.order(own, links.core * down_half, (1 - links.core) * down_half)
-    wide_kept, wide_given = links.order(shard_rows, 0, 0)
-    some_kept, some_given = links.order(shard_rows, output_mine, output_theirs)
+    half, mine, theirs = links.half_rows(shard_rows)
+    some_kept, some_given = links.order(shard_rows, mine, theirs)
+    cuts = (-(-shard_rows // 32) * 16, shard_rows - -(-shard_rows // 32) * 16)
 
     plan.have["x_all"] = links.far(inputs, plan.have.pop("x_near"))
-    plan.have["rows.given"], plan.have["rows.kept"] = rows_grad(
-        ((*have("inner", "dy"), down_half, down_given, down_kept),)
-    )
+    for name in ("inner", "act", "given"):
+        plan.have["far_" + name] = links.swap(plan.have[name])
+    names = ("d_resid", "low", "d_attn")
+    resid, kept, given = have("resid", "kept", "given")
+    plan.have |= dict(zip(names, feed_back(core, resid, cotangent, kept, given, gain_two, attention_got, pair_got)))
     plan.close()
 
-    for name in ("rows", "wide0", "wide1", "some"):
+    names = ("down.low", "down.high")
+    far_dy, inner, far_inner = have("far_dy", "inner", "far_inner")
+    starts = [(links.shard ^ hop) * own for hop in links.hops]
+    plan.have |= dict(zip(names, down_grad(cotangent, far_dy, inner, far_inner, links.core * down_cut, starts)))
+    plan.close()
+
+    for name in ("down", "wide0", "wide1", "some"):
         plan.start(name, links.reduce(plan, name, name == "some"))
-    plan.advance("rows")
-    cuts = (-(-shard_rows // 32) * 16, shard_rows - -(-shard_rows // 32) * 16)
-    act, slopes = have("act", "slopes")
-    made = wide_grad(act, slopes, shard_rows, cuts, wide_given, wide_kept, links.core)
-    names = [name + part for part in (".given", ".kept") for name in ("wide0", "wide1")]
-    plan.have |= dict(zip(names, made))
+    plan.advance("down")
+    names = ("wide0.low", "wide0.high", "wide1.low", "wide1.high")
+    act, far_act, kept, far_kept = have("act", "far_act", "kept", "far_given")
+    starts = [(links.shard ^ hop) * shard_rows for hop in links.hops]
+    plan.have |= dict(zip(names, wide_grad(act, far_act, kept, far_kept, shard_rows, cuts, starts)))
     plan.close()
 
-    plan.advance("rows", "wide0", "wide1")
-    names = ("d_resid", "d_resid_low", "d_attn")
-    made = feed_back(*have("resid", "dy", "slopes"), gains, attention_got, pair_got)
-    plan.have |= dict(zip(names, made))
-    plan.close()
-
     made = ()
-    hops = [("rows", "wide0"), ("rows", "wide0", "wide1")]
+    hops = [("down", "wide0"), ("down", "wide0", "wide1")]
     for m in range(micro):
         plan.advance(*hops[min(m, 1)])
         q, kv_now, o, do, lse_now = have("queries", "kv", "attn", "d_attn", "lse")
@@ -1023,16 +1047,16 @@
     plan.have["dkv.pieces"] = d_kv
     plan.have["d_queries"] = d_queries
     plan.start("dkv", links.collect(plan, "dkv"))
-    plan.advance("dkv", "wide0", "wide1", "rows")
+    plan.advance("dkv", "wide0", "wide1", "down")
     given, kept = attention_grad(
         plan.have["x_all"],
-        gains[0][:, None],
+        gain_one,
         cosine,
         sine,
         d_queries,
-        *have("attn_t", "d_resid_low"),
+        *have("attn_t", "low"),
         d_kv,
-        output_half,
+        half,
         some_given,
         some_kept,
     )
@@ -1047,15 +1071,20 @@
         have, done = plan.have, plan.have.setdefault("done", {})
         if "dkv" in have and "d_input" not in done:
             done["d_input"] = finish(
-                inputs, have["d_queries"], have["dkv"], have["d_resid"], gains, cosine, sine, *attention_got
+                inputs, have["d_queries"], have["dkv"], have["d_resid"], gain_one, cosine, sine, *attention_got
             )
-        if "rows" in have and "down" not in done:
-            value, other = have["rows"]
-            done["down"] = links.finish_rows(value[:, :width], other[:, :width], own)
+        if "down" in have and "down" not in done:
+            done["down"] = links.finish_rows(*have["down"], width).T
         if "wide0" in have and "wide1" in have and "gate" not in done:
-            halves = [links.finish_pair(*have[name]) for name in ("wide0", "wide1")]
-            done["gate"], done["upper"] = (jnp.concatenate(parts, axis=0) for parts in zip(*halves))
-            done["gain_two"] = gain_grad(norm_second, (w_gate, done["gate"]), (w_up, done["upper"]))
+            done["gate"], done["upper"], gain = settle_wide(
+                core,
+                norm_second.astype(F32)[:, None],
+                (have["wide0"], have["wide1"]),
+                cuts,
+                w_gate,
+                w_up,
+            )
+            done["gain_two"] = gain[:, 0]
         if "some" in have and "query" not in done:
             grad = links.finish_rows(*have["some"], shard_rows)
             first = rounded_up(width)
@@ -1068,7 +1097,7 @@
                 (value_weight, done["value"]),
             )
 
-    order = [("rows", "wide0", "wide1", "dkv", "some")]
+    order = []
     while plan.tasks:
         plan.advance(*(order.pop(0) if order else tuple(plan.tasks)))
         settle()

time: 430 us -> 406 us (0.944)
  other arithmetic: 60 us -> 43.6 us
  waiting for transfers between devices: 113 us -> 107 us
  local copies, waits for them, and re-layouts: 37.2 us -> 32.9 us
    convert_element_type x20 -> x17, other arithmetic: 35 us -> 20.5 us  [total(): return sum((part.astype(F32) for part in parts)).astype(parts[0].dtype)]
    unnamed x153 -> x145, local copies, waits for them, and re-layouts: 23.8 us -> 16.3 us
    ppermute x66 -> x67, waiting for transfers between devices: 113 us -> 107 us  [move(): return lax.ppermute(value, AXES, pairs)]
    pallas_call x2 -> x3, Pallas kernels: 15.9 us -> 19.6 us  [the longest x1 9.19 us: wide_grad(): pl.pallas_call(functools.partial(wide_grad_kernel, cuts, count), grid_spe...]
    ppermute x66 -> x67, starting transfers between devices: 70.9 us -> 69 us  [move(): return lax.ppermute(value, AXES, pairs)]
  transfers between devices with their start and end apart: 66 -> 67, of which waited for: 22 -> 19; matrix products, arithmetic and copies ran while one was open for 12% -> 11% of each run, Pallas kernels for 33% -> 35%
where the time goes in v8:
time: 406 us; the launch traced here: 398 us
  Pallas kernels  143 us (35%)
  waiting for transfers between devices  107 us (26%)
  starting transfers between devices  69 us (17%)
  other arithmetic  43.6 us (11%)
  local copies, waits for them, and re-layouts  32.9 us (8%)
    ppermute x67, waiting for transfers between devices, move(): return lax.ppermute(value, AXES, pairs)  107 us
    ppermute x67, starting transfers between devices, move(): return lax.ppermute(value, AXES, pairs)  69 us
    pallas_call x2, Pallas kernels, attend_back(): pl.pallas_call(functools.partial(attend_back_kernel, shards, seg_rows), g...  34.7 us
    pallas_call x1, Pallas kernels, feed(): pl.pallas_call(functools.partial(feed_kernel, counts), name='feed', in_sp...  26.4 us
    convert_element_type x17, other arithmetic, total(): return sum((part.astype(F32) for part in parts)).astype(parts[0].dtype)  20.5 us
    pallas_call x1, Pallas kernels, feed_back(): pl.pallas_call(functools.partial(feed_back_kernel, counts), name='feed_ba...  17.4 us
    pallas_call x1, Pallas kernels, attend(): pl.pallas_call(functools.partial(attend_kernel, shards, seg_rows), grid=(...  16.7 us
    unnamed x145, local copies, waits for them, and re-layouts  16.3 us
  transfers between devices with their start and end apart: 67, of which 19 were waited for; matrix products, arithmetic and copies ran while one was open for 11% of the time, Pallas kernels for 35%

profile of v8, /device:TPU:0, one launch (start us, length us, event | category | flops | bytes accessed | tf_op | source)
XLA Modules:
  0.0 397.9 jit_solution(7356115681198233142)
XLA Ops:
  3.6 2.4 broadcast_select_fusion.5
  6.0 2.9 collective-permute-start
  8.9 1.5 collective-permute-start.1
  11.1 2.9 collective-permute-start.4
  14.6 1.7 fusion.1
  17.2 2.0 dynamic-slice_select_fusion
  19.3 1.7 multiply_sine_fusion
  21.1 2.0 dynamic-slice_bitcast_fusion
  25.9 2.0 collective-permute-start.8
  28.1 11.6 %collective-permute-done.5.refs_6_ = bf16[240,1280]{1,0:T(8,128)(2,1)S(1)} collective-permute-done((bf16[240,1280]{1,0:T(8,128)(2,1)S(1)}, bf16[240,1280]{1,0:T(8,128)(2,1)S(1)}, u32[]{:S(2)}, u32[]{:S(2)}) %collective-permute-start.5) | collective-permute-done | bytes 614432 | tf_op jit(solution)/shard_map/ppermute | solution.py:88
  40.7 2.1 tile.20
  44.9 2.4 collective-permute-start.11
  47.3 1.9 collective-permute-start.12
  49.2 2.5 copy.72.cos_ref
  51.8 2.5 copy.73.sin_ref
  55.4 6.6 %project.1 = (bf16[512,960]{1,0:T(8,128)(2,1)}, bf16[512,640]{1,0:T(8,128)(2,1)S(1)}) custom-call(s32[16]{0:T(128)S(1)} %stack.194.starts_ref.s0_ref, bf16[2,960,256]{2,1,0:T(8,128)(2,1)} %bitcast.17.x_ref.refs_0_, f32[2,960]{1,0:T(2,128)S(1)} %maximum_convert_fusion.4.gains_ref, f32[2048,128]{1,0:T(8,128)} %copy.72.cos_ref, f32[2048,128]{1,0:T(8,128)} %copy.73.sin_ref, ...), custom_call_target="tpu_custom_call" | custom-call | flops 1572864000 | bytes 7536640 | tf_op jit(solution)/shard_map/project/pallas_call | solution.py:307
  64.1 1.8 collective-permute-start.15
  66.0 13.9 %collective-permute-done.15.refs_15_ = bf16[240,1280]{1,0:T(8,128)(2,1)S(1)} collective-permute-done((bf16[240,1280]{1,0:T(8,128)(2,1)}, bf16[240,1280]{1,0:T(8,128)(2,1)S(1)}, u32[]{:S(2)}, u32[]{:S(2)}) %collective-permute-start.15) | collective-permute-done | bytes 614432 | tf_op jit(solution)/shard_map/ppermute | solution.py:88
  80.6 1.3 collective-permute-start.16
  82.5 7.8 %collective-permute-done.17.refs_18_ = bf16[240,1280]{1,0:T(8,128)(2,1)S(1)} collective-permute-done((bf16[240,1280]{1,0:T(8,128)(2,1)}, bf16[240,1280]{1,0:T(8,128)(2,1)S(1)}, u32[]{:S(2)}, u32[]{:S(2)}) %collective-permute-start.17) | collective-permute-done | bytes 614432 | tf_op jit(solution)/shard_map/ppermute | solution.py:88
  90.3 2.0 collective-permute-done.21.refs_17_
  92.3 5.0 %collective-permute-done.16.refs_3_ = bf16[512,640]{1,0:T(8,128)(2,1)S(1)} collective-permute-done((bf16[512,640]{1,0:T(8,128)(2,1)S(1)}, bf16[512,640]{1,0:T(8,128)(2,1)S(1)}, u32[]{:S(2)}, u32[]{:S(2)}) %collective-permute-start.16) | collective-permute-done | bytes 655392 | tf_op jit(solution)/shard_map/ppermute | solution.py:88
  99.0 1.6 collective-permute-start.23
  101.9 16.7 %attend.1 = (bf16[512,960]{1,0:T(8,128)(2,1)S(1)}, f32[512,128]{1,0:T(8,128)S(1)}) custom-call(bf16[512,960]{1,0:T(8,128)(2,1)S(1)} %copy-done.26, bf16[512,640]{1,0:T(8,128)(2,1)S(1)} %get-tuple-element.506.refs_0_, bf16[512,640]{1,0:T(8,128)(2,1)S(1)} %collective-permute-done.13.refs_1_, bf16[512,640]{1,0:T(8,128)(2,1)S(1)} %collective-permute-done.14.refs_2_, ...), custom_call_target="tpu_custom_call" | custom-call | flops 8053063680 | bytes 983040 | tf_op jit(solution)/shard_map/attend/pallas_call | solution.py:811
  126.2 26.4 %feed.1 = (bf16[2,960,256]{2,1,0:T(8,128)(2,1)}, bf16[512,2560]{1,0:T(8,128)(2,1)}, bf16[512,2560]{1,0:T(8,128)(2,1)}, bf16[512,2560]{1,0:T(8,128)(2,1)}, bf16[9...) custom-call(s32[1]{0:T(128)} %bitcast.core_ref, s32[16]{0:T(128)} %copy-done.24, ...), custom_call_target="tpu_custom_call" | custom-call | flops 11010048000 | bytes 35389440 | tf_op jit(solution)/shard_map/feed/pallas_call | solution.py:385
  153.6 1.5 collective-permute-start.36
  156.3 17.4 %feed_back.1 = (f32[960,512]{1,0:T(8,128)}, bf16[512,1024]{1,0:T(8,128)(2,1)}, bf16[512,960]{1,0:T(8,128)(2,1)}) custom-call(s32[1]{0:T(128)} %bitcast.core_ref, s32[16]{0:T(128)} %copy-done.24, s32[28]{0:T(128)} %stack.197.s1_ref, f32[960,512]{1,0:T(8,128)} %get-tuple-element.408.resid_ref, bf16[2,960,256]{2,1,0:T(8,128)(2,1)} %bitcast.73, ...), custom_call_target="tpu_custom_call" | custom-call | flops 5976883200 | bytes 26935296 | tf_op jit(solution)/shard_map/feed_back/pallas_call | solution.py:437
  173.7 5.9 %down_grad.1 = (bf16[960,640]{1,0:T(8,128)(2,1)S(1)}, bf16[960,640]{1,0:T(8,128)(2,1)S(1)}) custom-call(s32[5]{0:T(128)S(1)} %stack.214.info_ref, bf16[2,960,256]{2,1,0:T(8,128)(2,1)S(1)} %bitcast.75, bf16[2,960,256]{2,1,0:T(8,128)(2,1)S(1)} %collective-permute-done.30.far_cot_ref, bf16[512,2560]{1,0:T(8,128)(2,1)} %get-tuple-element.432.inner_ref, ...), custom_call_target="tpu_custom_call" | custom-call | flops 2516582400 | bytes 9666560 | tf_op jit(solution)/shard_map/down_grad/pallas_call | solution.py:482
  180.3 9.2 %wide_grad.1 = (bf16[256,2560]{1,0:T(8,128)(2,1)S(1)}, bf16[256,2560]{1,0:T(8,128)(2,1)}, bf16[224,2560]{1,0:T(8,128)(2,1)S(1)}, bf16[224,2560]{1,0:T(8,128)(2,1)S(1)}) custom-call(s32[4]{0:T(128)S(1)} %pad_add_fusion.1.starts_ref, bf16[960,512]{1,0:T(8,128)(2,1)S(1)} %copy-done.28, bf16[960,512]{1,0:T(8,128)(2,1)S(1)} %collective-permute-done.33.far_left_ref, ...), custom_call_target="tpu_custom_call" | custom-call | flops 5033164800 | bytes 12124160 | tf_op jit(solution)/shard_map/wide_grad/pallas_call | solution.py:531
  189.5 6.9 %collective-permute-done.37 = bf16[960,640]{1,0:T(8,128)(2,1)S(1)} collective-permute-done((bf16[960,640]{1,0:T(8,128)(2,1)S(1)}, bf16[960,640]{1,0:T(8,128)(2,1)S(1)}, u32[]{:S(2)}, u32[]{:S(2)}) %collective-permute-start.37) | collective-permute-done | bytes 1228832 | tf_op jit(solution)/shard_map/ppermute | solution.py:88
  200.4 17.5 %attend_back.2 = (bf16[512,1024]{1,0:T(8,128)(2,1)S(1)}, bf16[2,512,640]{2,1,0:T(8,128)(2,1)}, bf16[2,512,640]{2,1,0:T(8,128)(2,1)}) custom-call(bf16[512,960]{1,0:T(8,128)(2,1)S(1)} %copy-done.27, bf16[512,640]{1,0:T(8,128)(2,1)S(1)} %copy-done.30, bf16[512,640]{1,0:T(8,128)(2,1)S(1)} %copy-done.32, bf16[512,640]{1,0:T(8,128)(2,1)S(1)} %copy-done.34, ...), custom_call_target="tpu_custom_call" | custom-call | flops 10066329600 | bytes 983040 | tf_op jit(solution)/shard_map/attend_back/pallas_call | solution.py:833
  217.9 3.2 collective-permute-done.39
  223.7 1.3 add_convert_fusion.11
  225.0 2.6 collective-permute-start.40
  227.6 17.2 %attend_back.3 = (bf16[512,1024]{1,0:T(8,128)(2,1)S(1)}, bf16[2,512,640]{2,1,0:T(8,128)(2,1)}, bf16[2,512,640]{2,1,0:T(8,128)(2,1)}) custom-call(bf16[512,960]{1,0:T(8,128)(2,1)S(1)} %copy-done.27, bf16[512,640]{1,0:T(8,128)(2,1)S(1)} %copy-done.30, bf16[512,640]{1,0:T(8,128)(2,1)S(1)} %copy-done.32, ...), custom_call_target="tpu_custom_call", output_to_operand_aliasing={{0}: (11, {}), {1}: (12, {}), {2}: (13, {})} | custom-call | flops 10066329600 | bytes 983040 | tf_op jit(solution)/shard_map/attend_back/pallas_call | solution.py:833
  245.8 2.1 collective-permute-start.45
  249.6 2.0 add_convert_fusion.16
  254.4 13.2 %attention_grad.1 = (bf16[512,2688]{1,0:T(8,128)(2,1)}, bf16[512,2688]{1,0:T(8,128)(2,1)}) custom-call(s32[8]{0:T(128)} %stack.227.starts_ref, f32[960,1]{1,0:T(8,128)} %copy.75.gain_ref, f32[2048,128]{1,0:T(8,128)} %copy.72.cos_ref, f32[2048,128]{1,0:T(8,128)} %copy.73.sin_ref, bf16[512,1024]{1,0:T(8,128)(2,1)} %copy-done.17, ...), custom_call_target="tpu_custom_call" | custom-call | flops 4697620480 | bytes 12058624 | tf_op jit(solution)/shard_map/attention_grad/pallas_call | solution.py:637
  267.9 4.1 %collective-permute-done.43 = bf16[2,512,640]{2,1,0:T(8,128)(2,1)} collective-permute-done((bf16[2,512,640]{2,1,0:T(8,128)(2,1)}, bf16[2,512,640]{2,1,0:T(8,128)(2,1)}, u32[]{:S(2)}, u32[]{:S(2)}) %collective-permute-start.43) | collective-permute-done | bytes 1310752 | tf_op jit(solution)/shard_map/ppermute | solution.py:88
  272.0 1.3 add_convert_fusion.5
  273.3 1.6 collective-permute-start.50
  276.4 2.1 add_convert_fusion.6
  279.3 1.4 add_convert_fusion.15
  280.8 5.4 %collective-permute-start.51 = (bf16[112,2560]{1,0:T(8,128)(2,1)S(1)}, bf16[112,2560]{1,0:T(8,128)(2,1)S(1)}, u32[]{:S(2)}, u32[]{:S(2)}) collective-permute-start(bf16[112,2560]{1,0:T(8,128)(2,1)S(1)} %add_convert_fusion.15), channel_id=1, source_target_pairs={{0,8},{1,9},{2,10},{3,11},{4,12},{5,13},{6,14},{7,15},{24,16},{25,... | collective-permute-start | bytes 1720328 | tf_op jit(solution)/shard_map/ppermute | solution.py:88
  286.2 12.3 %collective-permute-done.51 = bf16[112,2560]{1,0:T(8,128)(2,1)S(1)} collective-permute-done((bf16[112,2560]{1,0:T(8,128)(2,1)S(1)}, bf16[112,2560]{1,0:T(8,128)(2,1)S(1)}, u32[]{:S(2)}, u32[]{:S(2)}) %collective-permute-start.51) | collective-permute-done | bytes 573472 | tf_op jit(solution)/shard_map/ppermute | solution.py:88
  301.0 2.1 add_convert_fusion
  307.0 1.7 fusion.kv_ref
  308.7 8.6 %finish.1 = bf16[2,960,256]{2,1,0:T(8,128)(2,1)} custom-call(s32[16]{0:T(128)S(1)} %copy-done.25, bf16[2,960,256]{2,1,0:T(8,128)(2,1)} %bitcast.17.x_ref.refs_0_, bf16[512,1024]{1,0:T(8,128)(2,1)} %copy-done.17, bf16[512,640]{1,0:T(8,128)(2,1)S(1)} %fusion.kv_ref, f32[960,512]{1,0:T(8,128)} %get-tuple-element.559.dres_ref, f32[960,1]{1,0:T(8,128)S(1)} %copy-done.16, ...), custom_call_target="tpu_custom_call" | custom-call | flops 1572864000 | bytes 8912896 | tf_op jit(solution)/shard_map/finish/pallas_call | solution.py:683
  317.4 4.0 %collective-permute-done.53 = bf16[256,2688]{1,0:T(8,128)(2,1)S(1)} collective-permute-done((bf16[256,2688]{1,0:T(8,128)(2,1)S(1)}, bf16[256,2688]{1,0:T(8,128)(2,1)S(1)}, u32[]{:S(2)}, u32[]{:S(2)}) %collective-permute-start.53) | collective-permute-done | bytes 1376288 | tf_op jit(solution)/shard_map/ppermute | solution.py:88
  321.6 2.8 add_convert_fusion.2
  327.1 1.4 broadcast_select_fusion.3
  328.5 1.6 convert_bitcast_fusion
  330.1 14.0 %collective-permute-done.58 = bf16[112,2560]{1,0:T(8,128)(2,1)} collective-permute-done((bf16[112,2560]{1,0:T(8,128)(2,1)S(1)}, bf16[112,2560]{1,0:T(8,128)(2,1)}, u32[]{:S(2)}, u32[]{:S(2)}) %collective-permute-start.58) | collective-permute-done | bytes 573472 | tf_op jit(solution)/shard_map/ppermute | solution.py:88
  344.1 2.2 broadcast_select_fusion.6.refs_2_
  346.4 2.8 add_convert_fusion.1
  349.2 2.0 constant_dynamic-slice_fusion
  351.2 3.2 collective-permute-start.60
  355.6 6.0 %collective-permute-done.59 = bf16[32,2688]{1,0:T(8,128)(2,1)S(1)} collective-permute-done((bf16[32,2688]{1,0:T(8,128)(2,1)}, bf16[32,2688]{1,0:T(8,128)(2,1)S(1)}, u32[]{:S(2)}, u32[]{:S(2)}) %collective-permute-start.59) | collective-permute-done | bytes 172064 | tf_op jit(solution)/shard_map/ppermute | solution.py:88
  361.6 5.6 %collective-permute-done.60 = bf16[32,2688]{1,0:T(8,128)(2,1)S(1)} collective-permute-done((bf16[32,2688]{1,0:T(8,128)(2,1)}, bf16[32,2688]{1,0:T(8,128)(2,1)S(1)}, u32[]{:S(2)}, u32[]{:S(2)}) %collective-permute-start.60) | collective-permute-done | bytes 172064 | tf_op jit(solution)/shard_map/ppermute | solution.py:88
  369.0 3.4 collective-permute-start.63
  373.4 1.5 collective-permute-start.65
  376.1 4.5 %settle.1 = (f32[240,2560]{1,0:T(8,128)}, f32[240,2560]{1,0:T(8,128)}, f32[240,1]{1,0:T(8,128)S(1)}) custom-call(s32[1]{0:T(128)} %bitcast.core_ref, f32[240,1]{1,0:T(8,128)S(1)} %copy.81.gain_ref, bf16[128,2560]{1,0:T(8,128)(2,1)S(1)} %broadcast_select_fusion.1.refs_0_, bf16[128,2560]{1,0:T(8,128)(2,1)S(1)} %copy-done.21, ...), custom_call_target="tpu_custom_call" | custom-call | flops 2457600 | bytes 7372800 | tf_op jit(solution)/shard_map/settle/pallas_call | solution.py:572
  381.2 6.8 %collective-permute-done.64 = bf16[32,2688]{1,0:T(8,128)(2,1)} collective-permute-done((bf16[32,2688]{1,0:T(8,128)(2,1)S(1)}, bf16[32,2688]{1,0:T(8,128)(2,1)}, u32[]{:S(2)}, u32[]{:S(2)}) %collective-permute-start.64) | collective-permute-done | bytes 172064 | tf_op jit(solution)/shard_map/ppermute | solution.py:88
  389.6 2.1 collective-permute-done.66
  (309 shorter events, 65.8 us)
Async XLA Ops:
  6.0 18.3 %collective-permute-start = (bf16[240,1280]{1,0:T(8,128)(2,1)}, bf16[240,1280]{1,0:T(8,128)(2,1)S(1)}, u32[]{:S(2)}, u32[]{:S(2)}) collective-permute-start(bf16[240,1280]{1,0:T(8,128)(2,1)} %get-tuple-element.659), channel_id=1, source_target_pairs={{0,1},{1,0},{2,3},{3,2},{4,6},{5,7},{6,4},{7,5},{8,9},{9,8},{10,11... | collective-permute-start | bytes 1843208 | tf_op jit(solution)/shard_map/ppermute | solution.py:88
  8.9 15.4 %collective-permute-start.1 = (bf16[240,1280]{1,0:T(8,128)(2,1)}, bf16[240,1280]{1,0:T(8,128)(2,1)}, u32[]{:S(2)}, u32[]{:S(2)}) collective-permute-start(bf16[240,1280]{1,0:T(8,128)(2,1)} %get-tuple-element.659), channel_id=1, source_target_pairs={{0,2},{1,3},{2,0},{3,1},{4,5},{5,4},{6,7},{7,6},{8,10},{9,11},{10,... | collective-permute-start | bytes 1843208 | tf_op jit(solution)/shard_map/ppermute | solution.py:88
  10.5 12.9 %collective-permute-start.2 = (bf16[2,240]{1,0:T(2,128)(2,1)S(1)}, bf16[2,240]{1,0:T(2,128)(2,1)S(1)}, u32[]{:S(2)}, u32[]{:S(2)}) collective-permute-start(bf16[2,240]{1,0:T(2,128)(2,1)S(1)} %pad_maximum_fusion.5), channel_id=1, source_target_pairs={{0,1},{1,0},{2,3},{3,2},{4,5},{5,4},{6,7},{7,6},{8,9},{9,8},{10,11... | collective-permute-start | bytes 2888 | tf_op jit(solution)/shard_map/ppermute | solution.py:88
  11.1 12.3 %collective-permute-start.3 = (bf16[2,240]{1,0:T(2,128)(2,1)S(1)}, bf16[2,240]{1,0:T(2,128)(2,1)S(1)}, u32[]{:S(2)}, u32[]{:S(2)}) collective-permute-start(bf16[2,240]{1,0:T(2,128)(2,1)S(1)} %pad_maximum_fusion.5), channel_id=1, source_target_pairs={{0,2},{1,3},{2,0},{3,1},{4,6},{5,7},{6,4},{7,5},{8,10},{9,11},{10,... | collective-permute-start | bytes 2888 | tf_op jit(solution)/shard_map/ppermute | solution.py:88
  11.1 13.2 %collective-permute-start.4 = (bf16[2,240]{1,0:T(2,128)(2,1)S(1)}, bf16[2,240]{1,0:T(2,128)(2,1)S(1)}, u32[]{:S(2)}, u32[]{:S(2)}) collective-permute-start(bf16[2,240]{1,0:T(2,128)(2,1)S(1)} %pad_maximum_fusion.5), channel_id=1, source_target_pairs={{0,3},{1,2},{2,1},{3,0},{4,7},{5,6},{6,5},{7,4},{8,11},{9,10},{10,... | collective-permute-start | bytes 2888 | tf_op jit(solution)/shard_map/ppermute | solution.py:88
  24.3 15.5 %collective-permute-start.5 = (bf16[240,1280]{1,0:T(8,128)(2,1)S(1)}, bf16[240,1280]{1,0:T(8,128)(2,1)S(1)}, u32[]{:S(2)}, u32[]{:S(2)}) collective-permute-start(bf16[240,1280]{1,0:T(8,128)(2,1)S(1)} %collective-permute-done.refs_2_), channel_id=1, source_target_pairs={{0,2},{1,3},{2,0},{3,1},{4,5},{5,4},{6,7},{7,6},{8,10},{9,11},{10,... | collective-permute-start | bytes 1843208 | tf_op jit(solution)/shard_map/ppermute | solution.py:88
  25.0 14.8 %collective-permute-start.6 = (bf16[240,1280]{1,0:T(8,128)(2,1)S(1)}, bf16[240,1280]{1,0:T(8,128)(2,1)S(1)}, u32[]{:S(2)}, u32[]{:S(2)}) collective-permute-start(bf16[240,1280]{1,0:T(8,128)(2,1)S(1)} %collective-permute-done.refs_2_), channel_id=1, source_target_pairs={{0,4},{1,5},{2,6},{3,7},{4,0},{5,1},{6,2},{7,3},{8,12},{9,13},{10,... | collective-permute-start | bytes 1843208 | tf_op jit(solution)/shard_map/ppermute | solution.py:88
  25.8 13.9 %collective-permute-start.7 = (bf16[240,1280]{1,0:T(8,128)(2,1)}, bf16[240,1280]{1,0:T(8,128)(2,1)S(1)}, u32[]{:S(2)}, u32[]{:S(2)}) collective-permute-start(bf16[240,1280]{1,0:T(8,128)(2,1)} %collective-permute-done.1.refs_4_), channel_id=1, source_target_pairs={{0,4},{1,5},{2,6},{3,7},{4,0},{5,1},{6,2},{7,3},{8,12},{9,13},{10,... | collective-permute-start | bytes 1843208 | tf_op jit(solution)/shard_map/ppermute | solution.py:88
  25.9 14.7 %collective-permute-start.8 = (bf16[240,1280]{1,0:T(8,128)(2,1)}, bf16[240,1280]{1,0:T(8,128)(2,1)}, u32[]{:S(2)}, u32[]{:S(2)}) collective-permute-start(bf16[240,1280]{1,0:T(8,128)(2,1)} %dynamic-slice_select_fusion), channel_id=1, source_target_pairs={{0,1},{1,0},{2,3},{3,2},{4,6},{5,7},{6,4},{7,5},{8,9},{9,8},{10,11... | collective-permute-start | bytes 1843208 | tf_op jit(solution)/shard_map/ppermute | solution.py:88
  43.9 10.5 %collective-permute-start.9 = (bf16[240,1280]{1,0:T(8,128)(2,1)S(1)}, bf16[240,1280]{1,0:T(8,128)(2,1)}, u32[]{:S(2)}, u32[]{:S(2)}) collective-permute-start(bf16[240,1280]{1,0:T(8,128)(2,1)S(1)} %collective-permute-done.5.refs_6_), channel_id=1, source_target_pairs={{0,4},{1,5},{2,6},{3,7},{4,0},{5,1},{6,2},{7,3},{8,12},{9,13},{10,... | collective-permute-start | bytes 1843208 | tf_op jit(solution)/shard_map/ppermute | solution.py:88
  44.2 18.4 %collective-permute-start.10 = (bf16[240,1280]{1,0:T(8,128)(2,1)}, bf16[240,1280]{1,0:T(8,128)(2,1)}, u32[]{:S(2)}, u32[]{:S(2)}) collective-permute-start(bf16[240,1280]{1,0:T(8,128)(2,1)} %dynamic-slice_select_fusion), channel_id=1, source_target_pairs={{0,2},{1,3},{2,0},{3,1},{4,5},{5,4},{6,7},{7,6},{8,10},{9,11},{10,... | collective-permute-start | bytes 1843208 | tf_op jit(solution)/shard_map/ppermute | solution.py:88
  44.9 17.8 %collective-permute-start.11 = (bf16[240,1280]{1,0:T(8,128)(2,1)}, bf16[240,1280]{1,0:T(8,128)(2,1)}, u32[]{:S(2)}, u32[]{:S(2)}) collective-permute-start(bf16[240,1280]{1,0:T(8,128)(2,1)} %collective-permute-done.8.refs_10_), channel_id=1, source_target_pairs={{0,8},{1,9},{2,10},{3,11},{4,12},{5,13},{6,14},{7,15},{8,0},{9,1},... | collective-permute-start | bytes 1843208 | tf_op jit(solution)/shard_map/ppermute | solution.py:88
  47.3 15.4 %collective-permute-start.12 = (bf16[480,640]{1,0:T(8,128)(2,1)}, bf16[480,640]{1,0:T(8,128)(2,1)}, u32[]{:S(2)}, u32[]{:S(2)}) collective-permute-start(bf16[480,640]{1,0:T(8,128)(2,1)} %dynamic-slice_bitcast_fusion), channel_id=1, source_target_pairs={{0,1},{1,0},{2,3},{3,2},{4,6},{5,7},{6,4},{7,5},{8,9},{9,8},{10,11... | collective-permute-start | bytes 1843208 | tf_op jit(solution)/shard_map/ppermute | solution.py:88
  62.7 17.2 %collective-permute-start.13 = (bf16[512,640]{1,0:T(8,128)(2,1)S(1)}, bf16[512,640]{1,0:T(8,128)(2,1)S(1)}, u32[]{:S(2)}, u32[]{:S(2)}) collective-permute-start(bf16[512,640]{1,0:T(8,128)(2,1)S(1)} %get-tuple-element.506.refs_0_), channel_id=1, source_target_pairs={{0,1},{1,0},{2,3},{3,2},{4,6},{5,7},{6,4},{7,5},{8,9},{9,8},{10,11... | collective-permute-start | bytes 1966088 | tf_op jit(solution)/shard_map/ppermute | solution.py:88
  62.9 17.0 %collective-permute-start.14 = (bf16[512,640]{1,0:T(8,128)(2,1)S(1)}, bf16[512,640]{1,0:T(8,128)(2,1)S(1)}, u32[]{:S(2)}, u32[]{:S(2)}) collective-permute-start(bf16[512,640]{1,0:T(8,128)(2,1)S(1)} %get-tuple-element.506.refs_0_), channel_id=1, source_target_pairs={{0,2},{1,3},{2,0},{3,1},{4,5},{5,4},{6,7},{7,6},{8,10},{9,11},{10,... | collective-permute-start | bytes 1966088 | tf_op jit(solution)/shard_map/ppermute | solution.py:88
  64.1 15.7 %collective-permute-start.15 = (bf16[240,1280]{1,0:T(8,128)(2,1)}, bf16[240,1280]{1,0:T(8,128)(2,1)S(1)}, u32[]{:S(2)}, u32[]{:S(2)}) collective-permute-start(bf16[240,1280]{1,0:T(8,128)(2,1)} %collective-permute-done.10.refs_14_), channel_id=1, source_target_pairs={{0,8},{1,9},{2,10},{3,11},{4,12},{5,13},{6,14},{7,15},{8,0},{9,1},... | collective-permute-start | bytes 1843208 | tf_op jit(solution)/shard_map/ppermute | solution.py:88
  79.9 10.4 %collective-permute-start.17 = (bf16[240,1280]{1,0:T(8,128)(2,1)}, bf16[240,1280]{1,0:T(8,128)(2,1)S(1)}, u32[]{:S(2)}, u32[]{:S(2)}) collective-permute-start(bf16[240,1280]{1,0:T(8,128)(2,1)} %collective-permute-done.8.refs_10_), channel_id=1, source_target_pairs={{0,2},{1,3},{2,0},{3,1},{4,5},{5,4},{6,7},{7,6},{8,10},{9,11},{10,... | collective-permute-start | bytes 1843208 | tf_op jit(solution)/shard_map/ppermute | solution.py:88
  80.6 16.7 %collective-permute-start.16 = (bf16[512,640]{1,0:T(8,128)(2,1)S(1)}, bf16[512,640]{1,0:T(8,128)(2,1)S(1)}, u32[]{:S(2)}, u32[]{:S(2)}) collective-permute-start(bf16[512,640]{1,0:T(8,128)(2,1)S(1)} %collective-permute-done.13.refs_1_), channel_id=1, source_target_pairs={{0,2},{1,3},{2,0},{3,1},{4,5},{5,4},{6,7},{7,6},{8,10},{9,11},{10,... | collective-permute-start | bytes 1966088 | tf_op jit(solution)/shard_map/ppermute | solution.py:88
  82.0 8.3 %collective-permute-start.18 = (bf16[240,1280]{1,0:T(8,128)(2,1)}, bf16[240,1280]{1,0:T(8,128)(2,1)S(1)}, u32[]{:S(2)}, u32[]{:S(2)}) collective-permute-start(bf16[240,1280]{1,0:T(8,128)(2,1)} %collective-permute-done.8.refs_10_), channel_id=1, source_target_pairs={{0,4},{1,5},{2,6},{3,7},{4,0},{5,1},{6,2},{7,3},{8,12},{9,13},{10,... | collective-permute-start | bytes 1843208 | tf_op jit(solution)/shard_map/ppermute | solution.py:88
  82.0 8.4 %collective-permute-start.19 = (bf16[240,1280]{1,0:T(8,128)(2,1)}, bf16[240,1280]{1,0:T(8,128)(2,1)S(1)}, u32[]{:S(2)}, u32[]{:S(2)}) collective-permute-start(bf16[240,1280]{1,0:T(8,128)(2,1)} %collective-permute-done.10.refs_14_), channel_id=1, source_target_pairs={{0,4},{1,5},{2,6},{3,7},{4,0},{5,1},{6,2},{7,3},{8,12},{9,13},{10,... | collective-permute-start | bytes 1843208 | tf_op jit(solution)/shard_map/ppermute | solution.py:88
  82.5 7.9 %collective-permute-start.20 = (bf16[240,1280]{1,0:T(8,128)(2,1)}, bf16[240,1280]{1,0:T(8,128)(2,1)S(1)}, u32[]{:S(2)}, u32[]{:S(2)}) collective-permute-start(bf16[240,1280]{1,0:T(8,128)(2,1)} %collective-permute-done.11.refs_11_), channel_id=1, source_target_pairs={{0,4},{1,5},{2,6},{3,7},{4,0},{5,1},{6,2},{7,3},{8,12},{9,13},{10,... | collective-permute-start | bytes 1843208 | tf_op jit(solution)/shard_map/ppermute | solution.py:88
  97.3 23.0 %collective-permute-start.24 = (bf16[240,1280]{1,0:T(8,128)(2,1)S(1)}, bf16[240,1280]{1,0:T(8,128)(2,1)}, u32[]{:S(2)}, u32[]{:S(2)}) collective-permute-start(bf16[240,1280]{1,0:T(8,128)(2,1)S(1)} %collective-permute-done.17.refs_18_), channel_id=1, source_target_pairs={{0,8},{1,9},{2,10},{3,11},{4,12},{5,13},{6,14},{7,15},{8,0},{9,1},... | collective-permute-start | bytes 1843208 | tf_op jit(solution)/shard_map/ppermute | solution.py:88
  98.6 21.7 %collective-permute-start.25 = (bf16[240,1280]{1,0:T(8,128)(2,1)S(1)}, bf16[240,1280]{1,0:T(8,128)(2,1)S(1)}, u32[]{:S(2)}, u32[]{:S(2)}) collective-permute-start(bf16[240,1280]{1,0:T(8,128)(2,1)S(1)} %collective-permute-done.17.refs_18_), channel_id=1, source_target_pairs={{0,4},{1,5},{2,6},{3,7},{4,0},{5,1},{6,2},{7,3},{8,12},{9,13},{10,... | collective-permute-start | bytes 1843208 | tf_op jit(solution)/shard_map/ppermute | solution.py:88
  98.6 21.7 %collective-permute-start.22 = (bf16[480,640]{1,0:T(8,128)(2,1)}, bf16[480,640]{1,0:T(8,128)(2,1)}, u32[]{:S(2)}, u32[]{:S(2)}) collective-permute-start(bf16[480,640]{1,0:T(8,128)(2,1)} %dynamic-slice_bitcast_fusion), channel_id=1, source_target_pairs={{0,2},{1,3},{2,0},{3,1},{4,5},{5,4},{6,7},{7,6},{8,10},{9,11},{10,... | collective-permute-start | bytes 1843208 | tf_op jit(solution)/shard_map/ppermute | solution.py:88
  99.0 21.3 %collective-permute-start.23 = (bf16[480,640]{1,0:T(8,128)(2,1)}, bf16[480,640]{1,0:T(8,128)(2,1)}, u32[]{:S(2)}, u32[]{:S(2)}) collective-permute-start(bf16[480,640]{1,0:T(8,128)(2,1)} %collective-permute-done.12.refs_23_), channel_id=1, source_target_pairs={{0,2},{1,3},{2,0},{3,1},{4,5},{5,4},{6,7},{7,6},{8,10},{9,11},{10,... | collective-permute-start | bytes 1843208 | tf_op jit(solution)/shard_map/ppermute | solution.py:88
  121.2 4.0 %collective-permute-start.27 = (bf16[480,640]{1,0:T(8,128)(2,1)}, bf16[480,640]{1,0:T(8,128)(2,1)S(1)}, u32[]{:S(2)}, u32[]{:S(2)}) collective-permute-start(bf16[480,640]{1,0:T(8,128)(2,1)} %collective-permute-done.12.refs_23_), channel_id=1, source_target_pairs={{0,4},{1,5},{2,6},{3,7},{4,0},{5,1},{6,2},{7,3},{8,12},{9,13},{10,... | collective-permute-start | bytes 1843208 | tf_op jit(solution)/shard_map/ppermute | solution.py:88
  121.7 4.5 %collective-permute-start.28 = (bf16[480,640]{1,0:T(8,128)(2,1)}, bf16[480,640]{1,0:T(8,128)(2,1)}, u32[]{:S(2)}, u32[]{:S(2)}) collective-permute-start(bf16[480,640]{1,0:T(8,128)(2,1)} %collective-permute-done.22.refs_25_), channel_id=1, source_target_pairs={{0,4},{1,5},{2,6},{3,7},{4,0},{5,1},{6,2},{7,3},{8,12},{9,13},{10,... | collective-permute-start | bytes 1843208 | tf_op jit(solution)/shard_map/ppermute | solution.py:88
  121.7 4.5 %collective-permute-start.29 = (bf16[480,640]{1,0:T(8,128)(2,1)}, bf16[480,640]{1,0:T(8,128)(2,1)}, u32[]{:S(2)}, u32[]{:S(2)}) collective-permute-start(bf16[480,640]{1,0:T(8,128)(2,1)} %collective-permute-done.23.refs_27_), channel_id=1, source_target_pairs={{0,4},{1,5},{2,6},{3,7},{4,0},{5,1},{6,2},{7,3},{8,12},{9,13},{10,... | collective-permute-start | bytes 1843208 | tf_op jit(solution)/shard_map/ppermute | solution.py:88
  122.2 30.4 %collective-permute-start.31 = (bf16[2,960,256]{2,1,0:T(8,128)(2,1)}, bf16[2,960,256]{2,1,0:T(8,128)(2,1)}, u32[]{:S(2)}, u32[]{:S(2)}) collective-permute-start(bf16[2,960,256]{2,1,0:T(8,128)(2,1)} %bitcast.17.x_ref.refs_0_), channel_id=1, source_target_pairs={{0,1},{1,0},{2,3},{3,2},{4,6},{5,7},{6,4},{7,5},{8,9},{9,8},{10,11... | collective-permute-start | bytes 2949128 | tf_op jit(solution)/shard_map/ppermute | solution.py:88
  124.7 27.9 %collective-permute-start.32 = (bf16[2,960,256]{2,1,0:T(8,128)(2,1)}, bf16[2,960,256]{2,1,0:T(8,128)(2,1)}, u32[]{:S(2)}, u32[]{:S(2)}) collective-permute-start(bf16[2,960,256]{2,1,0:T(8,128)(2,1)} %bitcast.17.x_ref.refs_0_), channel_id=1, source_target_pairs={{0,2},{1,3},{2,0},{3,1},{4,5},{5,4},{6,7},{7,6},{8,10},{9,11},{10,... | collective-permute-start | bytes 2949128 | tf_op jit(solution)/shard_map/ppermute | solution.py:88
  126.0 26.6 %collective-permute-start.30 = (bf16[2,960,256]{2,1,0:T(8,128)(2,1)S(1)}, bf16[2,960,256]{2,1,0:T(8,128)(2,1)S(1)}, u32[]{:S(2)}, u32[]{:S(2)}) collective-permute-start(bf16[2,960,256]{2,1,0:T(8,128)(2,1)S(1)} %bitcast.74), channel_id=1, source_target_pairs={{0,4},{1,5},{2,6},{3,7},{4,0},{5,1},{6,2},{7,3},{8,12},{9,13},{10,... | collective-permute-start | bytes 2949128 | tf_op jit(solution)/shard_map/ppermute | solution.py:88
  152.6 21.0 %collective-permute-start.34 = (bf16[512,2560]{1,0:T(8,128)(2,1)}, bf16[512,2560]{1,0:T(8,128)(2,1)}, u32[]{:S(2)}, u32[]{:S(2)}) collective-permute-start(bf16[512,2560]{1,0:T(8,128)(2,1)} %get-tuple-element.410.given_ref), channel_id=1, source_target_pairs={{0,4},{1,5},{2,6},{3,7},{4,0},{5,1},{6,2},{7,3},{8,12},{9,13},{10,... | collective-permute-start | bytes 7864328 | tf_op jit(solution)/shard_map/ppermute | solution.py:88
  153.1 20.6 %collective-permute-start.35 = (bf16[512,2560]{1,0:T(8,128)(2,1)}, bf16[512,2560]{1,0:T(8,128)(2,1)}, u32[]{:S(2)}, u32[]{:S(2)}) collective-permute-start(bf16[512,2560]{1,0:T(8,128)(2,1)} %get-tuple-element.432.inner_ref), channel_id=1, source_target_pairs={{0,4},{1,5},{2,6},{3,7},{4,0},{5,1},{6,2},{7,3},{8,12},{9,13},{10,... | collective-permute-start | bytes 7864328 | tf_op jit(solution)/shard_map/ppermute | solution.py:88
  153.2 20.4 %collective-permute-start.33 = (bf16[960,512]{1,0:T(8,128)(2,1)}, bf16[960,512]{1,0:T(8,128)(2,1)S(1)}, u32[]{:S(2)}, u32[]{:S(2)}) collective-permute-start(bf16[960,512]{1,0:T(8,128)(2,1)} %get-tuple-element.451.left_ref), channel_id=1, source_target_pairs={{0,4},{1,5},{2,6},{3,7},{4,0},{5,1},{6,2},{7,3},{8,12},{9,13},{10,... | collective-permute-start | bytes 2949128 | tf_op jit(solution)/shard_map/ppermute | solution.py:88
  153.6 20.0 %collective-permute-start.36 = (bf16[2,960,256]{2,1,0:T(8,128)(2,1)}, bf16[2,960,256]{2,1,0:T(8,128)(2,1)}, u32[]{:S(2)}, u32[]{:S(2)}) collective-permute-start(bf16[2,960,256]{2,1,0:T(8,128)(2,1)} %collective-permute-done.31.refs_1_), channel_id=1, source_target_pairs={{0,2},{1,3},{2,0},{3,1},{4,5},{5,4},{6,7},{7,6},{8,10},{9,11},{10,... | collective-permute-start | bytes 2949128 | tf_op jit(solution)/shard_map/ppermute | solution.py:88
  179.6 16.8 %collective-permute-start.37 = (bf16[960,640]{1,0:T(8,128)(2,1)S(1)}, bf16[960,640]{1,0:T(8,128)(2,1)S(1)}, u32[]{:S(2)}, u32[]{:S(2)}) collective-permute-start(bf16[960,640]{1,0:T(8,128)(2,1)S(1)} %get-tuple-element.476), channel_id=1, source_target_pairs={{0,2},{1,3},{2,0},{3,1},{4,5},{5,4},{6,7},{7,6},{8,10},{9,11},{10,... | collective-permute-start | bytes 3686408 | tf_op jit(solution)/shard_map/ppermute | solution.py:88
  197.4 23.7 %collective-permute-start.39 = (bf16[256,2560]{1,0:T(8,128)(2,1)}, bf16[256,2560]{1,0:T(8,128)(2,1)S(1)}, u32[]{:S(2)}, u32[]{:S(2)}) collective-permute-start(bf16[256,2560]{1,0:T(8,128)(2,1)} %get-tuple-element.503), channel_id=1, source_target_pairs={{0,2},{1,3},{2,0},{3,1},{4,5},{5,4},{6,7},{7,6},{8,10},{9,11},{10,... | collective-permute-start | bytes 3932168 | tf_op jit(solution)/shard_map/ppermute | solution.py:88
  199.1 18.7 %collective-permute-start.38 = (bf16[480,640]{1,0:T(8,128)(2,1)S(1)}, bf16[480,640]{1,0:T(8,128)(2,1)S(1)}, u32[]{:S(2)}, u32[]{:S(2)}) collective-permute-start(bf16[480,640]{1,0:T(8,128)(2,1)S(1)} %add_convert_fusion.12), channel_id=1, source_target_pairs={{0,1},{1,0},{2,3},{3,2},{4,6},{5,7},{6,4},{7,5},{8,9},{9,8},{10,11... | collective-permute-start | bytes 1843208 | tf_op jit(solution)/shard_map/ppermute | solution.py:88
  221.3 23.5 %collective-permute-start.41 = (bf16[128,2560]{1,0:T(8,128)(2,1)S(1)}, bf16[128,2560]{1,0:T(8,128)(2,1)S(1)}, u32[]{:S(2)}, u32[]{:S(2)}) collective-permute-start(bf16[128,2560]{1,0:T(8,128)(2,1)S(1)} %add_convert_fusion.8), channel_id=1, source_target_pairs={{0,1},{1,0},{2,3},{3,2},{4,6},{5,7},{6,4},{7,5},{8,9},{9,8},{10,11... | collective-permute-start | bytes 1966088 | tf_op jit(solution)/shard_map/ppermute | solution.py:88
  222.5 22.3 %collective-permute-start.42 = (bf16[224,2560]{1,0:T(8,128)(2,1)S(1)}, bf16[224,2560]{1,0:T(8,128)(2,1)}, u32[]{:S(2)}, u32[]{:S(2)}) collective-permute-start(bf16[224,2560]{1,0:T(8,128)(2,1)S(1)} %get-tuple-element.530), channel_id=1, source_target_pairs={{0,2},{1,3},{2,0},{3,1},{4,5},{5,4},{6,7},{7,6},{8,10},{9,11},{10,... | collective-permute-start | bytes 3440648 | tf_op jit(solution)/shard_map/ppermute | solution.py:88
  225.0 19.8 %collective-permute-start.40 = (bf16[480,640]{1,0:T(8,128)(2,1)S(1)}, bf16[480,640]{1,0:T(8,128)(2,1)S(1)}, u32[]{:S(2)}, u32[]{:S(2)}) collective-permute-start(bf16[480,640]{1,0:T(8,128)(2,1)S(1)} %add_convert_fusion.11), channel_id=1, source_target_pairs={{0,8},{1,9},{2,10},{3,11},{4,12},{5,13},{6,14},{7,15},{24,16},{25,... | collective-permute-start | bytes 1843208 | tf_op jit(solution)/shard_map/ppermute | solution.py:88
  245.8 22.1 %collective-permute-start.45 = (bf16[128,2560]{1,0:T(8,128)(2,1)S(1)}, bf16[128,2560]{1,0:T(8,128)(2,1)}, u32[]{:S(2)}, u32[]{:S(2)}) collective-permute-start(bf16[128,2560]{1,0:T(8,128)(2,1)S(1)} %add_convert_fusion.7), channel_id=1, source_target_pairs={{0,8},{1,9},{2,10},{3,11},{4,12},{5,13},{6,14},{7,15},{24,16},{25,... | collective-permute-start | bytes 1966088 | tf_op jit(solution)/shard_map/ppermute | solution.py:88
  247.9 24.1 %collective-permute-start.43 = (bf16[2,512,640]{2,1,0:T(8,128)(2,1)}, bf16[2,512,640]{2,1,0:T(8,128)(2,1)}, u32[]{:S(2)}, u32[]{:S(2)}) collective-permute-start(bf16[2,512,640]{2,1,0:T(8,128)(2,1)} %get-tuple-element.535.refs_5_), channel_id=1, source_target_pairs={{0,2},{1,3},{2,0},{3,1},{4,5},{5,4},{6,7},{7,6},{8,10},{9,11},{10,... | collective-permute-start | bytes 3932168 | tf_op jit(solution)/shard_map/ppermute | solution.py:88
  248.9 18.9 %collective-permute-start.44 = (bf16[480,640]{1,0:T(8,128)(2,1)S(1)}, bf16[480,640]{1,0:T(8,128)(2,1)S(1)}, u32[]{:S(2)}, u32[]{:S(2)}) collective-permute-start(bf16[480,640]{1,0:T(8,128)(2,1)S(1)} %add_convert_fusion.10), channel_id=1, source_target_pairs={{8,16},{9,17},{10,18},{11,19},{12,20},{13,21},{14,22},{15,23},{16,... | collective-permute-start | bytes 1843208 | tf_op jit(solution)/shard_map/ppermute | solution.py:88
  251.6 16.2 %collective-permute-start.46 = (bf16[112,2560]{1,0:T(8,128)(2,1)}, bf16[112,2560]{1,0:T(8,128)(2,1)}, u32[]{:S(2)}, u32[]{:S(2)}) collective-permute-start(bf16[112,2560]{1,0:T(8,128)(2,1)} %add_convert_fusion.16), channel_id=1, source_target_pairs={{0,1},{1,0},{2,3},{3,2},{4,6},{5,7},{6,4},{7,5},{8,9},{9,8},{10,11... | collective-permute-start | bytes 1720328 | tf_op jit(solution)/shard_map/ppermute | solution.py:88
  272.0 26.5 %collective-permute-start.49 = (bf16[512,2688]{1,0:T(8,128)(2,1)}, bf16[512,2688]{1,0:T(8,128)(2,1)}, u32[]{:S(2)}, u32[]{:S(2)}) collective-permute-start(bf16[512,2688]{1,0:T(8,128)(2,1)} %get-tuple-element.555), channel_id=1, source_target_pairs={{0,4},{1,5},{2,6},{3,7},{4,0},{5,1},{6,2},{7,3},{8,12},{9,13},{10,... | collective-permute-start | bytes 8257544 | tf_op jit(solution)/shard_map/ppermute | solution.py:88
  273.3 25.2 %collective-permute-start.50 = (bf16[128,2560]{1,0:T(8,128)(2,1)S(1)}, bf16[128,2560]{1,0:T(8,128)(2,1)}, u32[]{:S(2)}, u32[]{:S(2)}) collective-permute-start(bf16[128,2560]{1,0:T(8,128)(2,1)S(1)} %add_convert_fusion.5), channel_id=1, source_target_pairs={{8,16},{9,17},{10,18},{11,19},{12,20},{13,21},{14,22},{15,23},{16,... | collective-permute-start | bytes 1966088 | tf_op jit(solution)/shard_map/ppermute | solution.py:88
  275.1 23.4 %collective-permute-start.48 = (bf16[480,640]{1,0:T(8,128)(2,1)S(1)}, bf16[480,640]{1,0:T(8,128)(2,1)}, u32[]{:S(2)}, u32[]{:S(2)}) collective-permute-start(bf16[480,640]{1,0:T(8,128)(2,1)S(1)} %add_convert_fusion.9), channel_id=1, source_target_pairs={{8,0},{9,1},{10,2},{11,3},{12,4},{13,5},{14,6},{15,7},{16,24},{17,... | collective-permute-start | bytes 1843208 | tf_op jit(solution)/shard_map/ppermute | solution.py:88
  278.5 20.0 %collective-permute-start.47 = (bf16[1,512,640]{2,1,0:T(8,128)(2,1)}, bf16[1,512,640]{2,1,0:T(8,128)(2,1)}, u32[]{:S(2)}, u32[]{:S(2)}) collective-permute-start(bf16[1,512,640]{2,1,0:T(8,128)(2,1)} %add_convert_fusion.6), channel_id=1, source_target_pairs={{0,1},{1,0},{2,3},{3,2},{4,6},{5,7},{6,4},{7,5},{8,9},{9,8},{10,11... | collective-permute-start | bytes 1966088 | tf_op jit(solution)/shard_map/ppermute | solution.py:88
  280.8 17.7 %collective-permute-start.51 = (bf16[112,2560]{1,0:T(8,128)(2,1)S(1)}, bf16[112,2560]{1,0:T(8,128)(2,1)S(1)}, u32[]{:S(2)}, u32[]{:S(2)}) collective-permute-start(bf16[112,2560]{1,0:T(8,128)(2,1)S(1)} %add_convert_fusion.15), channel_id=1, source_target_pairs={{0,8},{1,9},{2,10},{3,11},{4,12},{5,13},{6,14},{7,15},{24,16},{25,... | collective-permute-start | bytes 1720328 | tf_op jit(solution)/shard_map/ppermute | solution.py:88
  299.7 17.7 %collective-permute-start.54 = (bf16[128,2560]{1,0:T(8,128)(2,1)S(1)}, bf16[128,2560]{1,0:T(8,128)(2,1)S(1)}, u32[]{:S(2)}, u32[]{:S(2)}) collective-permute-start(bf16[128,2560]{1,0:T(8,128)(2,1)S(1)} %add_convert_fusion.3), channel_id=1, source_target_pairs={{8,0},{9,1},{10,2},{11,3},{12,4},{13,5},{14,6},{15,7},{16,24},{17,... | collective-permute-start | bytes 1966088 | tf_op jit(solution)/shard_map/ppermute | solution.py:88
  303.1 18.4 %collective-permute-start.53 = (bf16[256,2688]{1,0:T(8,128)(2,1)S(1)}, bf16[256,2688]{1,0:T(8,128)(2,1)S(1)}, u32[]{:S(2)}, u32[]{:S(2)}) collective-permute-start(bf16[256,2688]{1,0:T(8,128)(2,1)S(1)} %add_convert_fusion), channel_id=1, source_target_pairs={{0,2},{1,3},{2,0},{3,1},{4,5},{5,4},{6,7},{7,6},{8,10},{9,11},{10,... | collective-permute-start | bytes 4128776 | tf_op jit(solution)/shard_map/ppermute | solution.py:88
  305.6 11.8 %collective-permute-start.52 = (bf16[480,640]{1,0:T(8,128)(2,1)S(1)}, bf16[480,640]{1,0:T(8,128)(2,1)S(1)}, u32[]{:S(2)}, u32[]{:S(2)}) collective-permute-start(bf16[480,640]{1,0:T(8,128)(2,1)S(1)} %broadcast_select_fusion.4), channel_id=1, source_target_pairs={{0,4},{1,5},{2,6},{3,7},{4,0},{5,1},{6,2},{7,3},{8,12},{9,13},{10,... | collective-permute-start | bytes 1843208 | tf_op jit(solution)/shard_map/ppermute | solution.py:88
  305.9 11.5 %collective-permute-start.55 = (bf16[112,2560]{1,0:T(8,128)(2,1)S(1)}, bf16[112,2560]{1,0:T(8,128)(2,1)S(1)}, u32[]{:S(2)}, u32[]{:S(2)}) collective-permute-start(bf16[112,2560]{1,0:T(8,128)(2,1)S(1)} %add_convert_fusion.14), channel_id=1, source_target_pairs={{8,16},{9,17},{10,18},{11,19},{12,20},{13,21},{14,22},{15,23},{16,... | collective-permute-start | bytes 1720328 | tf_op jit(solution)/shard_map/ppermute | solution.py:88
  321.6 22.6 %collective-permute-start.57 = (bf16[128,2560]{1,0:T(8,128)(2,1)S(1)}, bf16[128,2560]{1,0:T(8,128)(2,1)S(1)}, u32[]{:S(2)}, u32[]{:S(2)}) collective-permute-start(bf16[128,2560]{1,0:T(8,128)(2,1)S(1)} %broadcast_select_fusion.1.refs_0_), channel_id=1, source_target_pairs={{0,4},{1,5},{2,6},{3,7},{4,0},{5,1},{6,2},{7,3},{8,12},{9,13},{10,... | collective-permute-start | bytes 1966088 | tf_op jit(solution)/shard_map/ppermute | solution.py:88
  324.4 19.7 %collective-permute-start.56 = (bf16[128,2688]{1,0:T(8,128)(2,1)}, bf16[128,2688]{1,0:T(8,128)(2,1)}, u32[]{:S(2)}, u32[]{:S(2)}) collective-permute-start(bf16[128,2688]{1,0:T(8,128)(2,1)} %add_convert_fusion.2), channel_id=1, source_target_pairs={{0,1},{1,0},{2,3},{3,2},{4,6},{5,7},{6,4},{7,5},{8,9},{9,8},{10,11... | collective-permute-start | bytes 2064392 | tf_op jit(solution)/shard_map/ppermute | solution.py:88
  325.8 18.3 %collective-permute-start.58 = (bf16[112,2560]{1,0:T(8,128)(2,1)S(1)}, bf16[112,2560]{1,0:T(8,128)(2,1)}, u32[]{:S(2)}, u32[]{:S(2)}) collective-permute-start(bf16[112,2560]{1,0:T(8,128)(2,1)S(1)} %add_convert_fusion.13), channel_id=1, source_target_pairs={{8,0},{9,1},{10,2},{11,3},{12,4},{13,5},{14,6},{15,7},{16,24},{17,... | collective-permute-start | bytes 1720328 | tf_op jit(solution)/shard_map/ppermute | solution.py:88
  346.4 21.5 %collective-permute-start.62 = (bf16[112,2560]{1,0:T(8,128)(2,1)}, bf16[112,2560]{1,0:T(8,128)(2,1)}, u32[]{:S(2)}, u32[]{:S(2)}) collective-permute-start(bf16[112,2560]{1,0:T(8,128)(2,1)} %broadcast_select_fusion.6.refs_2_), channel_id=1, source_target_pairs={{0,4},{1,5},{2,6},{3,7},{4,0},{5,1},{6,2},{7,3},{8,12},{9,13},{10,... | collective-permute-start | bytes 1720328 | tf_op jit(solution)/shard_map/ppermute | solution.py:88
  351.2 10.4 %collective-permute-start.59 = (bf16[32,2688]{1,0:T(8,128)(2,1)}, bf16[32,2688]{1,0:T(8,128)(2,1)S(1)}, u32[]{:S(2)}, u32[]{:S(2)}) collective-permute-start(bf16[32,2688]{1,0:T(8,128)(2,1)} %get-tuple-element.668), channel_id=1, source_target_pairs={{0,8},{1,9},{2,10},{3,11},{4,12},{5,13},{6,14},{7,15},{8,0},{9,1},... | collective-permute-start | bytes 516104 | tf_op jit(solution)/shard_map/ppermute | solution.py:88
  351.2 16.0 %collective-permute-start.60 = (bf16[32,2688]{1,0:T(8,128)(2,1)}, bf16[32,2688]{1,0:T(8,128)(2,1)S(1)}, u32[]{:S(2)}, u32[]{:S(2)}) collective-permute-start(bf16[32,2688]{1,0:T(8,128)(2,1)} %get-tuple-element.667), channel_id=1, source_target_pairs={{0,16},{1,17},{2,18},{3,19},{4,20},{5,21},{6,22},{7,23},{8,24},{9,... | collective-permute-start | bytes 516104 | tf_op jit(solution)/shard_map/ppermute | solution.py:88
  354.4 12.8 %collective-permute-start.61 = (bf16[32,2688]{1,0:T(8,128)(2,1)}, bf16[32,2688]{1,0:T(8,128)(2,1)}, u32[]{:S(2)}, u32[]{:S(2)}) collective-permute-start(bf16[32,2688]{1,0:T(8,128)(2,1)} %get-tuple-element.666), channel_id=1, source_target_pairs={{0,24},{1,25},{2,26},{3,27},{4,28},{5,29},{6,30},{7,31},{8,16},{9,... | collective-permute-start | bytes 516104 | tf_op jit(solution)/shard_map/ppermute | solution.py:88
  369.0 12.2 %collective-permute-start.63 = (bf16[32,2688]{1,0:T(8,128)(2,1)S(1)}, bf16[32,2688]{1,0:T(8,128)(2,1)}, u32[]{:S(2)}, u32[]{:S(2)}) collective-permute-start(bf16[32,2688]{1,0:T(8,128)(2,1)S(1)} %add_convert_fusion.17), channel_id=1, source_target_pairs={{0,8},{1,9},{2,10},{3,11},{4,12},{5,13},{6,14},{7,15},{8,0},{9,1},... | collective-permute-start | bytes 516104 | tf_op jit(solution)/shard_map/ppermute | solution.py:88
  372.4 15.7 %collective-permute-start.64 = (bf16[32,2688]{1,0:T(8,128)(2,1)S(1)}, bf16[32,2688]{1,0:T(8,128)(2,1)}, u32[]{:S(2)}, u32[]{:S(2)}) collective-permute-start(bf16[32,2688]{1,0:T(8,128)(2,1)S(1)} %add_convert_fusion.17), channel_id=1, source_target_pairs={{0,16},{1,17},{2,18},{3,19},{4,20},{5,21},{6,22},{7,23},{8,24},{9,... | collective-permute-start | bytes 516104 | tf_op jit(solution)/shard_map/ppermute | solution.py:88
  373.4 14.7 %collective-permute-start.65 = (bf16[32,2688]{1,0:T(8,128)(2,1)S(1)}, bf16[32,2688]{1,0:T(8,128)(2,1)}, u32[]{:S(2)}, u32[]{:S(2)}) collective-permute-start(bf16[32,2688]{1,0:T(8,128)(2,1)S(1)} %add_convert_fusion.17), channel_id=1, source_target_pairs={{0,24},{1,25},{2,26},{3,27},{4,28},{5,29},{6,30},{7,31},{8,16},{9,... | collective-permute-start | bytes 516104 | tf_op jit(solution)/shard_map/ppermute | solution.py:88
  (73 other events, 868.4 us)

commit v9 on v8

--- a/solution.py
+++ b/solution.py
@@ -235,22 +235,59 @@
 
 
 def load(pieces, starts_ref, whole, sems):
+    copies = copies_of(pieces, starts_ref, whole, sems, 0)
+    for _, copy in copies:
+        copy.start()
+    return lambda: [copy.wait() for _, copy in copies]
+
+
+def copies_of(pieces, starts_ref, whole, sems, row):
     copies = []
     for i, piece in enumerate(pieces):
-        rows = pl.ds(pl.multiple_of(starts_ref[2 * i], 16), piece.shape[0])
+        rows = pl.ds(pl.multiple_of(starts_ref[2 * i] - row, 16), piece.shape[0])
         if piece.shape[1] == whole.shape[1]:
             place = whole.at[rows, :]
         else:
             columns = pl.ds(pl.multiple_of(starts_ref[2 * i + 1], 128), piece.shape[1])
             place = whole.at[rows, columns]
-        copies.append(pltpu.make_async_copy(piece, place, sems.at[i]))
-        copies[-1].start()
+        copies.append((i, pltpu.make_async_copy(piece, place, sems.at[i])))
     return copies
 
 
-def wait(copies):
-    for copy in copies:
-        copy.wait()
+def load_lower(pieces, starts_ref, whole, sems, row):
+    if pieces[0].shape[0] > row:
+        copy = pltpu.make_async_copy(pieces[0].at[row:, :], whole, sems.at[0])
+        copy.start()
+        return copy.wait
+    copies = copies_of(pieces, starts_ref, whole, sems, row)
+
+    def each(act):
+        for i, copy in copies:
+            pl.when(starts_ref[2 * i] >= row)(functools.partial(act, copy))
+
+    each(lambda copy: copy.start())
+    return lambda: each(lambda copy: copy.wait())
+
+
+def load_halves(pieces, starts_ref, whole, sems):
+    half = whole.shape[1] // 2
+    copies = []
+    for i, piece in enumerate(pieces):
+        rows = pl.ds(pl.multiple_of(starts_ref[2 * i], 16), piece.shape[0])
+        for h in range(2):
+            columns = slice(h * half, (h + 1) * half)
+            source = piece.at[:, columns] if piece.shape[1] > half else piece
+            copy = pltpu.make_async_copy(source, whole.at[rows, columns], sems.at[i, h])
+            copies.append((h, None if piece.shape[1] > half else starts_ref[2 * i + 1] == h * half, copy))
+
+    def each(h, act):
+        for at, there, copy in copies:
+            if at == h and there is None:
+                act(copy)
+            elif at == h:
+                pl.when(there)(functools.partial(act, copy))
+
+    return lambda h: each(h, lambda copy: copy.start()), lambda h: each(h, lambda copy: copy.wait())
 
 
 IN_VMEM = pl.BlockSpec(memory_space=pltpu.VMEM)
@@ -275,11 +312,11 @@
 def project_kernel(count, starts_ref, x_ref, gains_ref, cos_ref, sin_ref, *refs):
     pieces = refs[:count]
     q_ref, kv_ref, whole, sems = refs[count:]
-    copies = load(pieces, starts_ref, whole, sems)
+    wait = load(pieces, starts_ref, whole, sems)
     x = upright(x_ref).astype(F32)
     width = x.shape[1]
     act = (x * rms_inverse(x) * gains_ref[0:1, :]).astype(BF)
-    wait(copies)
+    wait()
     cosine, sine = cos_ref[...], sin_ref[...]
     for first in range(0, width + KV_WIDTH, 256):
         linear = nn(act, whole[:width, first : first + 256])
@@ -334,26 +371,30 @@
     down_pieces = refs[counts[0] + counts[1] : total_count]
     out_ref, inner_ref, kept_ref, given_ref, act_t_ref, attn_t_ref, resid_ref = refs[total_count : total_count + 7]
     w_attn, w_pair, w_down, sum_ref, sems0, sems1, sems2 = refs[total_count + 7 :]
-    attention_copies = load(attention_pieces, s0_ref, w_attn, sems0)
-    pair_copies = load(pair_pieces, s1_ref, w_pair, sems1)
-    down_copies = load(down_pieces, s2_ref, w_down, sems2)
     width = x_ref.shape[1]
     hidden = w_pair.shape[1]
-    tile = hidden // 5
+    tile = hidden // 4
+    wait_attention = load_lower(attention_pieces, s0_ref, w_attn, sems0, width)
+    start_pair, wait_pair = load_halves(pair_pieces, s1_ref, w_pair, sems1)
+    start_pair(0)
+    wait_down = load(down_pieces, s2_ref, w_down, sems2)
+    start_pair(1)
     even = core_ref[0] == 0
     x = upright(x_ref).astype(F32)
     dy = upright(cot_ref)
     attn_t_ref[...] = jnp.transpose(attn_ref[...])
-    wait(attention_copies)
-    resid = x + nn(attn_ref[...], w_attn[width:, : rounded_up(width)])[:, :width]
+    wait_attention()
+    resid = x + nn(attn_ref[...], w_attn[:, : rounded_up(width)])[:, :width]
     resid_t = jnp.transpose(resid)
     resid_ref[...] = resid_t
     sum_ref[...] = resid_t
     act = (resid * rms_inverse(resid) * gains_ref[1:2, :]).astype(BF)
     act_t_ref[...] = jnp.transpose(act)
-    wait(pair_copies)
-    wait(down_copies)
+    wait_pair(0)
+    wait_down()
     for first in range(0, hidden, tile):
+        if first == hidden // 2:
+            wait_pair(1)
         here = slice(first, first + tile)
         gate = nn(act, w_pair[:width, here])
         upper = nn(act, w_pair[width:, here])
@@ -388,9 +429,10 @@
         in_specs=[IN_SMEM] * 4 + [IN_VMEM] * 4 + [ANYWHERE] * len(every),
         out_specs=(IN_VMEM,) * 7,
         out_shape=outs,
-        scratch_shapes=[pltpu.VMEM(shape, BF) for shape in shapes]
+        scratch_shapes=[pltpu.VMEM((width, shapes[0][1]), BF)]
+        + [pltpu.VMEM(shape, BF) for shape in shapes[1:]]
         + [pltpu.VMEM((width, tokens), F32)]
-        + [pltpu.SemaphoreType.DMA((count,)) for count in counts],
+        + [pltpu.SemaphoreType.DMA(size) for size in ((counts[0],), (counts[1], 2), (counts[2],))],
         cost_estimate=cost(
             2 * tokens * width * (4 * hidden + width), tokens * hidden, x, x, x, *outs, *every
         ),
@@ -401,15 +443,21 @@
 def feed_back_kernel(counts, core_ref, s0_ref, s1_ref, resid_ref, cot_ref, kept_ref, given_ref, gain_ref, *refs):
     total_count = sum(counts)
     dres_ref, low_ref, dattn_ref, w_attn, w_pair, sems0, sems1 = refs[total_count:]
-    pair_copies = load(refs[counts[0] : total_count], s1_ref, w_pair, sems1)
-    attention_copies = load(refs[: counts[0]], s0_ref, w_attn, sems0)
     width = resid_ref.shape[0]
+    start_pair, wait_pair = load_halves(refs[counts[0] : total_count], s1_ref, w_pair, sems1)
+    start_pair(0)
+    start_pair(1)
+    wait_attention = load_lower(refs[: counts[0]], s0_ref, w_attn, sems0, width)
     resid = resid_ref[...]
     root = lax.rsqrt(jnp.mean(resid * resid, axis=0, keepdims=True) + EPS)
     normed = resid * root
-    wait(pair_copies)
-    weight = lambda i: w_pair[pl.ds(pl.multiple_of(i * width, 16), width), :]
-    d_act = nt(weight(core_ref[0]), kept_ref[...]) + nt(weight(1 - core_ref[0]), given_ref[...])
+    half = w_pair.shape[1] // 2
+    for h in range(2):
+        columns = slice(h * half, (h + 1) * half)
+        weight = lambda i: w_pair[pl.ds(pl.multiple_of(i * width, 16), width), columns]
+        wait_pair(h)
+        part = nt(weight(core_ref[0]), kept_ref[:, columns]) + nt(weight(1 - core_ref[0]), given_ref[:, columns])
+        d_act = part if h == 0 else d_act + part
     d_normed = d_act * gain_ref[...]
     d_resid = across(cot_ref).astype(F32) + root * (
         d_normed - normed * jnp.mean(d_normed * normed, axis=0, keepdims=True)
@@ -419,8 +467,8 @@
     low_ref[:, :width] = jnp.transpose(low)
     if low_ref.shape[1] > width:
         low_ref[:, width:] = jnp.zeros((low_ref.shape[0], low_ref.shape[1] - width), BF)
-    wait(attention_copies)
-    dattn_ref[...] = jnp.transpose(nn(w_attn[width:, :width], low).astype(BF))
+    wait_attention()
+    dattn_ref[...] = jnp.transpose(nn(w_attn[:, :width], low).astype(BF))
 
 
 def feed_back(core, resid, dy, kept, given, gain, attention_got, pair_got):
@@ -440,8 +488,8 @@
         in_specs=[IN_SMEM] * 3 + [IN_VMEM] * 5 + [ANYWHERE] * len(every),
         out_specs=(IN_VMEM,) * 3,
         out_shape=outs,
-        scratch_shapes=[pltpu.VMEM(shape, BF) for shape in shapes]
-        + [pltpu.SemaphoreType.DMA((count,)) for count in counts],
+        scratch_shapes=[pltpu.VMEM((width, shapes[0][1]), BF), pltpu.VMEM(shapes[1], BF)]
+        + [pltpu.SemaphoreType.DMA(size) for size in ((counts[0],), (counts[1], 2))],
         cost_estimate=cost(
             2 * tokens * width * (2 * shapes[1][1] + width), 0, resid, dy, kept, given, *outs, *every
         ),
@@ -661,13 +709,13 @@
 def finish_kernel(count, starts_ref, x_ref, low_ref, kv_ref, dres_ref, gain_ref, cos_ref, sin_ref, *refs):
     pieces = refs[:count]
     dx_ref, whole, kv_turned, sems = refs[count:]
-    copies = load(pieces, starts_ref, whole, sems)
+    wait = load(pieces, starts_ref, whole, sems)
     turn_keys(kv_ref, kv_turned, 0, cos_ref[...], sin_ref[...])
     x = across(x_ref).astype(F32)
     width = x.shape[0]
     root = lax.rsqrt(jnp.mean(x * x, axis=0, keepdims=True) + EPS)
     normed = x * root
-    wait(copies)
+    wait()
     d_act = nt(whole[:width, :width], low_ref[:, :width])
     d_act += nt(whole[:width, width:], kv_turned[:, :KV_WIDTH])
     d_act += nt(whole[width:, width:], kv_turned[:, KV_WIDTH:])
@@ -1097,11 +1145,13 @@
                 (value_weight, done["value"]),
             )
 
-    order = []
+    order, rounds = [], 0
     while plan.tasks:
         plan.advance(*(order.pop(0) if order else tuple(plan.tasks)))
+        plan.advance(*{0: ('some',), 1: ('some',)}.get(rounds, ()))
         settle()
-        if plan.tasks:
+        rounds += 1
+        if rounds <= 2 and plan.tasks:
             plan.close()
 
     done = plan.have["done"]

time: 406 us -> 390 us (0.961)
  waiting for transfers between devices: 107 us -> 96 us
    ppermute x67, waiting for transfers between devices: 107 us -> 96 us  [move(): return lax.ppermute(value, AXES, pairs)]
    unnamed x145 -> x133, local copies, waits for them, and re-layouts: 16.3 us -> 15 us
  transfers between devices with their start and end apart: 67 -> 67, of which waited for: 19 -> 19; matrix products, arithmetic and copies ran while one was open for 11% -> 14% of each run, Pallas kernels for 35% -> 34%
where the time goes in v9:
time: 390 us; the launch traced here: 382 us
  Pallas kernels  141 us (36%)
  waiting for transfers between devices  96 us (25%)
  starting transfers between devices  72.6 us (19%)
  other arithmetic  41.1 us (11%)
  local copies, waits for them, and re-layouts  29.7 us (8%)
    ppermute x67, waiting for transfers between devices, move(): return lax.ppermute(value, AXES, pairs)  96 us
    ppermute x67, starting transfers between devices, move(): return lax.ppermute(value, AXES, pairs)  72.6 us
    pallas_call x2, Pallas kernels, attend_back(): pl.pallas_call(functools.partial(attend_back_kernel, shards, seg_rows), g...  34.4 us
    pallas_call x1, Pallas kernels, feed(): pl.pallas_call(functools.partial(feed_kernel, counts), name='feed', in_sp...  27.6 us
    convert_element_type x17, other arithmetic, total(): return sum((part.astype(F32) for part in parts)).astype(parts[0].dtype)  19.2 us
    pallas_call x1, Pallas kernels, attend(): pl.pallas_call(functools.partial(attend_kernel, shards, seg_rows), grid=(...  16.7 us
    pallas_call x1, Pallas kernels, feed_back(): pl.pallas_call(functools.partial(feed_back_kernel, counts), name='feed_ba...  15 us
    unnamed x133, local copies, waits for them, and re-layouts  15 us
  transfers between devices with their start and end apart: 67, of which 19 were waited for; matrix products, arithmetic and copies ran while one was open for 14% of the time, Pallas kernels for 34%

profile of v9, /device:TPU:0, one launch (start us, length us, event | category | flops | bytes accessed | tf_op | source)
XLA Modules:
  0.0 382.3 jit_solution(15525946306342402589)
XLA Ops:
  3.6 2.4 broadcast_select_fusion.5
  6.0 2.9 collective-permute-start
  8.9 1.5 collective-permute-start.1
  11.1 2.9 collective-permute-start.4
  14.6 1.7 fusion.1
  17.2 2.0 dynamic-slice_select_fusion
  19.3 1.7 multiply_sine_fusion
  21.1 2.0 dynamic-slice_bitcast_fusion
  25.9 2.0 collective-permute-start.8
  28.1 11.6 %collective-permute-done.5.refs_6_ = bf16[240,1280]{1,0:T(8,128)(2,1)S(1)} collective-permute-done((bf16[240,1280]{1,0:T(8,128)(2,1)S(1)}, bf16[240,1280]{1,0:T(8,128)(2,1)S(1)}, u32[]{:S(2)}, u32[]{:S(2)}) %collective-permute-start.5) | collective-permute-done | bytes 614432 | tf_op jit(solution)/shard_map/ppermute | solution.py:88
  40.7 2.1 tile.20
  44.9 2.4 collective-permute-start.11
  47.3 1.9 collective-permute-start.12
  49.2 2.5 copy.72.cos_ref
  51.8 2.5 copy.73.sin_ref
  55.4 6.6 %project.1 = (bf16[512,960]{1,0:T(8,128)(2,1)}, bf16[512,640]{1,0:T(8,128)(2,1)S(1)}) custom-call(s32[16]{0:T(128)S(1)} %stack.194.starts_ref.s0_ref, bf16[2,960,256]{2,1,0:T(8,128)(2,1)} %bitcast.17.x_ref.refs_0_, f32[2,960]{1,0:T(2,128)S(1)} %maximum_convert_fusion.4.gains_ref, f32[2048,128]{1,0:T(8,128)} %copy.72.cos_ref, f32[2048,128]{1,0:T(8,128)} %copy.73.sin_ref, ...), custom_call_target="tpu_custom_call" | custom-call | flops 1572864000 | bytes 7536640 | tf_op jit(solution)/shard_map/project/pallas_call | solution.py:344
  64.1 1.8 collective-permute-start.15
  66.0 13.9 %collective-permute-done.15.refs_15_ = bf16[240,1280]{1,0:T(8,128)(2,1)S(1)} collective-permute-done((bf16[240,1280]{1,0:T(8,128)(2,1)}, bf16[240,1280]{1,0:T(8,128)(2,1)S(1)}, u32[]{:S(2)}, u32[]{:S(2)}) %collective-permute-start.15) | collective-permute-done | bytes 614432 | tf_op jit(solution)/shard_map/ppermute | solution.py:88
  82.5 7.8 %collective-permute-done.17.refs_18_ = bf16[240,1280]{1,0:T(8,128)(2,1)S(1)} collective-permute-done((bf16[240,1280]{1,0:T(8,128)(2,1)}, bf16[240,1280]{1,0:T(8,128)(2,1)S(1)}, u32[]{:S(2)}, u32[]{:S(2)}) %collective-permute-start.17) | collective-permute-done | bytes 614432 | tf_op jit(solution)/shard_map/ppermute | solution.py:88
  90.3 2.0 collective-permute-done.21.refs_17_
  92.3 5.0 %collective-permute-done.16.refs_3_ = bf16[512,640]{1,0:T(8,128)(2,1)S(1)} collective-permute-done((bf16[512,640]{1,0:T(8,128)(2,1)S(1)}, bf16[512,640]{1,0:T(8,128)(2,1)S(1)}, u32[]{:S(2)}, u32[]{:S(2)}) %collective-permute-start.16) | collective-permute-done | bytes 655392 | tf_op jit(solution)/shard_map/ppermute | solution.py:88
  99.0 1.6 collective-permute-start.23
  101.9 16.7 %attend.1 = (bf16[512,960]{1,0:T(8,128)(2,1)S(1)}, f32[512,128]{1,0:T(8,128)S(1)}) custom-call(bf16[512,960]{1,0:T(8,128)(2,1)S(1)} %copy-done.24, bf16[512,640]{1,0:T(8,128)(2,1)S(1)} %get-tuple-element.476.refs_0_, bf16[512,640]{1,0:T(8,128)(2,1)S(1)} %collective-permute-done.13.refs_1_, bf16[512,640]{1,0:T(8,128)(2,1)S(1)} %collective-permute-done.14.refs_2_, ...), custom_call_target="tpu_custom_call" | custom-call | flops 8053063680 | bytes 983040 | tf_op jit(solution)/shard_map/attend/pallas_call | solution.py:859
  126.2 27.6 %feed.1 = (bf16[2,960,256]{2,1,0:T(8,128)(2,1)}, bf16[512,2560]{1,0:T(8,128)(2,1)}, bf16[512,2560]{1,0:T(8,128)(2,1)}, bf16[512,2560]{1,0:T(8,128)(2,1)}, bf16[9...) custom-call(s32[1]{0:T(128)} %bitcast.core_ref, s32[16]{0:T(128)} %copy-done.22, ...), custom_call_target="tpu_custom_call" | custom-call | flops 11010048000 | bytes 35389440 | tf_op jit(solution)/shard_map/feed/pallas_call | solution.py:426
  154.5 1.5 collective-permute-start.36
  157.0 15.0 %feed_back.1 = (f32[960,512]{1,0:T(8,128)}, bf16[512,1024]{1,0:T(8,128)(2,1)}, bf16[512,960]{1,0:T(8,128)(2,1)}) custom-call(s32[1]{0:T(128)} %bitcast.core_ref, s32[16]{0:T(128)} %copy-done.22, s32[28]{0:T(128)} %stack.197.s1_ref, f32[960,512]{1,0:T(8,128)} %get-tuple-element.378.resid_ref, bf16[2,960,256]{2,1,0:T(8,128)(2,1)} %bitcast.73, ...), custom_call_target="tpu_custom_call" | custom-call | flops 5976883200 | bytes 26935296 | tf_op jit(solution)/shard_map/feed_back/pallas_call | solution.py:485
  172.1 5.9 %down_grad.1 = (bf16[960,640]{1,0:T(8,128)(2,1)S(1)}, bf16[960,640]{1,0:T(8,128)(2,1)S(1)}) custom-call(s32[5]{0:T(128)S(1)} %stack.214.info_ref, bf16[2,960,256]{2,1,0:T(8,128)(2,1)S(1)} %bitcast.75, bf16[2,960,256]{2,1,0:T(8,128)(2,1)S(1)} %collective-permute-done.30.far_cot_ref, bf16[512,2560]{1,0:T(8,128)(2,1)} %get-tuple-element.402.inner_ref, ...), custom_call_target="tpu_custom_call" | custom-call | flops 2516582400 | bytes 9666560 | tf_op jit(solution)/shard_map/down_grad/pallas_call | solution.py:530
  178.7 9.4 %wide_grad.1 = (bf16[256,2560]{1,0:T(8,128)(2,1)S(1)}, bf16[256,2560]{1,0:T(8,128)(2,1)}, bf16[224,2560]{1,0:T(8,128)(2,1)S(1)}, bf16[224,2560]{1,0:T(8,128)(2,1)S(1)}) custom-call(s32[4]{0:T(128)S(1)} %pad_add_fusion.1.starts_ref, bf16[960,512]{1,0:T(8,128)(2,1)S(1)} %copy-done.26, bf16[960,512]{1,0:T(8,128)(2,1)S(1)} %collective-permute-done.33.far_left_ref, ...), custom_call_target="tpu_custom_call" | custom-call | flops 5033164800 | bytes 12124160 | tf_op jit(solution)/shard_map/wide_grad/pallas_call | solution.py:579
  188.2 6.6 %collective-permute-done.37 = bf16[960,640]{1,0:T(8,128)(2,1)S(1)} collective-permute-done((bf16[960,640]{1,0:T(8,128)(2,1)S(1)}, bf16[960,640]{1,0:T(8,128)(2,1)S(1)}, u32[]{:S(2)}, u32[]{:S(2)}) %collective-permute-start.37) | collective-permute-done | bytes 1228832 | tf_op jit(solution)/shard_map/ppermute | solution.py:88
  198.9 17.2 %attend_back.2 = (bf16[512,1024]{1,0:T(8,128)(2,1)S(1)}, bf16[2,512,640]{2,1,0:T(8,128)(2,1)}, bf16[2,512,640]{2,1,0:T(8,128)(2,1)}) custom-call(bf16[512,960]{1,0:T(8,128)(2,1)S(1)} %copy-done.25, bf16[512,640]{1,0:T(8,128)(2,1)S(1)} %copy-done.28, bf16[512,640]{1,0:T(8,128)(2,1)S(1)} %copy-done.30, bf16[512,640]{1,0:T(8,128)(2,1)S(1)} %copy-done.32, ...), custom_call_target="tpu_custom_call" | custom-call | flops 10066329600 | bytes 983040 | tf_op jit(solution)/shard_map/attend_back/pallas_call | solution.py:881
  216.1 3.9 %collective-permute-done.39 = bf16[256,2560]{1,0:T(8,128)(2,1)S(1)} collective-permute-done((bf16[256,2560]{1,0:T(8,128)(2,1)}, bf16[256,2560]{1,0:T(8,128)(2,1)S(1)}, u32[]{:S(2)}, u32[]{:S(2)}) %collective-permute-start.39) | collective-permute-done | bytes 1310752 | tf_op jit(solution)/shard_map/ppermute | solution.py:88
  223.4 2.6 collective-permute-start.40
  226.0 17.2 %attend_back.3 = (bf16[512,1024]{1,0:T(8,128)(2,1)S(1)}, bf16[2,512,640]{2,1,0:T(8,128)(2,1)}, bf16[2,512,640]{2,1,0:T(8,128)(2,1)}) custom-call(bf16[512,960]{1,0:T(8,128)(2,1)S(1)} %copy-done.25, bf16[512,640]{1,0:T(8,128)(2,1)S(1)} %copy-done.28, bf16[512,640]{1,0:T(8,128)(2,1)S(1)} %copy-done.30, ...), custom_call_target="tpu_custom_call", output_to_operand_aliasing={{0}: (11, {}), {1}: (12, {}), {2}: (13, {})} | custom-call | flops 10066329600 | bytes 983040 | tf_op jit(solution)/shard_map/attend_back/pallas_call | solution.py:881
  244.2 2.1 collective-permute-start.45
  248.4 2.0 add_convert_fusion.16
  253.0 13.2 %attention_grad.1 = (bf16[512,2688]{1,0:T(8,128)(2,1)}, bf16[512,2688]{1,0:T(8,128)(2,1)}) custom-call(s32[8]{0:T(128)} %stack.227.starts_ref, f32[960,1]{1,0:T(8,128)} %copy.75.gain_ref, f32[2048,128]{1,0:T(8,128)} %copy.72.cos_ref, f32[2048,128]{1,0:T(8,128)} %copy.73.sin_ref, bf16[512,1024]{1,0:T(8,128)(2,1)} %copy-done.17, ...), custom_call_target="tpu_custom_call" | custom-call | flops 4697620480 | bytes 12058624 | tf_op jit(solution)/shard_map/attention_grad/pallas_call | solution.py:685
  266.7 3.8 collective-permute-done.43
  271.9 1.5 collective-permute-start.51
  273.4 2.0 add_convert_fusion.9
  275.4 1.4 collective-permute-start.48
  276.9 1.7 add_convert_fusion
  280.1 2.1 add_convert_fusion.6
  283.1 1.4 add_convert_fusion.15
  284.5 5.4 %collective-permute-start.52 = (bf16[112,2560]{1,0:T(8,128)(2,1)S(1)}, bf16[112,2560]{1,0:T(8,128)(2,1)S(1)}, u32[]{:S(2)}, u32[]{:S(2)}) collective-permute-start(bf16[112,2560]{1,0:T(8,128)(2,1)S(1)} %add_convert_fusion.15), channel_id=1, source_target_pairs={{0,8},{1,9},{2,10},{3,11},{4,12},{5,13},{6,14},{7,15},{24,16},{25,... | collective-permute-start | bytes 1720328 | tf_op jit(solution)/shard_map/ppermute | solution.py:88
  290.2 11.8 %collective-permute-done.52 = bf16[112,2560]{1,0:T(8,128)(2,1)S(1)} collective-permute-done((bf16[112,2560]{1,0:T(8,128)(2,1)S(1)}, bf16[112,2560]{1,0:T(8,128)(2,1)S(1)}, u32[]{:S(2)}, u32[]{:S(2)}) %collective-permute-start.52) | collective-permute-done | bytes 573472 | tf_op jit(solution)/shard_map/ppermute | solution.py:88
  302.0 2.6 collective-permute-done.50
  305.4 1.8 add_convert_fusion.2
  309.7 1.5 collective-permute-start.58
  312.5 5.7 %collective-permute-done.54 = bf16[128,2688]{1,0:T(8,128)(2,1)S(1)} collective-permute-done((bf16[128,2688]{1,0:T(8,128)(2,1)S(1)}, bf16[128,2688]{1,0:T(8,128)(2,1)S(1)}, u32[]{:S(2)}, u32[]{:S(2)}) %collective-permute-start.54) | collective-permute-done | bytes 688160 | tf_op jit(solution)/shard_map/ppermute | solution.py:88
  318.2 2.0 add_convert_fusion.1
  320.3 7.3 %collective-permute-start.55 = (bf16[32,2688]{1,0:T(8,128)(2,1)S(1)}, bf16[32,2688]{1,0:T(8,128)(2,1)S(1)}, u32[]{:S(2)}, u32[]{:S(2)}) collective-permute-start(bf16[32,2688]{1,0:T(8,128)(2,1)S(1)} %get-tuple-element.608), channel_id=1, source_target_pairs={{0,8},{1,9},{2,10},{3,11},{4,12},{5,13},{6,14},{7,15},{8,0},{9,1},... | collective-permute-start | bytes 516104 | tf_op jit(solution)/shard_map/ppermute | solution.py:88
  327.6 2.5 collective-permute-start.57
  330.1 1.5 fusion.kv_ref
  331.7 8.6 %finish.1 = bf16[2,960,256]{2,1,0:T(8,128)(2,1)} custom-call(s32[16]{0:T(128)S(1)} %copy-done.23, bf16[2,960,256]{2,1,0:T(8,128)(2,1)} %bitcast.17.x_ref.refs_0_, bf16[512,1024]{1,0:T(8,128)(2,1)} %copy-done.17, bf16[512,640]{1,0:T(8,128)(2,1)S(1)} %fusion.kv_ref, f32[960,512]{1,0:T(8,128)} %get-tuple-element.529.dres_ref, f32[960,1]{1,0:T(8,128)S(1)} %copy-done.16, ...), custom_call_target="tpu_custom_call" | custom-call | flops 1572864000 | bytes 8912896 | tf_op jit(solution)/shard_map/finish/pallas_call | solution.py:731
  340.4 2.6 collective-permute-done.55
  343.1 1.6 collective-permute-start.60
  344.9 2.6 collective-permute-start.62
  349.3 1.6 convert_bitcast_fusion
  352.1 6.3 %collective-permute-done.61 = bf16[32,2688]{1,0:T(8,128)(2,1)S(1)} collective-permute-done((bf16[32,2688]{1,0:T(8,128)(2,1)S(1)}, bf16[32,2688]{1,0:T(8,128)(2,1)S(1)}, u32[]{:S(2)}, u32[]{:S(2)}) %collective-permute-start.61) | collective-permute-done | bytes 172064 | tf_op jit(solution)/shard_map/ppermute | solution.py:88
  358.8 9.3 %collective-permute-done.65 = bf16[112,2560]{1,0:T(8,128)(2,1)S(1)} collective-permute-done((bf16[112,2560]{1,0:T(8,128)(2,1)S(1)}, bf16[112,2560]{1,0:T(8,128)(2,1)S(1)}, u32[]{:S(2)}, u32[]{:S(2)}) %collective-permute-start.65) | collective-permute-done | bytes 573472 | tf_op jit(solution)/shard_map/ppermute | solution.py:88
  368.6 1.6 maximum_convert_fusion
  372.2 1.9 copy.84
  374.9 2.4 multiply_reduce_fusion
  378.0 3.3 settle.1
  (297 shorter events, 60.2 us)
Async XLA Ops:
  6.0 18.3 %collective-permute-start = (bf16[240,1280]{1,0:T(8,128)(2,1)}, bf16[240,1280]{1,0:T(8,128)(2,1)S(1)}, u32[]{:S(2)}, u32[]{:S(2)}) collective-permute-start(bf16[240,1280]{1,0:T(8,128)(2,1)} %get-tuple-element.599), channel_id=1, source_target_pairs={{0,1},{1,0},{2,3},{3,2},{4,6},{5,7},{6,4},{7,5},{8,9},{9,8},{10,11... | collective-permute-start | bytes 1843208 | tf_op jit(solution)/shard_map/ppermute | solution.py:88
  8.9 15.4 %collective-permute-start.1 = (bf16[240,1280]{1,0:T(8,128)(2,1)}, bf16[240,1280]{1,0:T(8,128)(2,1)}, u32[]{:S(2)}, u32[]{:S(2)}) collective-permute-start(bf16[240,1280]{1,0:T(8,128)(2,1)} %get-tuple-element.599), channel_id=1, source_target_pairs={{0,2},{1,3},{2,0},{3,1},{4,5},{5,4},{6,7},{7,6},{8,10},{9,11},{10,... | collective-permute-start | bytes 1843208 | tf_op jit(solution)/shard_map/ppermute | solution.py:88
  10.5 12.9 %collective-permute-start.2 = (bf16[2,240]{1,0:T(2,128)(2,1)S(1)}, bf16[2,240]{1,0:T(2,128)(2,1)S(1)}, u32[]{:S(2)}, u32[]{:S(2)}) collective-permute-start(bf16[2,240]{1,0:T(2,128)(2,1)S(1)} %pad_maximum_fusion.5), channel_id=1, source_target_pairs={{0,1},{1,0},{2,3},{3,2},{4,5},{5,4},{6,7},{7,6},{8,9},{9,8},{10,11... | collective-permute-start | bytes 2888 | tf_op jit(solution)/shard_map/ppermute | solution.py:88
  11.1 12.3 %collective-permute-start.3 = (bf16[2,240]{1,0:T(2,128)(2,1)S(1)}, bf16[2,240]{1,0:T(2,128)(2,1)S(1)}, u32[]{:S(2)}, u32[]{:S(2)}) collective-permute-start(bf16[2,240]{1,0:T(2,128)(2,1)S(1)} %pad_maximum_fusion.5), channel_id=1, source_target_pairs={{0,2},{1,3},{2,0},{3,1},{4,6},{5,7},{6,4},{7,5},{8,10},{9,11},{10,... | collective-permute-start | bytes 2888 | tf_op jit(solution)/shard_map/ppermute | solution.py:88
  11.1 13.2 %collective-permute-start.4 = (bf16[2,240]{1,0:T(2,128)(2,1)S(1)}, bf16[2,240]{1,0:T(2,128)(2,1)S(1)}, u32[]{:S(2)}, u32[]{:S(2)}) collective-permute-start(bf16[2,240]{1,0:T(2,128)(2,1)S(1)} %pad_maximum_fusion.5), channel_id=1, source_target_pairs={{0,3},{1,2},{2,1},{3,0},{4,7},{5,6},{6,5},{7,4},{8,11},{9,10},{10,... | collective-permute-start | bytes 2888 | tf_op jit(solution)/shard_map/ppermute | solution.py:88
  24.3 15.5 %collective-permute-start.5 = (bf16[240,1280]{1,0:T(8,128)(2,1)S(1)}, bf16[240,1280]{1,0:T(8,128)(2,1)S(1)}, u32[]{:S(2)}, u32[]{:S(2)}) collective-permute-start(bf16[240,1280]{1,0:T(8,128)(2,1)S(1)} %collective-permute-done.refs_2_), channel_id=1, source_target_pairs={{0,2},{1,3},{2,0},{3,1},{4,5},{5,4},{6,7},{7,6},{8,10},{9,11},{10,... | collective-permute-start | bytes 1843208 | tf_op jit(solution)/shard_map/ppermute | solution.py:88
  25.0 14.8 %collective-permute-start.6 = (bf16[240,1280]{1,0:T(8,128)(2,1)S(1)}, bf16[240,1280]{1,0:T(8,128)(2,1)S(1)}, u32[]{:S(2)}, u32[]{:S(2)}) collective-permute-start(bf16[240,1280]{1,0:T(8,128)(2,1)S(1)} %collective-permute-done.refs_2_), channel_id=1, source_target_pairs={{0,4},{1,5},{2,6},{3,7},{4,0},{5,1},{6,2},{7,3},{8,12},{9,13},{10,... | collective-permute-start | bytes 1843208 | tf_op jit(solution)/shard_map/ppermute | solution.py:88
  25.8 13.9 %collective-permute-start.7 = (bf16[240,1280]{1,0:T(8,128)(2,1)}, bf16[240,1280]{1,0:T(8,128)(2,1)S(1)}, u32[]{:S(2)}, u32[]{:S(2)}) collective-permute-start(bf16[240,1280]{1,0:T(8,128)(2,1)} %collective-permute-done.1.refs_4_), channel_id=1, source_target_pairs={{0,4},{1,5},{2,6},{3,7},{4,0},{5,1},{6,2},{7,3},{8,12},{9,13},{10,... | collective-permute-start | bytes 1843208 | tf_op jit(solution)/shard_map/ppermute | solution.py:88
  25.9 14.8 %collective-permute-start.8 = (bf16[240,1280]{1,0:T(8,128)(2,1)}, bf16[240,1280]{1,0:T(8,128)(2,1)}, u32[]{:S(2)}, u32[]{:S(2)}) collective-permute-start(bf16[240,1280]{1,0:T(8,128)(2,1)} %dynamic-slice_select_fusion), channel_id=1, source_target_pairs={{0,1},{1,0},{2,3},{3,2},{4,6},{5,7},{6,4},{7,5},{8,9},{9,8},{10,11... | collective-permute-start | bytes 1843208 | tf_op jit(solution)/shard_map/ppermute | solution.py:88
  43.9 10.5 %collective-permute-start.9 = (bf16[240,1280]{1,0:T(8,128)(2,1)S(1)}, bf16[240,1280]{1,0:T(8,128)(2,1)}, u32[]{:S(2)}, u32[]{:S(2)}) collective-permute-start(bf16[240,1280]{1,0:T(8,128)(2,1)S(1)} %collective-permute-done.5.refs_6_), channel_id=1, source_target_pairs={{0,4},{1,5},{2,6},{3,7},{4,0},{5,1},{6,2},{7,3},{8,12},{9,13},{10,... | collective-permute-start | bytes 1843208 | tf_op jit(solution)/shard_map/ppermute | solution.py:88
  44.2 18.4 %collective-permute-start.10 = (bf16[240,1280]{1,0:T(8,128)(2,1)}, bf16[240,1280]{1,0:T(8,128)(2,1)}, u32[]{:S(2)}, u32[]{:S(2)}) collective-permute-start(bf16[240,1280]{1,0:T(8,128)(2,1)} %dynamic-slice_select_fusion), channel_id=1, source_target_pairs={{0,2},{1,3},{2,0},{3,1},{4,5},{5,4},{6,7},{7,6},{8,10},{9,11},{10,... | collective-permute-start | bytes 1843208 | tf_op jit(solution)/shard_map/ppermute | solution.py:88
  44.9 17.8 %collective-permute-start.11 = (bf16[240,1280]{1,0:T(8,128)(2,1)}, bf16[240,1280]{1,0:T(8,128)(2,1)}, u32[]{:S(2)}, u32[]{:S(2)}) collective-permute-start(bf16[240,1280]{1,0:T(8,128)(2,1)} %collective-permute-done.8.refs_10_), channel_id=1, source_target_pairs={{0,8},{1,9},{2,10},{3,11},{4,12},{5,13},{6,14},{7,15},{8,0},{9,1},... | collective-permute-start | bytes 1843208 | tf_op jit(solution)/shard_map/ppermute | solution.py:88
  47.3 15.4 %collective-permute-start.12 = (bf16[480,640]{1,0:T(8,128)(2,1)}, bf16[480,640]{1,0:T(8,128)(2,1)}, u32[]{:S(2)}, u32[]{:S(2)}) collective-permute-start(bf16[480,640]{1,0:T(8,128)(2,1)} %dynamic-slice_bitcast_fusion), channel_id=1, source_target_pairs={{0,1},{1,0},{2,3},{3,2},{4,6},{5,7},{6,4},{7,5},{8,9},{9,8},{10,11... | collective-permute-start | bytes 1843208 | tf_op jit(solution)/shard_map/ppermute | solution.py:88
  62.7 17.2 %collective-permute-start.13 = (bf16[512,640]{1,0:T(8,128)(2,1)S(1)}, bf16[512,640]{1,0:T(8,128)(2,1)S(1)}, u32[]{:S(2)}, u32[]{:S(2)}) collective-permute-start(bf16[512,640]{1,0:T(8,128)(2,1)S(1)} %get-tuple-element.476.refs_0_), channel_id=1, source_target_pairs={{0,1},{1,0},{2,3},{3,2},{4,6},{5,7},{6,4},{7,5},{8,9},{9,8},{10,11... | collective-permute-start | bytes 1966088 | tf_op jit(solution)/shard_map/ppermute | solution.py:88
  62.9 17.0 %collective-permute-start.14 = (bf16[512,640]{1,0:T(8,128)(2,1)S(1)}, bf16[512,640]{1,0:T(8,128)(2,1)S(1)}, u32[]{:S(2)}, u32[]{:S(2)}) collective-permute-start(bf16[512,640]{1,0:T(8,128)(2,1)S(1)} %get-tuple-element.476.refs_0_), channel_id=1, source_target_pairs={{0,2},{1,3},{2,0},{3,1},{4,5},{5,4},{6,7},{7,6},{8,10},{9,11},{10,... | collective-permute-start | bytes 1966088 | tf_op jit(solution)/shard_map/ppermute | solution.py:88
  64.1 15.7 %collective-permute-start.15 = (bf16[240,1280]{1,0:T(8,128)(2,1)}, bf16[240,1280]{1,0:T(8,128)(2,1)S(1)}, u32[]{:S(2)}, u32[]{:S(2)}) collective-permute-start(bf16[240,1280]{1,0:T(8,128)(2,1)} %collective-permute-done.10.refs_14_), channel_id=1, source_target_pairs={{0,8},{1,9},{2,10},{3,11},{4,12},{5,13},{6,14},{7,15},{8,0},{9,1},... | collective-permute-start | bytes 1843208 | tf_op jit(solution)/shard_map/ppermute | solution.py:88
  79.9 10.4 %collective-permute-start.17 = (bf16[240,1280]{1,0:T(8,128)(2,1)}, bf16[240,1280]{1,0:T(8,128)(2,1)S(1)}, u32[]{:S(2)}, u32[]{:S(2)}) collective-permute-start(bf16[240,1280]{1,0:T(8,128)(2,1)} %collective-permute-done.8.refs_10_), channel_id=1, source_target_pairs={{0,2},{1,3},{2,0},{3,1},{4,5},{5,4},{6,7},{7,6},{8,10},{9,11},{10,... | collective-permute-start | bytes 1843208 | tf_op jit(solution)/shard_map/ppermute | solution.py:88
  80.6 16.7 %collective-permute-start.16 = (bf16[512,640]{1,0:T(8,128)(2,1)S(1)}, bf16[512,640]{1,0:T(8,128)(2,1)S(1)}, u32[]{:S(2)}, u32[]{:S(2)}) collective-permute-start(bf16[512,640]{1,0:T(8,128)(2,1)S(1)} %collective-permute-done.13.refs_1_), channel_id=1, source_target_pairs={{0,2},{1,3},{2,0},{3,1},{4,5},{5,4},{6,7},{7,6},{8,10},{9,11},{10,... | collective-permute-start | bytes 1966088 | tf_op jit(solution)/shard_map/ppermute | solution.py:88
  82.0 8.3 %collective-permute-start.18 = (bf16[240,1280]{1,0:T(8,128)(2,1)}, bf16[240,1280]{1,0:T(8,128)(2,1)S(1)}, u32[]{:S(2)}, u32[]{:S(2)}) collective-permute-start(bf16[240,1280]{1,0:T(8,128)(2,1)} %collective-permute-done.8.refs_10_), channel_id=1, source_target_pairs={{0,4},{1,5},{2,6},{3,7},{4,0},{5,1},{6,2},{7,3},{8,12},{9,13},{10,... | collective-permute-start | bytes 1843208 | tf_op jit(solution)/shard_map/ppermute | solution.py:88
  82.0 8.4 %collective-permute-start.19 = (bf16[240,1280]{1,0:T(8,128)(2,1)}, bf16[240,1280]{1,0:T(8,128)(2,1)S(1)}, u32[]{:S(2)}, u32[]{:S(2)}) collective-permute-start(bf16[240,1280]{1,0:T(8,128)(2,1)} %collective-permute-done.10.refs_14_), channel_id=1, source_target_pairs={{0,4},{1,5},{2,6},{3,7},{4,0},{5,1},{6,2},{7,3},{8,12},{9,13},{10,... | collective-permute-start | bytes 1843208 | tf_op jit(solution)/shard_map/ppermute | solution.py:88
  82.5 7.9 %collective-permute-start.20 = (bf16[240,1280]{1,0:T(8,128)(2,1)}, bf16[240,1280]{1,0:T(8,128)(2,1)S(1)}, u32[]{:S(2)}, u32[]{:S(2)}) collective-permute-start(bf16[240,1280]{1,0:T(8,128)(2,1)} %collective-permute-done.11.refs_11_), channel_id=1, source_target_pairs={{0,4},{1,5},{2,6},{3,7},{4,0},{5,1},{6,2},{7,3},{8,12},{9,13},{10,... | collective-permute-start | bytes 1843208 | tf_op jit(solution)/shard_map/ppermute | solution.py:88
  97.3 23.0 %collective-permute-start.24 = (bf16[240,1280]{1,0:T(8,128)(2,1)S(1)}, bf16[240,1280]{1,0:T(8,128)(2,1)}, u32[]{:S(2)}, u32[]{:S(2)}) collective-permute-start(bf16[240,1280]{1,0:T(8,128)(2,1)S(1)} %collective-permute-done.17.refs_18_), channel_id=1, source_target_pairs={{0,8},{1,9},{2,10},{3,11},{4,12},{5,13},{6,14},{7,15},{8,0},{9,1},... | collective-permute-start | bytes 1843208 | tf_op jit(solution)/shard_map/ppermute | solution.py:88
  98.6 21.8 %collective-permute-start.25 = (bf16[240,1280]{1,0:T(8,128)(2,1)S(1)}, bf16[240,1280]{1,0:T(8,128)(2,1)S(1)}, u32[]{:S(2)}, u32[]{:S(2)}) collective-permute-start(bf16[240,1280]{1,0:T(8,128)(2,1)S(1)} %collective-permute-done.17.refs_18_), channel_id=1, source_target_pairs={{0,4},{1,5},{2,6},{3,7},{4,0},{5,1},{6,2},{7,3},{8,12},{9,13},{10,... | collective-permute-start | bytes 1843208 | tf_op jit(solution)/shard_map/ppermute | solution.py:88
  98.6 21.7 %collective-permute-start.22 = (bf16[480,640]{1,0:T(8,128)(2,1)}, bf16[480,640]{1,0:T(8,128)(2,1)}, u32[]{:S(2)}, u32[]{:S(2)}) collective-permute-start(bf16[480,640]{1,0:T(8,128)(2,1)} %dynamic-slice_bitcast_fusion), channel_id=1, source_target_pairs={{0,2},{1,3},{2,0},{3,1},{4,5},{5,4},{6,7},{7,6},{8,10},{9,11},{10,... | collective-permute-start | bytes 1843208 | tf_op jit(solution)/shard_map/ppermute | solution.py:88
  99.0 21.3 %collective-permute-start.23 = (bf16[480,640]{1,0:T(8,128)(2,1)}, bf16[480,640]{1,0:T(8,128)(2,1)}, u32[]{:S(2)}, u32[]{:S(2)}) collective-permute-start(bf16[480,640]{1,0:T(8,128)(2,1)} %collective-permute-done.12.refs_23_), channel_id=1, source_target_pairs={{0,2},{1,3},{2,0},{3,1},{4,5},{5,4},{6,7},{7,6},{8,10},{9,11},{10,... | collective-permute-start | bytes 1843208 | tf_op jit(solution)/shard_map/ppermute | solution.py:88
  121.7 4.5 %collective-permute-start.28 = (bf16[480,640]{1,0:T(8,128)(2,1)}, bf16[480,640]{1,0:T(8,128)(2,1)}, u32[]{:S(2)}, u32[]{:S(2)}) collective-permute-start(bf16[480,640]{1,0:T(8,128)(2,1)} %collective-permute-done.22.refs_25_), channel_id=1, source_target_pairs={{0,4},{1,5},{2,6},{3,7},{4,0},{5,1},{6,2},{7,3},{8,12},{9,13},{10,... | collective-permute-start | bytes 1843208 | tf_op jit(solution)/shard_map/ppermute | solution.py:88
  121.7 4.5 %collective-permute-start.29 = (bf16[480,640]{1,0:T(8,128)(2,1)}, bf16[480,640]{1,0:T(8,128)(2,1)}, u32[]{:S(2)}, u32[]{:S(2)}) collective-permute-start(bf16[480,640]{1,0:T(8,128)(2,1)} %collective-permute-done.23.refs_27_), channel_id=1, source_target_pairs={{0,4},{1,5},{2,6},{3,7},{4,0},{5,1},{6,2},{7,3},{8,12},{9,13},{10,... | collective-permute-start | bytes 1843208 | tf_op jit(solution)/shard_map/ppermute | solution.py:88
  122.2 31.6 %collective-permute-start.31 = (bf16[2,960,256]{2,1,0:T(8,128)(2,1)}, bf16[2,960,256]{2,1,0:T(8,128)(2,1)}, u32[]{:S(2)}, u32[]{:S(2)}) collective-permute-start(bf16[2,960,256]{2,1,0:T(8,128)(2,1)} %bitcast.17.x_ref.refs_0_), channel_id=1, source_target_pairs={{0,1},{1,0},{2,3},{3,2},{4,6},{5,7},{6,4},{7,5},{8,9},{9,8},{10,11... | collective-permute-start | bytes 2949128 | tf_op jit(solution)/shard_map/ppermute | solution.py:88
  124.7 29.1 %collective-permute-start.32 = (bf16[2,960,256]{2,1,0:T(8,128)(2,1)}, bf16[2,960,256]{2,1,0:T(8,128)(2,1)}, u32[]{:S(2)}, u32[]{:S(2)}) collective-permute-start(bf16[2,960,256]{2,1,0:T(8,128)(2,1)} %bitcast.17.x_ref.refs_0_), channel_id=1, source_target_pairs={{0,2},{1,3},{2,0},{3,1},{4,5},{5,4},{6,7},{7,6},{8,10},{9,11},{10,... | collective-permute-start | bytes 2949128 | tf_op jit(solution)/shard_map/ppermute | solution.py:88
  126.0 27.8 %collective-permute-start.30 = (bf16[2,960,256]{2,1,0:T(8,128)(2,1)S(1)}, bf16[2,960,256]{2,1,0:T(8,128)(2,1)S(1)}, u32[]{:S(2)}, u32[]{:S(2)}) collective-permute-start(bf16[2,960,256]{2,1,0:T(8,128)(2,1)S(1)} %bitcast.74), channel_id=1, source_target_pairs={{0,4},{1,5},{2,6},{3,7},{4,0},{5,1},{6,2},{7,3},{8,12},{9,13},{10,... | collective-permute-start | bytes 2949128 | tf_op jit(solution)/shard_map/ppermute | solution.py:88
  153.8 18.2 %collective-permute-start.34 = (bf16[512,2560]{1,0:T(8,128)(2,1)}, bf16[512,2560]{1,0:T(8,128)(2,1)}, u32[]{:S(2)}, u32[]{:S(2)}) collective-permute-start(bf16[512,2560]{1,0:T(8,128)(2,1)} %get-tuple-element.380.given_ref), channel_id=1, source_target_pairs={{0,4},{1,5},{2,6},{3,7},{4,0},{5,1},{6,2},{7,3},{8,12},{9,13},{10,... | collective-permute-start | bytes 7864328 | tf_op jit(solution)/shard_map/ppermute | solution.py:88
  153.9 18.1 %collective-permute-start.35 = (bf16[512,2560]{1,0:T(8,128)(2,1)}, bf16[512,2560]{1,0:T(8,128)(2,1)}, u32[]{:S(2)}, u32[]{:S(2)}) collective-permute-start(bf16[512,2560]{1,0:T(8,128)(2,1)} %get-tuple-element.402.inner_ref), channel_id=1, source_target_pairs={{0,4},{1,5},{2,6},{3,7},{4,0},{5,1},{6,2},{7,3},{8,12},{9,13},{10,... | collective-permute-start | bytes 7864328 | tf_op jit(solution)/shard_map/ppermute | solution.py:88
  154.4 17.6 %collective-permute-start.33 = (bf16[960,512]{1,0:T(8,128)(2,1)}, bf16[960,512]{1,0:T(8,128)(2,1)S(1)}, u32[]{:S(2)}, u32[]{:S(2)}) collective-permute-start(bf16[960,512]{1,0:T(8,128)(2,1)} %get-tuple-element.421.left_ref), channel_id=1, source_target_pairs={{0,4},{1,5},{2,6},{3,7},{4,0},{5,1},{6,2},{7,3},{8,12},{9,13},{10,... | collective-permute-start | bytes 2949128 | tf_op jit(solution)/shard_map/ppermute | solution.py:88
  154.5 17.6 %collective-permute-start.36 = (bf16[2,960,256]{2,1,0:T(8,128)(2,1)}, bf16[2,960,256]{2,1,0:T(8,128)(2,1)}, u32[]{:S(2)}, u32[]{:S(2)}) collective-permute-start(bf16[2,960,256]{2,1,0:T(8,128)(2,1)} %collective-permute-done.31.refs_1_), channel_id=1, source_target_pairs={{0,2},{1,3},{2,0},{3,1},{4,5},{5,4},{6,7},{7,6},{8,10},{9,11},{10,... | collective-permute-start | bytes 2949128 | tf_op jit(solution)/shard_map/ppermute | solution.py:88
  178.0 16.8 %collective-permute-start.37 = (bf16[960,640]{1,0:T(8,128)(2,1)S(1)}, bf16[960,640]{1,0:T(8,128)(2,1)S(1)}, u32[]{:S(2)}, u32[]{:S(2)}) collective-permute-start(bf16[960,640]{1,0:T(8,128)(2,1)S(1)} %get-tuple-element.446), channel_id=1, source_target_pairs={{0,2},{1,3},{2,0},{3,1},{4,5},{5,4},{6,7},{7,6},{8,10},{9,11},{10,... | collective-permute-start | bytes 3686408 | tf_op jit(solution)/shard_map/ppermute | solution.py:88
  195.8 24.1 %collective-permute-start.39 = (bf16[256,2560]{1,0:T(8,128)(2,1)}, bf16[256,2560]{1,0:T(8,128)(2,1)S(1)}, u32[]{:S(2)}, u32[]{:S(2)}) collective-permute-start(bf16[256,2560]{1,0:T(8,128)(2,1)} %get-tuple-element.473), channel_id=1, source_target_pairs={{0,2},{1,3},{2,0},{3,1},{4,5},{5,4},{6,7},{7,6},{8,10},{9,11},{10,... | collective-permute-start | bytes 3932168 | tf_op jit(solution)/shard_map/ppermute | solution.py:88
  197.6 18.4 %collective-permute-start.38 = (bf16[480,640]{1,0:T(8,128)(2,1)S(1)}, bf16[480,640]{1,0:T(8,128)(2,1)S(1)}, u32[]{:S(2)}, u32[]{:S(2)}) collective-permute-start(bf16[480,640]{1,0:T(8,128)(2,1)S(1)} %add_convert_fusion.12), channel_id=1, source_target_pairs={{0,1},{1,0},{2,3},{3,2},{4,6},{5,7},{6,4},{7,5},{8,9},{9,8},{10,11... | collective-permute-start | bytes 1843208 | tf_op jit(solution)/shard_map/ppermute | solution.py:88
  220.1 23.2 %collective-permute-start.41 = (bf16[128,2560]{1,0:T(8,128)(2,1)S(1)}, bf16[128,2560]{1,0:T(8,128)(2,1)S(1)}, u32[]{:S(2)}, u32[]{:S(2)}) collective-permute-start(bf16[128,2560]{1,0:T(8,128)(2,1)S(1)} %add_convert_fusion.8), channel_id=1, source_target_pairs={{0,1},{1,0},{2,3},{3,2},{4,6},{5,7},{6,4},{7,5},{8,9},{9,8},{10,11... | collective-permute-start | bytes 1966088 | tf_op jit(solution)/shard_map/ppermute | solution.py:88
  221.3 22.0 %collective-permute-start.42 = (bf16[224,2560]{1,0:T(8,128)(2,1)S(1)}, bf16[224,2560]{1,0:T(8,128)(2,1)}, u32[]{:S(2)}, u32[]{:S(2)}) collective-permute-start(bf16[224,2560]{1,0:T(8,128)(2,1)S(1)} %get-tuple-element.500), channel_id=1, source_target_pairs={{0,2},{1,3},{2,0},{3,1},{4,5},{5,4},{6,7},{7,6},{8,10},{9,11},{10,... | collective-permute-start | bytes 3440648 | tf_op jit(solution)/shard_map/ppermute | solution.py:88
  223.4 19.8 %collective-permute-start.40 = (bf16[480,640]{1,0:T(8,128)(2,1)S(1)}, bf16[480,640]{1,0:T(8,128)(2,1)S(1)}, u32[]{:S(2)}, u32[]{:S(2)}) collective-permute-start(bf16[480,640]{1,0:T(8,128)(2,1)S(1)} %add_convert_fusion.11), channel_id=1, source_target_pairs={{0,8},{1,9},{2,10},{3,11},{4,12},{5,13},{6,14},{7,15},{24,16},{25,... | collective-permute-start | bytes 1843208 | tf_op jit(solution)/shard_map/ppermute | solution.py:88
  244.2 22.4 %collective-permute-start.45 = (bf16[128,2560]{1,0:T(8,128)(2,1)S(1)}, bf16[128,2560]{1,0:T(8,128)(2,1)}, u32[]{:S(2)}, u32[]{:S(2)}) collective-permute-start(bf16[128,2560]{1,0:T(8,128)(2,1)S(1)} %add_convert_fusion.7), channel_id=1, source_target_pairs={{0,8},{1,9},{2,10},{3,11},{4,12},{5,13},{6,14},{7,15},{24,16},{25,... | collective-permute-start | bytes 1966088 | tf_op jit(solution)/shard_map/ppermute | solution.py:88
  246.4 24.1 %collective-permute-start.43 = (bf16[2,512,640]{2,1,0:T(8,128)(2,1)}, bf16[2,512,640]{2,1,0:T(8,128)(2,1)}, u32[]{:S(2)}, u32[]{:S(2)}) collective-permute-start(bf16[2,512,640]{2,1,0:T(8,128)(2,1)} %get-tuple-element.505.refs_5_), channel_id=1, source_target_pairs={{0,2},{1,3},{2,0},{3,1},{4,5},{5,4},{6,7},{7,6},{8,10},{9,11},{10,... | collective-permute-start | bytes 3932168 | tf_op jit(solution)/shard_map/ppermute | solution.py:88
  247.7 18.9 %collective-permute-start.44 = (bf16[480,640]{1,0:T(8,128)(2,1)S(1)}, bf16[480,640]{1,0:T(8,128)(2,1)S(1)}, u32[]{:S(2)}, u32[]{:S(2)}) collective-permute-start(bf16[480,640]{1,0:T(8,128)(2,1)S(1)} %add_convert_fusion.10), channel_id=1, source_target_pairs={{8,16},{9,17},{10,18},{11,19},{12,20},{13,21},{14,22},{15,23},{16,... | collective-permute-start | bytes 1843208 | tf_op jit(solution)/shard_map/ppermute | solution.py:88
  250.4 16.2 %collective-permute-start.46 = (bf16[112,2560]{1,0:T(8,128)(2,1)}, bf16[112,2560]{1,0:T(8,128)(2,1)}, u32[]{:S(2)}, u32[]{:S(2)}) collective-permute-start(bf16[112,2560]{1,0:T(8,128)(2,1)} %add_convert_fusion.16), channel_id=1, source_target_pairs={{0,1},{1,0},{2,3},{3,2},{4,6},{5,7},{6,4},{7,5},{8,9},{9,8},{10,11... | collective-permute-start | bytes 1720328 | tf_op jit(solution)/shard_map/ppermute | solution.py:88
  270.5 6.4 %collective-permute-start.49 = (bf16[512,2688]{1,0:T(8,128)(2,1)}, bf16[512,2688]{1,0:T(8,128)(2,1)S(1)}, u32[]{:S(2)}, u32[]{:S(2)}) collective-permute-start(bf16[512,2688]{1,0:T(8,128)(2,1)} %get-tuple-element.525), channel_id=1, source_target_pairs={{0,4},{1,5},{2,6},{3,7},{4,0},{5,1},{6,2},{7,3},{8,12},{9,13},{10,... | collective-permute-start | bytes 8257544 | tf_op jit(solution)/shard_map/ppermute | solution.py:88
  271.9 30.1 %collective-permute-start.51 = (bf16[128,2560]{1,0:T(8,128)(2,1)S(1)}, bf16[128,2560]{1,0:T(8,128)(2,1)}, u32[]{:S(2)}, u32[]{:S(2)}) collective-permute-start(bf16[128,2560]{1,0:T(8,128)(2,1)S(1)} %add_convert_fusion.5), channel_id=1, source_target_pairs={{8,16},{9,17},{10,18},{11,19},{12,20},{13,21},{14,22},{15,23},{16,... | collective-permute-start | bytes 1966088 | tf_op jit(solution)/shard_map/ppermute | solution.py:88
  275.4 26.6 %collective-permute-start.48 = (bf16[480,640]{1,0:T(8,128)(2,1)}, bf16[480,640]{1,0:T(8,128)(2,1)}, u32[]{:S(2)}, u32[]{:S(2)}) collective-permute-start(bf16[480,640]{1,0:T(8,128)(2,1)} %add_convert_fusion.9), channel_id=1, source_target_pairs={{8,0},{9,1},{10,2},{11,3},{12,4},{13,5},{14,6},{15,7},{16,24},{17,... | collective-permute-start | bytes 1843208 | tf_op jit(solution)/shard_map/ppermute | solution.py:88
  278.9 25.6 %collective-permute-start.50 = (bf16[256,2688]{1,0:T(8,128)(2,1)}, bf16[256,2688]{1,0:T(8,128)(2,1)}, u32[]{:S(2)}, u32[]{:S(2)}) collective-permute-start(bf16[256,2688]{1,0:T(8,128)(2,1)} %add_convert_fusion), channel_id=1, source_target_pairs={{0,2},{1,3},{2,0},{3,1},{4,5},{5,4},{6,7},{7,6},{8,10},{9,11},{10,... | collective-permute-start | bytes 4128776 | tf_op jit(solution)/shard_map/ppermute | solution.py:88
  282.2 19.8 %collective-permute-start.47 = (bf16[1,512,640]{2,1,0:T(8,128)(2,1)}, bf16[1,512,640]{2,1,0:T(8,128)(2,1)}, u32[]{:S(2)}, u32[]{:S(2)}) collective-permute-start(bf16[1,512,640]{2,1,0:T(8,128)(2,1)} %add_convert_fusion.6), channel_id=1, source_target_pairs={{0,1},{1,0},{2,3},{3,2},{4,6},{5,7},{6,4},{7,5},{8,9},{9,8},{10,11... | collective-permute-start | bytes 1966088 | tf_op jit(solution)/shard_map/ppermute | solution.py:88
  284.5 17.4 %collective-permute-start.52 = (bf16[112,2560]{1,0:T(8,128)(2,1)S(1)}, bf16[112,2560]{1,0:T(8,128)(2,1)S(1)}, u32[]{:S(2)}, u32[]{:S(2)}) collective-permute-start(bf16[112,2560]{1,0:T(8,128)(2,1)S(1)} %add_convert_fusion.15), channel_id=1, source_target_pairs={{0,8},{1,9},{2,10},{3,11},{4,12},{5,13},{6,14},{7,15},{24,16},{25,... | collective-permute-start | bytes 1720328 | tf_op jit(solution)/shard_map/ppermute | solution.py:88
  304.7 22.9 %collective-permute-start.59 = (bf16[112,2560]{1,0:T(8,128)(2,1)S(1)}, bf16[112,2560]{1,0:T(8,128)(2,1)S(1)}, u32[]{:S(2)}, u32[]{:S(2)}) collective-permute-start(bf16[112,2560]{1,0:T(8,128)(2,1)S(1)} %add_convert_fusion.14), channel_id=1, source_target_pairs={{8,16},{9,17},{10,18},{11,19},{12,20},{13,21},{14,22},{15,23},{16,... | collective-permute-start | bytes 1720328 | tf_op jit(solution)/shard_map/ppermute | solution.py:88
  307.2 11.0 %collective-permute-start.54 = (bf16[128,2688]{1,0:T(8,128)(2,1)S(1)}, bf16[128,2688]{1,0:T(8,128)(2,1)S(1)}, u32[]{:S(2)}, u32[]{:S(2)}) collective-permute-start(bf16[128,2688]{1,0:T(8,128)(2,1)S(1)} %add_convert_fusion.2), channel_id=1, source_target_pairs={{0,1},{1,0},{2,3},{3,2},{4,6},{5,7},{6,4},{7,5},{8,9},{9,8},{10,11... | collective-permute-start | bytes 2064392 | tf_op jit(solution)/shard_map/ppermute | solution.py:88
  309.7 30.7 %collective-permute-start.58 = (bf16[128,2560]{1,0:T(8,128)(2,1)S(1)}, bf16[128,2560]{1,0:T(8,128)(2,1)S(1)}, u32[]{:S(2)}, u32[]{:S(2)}) collective-permute-start(bf16[128,2560]{1,0:T(8,128)(2,1)S(1)} %add_convert_fusion.3), channel_id=1, source_target_pairs={{8,0},{9,1},{10,2},{11,3},{12,4},{13,5},{14,6},{15,7},{16,24},{17,... | collective-permute-start | bytes 1966088 | tf_op jit(solution)/shard_map/ppermute | solution.py:88
  312.4 28.0 %collective-permute-start.53 = (bf16[480,640]{1,0:T(8,128)(2,1)S(1)}, bf16[480,640]{1,0:T(8,128)(2,1)S(1)}, u32[]{:S(2)}, u32[]{:S(2)}) collective-permute-start(bf16[480,640]{1,0:T(8,128)(2,1)S(1)} %broadcast_select_fusion.4), channel_id=1, source_target_pairs={{0,4},{1,5},{2,6},{3,7},{4,0},{5,1},{6,2},{7,3},{8,12},{9,13},{10,... | collective-permute-start | bytes 1843208 | tf_op jit(solution)/shard_map/ppermute | solution.py:88
  320.3 22.6 %collective-permute-start.55 = (bf16[32,2688]{1,0:T(8,128)(2,1)S(1)}, bf16[32,2688]{1,0:T(8,128)(2,1)S(1)}, u32[]{:S(2)}, u32[]{:S(2)}) collective-permute-start(bf16[32,2688]{1,0:T(8,128)(2,1)S(1)} %get-tuple-element.608), channel_id=1, source_target_pairs={{0,8},{1,9},{2,10},{3,11},{4,12},{5,13},{6,14},{7,15},{8,0},{9,1},... | collective-permute-start | bytes 516104 | tf_op jit(solution)/shard_map/ppermute | solution.py:88
  327.6 15.4 %collective-permute-start.56 = (bf16[32,2688]{1,0:T(8,128)(2,1)S(1)}, bf16[32,2688]{1,0:T(8,128)(2,1)S(1)}, u32[]{:S(2)}, u32[]{:S(2)}) collective-permute-start(bf16[32,2688]{1,0:T(8,128)(2,1)S(1)} %get-tuple-element.607), channel_id=1, source_target_pairs={{0,16},{1,17},{2,18},{3,19},{4,20},{5,21},{6,22},{7,23},{8,24},{9,... | collective-permute-start | bytes 516104 | tf_op jit(solution)/shard_map/ppermute | solution.py:88
  327.6 15.3 %collective-permute-start.57 = (bf16[32,2688]{1,0:T(8,128)(2,1)S(1)}, bf16[32,2688]{1,0:T(8,128)(2,1)S(1)}, u32[]{:S(2)}, u32[]{:S(2)}) collective-permute-start(bf16[32,2688]{1,0:T(8,128)(2,1)S(1)} %get-tuple-element.606), channel_id=1, source_target_pairs={{0,24},{1,25},{2,26},{3,27},{4,28},{5,29},{6,30},{7,31},{8,16},{9,... | collective-permute-start | bytes 516104 | tf_op jit(solution)/shard_map/ppermute | solution.py:88
  343.1 9.0 %collective-permute-start.60 = (bf16[32,2688]{1,0:T(8,128)(2,1)S(1)}, bf16[32,2688]{1,0:T(8,128)(2,1)S(1)}, u32[]{:S(2)}, u32[]{:S(2)}) collective-permute-start(bf16[32,2688]{1,0:T(8,128)(2,1)S(1)} %add_convert_fusion.17), channel_id=1, source_target_pairs={{0,8},{1,9},{2,10},{3,11},{4,12},{5,13},{6,14},{7,15},{8,0},{9,1},... | collective-permute-start | bytes 516104 | tf_op jit(solution)/shard_map/ppermute | solution.py:88
  344.6 13.8 %collective-permute-start.61 = (bf16[32,2688]{1,0:T(8,128)(2,1)S(1)}, bf16[32,2688]{1,0:T(8,128)(2,1)S(1)}, u32[]{:S(2)}, u32[]{:S(2)}) collective-permute-start(bf16[32,2688]{1,0:T(8,128)(2,1)S(1)} %add_convert_fusion.17), channel_id=1, source_target_pairs={{0,16},{1,17},{2,18},{3,19},{4,20},{5,21},{6,22},{7,23},{8,24},{9,... | collective-permute-start | bytes 516104 | tf_op jit(solution)/shard_map/ppermute | solution.py:88
  344.9 13.5 %collective-permute-start.62 = (bf16[32,2688]{1,0:T(8,128)(2,1)S(1)}, bf16[32,2688]{1,0:T(8,128)(2,1)S(1)}, u32[]{:S(2)}, u32[]{:S(2)}) collective-permute-start(bf16[32,2688]{1,0:T(8,128)(2,1)S(1)} %add_convert_fusion.17), channel_id=1, source_target_pairs={{0,24},{1,25},{2,26},{3,27},{4,28},{5,29},{6,30},{7,31},{8,16},{9,... | collective-permute-start | bytes 516104 | tf_op jit(solution)/shard_map/ppermute | solution.py:88
  347.8 20.4 %collective-permute-start.65 = (bf16[112,2560]{1,0:T(8,128)(2,1)S(1)}, bf16[112,2560]{1,0:T(8,128)(2,1)S(1)}, u32[]{:S(2)}, u32[]{:S(2)}) collective-permute-start(bf16[112,2560]{1,0:T(8,128)(2,1)S(1)} %add_convert_fusion.13), channel_id=1, source_target_pairs={{8,0},{9,1},{10,2},{11,3},{12,4},{13,5},{14,6},{15,7},{16,24},{17,... | collective-permute-start | bytes 1720328 | tf_op jit(solution)/shard_map/ppermute | solution.py:88
  349.2 28.7 %collective-permute-start.64 = (bf16[128,2560]{1,0:T(8,128)(2,1)S(1)}, bf16[128,2560]{1,0:T(8,128)(2,1)S(1)}, u32[]{:S(2)}, u32[]{:S(2)}) collective-permute-start(bf16[128,2560]{1,0:T(8,128)(2,1)S(1)} %broadcast_select_fusion.1.refs_0_), channel_id=1, source_target_pairs={{0,4},{1,5},{2,6},{3,7},{4,0},{5,1},{6,2},{7,3},{8,12},{9,13},{10,... | collective-permute-start | bytes 1966088 | tf_op jit(solution)/shard_map/ppermute | solution.py:88
  358.8 9.6 %collective-permute-start.63 = (bf16[128,2688]{1,0:T(8,128)(2,1)S(1)}, bf16[128,2688]{1,0:T(8,128)(2,1)S(1)}, u32[]{:S(2)}, u32[]{:S(2)}) collective-permute-start(bf16[128,2688]{1,0:T(8,128)(2,1)S(1)} %bitcast.76), channel_id=1, source_target_pairs={{0,4},{1,5},{2,6},{3,7},{4,0},{5,1},{6,2},{7,3},{8,12},{9,13},{10,... | collective-permute-start | bytes 2064392 | tf_op jit(solution)/shard_map/ppermute | solution.py:88
  368.2 9.7 %collective-permute-start.66 = (bf16[112,2560]{1,0:T(8,128)(2,1)S(1)}, bf16[112,2560]{1,0:T(8,128)(2,1)S(1)}, u32[]{:S(2)}, u32[]{:S(2)}) collective-permute-start(bf16[112,2560]{1,0:T(8,128)(2,1)S(1)} %broadcast_select_fusion.6.refs_2_), channel_id=1, source_target_pairs={{0,4},{1,5},{2,6},{3,7},{4,0},{5,1},{6,2},{7,3},{8,12},{9,13},{10,... | collective-permute-start | bytes 1720328 | tf_op jit(solution)/shard_map/ppermute | solution.py:88
  (67 other events, 842.7 us)

commit v10 on v9

--- a/solution.py
+++ b/solution.py
@@ -626,6 +626,56 @@
         cost_estimate=cost(4 * w_left.size, 0, out, out, *args),
         compiler_params=pltpu.CompilerParams(vmem_limit_bytes=VMEM_LIMIT),
     )(core, gain, *args, w_left, w_right)
+
+
+def settle_some_kernel(core_ref, gain_ref, mine_ref, theirs_ref, wq_ref, wk_ref, wv_ref, *refs):
+    q_ref, o_ref, k_ref, v_ref, sum_ref, kv = refs
+    rows, width = q_ref.shape
+    half, wide = mine_ref.shape[0], rounded_up(width)
+    even = core_ref[0] == 0
+    mine, theirs = mine_ref[...].astype(F32), theirs_ref[...].astype(F32)
+    parts = (
+        (0, jnp.where(even, mine, theirs)[: rows - half]),
+        (rows - half, jnp.where(even, theirs, mine)),
+    )
+    for at, part in parts:
+        here = slice(at, at + part.shape[0])
+        q_ref[here, :] = part[:, :width]
+        o_ref[here, :] = part[:, wide : wide + width]
+        kv[here, :] = part[:, 2 * wide :]
+        sum_ref[here, :] = jnp.sum(wq_ref[here, :].astype(F32) * part[:, :width], axis=1, keepdims=True)
+    sums = sum_ref[...]
+    for out_ref, w_ref, first in ((k_ref, wk_ref, 0), (v_ref, wv_ref, KV_WIDTH)):
+        grad = kv[:, first : first + KV_WIDTH]
+        out_ref[...] = jnp.transpose(grad)
+        weight = jnp.transpose(w_ref[...]).astype(F32)
+        sums += jnp.sum(weight * grad, axis=1, keepdims=True)
+    sum_ref[...] = sums / gain_ref[...]
+
+
+def settle_some(core, gain, mine, theirs, w_query, w_key, w_value):
+    rows, width = w_query.shape
+    half, wide = mine.shape[0], rounded_up(width)
+    if (rows - half) % 16:
+        low, high = jnp.where(core[0] == 0, mine, theirs), jnp.where(core[0] == 0, theirs, mine)
+        grad = jnp.concatenate([low[: rows - half], high]).astype(F32)
+        key, value = grad[:, 2 * wide : 2 * wide + KV_WIDTH], grad[:, 2 * wide + KV_WIDTH :]
+        pairs = ((w_query, grad[:, :width]), (w_key.T, key), (w_value.T, value))
+        sums = sum(jnp.sum(w.astype(F32) * g, axis=1, keepdims=True) for w, g in pairs)
+        return grad[:, :width], grad[:, wide : wide + width], key.T, value.T, sums / gain
+    outs = (jax.ShapeDtypeStruct((rows, width), F32),) * 2
+    outs += (jax.ShapeDtypeStruct((KV_WIDTH, rows), F32),) * 2
+    outs += (jax.ShapeDtypeStruct((rows, 1), F32),)
+    return pl.pallas_call(
+        settle_some_kernel,
+        name="settle_some",
+        in_specs=[IN_SMEM] + [IN_VMEM] * 6,
+        out_specs=(IN_VMEM,) * 5,
+        out_shape=outs,
+        scratch_shapes=[pltpu.VMEM((rows, 2 * KV_WIDTH), F32)],
+        cost_estimate=cost(4 * w_query.size, 0, mine, theirs, *outs),
+        compiler_params=pltpu.CompilerParams(vmem_limit_bytes=VMEM_LIMIT),
+    )(core, gain, mine, theirs, w_query, w_key, w_value)
 
 
 def turn_keys(source, target, at, cosine, sine):
@@ -1111,10 +1161,6 @@
     plan.have["some.given"], plan.have["some.kept"] = given, kept
     plan.close()
 
-    def gain_grad(gain, *pairs):
-        sums = sum(jnp.sum(weight.astype(F32) * grad, axis=1) for weight, grad in pairs)
-        return sums / gain.astype(F32)
-
     def settle():
         have, done = plan.have, plan.have.setdefault("done", {})
         if "dkv" in have and "d_input" not in done:
@@ -1134,16 +1180,15 @@
             )
             done["gain_two"] = gain[:, 0]
         if "some" in have and "query" not in done:
-            grad = links.finish_rows(*have["some"], shard_rows)
-            first = rounded_up(width)
-            done["query"], done["output"] = grad[:, :width], grad[:, first : first + width]
-            done["key"], done["value"] = jnp.split(grad[:, 2 * first :], 2, axis=1)
-            done["gain_one"] = gain_grad(
-                norm_first,
-                (w_query, done["query"]),
-                (key_weight, done["key"]),
-                (value_weight, done["value"]),
+            done["query"], done["output"], key, value, gain = settle_some(
+                core,
+                norm_first.astype(F32)[:, None],
+                *have["some"],
+                w_query,
+                key_weight.T,
+                value_weight.T,
             )
+            done["key"], done["value"], done["gain_one"] = key.T, value.T, gain[:, 0]
 
     order, rounds = [], 0
     while plan.tasks:

time: 390 us -> 386 us (0.990)
  other arithmetic: 41.1 us -> 35.7 us
  Pallas kernels: 141 us -> 145 us
    unnamed x133 -> x127, local copies, waits for them, and re-layouts: 15 us -> 11.2 us
  transfers between devices with their start and end apart: 67 -> 67, of which waited for: 19 -> 19; matrix products, arithmetic and copies ran while one was open for 14% -> 12% of each run, Pallas kernels for 34% -> 35%
where the time goes in v10:
time: 386 us; the launch traced here: 379 us
  Pallas kernels  145 us (38%)
  waiting for transfers between devices  97.1 us (25%)
  starting transfers between devices  72.6 us (19%)
  other arithmetic  35.7 us (9%)
  local copies, waits for them, and re-layouts  26 us (7%)
    ppermute x67, waiting for transfers between devices, move(): return lax.ppermute(value, AXES, pairs)  97.1 us
    ppermute x67, starting transfers between devices, move(): return lax.ppermute(value, AXES, pairs)  72.6 us
    pallas_call x2, Pallas kernels, attend_back(): pl.pallas_call(functools.partial(attend_back_kernel, shards, seg_rows), g...  34.4 us
    pallas_call x1, Pallas kernels, feed(): pl.pallas_call(functools.partial(feed_kernel, counts), name='feed', in_sp...  27.5 us
    convert_element_type x17, other arithmetic, total(): return sum((part.astype(F32) for part in parts)).astype(parts[0].dtype)  18.4 us
    pallas_call x1, Pallas kernels, attend(): pl.pallas_call(functools.partial(attend_kernel, shards, seg_rows), grid=(...  16.7 us
    pallas_call x1, Pallas kernels, feed_back(): pl.pallas_call(functools.partial(feed_back_kernel, counts), name='feed_ba...  15 us
    pallas_call x1, Pallas kernels, attention_grad(): pl.pallas_call(functools.partial(attention_grad_kernel, shards, half), na...  13.2 us
  transfers between devices with their start and end apart: 67, of which 19 were waited for; matrix products, arithmetic and copies ran while one was open for 12% of the time, Pallas kernels for 35%

profile of v10, /device:TPU:0, one launch (start us, length us, event | category | flops | bytes accessed | tf_op | source)
XLA Modules:
  0.0 378.9 jit_solution(9766629574723962662)
XLA Ops:
  2.9 2.4 broadcast_select_fusion.4
  5.2 2.9 collective-permute-start
  8.2 1.5 collective-permute-start.1
  10.4 2.9 collective-permute-start.4
  13.9 1.7 fusion.1
  16.5 2.0 dynamic-slice_select_fusion
  18.6 1.7 multiply_sine_fusion
  20.3 2.0 dynamic-slice_bitcast_fusion
  25.2 2.0 collective-permute-start.8
  27.4 11.6 %collective-permute-done.5.refs_6_ = bf16[240,1280]{1,0:T(8,128)(2,1)S(1)} collective-permute-done((bf16[240,1280]{1,0:T(8,128)(2,1)S(1)}, bf16[240,1280]{1,0:T(8,128)(2,1)S(1)}, u32[]{:S(2)}, u32[]{:S(2)}) %collective-permute-start.5) | collective-permute-done | bytes 614432 | tf_op jit(solution)/shard_map/ppermute | solution.py:88
  39.9 2.1 tile.20
  44.1 2.4 collective-permute-start.11
  46.5 1.9 collective-permute-start.12
  48.5 2.5 copy.62.cos_ref
  51.0 2.5 copy.63.sin_ref
  54.7 6.6 %project.1 = (bf16[512,960]{1,0:T(8,128)(2,1)}, bf16[512,640]{1,0:T(8,128)(2,1)S(1)}) custom-call(s32[16]{0:T(128)S(1)} %stack.194.starts_ref.s0_ref, bf16[2,960,256]{2,1,0:T(8,128)(2,1)} %bitcast.17.x_ref.refs_0_, f32[2,960]{1,0:T(2,128)S(1)} %maximum_convert_fusion.gains_ref, f32[2048,128]{1,0:T(8,128)} %copy.62.cos_ref, f32[2048,128]{1,0:T(8,128)} %copy.63.sin_ref, ...), custom_call_target="tpu_custom_call" | custom-call | flops 1572864000 | bytes 7536640 | tf_op jit(solution)/shard_map/project/pallas_call | solution.py:344
  63.4 1.8 collective-permute-start.15
  65.2 13.9 %collective-permute-done.15.refs_15_ = bf16[240,1280]{1,0:T(8,128)(2,1)S(1)} collective-permute-done((bf16[240,1280]{1,0:T(8,128)(2,1)}, bf16[240,1280]{1,0:T(8,128)(2,1)S(1)}, u32[]{:S(2)}, u32[]{:S(2)}) %collective-permute-start.15) | collective-permute-done | bytes 614432 | tf_op jit(solution)/shard_map/ppermute | solution.py:88
  79.9 1.3 collective-permute-start.16
  81.7 7.8 %collective-permute-done.17.refs_18_ = bf16[240,1280]{1,0:T(8,128)(2,1)S(1)} collective-permute-done((bf16[240,1280]{1,0:T(8,128)(2,1)}, bf16[240,1280]{1,0:T(8,128)(2,1)S(1)}, u32[]{:S(2)}, u32[]{:S(2)}) %collective-permute-start.17) | collective-permute-done | bytes 614432 | tf_op jit(solution)/shard_map/ppermute | solution.py:88
  89.6 2.0 collective-permute-done.21.refs_17_
  91.6 5.0 %collective-permute-done.16.refs_3_ = bf16[512,640]{1,0:T(8,128)(2,1)S(1)} collective-permute-done((bf16[512,640]{1,0:T(8,128)(2,1)S(1)}, bf16[512,640]{1,0:T(8,128)(2,1)S(1)}, u32[]{:S(2)}, u32[]{:S(2)}) %collective-permute-start.16) | collective-permute-done | bytes 655392 | tf_op jit(solution)/shard_map/ppermute | solution.py:88
  98.3 1.6 collective-permute-start.23
  101.1 16.7 %attend.1 = (bf16[512,960]{1,0:T(8,128)(2,1)S(1)}, f32[512,128]{1,0:T(8,128)S(1)}) custom-call(bf16[512,960]{1,0:T(8,128)(2,1)S(1)} %copy-done.27, bf16[512,640]{1,0:T(8,128)(2,1)S(1)} %get-tuple-element.481.refs_0_, bf16[512,640]{1,0:T(8,128)(2,1)S(1)} %collective-permute-done.13.refs_1_, bf16[512,640]{1,0:T(8,128)(2,1)S(1)} %collective-permute-done.14.refs_2_, ...), custom_call_target="tpu_custom_call" | custom-call | flops 8053063680 | bytes 983040 | tf_op jit(solution)/shard_map/attend/pallas_call | solution.py:909
  125.4 27.5 %feed.1 = (bf16[2,960,256]{2,1,0:T(8,128)(2,1)}, bf16[512,2560]{1,0:T(8,128)(2,1)}, bf16[512,2560]{1,0:T(8,128)(2,1)}, bf16[512,2560]{1,0:T(8,128)(2,1)}, bf16[9...) custom-call(s32[1]{0:T(128)} %bitcast.core_ref, s32[16]{0:T(128)} %copy-done.25, ...), custom_call_target="tpu_custom_call" | custom-call | flops 11010048000 | bytes 35389440 | tf_op jit(solution)/shard_map/feed/pallas_call | solution.py:426
  153.7 1.5 collective-permute-start.36
  156.3 15.0 %feed_back.1 = (f32[960,512]{1,0:T(8,128)}, bf16[512,1024]{1,0:T(8,128)(2,1)}, bf16[512,960]{1,0:T(8,128)(2,1)}) custom-call(s32[1]{0:T(128)} %bitcast.core_ref, s32[16]{0:T(128)} %copy-done.25, s32[28]{0:T(128)} %stack.197.s1_ref, f32[960,512]{1,0:T(8,128)} %get-tuple-element.383.resid_ref, bf16[2,960,256]{2,1,0:T(8,128)(2,1)} %bitcast.79, ...), custom_call_target="tpu_custom_call" | custom-call | flops 5976883200 | bytes 26935296 | tf_op jit(solution)/shard_map/feed_back/pallas_call | solution.py:485
  171.4 5.9 %down_grad.1 = (bf16[960,640]{1,0:T(8,128)(2,1)S(1)}, bf16[960,640]{1,0:T(8,128)(2,1)S(1)}) custom-call(s32[5]{0:T(128)S(1)} %stack.214.info_ref, bf16[2,960,256]{2,1,0:T(8,128)(2,1)S(1)} %bitcast.81, bf16[2,960,256]{2,1,0:T(8,128)(2,1)S(1)} %collective-permute-done.30.far_cot_ref, bf16[512,2560]{1,0:T(8,128)(2,1)} %get-tuple-element.407.inner_ref, ...), custom_call_target="tpu_custom_call" | custom-call | flops 2516582400 | bytes 9666560 | tf_op jit(solution)/shard_map/down_grad/pallas_call | solution.py:530
  177.9 9.4 %wide_grad.1 = (bf16[256,2560]{1,0:T(8,128)(2,1)S(1)}, bf16[256,2560]{1,0:T(8,128)(2,1)}, bf16[224,2560]{1,0:T(8,128)(2,1)S(1)}, bf16[224,2560]{1,0:T(8,128)(2,1)S(1)}) custom-call(s32[4]{0:T(128)S(1)} %pad_add_fusion.1.starts_ref, bf16[960,512]{1,0:T(8,128)(2,1)S(1)} %copy-done.29, bf16[960,512]{1,0:T(8,128)(2,1)S(1)} %collective-permute-done.33.far_left_ref, ...), custom_call_target="tpu_custom_call" | custom-call | flops 5033164800 | bytes 12124160 | tf_op jit(solution)/shard_map/wide_grad/pallas_call | solution.py:579
  187.4 6.7 %collective-permute-done.37 = bf16[960,640]{1,0:T(8,128)(2,1)S(1)} collective-permute-done((bf16[960,640]{1,0:T(8,128)(2,1)S(1)}, bf16[960,640]{1,0:T(8,128)(2,1)S(1)}, u32[]{:S(2)}, u32[]{:S(2)}) %collective-permute-start.37) | collective-permute-done | bytes 1228832 | tf_op jit(solution)/shard_map/ppermute | solution.py:88
  198.1 17.2 %attend_back.2 = (bf16[512,1024]{1,0:T(8,128)(2,1)S(1)}, bf16[2,512,640]{2,1,0:T(8,128)(2,1)}, bf16[2,512,640]{2,1,0:T(8,128)(2,1)}) custom-call(bf16[512,960]{1,0:T(8,128)(2,1)S(1)} %copy-done.28, bf16[512,640]{1,0:T(8,128)(2,1)S(1)} %copy-done.31, bf16[512,640]{1,0:T(8,128)(2,1)S(1)} %copy-done.33, bf16[512,640]{1,0:T(8,128)(2,1)S(1)} %copy-done.35, ...), custom_call_target="tpu_custom_call" | custom-call | flops 10066329600 | bytes 983040 | tf_op jit(solution)/shard_map/attend_back/pallas_call | solution.py:931
  215.3 3.8 %collective-permute-done.39 = bf16[256,2560]{1,0:T(8,128)(2,1)S(1)} collective-permute-done((bf16[256,2560]{1,0:T(8,128)(2,1)}, bf16[256,2560]{1,0:T(8,128)(2,1)S(1)}, u32[]{:S(2)}, u32[]{:S(2)}) %collective-permute-start.39) | collective-permute-done | bytes 1310752 | tf_op jit(solution)/shard_map/ppermute | solution.py:88
  222.7 2.6 collective-permute-start.40
  225.3 17.2 %attend_back.3 = (bf16[512,1024]{1,0:T(8,128)(2,1)S(1)}, bf16[2,512,640]{2,1,0:T(8,128)(2,1)}, bf16[2,512,640]{2,1,0:T(8,128)(2,1)}) custom-call(bf16[512,960]{1,0:T(8,128)(2,1)S(1)} %copy-done.28, bf16[512,640]{1,0:T(8,128)(2,1)S(1)} %copy-done.31, bf16[512,640]{1,0:T(8,128)(2,1)S(1)} %copy-done.33, ...), custom_call_target="tpu_custom_call", output_to_operand_aliasing={{0}: (11, {}), {1}: (12, {}), {2}: (13, {})} | custom-call | flops 10066329600 | bytes 983040 | tf_op jit(solution)/shard_map/attend_back/pallas_call | solution.py:931
  243.4 2.1 collective-permute-start.45
  247.6 2.0 add_convert_fusion.16
  252.2 13.2 %attention_grad.1 = (bf16[512,2688]{1,0:T(8,128)(2,1)}, bf16[512,2688]{1,0:T(8,128)(2,1)}) custom-call(s32[8]{0:T(128)} %stack.227.starts_ref, f32[960,1]{1,0:T(8,128)} %copy.65.gain_ref, f32[2048,128]{1,0:T(8,128)} %copy.62.cos_ref, f32[2048,128]{1,0:T(8,128)} %copy.63.sin_ref, bf16[512,1024]{1,0:T(8,128)(2,1)} %copy-done.18, ...), custom_call_target="tpu_custom_call" | custom-call | flops 4697620480 | bytes 12058624 | tf_op jit(solution)/shard_map/attention_grad/pallas_call | solution.py:735
  265.9 3.7 collective-permute-done.43
  269.6 1.4 add_convert_fusion.5
  271.0 1.5 collective-permute-start.51
  273.8 1.4 collective-permute-start.48
  275.2 1.7 add_convert_fusion
  278.2 2.1 add_convert_fusion.6
  281.2 1.4 add_convert_fusion.15
  282.6 5.4 %collective-permute-start.52 = (bf16[112,2560]{1,0:T(8,128)(2,1)S(1)}, bf16[112,2560]{1,0:T(8,128)(2,1)S(1)}, u32[]{:S(2)}, u32[]{:S(2)}) collective-permute-start(bf16[112,2560]{1,0:T(8,128)(2,1)S(1)} %add_convert_fusion.15), channel_id=1, source_target_pairs={{0,8},{1,9},{2,10},{3,11},{4,12},{5,13},{6,14},{7,15},{24,16},{25,... | collective-permute-start | bytes 1720328 | tf_op jit(solution)/shard_map/ppermute | solution.py:88
  288.1 12.0 %collective-permute-done.52 = bf16[112,2560]{1,0:T(8,128)(2,1)S(1)} collective-permute-done((bf16[112,2560]{1,0:T(8,128)(2,1)S(1)}, bf16[112,2560]{1,0:T(8,128)(2,1)S(1)}, u32[]{:S(2)}, u32[]{:S(2)}) %collective-permute-start.52) | collective-permute-done | bytes 573472 | tf_op jit(solution)/shard_map/ppermute | solution.py:88
  300.1 2.5 collective-permute-done.50
  303.5 1.8 add_convert_fusion.2
  307.8 1.5 collective-permute-start.58
  310.6 5.7 %collective-permute-done.54 = bf16[128,2688]{1,0:T(8,128)(2,1)S(1)} collective-permute-done((bf16[128,2688]{1,0:T(8,128)(2,1)S(1)}, bf16[128,2688]{1,0:T(8,128)(2,1)S(1)}, u32[]{:S(2)}, u32[]{:S(2)}) %collective-permute-start.54) | collective-permute-done | bytes 688160 | tf_op jit(solution)/shard_map/ppermute | solution.py:88
  316.3 2.0 add_convert_fusion.1
  318.4 7.3 %collective-permute-start.55 = (bf16[32,2688]{1,0:T(8,128)(2,1)S(1)}, bf16[32,2688]{1,0:T(8,128)(2,1)S(1)}, u32[]{:S(2)}, u32[]{:S(2)}) collective-permute-start(bf16[32,2688]{1,0:T(8,128)(2,1)S(1)} %get-tuple-element.566), channel_id=1, source_target_pairs={{0,8},{1,9},{2,10},{3,11},{4,12},{5,13},{6,14},{7,15},{8,0},{9,1},... | collective-permute-start | bytes 516104 | tf_op jit(solution)/shard_map/ppermute | solution.py:88
  325.7 2.5 collective-permute-start.57
  328.2 1.5 fusion.kv_ref
  329.8 8.6 %finish.1 = bf16[2,960,256]{2,1,0:T(8,128)(2,1)} custom-call(s32[16]{0:T(128)S(1)} %copy-done.26, bf16[2,960,256]{2,1,0:T(8,128)(2,1)} %bitcast.17.x_ref.refs_0_, bf16[512,1024]{1,0:T(8,128)(2,1)} %copy-done.18, bf16[512,640]{1,0:T(8,128)(2,1)S(1)} %fusion.kv_ref, f32[960,512]{1,0:T(8,128)} %get-tuple-element.534.dres_ref, f32[960,1]{1,0:T(8,128)S(1)} %copy-done.17, ...), custom_call_target="tpu_custom_call" | custom-call | flops 1572864000 | bytes 8912896 | tf_op jit(solution)/shard_map/finish/pallas_call | solution.py:781
  338.5 2.5 collective-permute-done.55
  341.1 1.6 collective-permute-start.60
  342.9 2.6 collective-permute-start.62
  347.9 2.1 collective-permute-done.60
  350.1 6.4 %collective-permute-done.61 = bf16[32,2688]{1,0:T(8,128)(2,1)S(1)} collective-permute-done((bf16[32,2688]{1,0:T(8,128)(2,1)S(1)}, bf16[32,2688]{1,0:T(8,128)(2,1)S(1)}, u32[]{:S(2)}, u32[]{:S(2)}) %collective-permute-start.61) | collective-permute-done | bytes 172064 | tf_op jit(solution)/shard_map/ppermute | solution.py:88
  356.9 9.3 %collective-permute-done.65 = bf16[112,2560]{1,0:T(8,128)(2,1)S(1)} collective-permute-done((bf16[112,2560]{1,0:T(8,128)(2,1)S(1)}, bf16[112,2560]{1,0:T(8,128)(2,1)S(1)}, u32[]{:S(2)}, u32[]{:S(2)}) %collective-permute-start.65) | collective-permute-done | bytes 573472 | tf_op jit(solution)/shard_map/ppermute | solution.py:88
  367.6 1.6 convert_bitcast_fusion
  369.2 3.0 settle_some.1
  372.9 4.9 %settle.1 = (f32[240,2560]{1,0:T(8,128)}, f32[240,2560]{1,0:T(8,128)}, f32[240,1]{1,0:T(8,128)S(1)}) custom-call(s32[1]{0:T(128)} %bitcast.core_ref, f32[240,1]{1,0:T(8,128)S(1)} %copy.72.gain_ref, bf16[128,2560]{1,0:T(8,128)(2,1)} %broadcast_select_fusion.refs_0_, bf16[128,2560]{1,0:T(8,128)(2,1)} %collective-permute-done.64.refs_1_, ...), custom_call_target="tpu_custom_call" | custom-call | flops 2457600 | bytes 7372800 | tf_op jit(solution)/shard_map/settle/pallas_call | solution.py:620
  (288 shorter events, 55.2 us)
Async XLA Ops:
  5.2 18.3 %collective-permute-start = (bf16[240,1280]{1,0:T(8,128)(2,1)}, bf16[240,1280]{1,0:T(8,128)(2,1)S(1)}, u32[]{:S(2)}, u32[]{:S(2)}) collective-permute-start(bf16[240,1280]{1,0:T(8,128)(2,1)} %get-tuple-element.559), channel_id=1, source_target_pairs={{0,1},{1,0},{2,3},{3,2},{4,6},{5,7},{6,4},{7,5},{8,9},{9,8},{10,11... | collective-permute-start | bytes 1843208 | tf_op jit(solution)/shard_map/ppermute | solution.py:88
  8.2 15.4 %collective-permute-start.1 = (bf16[240,1280]{1,0:T(8,128)(2,1)}, bf16[240,1280]{1,0:T(8,128)(2,1)}, u32[]{:S(2)}, u32[]{:S(2)}) collective-permute-start(bf16[240,1280]{1,0:T(8,128)(2,1)} %get-tuple-element.559), channel_id=1, source_target_pairs={{0,2},{1,3},{2,0},{3,1},{4,5},{5,4},{6,7},{7,6},{8,10},{9,11},{10,... | collective-permute-start | bytes 1843208 | tf_op jit(solution)/shard_map/ppermute | solution.py:88
  9.7 12.9 %collective-permute-start.2 = (bf16[2,240]{1,0:T(2,128)(2,1)S(1)}, bf16[2,240]{1,0:T(2,128)(2,1)S(1)}, u32[]{:S(2)}, u32[]{:S(2)}) collective-permute-start(bf16[2,240]{1,0:T(2,128)(2,1)S(1)} %pad_maximum_fusion.5), channel_id=1, source_target_pairs={{0,1},{1,0},{2,3},{3,2},{4,5},{5,4},{6,7},{7,6},{8,9},{9,8},{10,11... | collective-permute-start | bytes 2888 | tf_op jit(solution)/shard_map/ppermute | solution.py:88
  10.3 12.3 %collective-permute-start.3 = (bf16[2,240]{1,0:T(2,128)(2,1)S(1)}, bf16[2,240]{1,0:T(2,128)(2,1)S(1)}, u32[]{:S(2)}, u32[]{:S(2)}) collective-permute-start(bf16[2,240]{1,0:T(2,128)(2,1)S(1)} %pad_maximum_fusion.5), channel_id=1, source_target_pairs={{0,2},{1,3},{2,0},{3,1},{4,6},{5,7},{6,4},{7,5},{8,10},{9,11},{10,... | collective-permute-start | bytes 2888 | tf_op jit(solution)/shard_map/ppermute | solution.py:88
  10.4 13.2 %collective-permute-start.4 = (bf16[2,240]{1,0:T(2,128)(2,1)S(1)}, bf16[2,240]{1,0:T(2,128)(2,1)S(1)}, u32[]{:S(2)}, u32[]{:S(2)}) collective-permute-start(bf16[2,240]{1,0:T(2,128)(2,1)S(1)} %pad_maximum_fusion.5), channel_id=1, source_target_pairs={{0,3},{1,2},{2,1},{3,0},{4,7},{5,6},{6,5},{7,4},{8,11},{9,10},{10,... | collective-permute-start | bytes 2888 | tf_op jit(solution)/shard_map/ppermute | solution.py:88
  23.6 15.5 %collective-permute-start.5 = (bf16[240,1280]{1,0:T(8,128)(2,1)S(1)}, bf16[240,1280]{1,0:T(8,128)(2,1)S(1)}, u32[]{:S(2)}, u32[]{:S(2)}) collective-permute-start(bf16[240,1280]{1,0:T(8,128)(2,1)S(1)} %collective-permute-done.refs_2_), channel_id=1, source_target_pairs={{0,2},{1,3},{2,0},{3,1},{4,5},{5,4},{6,7},{7,6},{8,10},{9,11},{10,... | collective-permute-start | bytes 1843208 | tf_op jit(solution)/shard_map/ppermute | solution.py:88
  24.2 14.8 %collective-permute-start.6 = (bf16[240,1280]{1,0:T(8,128)(2,1)S(1)}, bf16[240,1280]{1,0:T(8,128)(2,1)S(1)}, u32[]{:S(2)}, u32[]{:S(2)}) collective-permute-start(bf16[240,1280]{1,0:T(8,128)(2,1)S(1)} %collective-permute-done.refs_2_), channel_id=1, source_target_pairs={{0,4},{1,5},{2,6},{3,7},{4,0},{5,1},{6,2},{7,3},{8,12},{9,13},{10,... | collective-permute-start | bytes 1843208 | tf_op jit(solution)/shard_map/ppermute | solution.py:88
  25.1 13.9 %collective-permute-start.7 = (bf16[240,1280]{1,0:T(8,128)(2,1)}, bf16[240,1280]{1,0:T(8,128)(2,1)S(1)}, u32[]{:S(2)}, u32[]{:S(2)}) collective-permute-start(bf16[240,1280]{1,0:T(8,128)(2,1)} %collective-permute-done.1.refs_4_), channel_id=1, source_target_pairs={{0,4},{1,5},{2,6},{3,7},{4,0},{5,1},{6,2},{7,3},{8,12},{9,13},{10,... | collective-permute-start | bytes 1843208 | tf_op jit(solution)/shard_map/ppermute | solution.py:88
  25.2 14.7 %collective-permute-start.8 = (bf16[240,1280]{1,0:T(8,128)(2,1)}, bf16[240,1280]{1,0:T(8,128)(2,1)}, u32[]{:S(2)}, u32[]{:S(2)}) collective-permute-start(bf16[240,1280]{1,0:T(8,128)(2,1)} %dynamic-slice_select_fusion), channel_id=1, source_target_pairs={{0,1},{1,0},{2,3},{3,2},{4,6},{5,7},{6,4},{7,5},{8,9},{9,8},{10,11... | collective-permute-start | bytes 1843208 | tf_op jit(solution)/shard_map/ppermute | solution.py:88
  43.1 10.5 %collective-permute-start.9 = (bf16[240,1280]{1,0:T(8,128)(2,1)S(1)}, bf16[240,1280]{1,0:T(8,128)(2,1)}, u32[]{:S(2)}, u32[]{:S(2)}) collective-permute-start(bf16[240,1280]{1,0:T(8,128)(2,1)S(1)} %collective-permute-done.5.refs_6_), channel_id=1, source_target_pairs={{0,4},{1,5},{2,6},{3,7},{4,0},{5,1},{6,2},{7,3},{8,12},{9,13},{10,... | collective-permute-start | bytes 1843208 | tf_op jit(solution)/shard_map/ppermute | solution.py:88
  43.5 18.4 %collective-permute-start.10 = (bf16[240,1280]{1,0:T(8,128)(2,1)}, bf16[240,1280]{1,0:T(8,128)(2,1)}, u32[]{:S(2)}, u32[]{:S(2)}) collective-permute-start(bf16[240,1280]{1,0:T(8,128)(2,1)} %dynamic-slice_select_fusion), channel_id=1, source_target_pairs={{0,2},{1,3},{2,0},{3,1},{4,5},{5,4},{6,7},{7,6},{8,10},{9,11},{10,... | collective-permute-start | bytes 1843208 | tf_op jit(solution)/shard_map/ppermute | solution.py:88
  44.1 17.7 %collective-permute-start.11 = (bf16[240,1280]{1,0:T(8,128)(2,1)}, bf16[240,1280]{1,0:T(8,128)(2,1)}, u32[]{:S(2)}, u32[]{:S(2)}) collective-permute-start(bf16[240,1280]{1,0:T(8,128)(2,1)} %collective-permute-done.8.refs_10_), channel_id=1, source_target_pairs={{0,8},{1,9},{2,10},{3,11},{4,12},{5,13},{6,14},{7,15},{8,0},{9,1},... | collective-permute-start | bytes 1843208 | tf_op jit(solution)/shard_map/ppermute | solution.py:88
  46.5 15.4 %collective-permute-start.12 = (bf16[480,640]{1,0:T(8,128)(2,1)}, bf16[480,640]{1,0:T(8,128)(2,1)}, u32[]{:S(2)}, u32[]{:S(2)}) collective-permute-start(bf16[480,640]{1,0:T(8,128)(2,1)} %dynamic-slice_bitcast_fusion), channel_id=1, source_target_pairs={{0,1},{1,0},{2,3},{3,2},{4,6},{5,7},{6,4},{7,5},{8,9},{9,8},{10,11... | collective-permute-start | bytes 1843208 | tf_op jit(solution)/shard_map/ppermute | solution.py:88
  61.9 17.2 %collective-permute-start.13 = (bf16[512,640]{1,0:T(8,128)(2,1)S(1)}, bf16[512,640]{1,0:T(8,128)(2,1)S(1)}, u32[]{:S(2)}, u32[]{:S(2)}) collective-permute-start(bf16[512,640]{1,0:T(8,128)(2,1)S(1)} %get-tuple-element.481.refs_0_), channel_id=1, source_target_pairs={{0,1},{1,0},{2,3},{3,2},{4,6},{5,7},{6,4},{7,5},{8,9},{9,8},{10,11... | collective-permute-start | bytes 1966088 | tf_op jit(solution)/shard_map/ppermute | solution.py:88
  62.1 17.0 %collective-permute-start.14 = (bf16[512,640]{1,0:T(8,128)(2,1)S(1)}, bf16[512,640]{1,0:T(8,128)(2,1)S(1)}, u32[]{:S(2)}, u32[]{:S(2)}) collective-permute-start(bf16[512,640]{1,0:T(8,128)(2,1)S(1)} %get-tuple-element.481.refs_0_), channel_id=1, source_target_pairs={{0,2},{1,3},{2,0},{3,1},{4,5},{5,4},{6,7},{7,6},{8,10},{9,11},{10,... | collective-permute-start | bytes 1966088 | tf_op jit(solution)/shard_map/ppermute | solution.py:88
  63.4 15.7 %collective-permute-start.15 = (bf16[240,1280]{1,0:T(8,128)(2,1)}, bf16[240,1280]{1,0:T(8,128)(2,1)S(1)}, u32[]{:S(2)}, u32[]{:S(2)}) collective-permute-start(bf16[240,1280]{1,0:T(8,128)(2,1)} %collective-permute-done.10.refs_14_), channel_id=1, source_target_pairs={{0,8},{1,9},{2,10},{3,11},{4,12},{5,13},{6,14},{7,15},{8,0},{9,1},... | collective-permute-start | bytes 1843208 | tf_op jit(solution)/shard_map/ppermute | solution.py:88
  79.1 10.4 %collective-permute-start.17 = (bf16[240,1280]{1,0:T(8,128)(2,1)}, bf16[240,1280]{1,0:T(8,128)(2,1)S(1)}, u32[]{:S(2)}, u32[]{:S(2)}) collective-permute-start(bf16[240,1280]{1,0:T(8,128)(2,1)} %collective-permute-done.8.refs_10_), channel_id=1, source_target_pairs={{0,2},{1,3},{2,0},{3,1},{4,5},{5,4},{6,7},{7,6},{8,10},{9,11},{10,... | collective-permute-start | bytes 1843208 | tf_op jit(solution)/shard_map/ppermute | solution.py:88
  79.9 16.7 %collective-permute-start.16 = (bf16[512,640]{1,0:T(8,128)(2,1)S(1)}, bf16[512,640]{1,0:T(8,128)(2,1)S(1)}, u32[]{:S(2)}, u32[]{:S(2)}) collective-permute-start(bf16[512,640]{1,0:T(8,128)(2,1)S(1)} %collective-permute-done.13.refs_1_), channel_id=1, source_target_pairs={{0,2},{1,3},{2,0},{3,1},{4,5},{5,4},{6,7},{7,6},{8,10},{9,11},{10,... | collective-permute-start | bytes 1966088 | tf_op jit(solution)/shard_map/ppermute | solution.py:88
  81.2 8.3 %collective-permute-start.18 = (bf16[240,1280]{1,0:T(8,128)(2,1)}, bf16[240,1280]{1,0:T(8,128)(2,1)S(1)}, u32[]{:S(2)}, u32[]{:S(2)}) collective-permute-start(bf16[240,1280]{1,0:T(8,128)(2,1)} %collective-permute-done.8.refs_10_), channel_id=1, source_target_pairs={{0,4},{1,5},{2,6},{3,7},{4,0},{5,1},{6,2},{7,3},{8,12},{9,13},{10,... | collective-permute-start | bytes 1843208 | tf_op jit(solution)/shard_map/ppermute | solution.py:88
  81.2 8.4 %collective-permute-start.19 = (bf16[240,1280]{1,0:T(8,128)(2,1)}, bf16[240,1280]{1,0:T(8,128)(2,1)S(1)}, u32[]{:S(2)}, u32[]{:S(2)}) collective-permute-start(bf16[240,1280]{1,0:T(8,128)(2,1)} %collective-permute-done.10.refs_14_), channel_id=1, source_target_pairs={{0,4},{1,5},{2,6},{3,7},{4,0},{5,1},{6,2},{7,3},{8,12},{9,13},{10,... | collective-permute-start | bytes 1843208 | tf_op jit(solution)/shard_map/ppermute | solution.py:88
  81.7 7.9 %collective-permute-start.20 = (bf16[240,1280]{1,0:T(8,128)(2,1)}, bf16[240,1280]{1,0:T(8,128)(2,1)S(1)}, u32[]{:S(2)}, u32[]{:S(2)}) collective-permute-start(bf16[240,1280]{1,0:T(8,128)(2,1)} %collective-permute-done.11.refs_11_), channel_id=1, source_target_pairs={{0,4},{1,5},{2,6},{3,7},{4,0},{5,1},{6,2},{7,3},{8,12},{9,13},{10,... | collective-permute-start | bytes 1843208 | tf_op jit(solution)/shard_map/ppermute | solution.py:88
  96.6 23.0 %collective-permute-start.24 = (bf16[240,1280]{1,0:T(8,128)(2,1)S(1)}, bf16[240,1280]{1,0:T(8,128)(2,1)}, u32[]{:S(2)}, u32[]{:S(2)}) collective-permute-start(bf16[240,1280]{1,0:T(8,128)(2,1)S(1)} %collective-permute-done.17.refs_18_), channel_id=1, source_target_pairs={{0,8},{1,9},{2,10},{3,11},{4,12},{5,13},{6,14},{7,15},{8,0},{9,1},... | collective-permute-start | bytes 1843208 | tf_op jit(solution)/shard_map/ppermute | solution.py:88
  97.9 21.7 %collective-permute-start.25 = (bf16[240,1280]{1,0:T(8,128)(2,1)S(1)}, bf16[240,1280]{1,0:T(8,128)(2,1)S(1)}, u32[]{:S(2)}, u32[]{:S(2)}) collective-permute-start(bf16[240,1280]{1,0:T(8,128)(2,1)S(1)} %collective-permute-done.17.refs_18_), channel_id=1, source_target_pairs={{0,4},{1,5},{2,6},{3,7},{4,0},{5,1},{6,2},{7,3},{8,12},{9,13},{10,... | collective-permute-start | bytes 1843208 | tf_op jit(solution)/shard_map/ppermute | solution.py:88
  97.9 21.7 %collective-permute-start.22 = (bf16[480,640]{1,0:T(8,128)(2,1)}, bf16[480,640]{1,0:T(8,128)(2,1)}, u32[]{:S(2)}, u32[]{:S(2)}) collective-permute-start(bf16[480,640]{1,0:T(8,128)(2,1)} %dynamic-slice_bitcast_fusion), channel_id=1, source_target_pairs={{0,2},{1,3},{2,0},{3,1},{4,5},{5,4},{6,7},{7,6},{8,10},{9,11},{10,... | collective-permute-start | bytes 1843208 | tf_op jit(solution)/shard_map/ppermute | solution.py:88
  98.3 21.3 %collective-permute-start.23 = (bf16[480,640]{1,0:T(8,128)(2,1)}, bf16[480,640]{1,0:T(8,128)(2,1)}, u32[]{:S(2)}, u32[]{:S(2)}) collective-permute-start(bf16[480,640]{1,0:T(8,128)(2,1)} %collective-permute-done.12.refs_23_), channel_id=1, source_target_pairs={{0,2},{1,3},{2,0},{3,1},{4,5},{5,4},{6,7},{7,6},{8,10},{9,11},{10,... | collective-permute-start | bytes 1843208 | tf_op jit(solution)/shard_map/ppermute | solution.py:88
  120.9 4.5 %collective-permute-start.28 = (bf16[480,640]{1,0:T(8,128)(2,1)}, bf16[480,640]{1,0:T(8,128)(2,1)}, u32[]{:S(2)}, u32[]{:S(2)}) collective-permute-start(bf16[480,640]{1,0:T(8,128)(2,1)} %collective-permute-done.22.refs_25_), channel_id=1, source_target_pairs={{0,4},{1,5},{2,6},{3,7},{4,0},{5,1},{6,2},{7,3},{8,12},{9,13},{10,... | collective-permute-start | bytes 1843208 | tf_op jit(solution)/shard_map/ppermute | solution.py:88
  120.9 4.5 %collective-permute-start.29 = (bf16[480,640]{1,0:T(8,128)(2,1)}, bf16[480,640]{1,0:T(8,128)(2,1)}, u32[]{:S(2)}, u32[]{:S(2)}) collective-permute-start(bf16[480,640]{1,0:T(8,128)(2,1)} %collective-permute-done.23.refs_27_), channel_id=1, source_target_pairs={{0,4},{1,5},{2,6},{3,7},{4,0},{5,1},{6,2},{7,3},{8,12},{9,13},{10,... | collective-permute-start | bytes 1843208 | tf_op jit(solution)/shard_map/ppermute | solution.py:88
  121.4 31.5 %collective-permute-start.31 = (bf16[2,960,256]{2,1,0:T(8,128)(2,1)}, bf16[2,960,256]{2,1,0:T(8,128)(2,1)}, u32[]{:S(2)}, u32[]{:S(2)}) collective-permute-start(bf16[2,960,256]{2,1,0:T(8,128)(2,1)} %bitcast.17.x_ref.refs_0_), channel_id=1, source_target_pairs={{0,1},{1,0},{2,3},{3,2},{4,6},{5,7},{6,4},{7,5},{8,9},{9,8},{10,11... | collective-permute-start | bytes 2949128 | tf_op jit(solution)/shard_map/ppermute | solution.py:88
  123.9 29.0 %collective-permute-start.32 = (bf16[2,960,256]{2,1,0:T(8,128)(2,1)}, bf16[2,960,256]{2,1,0:T(8,128)(2,1)}, u32[]{:S(2)}, u32[]{:S(2)}) collective-permute-start(bf16[2,960,256]{2,1,0:T(8,128)(2,1)} %bitcast.17.x_ref.refs_0_), channel_id=1, source_target_pairs={{0,2},{1,3},{2,0},{3,1},{4,5},{5,4},{6,7},{7,6},{8,10},{9,11},{10,... | collective-permute-start | bytes 2949128 | tf_op jit(solution)/shard_map/ppermute | solution.py:88
  125.2 27.7 %collective-permute-start.30 = (bf16[2,960,256]{2,1,0:T(8,128)(2,1)S(1)}, bf16[2,960,256]{2,1,0:T(8,128)(2,1)S(1)}, u32[]{:S(2)}, u32[]{:S(2)}) collective-permute-start(bf16[2,960,256]{2,1,0:T(8,128)(2,1)S(1)} %bitcast.80), channel_id=1, source_target_pairs={{0,4},{1,5},{2,6},{3,7},{4,0},{5,1},{6,2},{7,3},{8,12},{9,13},{10,... | collective-permute-start | bytes 2949128 | tf_op jit(solution)/shard_map/ppermute | solution.py:88
  153.0 18.4 %collective-permute-start.34 = (bf16[512,2560]{1,0:T(8,128)(2,1)}, bf16[512,2560]{1,0:T(8,128)(2,1)}, u32[]{:S(2)}, u32[]{:S(2)}) collective-permute-start(bf16[512,2560]{1,0:T(8,128)(2,1)} %get-tuple-element.385.given_ref), channel_id=1, source_target_pairs={{0,4},{1,5},{2,6},{3,7},{4,0},{5,1},{6,2},{7,3},{8,12},{9,13},{10,... | collective-permute-start | bytes 7864328 | tf_op jit(solution)/shard_map/ppermute | solution.py:88
  153.2 18.2 %collective-permute-start.35 = (bf16[512,2560]{1,0:T(8,128)(2,1)}, bf16[512,2560]{1,0:T(8,128)(2,1)}, u32[]{:S(2)}, u32[]{:S(2)}) collective-permute-start(bf16[512,2560]{1,0:T(8,128)(2,1)} %get-tuple-element.407.inner_ref), channel_id=1, source_target_pairs={{0,4},{1,5},{2,6},{3,7},{4,0},{5,1},{6,2},{7,3},{8,12},{9,13},{10,... | collective-permute-start | bytes 7864328 | tf_op jit(solution)/shard_map/ppermute | solution.py:88
  153.6 17.8 %collective-permute-start.33 = (bf16[960,512]{1,0:T(8,128)(2,1)}, bf16[960,512]{1,0:T(8,128)(2,1)S(1)}, u32[]{:S(2)}, u32[]{:S(2)}) collective-permute-start(bf16[960,512]{1,0:T(8,128)(2,1)} %get-tuple-element.426.left_ref), channel_id=1, source_target_pairs={{0,4},{1,5},{2,6},{3,7},{4,0},{5,1},{6,2},{7,3},{8,12},{9,13},{10,... | collective-permute-start | bytes 2949128 | tf_op jit(solution)/shard_map/ppermute | solution.py:88
  153.7 17.6 %collective-permute-start.36 = (bf16[2,960,256]{2,1,0:T(8,128)(2,1)}, bf16[2,960,256]{2,1,0:T(8,128)(2,1)}, u32[]{:S(2)}, u32[]{:S(2)}) collective-permute-start(bf16[2,960,256]{2,1,0:T(8,128)(2,1)} %collective-permute-done.31.refs_1_), channel_id=1, source_target_pairs={{0,2},{1,3},{2,0},{3,1},{4,5},{5,4},{6,7},{7,6},{8,10},{9,11},{10,... | collective-permute-start | bytes 2949128 | tf_op jit(solution)/shard_map/ppermute | solution.py:88
  177.3 16.8 %collective-permute-start.37 = (bf16[960,640]{1,0:T(8,128)(2,1)S(1)}, bf16[960,640]{1,0:T(8,128)(2,1)S(1)}, u32[]{:S(2)}, u32[]{:S(2)}) collective-permute-start(bf16[960,640]{1,0:T(8,128)(2,1)S(1)} %get-tuple-element.451), channel_id=1, source_target_pairs={{0,2},{1,3},{2,0},{3,1},{4,5},{5,4},{6,7},{7,6},{8,10},{9,11},{10,... | collective-permute-start | bytes 3686408 | tf_op jit(solution)/shard_map/ppermute | solution.py:88
  195.1 24.0 %collective-permute-start.39 = (bf16[256,2560]{1,0:T(8,128)(2,1)}, bf16[256,2560]{1,0:T(8,128)(2,1)S(1)}, u32[]{:S(2)}, u32[]{:S(2)}) collective-permute-start(bf16[256,2560]{1,0:T(8,128)(2,1)} %get-tuple-element.478), channel_id=1, source_target_pairs={{0,2},{1,3},{2,0},{3,1},{4,5},{5,4},{6,7},{7,6},{8,10},{9,11},{10,... | collective-permute-start | bytes 3932168 | tf_op jit(solution)/shard_map/ppermute | solution.py:88
  196.8 18.4 %collective-permute-start.38 = (bf16[480,640]{1,0:T(8,128)(2,1)S(1)}, bf16[480,640]{1,0:T(8,128)(2,1)S(1)}, u32[]{:S(2)}, u32[]{:S(2)}) collective-permute-start(bf16[480,640]{1,0:T(8,128)(2,1)S(1)} %add_convert_fusion.12), channel_id=1, source_target_pairs={{0,1},{1,0},{2,3},{3,2},{4,6},{5,7},{6,4},{7,5},{8,9},{9,8},{10,11... | collective-permute-start | bytes 1843208 | tf_op jit(solution)/shard_map/ppermute | solution.py:88
  219.3 23.2 %collective-permute-start.41 = (bf16[128,2560]{1,0:T(8,128)(2,1)S(1)}, bf16[128,2560]{1,0:T(8,128)(2,1)S(1)}, u32[]{:S(2)}, u32[]{:S(2)}) collective-permute-start(bf16[128,2560]{1,0:T(8,128)(2,1)S(1)} %add_convert_fusion.8), channel_id=1, source_target_pairs={{0,1},{1,0},{2,3},{3,2},{4,6},{5,7},{6,4},{7,5},{8,9},{9,8},{10,11... | collective-permute-start | bytes 1966088 | tf_op jit(solution)/shard_map/ppermute | solution.py:88
  220.5 22.0 %collective-permute-start.42 = (bf16[224,2560]{1,0:T(8,128)(2,1)S(1)}, bf16[224,2560]{1,0:T(8,128)(2,1)}, u32[]{:S(2)}, u32[]{:S(2)}) collective-permute-start(bf16[224,2560]{1,0:T(8,128)(2,1)S(1)} %get-tuple-element.505), channel_id=1, source_target_pairs={{0,2},{1,3},{2,0},{3,1},{4,5},{5,4},{6,7},{7,6},{8,10},{9,11},{10,... | collective-permute-start | bytes 3440648 | tf_op jit(solution)/shard_map/ppermute | solution.py:88
  222.7 19.8 %collective-permute-start.40 = (bf16[480,640]{1,0:T(8,128)(2,1)S(1)}, bf16[480,640]{1,0:T(8,128)(2,1)S(1)}, u32[]{:S(2)}, u32[]{:S(2)}) collective-permute-start(bf16[480,640]{1,0:T(8,128)(2,1)S(1)} %add_convert_fusion.11), channel_id=1, source_target_pairs={{0,8},{1,9},{2,10},{3,11},{4,12},{5,13},{6,14},{7,15},{24,16},{25,... | collective-permute-start | bytes 1843208 | tf_op jit(solution)/shard_map/ppermute | solution.py:88
  243.4 22.5 %collective-permute-start.45 = (bf16[128,2560]{1,0:T(8,128)(2,1)S(1)}, bf16[128,2560]{1,0:T(8,128)(2,1)}, u32[]{:S(2)}, u32[]{:S(2)}) collective-permute-start(bf16[128,2560]{1,0:T(8,128)(2,1)S(1)} %add_convert_fusion.7), channel_id=1, source_target_pairs={{0,8},{1,9},{2,10},{3,11},{4,12},{5,13},{6,14},{7,15},{24,16},{25,... | collective-permute-start | bytes 1966088 | tf_op jit(solution)/shard_map/ppermute | solution.py:88
  245.6 24.1 %collective-permute-start.43 = (bf16[2,512,640]{2,1,0:T(8,128)(2,1)}, bf16[2,512,640]{2,1,0:T(8,128)(2,1)}, u32[]{:S(2)}, u32[]{:S(2)}) collective-permute-start(bf16[2,512,640]{2,1,0:T(8,128)(2,1)} %get-tuple-element.510.refs_5_), channel_id=1, source_target_pairs={{0,2},{1,3},{2,0},{3,1},{4,5},{5,4},{6,7},{7,6},{8,10},{9,11},{10,... | collective-permute-start | bytes 3932168 | tf_op jit(solution)/shard_map/ppermute | solution.py:88
  246.9 18.9 %collective-permute-start.44 = (bf16[480,640]{1,0:T(8,128)(2,1)S(1)}, bf16[480,640]{1,0:T(8,128)(2,1)S(1)}, u32[]{:S(2)}, u32[]{:S(2)}) collective-permute-start(bf16[480,640]{1,0:T(8,128)(2,1)S(1)} %add_convert_fusion.10), channel_id=1, source_target_pairs={{8,16},{9,17},{10,18},{11,19},{12,20},{13,21},{14,22},{15,23},{16,... | collective-permute-start | bytes 1843208 | tf_op jit(solution)/shard_map/ppermute | solution.py:88
  249.7 16.2 %collective-permute-start.46 = (bf16[112,2560]{1,0:T(8,128)(2,1)}, bf16[112,2560]{1,0:T(8,128)(2,1)}, u32[]{:S(2)}, u32[]{:S(2)}) collective-permute-start(bf16[112,2560]{1,0:T(8,128)(2,1)} %add_convert_fusion.16), channel_id=1, source_target_pairs={{0,1},{1,0},{2,3},{3,2},{4,6},{5,7},{6,4},{7,5},{8,9},{9,8},{10,11... | collective-permute-start | bytes 1720328 | tf_op jit(solution)/shard_map/ppermute | solution.py:88
  269.6 5.6 %collective-permute-start.49 = (bf16[512,2688]{1,0:T(8,128)(2,1)}, bf16[512,2688]{1,0:T(8,128)(2,1)S(1)}, u32[]{:S(2)}, u32[]{:S(2)}) collective-permute-start(bf16[512,2688]{1,0:T(8,128)(2,1)} %get-tuple-element.530), channel_id=1, source_target_pairs={{0,4},{1,5},{2,6},{3,7},{4,0},{5,1},{6,2},{7,3},{8,12},{9,13},{10,... | collective-permute-start | bytes 8257544 | tf_op jit(solution)/shard_map/ppermute | solution.py:88
  271.0 29.1 %collective-permute-start.51 = (bf16[128,2560]{1,0:T(8,128)(2,1)S(1)}, bf16[128,2560]{1,0:T(8,128)(2,1)}, u32[]{:S(2)}, u32[]{:S(2)}) collective-permute-start(bf16[128,2560]{1,0:T(8,128)(2,1)S(1)} %add_convert_fusion.5), channel_id=1, source_target_pairs={{8,16},{9,17},{10,18},{11,19},{12,20},{13,21},{14,22},{15,23},{16,... | collective-permute-start | bytes 1966088 | tf_op jit(solution)/shard_map/ppermute | solution.py:88
  273.8 26.3 %collective-permute-start.48 = (bf16[480,640]{1,0:T(8,128)(2,1)S(1)}, bf16[480,640]{1,0:T(8,128)(2,1)}, u32[]{:S(2)}, u32[]{:S(2)}) collective-permute-start(bf16[480,640]{1,0:T(8,128)(2,1)S(1)} %add_convert_fusion.9), channel_id=1, source_target_pairs={{8,0},{9,1},{10,2},{11,3},{12,4},{13,5},{14,6},{15,7},{16,24},{17,... | collective-permute-start | bytes 1843208 | tf_op jit(solution)/shard_map/ppermute | solution.py:88
  277.0 25.6 %collective-permute-start.50 = (bf16[256,2688]{1,0:T(8,128)(2,1)}, bf16[256,2688]{1,0:T(8,128)(2,1)}, u32[]{:S(2)}, u32[]{:S(2)}) collective-permute-start(bf16[256,2688]{1,0:T(8,128)(2,1)} %add_convert_fusion), channel_id=1, source_target_pairs={{0,2},{1,3},{2,0},{3,1},{4,5},{5,4},{6,7},{7,6},{8,10},{9,11},{10,... | collective-permute-start | bytes 4128776 | tf_op jit(solution)/shard_map/ppermute | solution.py:88
  280.3 19.8 %collective-permute-start.47 = (bf16[1,512,640]{2,1,0:T(8,128)(2,1)}, bf16[1,512,640]{2,1,0:T(8,128)(2,1)}, u32[]{:S(2)}, u32[]{:S(2)}) collective-permute-start(bf16[1,512,640]{2,1,0:T(8,128)(2,1)} %add_convert_fusion.6), channel_id=1, source_target_pairs={{0,1},{1,0},{2,3},{3,2},{4,6},{5,7},{6,4},{7,5},{8,9},{9,8},{10,11... | collective-permute-start | bytes 1966088 | tf_op jit(solution)/shard_map/ppermute | solution.py:88
  282.6 17.4 %collective-permute-start.52 = (bf16[112,2560]{1,0:T(8,128)(2,1)S(1)}, bf16[112,2560]{1,0:T(8,128)(2,1)S(1)}, u32[]{:S(2)}, u32[]{:S(2)}) collective-permute-start(bf16[112,2560]{1,0:T(8,128)(2,1)S(1)} %add_convert_fusion.15), channel_id=1, source_target_pairs={{0,8},{1,9},{2,10},{3,11},{4,12},{5,13},{6,14},{7,15},{24,16},{25,... | collective-permute-start | bytes 1720328 | tf_op jit(solution)/shard_map/ppermute | solution.py:88
  302.8 22.9 %collective-permute-start.59 = (bf16[112,2560]{1,0:T(8,128)(2,1)S(1)}, bf16[112,2560]{1,0:T(8,128)(2,1)S(1)}, u32[]{:S(2)}, u32[]{:S(2)}) collective-permute-start(bf16[112,2560]{1,0:T(8,128)(2,1)S(1)} %add_convert_fusion.14), channel_id=1, source_target_pairs={{8,16},{9,17},{10,18},{11,19},{12,20},{13,21},{14,22},{15,23},{16,... | collective-permute-start | bytes 1720328 | tf_op jit(solution)/shard_map/ppermute | solution.py:88
  305.3 11.0 %collective-permute-start.54 = (bf16[128,2688]{1,0:T(8,128)(2,1)S(1)}, bf16[128,2688]{1,0:T(8,128)(2,1)S(1)}, u32[]{:S(2)}, u32[]{:S(2)}) collective-permute-start(bf16[128,2688]{1,0:T(8,128)(2,1)S(1)} %add_convert_fusion.2), channel_id=1, source_target_pairs={{0,1},{1,0},{2,3},{3,2},{4,6},{5,7},{6,4},{7,5},{8,9},{9,8},{10,11... | collective-permute-start | bytes 2064392 | tf_op jit(solution)/shard_map/ppermute | solution.py:88
  307.8 30.7 %collective-permute-start.58 = (bf16[128,2560]{1,0:T(8,128)(2,1)S(1)}, bf16[128,2560]{1,0:T(8,128)(2,1)S(1)}, u32[]{:S(2)}, u32[]{:S(2)}) collective-permute-start(bf16[128,2560]{1,0:T(8,128)(2,1)S(1)} %add_convert_fusion.3), channel_id=1, source_target_pairs={{8,0},{9,1},{10,2},{11,3},{12,4},{13,5},{14,6},{15,7},{16,24},{17,... | collective-permute-start | bytes 1966088 | tf_op jit(solution)/shard_map/ppermute | solution.py:88
  310.5 27.9 %collective-permute-start.53 = (bf16[480,640]{1,0:T(8,128)(2,1)S(1)}, bf16[480,640]{1,0:T(8,128)(2,1)S(1)}, u32[]{:S(2)}, u32[]{:S(2)}) collective-permute-start(bf16[480,640]{1,0:T(8,128)(2,1)S(1)} %broadcast_select_fusion.3), channel_id=1, source_target_pairs={{0,4},{1,5},{2,6},{3,7},{4,0},{5,1},{6,2},{7,3},{8,12},{9,13},{10,... | collective-permute-start | bytes 1843208 | tf_op jit(solution)/shard_map/ppermute | solution.py:88
  318.4 22.6 %collective-permute-start.55 = (bf16[32,2688]{1,0:T(8,128)(2,1)S(1)}, bf16[32,2688]{1,0:T(8,128)(2,1)S(1)}, u32[]{:S(2)}, u32[]{:S(2)}) collective-permute-start(bf16[32,2688]{1,0:T(8,128)(2,1)S(1)} %get-tuple-element.566), channel_id=1, source_target_pairs={{0,8},{1,9},{2,10},{3,11},{4,12},{5,13},{6,14},{7,15},{8,0},{9,1},... | collective-permute-start | bytes 516104 | tf_op jit(solution)/shard_map/ppermute | solution.py:88
  325.7 15.3 %collective-permute-start.56 = (bf16[32,2688]{1,0:T(8,128)(2,1)S(1)}, bf16[32,2688]{1,0:T(8,128)(2,1)S(1)}, u32[]{:S(2)}, u32[]{:S(2)}) collective-permute-start(bf16[32,2688]{1,0:T(8,128)(2,1)S(1)} %get-tuple-element.565), channel_id=1, source_target_pairs={{0,16},{1,17},{2,18},{3,19},{4,20},{5,21},{6,22},{7,23},{8,24},{9,... | collective-permute-start | bytes 516104 | tf_op jit(solution)/shard_map/ppermute | solution.py:88
  325.7 15.3 %collective-permute-start.57 = (bf16[32,2688]{1,0:T(8,128)(2,1)S(1)}, bf16[32,2688]{1,0:T(8,128)(2,1)S(1)}, u32[]{:S(2)}, u32[]{:S(2)}) collective-permute-start(bf16[32,2688]{1,0:T(8,128)(2,1)S(1)} %get-tuple-element.564), channel_id=1, source_target_pairs={{0,24},{1,25},{2,26},{3,27},{4,28},{5,29},{6,30},{7,31},{8,16},{9,... | collective-permute-start | bytes 516104 | tf_op jit(solution)/shard_map/ppermute | solution.py:88
  341.1 8.9 %collective-permute-start.60 = (bf16[32,2688]{1,0:T(8,128)(2,1)S(1)}, bf16[32,2688]{1,0:T(8,128)(2,1)S(1)}, u32[]{:S(2)}, u32[]{:S(2)}) collective-permute-start(bf16[32,2688]{1,0:T(8,128)(2,1)S(1)} %add_convert_fusion.17), channel_id=1, source_target_pairs={{0,8},{1,9},{2,10},{3,11},{4,12},{5,13},{6,14},{7,15},{8,0},{9,1},... | collective-permute-start | bytes 516104 | tf_op jit(solution)/shard_map/ppermute | solution.py:88
  342.7 13.8 %collective-permute-start.61 = (bf16[32,2688]{1,0:T(8,128)(2,1)S(1)}, bf16[32,2688]{1,0:T(8,128)(2,1)S(1)}, u32[]{:S(2)}, u32[]{:S(2)}) collective-permute-start(bf16[32,2688]{1,0:T(8,128)(2,1)S(1)} %add_convert_fusion.17), channel_id=1, source_target_pairs={{0,16},{1,17},{2,18},{3,19},{4,20},{5,21},{6,22},{7,23},{8,24},{9,... | collective-permute-start | bytes 516104 | tf_op jit(solution)/shard_map/ppermute | solution.py:88
  342.9 13.5 %collective-permute-start.62 = (bf16[32,2688]{1,0:T(8,128)(2,1)S(1)}, bf16[32,2688]{1,0:T(8,128)(2,1)S(1)}, u32[]{:S(2)}, u32[]{:S(2)}) collective-permute-start(bf16[32,2688]{1,0:T(8,128)(2,1)S(1)} %add_convert_fusion.17), channel_id=1, source_target_pairs={{0,24},{1,25},{2,26},{3,27},{4,28},{5,29},{6,30},{7,31},{8,16},{9,... | collective-permute-start | bytes 516104 | tf_op jit(solution)/shard_map/ppermute | solution.py:88
  345.7 20.5 %collective-permute-start.65 = (bf16[112,2560]{1,0:T(8,128)(2,1)S(1)}, bf16[112,2560]{1,0:T(8,128)(2,1)S(1)}, u32[]{:S(2)}, u32[]{:S(2)}) collective-permute-start(bf16[112,2560]{1,0:T(8,128)(2,1)S(1)} %add_convert_fusion.13), channel_id=1, source_target_pairs={{8,0},{9,1},{10,2},{11,3},{12,4},{13,5},{14,6},{15,7},{16,24},{17,... | collective-permute-start | bytes 1720328 | tf_op jit(solution)/shard_map/ppermute | solution.py:88
  347.9 25.0 %collective-permute-start.64 = (bf16[128,2560]{1,0:T(8,128)(2,1)}, bf16[128,2560]{1,0:T(8,128)(2,1)}, u32[]{:S(2)}, u32[]{:S(2)}) collective-permute-start(bf16[128,2560]{1,0:T(8,128)(2,1)} %broadcast_select_fusion.refs_0_), channel_id=1, source_target_pairs={{0,4},{1,5},{2,6},{3,7},{4,0},{5,1},{6,2},{7,3},{8,12},{9,13},{10,... | collective-permute-start | bytes 1966088 | tf_op jit(solution)/shard_map/ppermute | solution.py:88
  356.8 12.4 %collective-permute-start.63 = (bf16[128,2688]{1,0:T(8,128)(2,1)S(1)}, bf16[128,2688]{1,0:T(8,128)(2,1)}, u32[]{:S(2)}, u32[]{:S(2)}) collective-permute-start(bf16[128,2688]{1,0:T(8,128)(2,1)S(1)} %bitcast.76), channel_id=1, source_target_pairs={{0,4},{1,5},{2,6},{3,7},{4,0},{5,1},{6,2},{7,3},{8,12},{9,13},{10,... | collective-permute-start | bytes 2064392 | tf_op jit(solution)/shard_map/ppermute | solution.py:88
  367.1 5.8 %collective-permute-start.66 = (bf16[112,2560]{1,0:T(8,128)(2,1)}, bf16[112,2560]{1,0:T(8,128)(2,1)}, u32[]{:S(2)}, u32[]{:S(2)}) collective-permute-start(bf16[112,2560]{1,0:T(8,128)(2,1)} %broadcast_select_fusion.5.refs_2_), channel_id=1, source_target_pairs={{0,4},{1,5},{2,6},{3,7},{4,0},{5,1},{6,2},{7,3},{8,12},{9,13},{10,... | collective-permute-start | bytes 1720328 | tf_op jit(solution)/shard_map/ppermute | solution.py:88
  (65 other events, 846.0 us)

commit v11 on v10

--- a/solution.py
+++ b/solution.py
@@ -20,7 +20,7 @@
 BF = jnp.bfloat16
 F32 = jnp.float32
 CLOSED = -1e30
-VMEM_LIMIT = 48 << 20
+VMEM_LIMIT = 32 << 20
 VMEM_MOST = 60 << 20
 
 

time: 386 us -> 384 us (level)
  Pallas kernels: 145 us -> 138 us
  waiting for transfers between devices: 97.1 us -> 102 us
    ppermute x67, waiting for transfers between devices: 97.1 us -> 102 us  [move(): return lax.ppermute(value, AXES, pairs)]
    unnamed x127 -> x163, local copies, waits for them, and re-layouts: 11.2 us -> 12.8 us
  transfers between devices with their start and end apart: 67 -> 67, of which waited for: 19 -> 21; matrix products, arithmetic and copies ran while one was open for 12% -> 10% of each run, Pallas kernels for 35% -> 34%
where the time goes in v11:
time: 384 us; the launch traced here: 377 us
  Pallas kernels  138 us (36%)
  waiting for transfers between devices  102 us (27%)
  starting transfers between devices  73.9 us (19%)
  other arithmetic  34.5 us (9%)
  local copies, waits for them, and re-layouts  26 us (7%)
    ppermute x67, waiting for transfers between devices, move(): return lax.ppermute(value, AXES, pairs)  102 us
    ppermute x67, starting transfers between devices, move(): return lax.ppermute(value, AXES, pairs)  73.9 us
    pallas_call x2, Pallas kernels, attend_back(): pl.pallas_call(functools.partial(attend_back_kernel, shards, seg_rows), g...  31.7 us
    pallas_call x1, Pallas kernels, feed(): pl.pallas_call(functools.partial(feed_kernel, counts), name='feed', in_sp...  27.4 us
    convert_element_type x17, other arithmetic, total(): return sum((part.astype(F32) for part in parts)).astype(parts[0].dtype)  16.9 us
    pallas_call x1, Pallas kernels, attend(): pl.pallas_call(functools.partial(attend_kernel, shards, seg_rows), grid=(...  16.8 us
    pallas_call x1, Pallas kernels, feed_back(): pl.pallas_call(functools.partial(feed_back_kernel, counts), name='feed_ba...  15 us
    pallas_call x1, Pallas kernels, attention_grad(): pl.pallas_call(functools.partial(attention_grad_kernel, shards, half), na...  13.3 us
  transfers between devices with their start and end apart: 67, of which 21 were waited for; matrix products, arithmetic and copies ran while one was open for 10% of the time, Pallas kernels for 34%

profile of v11, /device:TPU:0, one launch (start us, length us, event | category | flops | bytes accessed | tf_op | source)
XLA Modules:
  0.0 377.1 jit_solution(14705672344168061690)
XLA Ops:
  2.9 2.4 broadcast_select_fusion.4
  5.2 2.9 collective-permute-start
  8.2 1.5 collective-permute-start.1
  10.4 2.9 collective-permute-start.4
  13.9 1.7 fusion.1
  16.5 2.0 dynamic-slice_select_fusion
  18.6 1.8 multiply_sine_fusion
  20.4 2.0 dynamic-slice_bitcast_fusion
  25.2 2.0 collective-permute-start.8
  27.4 11.7 %collective-permute-done.5.refs_6_ = bf16[240,1280]{1,0:T(8,128)(2,1)} collective-permute-done((bf16[240,1280]{1,0:T(8,128)(2,1)S(1)}, bf16[240,1280]{1,0:T(8,128)(2,1)}, u32[]{:S(2)}, u32[]{:S(2)}) %collective-permute-start.5) | collective-permute-done | bytes 614432 | tf_op jit(solution)/shard_map/ppermute | solution.py:88
  39.5 2.2 tile.20
  44.2 2.4 collective-permute-start.11
  46.6 1.6 collective-permute-start.12
  48.3 1.6 copy.62.cos_ref
  49.8 1.9 copy.63.sin_ref
  51.8 1.4 copy-done.12
  56.6 5.0 %project.1 = (bf16[512,960]{1,0:T(8,128)(2,1)S(1)}, bf16[512,640]{1,0:T(8,128)(2,1)S(1)}) custom-call(s32[16]{0:T(128)S(1)} %stack.194.starts_ref.s0_ref, bf16[2,960,256]{2,1,0:T(8,128)(2,1)S(1)} %bitcast.78, f32[2,960]{1,0:T(2,128)S(1)} %maximum_convert_fusion.gains_ref, f32[2048,128]{1,0:T(8,128)S(1)} %copy.62.cos_ref, f32[2048,128]{1,0:T(8,128)S(1)} %copy.63.sin_ref, ...), custom_call_target="tpu_custom_call" | custom-call | flops 1572864000 | bytes 7536640 | tf_op jit(solution)/shard_map/project/pallas_call | solution.py:344
  63.2 1.8 collective-permute-start.15
  64.9 13.9 %collective-permute-done.15.refs_15_ = bf16[240,1280]{1,0:T(8,128)(2,1)S(1)} collective-permute-done((bf16[240,1280]{1,0:T(8,128)(2,1)}, bf16[240,1280]{1,0:T(8,128)(2,1)S(1)}, u32[]{:S(2)}, u32[]{:S(2)}) %collective-permute-start.15) | collective-permute-done | bytes 614432 | tf_op jit(solution)/shard_map/ppermute | solution.py:88
  81.6 7.8 %collective-permute-done.17.refs_18_ = bf16[240,1280]{1,0:T(8,128)(2,1)S(1)} collective-permute-done((bf16[240,1280]{1,0:T(8,128)(2,1)}, bf16[240,1280]{1,0:T(8,128)(2,1)S(1)}, u32[]{:S(2)}, u32[]{:S(2)}) %collective-permute-start.17) | collective-permute-done | bytes 614432 | tf_op jit(solution)/shard_map/ppermute | solution.py:88
  89.4 2.0 collective-permute-done.21.refs_17_
  91.4 5.0 %collective-permute-done.16.refs_3_ = bf16[512,640]{1,0:T(8,128)(2,1)S(1)} collective-permute-done((bf16[512,640]{1,0:T(8,128)(2,1)S(1)}, bf16[512,640]{1,0:T(8,128)(2,1)S(1)}, u32[]{:S(2)}, u32[]{:S(2)}) %collective-permute-start.16) | collective-permute-done | bytes 655392 | tf_op jit(solution)/shard_map/ppermute | solution.py:88
  99.7 16.8 %attend.1 = (bf16[512,960]{1,0:T(8,128)(2,1)S(1)}, f32[512,128]{1,0:T(8,128)S(1)}) custom-call(bf16[512,960]{1,0:T(8,128)(2,1)S(1)} %get-tuple-element.480.q_ref, bf16[512,640]{1,0:T(8,128)(2,1)S(1)} %get-tuple-element.481.refs_0_, bf16[512,640]{1,0:T(8,128)(2,1)S(1)} %collective-permute-done.13.refs_1_, ...), custom_call_target="tpu_custom_call" | custom-call | flops 8053063680 | bytes 983040 | tf_op jit(solution)/shard_map/attend/pallas_call | solution.py:909
  119.4 1.7 collective-permute-start.31
  123.9 27.4 %feed.1 = (bf16[2,960,256]{2,1,0:T(8,128)(2,1)}, bf16[512,2560]{1,0:T(8,128)(2,1)}, bf16[512,2560]{1,0:T(8,128)(2,1)}, bf16[512,2560]{1,0:T(8,128)(2,1)}, bf16[9...) custom-call(s32[1]{0:T(128)} %bitcast.core_ref, s32[16]{0:T(128)} %copy-done.38, ...), custom_call_target="tpu_custom_call" | custom-call | flops 11010048000 | bytes 35389440 | tf_op jit(solution)/shard_map/feed/pallas_call | solution.py:426
  155.5 15.0 %feed_back.1 = (f32[960,512]{1,0:T(8,128)}, bf16[512,1024]{1,0:T(8,128)(2,1)}, bf16[512,960]{1,0:T(8,128)(2,1)}) custom-call(s32[1]{0:T(128)} %bitcast.core_ref, s32[16]{0:T(128)} %copy-done.38, s32[28]{0:T(128)} %stack.197.s1_ref, f32[960,512]{1,0:T(8,128)} %get-tuple-element.383.resid_ref, bf16[2,960,256]{2,1,0:T(8,128)(2,1)} %bitcast.85, ...), custom_call_target="tpu_custom_call" | custom-call | flops 5976883200 | bytes 26935296 | tf_op jit(solution)/shard_map/feed_back/pallas_call | solution.py:485
  171.8 5.2 %down_grad.1 = (bf16[960,640]{1,0:T(8,128)(2,1)S(1)}, bf16[960,640]{1,0:T(8,128)(2,1)S(1)}) custom-call(s32[5]{0:T(128)S(1)} %stack.214.info_ref, bf16[2,960,256]{2,1,0:T(8,128)(2,1)S(1)} %bitcast.87, bf16[2,960,256]{2,1,0:T(8,128)(2,1)S(1)} %copy-done.46, bf16[512,2560]{1,0:T(8,128)(2,1)S(1)} %copy-done.40, ...), custom_call_target="tpu_custom_call" | custom-call | flops 2516582400 | bytes 9666560 | tf_op jit(solution)/shard_map/down_grad/pallas_call | solution.py:530
  178.0 9.2 %wide_grad.1 = (bf16[256,2560]{1,0:T(8,128)(2,1)S(1)}, bf16[256,2560]{1,0:T(8,128)(2,1)S(1)}, bf16[224,2560]{1,0:T(8,128)(2,1)S(1)}, bf16[224,2560]{1,0:T(8,128)(2,1)S(1)}) custom-call(s32[4]{0:T(128)S(1)} %pad_add_fusion.1.starts_ref, bf16[960,512]{1,0:T(8,128)(2,1)S(1)} %copy-done.44, bf16[960,512]{1,0:T(8,128)(2,1)} %collective-permute-done.33.far_left_ref, ...), custom_call_target="tpu_custom_call" | custom-call | flops 5033164800 | bytes 12124160 | tf_op jit(solution)/shard_map/wide_grad/pallas_call | solution.py:579
  187.2 6.6 %collective-permute-done.37 = bf16[960,640]{1,0:T(8,128)(2,1)S(1)} collective-permute-done((bf16[960,640]{1,0:T(8,128)(2,1)S(1)}, bf16[960,640]{1,0:T(8,128)(2,1)S(1)}, u32[]{:S(2)}, u32[]{:S(2)}) %collective-permute-start.37) | collective-permute-done | bytes 1228832 | tf_op jit(solution)/shard_map/ppermute | solution.py:88
  195.8 15.8 %attend_back.2 = (bf16[512,1024]{1,0:T(8,128)(2,1)S(1)}, bf16[2,512,640]{2,1,0:T(8,128)(2,1)S(1)}, bf16[2,512,640]{2,1,0:T(8,128)(2,1)}) custom-call(bf16[512,960]{1,0:T(8,128)(2,1)S(1)} %copy-done.42, bf16[512,640]{1,0:T(8,128)(2,1)S(1)} %copy-done.48, bf16[512,640]{1,0:T(8,128)(2,1)S(1)} %copy-done.50, bf16[512,640]{1,0:T(8,128)(2,1)S(1)} %copy-done.52, ...), custom_call_target="tpu_custom_call" | custom-call | flops 10066329600 | bytes 983040 | tf_op jit(solution)/shard_map/attend_back/pallas_call | solution.py:931
  211.6 5.2 %collective-permute-done.39 = bf16[256,2560]{1,0:T(8,128)(2,1)S(1)} collective-permute-done((bf16[256,2560]{1,0:T(8,128)(2,1)S(1)}, bf16[256,2560]{1,0:T(8,128)(2,1)S(1)}, u32[]{:S(2)}, u32[]{:S(2)}) %collective-permute-start.39) | collective-permute-done | bytes 1310752 | tf_op jit(solution)/shard_map/ppermute | solution.py:88
  219.2 2.5 collective-permute-start.40
  221.7 15.8 %attend_back.3 = (bf16[512,1024]{1,0:T(8,128)(2,1)S(1)}, bf16[2,512,640]{2,1,0:T(8,128)(2,1)S(1)}, bf16[2,512,640]{2,1,0:T(8,128)(2,1)}) custom-call(bf16[512,960]{1,0:T(8,128)(2,1)S(1)} %copy-done.42, bf16[512,640]{1,0:T(8,128)(2,1)S(1)} %copy-done.48, ...), custom_call_target="tpu_custom_call", output_to_operand_aliasing={{0}: (11, {}), {1}: (12, {}), {2}: (13, {})} | custom-call | flops 10066329600 | bytes 983040 | tf_op jit(solution)/shard_map/attend_back/pallas_call | solution.py:931
  238.2 1.4 add_convert_fusion.7
  239.6 3.0 collective-permute-start.45
  248.3 13.3 %attention_grad.1 = (bf16[512,2688]{1,0:T(8,128)(2,1)}, bf16[512,2688]{1,0:T(8,128)(2,1)}) custom-call(s32[8]{0:T(128)} %stack.227.starts_ref, f32[960,1]{1,0:T(8,128)} %copy.65.gain_ref, f32[2048,128]{1,0:T(8,128)} %copy-done.4, f32[2048,128]{1,0:T(8,128)} %copy-done.6, bf16[512,1024]{1,0:T(8,128)(2,1)} %copy-done.29, ...), custom_call_target="tpu_custom_call" | custom-call | flops 4697620480 | bytes 12058624 | tf_op jit(solution)/shard_map/attention_grad/pallas_call | solution.py:735
  261.6 5.1 %collective-permute-done.43 = bf16[2,512,640]{2,1,0:T(8,128)(2,1)} collective-permute-done((bf16[2,512,640]{2,1,0:T(8,128)(2,1)}, bf16[2,512,640]{2,1,0:T(8,128)(2,1)}, u32[]{:S(2)}, u32[]{:S(2)}) %collective-permute-start.43) | collective-permute-done | bytes 1310752 | tf_op jit(solution)/shard_map/ppermute | solution.py:88
  266.7 1.6 add_convert_fusion.5
  268.3 1.5 collective-permute-start.51
  270.8 1.4 collective-permute-start.48
  272.2 1.7 add_convert_fusion
  275.2 2.1 add_convert_fusion.6
  279.5 5.4 %collective-permute-start.52 = (bf16[112,2560]{1,0:T(8,128)(2,1)}, bf16[112,2560]{1,0:T(8,128)(2,1)S(1)}, u32[]{:S(2)}, u32[]{:S(2)}) collective-permute-start(bf16[112,2560]{1,0:T(8,128)(2,1)} %add_convert_fusion.15), channel_id=1, source_target_pairs={{0,8},{1,9},{2,10},{3,11},{4,12},{5,13},{6,14},{7,15},{24,16},{25,... | collective-permute-start | bytes 1720328 | tf_op jit(solution)/shard_map/ppermute | solution.py:88
  285.0 12.3 %collective-permute-done.52 = bf16[112,2560]{1,0:T(8,128)(2,1)S(1)} collective-permute-done((bf16[112,2560]{1,0:T(8,128)(2,1)}, bf16[112,2560]{1,0:T(8,128)(2,1)S(1)}, u32[]{:S(2)}, u32[]{:S(2)}) %collective-permute-start.52) | collective-permute-done | bytes 573472 | tf_op jit(solution)/shard_map/ppermute | solution.py:88
  297.3 2.6 collective-permute-done.50
  301.7 1.8 add_convert_fusion.2
  304.6 1.3 add_convert_fusion.3
  305.9 1.5 collective-permute-start.58
  308.8 5.7 %collective-permute-done.54 = bf16[128,2688]{1,0:T(8,128)(2,1)S(1)} collective-permute-done((bf16[128,2688]{1,0:T(8,128)(2,1)S(1)}, bf16[128,2688]{1,0:T(8,128)(2,1)S(1)}, u32[]{:S(2)}, u32[]{:S(2)}) %collective-permute-start.54) | collective-permute-done | bytes 688160 | tf_op jit(solution)/shard_map/ppermute | solution.py:88
  314.5 2.0 add_convert_fusion.1
  316.6 7.5 %collective-permute-start.55 = (bf16[32,2688]{1,0:T(8,128)(2,1)S(1)}, bf16[32,2688]{1,0:T(8,128)(2,1)S(1)}, u32[]{:S(2)}, u32[]{:S(2)}) collective-permute-start(bf16[32,2688]{1,0:T(8,128)(2,1)S(1)} %get-tuple-element.566), channel_id=1, source_target_pairs={{0,8},{1,9},{2,10},{3,11},{4,12},{5,13},{6,14},{7,15},{8,0},{9,1},... | collective-permute-start | bytes 516104 | tf_op jit(solution)/shard_map/ppermute | solution.py:88
  324.1 2.5 collective-permute-start.57
  326.6 1.5 fusion.kv_ref
  328.3 6.9 %finish.1 = bf16[2,960,256]{2,1,0:T(8,128)(2,1)} custom-call(s32[16]{0:T(128)S(1)} %copy-done.39, bf16[2,960,256]{2,1,0:T(8,128)(2,1)S(1)} %bitcast.81, bf16[512,1024]{1,0:T(8,128)(2,1)S(1)} %copy-done.30, bf16[512,640]{1,0:T(8,128)(2,1)S(1)} %fusion.kv_ref, f32[960,512]{1,0:T(8,128)S(1)} %copy-done.24, f32[960,1]{1,0:T(8,128)S(1)} %copy-done.26, ...), custom_call_target="tpu_custom_call" | custom-call | flops 1572864000 | bytes 8912896 | tf_op jit(solution)/shard_map/finish/pallas_call | solution.py:781
  335.2 1.4 collective-permute-done.58
  336.6 2.6 collective-permute-done.55
  339.3 1.8 collective-permute-start.60
  341.2 2.6 collective-permute-start.62
  346.1 1.6 collective-permute-done.60
  347.7 7.2 %collective-permute-done.61 = bf16[32,2688]{1,0:T(8,128)(2,1)S(1)} collective-permute-done((bf16[32,2688]{1,0:T(8,128)(2,1)S(1)}, bf16[32,2688]{1,0:T(8,128)(2,1)S(1)}, u32[]{:S(2)}, u32[]{:S(2)}) %collective-permute-start.61) | collective-permute-done | bytes 172064 | tf_op jit(solution)/shard_map/ppermute | solution.py:88
  355.3 9.1 %collective-permute-done.65 = bf16[112,2560]{1,0:T(8,128)(2,1)S(1)} collective-permute-done((bf16[112,2560]{1,0:T(8,128)(2,1)S(1)}, bf16[112,2560]{1,0:T(8,128)(2,1)S(1)}, u32[]{:S(2)}, u32[]{:S(2)}) %collective-permute-start.65) | collective-permute-done | bytes 573472 | tf_op jit(solution)/shard_map/ppermute | solution.py:88
  365.8 1.6 convert_bitcast_fusion
  367.4 3.0 settle_some.1
  371.1 4.9 %settle.1 = (f32[240,2560]{1,0:T(8,128)}, f32[240,2560]{1,0:T(8,128)}, f32[240,1]{1,0:T(8,128)S(1)}) custom-call(s32[1]{0:T(128)} %bitcast.core_ref, f32[240,1]{1,0:T(8,128)S(1)} %copy.72.gain_ref, bf16[128,2560]{1,0:T(8,128)(2,1)} %broadcast_select_fusion.refs_0_, bf16[128,2560]{1,0:T(8,128)(2,1)} %collective-permute-done.64.refs_1_, ...), custom_call_target="tpu_custom_call" | custom-call | flops 2457600 | bytes 7372800 | tf_op jit(solution)/shard_map/settle/pallas_call | solution.py:620
  (324 shorter events, 58.0 us)
Async XLA Ops:
  5.2 18.3 %collective-permute-start = (bf16[240,1280]{1,0:T(8,128)(2,1)}, bf16[240,1280]{1,0:T(8,128)(2,1)S(1)}, u32[]{:S(2)}, u32[]{:S(2)}) collective-permute-start(bf16[240,1280]{1,0:T(8,128)(2,1)} %get-tuple-element.559), channel_id=1, source_target_pairs={{0,1},{1,0},{2,3},{3,2},{4,6},{5,7},{6,4},{7,5},{8,9},{9,8},{10,11... | collective-permute-start | bytes 1843208 | tf_op jit(solution)/shard_map/ppermute | solution.py:88
  8.2 15.4 %collective-permute-start.1 = (bf16[240,1280]{1,0:T(8,128)(2,1)}, bf16[240,1280]{1,0:T(8,128)(2,1)}, u32[]{:S(2)}, u32[]{:S(2)}) collective-permute-start(bf16[240,1280]{1,0:T(8,128)(2,1)} %get-tuple-element.559), channel_id=1, source_target_pairs={{0,2},{1,3},{2,0},{3,1},{4,5},{5,4},{6,7},{7,6},{8,10},{9,11},{10,... | collective-permute-start | bytes 1843208 | tf_op jit(solution)/shard_map/ppermute | solution.py:88
  9.7 12.9 %collective-permute-start.2 = (bf16[2,240]{1,0:T(2,128)(2,1)S(1)}, bf16[2,240]{1,0:T(2,128)(2,1)S(1)}, u32[]{:S(2)}, u32[]{:S(2)}) collective-permute-start(bf16[2,240]{1,0:T(2,128)(2,1)S(1)} %pad_maximum_fusion.5), channel_id=1, source_target_pairs={{0,1},{1,0},{2,3},{3,2},{4,5},{5,4},{6,7},{7,6},{8,9},{9,8},{10,11... | collective-permute-start | bytes 2888 | tf_op jit(solution)/shard_map/ppermute | solution.py:88
  10.3 12.3 %collective-permute-start.3 = (bf16[2,240]{1,0:T(2,128)(2,1)S(1)}, bf16[2,240]{1,0:T(2,128)(2,1)S(1)}, u32[]{:S(2)}, u32[]{:S(2)}) collective-permute-start(bf16[2,240]{1,0:T(2,128)(2,1)S(1)} %pad_maximum_fusion.5), channel_id=1, source_target_pairs={{0,2},{1,3},{2,0},{3,1},{4,6},{5,7},{6,4},{7,5},{8,10},{9,11},{10,... | collective-permute-start | bytes 2888 | tf_op jit(solution)/shard_map/ppermute | solution.py:88
  10.4 13.2 %collective-permute-start.4 = (bf16[2,240]{1,0:T(2,128)(2,1)S(1)}, bf16[2,240]{1,0:T(2,128)(2,1)S(1)}, u32[]{:S(2)}, u32[]{:S(2)}) collective-permute-start(bf16[2,240]{1,0:T(2,128)(2,1)S(1)} %pad_maximum_fusion.5), channel_id=1, source_target_pairs={{0,3},{1,2},{2,1},{3,0},{4,7},{5,6},{6,5},{7,4},{8,11},{9,10},{10,... | collective-permute-start | bytes 2888 | tf_op jit(solution)/shard_map/ppermute | solution.py:88
  23.6 15.6 %collective-permute-start.5 = (bf16[240,1280]{1,0:T(8,128)(2,1)S(1)}, bf16[240,1280]{1,0:T(8,128)(2,1)}, u32[]{:S(2)}, u32[]{:S(2)}) collective-permute-start(bf16[240,1280]{1,0:T(8,128)(2,1)S(1)} %collective-permute-done.refs_2_), channel_id=1, source_target_pairs={{0,2},{1,3},{2,0},{3,1},{4,5},{5,4},{6,7},{7,6},{8,10},{9,11},{10,... | collective-permute-start | bytes 1843208 | tf_op jit(solution)/shard_map/ppermute | solution.py:88
  24.2 14.9 %collective-permute-start.6 = (bf16[240,1280]{1,0:T(8,128)(2,1)S(1)}, bf16[240,1280]{1,0:T(8,128)(2,1)S(1)}, u32[]{:S(2)}, u32[]{:S(2)}) collective-permute-start(bf16[240,1280]{1,0:T(8,128)(2,1)S(1)} %collective-permute-done.refs_2_), channel_id=1, source_target_pairs={{0,4},{1,5},{2,6},{3,7},{4,0},{5,1},{6,2},{7,3},{8,12},{9,13},{10,... | collective-permute-start | bytes 1843208 | tf_op jit(solution)/shard_map/ppermute | solution.py:88
  25.1 14.0 %collective-permute-start.7 = (bf16[240,1280]{1,0:T(8,128)(2,1)}, bf16[240,1280]{1,0:T(8,128)(2,1)S(1)}, u32[]{:S(2)}, u32[]{:S(2)}) collective-permute-start(bf16[240,1280]{1,0:T(8,128)(2,1)} %collective-permute-done.1.refs_4_), channel_id=1, source_target_pairs={{0,4},{1,5},{2,6},{3,7},{4,0},{5,1},{6,2},{7,3},{8,12},{9,13},{10,... | collective-permute-start | bytes 1843208 | tf_op jit(solution)/shard_map/ppermute | solution.py:88
  25.2 14.3 %collective-permute-start.8 = (bf16[240,1280]{1,0:T(8,128)(2,1)}, bf16[240,1280]{1,0:T(8,128)(2,1)}, u32[]{:S(2)}, u32[]{:S(2)}) collective-permute-start(bf16[240,1280]{1,0:T(8,128)(2,1)} %dynamic-slice_select_fusion), channel_id=1, source_target_pairs={{0,1},{1,0},{2,3},{3,2},{4,6},{5,7},{6,4},{7,5},{8,9},{9,8},{10,11... | collective-permute-start | bytes 1843208 | tf_op jit(solution)/shard_map/ppermute | solution.py:88
  42.8 9.0 %collective-permute-start.9 = (bf16[240,1280]{1,0:T(8,128)(2,1)}, bf16[240,1280]{1,0:T(8,128)(2,1)}, u32[]{:S(2)}, u32[]{:S(2)}) collective-permute-start(bf16[240,1280]{1,0:T(8,128)(2,1)} %collective-permute-done.5.refs_6_), channel_id=1, source_target_pairs={{0,4},{1,5},{2,6},{3,7},{4,0},{5,1},{6,2},{7,3},{8,12},{9,13},{10,... | collective-permute-start | bytes 1843208 | tf_op jit(solution)/shard_map/ppermute | solution.py:88
  43.5 18.1 %collective-permute-start.10 = (bf16[240,1280]{1,0:T(8,128)(2,1)}, bf16[240,1280]{1,0:T(8,128)(2,1)}, u32[]{:S(2)}, u32[]{:S(2)}) collective-permute-start(bf16[240,1280]{1,0:T(8,128)(2,1)} %dynamic-slice_select_fusion), channel_id=1, source_target_pairs={{0,2},{1,3},{2,0},{3,1},{4,5},{5,4},{6,7},{7,6},{8,10},{9,11},{10,... | collective-permute-start | bytes 1843208 | tf_op jit(solution)/shard_map/ppermute | solution.py:88
  44.2 17.4 %collective-permute-start.11 = (bf16[240,1280]{1,0:T(8,128)(2,1)}, bf16[240,1280]{1,0:T(8,128)(2,1)}, u32[]{:S(2)}, u32[]{:S(2)}) collective-permute-start(bf16[240,1280]{1,0:T(8,128)(2,1)} %collective-permute-done.8.refs_10_), channel_id=1, source_target_pairs={{0,8},{1,9},{2,10},{3,11},{4,12},{5,13},{6,14},{7,15},{8,0},{9,1},... | collective-permute-start | bytes 1843208 | tf_op jit(solution)/shard_map/ppermute | solution.py:88
  46.6 15.0 %collective-permute-start.12 = (bf16[480,640]{1,0:T(8,128)(2,1)}, bf16[480,640]{1,0:T(8,128)(2,1)}, u32[]{:S(2)}, u32[]{:S(2)}) collective-permute-start(bf16[480,640]{1,0:T(8,128)(2,1)} %dynamic-slice_bitcast_fusion), channel_id=1, source_target_pairs={{0,1},{1,0},{2,3},{3,2},{4,6},{5,7},{6,4},{7,5},{8,9},{9,8},{10,11... | collective-permute-start | bytes 1843208 | tf_op jit(solution)/shard_map/ppermute | solution.py:88
  61.7 17.3 %collective-permute-start.13 = (bf16[512,640]{1,0:T(8,128)(2,1)S(1)}, bf16[512,640]{1,0:T(8,128)(2,1)S(1)}, u32[]{:S(2)}, u32[]{:S(2)}) collective-permute-start(bf16[512,640]{1,0:T(8,128)(2,1)S(1)} %get-tuple-element.481.refs_0_), channel_id=1, source_target_pairs={{0,1},{1,0},{2,3},{3,2},{4,6},{5,7},{6,4},{7,5},{8,9},{9,8},{10,11... | collective-permute-start | bytes 1966088 | tf_op jit(solution)/shard_map/ppermute | solution.py:88
  62.2 16.8 %collective-permute-start.14 = (bf16[512,640]{1,0:T(8,128)(2,1)S(1)}, bf16[512,640]{1,0:T(8,128)(2,1)S(1)}, u32[]{:S(2)}, u32[]{:S(2)}) collective-permute-start(bf16[512,640]{1,0:T(8,128)(2,1)S(1)} %get-tuple-element.481.refs_0_), channel_id=1, source_target_pairs={{0,2},{1,3},{2,0},{3,1},{4,5},{5,4},{6,7},{7,6},{8,10},{9,11},{10,... | collective-permute-start | bytes 1966088 | tf_op jit(solution)/shard_map/ppermute | solution.py:88
  63.2 15.7 %collective-permute-start.15 = (bf16[240,1280]{1,0:T(8,128)(2,1)}, bf16[240,1280]{1,0:T(8,128)(2,1)S(1)}, u32[]{:S(2)}, u32[]{:S(2)}) collective-permute-start(bf16[240,1280]{1,0:T(8,128)(2,1)} %collective-permute-done.10.refs_14_), channel_id=1, source_target_pairs={{0,8},{1,9},{2,10},{3,11},{4,12},{5,13},{6,14},{7,15},{8,0},{9,1},... | collective-permute-start | bytes 1843208 | tf_op jit(solution)/shard_map/ppermute | solution.py:88
  79.0 10.4 %collective-permute-start.17 = (bf16[240,1280]{1,0:T(8,128)(2,1)}, bf16[240,1280]{1,0:T(8,128)(2,1)S(1)}, u32[]{:S(2)}, u32[]{:S(2)}) collective-permute-start(bf16[240,1280]{1,0:T(8,128)(2,1)} %collective-permute-done.8.refs_10_), channel_id=1, source_target_pairs={{0,2},{1,3},{2,0},{3,1},{4,5},{5,4},{6,7},{7,6},{8,10},{9,11},{10,... | collective-permute-start | bytes 1843208 | tf_op jit(solution)/shard_map/ppermute | solution.py:88
  79.8 16.6 %collective-permute-start.16 = (bf16[512,640]{1,0:T(8,128)(2,1)S(1)}, bf16[512,640]{1,0:T(8,128)(2,1)S(1)}, u32[]{:S(2)}, u32[]{:S(2)}) collective-permute-start(bf16[512,640]{1,0:T(8,128)(2,1)S(1)} %collective-permute-done.13.refs_1_), channel_id=1, source_target_pairs={{0,2},{1,3},{2,0},{3,1},{4,5},{5,4},{6,7},{7,6},{8,10},{9,11},{10,... | collective-permute-start | bytes 1966088 | tf_op jit(solution)/shard_map/ppermute | solution.py:88
  81.1 8.3 %collective-permute-start.18 = (bf16[240,1280]{1,0:T(8,128)(2,1)}, bf16[240,1280]{1,0:T(8,128)(2,1)S(1)}, u32[]{:S(2)}, u32[]{:S(2)}) collective-permute-start(bf16[240,1280]{1,0:T(8,128)(2,1)} %collective-permute-done.8.refs_10_), channel_id=1, source_target_pairs={{0,4},{1,5},{2,6},{3,7},{4,0},{5,1},{6,2},{7,3},{8,12},{9,13},{10,... | collective-permute-start | bytes 1843208 | tf_op jit(solution)/shard_map/ppermute | solution.py:88
  81.1 8.4 %collective-permute-start.19 = (bf16[240,1280]{1,0:T(8,128)(2,1)}, bf16[240,1280]{1,0:T(8,128)(2,1)S(1)}, u32[]{:S(2)}, u32[]{:S(2)}) collective-permute-start(bf16[240,1280]{1,0:T(8,128)(2,1)} %collective-permute-done.10.refs_14_), channel_id=1, source_target_pairs={{0,4},{1,5},{2,6},{3,7},{4,0},{5,1},{6,2},{7,3},{8,12},{9,13},{10,... | collective-permute-start | bytes 1843208 | tf_op jit(solution)/shard_map/ppermute | solution.py:88
  81.6 7.9 %collective-permute-start.20 = (bf16[240,1280]{1,0:T(8,128)(2,1)}, bf16[240,1280]{1,0:T(8,128)(2,1)S(1)}, u32[]{:S(2)}, u32[]{:S(2)}) collective-permute-start(bf16[240,1280]{1,0:T(8,128)(2,1)} %collective-permute-done.11.refs_11_), channel_id=1, source_target_pairs={{0,4},{1,5},{2,6},{3,7},{4,0},{5,1},{6,2},{7,3},{8,12},{9,13},{10,... | collective-permute-start | bytes 1843208 | tf_op jit(solution)/shard_map/ppermute | solution.py:88
  96.4 21.8 %collective-permute-start.24 = (bf16[240,1280]{1,0:T(8,128)(2,1)S(1)}, bf16[240,1280]{1,0:T(8,128)(2,1)}, u32[]{:S(2)}, u32[]{:S(2)}) collective-permute-start(bf16[240,1280]{1,0:T(8,128)(2,1)S(1)} %collective-permute-done.17.refs_18_), channel_id=1, source_target_pairs={{0,8},{1,9},{2,10},{3,11},{4,12},{5,13},{6,14},{7,15},{8,0},{9,1},... | collective-permute-start | bytes 1843208 | tf_op jit(solution)/shard_map/ppermute | solution.py:88
  97.6 20.6 %collective-permute-start.25 = (bf16[240,1280]{1,0:T(8,128)(2,1)S(1)}, bf16[240,1280]{1,0:T(8,128)(2,1)S(1)}, u32[]{:S(2)}, u32[]{:S(2)}) collective-permute-start(bf16[240,1280]{1,0:T(8,128)(2,1)S(1)} %collective-permute-done.17.refs_18_), channel_id=1, source_target_pairs={{0,4},{1,5},{2,6},{3,7},{4,0},{5,1},{6,2},{7,3},{8,12},{9,13},{10,... | collective-permute-start | bytes 1843208 | tf_op jit(solution)/shard_map/ppermute | solution.py:88
  97.7 20.6 %collective-permute-start.22 = (bf16[480,640]{1,0:T(8,128)(2,1)}, bf16[480,640]{1,0:T(8,128)(2,1)}, u32[]{:S(2)}, u32[]{:S(2)}) collective-permute-start(bf16[480,640]{1,0:T(8,128)(2,1)} %dynamic-slice_bitcast_fusion), channel_id=1, source_target_pairs={{0,2},{1,3},{2,0},{3,1},{4,5},{5,4},{6,7},{7,6},{8,10},{9,11},{10,... | collective-permute-start | bytes 1843208 | tf_op jit(solution)/shard_map/ppermute | solution.py:88
  98.7 19.6 %collective-permute-start.23 = (bf16[480,640]{1,0:T(8,128)(2,1)}, bf16[480,640]{1,0:T(8,128)(2,1)}, u32[]{:S(2)}, u32[]{:S(2)}) collective-permute-start(bf16[480,640]{1,0:T(8,128)(2,1)} %collective-permute-done.12.refs_23_), channel_id=1, source_target_pairs={{0,2},{1,3},{2,0},{3,1},{4,5},{5,4},{6,7},{7,6},{8,10},{9,11},{10,... | collective-permute-start | bytes 1843208 | tf_op jit(solution)/shard_map/ppermute | solution.py:88
  118.8 5.1 %collective-permute-start.28 = (bf16[480,640]{1,0:T(8,128)(2,1)}, bf16[480,640]{1,0:T(8,128)(2,1)}, u32[]{:S(2)}, u32[]{:S(2)}) collective-permute-start(bf16[480,640]{1,0:T(8,128)(2,1)} %collective-permute-done.22.refs_25_), channel_id=1, source_target_pairs={{0,4},{1,5},{2,6},{3,7},{4,0},{5,1},{6,2},{7,3},{8,12},{9,13},{10,... | collective-permute-start | bytes 1843208 | tf_op jit(solution)/shard_map/ppermute | solution.py:88
  119.1 4.8 %collective-permute-start.29 = (bf16[480,640]{1,0:T(8,128)(2,1)}, bf16[480,640]{1,0:T(8,128)(2,1)}, u32[]{:S(2)}, u32[]{:S(2)}) collective-permute-start(bf16[480,640]{1,0:T(8,128)(2,1)} %collective-permute-done.23.refs_27_), channel_id=1, source_target_pairs={{0,4},{1,5},{2,6},{3,7},{4,0},{5,1},{6,2},{7,3},{8,12},{9,13},{10,... | collective-permute-start | bytes 1843208 | tf_op jit(solution)/shard_map/ppermute | solution.py:88
  119.4 32.0 %collective-permute-start.31 = (bf16[2,960,256]{2,1,0:T(8,128)(2,1)S(1)}, bf16[2,960,256]{2,1,0:T(8,128)(2,1)}, u32[]{:S(2)}, u32[]{:S(2)}) collective-permute-start(bf16[2,960,256]{2,1,0:T(8,128)(2,1)S(1)} %bitcast.79), channel_id=1, source_target_pairs={{0,1},{1,0},{2,3},{3,2},{4,6},{5,7},{6,4},{7,5},{8,9},{9,8},{10,11... | collective-permute-start | bytes 2949128 | tf_op jit(solution)/shard_map/ppermute | solution.py:88
  122.3 29.1 %collective-permute-start.32 = (bf16[2,960,256]{2,1,0:T(8,128)(2,1)S(1)}, bf16[2,960,256]{2,1,0:T(8,128)(2,1)}, u32[]{:S(2)}, u32[]{:S(2)}) collective-permute-start(bf16[2,960,256]{2,1,0:T(8,128)(2,1)S(1)} %bitcast.80), channel_id=1, source_target_pairs={{0,2},{1,3},{2,0},{3,1},{4,5},{5,4},{6,7},{7,6},{8,10},{9,11},{10,... | collective-permute-start | bytes 2949128 | tf_op jit(solution)/shard_map/ppermute | solution.py:88
  123.9 27.5 %collective-permute-start.30 = (bf16[2,960,256]{2,1,0:T(8,128)(2,1)S(1)}, bf16[2,960,256]{2,1,0:T(8,128)(2,1)S(1)}, u32[]{:S(2)}, u32[]{:S(2)}) collective-permute-start(bf16[2,960,256]{2,1,0:T(8,128)(2,1)S(1)} %bitcast.86), channel_id=1, source_target_pairs={{0,4},{1,5},{2,6},{3,7},{4,0},{5,1},{6,2},{7,3},{8,12},{9,13},{10,... | collective-permute-start | bytes 2949128 | tf_op jit(solution)/shard_map/ppermute | solution.py:88
  152.4 18.2 %collective-permute-start.34 = (bf16[512,2560]{1,0:T(8,128)(2,1)}, bf16[512,2560]{1,0:T(8,128)(2,1)}, u32[]{:S(2)}, u32[]{:S(2)}) collective-permute-start(bf16[512,2560]{1,0:T(8,128)(2,1)} %get-tuple-element.385.given_ref), channel_id=1, source_target_pairs={{0,4},{1,5},{2,6},{3,7},{4,0},{5,1},{6,2},{7,3},{8,12},{9,13},{10,... | collective-permute-start | bytes 7864328 | tf_op jit(solution)/shard_map/ppermute | solution.py:88
  152.6 17.9 %collective-permute-start.35 = (bf16[512,2560]{1,0:T(8,128)(2,1)}, bf16[512,2560]{1,0:T(8,128)(2,1)}, u32[]{:S(2)}, u32[]{:S(2)}) collective-permute-start(bf16[512,2560]{1,0:T(8,128)(2,1)} %get-tuple-element.407.inner_ref), channel_id=1, source_target_pairs={{0,4},{1,5},{2,6},{3,7},{4,0},{5,1},{6,2},{7,3},{8,12},{9,13},{10,... | collective-permute-start | bytes 7864328 | tf_op jit(solution)/shard_map/ppermute | solution.py:88
  152.9 17.6 %collective-permute-start.33 = (bf16[960,512]{1,0:T(8,128)(2,1)}, bf16[960,512]{1,0:T(8,128)(2,1)}, u32[]{:S(2)}, u32[]{:S(2)}) collective-permute-start(bf16[960,512]{1,0:T(8,128)(2,1)} %get-tuple-element.426.left_ref), channel_id=1, source_target_pairs={{0,4},{1,5},{2,6},{3,7},{4,0},{5,1},{6,2},{7,3},{8,12},{9,13},{10,... | collective-permute-start | bytes 2949128 | tf_op jit(solution)/shard_map/ppermute | solution.py:88
  153.1 17.4 %collective-permute-start.36 = (bf16[2,960,256]{2,1,0:T(8,128)(2,1)}, bf16[2,960,256]{2,1,0:T(8,128)(2,1)}, u32[]{:S(2)}, u32[]{:S(2)}) collective-permute-start(bf16[2,960,256]{2,1,0:T(8,128)(2,1)} %collective-permute-done.31.refs_1_), channel_id=1, source_target_pairs={{0,2},{1,3},{2,0},{3,1},{4,5},{5,4},{6,7},{7,6},{8,10},{9,11},{10,... | collective-permute-start | bytes 2949128 | tf_op jit(solution)/shard_map/ppermute | solution.py:88
  177.0 16.8 %collective-permute-start.37 = (bf16[960,640]{1,0:T(8,128)(2,1)S(1)}, bf16[960,640]{1,0:T(8,128)(2,1)S(1)}, u32[]{:S(2)}, u32[]{:S(2)}) collective-permute-start(bf16[960,640]{1,0:T(8,128)(2,1)S(1)} %get-tuple-element.451), channel_id=1, source_target_pairs={{0,2},{1,3},{2,0},{3,1},{4,5},{5,4},{6,7},{7,6},{8,10},{9,11},{10,... | collective-permute-start | bytes 3686408 | tf_op jit(solution)/shard_map/ppermute | solution.py:88
  193.8 23.1 %collective-permute-start.39 = (bf16[256,2560]{1,0:T(8,128)(2,1)S(1)}, bf16[256,2560]{1,0:T(8,128)(2,1)S(1)}, u32[]{:S(2)}, u32[]{:S(2)}) collective-permute-start(bf16[256,2560]{1,0:T(8,128)(2,1)S(1)} %get-tuple-element.478), channel_id=1, source_target_pairs={{0,2},{1,3},{2,0},{3,1},{4,5},{5,4},{6,7},{7,6},{8,10},{9,11},{10,... | collective-permute-start | bytes 3932168 | tf_op jit(solution)/shard_map/ppermute | solution.py:88
  194.7 16.9 %collective-permute-start.38 = (bf16[480,640]{1,0:T(8,128)(2,1)S(1)}, bf16[480,640]{1,0:T(8,128)(2,1)S(1)}, u32[]{:S(2)}, u32[]{:S(2)}) collective-permute-start(bf16[480,640]{1,0:T(8,128)(2,1)S(1)} %add_convert_fusion.12), channel_id=1, source_target_pairs={{0,1},{1,0},{2,3},{3,2},{4,6},{5,7},{6,4},{7,5},{8,9},{9,8},{10,11... | collective-permute-start | bytes 1843208 | tf_op jit(solution)/shard_map/ppermute | solution.py:88
  217.0 20.6 %collective-permute-start.41 = (bf16[128,2560]{1,0:T(8,128)(2,1)S(1)}, bf16[128,2560]{1,0:T(8,128)(2,1)S(1)}, u32[]{:S(2)}, u32[]{:S(2)}) collective-permute-start(bf16[128,2560]{1,0:T(8,128)(2,1)S(1)} %add_convert_fusion.8), channel_id=1, source_target_pairs={{0,1},{1,0},{2,3},{3,2},{4,6},{5,7},{6,4},{7,5},{8,9},{9,8},{10,11... | collective-permute-start | bytes 1966088 | tf_op jit(solution)/shard_map/ppermute | solution.py:88
  218.1 20.1 %collective-permute-start.42 = (bf16[224,2560]{1,0:T(8,128)(2,1)S(1)}, bf16[224,2560]{1,0:T(8,128)(2,1)S(1)}, u32[]{:S(2)}, u32[]{:S(2)}) collective-permute-start(bf16[224,2560]{1,0:T(8,128)(2,1)S(1)} %get-tuple-element.505), channel_id=1, source_target_pairs={{0,2},{1,3},{2,0},{3,1},{4,5},{5,4},{6,7},{7,6},{8,10},{9,11},{10,... | collective-permute-start | bytes 3440648 | tf_op jit(solution)/shard_map/ppermute | solution.py:88
  219.2 18.4 %collective-permute-start.40 = (bf16[480,640]{1,0:T(8,128)(2,1)S(1)}, bf16[480,640]{1,0:T(8,128)(2,1)S(1)}, u32[]{:S(2)}, u32[]{:S(2)}) collective-permute-start(bf16[480,640]{1,0:T(8,128)(2,1)S(1)} %add_convert_fusion.11), channel_id=1, source_target_pairs={{0,8},{1,9},{2,10},{3,11},{4,12},{5,13},{6,14},{7,15},{24,16},{25,... | collective-permute-start | bytes 1843208 | tf_op jit(solution)/shard_map/ppermute | solution.py:88
  239.6 22.0 %collective-permute-start.45 = (bf16[128,2560]{1,0:T(8,128)(2,1)}, bf16[128,2560]{1,0:T(8,128)(2,1)}, u32[]{:S(2)}, u32[]{:S(2)}) collective-permute-start(bf16[128,2560]{1,0:T(8,128)(2,1)} %add_convert_fusion.7), channel_id=1, source_target_pairs={{0,8},{1,9},{2,10},{3,11},{4,12},{5,13},{6,14},{7,15},{24,16},{25,... | collective-permute-start | bytes 1966088 | tf_op jit(solution)/shard_map/ppermute | solution.py:88
  242.6 24.1 %collective-permute-start.43 = (bf16[2,512,640]{2,1,0:T(8,128)(2,1)}, bf16[2,512,640]{2,1,0:T(8,128)(2,1)}, u32[]{:S(2)}, u32[]{:S(2)}) collective-permute-start(bf16[2,512,640]{2,1,0:T(8,128)(2,1)} %get-tuple-element.510.refs_5_), channel_id=1, source_target_pairs={{0,2},{1,3},{2,0},{3,1},{4,5},{5,4},{6,7},{7,6},{8,10},{9,11},{10,... | collective-permute-start | bytes 3932168 | tf_op jit(solution)/shard_map/ppermute | solution.py:88
  243.7 17.8 %collective-permute-start.44 = (bf16[480,640]{1,0:T(8,128)(2,1)S(1)}, bf16[480,640]{1,0:T(8,128)(2,1)S(1)}, u32[]{:S(2)}, u32[]{:S(2)}) collective-permute-start(bf16[480,640]{1,0:T(8,128)(2,1)S(1)} %add_convert_fusion.10), channel_id=1, source_target_pairs={{8,16},{9,17},{10,18},{11,19},{12,20},{13,21},{14,22},{15,23},{16,... | collective-permute-start | bytes 1843208 | tf_op jit(solution)/shard_map/ppermute | solution.py:88
  245.4 16.2 %collective-permute-start.46 = (bf16[112,2560]{1,0:T(8,128)(2,1)}, bf16[112,2560]{1,0:T(8,128)(2,1)S(1)}, u32[]{:S(2)}, u32[]{:S(2)}) collective-permute-start(bf16[112,2560]{1,0:T(8,128)(2,1)} %add_convert_fusion.16), channel_id=1, source_target_pairs={{0,1},{1,0},{2,3},{3,2},{4,6},{5,7},{6,4},{7,5},{8,9},{9,8},{10,11... | collective-permute-start | bytes 1720328 | tf_op jit(solution)/shard_map/ppermute | solution.py:88
  266.7 5.5 %collective-permute-start.49 = (bf16[512,2688]{1,0:T(8,128)(2,1)}, bf16[512,2688]{1,0:T(8,128)(2,1)S(1)}, u32[]{:S(2)}, u32[]{:S(2)}) collective-permute-start(bf16[512,2688]{1,0:T(8,128)(2,1)} %get-tuple-element.530), channel_id=1, source_target_pairs={{0,4},{1,5},{2,6},{3,7},{4,0},{5,1},{6,2},{7,3},{8,12},{9,13},{10,... | collective-permute-start | bytes 8257544 | tf_op jit(solution)/shard_map/ppermute | solution.py:88
  268.3 29.0 %collective-permute-start.51 = (bf16[128,2560]{1,0:T(8,128)(2,1)S(1)}, bf16[128,2560]{1,0:T(8,128)(2,1)}, u32[]{:S(2)}, u32[]{:S(2)}) collective-permute-start(bf16[128,2560]{1,0:T(8,128)(2,1)S(1)} %add_convert_fusion.5), channel_id=1, source_target_pairs={{8,16},{9,17},{10,18},{11,19},{12,20},{13,21},{14,22},{15,23},{16,... | collective-permute-start | bytes 1966088 | tf_op jit(solution)/shard_map/ppermute | solution.py:88
  270.8 26.5 %collective-permute-start.48 = (bf16[480,640]{1,0:T(8,128)(2,1)}, bf16[480,640]{1,0:T(8,128)(2,1)}, u32[]{:S(2)}, u32[]{:S(2)}) collective-permute-start(bf16[480,640]{1,0:T(8,128)(2,1)} %add_convert_fusion.9), channel_id=1, source_target_pairs={{8,0},{9,1},{10,2},{11,3},{12,4},{13,5},{14,6},{15,7},{16,24},{17,... | collective-permute-start | bytes 1843208 | tf_op jit(solution)/shard_map/ppermute | solution.py:88
  274.2 25.6 %collective-permute-start.50 = (bf16[256,2688]{1,0:T(8,128)(2,1)}, bf16[256,2688]{1,0:T(8,128)(2,1)}, u32[]{:S(2)}, u32[]{:S(2)}) collective-permute-start(bf16[256,2688]{1,0:T(8,128)(2,1)} %add_convert_fusion), channel_id=1, source_target_pairs={{0,2},{1,3},{2,0},{3,1},{4,5},{5,4},{6,7},{7,6},{8,10},{9,11},{10,... | collective-permute-start | bytes 4128776 | tf_op jit(solution)/shard_map/ppermute | solution.py:88
  277.2 20.0 %collective-permute-start.47 = (bf16[1,512,640]{2,1,0:T(8,128)(2,1)}, bf16[1,512,640]{2,1,0:T(8,128)(2,1)}, u32[]{:S(2)}, u32[]{:S(2)}) collective-permute-start(bf16[1,512,640]{2,1,0:T(8,128)(2,1)} %add_convert_fusion.6), channel_id=1, source_target_pairs={{0,1},{1,0},{2,3},{3,2},{4,6},{5,7},{6,4},{7,5},{8,9},{9,8},{10,11... | collective-permute-start | bytes 1966088 | tf_op jit(solution)/shard_map/ppermute | solution.py:88
  279.5 17.8 %collective-permute-start.52 = (bf16[112,2560]{1,0:T(8,128)(2,1)}, bf16[112,2560]{1,0:T(8,128)(2,1)S(1)}, u32[]{:S(2)}, u32[]{:S(2)}) collective-permute-start(bf16[112,2560]{1,0:T(8,128)(2,1)} %add_convert_fusion.15), channel_id=1, source_target_pairs={{0,8},{1,9},{2,10},{3,11},{4,12},{5,13},{6,14},{7,15},{24,16},{25,... | collective-permute-start | bytes 1720328 | tf_op jit(solution)/shard_map/ppermute | solution.py:88
  301.0 23.1 %collective-permute-start.59 = (bf16[112,2560]{1,0:T(8,128)(2,1)S(1)}, bf16[112,2560]{1,0:T(8,128)(2,1)S(1)}, u32[]{:S(2)}, u32[]{:S(2)}) collective-permute-start(bf16[112,2560]{1,0:T(8,128)(2,1)S(1)} %add_convert_fusion.14), channel_id=1, source_target_pairs={{8,16},{9,17},{10,18},{11,19},{12,20},{13,21},{14,22},{15,23},{16,... | collective-permute-start | bytes 1720328 | tf_op jit(solution)/shard_map/ppermute | solution.py:88
  303.5 11.0 %collective-permute-start.54 = (bf16[128,2688]{1,0:T(8,128)(2,1)S(1)}, bf16[128,2688]{1,0:T(8,128)(2,1)S(1)}, u32[]{:S(2)}, u32[]{:S(2)}) collective-permute-start(bf16[128,2688]{1,0:T(8,128)(2,1)S(1)} %add_convert_fusion.2), channel_id=1, source_target_pairs={{0,1},{1,0},{2,3},{3,2},{4,6},{5,7},{6,4},{7,5},{8,9},{9,8},{10,11... | collective-permute-start | bytes 2064392 | tf_op jit(solution)/shard_map/ppermute | solution.py:88
  305.9 30.7 %collective-permute-start.58 = (bf16[128,2560]{1,0:T(8,128)(2,1)S(1)}, bf16[128,2560]{1,0:T(8,128)(2,1)S(1)}, u32[]{:S(2)}, u32[]{:S(2)}) collective-permute-start(bf16[128,2560]{1,0:T(8,128)(2,1)S(1)} %add_convert_fusion.3), channel_id=1, source_target_pairs={{8,0},{9,1},{10,2},{11,3},{12,4},{13,5},{14,6},{15,7},{16,24},{17,... | collective-permute-start | bytes 1966088 | tf_op jit(solution)/shard_map/ppermute | solution.py:88
  308.7 26.4 %collective-permute-start.53 = (bf16[480,640]{1,0:T(8,128)(2,1)S(1)}, bf16[480,640]{1,0:T(8,128)(2,1)S(1)}, u32[]{:S(2)}, u32[]{:S(2)}) collective-permute-start(bf16[480,640]{1,0:T(8,128)(2,1)S(1)} %broadcast_select_fusion.3), channel_id=1, source_target_pairs={{0,4},{1,5},{2,6},{3,7},{4,0},{5,1},{6,2},{7,3},{8,12},{9,13},{10,... | collective-permute-start | bytes 1843208 | tf_op jit(solution)/shard_map/ppermute | solution.py:88
  316.6 22.6 %collective-permute-start.55 = (bf16[32,2688]{1,0:T(8,128)(2,1)S(1)}, bf16[32,2688]{1,0:T(8,128)(2,1)S(1)}, u32[]{:S(2)}, u32[]{:S(2)}) collective-permute-start(bf16[32,2688]{1,0:T(8,128)(2,1)S(1)} %get-tuple-element.566), channel_id=1, source_target_pairs={{0,8},{1,9},{2,10},{3,11},{4,12},{5,13},{6,14},{7,15},{8,0},{9,1},... | collective-permute-start | bytes 516104 | tf_op jit(solution)/shard_map/ppermute | solution.py:88
  324.1 15.1 %collective-permute-start.56 = (bf16[32,2688]{1,0:T(8,128)(2,1)S(1)}, bf16[32,2688]{1,0:T(8,128)(2,1)S(1)}, u32[]{:S(2)}, u32[]{:S(2)}) collective-permute-start(bf16[32,2688]{1,0:T(8,128)(2,1)S(1)} %get-tuple-element.565), channel_id=1, source_target_pairs={{0,16},{1,17},{2,18},{3,19},{4,20},{5,21},{6,22},{7,23},{8,24},{9,... | collective-permute-start | bytes 516104 | tf_op jit(solution)/shard_map/ppermute | solution.py:88
  324.1 15.1 %collective-permute-start.57 = (bf16[32,2688]{1,0:T(8,128)(2,1)S(1)}, bf16[32,2688]{1,0:T(8,128)(2,1)S(1)}, u32[]{:S(2)}, u32[]{:S(2)}) collective-permute-start(bf16[32,2688]{1,0:T(8,128)(2,1)S(1)} %get-tuple-element.564), channel_id=1, source_target_pairs={{0,24},{1,25},{2,26},{3,27},{4,28},{5,29},{6,30},{7,31},{8,16},{9,... | collective-permute-start | bytes 516104 | tf_op jit(solution)/shard_map/ppermute | solution.py:88
  339.3 8.4 %collective-permute-start.60 = (bf16[32,2688]{1,0:T(8,128)(2,1)S(1)}, bf16[32,2688]{1,0:T(8,128)(2,1)S(1)}, u32[]{:S(2)}, u32[]{:S(2)}) collective-permute-start(bf16[32,2688]{1,0:T(8,128)(2,1)S(1)} %add_convert_fusion.17), channel_id=1, source_target_pairs={{0,8},{1,9},{2,10},{3,11},{4,12},{5,13},{6,14},{7,15},{8,0},{9,1},... | collective-permute-start | bytes 516104 | tf_op jit(solution)/shard_map/ppermute | solution.py:88
  341.1 13.8 %collective-permute-start.61 = (bf16[32,2688]{1,0:T(8,128)(2,1)S(1)}, bf16[32,2688]{1,0:T(8,128)(2,1)S(1)}, u32[]{:S(2)}, u32[]{:S(2)}) collective-permute-start(bf16[32,2688]{1,0:T(8,128)(2,1)S(1)} %add_convert_fusion.17), channel_id=1, source_target_pairs={{0,16},{1,17},{2,18},{3,19},{4,20},{5,21},{6,22},{7,23},{8,24},{9,... | collective-permute-start | bytes 516104 | tf_op jit(solution)/shard_map/ppermute | solution.py:88
  341.2 13.7 %collective-permute-start.62 = (bf16[32,2688]{1,0:T(8,128)(2,1)S(1)}, bf16[32,2688]{1,0:T(8,128)(2,1)S(1)}, u32[]{:S(2)}, u32[]{:S(2)}) collective-permute-start(bf16[32,2688]{1,0:T(8,128)(2,1)S(1)} %add_convert_fusion.17), channel_id=1, source_target_pairs={{0,24},{1,25},{2,26},{3,27},{4,28},{5,29},{6,30},{7,31},{8,16},{9,... | collective-permute-start | bytes 516104 | tf_op jit(solution)/shard_map/ppermute | solution.py:88
  343.9 20.5 %collective-permute-start.65 = (bf16[112,2560]{1,0:T(8,128)(2,1)S(1)}, bf16[112,2560]{1,0:T(8,128)(2,1)S(1)}, u32[]{:S(2)}, u32[]{:S(2)}) collective-permute-start(bf16[112,2560]{1,0:T(8,128)(2,1)S(1)} %add_convert_fusion.13), channel_id=1, source_target_pairs={{8,0},{9,1},{10,2},{11,3},{12,4},{13,5},{14,6},{15,7},{16,24},{17,... | collective-permute-start | bytes 1720328 | tf_op jit(solution)/shard_map/ppermute | solution.py:88
  346.1 25.0 %collective-permute-start.64 = (bf16[128,2560]{1,0:T(8,128)(2,1)}, bf16[128,2560]{1,0:T(8,128)(2,1)}, u32[]{:S(2)}, u32[]{:S(2)}) collective-permute-start(bf16[128,2560]{1,0:T(8,128)(2,1)} %broadcast_select_fusion.refs_0_), channel_id=1, source_target_pairs={{0,4},{1,5},{2,6},{3,7},{4,0},{5,1},{6,2},{7,3},{8,12},{9,13},{10,... | collective-permute-start | bytes 1966088 | tf_op jit(solution)/shard_map/ppermute | solution.py:88
  355.3 12.1 %collective-permute-start.63 = (bf16[128,2688]{1,0:T(8,128)(2,1)S(1)}, bf16[128,2688]{1,0:T(8,128)(2,1)}, u32[]{:S(2)}, u32[]{:S(2)}) collective-permute-start(bf16[128,2688]{1,0:T(8,128)(2,1)S(1)} %bitcast.82), channel_id=1, source_target_pairs={{0,4},{1,5},{2,6},{3,7},{4,0},{5,1},{6,2},{7,3},{8,12},{9,13},{10,... | collective-permute-start | bytes 2064392 | tf_op jit(solution)/shard_map/ppermute | solution.py:88
  365.3 5.8 %collective-permute-start.66 = (bf16[112,2560]{1,0:T(8,128)(2,1)}, bf16[112,2560]{1,0:T(8,128)(2,1)}, u32[]{:S(2)}, u32[]{:S(2)}) collective-permute-start(bf16[112,2560]{1,0:T(8,128)(2,1)} %broadcast_select_fusion.5.refs_2_), channel_id=1, source_target_pairs={{0,4},{1,5},{2,6},{3,7},{4,0},{5,1},{6,2},{7,3},{8,12},{9,13},{10,... | collective-permute-start | bytes 1720328 | tf_op jit(solution)/shard_map/ppermute | solution.py:88
  (83 other events, 1103.8 us)

commit v12 on v11

--- a/solution.py
+++ b/solution.py
@@ -373,7 +373,7 @@
     w_attn, w_pair, w_down, sum_ref, sems0, sems1, sems2 = refs[total_count + 7 :]
     width = x_ref.shape[1]
     hidden = w_pair.shape[1]
-    tile = hidden // 4
+    tile = hidden // 2
     wait_attention = load_lower(attention_pieces, s0_ref, w_attn, sems0, width)
     start_pair, wait_pair = load_halves(pair_pieces, s1_ref, w_pair, sems1)
     start_pair(0)

time: 384 us -> 382 us (level)
  no operation moved by 1% of the time
where the time goes in v12:
time: 382 us; the launch traced here: 374 us
  Pallas kernels  136 us (36%)
  waiting for transfers between devices  102 us (27%)
  starting transfers between devices  73.9 us (19%)
  other arithmetic  34.4 us (9%)
  local copies, waits for them, and re-layouts  26 us (7%)
    ppermute x67, waiting for transfers between devices, move(): return lax.ppermute(value, AXES, pairs)  102 us
    ppermute x67, starting transfers between devices, move(): return lax.ppermute(value, AXES, pairs)  73.9 us
    pallas_call x2, Pallas kernels, attend_back(): pl.pallas_call(functools.partial(attend_back_kernel, shards, seg_rows), g...  31.9 us
    pallas_call x1, Pallas kernels, feed(): pl.pallas_call(functools.partial(feed_kernel, counts), name='feed', in_sp...  25 us
    convert_element_type x17, other arithmetic, total(): return sum((part.astype(F32) for part in parts)).astype(parts[0].dtype)  16.9 us
    pallas_call x1, Pallas kernels, attend(): pl.pallas_call(functools.partial(attend_kernel, shards, seg_rows), grid=(...  16.8 us
    pallas_call x1, Pallas kernels, feed_back(): pl.pallas_call(functools.partial(feed_back_kernel, counts), name='feed_ba...  15 us
    pallas_call x1, Pallas kernels, attention_grad(): pl.pallas_call(functools.partial(attention_grad_kernel, shards, half), na...  13.3 us
  transfers between devices with their start and end apart: 67, of which 21 were waited for; matrix products, arithmetic and copies ran while one was open for 10% of the time, Pallas kernels for 34%

profile of v12, /device:TPU:0, one launch (start us, length us, event | category | flops | bytes accessed | tf_op | source)
XLA Modules:
  0.0 374.5 jit_solution(10275310489491778323)
XLA Ops:
  2.9 2.4 broadcast_select_fusion.4
  5.2 2.9 collective-permute-start
  8.2 1.5 collective-permute-start.1
  10.4 2.9 collective-permute-start.4
  13.9 1.7 fusion.1
  16.5 2.0 dynamic-slice_select_fusion
  18.6 1.8 multiply_sine_fusion
  20.4 2.0 dynamic-slice_bitcast_fusion
  25.2 2.0 collective-permute-start.8
  27.4 11.7 %collective-permute-done.5.refs_6_ = bf16[240,1280]{1,0:T(8,128)(2,1)} collective-permute-done((bf16[240,1280]{1,0:T(8,128)(2,1)S(1)}, bf16[240,1280]{1,0:T(8,128)(2,1)}, u32[]{:S(2)}, u32[]{:S(2)}) %collective-permute-start.5) | collective-permute-done | bytes 614432 | tf_op jit(solution)/shard_map/ppermute | solution.py:88
  39.5 2.2 tile.20
  44.2 2.4 collective-permute-start.11
  46.6 1.6 collective-permute-start.12
  48.3 1.6 copy.62.cos_ref
  49.8 1.9 copy.63.sin_ref
  51.8 1.4 copy-done.12
  56.6 5.0 %project.1 = (bf16[512,960]{1,0:T(8,128)(2,1)S(1)}, bf16[512,640]{1,0:T(8,128)(2,1)S(1)}) custom-call(s32[16]{0:T(128)S(1)} %stack.194.starts_ref.s0_ref, bf16[2,960,256]{2,1,0:T(8,128)(2,1)S(1)} %bitcast.78, f32[2,960]{1,0:T(2,128)S(1)} %maximum_convert_fusion.gains_ref, f32[2048,128]{1,0:T(8,128)S(1)} %copy.62.cos_ref, f32[2048,128]{1,0:T(8,128)S(1)} %copy.63.sin_ref, ...), custom_call_target="tpu_custom_call" | custom-call | flops 1572864000 | bytes 7536640 | tf_op jit(solution)/shard_map/project/pallas_call | solution.py:344
  63.2 1.8 collective-permute-start.15
  64.9 13.9 %collective-permute-done.15.refs_15_ = bf16[240,1280]{1,0:T(8,128)(2,1)S(1)} collective-permute-done((bf16[240,1280]{1,0:T(8,128)(2,1)}, bf16[240,1280]{1,0:T(8,128)(2,1)S(1)}, u32[]{:S(2)}, u32[]{:S(2)}) %collective-permute-start.15) | collective-permute-done | bytes 614432 | tf_op jit(solution)/shard_map/ppermute | solution.py:88
  81.6 7.8 %collective-permute-done.17.refs_18_ = bf16[240,1280]{1,0:T(8,128)(2,1)S(1)} collective-permute-done((bf16[240,1280]{1,0:T(8,128)(2,1)}, bf16[240,1280]{1,0:T(8,128)(2,1)S(1)}, u32[]{:S(2)}, u32[]{:S(2)}) %collective-permute-start.17) | collective-permute-done | bytes 614432 | tf_op jit(solution)/shard_map/ppermute | solution.py:88
  89.4 2.0 collective-permute-done.21.refs_17_
  91.4 5.0 %collective-permute-done.16.refs_3_ = bf16[512,640]{1,0:T(8,128)(2,1)S(1)} collective-permute-done((bf16[512,640]{1,0:T(8,128)(2,1)S(1)}, bf16[512,640]{1,0:T(8,128)(2,1)S(1)}, u32[]{:S(2)}, u32[]{:S(2)}) %collective-permute-start.16) | collective-permute-done | bytes 655392 | tf_op jit(solution)/shard_map/ppermute | solution.py:88
  99.7 16.8 %attend.1 = (bf16[512,960]{1,0:T(8,128)(2,1)S(1)}, f32[512,128]{1,0:T(8,128)S(1)}) custom-call(bf16[512,960]{1,0:T(8,128)(2,1)S(1)} %get-tuple-element.480.q_ref, bf16[512,640]{1,0:T(8,128)(2,1)S(1)} %get-tuple-element.481.refs_0_, bf16[512,640]{1,0:T(8,128)(2,1)S(1)} %collective-permute-done.13.refs_1_, ...), custom_call_target="tpu_custom_call" | custom-call | flops 8053063680 | bytes 983040 | tf_op jit(solution)/shard_map/attend/pallas_call | solution.py:909
  119.4 1.7 collective-permute-start.31
  123.9 25.0 %feed.1 = (bf16[2,960,256]{2,1,0:T(8,128)(2,1)}, bf16[512,2560]{1,0:T(8,128)(2,1)}, bf16[512,2560]{1,0:T(8,128)(2,1)}, bf16[512,2560]{1,0:T(8,128)(2,1)}, bf16[9...) custom-call(s32[1]{0:T(128)} %bitcast.core_ref, s32[16]{0:T(128)} %copy-done.38, ...), custom_call_target="tpu_custom_call" | custom-call | flops 11010048000 | bytes 35389440 | tf_op jit(solution)/shard_map/feed/pallas_call | solution.py:426
  153.0 15.0 %feed_back.1 = (f32[960,512]{1,0:T(8,128)}, bf16[512,1024]{1,0:T(8,128)(2,1)}, bf16[512,960]{1,0:T(8,128)(2,1)}) custom-call(s32[1]{0:T(128)} %bitcast.core_ref, s32[16]{0:T(128)} %copy-done.38, s32[28]{0:T(128)} %stack.197.s1_ref, f32[960,512]{1,0:T(8,128)} %get-tuple-element.383.resid_ref, bf16[2,960,256]{2,1,0:T(8,128)(2,1)} %bitcast.85, ...), custom_call_target="tpu_custom_call" | custom-call | flops 5976883200 | bytes 26935296 | tf_op jit(solution)/shard_map/feed_back/pallas_call | solution.py:485
  169.3 5.2 %down_grad.1 = (bf16[960,640]{1,0:T(8,128)(2,1)S(1)}, bf16[960,640]{1,0:T(8,128)(2,1)S(1)}) custom-call(s32[5]{0:T(128)S(1)} %stack.214.info_ref, bf16[2,960,256]{2,1,0:T(8,128)(2,1)S(1)} %bitcast.87, bf16[2,960,256]{2,1,0:T(8,128)(2,1)S(1)} %copy-done.46, bf16[512,2560]{1,0:T(8,128)(2,1)S(1)} %copy-done.40, ...), custom_call_target="tpu_custom_call" | custom-call | flops 2516582400 | bytes 9666560 | tf_op jit(solution)/shard_map/down_grad/pallas_call | solution.py:530
  175.5 9.0 %wide_grad.1 = (bf16[256,2560]{1,0:T(8,128)(2,1)S(1)}, bf16[256,2560]{1,0:T(8,128)(2,1)S(1)}, bf16[224,2560]{1,0:T(8,128)(2,1)S(1)}, bf16[224,2560]{1,0:T(8,128)(2,1)S(1)}) custom-call(s32[4]{0:T(128)S(1)} %pad_add_fusion.1.starts_ref, bf16[960,512]{1,0:T(8,128)(2,1)S(1)} %copy-done.44, bf16[960,512]{1,0:T(8,128)(2,1)} %collective-permute-done.33.far_left_ref, ...), custom_call_target="tpu_custom_call" | custom-call | flops 5033164800 | bytes 12124160 | tf_op jit(solution)/shard_map/wide_grad/pallas_call | solution.py:579
  184.6 6.8 %collective-permute-done.37 = bf16[960,640]{1,0:T(8,128)(2,1)S(1)} collective-permute-done((bf16[960,640]{1,0:T(8,128)(2,1)S(1)}, bf16[960,640]{1,0:T(8,128)(2,1)S(1)}, u32[]{:S(2)}, u32[]{:S(2)}) %collective-permute-start.37) | collective-permute-done | bytes 1228832 | tf_op jit(solution)/shard_map/ppermute | solution.py:88
  193.3 16.1 %attend_back.2 = (bf16[512,1024]{1,0:T(8,128)(2,1)S(1)}, bf16[2,512,640]{2,1,0:T(8,128)(2,1)S(1)}, bf16[2,512,640]{2,1,0:T(8,128)(2,1)}) custom-call(bf16[512,960]{1,0:T(8,128)(2,1)S(1)} %copy-done.42, bf16[512,640]{1,0:T(8,128)(2,1)S(1)} %copy-done.48, bf16[512,640]{1,0:T(8,128)(2,1)S(1)} %copy-done.50, bf16[512,640]{1,0:T(8,128)(2,1)S(1)} %copy-done.52, ...), custom_call_target="tpu_custom_call" | custom-call | flops 10066329600 | bytes 983040 | tf_op jit(solution)/shard_map/attend_back/pallas_call | solution.py:931
  209.5 4.9 %collective-permute-done.39 = bf16[256,2560]{1,0:T(8,128)(2,1)S(1)} collective-permute-done((bf16[256,2560]{1,0:T(8,128)(2,1)S(1)}, bf16[256,2560]{1,0:T(8,128)(2,1)S(1)}, u32[]{:S(2)}, u32[]{:S(2)}) %collective-permute-start.39) | collective-permute-done | bytes 1310752 | tf_op jit(solution)/shard_map/ppermute | solution.py:88
  216.8 2.5 collective-permute-start.40
  219.3 15.8 %attend_back.3 = (bf16[512,1024]{1,0:T(8,128)(2,1)S(1)}, bf16[2,512,640]{2,1,0:T(8,128)(2,1)S(1)}, bf16[2,512,640]{2,1,0:T(8,128)(2,1)}) custom-call(bf16[512,960]{1,0:T(8,128)(2,1)S(1)} %copy-done.42, bf16[512,640]{1,0:T(8,128)(2,1)S(1)} %copy-done.48, ...), custom_call_target="tpu_custom_call", output_to_operand_aliasing={{0}: (11, {}), {1}: (12, {}), {2}: (13, {})} | custom-call | flops 10066329600 | bytes 983040 | tf_op jit(solution)/shard_map/attend_back/pallas_call | solution.py:931
  235.7 1.4 add_convert_fusion.7
  237.1 3.1 collective-permute-start.45
  245.9 13.3 %attention_grad.1 = (bf16[512,2688]{1,0:T(8,128)(2,1)}, bf16[512,2688]{1,0:T(8,128)(2,1)}) custom-call(s32[8]{0:T(128)} %stack.227.starts_ref, f32[960,1]{1,0:T(8,128)} %copy.65.gain_ref, f32[2048,128]{1,0:T(8,128)} %copy-done.4, f32[2048,128]{1,0:T(8,128)} %copy-done.6, bf16[512,1024]{1,0:T(8,128)(2,1)} %copy-done.29, ...), custom_call_target="tpu_custom_call" | custom-call | flops 4697620480 | bytes 12058624 | tf_op jit(solution)/shard_map/attention_grad/pallas_call | solution.py:735
  259.1 5.1 %collective-permute-done.43 = bf16[2,512,640]{2,1,0:T(8,128)(2,1)} collective-permute-done((bf16[2,512,640]{2,1,0:T(8,128)(2,1)}, bf16[2,512,640]{2,1,0:T(8,128)(2,1)}, u32[]{:S(2)}, u32[]{:S(2)}) %collective-permute-start.43) | collective-permute-done | bytes 1310752 | tf_op jit(solution)/shard_map/ppermute | solution.py:88
  264.2 1.6 add_convert_fusion.5
  265.8 1.5 collective-permute-start.51
  268.3 1.4 collective-permute-start.48
  269.8 1.7 add_convert_fusion
  272.7 2.1 add_convert_fusion.6
  277.0 5.4 %collective-permute-start.52 = (bf16[112,2560]{1,0:T(8,128)(2,1)}, bf16[112,2560]{1,0:T(8,128)(2,1)S(1)}, u32[]{:S(2)}, u32[]{:S(2)}) collective-permute-start(bf16[112,2560]{1,0:T(8,128)(2,1)} %add_convert_fusion.15), channel_id=1, source_target_pairs={{0,8},{1,9},{2,10},{3,11},{4,12},{5,13},{6,14},{7,15},{24,16},{25,... | collective-permute-start | bytes 1720328 | tf_op jit(solution)/shard_map/ppermute | solution.py:88
  282.5 12.3 %collective-permute-done.52 = bf16[112,2560]{1,0:T(8,128)(2,1)S(1)} collective-permute-done((bf16[112,2560]{1,0:T(8,128)(2,1)}, bf16[112,2560]{1,0:T(8,128)(2,1)S(1)}, u32[]{:S(2)}, u32[]{:S(2)}) %collective-permute-start.52) | collective-permute-done | bytes 573472 | tf_op jit(solution)/shard_map/ppermute | solution.py:88
  294.8 2.6 collective-permute-done.50
  299.3 1.8 add_convert_fusion.2
  302.1 1.3 add_convert_fusion.3
  303.4 1.5 collective-permute-start.58
  306.3 5.7 %collective-permute-done.54 = bf16[128,2688]{1,0:T(8,128)(2,1)S(1)} collective-permute-done((bf16[128,2688]{1,0:T(8,128)(2,1)S(1)}, bf16[128,2688]{1,0:T(8,128)(2,1)S(1)}, u32[]{:S(2)}, u32[]{:S(2)}) %collective-permute-start.54) | collective-permute-done | bytes 688160 | tf_op jit(solution)/shard_map/ppermute | solution.py:88
  312.1 2.0 add_convert_fusion.1
  314.2 7.5 %collective-permute-start.55 = (bf16[32,2688]{1,0:T(8,128)(2,1)S(1)}, bf16[32,2688]{1,0:T(8,128)(2,1)S(1)}, u32[]{:S(2)}, u32[]{:S(2)}) collective-permute-start(bf16[32,2688]{1,0:T(8,128)(2,1)S(1)} %get-tuple-element.566), channel_id=1, source_target_pairs={{0,8},{1,9},{2,10},{3,11},{4,12},{5,13},{6,14},{7,15},{8,0},{9,1},... | collective-permute-start | bytes 516104 | tf_op jit(solution)/shard_map/ppermute | solution.py:88
  321.7 2.5 collective-permute-start.57
  324.2 1.5 fusion.kv_ref
  325.8 6.9 %finish.1 = bf16[2,960,256]{2,1,0:T(8,128)(2,1)} custom-call(s32[16]{0:T(128)S(1)} %copy-done.39, bf16[2,960,256]{2,1,0:T(8,128)(2,1)S(1)} %bitcast.81, bf16[512,1024]{1,0:T(8,128)(2,1)S(1)} %copy-done.30, bf16[512,640]{1,0:T(8,128)(2,1)S(1)} %fusion.kv_ref, f32[960,512]{1,0:T(8,128)S(1)} %copy-done.24, f32[960,1]{1,0:T(8,128)S(1)} %copy-done.26, ...), custom_call_target="tpu_custom_call" | custom-call | flops 1572864000 | bytes 8912896 | tf_op jit(solution)/shard_map/finish/pallas_call | solution.py:781
  332.8 1.4 collective-permute-done.58
  334.2 2.6 collective-permute-done.55
  336.9 1.8 collective-permute-start.60
  338.7 2.6 collective-permute-start.62
  343.7 1.6 collective-permute-done.60
  345.3 7.2 %collective-permute-done.61 = bf16[32,2688]{1,0:T(8,128)(2,1)S(1)} collective-permute-done((bf16[32,2688]{1,0:T(8,128)(2,1)S(1)}, bf16[32,2688]{1,0:T(8,128)(2,1)S(1)}, u32[]{:S(2)}, u32[]{:S(2)}) %collective-permute-start.61) | collective-permute-done | bytes 172064 | tf_op jit(solution)/shard_map/ppermute | solution.py:88
  352.9 9.1 %collective-permute-done.65 = bf16[112,2560]{1,0:T(8,128)(2,1)S(1)} collective-permute-done((bf16[112,2560]{1,0:T(8,128)(2,1)S(1)}, bf16[112,2560]{1,0:T(8,128)(2,1)S(1)}, u32[]{:S(2)}, u32[]{:S(2)}) %collective-permute-start.65) | collective-permute-done | bytes 573472 | tf_op jit(solution)/shard_map/ppermute | solution.py:88
  363.4 1.6 convert_bitcast_fusion
  365.0 3.0 settle_some.1
  368.7 4.9 %settle.1 = (f32[240,2560]{1,0:T(8,128)}, f32[240,2560]{1,0:T(8,128)}, f32[240,1]{1,0:T(8,128)S(1)}) custom-call(s32[1]{0:T(128)} %bitcast.core_ref, f32[240,1]{1,0:T(8,128)S(1)} %copy.72.gain_ref, bf16[128,2560]{1,0:T(8,128)(2,1)} %broadcast_select_fusion.refs_0_, bf16[128,2560]{1,0:T(8,128)(2,1)} %collective-permute-done.64.refs_1_, ...), custom_call_target="tpu_custom_call" | custom-call | flops 2457600 | bytes 7372800 | tf_op jit(solution)/shard_map/settle/pallas_call | solution.py:620
  (324 shorter events, 58.0 us)
Async XLA Ops:
  5.2 18.3 %collective-permute-start = (bf16[240,1280]{1,0:T(8,128)(2,1)}, bf16[240,1280]{1,0:T(8,128)(2,1)S(1)}, u32[]{:S(2)}, u32[]{:S(2)}) collective-permute-start(bf16[240,1280]{1,0:T(8,128)(2,1)} %get-tuple-element.559), channel_id=1, source_target_pairs={{0,1},{1,0},{2,3},{3,2},{4,6},{5,7},{6,4},{7,5},{8,9},{9,8},{10,11... | collective-permute-start | bytes 1843208 | tf_op jit(solution)/shard_map/ppermute | solution.py:88
  8.2 15.4 %collective-permute-start.1 = (bf16[240,1280]{1,0:T(8,128)(2,1)}, bf16[240,1280]{1,0:T(8,128)(2,1)}, u32[]{:S(2)}, u32[]{:S(2)}) collective-permute-start(bf16[240,1280]{1,0:T(8,128)(2,1)} %get-tuple-element.559), channel_id=1, source_target_pairs={{0,2},{1,3},{2,0},{3,1},{4,5},{5,4},{6,7},{7,6},{8,10},{9,11},{10,... | collective-permute-start | bytes 1843208 | tf_op jit(solution)/shard_map/ppermute | solution.py:88
  9.7 12.9 %collective-permute-start.2 = (bf16[2,240]{1,0:T(2,128)(2,1)S(1)}, bf16[2,240]{1,0:T(2,128)(2,1)S(1)}, u32[]{:S(2)}, u32[]{:S(2)}) collective-permute-start(bf16[2,240]{1,0:T(2,128)(2,1)S(1)} %pad_maximum_fusion.5), channel_id=1, source_target_pairs={{0,1},{1,0},{2,3},{3,2},{4,5},{5,4},{6,7},{7,6},{8,9},{9,8},{10,11... | collective-permute-start | bytes 2888 | tf_op jit(solution)/shard_map/ppermute | solution.py:88
  10.3 12.3 %collective-permute-start.3 = (bf16[2,240]{1,0:T(2,128)(2,1)S(1)}, bf16[2,240]{1,0:T(2,128)(2,1)S(1)}, u32[]{:S(2)}, u32[]{:S(2)}) collective-permute-start(bf16[2,240]{1,0:T(2,128)(2,1)S(1)} %pad_maximum_fusion.5), channel_id=1, source_target_pairs={{0,2},{1,3},{2,0},{3,1},{4,6},{5,7},{6,4},{7,5},{8,10},{9,11},{10,... | collective-permute-start | bytes 2888 | tf_op jit(solution)/shard_map/ppermute | solution.py:88
  10.4 13.2 %collective-permute-start.4 = (bf16[2,240]{1,0:T(2,128)(2,1)S(1)}, bf16[2,240]{1,0:T(2,128)(2,1)S(1)}, u32[]{:S(2)}, u32[]{:S(2)}) collective-permute-start(bf16[2,240]{1,0:T(2,128)(2,1)S(1)} %pad_maximum_fusion.5), channel_id=1, source_target_pairs={{0,3},{1,2},{2,1},{3,0},{4,7},{5,6},{6,5},{7,4},{8,11},{9,10},{10,... | collective-permute-start | bytes 2888 | tf_op jit(solution)/shard_map/ppermute | solution.py:88
  23.6 15.6 %collective-permute-start.5 = (bf16[240,1280]{1,0:T(8,128)(2,1)S(1)}, bf16[240,1280]{1,0:T(8,128)(2,1)}, u32[]{:S(2)}, u32[]{:S(2)}) collective-permute-start(bf16[240,1280]{1,0:T(8,128)(2,1)S(1)} %collective-permute-done.refs_2_), channel_id=1, source_target_pairs={{0,2},{1,3},{2,0},{3,1},{4,5},{5,4},{6,7},{7,6},{8,10},{9,11},{10,... | collective-permute-start | bytes 1843208 | tf_op jit(solution)/shard_map/ppermute | solution.py:88
  24.2 14.9 %collective-permute-start.6 = (bf16[240,1280]{1,0:T(8,128)(2,1)S(1)}, bf16[240,1280]{1,0:T(8,128)(2,1)S(1)}, u32[]{:S(2)}, u32[]{:S(2)}) collective-permute-start(bf16[240,1280]{1,0:T(8,128)(2,1)S(1)} %collective-permute-done.refs_2_), channel_id=1, source_target_pairs={{0,4},{1,5},{2,6},{3,7},{4,0},{5,1},{6,2},{7,3},{8,12},{9,13},{10,... | collective-permute-start | bytes 1843208 | tf_op jit(solution)/shard_map/ppermute | solution.py:88
  25.1 14.0 %collective-permute-start.7 = (bf16[240,1280]{1,0:T(8,128)(2,1)}, bf16[240,1280]{1,0:T(8,128)(2,1)S(1)}, u32[]{:S(2)}, u32[]{:S(2)}) collective-permute-start(bf16[240,1280]{1,0:T(8,128)(2,1)} %collective-permute-done.1.refs_4_), channel_id=1, source_target_pairs={{0,4},{1,5},{2,6},{3,7},{4,0},{5,1},{6,2},{7,3},{8,12},{9,13},{10,... | collective-permute-start | bytes 1843208 | tf_op jit(solution)/shard_map/ppermute | solution.py:88
  25.2 14.3 %collective-permute-start.8 = (bf16[240,1280]{1,0:T(8,128)(2,1)}, bf16[240,1280]{1,0:T(8,128)(2,1)}, u32[]{:S(2)}, u32[]{:S(2)}) collective-permute-start(bf16[240,1280]{1,0:T(8,128)(2,1)} %dynamic-slice_select_fusion), channel_id=1, source_target_pairs={{0,1},{1,0},{2,3},{3,2},{4,6},{5,7},{6,4},{7,5},{8,9},{9,8},{10,11... | collective-permute-start | bytes 1843208 | tf_op jit(solution)/shard_map/ppermute | solution.py:88
  42.8 9.0 %collective-permute-start.9 = (bf16[240,1280]{1,0:T(8,128)(2,1)}, bf16[240,1280]{1,0:T(8,128)(2,1)}, u32[]{:S(2)}, u32[]{:S(2)}) collective-permute-start(bf16[240,1280]{1,0:T(8,128)(2,1)} %collective-permute-done.5.refs_6_), channel_id=1, source_target_pairs={{0,4},{1,5},{2,6},{3,7},{4,0},{5,1},{6,2},{7,3},{8,12},{9,13},{10,... | collective-permute-start | bytes 1843208 | tf_op jit(solution)/shard_map/ppermute | solution.py:88
  43.5 18.1 %collective-permute-start.10 = (bf16[240,1280]{1,0:T(8,128)(2,1)}, bf16[240,1280]{1,0:T(8,128)(2,1)}, u32[]{:S(2)}, u32[]{:S(2)}) collective-permute-start(bf16[240,1280]{1,0:T(8,128)(2,1)} %dynamic-slice_select_fusion), channel_id=1, source_target_pairs={{0,2},{1,3},{2,0},{3,1},{4,5},{5,4},{6,7},{7,6},{8,10},{9,11},{10,... | collective-permute-start | bytes 1843208 | tf_op jit(solution)/shard_map/ppermute | solution.py:88
  44.2 17.4 %collective-permute-start.11 = (bf16[240,1280]{1,0:T(8,128)(2,1)}, bf16[240,1280]{1,0:T(8,128)(2,1)}, u32[]{:S(2)}, u32[]{:S(2)}) collective-permute-start(bf16[240,1280]{1,0:T(8,128)(2,1)} %collective-permute-done.8.refs_10_), channel_id=1, source_target_pairs={{0,8},{1,9},{2,10},{3,11},{4,12},{5,13},{6,14},{7,15},{8,0},{9,1},... | collective-permute-start | bytes 1843208 | tf_op jit(solution)/shard_map/ppermute | solution.py:88
  46.6 15.0 %collective-permute-start.12 = (bf16[480,640]{1,0:T(8,128)(2,1)}, bf16[480,640]{1,0:T(8,128)(2,1)}, u32[]{:S(2)}, u32[]{:S(2)}) collective-permute-start(bf16[480,640]{1,0:T(8,128)(2,1)} %dynamic-slice_bitcast_fusion), channel_id=1, source_target_pairs={{0,1},{1,0},{2,3},{3,2},{4,6},{5,7},{6,4},{7,5},{8,9},{9,8},{10,11... | collective-permute-start | bytes 1843208 | tf_op jit(solution)/shard_map/ppermute | solution.py:88
  61.7 17.3 %collective-permute-start.13 = (bf16[512,640]{1,0:T(8,128)(2,1)S(1)}, bf16[512,640]{1,0:T(8,128)(2,1)S(1)}, u32[]{:S(2)}, u32[]{:S(2)}) collective-permute-start(bf16[512,640]{1,0:T(8,128)(2,1)S(1)} %get-tuple-element.481.refs_0_), channel_id=1, source_target_pairs={{0,1},{1,0},{2,3},{3,2},{4,6},{5,7},{6,4},{7,5},{8,9},{9,8},{10,11... | collective-permute-start | bytes 1966088 | tf_op jit(solution)/shard_map/ppermute | solution.py:88
  62.2 16.8 %collective-permute-start.14 = (bf16[512,640]{1,0:T(8,128)(2,1)S(1)}, bf16[512,640]{1,0:T(8,128)(2,1)S(1)}, u32[]{:S(2)}, u32[]{:S(2)}) collective-permute-start(bf16[512,640]{1,0:T(8,128)(2,1)S(1)} %get-tuple-element.481.refs_0_), channel_id=1, source_target_pairs={{0,2},{1,3},{2,0},{3,1},{4,5},{5,4},{6,7},{7,6},{8,10},{9,11},{10,... | collective-permute-start | bytes 1966088 | tf_op jit(solution)/shard_map/ppermute | solution.py:88
  63.2 15.7 %collective-permute-start.15 = (bf16[240,1280]{1,0:T(8,128)(2,1)}, bf16[240,1280]{1,0:T(8,128)(2,1)S(1)}, u32[]{:S(2)}, u32[]{:S(2)}) collective-permute-start(bf16[240,1280]{1,0:T(8,128)(2,1)} %collective-permute-done.10.refs_14_), channel_id=1, source_target_pairs={{0,8},{1,9},{2,10},{3,11},{4,12},{5,13},{6,14},{7,15},{8,0},{9,1},... | collective-permute-start | bytes 1843208 | tf_op jit(solution)/shard_map/ppermute | solution.py:88
  79.0 10.4 %collective-permute-start.17 = (bf16[240,1280]{1,0:T(8,128)(2,1)}, bf16[240,1280]{1,0:T(8,128)(2,1)S(1)}, u32[]{:S(2)}, u32[]{:S(2)}) collective-permute-start(bf16[240,1280]{1,0:T(8,128)(2,1)} %collective-permute-done.8.refs_10_), channel_id=1, source_target_pairs={{0,2},{1,3},{2,0},{3,1},{4,5},{5,4},{6,7},{7,6},{8,10},{9,11},{10,... | collective-permute-start | bytes 1843208 | tf_op jit(solution)/shard_map/ppermute | solution.py:88
  79.8 16.6 %collective-permute-start.16 = (bf16[512,640]{1,0:T(8,128)(2,1)S(1)}, bf16[512,640]{1,0:T(8,128)(2,1)S(1)}, u32[]{:S(2)}, u32[]{:S(2)}) collective-permute-start(bf16[512,640]{1,0:T(8,128)(2,1)S(1)} %collective-permute-done.13.refs_1_), channel_id=1, source_target_pairs={{0,2},{1,3},{2,0},{3,1},{4,5},{5,4},{6,7},{7,6},{8,10},{9,11},{10,... | collective-permute-start | bytes 1966088 | tf_op jit(solution)/shard_map/ppermute | solution.py:88
  81.1 8.3 %collective-permute-start.18 = (bf16[240,1280]{1,0:T(8,128)(2,1)}, bf16[240,1280]{1,0:T(8,128)(2,1)S(1)}, u32[]{:S(2)}, u32[]{:S(2)}) collective-permute-start(bf16[240,1280]{1,0:T(8,128)(2,1)} %collective-permute-done.8.refs_10_), channel_id=1, source_target_pairs={{0,4},{1,5},{2,6},{3,7},{4,0},{5,1},{6,2},{7,3},{8,12},{9,13},{10,... | collective-permute-start | bytes 1843208 | tf_op jit(solution)/shard_map/ppermute | solution.py:88
  81.1 8.4 %collective-permute-start.19 = (bf16[240,1280]{1,0:T(8,128)(2,1)}, bf16[240,1280]{1,0:T(8,128)(2,1)S(1)}, u32[]{:S(2)}, u32[]{:S(2)}) collective-permute-start(bf16[240,1280]{1,0:T(8,128)(2,1)} %collective-permute-done.10.refs_14_), channel_id=1, source_target_pairs={{0,4},{1,5},{2,6},{3,7},{4,0},{5,1},{6,2},{7,3},{8,12},{9,13},{10,... | collective-permute-start | bytes 1843208 | tf_op jit(solution)/shard_map/ppermute | solution.py:88
  81.6 7.9 %collective-permute-start.20 = (bf16[240,1280]{1,0:T(8,128)(2,1)}, bf16[240,1280]{1,0:T(8,128)(2,1)S(1)}, u32[]{:S(2)}, u32[]{:S(2)}) collective-permute-start(bf16[240,1280]{1,0:T(8,128)(2,1)} %collective-permute-done.11.refs_11_), channel_id=1, source_target_pairs={{0,4},{1,5},{2,6},{3,7},{4,0},{5,1},{6,2},{7,3},{8,12},{9,13},{10,... | collective-permute-start | bytes 1843208 | tf_op jit(solution)/shard_map/ppermute | solution.py:88
  96.4 21.8 %collective-permute-start.24 = (bf16[240,1280]{1,0:T(8,128)(2,1)S(1)}, bf16[240,1280]{1,0:T(8,128)(2,1)}, u32[]{:S(2)}, u32[]{:S(2)}) collective-permute-start(bf16[240,1280]{1,0:T(8,128)(2,1)S(1)} %collective-permute-done.17.refs_18_), channel_id=1, source_target_pairs={{0,8},{1,9},{2,10},{3,11},{4,12},{5,13},{6,14},{7,15},{8,0},{9,1},... | collective-permute-start | bytes 1843208 | tf_op jit(solution)/shard_map/ppermute | solution.py:88
  97.6 20.6 %collective-permute-start.25 = (bf16[240,1280]{1,0:T(8,128)(2,1)S(1)}, bf16[240,1280]{1,0:T(8,128)(2,1)S(1)}, u32[]{:S(2)}, u32[]{:S(2)}) collective-permute-start(bf16[240,1280]{1,0:T(8,128)(2,1)S(1)} %collective-permute-done.17.refs_18_), channel_id=1, source_target_pairs={{0,4},{1,5},{2,6},{3,7},{4,0},{5,1},{6,2},{7,3},{8,12},{9,13},{10,... | collective-permute-start | bytes 1843208 | tf_op jit(solution)/shard_map/ppermute | solution.py:88
  97.7 20.6 %collective-permute-start.22 = (bf16[480,640]{1,0:T(8,128)(2,1)}, bf16[480,640]{1,0:T(8,128)(2,1)}, u32[]{:S(2)}, u32[]{:S(2)}) collective-permute-start(bf16[480,640]{1,0:T(8,128)(2,1)} %dynamic-slice_bitcast_fusion), channel_id=1, source_target_pairs={{0,2},{1,3},{2,0},{3,1},{4,5},{5,4},{6,7},{7,6},{8,10},{9,11},{10,... | collective-permute-start | bytes 1843208 | tf_op jit(solution)/shard_map/ppermute | solution.py:88
  98.7 19.6 %collective-permute-start.23 = (bf16[480,640]{1,0:T(8,128)(2,1)}, bf16[480,640]{1,0:T(8,128)(2,1)}, u32[]{:S(2)}, u32[]{:S(2)}) collective-permute-start(bf16[480,640]{1,0:T(8,128)(2,1)} %collective-permute-done.12.refs_23_), channel_id=1, source_target_pairs={{0,2},{1,3},{2,0},{3,1},{4,5},{5,4},{6,7},{7,6},{8,10},{9,11},{10,... | collective-permute-start | bytes 1843208 | tf_op jit(solution)/shard_map/ppermute | solution.py:88
  118.8 5.1 %collective-permute-start.28 = (bf16[480,640]{1,0:T(8,128)(2,1)}, bf16[480,640]{1,0:T(8,128)(2,1)}, u32[]{:S(2)}, u32[]{:S(2)}) collective-permute-start(bf16[480,640]{1,0:T(8,128)(2,1)} %collective-permute-done.22.refs_25_), channel_id=1, source_target_pairs={{0,4},{1,5},{2,6},{3,7},{4,0},{5,1},{6,2},{7,3},{8,12},{9,13},{10,... | collective-permute-start | bytes 1843208 | tf_op jit(solution)/shard_map/ppermute | solution.py:88
  119.1 4.8 %collective-permute-start.29 = (bf16[480,640]{1,0:T(8,128)(2,1)}, bf16[480,640]{1,0:T(8,128)(2,1)}, u32[]{:S(2)}, u32[]{:S(2)}) collective-permute-start(bf16[480,640]{1,0:T(8,128)(2,1)} %collective-permute-done.23.refs_27_), channel_id=1, source_target_pairs={{0,4},{1,5},{2,6},{3,7},{4,0},{5,1},{6,2},{7,3},{8,12},{9,13},{10,... | collective-permute-start | bytes 1843208 | tf_op jit(solution)/shard_map/ppermute | solution.py:88
  119.4 29.6 %collective-permute-start.31 = (bf16[2,960,256]{2,1,0:T(8,128)(2,1)S(1)}, bf16[2,960,256]{2,1,0:T(8,128)(2,1)}, u32[]{:S(2)}, u32[]{:S(2)}) collective-permute-start(bf16[2,960,256]{2,1,0:T(8,128)(2,1)S(1)} %bitcast.79), channel_id=1, source_target_pairs={{0,1},{1,0},{2,3},{3,2},{4,6},{5,7},{6,4},{7,5},{8,9},{9,8},{10,11... | collective-permute-start | bytes 2949128 | tf_op jit(solution)/shard_map/ppermute | solution.py:88
  122.3 26.7 %collective-permute-start.32 = (bf16[2,960,256]{2,1,0:T(8,128)(2,1)S(1)}, bf16[2,960,256]{2,1,0:T(8,128)(2,1)}, u32[]{:S(2)}, u32[]{:S(2)}) collective-permute-start(bf16[2,960,256]{2,1,0:T(8,128)(2,1)S(1)} %bitcast.80), channel_id=1, source_target_pairs={{0,2},{1,3},{2,0},{3,1},{4,5},{5,4},{6,7},{7,6},{8,10},{9,11},{10,... | collective-permute-start | bytes 2949128 | tf_op jit(solution)/shard_map/ppermute | solution.py:88
  123.9 25.1 %collective-permute-start.30 = (bf16[2,960,256]{2,1,0:T(8,128)(2,1)S(1)}, bf16[2,960,256]{2,1,0:T(8,128)(2,1)S(1)}, u32[]{:S(2)}, u32[]{:S(2)}) collective-permute-start(bf16[2,960,256]{2,1,0:T(8,128)(2,1)S(1)} %bitcast.86), channel_id=1, source_target_pairs={{0,4},{1,5},{2,6},{3,7},{4,0},{5,1},{6,2},{7,3},{8,12},{9,13},{10,... | collective-permute-start | bytes 2949128 | tf_op jit(solution)/shard_map/ppermute | solution.py:88
  149.9 18.1 %collective-permute-start.34 = (bf16[512,2560]{1,0:T(8,128)(2,1)}, bf16[512,2560]{1,0:T(8,128)(2,1)}, u32[]{:S(2)}, u32[]{:S(2)}) collective-permute-start(bf16[512,2560]{1,0:T(8,128)(2,1)} %get-tuple-element.385.given_ref), channel_id=1, source_target_pairs={{0,4},{1,5},{2,6},{3,7},{4,0},{5,1},{6,2},{7,3},{8,12},{9,13},{10,... | collective-permute-start | bytes 7864328 | tf_op jit(solution)/shard_map/ppermute | solution.py:88
  150.2 17.9 %collective-permute-start.35 = (bf16[512,2560]{1,0:T(8,128)(2,1)}, bf16[512,2560]{1,0:T(8,128)(2,1)}, u32[]{:S(2)}, u32[]{:S(2)}) collective-permute-start(bf16[512,2560]{1,0:T(8,128)(2,1)} %get-tuple-element.407.inner_ref), channel_id=1, source_target_pairs={{0,4},{1,5},{2,6},{3,7},{4,0},{5,1},{6,2},{7,3},{8,12},{9,13},{10,... | collective-permute-start | bytes 7864328 | tf_op jit(solution)/shard_map/ppermute | solution.py:88
  150.4 17.6 %collective-permute-start.33 = (bf16[960,512]{1,0:T(8,128)(2,1)}, bf16[960,512]{1,0:T(8,128)(2,1)}, u32[]{:S(2)}, u32[]{:S(2)}) collective-permute-start(bf16[960,512]{1,0:T(8,128)(2,1)} %get-tuple-element.426.left_ref), channel_id=1, source_target_pairs={{0,4},{1,5},{2,6},{3,7},{4,0},{5,1},{6,2},{7,3},{8,12},{9,13},{10,... | collective-permute-start | bytes 2949128 | tf_op jit(solution)/shard_map/ppermute | solution.py:88
  150.7 17.4 %collective-permute-start.36 = (bf16[2,960,256]{2,1,0:T(8,128)(2,1)}, bf16[2,960,256]{2,1,0:T(8,128)(2,1)}, u32[]{:S(2)}, u32[]{:S(2)}) collective-permute-start(bf16[2,960,256]{2,1,0:T(8,128)(2,1)} %collective-permute-done.31.refs_1_), channel_id=1, source_target_pairs={{0,2},{1,3},{2,0},{3,1},{4,5},{5,4},{6,7},{7,6},{8,10},{9,11},{10,... | collective-permute-start | bytes 2949128 | tf_op jit(solution)/shard_map/ppermute | solution.py:88
  174.5 16.8 %collective-permute-start.37 = (bf16[960,640]{1,0:T(8,128)(2,1)S(1)}, bf16[960,640]{1,0:T(8,128)(2,1)S(1)}, u32[]{:S(2)}, u32[]{:S(2)}) collective-permute-start(bf16[960,640]{1,0:T(8,128)(2,1)S(1)} %get-tuple-element.451), channel_id=1, source_target_pairs={{0,2},{1,3},{2,0},{3,1},{4,5},{5,4},{6,7},{7,6},{8,10},{9,11},{10,... | collective-permute-start | bytes 3686408 | tf_op jit(solution)/shard_map/ppermute | solution.py:88
  191.3 23.1 %collective-permute-start.39 = (bf16[256,2560]{1,0:T(8,128)(2,1)S(1)}, bf16[256,2560]{1,0:T(8,128)(2,1)S(1)}, u32[]{:S(2)}, u32[]{:S(2)}) collective-permute-start(bf16[256,2560]{1,0:T(8,128)(2,1)S(1)} %get-tuple-element.478), channel_id=1, source_target_pairs={{0,2},{1,3},{2,0},{3,1},{4,5},{5,4},{6,7},{7,6},{8,10},{9,11},{10,... | collective-permute-start | bytes 3932168 | tf_op jit(solution)/shard_map/ppermute | solution.py:88
  192.3 17.2 %collective-permute-start.38 = (bf16[480,640]{1,0:T(8,128)(2,1)S(1)}, bf16[480,640]{1,0:T(8,128)(2,1)S(1)}, u32[]{:S(2)}, u32[]{:S(2)}) collective-permute-start(bf16[480,640]{1,0:T(8,128)(2,1)S(1)} %add_convert_fusion.12), channel_id=1, source_target_pairs={{0,1},{1,0},{2,3},{3,2},{4,6},{5,7},{6,4},{7,5},{8,9},{9,8},{10,11... | collective-permute-start | bytes 1843208 | tf_op jit(solution)/shard_map/ppermute | solution.py:88
  214.5 20.6 %collective-permute-start.41 = (bf16[128,2560]{1,0:T(8,128)(2,1)S(1)}, bf16[128,2560]{1,0:T(8,128)(2,1)S(1)}, u32[]{:S(2)}, u32[]{:S(2)}) collective-permute-start(bf16[128,2560]{1,0:T(8,128)(2,1)S(1)} %add_convert_fusion.8), channel_id=1, source_target_pairs={{0,1},{1,0},{2,3},{3,2},{4,6},{5,7},{6,4},{7,5},{8,9},{9,8},{10,11... | collective-permute-start | bytes 1966088 | tf_op jit(solution)/shard_map/ppermute | solution.py:88
  215.7 20.1 %collective-permute-start.42 = (bf16[224,2560]{1,0:T(8,128)(2,1)S(1)}, bf16[224,2560]{1,0:T(8,128)(2,1)S(1)}, u32[]{:S(2)}, u32[]{:S(2)}) collective-permute-start(bf16[224,2560]{1,0:T(8,128)(2,1)S(1)} %get-tuple-element.505), channel_id=1, source_target_pairs={{0,2},{1,3},{2,0},{3,1},{4,5},{5,4},{6,7},{7,6},{8,10},{9,11},{10,... | collective-permute-start | bytes 3440648 | tf_op jit(solution)/shard_map/ppermute | solution.py:88
  216.8 18.3 %collective-permute-start.40 = (bf16[480,640]{1,0:T(8,128)(2,1)S(1)}, bf16[480,640]{1,0:T(8,128)(2,1)S(1)}, u32[]{:S(2)}, u32[]{:S(2)}) collective-permute-start(bf16[480,640]{1,0:T(8,128)(2,1)S(1)} %add_convert_fusion.11), channel_id=1, source_target_pairs={{0,8},{1,9},{2,10},{3,11},{4,12},{5,13},{6,14},{7,15},{24,16},{25,... | collective-permute-start | bytes 1843208 | tf_op jit(solution)/shard_map/ppermute | solution.py:88
  237.1 22.1 %collective-permute-start.45 = (bf16[128,2560]{1,0:T(8,128)(2,1)}, bf16[128,2560]{1,0:T(8,128)(2,1)}, u32[]{:S(2)}, u32[]{:S(2)}) collective-permute-start(bf16[128,2560]{1,0:T(8,128)(2,1)} %add_convert_fusion.7), channel_id=1, source_target_pairs={{0,8},{1,9},{2,10},{3,11},{4,12},{5,13},{6,14},{7,15},{24,16},{25,... | collective-permute-start | bytes 1966088 | tf_op jit(solution)/shard_map/ppermute | solution.py:88
  240.2 24.1 %collective-permute-start.43 = (bf16[2,512,640]{2,1,0:T(8,128)(2,1)}, bf16[2,512,640]{2,1,0:T(8,128)(2,1)}, u32[]{:S(2)}, u32[]{:S(2)}) collective-permute-start(bf16[2,512,640]{2,1,0:T(8,128)(2,1)} %get-tuple-element.510.refs_5_), channel_id=1, source_target_pairs={{0,2},{1,3},{2,0},{3,1},{4,5},{5,4},{6,7},{7,6},{8,10},{9,11},{10,... | collective-permute-start | bytes 3932168 | tf_op jit(solution)/shard_map/ppermute | solution.py:88
  241.3 17.8 %collective-permute-start.44 = (bf16[480,640]{1,0:T(8,128)(2,1)S(1)}, bf16[480,640]{1,0:T(8,128)(2,1)S(1)}, u32[]{:S(2)}, u32[]{:S(2)}) collective-permute-start(bf16[480,640]{1,0:T(8,128)(2,1)S(1)} %add_convert_fusion.10), channel_id=1, source_target_pairs={{8,16},{9,17},{10,18},{11,19},{12,20},{13,21},{14,22},{15,23},{16,... | collective-permute-start | bytes 1843208 | tf_op jit(solution)/shard_map/ppermute | solution.py:88
  242.9 16.2 %collective-permute-start.46 = (bf16[112,2560]{1,0:T(8,128)(2,1)}, bf16[112,2560]{1,0:T(8,128)(2,1)S(1)}, u32[]{:S(2)}, u32[]{:S(2)}) collective-permute-start(bf16[112,2560]{1,0:T(8,128)(2,1)} %add_convert_fusion.16), channel_id=1, source_target_pairs={{0,1},{1,0},{2,3},{3,2},{4,6},{5,7},{6,4},{7,5},{8,9},{9,8},{10,11... | collective-permute-start | bytes 1720328 | tf_op jit(solution)/shard_map/ppermute | solution.py:88
  264.2 5.5 %collective-permute-start.49 = (bf16[512,2688]{1,0:T(8,128)(2,1)}, bf16[512,2688]{1,0:T(8,128)(2,1)S(1)}, u32[]{:S(2)}, u32[]{:S(2)}) collective-permute-start(bf16[512,2688]{1,0:T(8,128)(2,1)} %get-tuple-element.530), channel_id=1, source_target_pairs={{0,4},{1,5},{2,6},{3,7},{4,0},{5,1},{6,2},{7,3},{8,12},{9,13},{10,... | collective-permute-start | bytes 8257544 | tf_op jit(solution)/shard_map/ppermute | solution.py:88
  265.8 29.0 %collective-permute-start.51 = (bf16[128,2560]{1,0:T(8,128)(2,1)S(1)}, bf16[128,2560]{1,0:T(8,128)(2,1)}, u32[]{:S(2)}, u32[]{:S(2)}) collective-permute-start(bf16[128,2560]{1,0:T(8,128)(2,1)S(1)} %add_convert_fusion.5), channel_id=1, source_target_pairs={{8,16},{9,17},{10,18},{11,19},{12,20},{13,21},{14,22},{15,23},{16,... | collective-permute-start | bytes 1966088 | tf_op jit(solution)/shard_map/ppermute | solution.py:88
  268.3 26.5 %collective-permute-start.48 = (bf16[480,640]{1,0:T(8,128)(2,1)}, bf16[480,640]{1,0:T(8,128)(2,1)}, u32[]{:S(2)}, u32[]{:S(2)}) collective-permute-start(bf16[480,640]{1,0:T(8,128)(2,1)} %add_convert_fusion.9), channel_id=1, source_target_pairs={{8,0},{9,1},{10,2},{11,3},{12,4},{13,5},{14,6},{15,7},{16,24},{17,... | collective-permute-start | bytes 1843208 | tf_op jit(solution)/shard_map/ppermute | solution.py:88
  271.7 25.6 %collective-permute-start.50 = (bf16[256,2688]{1,0:T(8,128)(2,1)}, bf16[256,2688]{1,0:T(8,128)(2,1)}, u32[]{:S(2)}, u32[]{:S(2)}) collective-permute-start(bf16[256,2688]{1,0:T(8,128)(2,1)} %add_convert_fusion), channel_id=1, source_target_pairs={{0,2},{1,3},{2,0},{3,1},{4,5},{5,4},{6,7},{7,6},{8,10},{9,11},{10,... | collective-permute-start | bytes 4128776 | tf_op jit(solution)/shard_map/ppermute | solution.py:88
  274.8 20.0 %collective-permute-start.47 = (bf16[1,512,640]{2,1,0:T(8,128)(2,1)}, bf16[1,512,640]{2,1,0:T(8,128)(2,1)}, u32[]{:S(2)}, u32[]{:S(2)}) collective-permute-start(bf16[1,512,640]{2,1,0:T(8,128)(2,1)} %add_convert_fusion.6), channel_id=1, source_target_pairs={{0,1},{1,0},{2,3},{3,2},{4,6},{5,7},{6,4},{7,5},{8,9},{9,8},{10,11... | collective-permute-start | bytes 1966088 | tf_op jit(solution)/shard_map/ppermute | solution.py:88
  277.0 17.8 %collective-permute-start.52 = (bf16[112,2560]{1,0:T(8,128)(2,1)}, bf16[112,2560]{1,0:T(8,128)(2,1)S(1)}, u32[]{:S(2)}, u32[]{:S(2)}) collective-permute-start(bf16[112,2560]{1,0:T(8,128)(2,1)} %add_convert_fusion.15), channel_id=1, source_target_pairs={{0,8},{1,9},{2,10},{3,11},{4,12},{5,13},{6,14},{7,15},{24,16},{25,... | collective-permute-start | bytes 1720328 | tf_op jit(solution)/shard_map/ppermute | solution.py:88
  298.6 23.1 %collective-permute-start.59 = (bf16[112,2560]{1,0:T(8,128)(2,1)S(1)}, bf16[112,2560]{1,0:T(8,128)(2,1)S(1)}, u32[]{:S(2)}, u32[]{:S(2)}) collective-permute-start(bf16[112,2560]{1,0:T(8,128)(2,1)S(1)} %add_convert_fusion.14), channel_id=1, source_target_pairs={{8,16},{9,17},{10,18},{11,19},{12,20},{13,21},{14,22},{15,23},{16,... | collective-permute-start | bytes 1720328 | tf_op jit(solution)/shard_map/ppermute | solution.py:88
  301.1 11.0 %collective-permute-start.54 = (bf16[128,2688]{1,0:T(8,128)(2,1)S(1)}, bf16[128,2688]{1,0:T(8,128)(2,1)S(1)}, u32[]{:S(2)}, u32[]{:S(2)}) collective-permute-start(bf16[128,2688]{1,0:T(8,128)(2,1)S(1)} %add_convert_fusion.2), channel_id=1, source_target_pairs={{0,1},{1,0},{2,3},{3,2},{4,6},{5,7},{6,4},{7,5},{8,9},{9,8},{10,11... | collective-permute-start | bytes 2064392 | tf_op jit(solution)/shard_map/ppermute | solution.py:88
  303.4 30.7 %collective-permute-start.58 = (bf16[128,2560]{1,0:T(8,128)(2,1)S(1)}, bf16[128,2560]{1,0:T(8,128)(2,1)S(1)}, u32[]{:S(2)}, u32[]{:S(2)}) collective-permute-start(bf16[128,2560]{1,0:T(8,128)(2,1)S(1)} %add_convert_fusion.3), channel_id=1, source_target_pairs={{8,0},{9,1},{10,2},{11,3},{12,4},{13,5},{14,6},{15,7},{16,24},{17,... | collective-permute-start | bytes 1966088 | tf_op jit(solution)/shard_map/ppermute | solution.py:88
  306.2 26.5 %collective-permute-start.53 = (bf16[480,640]{1,0:T(8,128)(2,1)S(1)}, bf16[480,640]{1,0:T(8,128)(2,1)S(1)}, u32[]{:S(2)}, u32[]{:S(2)}) collective-permute-start(bf16[480,640]{1,0:T(8,128)(2,1)S(1)} %broadcast_select_fusion.3), channel_id=1, source_target_pairs={{0,4},{1,5},{2,6},{3,7},{4,0},{5,1},{6,2},{7,3},{8,12},{9,13},{10,... | collective-permute-start | bytes 1843208 | tf_op jit(solution)/shard_map/ppermute | solution.py:88
  314.2 22.6 %collective-permute-start.55 = (bf16[32,2688]{1,0:T(8,128)(2,1)S(1)}, bf16[32,2688]{1,0:T(8,128)(2,1)S(1)}, u32[]{:S(2)}, u32[]{:S(2)}) collective-permute-start(bf16[32,2688]{1,0:T(8,128)(2,1)S(1)} %get-tuple-element.566), channel_id=1, source_target_pairs={{0,8},{1,9},{2,10},{3,11},{4,12},{5,13},{6,14},{7,15},{8,0},{9,1},... | collective-permute-start | bytes 516104 | tf_op jit(solution)/shard_map/ppermute | solution.py:88
  321.6 15.1 %collective-permute-start.56 = (bf16[32,2688]{1,0:T(8,128)(2,1)S(1)}, bf16[32,2688]{1,0:T(8,128)(2,1)S(1)}, u32[]{:S(2)}, u32[]{:S(2)}) collective-permute-start(bf16[32,2688]{1,0:T(8,128)(2,1)S(1)} %get-tuple-element.565), channel_id=1, source_target_pairs={{0,16},{1,17},{2,18},{3,19},{4,20},{5,21},{6,22},{7,23},{8,24},{9,... | collective-permute-start | bytes 516104 | tf_op jit(solution)/shard_map/ppermute | solution.py:88
  321.7 15.1 %collective-permute-start.57 = (bf16[32,2688]{1,0:T(8,128)(2,1)S(1)}, bf16[32,2688]{1,0:T(8,128)(2,1)S(1)}, u32[]{:S(2)}, u32[]{:S(2)}) collective-permute-start(bf16[32,2688]{1,0:T(8,128)(2,1)S(1)} %get-tuple-element.564), channel_id=1, source_target_pairs={{0,24},{1,25},{2,26},{3,27},{4,28},{5,29},{6,30},{7,31},{8,16},{9,... | collective-permute-start | bytes 516104 | tf_op jit(solution)/shard_map/ppermute | solution.py:88
  336.9 8.4 %collective-permute-start.60 = (bf16[32,2688]{1,0:T(8,128)(2,1)S(1)}, bf16[32,2688]{1,0:T(8,128)(2,1)S(1)}, u32[]{:S(2)}, u32[]{:S(2)}) collective-permute-start(bf16[32,2688]{1,0:T(8,128)(2,1)S(1)} %add_convert_fusion.17), channel_id=1, source_target_pairs={{0,8},{1,9},{2,10},{3,11},{4,12},{5,13},{6,14},{7,15},{8,0},{9,1},... | collective-permute-start | bytes 516104 | tf_op jit(solution)/shard_map/ppermute | solution.py:88
  338.7 13.8 %collective-permute-start.61 = (bf16[32,2688]{1,0:T(8,128)(2,1)S(1)}, bf16[32,2688]{1,0:T(8,128)(2,1)S(1)}, u32[]{:S(2)}, u32[]{:S(2)}) collective-permute-start(bf16[32,2688]{1,0:T(8,128)(2,1)S(1)} %add_convert_fusion.17), channel_id=1, source_target_pairs={{0,16},{1,17},{2,18},{3,19},{4,20},{5,21},{6,22},{7,23},{8,24},{9,... | collective-permute-start | bytes 516104 | tf_op jit(solution)/shard_map/ppermute | solution.py:88
  338.7 13.7 %collective-permute-start.62 = (bf16[32,2688]{1,0:T(8,128)(2,1)S(1)}, bf16[32,2688]{1,0:T(8,128)(2,1)S(1)}, u32[]{:S(2)}, u32[]{:S(2)}) collective-permute-start(bf16[32,2688]{1,0:T(8,128)(2,1)S(1)} %add_convert_fusion.17), channel_id=1, source_target_pairs={{0,24},{1,25},{2,26},{3,27},{4,28},{5,29},{6,30},{7,31},{8,16},{9,... | collective-permute-start | bytes 516104 | tf_op jit(solution)/shard_map/ppermute | solution.py:88
  341.5 20.5 %collective-permute-start.65 = (bf16[112,2560]{1,0:T(8,128)(2,1)S(1)}, bf16[112,2560]{1,0:T(8,128)(2,1)S(1)}, u32[]{:S(2)}, u32[]{:S(2)}) collective-permute-start(bf16[112,2560]{1,0:T(8,128)(2,1)S(1)} %add_convert_fusion.13), channel_id=1, source_target_pairs={{8,0},{9,1},{10,2},{11,3},{12,4},{13,5},{14,6},{15,7},{16,24},{17,... | collective-permute-start | bytes 1720328 | tf_op jit(solution)/shard_map/ppermute | solution.py:88
  343.7 25.0 %collective-permute-start.64 = (bf16[128,2560]{1,0:T(8,128)(2,1)}, bf16[128,2560]{1,0:T(8,128)(2,1)}, u32[]{:S(2)}, u32[]{:S(2)}) collective-permute-start(bf16[128,2560]{1,0:T(8,128)(2,1)} %broadcast_select_fusion.refs_0_), channel_id=1, source_target_pairs={{0,4},{1,5},{2,6},{3,7},{4,0},{5,1},{6,2},{7,3},{8,12},{9,13},{10,... | collective-permute-start | bytes 1966088 | tf_op jit(solution)/shard_map/ppermute | solution.py:88
  352.8 12.1 %collective-permute-start.63 = (bf16[128,2688]{1,0:T(8,128)(2,1)S(1)}, bf16[128,2688]{1,0:T(8,128)(2,1)}, u32[]{:S(2)}, u32[]{:S(2)}) collective-permute-start(bf16[128,2688]{1,0:T(8,128)(2,1)S(1)} %bitcast.82), channel_id=1, source_target_pairs={{0,4},{1,5},{2,6},{3,7},{4,0},{5,1},{6,2},{7,3},{8,12},{9,13},{10,... | collective-permute-start | bytes 2064392 | tf_op jit(solution)/shard_map/ppermute | solution.py:88
  362.9 5.8 %collective-permute-start.66 = (bf16[112,2560]{1,0:T(8,128)(2,1)}, bf16[112,2560]{1,0:T(8,128)(2,1)}, u32[]{:S(2)}, u32[]{:S(2)}) collective-permute-start(bf16[112,2560]{1,0:T(8,128)(2,1)} %broadcast_select_fusion.5.refs_2_), channel_id=1, source_target_pairs={{0,4},{1,5},{2,6},{3,7},{4,0},{5,1},{6,2},{7,3},{8,12},{9,13},{10,... | collective-permute-start | bytes 1720328 | tf_op jit(solution)/shard_map/ppermute | solution.py:88
  (83 other events, 1104.5 us)
